TPU v7x, 128 devices: a whole 4x4x4 slice. The times are simulated.
128 devices in a mesh: tm: 32 (over x, y, core), space: 4 (over z).
Axes of the slice: x: 4, y: 4, z: 4, core: 2. Of those that a mesh axis runs over, the one named last changes fastest.
Arguments:
- right_side: float32 [32, 4, 16, 64, 128], P('tm', None, 'space'), may hold values from -4 to 6
- metric: float32 [32, 16, 64, 128], P('tm', 'space'), may hold values from 0.5 to 2
- wall_mask: int32 [16, 64, 128], P('space'), may hold values from 0 to 2, as said below
Outputs:
- solution: float32 [32, 4, 16, 64, 128], P('tm', None, 'space')
Inputs may be any that keep to these rules, and one draw needn't show every extreme that they name: `wall_mask`: 0 marks a fluid node, 1 a wall node, 2 an inlet node; inlet nodes lie only in the x-plane 0, and every draw has nodes of all three kinds.
All inputs are finite; a program needn't handle non-finite values.
Results may differ from a plain program's by a relative error of at most 0.0001.
Values sent between devices are 32-bit elements; how exact they have to be, the bound alone decides.
A program may use at most 128 MiB of HBM per device.

v0:
```python
import jax
import jax.numpy as jnp
from jax import lax
from jax.sharding import PartitionSpec as P

CYCLES = 2
NU = 2
COARSE_SWEEPS = 4


OMEGA = 0.6


def with_halo(block, sides, width):
    for axis, dim in sides:
        count = lax.axis_size(axis)
        forward = [(i, i + 1) for i in range(count - 1)]
        backward = [(target, source) for source, target in forward]
        low = lax.ppermute(
            lax.slice_in_dim(block, block.shape[dim] - width, None, axis=dim), axis, forward
        )
        high = lax.ppermute(lax.slice_in_dim(block, 0, width, axis=dim), axis, backward)
        block = jnp.concatenate([low, block, high], axis=dim)
    return block


def from_behind(array, axis, by):
    size = lax.axis_size(axis)
    pairs = [(i, i + by) for i in range(size) if 0 <= i + by < size]
    return lax.ppermute(array, axis, pairs)


def spread_2(array, axis, root):
    mine = lax.axis_index(axis) == root
    return lax.psum(jnp.where(mine, array, jnp.zeros_like(array)), axis)


def stencil_apply(padded, metric, earlier, spacing, pinned):
    center = padded[:, :, 1:-1]
    ahead_x = padded[:, :, 2:]
    behind_x = padded[:, :, :-2]
    padded_yz = jnp.pad(center, ((0, 0), (0, 0), (0, 0), (1, 1), (1, 1)))
    ahead_y = padded_yz[:, :, :, 2:, 1:-1]
    behind_y = padded_yz[:, :, :, :-2, 1:-1]
    ahead_z = padded_yz[:, :, :, 1:-1, 2:]
    behind_z = padded_yz[:, :, :, 1:-1, :-2]
    inverse_square = 1.0 / (spacing * spacing)
    half_inverse = 0.5 / spacing
    laplace = (
        6.0 * center - ahead_x - behind_x - ahead_y - behind_y - ahead_z - behind_z
    ) * inverse_square
    grad_x = (ahead_x[:, 3] - behind_x[:, 3]) * half_inverse
    grad_y = (ahead_y[:, 3] - behind_y[:, 3]) * half_inverse
    grad_z = (ahead_z[:, 3] - behind_z[:, 3]) * half_inverse
    divergence = (
        ahead_x[:, 0]
        - behind_x[:, 0]
        + (ahead_y[:, 1] - behind_y[:, 1])
        + (ahead_z[:, 2] - behind_z[:, 2])
    ) * half_inverse
    coupling = jnp.stack([grad_x, grad_y, grad_z, divergence], axis=1)
    result = 2.0 * metric[:, None] * (center - earlier) + laplace + coupling
    if pinned is None:
        return result
    return jnp.where(pinned > 0, center, result)


def diagonal_of(metric, spacing, pinned):
    diagonal = 2.0 * metric[:, None] + 6.0 / (spacing * spacing)
    if pinned is None:
        return diagonal
    return jnp.where(pinned > 0, 1.0, diagonal)


def build_pinned(wall_mask):
    moving = (wall_mask > 0).astype(jnp.int32)
    walled = (wall_mask == 1).astype(jnp.int32)
    return jnp.stack([moving, walled, walled, jnp.zeros_like(walled)], axis=0)[None]


def restrict(values):
    dims_all = values.shape
    leading = dims_all[:-3]
    depth_x, height_y, width_z = dims_all[-3:]
    blocks = values.reshape(leading + (depth_x // 2, 2, height_y // 2, 2, width_z // 2, 2))
    offset = len(leading)
    return jnp.sum(blocks, axis=(offset + 1, offset + 3, offset + 5)) * 0.125


def prolong(values):
    dims_all = values.shape
    leading = dims_all[:-3]
    depth_x, height_y, width_z = dims_all[-3:]
    spread = jnp.broadcast_to(
        values.reshape(leading + (depth_x, 1, height_y, 1, width_z, 1)),
        leading + (depth_x, 2, height_y, 2, width_z, 2),
    )
    return spread.reshape(leading + (2 * depth_x, 2 * height_y, 2 * width_z))


def coarse_solve(source, metric, spacing):
    diagonal = 2.0 * metric[:, None] + 6.0 / (spacing * spacing)

    def advance(earlier, inputs):
        source_now, metric_now, diagonal_now = inputs
        target = source_now + 2.0 * metric_now[None] * earlier
        iterate = jnp.zeros_like(source_now)
        nothing = jnp.zeros_like(source_now)[None]
        for repeat in range(COARSE_SWEEPS):
            padded = jnp.pad(iterate[None], ((0, 0), (0, 0), (1, 1), (0, 0), (0, 0)))
            applied = stencil_apply(padded, metric_now[None], nothing, spacing, None)[0]
            iterate = iterate + (target - applied) / diagonal_now
        return (iterate, iterate)

    initial = jnp.zeros_like(source[0])
    final_state, history = lax.scan(advance, initial, (source, metric, diagonal))
    return history


def apply_local(values, metric, spacing, pinned):
    padded = with_halo(values, (("space", 2),), 1)
    arrived = from_behind(values, "tm", 1)
    earlier = jnp.concatenate([arrived, values[:-1]], axis=0)
    return stencil_apply(padded, metric, earlier, spacing, pinned)


def assemble(flat_source, flat_metric, time_devs, plane_devs, local_dims):
    local_steps, components, planes, height_y, width_z = local_dims
    whole_source = flat_source.reshape(
        time_devs, plane_devs, local_steps, components, planes, height_y, width_z
    )
    whole_source = whole_source.transpose(0, 2, 3, 1, 4, 5, 6).reshape(
        time_devs * local_steps, components, plane_devs * planes, height_y, width_z
    )
    whole_metric = flat_metric.reshape(
        time_devs, plane_devs, local_steps, planes, height_y, width_z
    )
    whole_metric = whole_metric.transpose(0, 2, 1, 3, 4, 5).reshape(
        time_devs * local_steps, plane_devs * planes, height_y, width_z
    )
    return (whole_source, whole_metric)


def coarse_correction(source, metric_two):
    time_devs = lax.axis_size("tm")
    plane_devs = lax.axis_size("space")
    time_at = lax.axis_index("tm")
    plane_at = lax.axis_index("space")
    local_dims = source.shape
    local_steps, components, planes, height_y, width_z = local_dims
    source_flat = source.reshape(1, -1)
    metric_flat = metric_two.reshape(1, -1)
    flat_source, flat_metric = (
        lax.all_gather(source_flat, ("tm", "space"), axis=0, tiled=True),
        lax.all_gather(metric_flat, ("tm", "space"), axis=0, tiled=True),
    )
    whole_source, whole_metric = assemble(
        flat_source, flat_metric, time_devs, plane_devs, local_dims
    )
    solved = coarse_solve(whole_source, whole_metric, 4.0)
    owner = jnp.logical_and(time_at == 0, plane_at == 0)
    solved = jnp.where(owner, solved, jnp.zeros_like(solved))
    whole = spread_2(solved, ("tm", "space"), 0)
    return lax.dynamic_slice(
        whole,
        (time_at * local_steps, 0, plane_at * planes, 0, 0),
        (local_steps, components, planes, height_y, width_z),
    )


def per_device(right_side, metric, wall_mask):
    pinned = build_pinned(wall_mask)
    metric_one = restrict(metric)
    metric_two = restrict(metric_one)
    metrics = (metric, metric_one)
    pinned_levels = (pinned, None)

    def cycle(depth, values, source):
        spacing = 2.0**depth
        diagonal = diagonal_of(metrics[depth], spacing, pinned_levels[depth])
        for repeat in range(NU):
            values = (
                values
                + OMEGA
                * (source - apply_local(values, metrics[depth], spacing, pinned_levels[depth]))
                / diagonal
            )
        residual = source - apply_local(values, metrics[depth], spacing, pinned_levels[depth])
        coarse_source = restrict(residual)
        if depth == 1:
            correction = coarse_correction(coarse_source, metric_two)
        else:
            correction = cycle(1, jnp.zeros_like(coarse_source), coarse_source)
        values = values + prolong(correction)
        for repeat in range(NU):
            values = (
                values
                + OMEGA
                * (source - apply_local(values, metrics[depth], spacing, pinned_levels[depth]))
                / diagonal
            )
        return values

    solution = jnp.zeros_like(right_side)
    for repeat in range(CYCLES):
        solution = cycle(0, solution, right_side)
    return solution


def solution(mesh):
    placed = (
        P("tm", None, "space", None, None),
        P("tm", "space", None, None),
        P("space", None, None),
    )
    return jax.shard_map(
        per_device,
        mesh=mesh,
        in_specs=placed,
        out_specs=P("tm", None, "space", None, None),
        check_vma=False,
    )
```

profile of v0, /device:TPU:2, one launch (start us, length us, event | category | flops | bytes accessed | tf_op | source)
XLA Modules:
  0.0 1115.3 jit_solution(10426448366335955256)
XLA Ops:
  8.0 4.6 collective-permute-start.2
  17.6 7.6 collective-permute-done
  27.7 3.8 collective-permute-start.5
  34.1 5.2 collective-permute-start.11
  39.3 9.8 reshape.1435
  49.1 4.0 reduce_sum.61
  55.9 3.9 collective-permute-start.8
  63.2 3.5 collective-permute-done.7
  67.3 8.8 copy.398
  76.1 13.0 %reduce_sum.60 = f32[4,2,32,64]{0,3,2,1:T(8,128)} reduce(f32[4,2,2,32,2,64,2]{0,6,5,4,3,2,1:T(2,128)} %bitcast.226, f32[]{:T(128)} %constant.217.clone.1), dimensions={2,4,6}, to_apply=%region_0.0 | reduce | flops 114688 | bytes 589828 | tf_op jit(solution)/shard_map/reduce_sum | solution.py:87
  92.3 3.8 collective-permute-start.14
  99.3 2.9 collective-permute-done.13
  102.4 3.4 collective-permute-done.12
  106.0 4.5 collective-permute-start.17
  113.8 2.9 collective-permute-done.16
  116.8 3.4 collective-permute-done.15
  123.4 61.0 %all-gather.1 = f32[128,1,512]{2,1,0:T(1,128)S(1)} all-gather(f32[1,1,512]{2,1,0:T(1,128)S(1)} %reshape.1445), channel_id=1, replica_groups=mesh['tm'=32,'space'=4] {'tm','space'}, dimensions={0}, use_global_device_ids=true | all-gather | bytes 264192 | tf_op jit(solution)/shard_map/all_gather | solution.py:155
  188.2 3.7 reduce.14
  192.0 2.8 reshape.1436
  197.3 139.7 %while.36 = (s32[]{:T(128)}, f32[4,4,16,32]{3,2,1,0:T(8,128)S(1)}, f32[32,4,4,16,32]{4,3,1,2,0:T(8,128)}, f32[32,4,4,16,32]{4,3,1,2,0:T(8,128)}, f32[32,4,16,32]...) while((s32[]{:T(128)}, f32[4,4,16,32]{3,2,1,0:T(8,128)S(1)}, ...), condition=%wide.region_7.8_spmd.clone, body=%wide.region_6.7_spmd.clone.sunk | while | flops 726035 | bytes 1315095 | solution.py:116
  337.0 3.0 select_select_fusion.1
  340.0 153.9 %all-reduce.42.cloned.1.call-done = f32[32,4,4,16,32]{4,3,1,2,0:T(8,128)} async-done(((f32[32,4,4,16,32]{4,3,1,2,0:T(8,128)}), f32[32,4,4,16,32]{4,3,1,2,0:T(8,128)}) %all-reduce.42.cloned.1.call-update) | async-done | bytes 1048592 | tf_op jit(solution)/shard_map/psum | solution.py:35
  501.1 2.9 collective-permute-done.19
  504.1 3.4 collective-permute-done.18
  507.7 4.5 collective-permute-start.23
  515.5 2.9 collective-permute-done.22
  518.5 3.4 collective-permute-done.21
  524.1 8.9 broadcast_in_dim.179
  533.0 10.0 copy.409
  545.1 4.6 collective-permute-start.26
  552.1 4.4 collective-permute-done.25
  559.2 3.6 collective-permute-start.29
  565.3 4.4 collective-permute-done.28
  572.4 3.6 collective-permute-start.32
  578.4 4.4 collective-permute-done.31
  585.5 3.6 collective-permute-start.35
  591.6 4.4 collective-permute-done.34
  598.7 3.6 collective-permute-start.38
  604.7 4.4 collective-permute-done.37
  609.8 8.8 copy.410
  618.6 13.0 %reduce_sum.83 = f32[4,2,32,64]{0,3,2,1:T(8,128)} reduce(f32[4,2,2,32,2,64,2]{0,6,5,4,3,2,1:T(2,128)} %bitcast.228, f32[]{:T(128)} %constant.217.clone.1), dimensions={2,4,6}, to_apply=%region_9.10 | reduce | flops 114688 | bytes 589828 | tf_op jit(solution)/shard_map/reduce_sum | solution.py:87
  634.0 3.6 collective-permute-start.41
  640.8 2.9 collective-permute-done.40
  643.8 3.4 collective-permute-done.39
  647.4 4.5 collective-permute-start.44
  655.2 2.9 collective-permute-done.43
  658.2 3.4 collective-permute-done.42
  664.2 62.6 %all-gather.8.cloned.1.call-done = f32[128,1,2048]{2,1,0:T(1,128)} async-done(((f32[1,1,2048]{2,1,0:T(1,128)}), f32[128,1,2048]{2,1,0:T(1,128)}) %all-gather.8.cloned.1.call-update) | async-done | bytes 1048592 | tf_op jit(solution)/shard_map/all_gather | solution.py:154
  726.8 3.7 reduce.17
  730.5 2.8 reshape.1439
  735.8 139.7 %while.37 = (s32[]{:T(128)}, f32[4,4,16,32]{3,2,1,0:T(8,128)S(1)}, f32[32,4,4,16,32]{4,3,1,2,0:T(8,128)}, f32[32,4,4,16,32]{4,3,1,2,0:T(8,128)}, f32[32,4,16,32]...) while((s32[]{:T(128)}, f32[4,4,16,32]{3,2,1,0:T(8,128)S(1)}, ...), condition=%wide.region_13.14_spmd.clone, body=%wide.region_12.13_spmd.clone.sunk | while | flops 726035 | bytes 1315095 | solution.py:116
  875.5 3.0 select_select_fusion
  878.5 152.8 %all-reduce.44.cloned.1.call-done = f32[32,4,4,16,32]{4,3,1,2,0:T(8,128)} async-done(((f32[32,4,4,16,32]{4,3,1,2,0:T(8,128)}), f32[32,4,4,16,32]{4,3,1,2,0:T(8,128)}) %all-reduce.44.cloned.1.call-update) | async-done | bytes 1048592 | tf_op jit(solution)/shard_map/psum | solution.py:35
  1038.4 2.9 collective-permute-done.46
  1041.4 3.4 collective-permute-done.45
  1045.0 4.5 collective-permute-start.50
  1052.8 2.9 collective-permute-done.49
  1055.9 3.4 collective-permute-done.48
  1061.5 8.9 broadcast_in_dim.186
  1070.4 10.0 copy.421
  1082.4 4.6 collective-permute-start.53
  1089.5 4.4 collective-permute-done.52
  1096.6 3.6 collective-permute-start.56
  1102.6 4.4 collective-permute-done.55
  (1341 shorter events, 390.6 us)
Async XLA Ops:
  6.5 18.7 %copy-start = (f32[1,4,4,64,128]{4,3,2,1,0:T(8,128)S(1)}, f32[1,4,4,64,128]{4,3,2,1,0:T(8,128)}, u32[]{:S(2)}) copy-start(f32[1,4,4,64,128]{4,3,2,1,0:T(8,128)} %param.7) | copy-start | bytes 1572868
  6.5 181.7 %all-gather.6.cloned.1.call-start = ((), (), s32[]{:S(2)}) async-start(), calls=%async_computation.2 | async-start | bytes 1056768 | tf_op jit(solution)/shard_map/all_gather | solution.py:154
  6.6 10.8 collective-permute-start.1
  8.0 9.4 collective-permute-start.2
  12.6 12.6 %collective-permute-start = (f32[1,4,4,64,128]{4,3,2,1,0:T(8,128)S(1)}, f32[1,4,4,64,128]{4,3,2,1,0:T(8,128)S(1)}, u32[]{:S(2)}, u32[]{:S(2)}) collective-permute-start(f32[1,4,4,64,128]{4,3,2,1,0:T(8,128)S(1)} %broadcast.1333), channel_id=1, source_target_pairs={{0,4},{4,8},{8,12},{12,16},{16,20},{20,24},{24,28},{28,32},{32,36}... | collective-permute-start | bytes 1572872 | tf_op jit(solution)/shard_map/ppermute | solution.py:30
  17.6 21.7 %copy-start.1 = (f32[1,4,64,128]{3,2,1,0:T(8,128)S(1)}, f32[1,4,64,128]{3,2,1,0:T(8,128)}, u32[]{:S(2)}) copy-start(f32[1,4,64,128]{3,2,1,0:T(8,128)} %param.8) | copy-start | bytes 393220
  25.7 27.7 %collective-permute-start.3 = (f32[1,4,4,64,128]{4,3,2,1,0:T(8,128)S(1)}, f32[1,4,4,64,128]{4,3,2,1,0:T(8,128)S(1)}, u32[]{:S(2)}, u32[]{:S(2)}) collective-permute-start(f32[1,4,4,64,128]{4,3,2,1,0:T(8,128)S(1)} %get-tuple-element.467), channel_id=1, source_target_pairs={{0,4},{4,8},{8,12},{12,16},{16,20},{20,24},{24,28},{28,32},{32,36}... | collective-permute-start | bytes 1572872 | tf_op jit(solution)/shard_map/ppermute | solution.py:30
  27.7 25.5 %collective-permute-start.5 = (f32[1,4,1,64,128]{4,3,2,1,0:T(8,128)S(1)}, f32[1,4,1,64,128]{4,3,2,1,0:T(8,128)S(1)}, u32[]{:S(2)}, u32[]{:S(2)}) collective-permute-start(f32[1,4,1,64,128]{4,3,2,1,0:T(8,128)S(1)} %get-tuple-element.568), channel_id=1, source_target_pairs={{0,1},{1,2},{2,3},{4,5},{5,6},{6,7},{8,9},{9,10},{10,11},{12,13},{... | collective-permute-start | bytes 393224 | tf_op jit(solution)/shard_map/ppermute | solution.py:19
  31.5 21.6 %collective-permute-start.4 = (f32[1,4,1,64,128]{4,3,2,1,0:T(8,128)S(1)}, f32[1,4,1,64,128]{4,3,2,1,0:T(8,128)S(1)}, u32[]{:S(2)}, u32[]{:S(2)}) collective-permute-start(f32[1,4,1,64,128]{4,3,2,1,0:T(8,128)S(1)} %get-tuple-element.567), channel_id=1, source_target_pairs={{1,0},{2,1},{3,2},{5,4},{6,5},{7,6},{9,8},{10,9},{11,10},{13,12},{... | collective-permute-start | bytes 393224 | tf_op jit(solution)/shard_map/ppermute | solution.py:22
  32.8 28.3 %collective-permute-start.10 = (f32[1,4,1,32,64]{4,3,2,1,0:T(8,128)S(1)}, f32[1,4,1,32,64]{4,3,2,1,0:T(8,128)S(1)}, u32[]{:S(2)}, u32[]{:S(2)}) collective-permute-start(f32[1,4,1,32,64]{4,3,2,1,0:T(8,128)S(1)} %broadcast.1342), channel_id=1, source_target_pairs={{1,0},{2,1},{3,2},{5,4},{6,5},{7,6},{9,8},{10,9},{11,10},{13,12},{... | collective-permute-start | bytes 98312 | tf_op jit(solution)/shard_map/ppermute | solution.py:22
  34.1 29.0 %collective-permute-start.11 = (f32[1,4,1,32,64]{4,3,2,1,0:T(8,128)S(1)}, f32[1,4,1,32,64]{4,3,2,1,0:T(8,128)S(1)}, u32[]{:S(2)}, u32[]{:S(2)}) collective-permute-start(f32[1,4,1,32,64]{4,3,2,1,0:T(8,128)S(1)} %broadcast.1342), channel_id=1, source_target_pairs={{0,1},{1,2},{2,3},{4,5},{5,6},{6,7},{8,9},{9,10},{10,11},{12,13},{... | collective-permute-start | bytes 98312 | tf_op jit(solution)/shard_map/ppermute | solution.py:19
  53.9 13.0 %collective-permute-start.6 = (f32[1,4,4,64,128]{4,3,2,1,0:T(8,128)S(1)}, f32[1,4,4,64,128]{4,3,2,1,0:T(8,128)S(1)}, u32[]{:S(2)}, u32[]{:S(2)}) collective-permute-start(f32[1,4,4,64,128]{4,3,2,1,0:T(8,128)S(1)} %fusion.283), channel_id=1, source_target_pairs={{0,4},{4,8},{8,12},{12,16},{16,20},{20,24},{24,28},{28,32},{32,36}... | collective-permute-start | bytes 1572872 | tf_op jit(solution)/shard_map/ppermute | solution.py:30
  55.9 7.3 collective-permute-start.8
  59.8 6.9 collective-permute-start.7
  61.1 30.3 %collective-permute-start.9 = (f32[1,4,2,32,64]{4,3,2,1,0:T(8,128)S(1)}, f32[1,4,2,32,64]{4,3,2,1,0:T(8,128)S(1)}, u32[]{:S(2)}, u32[]{:S(2)}) collective-permute-start(f32[1,4,2,32,64]{4,3,2,1,0:T(8,128)S(1)} %broadcast.1341), channel_id=1, source_target_pairs={{0,4},{4,8},{8,12},{12,16},{16,20},{20,24},{24,28},{28,32},{32,36}... | collective-permute-start | bytes 196616 | tf_op jit(solution)/shard_map/ppermute | solution.py:30
  92.3 7.1 collective-permute-start.14
  96.1 6.2 collective-permute-start.13
  97.4 8.4 collective-permute-start.12
  106.0 7.8 collective-permute-start.17
  110.5 6.2 collective-permute-start.16
  111.8 8.4 collective-permute-start.15
  122.5 371.5 %all-reduce.42.cloned.1.call-start = ((), (), s32[]{:S(2)}) async-start(), calls=%async_computation | async-start | bytes 8388608 | tf_op jit(solution)/shard_map/psum | solution.py:35
  340.0 386.8 %all-gather.8.cloned.1.call-start = ((), (), s32[]{:S(2)}) async-start(), calls=%async_computation.3 | async-start | bytes 1056768 | tf_op jit(solution)/shard_map/all_gather | solution.py:154
  495.8 5.2 collective-permute-start.20
  497.8 6.2 collective-permute-start.19
  499.1 8.4 collective-permute-start.18
  507.7 7.8 collective-permute-start.23
  512.2 6.2 collective-permute-start.22
  513.5 8.4 collective-permute-start.21
  543.1 13.6 %collective-permute-start.24 = (f32[1,4,4,64,128]{4,3,2,1,0:T(8,128)S(1)}, f32[1,4,4,64,128]{4,3,2,1,0:T(8,128)S(1)}, u32[]{:S(2)}, u32[]{:S(2)}) collective-permute-start(f32[1,4,4,64,128]{4,3,2,1,0:T(8,128)S(1)} %add.1076), channel_id=1, source_target_pairs={{0,4},{4,8},{8,12},{12,16},{16,20},{20,24},{24,28},{28,32},{32,36}... | collective-permute-start | bytes 1572872 | tf_op jit(solution)/shard_map/ppermute | solution.py:30
  545.1 7.1 collective-permute-start.26
  549.6 6.9 collective-permute-start.25
  557.3 12.6 %collective-permute-start.27 = (f32[1,4,4,64,128]{4,3,2,1,0:T(8,128)S(1)}, f32[1,4,4,64,128]{4,3,2,1,0:T(8,128)S(1)}, u32[]{:S(2)}, u32[]{:S(2)}) collective-permute-start(f32[1,4,4,64,128]{4,3,2,1,0:T(8,128)S(1)} %fusion.257), channel_id=1, source_target_pairs={{0,4},{4,8},{8,12},{12,16},{16,20},{20,24},{24,28},{28,32},{32,36}... | collective-permute-start | bytes 1572872 | tf_op jit(solution)/shard_map/ppermute | solution.py:30
  559.2 6.1 collective-permute-start.29
  562.8 6.9 collective-permute-start.28
  570.4 12.6 %collective-permute-start.30 = (f32[1,4,4,64,128]{4,3,2,1,0:T(8,128)S(1)}, f32[1,4,4,64,128]{4,3,2,1,0:T(8,128)S(1)}, u32[]{:S(2)}, u32[]{:S(2)}) collective-permute-start(f32[1,4,4,64,128]{4,3,2,1,0:T(8,128)S(1)} %fusion.243), channel_id=1, source_target_pairs={{0,4},{4,8},{8,12},{12,16},{16,20},{20,24},{24,28},{28,32},{32,36}... | collective-permute-start | bytes 1572872 | tf_op jit(solution)/shard_map/ppermute | solution.py:30
  572.4 6.1 collective-permute-start.32
  575.9 6.9 collective-permute-start.31
  583.6 12.6 %collective-permute-start.33 = (f32[1,4,4,64,128]{4,3,2,1,0:T(8,128)S(1)}, f32[1,4,4,64,128]{4,3,2,1,0:T(8,128)S(1)}, u32[]{:S(2)}, u32[]{:S(2)}) collective-permute-start(f32[1,4,4,64,128]{4,3,2,1,0:T(8,128)S(1)} %fusion.229), channel_id=1, source_target_pairs={{0,4},{4,8},{8,12},{12,16},{16,20},{20,24},{24,28},{28,32},{32,36}... | collective-permute-start | bytes 1572872 | tf_op jit(solution)/shard_map/ppermute | solution.py:30
  585.5 6.1 collective-permute-start.35
  589.1 6.9 collective-permute-start.34
  596.7 12.6 %collective-permute-start.36 = (f32[1,4,4,64,128]{4,3,2,1,0:T(8,128)S(1)}, f32[1,4,4,64,128]{4,3,2,1,0:T(8,128)S(1)}, u32[]{:S(2)}, u32[]{:S(2)}) collective-permute-start(f32[1,4,4,64,128]{4,3,2,1,0:T(8,128)S(1)} %fusion.215), channel_id=1, source_target_pairs={{0,4},{4,8},{8,12},{12,16},{16,20},{20,24},{24,28},{28,32},{32,36}... | collective-permute-start | bytes 1572872 | tf_op jit(solution)/shard_map/ppermute | solution.py:30
  598.7 6.1 collective-permute-start.38
  602.2 6.9 collective-permute-start.37
  631.6 2.3 copy-start.2
  634.0 6.8 collective-permute-start.41
  637.5 6.2 collective-permute-start.40
  638.8 8.4 collective-permute-start.39
  647.4 7.8 collective-permute-start.44
  652.0 6.2 collective-permute-start.43
  653.3 8.4 collective-permute-start.42
  664.0 367.4 %all-reduce.44.cloned.1.call-start = ((), (), s32[]{:S(2)}) async-start(), calls=%async_computation.1 | async-start | bytes 8388608 | tf_op jit(solution)/shard_map/psum | solution.py:35
  1033.2 5.2 collective-permute-start.47
  1035.2 6.2 collective-permute-start.46
  1036.5 8.4 collective-permute-start.45
  1045.0 7.8 collective-permute-start.50
  1049.6 6.2 collective-permute-start.49
  1050.9 8.4 collective-permute-start.48
  1080.5 13.6 %collective-permute-start.51 = (f32[1,4,4,64,128]{4,3,2,1,0:T(8,128)S(1)}, f32[1,4,4,64,128]{4,3,2,1,0:T(8,128)S(1)}, u32[]{:S(2)}, u32[]{:S(2)}) collective-permute-start(f32[1,4,4,64,128]{4,3,2,1,0:T(8,128)S(1)} %add.1121), channel_id=1, source_target_pairs={{0,4},{4,8},{8,12},{12,16},{16,20},{20,24},{24,28},{28,32},{32,36}... | collective-permute-start | bytes 1572872 | tf_op jit(solution)/shard_map/ppermute | solution.py:30
  1082.4 7.1 collective-permute-start.53
  1087.0 6.9 collective-permute-start.52
  1094.6 12.6 %collective-permute-start.54 = (f32[1,4,4,64,128]{4,3,2,1,0:T(8,128)S(1)}, f32[1,4,4,64,128]{4,3,2,1,0:T(8,128)S(1)}, u32[]{:S(2)}, u32[]{:S(2)}) collective-permute-start(f32[1,4,4,64,128]{4,3,2,1,0:T(8,128)S(1)} %fusion.189), channel_id=1, source_target_pairs={{0,4},{4,8},{8,12},{12,16},{16,20},{20,24},{24,28},{28,32},{32,36}... | collective-permute-start | bytes 1572872 | tf_op jit(solution)/shard_map/ppermute | solution.py:30
  1096.6 6.1 collective-permute-start.56
  1100.1 6.9 collective-permute-start.55
Sparse Core Ops, SparseCore 0:
  122.6 62.4 all-gather.5
  340.1 153.8 all-reduce.41
  664.1 62.6 all-gather.7
  878.7 152.6 all-reduce.43
where the time goes:
time: 1140 us; the launch traced here: 1120 us
  waiting for transfers between devices  470 us (41%)
  other arithmetic  240 us (21%)
  local copies, waits for them, and re-layouts  191 us (17%)
  starting transfers between devices  136 us (12%)
  blocking collectives  61 us (5%)
  between operations  14.5 us (1%)
    psum x2, waiting for transfers between devices, spread_2(): return lax.psum(jnp.where(mine, array, jnp.zeros_like(array)), axis)  307 us
    ppermute x19, starting transfers between devices, with_halo(): lax.ppermute(lax.slice_in_dim(block, block.shape[dim] - width, None, axis...  73.9 us
    broadcast_in_dim x64, other arithmetic, advance(): padded = jnp.pad(iterate[None], ((0, 0), (0, 0), (1, 1), (0, 0), (0, 0)))  63.8 us
    all_gather x2, waiting for transfers between devices, coarse_correction(): lax.all_gather(source_flat, ('tm', 'space'), axis=0, tiled=True)  62.6 us
    all_gather x1, blocking collectives, coarse_correction(): lax.all_gather(metric_flat, ('tm', 'space'), axis=0, tiled=True)  61 us
    ppermute x19, waiting for transfers between devices, with_halo(): lax.ppermute(lax.slice_in_dim(block, 0, width, axis=dim), axis, backward)  57.4 us
    mul x64, other arithmetic, advance(): target = source_now + 2.0 * metric_now[None] * earlier  49 us
    div x64, local copies, waits for them, and re-layouts, advance(): iterate = iterate + (target - applied) / diagonal_now  48.6 us
  transfers between devices with their start and end apart: 61, of which 35 were waited for; matrix products, arithmetic and copies ran while one was open for 4% of the time, Pallas kernels for 0%

commit v1 on v0

--- a/solution.py
+++ b/solution.py
@@ -28,11 +28,6 @@
     size = lax.axis_size(axis)
     pairs = [(i, i + by) for i in range(size) if 0 <= i + by < size]
     return lax.ppermute(array, axis, pairs)
-
-
-def spread_2(array, axis, root):
-    mine = lax.axis_index(axis) == root
-    return lax.psum(jnp.where(mine, array, jnp.zeros_like(array)), axis)
 
 
 def stencil_apply(padded, metric, earlier, spacing, pinned):
@@ -141,7 +136,7 @@
     return (whole_source, whole_metric)
 
 
-def coarse_correction(source, metric_two):
+def coarse_correction(source, metric_two, gathered):
     time_devs = lax.axis_size("tm")
     plane_devs = lax.axis_size("space")
     time_at = lax.axis_index("tm")
@@ -149,20 +144,22 @@
     local_dims = source.shape
     local_steps, components, planes, height_y, width_z = local_dims
     source_flat = source.reshape(1, -1)
-    metric_flat = metric_two.reshape(1, -1)
-    flat_source, flat_metric = (
-        lax.all_gather(source_flat, ("tm", "space"), axis=0, tiled=True),
-        lax.all_gather(metric_flat, ("tm", "space"), axis=0, tiled=True),
-    )
+    cut = source_flat.shape[1]
+    if "metric" in gathered:
+        flat_source = lax.all_gather(source_flat, ("tm", "space"), axis=0, tiled=True)
+        flat_metric = gathered["metric"]
+    else:
+        both = jnp.concatenate([source_flat, metric_two.reshape(1, -1)], axis=1)
+        flat_both = lax.all_gather(both, ("tm", "space"), axis=0, tiled=True)
+        flat_source = flat_both[:, :cut]
+        flat_metric = flat_both[:, cut:]
+        gathered["metric"] = flat_metric
     whole_source, whole_metric = assemble(
         flat_source, flat_metric, time_devs, plane_devs, local_dims
     )
     solved = coarse_solve(whole_source, whole_metric, 4.0)
-    owner = jnp.logical_and(time_at == 0, plane_at == 0)
-    solved = jnp.where(owner, solved, jnp.zeros_like(solved))
-    whole = spread_2(solved, ("tm", "space"), 0)
     return lax.dynamic_slice(
-        whole,
+        solved,
         (time_at * local_steps, 0, plane_at * planes, 0, 0),
         (local_steps, components, planes, height_y, width_z),
     )
@@ -174,6 +171,7 @@
     metric_two = restrict(metric_one)
     metrics = (metric, metric_one)
     pinned_levels = (pinned, None)
+    gathered = {}
 
     def cycle(depth, values, source):
         spacing = 2.0**depth
@@ -188,7 +186,7 @@
         residual = source - apply_local(values, metrics[depth], spacing, pinned_levels[depth])
         coarse_source = restrict(residual)
         if depth == 1:
-            correction = coarse_correction(coarse_source, metric_two)
+            correction = coarse_correction(coarse_source, metric_two, gathered)
         else:
             correction = cycle(1, jnp.zeros_like(coarse_source), coarse_source)
         values = values + prolong(correction)

time: 1140 us -> 816 us (0.72)
  waiting for transfers between devices: 470 us -> 226 us
  blocking collectives: 61 us -> 0 us
    psum x2 -> x0, waiting for transfers between devices: 307 us -> none  [spread_2(): return lax.psum(jnp.where(mine, array, jnp.zeros_like(array)), axis)]
    all_gather x0 -> x1, waiting for transfers between devices: none -> 62.6 us  [coarse_correction(): flat_both = lax.all_gather(both, ('tm', 'space'), axis=0, tiled=True)]
    all_gather x1 -> x0, blocking collectives: 61 us -> none  [coarse_correction(): lax.all_gather(metric_flat, ('tm', 'space'), axis=0, tiled=True)]
    all_gather x2 -> x1, waiting for transfers between devices: 62.6 us -> 62.1 us  [coarse_correction(): lax.all_gather(source_flat, ('tm', 'space'), axis=0, tiled=True)]
  transfers between devices with their start and end apart: 61 -> 59, of which waited for: 35 -> 34; matrix products, arithmetic and copies ran while one was open for 4% -> 6% of each run, Pallas kernels for 0% -> 0%
where the time goes in v1:
time: 816 us; the launch traced here: 803 us
  other arithmetic  229 us (28%)
  waiting for transfers between devices  226 us (28%)
  local copies, waits for them, and re-layouts  193 us (24%)
  starting transfers between devices  137 us (17%)
  between operations  14.6 us (2%)
    ppermute x19, starting transfers between devices, with_halo(): lax.ppermute(lax.slice_in_dim(block, block.shape[dim] - width, None, axis...  75 us
    broadcast_in_dim x64, other arithmetic, advance(): padded = jnp.pad(iterate[None], ((0, 0), (0, 0), (1, 1), (0, 0), (0, 0)))  63.8 us
    all_gather x1, waiting for transfers between devices, coarse_correction(): flat_both = lax.all_gather(both, ('tm', 'space'), axis=0, tiled=True)  62.6 us
    all_gather x1, waiting for transfers between devices, coarse_correction(): lax.all_gather(source_flat, ('tm', 'space'), axis=0, tiled=True)  62.1 us
    ppermute x19, waiting for transfers between devices, with_halo(): lax.ppermute(lax.slice_in_dim(block, 0, width, axis=dim), axis, backward)  56.6 us
    mul x64, other arithmetic, advance(): target = source_now + 2.0 * metric_now[None] * earlier  49 us
    div x64, local copies, waits for them, and re-layouts, advance(): iterate = iterate + (target - applied) / diagonal_now  48.6 us
    broadcast_in_dim x14, local copies, waits for them, and re-layouts, prolong(): jnp.broadcast_to(values.reshape(leading + (depth_x, 1, height_y, 1, width...  45.5 us
  transfers between devices with their start and end apart: 59, of which 34 were waited for; matrix products, arithmetic and copies ran while one was open for 6% of the time, Pallas kernels for 0%

profile of v1, /device:TPU:2, one launch (start us, length us, event | category | flops | bytes accessed | tf_op | source)
XLA Modules:
  0.0 802.5 jit_solution(11677441846512501886)
XLA Ops:
  8.0 4.6 collective-permute-start.2
  16.9 8.5 %collective-permute-done = f32[1,4,4,64,128]{4,3,2,1,0:T(8,128)S(1)} collective-permute-done((f32[1,4,4,64,128]{4,3,2,1,0:T(8,128)S(1)}, f32[1,4,4,64,128]{4,3,2,1,0:T(8,128)S(1)}, u32[]{:S(2)}, u32[]{:S(2)}) %collective-permute-start) | collective-permute-done | bytes 524320 | tf_op jit(solution)/shard_map/ppermute | solution.py:30
  27.8 3.8 collective-permute-start.5
  34.3 5.2 collective-permute-start.11
  39.4 9.8 %reshape.1434 = f32[2,2,32,2,64,2]{5,4,3,2,1,0:T(8,128)} reshape(f32[1,4,64,128]{3,2,1,0:T(8,128)S(1)} %copy-done.1) | data formatting | bytes 262144 | tf_op jit(solution)/shard_map/reshape | solution.py:80
  49.2 4.0 reduce_sum.61
  56.0 3.9 collective-permute-start.8
  63.3 3.5 collective-permute-done.7
  67.4 8.8 %copy.388 = f32[1,4,4,64,128]{1,4,3,2,0:T(8,128)} copy(f32[1,4,4,64,128]{4,3,2,1,0:T(8,128)S(1)} %fusion.269) | data formatting | bytes 1048576 | tf_op jit(solution)/shard_map/sub | solution.py:186
  76.2 13.0 %reduce_sum.60 = f32[4,2,32,64]{0,3,2,1:T(8,128)} reduce(f32[4,2,2,32,2,64,2]{0,6,5,4,3,2,1:T(2,128)} %bitcast.231, f32[]{:T(128)} %constant.217.clone.1), dimensions={2,4,6}, to_apply=%region_0.0 | reduce | flops 114688 | bytes 589828 | tf_op jit(solution)/shard_map/reduce_sum | solution.py:82
  89.3 2.3 copy.389
  92.4 3.8 collective-permute-start.14
  102.5 4.1 collective-permute-done.12
  106.8 4.5 collective-permute-start.17
  114.7 2.8 collective-permute-done.16
  117.6 3.5 collective-permute-done.15
  123.7 62.6 %all-gather.5.cloned.1.call-done = f32[128,1,2560]{2,1,0:T(1,128)} async-done(((f32[1,1,2560]{2,1,0:T(1,128)}), f32[128,1,2560]{2,1,0:T(1,128)}) %all-gather.5.cloned.1.call-update) | async-done | bytes 1310736 | tf_op jit(solution)/shard_map/all_gather | solution.py:153
  188.5 2.7 reshape.1435
  194.7 2.6 broadcast.1348.clone2
  197.3 139.5 %while.36 = (s32[]{:T(128)}, f32[4,4,16,32]{3,2,1,0:T(8,128)S(1)}, f32[32,4,4,16,32]{4,3,1,2,0:T(8,128)}, f32[32,4,4,16,32]{4,3,1,2,0:T(8,128)}, f32[32,4,16,32]...) while((s32[]{:T(128)}, f32[4,4,16,32]{3,2,1,0:T(8,128)S(1)}, ...), condition=%wide.region_7.8_spmd.clone, body=%wide.region_6.7_spmd.clone.sunk | while | flops 726035 | bytes 1315095 | solution.py:111
  338.6 2.6 collective-permute-start.20
  344.4 2.9 collective-permute-done.19
  347.5 3.4 collective-permute-done.18
  351.1 4.5 collective-permute-start.23
  358.9 2.9 collective-permute-done.22
  361.9 3.4 collective-permute-done.21
  367.5 8.9 %broadcast_in_dim.179 = f32[4,2,2,32,2,64,2]{0,6,5,4,3,2,1:T(2,128)} broadcast(f32[4,2,32,64]{0,3,2,1:T(8,128)} %copy.397), dimensions={0,1,3,5} | broadcast | bytes 589824 | tf_op jit(solution)/shard_map/broadcast_in_dim | solution.py:89
  376.4 10.0 %copy.398 = f32[1,4,4,64,128]{4,3,2,1,0:T(8,128)S(1)} copy(f32[1,4,4,64,128]{1,4,3,2,0:T(8,128)} %bitcast.232) | data formatting | bytes 1048576 | tf_op jit(solution)/shard_map/broadcast_in_dim | solution.py:89
  388.4 4.6 collective-permute-start.26
  395.5 4.4 collective-permute-done.25
  402.6 3.6 collective-permute-start.29
  408.7 4.4 collective-permute-done.28
  415.7 3.6 collective-permute-start.32
  421.8 4.4 collective-permute-done.31
  428.9 3.6 collective-permute-start.35
  434.9 4.4 collective-permute-done.34
  442.0 3.6 collective-permute-start.38
  448.1 4.4 collective-permute-done.37
  453.1 8.8 %copy.399 = f32[1,4,4,64,128]{1,4,3,2,0:T(8,128)} copy(f32[1,4,4,64,128]{4,3,2,1,0:T(8,128)S(1)} %fusion.201) | data formatting | bytes 1048576 | tf_op jit(solution)/shard_map/sub | solution.py:186
  461.9 13.0 %reduce_sum.83 = f32[4,2,32,64]{0,3,2,1:T(8,128)} reduce(f32[4,2,2,32,2,64,2]{0,6,5,4,3,2,1:T(2,128)} %bitcast.233, f32[]{:T(128)} %constant.217.clone.1), dimensions={2,4,6}, to_apply=%region_8.9 | reduce | flops 114688 | bytes 589828 | tf_op jit(solution)/shard_map/reduce_sum | solution.py:82
  475.0 2.3 copy.400
  477.3 3.6 collective-permute-start.41
  484.1 2.9 collective-permute-done.40
  487.2 3.4 collective-permute-done.39
  490.8 4.5 collective-permute-start.44
  498.6 2.9 collective-permute-done.43
  501.6 3.4 collective-permute-done.42
  507.4 62.1 %all-gather.7.cloned.1.call-done = f32[128,1,2048]{2,1,0:T(1,128)} async-done(((f32[1,1,2048]{2,1,0:T(1,128)}), f32[128,1,2048]{2,1,0:T(1,128)}) %all-gather.7.cloned.1.call-update) | async-done | bytes 1048592 | tf_op jit(solution)/shard_map/all_gather | solution.py:149
  569.4 3.7 reduce.14
  573.1 2.8 reshape.1438
  575.9 2.6 broadcast.1348.clone
  578.5 139.5 %while.37 = (s32[]{:T(128)}, f32[4,4,16,32]{3,2,1,0:T(8,128)S(1)}, f32[32,4,4,16,32]{4,3,1,2,0:T(8,128)}, f32[32,4,4,16,32]{4,3,1,2,0:T(8,128)}, f32[32,4,16,32]...) while((s32[]{:T(128)}, f32[4,4,16,32]{3,2,1,0:T(8,128)S(1)}, ...), condition=%wide.region_12.13_spmd.clone, body=%wide.region_11.12_spmd.clone.sunk | while | flops 726035 | bytes 1315095 | solution.py:111
  719.8 2.5 collective-permute-start.47
  725.5 2.9 collective-permute-done.46
  728.6 3.4 collective-permute-done.45
  732.2 4.5 collective-permute-start.50
  740.0 2.9 collective-permute-done.49
  743.0 3.4 collective-permute-done.48
  748.6 8.9 %broadcast_in_dim.186 = f32[4,2,2,32,2,64,2]{0,6,5,4,3,2,1:T(2,128)} broadcast(f32[4,2,32,64]{0,3,2,1:T(8,128)} %copy.408), dimensions={0,1,3,5} | broadcast | bytes 589824 | tf_op jit(solution)/shard_map/broadcast_in_dim | solution.py:89
  757.5 10.0 %copy.409 = f32[1,4,4,64,128]{4,3,2,1,0:T(8,128)S(1)} copy(f32[1,4,4,64,128]{1,4,3,2,0:T(8,128)} %bitcast.234) | data formatting | bytes 1048576 | tf_op jit(solution)/shard_map/broadcast_in_dim | solution.py:89
  769.5 4.6 collective-permute-start.53
  776.6 4.4 collective-permute-done.52
  783.7 3.6 collective-permute-start.56
  789.8 4.4 collective-permute-done.55
  (1334 shorter events, 379.7 us)
Async XLA Ops:
  6.5 10.1 %copy-start.1 = (f32[1,4,64,128]{3,2,1,0:T(8,128)S(1)}, f32[1,4,64,128]{3,2,1,0:T(8,128)}, u32[]{:S(2)}) copy-start(f32[1,4,64,128]{3,2,1,0:T(8,128)} %param.8) | copy-start | bytes 393220
  6.5 179.7 %all-gather.5.cloned.1.call-start = ((), (), s32[]{:S(2)}) async-start(), calls=%async_computation | async-start | bytes 1320960 | tf_op jit(solution)/shard_map/all_gather | solution.py:153
  6.6 10.1 %collective-permute-start.1 = (f32[1,4,1,64,128]{4,3,2,1,0:T(8,128)S(1)}, f32[1,4,1,64,128]{4,3,2,1,0:T(8,128)S(1)}, u32[]{:S(2)}, u32[]{:S(2)}) collective-permute-start(f32[1,4,1,64,128]{4,3,2,1,0:T(8,128)S(1)} %broadcast.1335), channel_id=1, source_target_pairs={{1,0},{2,1},{3,2},{5,4},{6,5},{7,6},{9,8},{10,9},{11,10},{13,12},{... | collective-permute-start | bytes 393224 | tf_op jit(solution)/shard_map/ppermute | solution.py:22
  8.0 8.7 %collective-permute-start.2 = (f32[1,4,1,64,128]{4,3,2,1,0:T(8,128)S(1)}, f32[1,4,1,64,128]{4,3,2,1,0:T(8,128)S(1)}, u32[]{:S(2)}, u32[]{:S(2)}) collective-permute-start(f32[1,4,1,64,128]{4,3,2,1,0:T(8,128)S(1)} %broadcast.1335), channel_id=1, source_target_pairs={{0,1},{1,2},{2,3},{4,5},{5,6},{6,7},{8,9},{9,10},{10,11},{12,13},{... | collective-permute-start | bytes 393224 | tf_op jit(solution)/shard_map/ppermute | solution.py:19
  12.6 12.8 %copy-start = (f32[1,4,4,64,128]{4,3,2,1,0:T(8,128)S(1)}, f32[1,4,4,64,128]{4,3,2,1,0:T(8,128)}, u32[]{:S(2)}) copy-start(f32[1,4,4,64,128]{4,3,2,1,0:T(8,128)} %param.7) | copy-start | bytes 1572868
  12.6 12.7 %collective-permute-start = (f32[1,4,4,64,128]{4,3,2,1,0:T(8,128)S(1)}, f32[1,4,4,64,128]{4,3,2,1,0:T(8,128)S(1)}, u32[]{:S(2)}, u32[]{:S(2)}) collective-permute-start(f32[1,4,4,64,128]{4,3,2,1,0:T(8,128)S(1)} %broadcast.1333), channel_id=1, source_target_pairs={{0,4},{4,8},{8,12},{12,16},{16,20},{20,24},{24,28},{28,32},{32,36}... | collective-permute-start | bytes 1572872 | tf_op jit(solution)/shard_map/ppermute | solution.py:30
  25.9 27.6 %collective-permute-start.3 = (f32[1,4,4,64,128]{4,3,2,1,0:T(8,128)S(1)}, f32[1,4,4,64,128]{4,3,2,1,0:T(8,128)S(1)}, u32[]{:S(2)}, u32[]{:S(2)}) collective-permute-start(f32[1,4,4,64,128]{4,3,2,1,0:T(8,128)S(1)} %get-tuple-element.465), channel_id=1, source_target_pairs={{0,4},{4,8},{8,12},{12,16},{16,20},{20,24},{24,28},{28,32},{32,36}... | collective-permute-start | bytes 1572872 | tf_op jit(solution)/shard_map/ppermute | solution.py:30
  27.8 25.5 %collective-permute-start.5 = (f32[1,4,1,64,128]{4,3,2,1,0:T(8,128)S(1)}, f32[1,4,1,64,128]{4,3,2,1,0:T(8,128)S(1)}, u32[]{:S(2)}, u32[]{:S(2)}) collective-permute-start(f32[1,4,1,64,128]{4,3,2,1,0:T(8,128)S(1)} %get-tuple-element.568), channel_id=1, source_target_pairs={{0,1},{1,2},{2,3},{4,5},{5,6},{6,7},{8,9},{9,10},{10,11},{12,13},{... | collective-permute-start | bytes 393224 | tf_op jit(solution)/shard_map/ppermute | solution.py:19
  31.6 21.6 %collective-permute-start.4 = (f32[1,4,1,64,128]{4,3,2,1,0:T(8,128)S(1)}, f32[1,4,1,64,128]{4,3,2,1,0:T(8,128)S(1)}, u32[]{:S(2)}, u32[]{:S(2)}) collective-permute-start(f32[1,4,1,64,128]{4,3,2,1,0:T(8,128)S(1)} %get-tuple-element.567), channel_id=1, source_target_pairs={{1,0},{2,1},{3,2},{5,4},{6,5},{7,6},{9,8},{10,9},{11,10},{13,12},{... | collective-permute-start | bytes 393224 | tf_op jit(solution)/shard_map/ppermute | solution.py:22
  33.0 28.3 %collective-permute-start.10 = (f32[1,4,1,32,64]{4,3,2,1,0:T(8,128)S(1)}, f32[1,4,1,32,64]{4,3,2,1,0:T(8,128)S(1)}, u32[]{:S(2)}, u32[]{:S(2)}) collective-permute-start(f32[1,4,1,32,64]{4,3,2,1,0:T(8,128)S(1)} %broadcast.1342), channel_id=1, source_target_pairs={{1,0},{2,1},{3,2},{5,4},{6,5},{7,6},{9,8},{10,9},{11,10},{13,12},{... | collective-permute-start | bytes 98312 | tf_op jit(solution)/shard_map/ppermute | solution.py:22
  34.3 28.9 %collective-permute-start.11 = (f32[1,4,1,32,64]{4,3,2,1,0:T(8,128)S(1)}, f32[1,4,1,32,64]{4,3,2,1,0:T(8,128)S(1)}, u32[]{:S(2)}, u32[]{:S(2)}) collective-permute-start(f32[1,4,1,32,64]{4,3,2,1,0:T(8,128)S(1)} %broadcast.1342), channel_id=1, source_target_pairs={{0,1},{1,2},{2,3},{4,5},{5,6},{6,7},{8,9},{9,10},{10,11},{12,13},{... | collective-permute-start | bytes 98312 | tf_op jit(solution)/shard_map/ppermute | solution.py:19
  54.0 13.0 %collective-permute-start.6 = (f32[1,4,4,64,128]{4,3,2,1,0:T(8,128)S(1)}, f32[1,4,4,64,128]{4,3,2,1,0:T(8,128)S(1)}, u32[]{:S(2)}, u32[]{:S(2)}) collective-permute-start(f32[1,4,4,64,128]{4,3,2,1,0:T(8,128)S(1)} %fusion.283), channel_id=1, source_target_pairs={{0,4},{4,8},{8,12},{12,16},{16,20},{20,24},{24,28},{28,32},{32,36}... | collective-permute-start | bytes 1572872 | tf_op jit(solution)/shard_map/ppermute | solution.py:30
  56.0 7.3 collective-permute-start.8
  59.9 6.9 collective-permute-start.7
  61.3 30.3 %collective-permute-start.9 = (f32[1,4,2,32,64]{4,3,2,1,0:T(8,128)S(1)}, f32[1,4,2,32,64]{4,3,2,1,0:T(8,128)S(1)}, u32[]{:S(2)}, u32[]{:S(2)}) collective-permute-start(f32[1,4,2,32,64]{4,3,2,1,0:T(8,128)S(1)} %broadcast.1341), channel_id=1, source_target_pairs={{0,4},{4,8},{8,12},{12,16},{16,20},{20,24},{24,28},{28,32},{32,36}... | collective-permute-start | bytes 196616 | tf_op jit(solution)/shard_map/ppermute | solution.py:30
  92.4 7.7 collective-permute-start.14
  96.2 6.2 collective-permute-start.13
  98.2 8.4 %collective-permute-start.12 = (f32[1,4,2,32,64]{4,3,2,1,0:T(8,128)S(1)}, f32[1,4,2,32,64]{4,3,2,1,0:T(8,128)S(1)}, u32[]{:S(2)}, u32[]{:S(2)}) collective-permute-start(f32[1,4,2,32,64]{4,3,2,1,0:T(8,128)S(1)} %get-tuple-element.463), channel_id=1, source_target_pairs={{0,4},{4,8},{8,12},{12,16},{16,20},{20,24},{24,28},{28,32},{32,36}... | collective-permute-start | bytes 196616 | tf_op jit(solution)/shard_map/ppermute | solution.py:30
  106.8 7.9 collective-permute-start.17
  111.3 6.2 collective-permute-start.16
  112.7 8.4 %collective-permute-start.15 = (f32[1,4,2,32,64]{4,3,2,1,0:T(8,128)S(1)}, f32[1,4,2,32,64]{4,3,2,1,0:T(8,128)S(1)}, u32[]{:S(2)}, u32[]{:S(2)}) collective-permute-start(f32[1,4,2,32,64]{4,3,2,1,0:T(8,128)S(1)} %fusion.419), channel_id=1, source_target_pairs={{0,4},{4,8},{8,12},{12,16},{16,20},{20,24},{24,28},{28,32},{32,36}... | collective-permute-start | bytes 196616 | tf_op jit(solution)/shard_map/ppermute | solution.py:30
  123.4 446.0 %all-gather.7.cloned.1.call-start = ((), (), s32[]{:S(2)}) async-start(), calls=%async_computation.1 | async-start | bytes 1056768 | tf_op jit(solution)/shard_map/all_gather | solution.py:149
  338.6 5.8 collective-permute-start.20
  341.2 6.2 collective-permute-start.19
  342.5 8.4 %collective-permute-start.18 = (f32[1,4,2,32,64]{4,3,2,1,0:T(8,128)S(1)}, f32[1,4,2,32,64]{4,3,2,1,0:T(8,128)S(1)}, u32[]{:S(2)}, u32[]{:S(2)}) collective-permute-start(f32[1,4,2,32,64]{4,3,2,1,0:T(8,128)S(1)} %broadcast_add_fusion.1), channel_id=1, source_target_pairs={{0,4},{4,8},{8,12},{12,16},{16,20},{20,24},{24,28},{28,32},{32,36}... | collective-permute-start | bytes 196616 | tf_op jit(solution)/shard_map/ppermute | solution.py:30
  351.1 7.8 collective-permute-start.23
  355.6 6.2 collective-permute-start.22
  356.9 8.4 %collective-permute-start.21 = (f32[1,4,2,32,64]{4,3,2,1,0:T(8,128)S(1)}, f32[1,4,2,32,64]{4,3,2,1,0:T(8,128)S(1)}, u32[]{:S(2)}, u32[]{:S(2)}) collective-permute-start(f32[1,4,2,32,64]{4,3,2,1,0:T(8,128)S(1)} %fusion.391), channel_id=1, source_target_pairs={{0,4},{4,8},{8,12},{12,16},{16,20},{20,24},{24,28},{28,32},{32,36}... | collective-permute-start | bytes 196616 | tf_op jit(solution)/shard_map/ppermute | solution.py:30
  386.5 13.6 %collective-permute-start.24 = (f32[1,4,4,64,128]{4,3,2,1,0:T(8,128)S(1)}, f32[1,4,4,64,128]{4,3,2,1,0:T(8,128)S(1)}, u32[]{:S(2)}, u32[]{:S(2)}) collective-permute-start(f32[1,4,4,64,128]{4,3,2,1,0:T(8,128)S(1)} %add.1067), channel_id=1, source_target_pairs={{0,4},{4,8},{8,12},{12,16},{16,20},{20,24},{24,28},{28,32},{32,36}... | collective-permute-start | bytes 1572872 | tf_op jit(solution)/shard_map/ppermute | solution.py:30
  388.4 7.1 collective-permute-start.26
  393.0 6.9 collective-permute-start.25
  400.6 12.6 %collective-permute-start.27 = (f32[1,4,4,64,128]{4,3,2,1,0:T(8,128)S(1)}, f32[1,4,4,64,128]{4,3,2,1,0:T(8,128)S(1)}, u32[]{:S(2)}, u32[]{:S(2)}) collective-permute-start(f32[1,4,4,64,128]{4,3,2,1,0:T(8,128)S(1)} %fusion.257), channel_id=1, source_target_pairs={{0,4},{4,8},{8,12},{12,16},{16,20},{20,24},{24,28},{28,32},{32,36}... | collective-permute-start | bytes 1572872 | tf_op jit(solution)/shard_map/ppermute | solution.py:30
  402.6 6.1 collective-permute-start.29
  406.2 6.9 collective-permute-start.28
  413.8 12.6 %collective-permute-start.30 = (f32[1,4,4,64,128]{4,3,2,1,0:T(8,128)S(1)}, f32[1,4,4,64,128]{4,3,2,1,0:T(8,128)S(1)}, u32[]{:S(2)}, u32[]{:S(2)}) collective-permute-start(f32[1,4,4,64,128]{4,3,2,1,0:T(8,128)S(1)} %fusion.243), channel_id=1, source_target_pairs={{0,4},{4,8},{8,12},{12,16},{16,20},{20,24},{24,28},{28,32},{32,36}... | collective-permute-start | bytes 1572872 | tf_op jit(solution)/shard_map/ppermute | solution.py:30
  415.7 6.1 collective-permute-start.32
  419.3 6.9 collective-permute-start.31
  426.9 12.6 %collective-permute-start.33 = (f32[1,4,4,64,128]{4,3,2,1,0:T(8,128)S(1)}, f32[1,4,4,64,128]{4,3,2,1,0:T(8,128)S(1)}, u32[]{:S(2)}, u32[]{:S(2)}) collective-permute-start(f32[1,4,4,64,128]{4,3,2,1,0:T(8,128)S(1)} %fusion.229), channel_id=1, source_target_pairs={{0,4},{4,8},{8,12},{12,16},{16,20},{20,24},{24,28},{28,32},{32,36}... | collective-permute-start | bytes 1572872 | tf_op jit(solution)/shard_map/ppermute | solution.py:30
  428.9 6.1 collective-permute-start.35
  432.4 6.9 collective-permute-start.34
  440.1 12.6 %collective-permute-start.36 = (f32[1,4,4,64,128]{4,3,2,1,0:T(8,128)S(1)}, f32[1,4,4,64,128]{4,3,2,1,0:T(8,128)S(1)}, u32[]{:S(2)}, u32[]{:S(2)}) collective-permute-start(f32[1,4,4,64,128]{4,3,2,1,0:T(8,128)S(1)} %fusion.215), channel_id=1, source_target_pairs={{0,4},{4,8},{8,12},{12,16},{16,20},{20,24},{24,28},{28,32},{32,36}... | collective-permute-start | bytes 1572872 | tf_op jit(solution)/shard_map/ppermute | solution.py:30
  442.0 6.1 collective-permute-start.38
  445.6 6.9 collective-permute-start.37
  475.0 2.3 copy-start.2
  477.3 6.8 collective-permute-start.41
  480.9 6.2 collective-permute-start.40
  482.2 8.4 %collective-permute-start.39 = (f32[1,4,2,32,64]{4,3,2,1,0:T(8,128)S(1)}, f32[1,4,2,32,64]{4,3,2,1,0:T(8,128)S(1)}, u32[]{:S(2)}, u32[]{:S(2)}) collective-permute-start(f32[1,4,2,32,64]{4,3,2,1,0:T(8,128)S(1)} %fusion.561), channel_id=1, source_target_pairs={{0,4},{4,8},{8,12},{12,16},{16,20},{20,24},{24,28},{28,32},{32,36}... | collective-permute-start | bytes 196616 | tf_op jit(solution)/shard_map/ppermute | solution.py:30
  490.8 7.8 collective-permute-start.44
  495.3 6.2 collective-permute-start.43
  496.6 8.4 %collective-permute-start.42 = (f32[1,4,2,32,64]{4,3,2,1,0:T(8,128)S(1)}, f32[1,4,2,32,64]{4,3,2,1,0:T(8,128)S(1)}, u32[]{:S(2)}, u32[]{:S(2)}) collective-permute-start(f32[1,4,2,32,64]{4,3,2,1,0:T(8,128)S(1)} %fusion.361), channel_id=1, source_target_pairs={{0,4},{4,8},{8,12},{12,16},{16,20},{20,24},{24,28},{28,32},{32,36}... | collective-permute-start | bytes 196616 | tf_op jit(solution)/shard_map/ppermute | solution.py:30
  719.8 5.7 collective-permute-start.47
  722.3 6.2 collective-permute-start.46
  723.6 8.4 %collective-permute-start.45 = (f32[1,4,2,32,64]{4,3,2,1,0:T(8,128)S(1)}, f32[1,4,2,32,64]{4,3,2,1,0:T(8,128)S(1)}, u32[]{:S(2)}, u32[]{:S(2)}) collective-permute-start(f32[1,4,2,32,64]{4,3,2,1,0:T(8,128)S(1)} %broadcast_add_fusion), channel_id=1, source_target_pairs={{0,4},{4,8},{8,12},{12,16},{16,20},{20,24},{24,28},{28,32},{32,36}... | collective-permute-start | bytes 196616 | tf_op jit(solution)/shard_map/ppermute | solution.py:30
  732.2 7.8 collective-permute-start.50
  736.7 6.2 collective-permute-start.49
  738.0 8.4 %collective-permute-start.48 = (f32[1,4,2,32,64]{4,3,2,1,0:T(8,128)S(1)}, f32[1,4,2,32,64]{4,3,2,1,0:T(8,128)S(1)}, u32[]{:S(2)}, u32[]{:S(2)}) collective-permute-start(f32[1,4,2,32,64]{4,3,2,1,0:T(8,128)S(1)} %fusion.333), channel_id=1, source_target_pairs={{0,4},{4,8},{8,12},{12,16},{16,20},{20,24},{24,28},{28,32},{32,36}... | collective-permute-start | bytes 196616 | tf_op jit(solution)/shard_map/ppermute | solution.py:30
  767.6 13.6 %collective-permute-start.51 = (f32[1,4,4,64,128]{4,3,2,1,0:T(8,128)S(1)}, f32[1,4,4,64,128]{4,3,2,1,0:T(8,128)S(1)}, u32[]{:S(2)}, u32[]{:S(2)}) collective-permute-start(f32[1,4,4,64,128]{4,3,2,1,0:T(8,128)S(1)} %add.1112), channel_id=1, source_target_pairs={{0,4},{4,8},{8,12},{12,16},{16,20},{20,24},{24,28},{28,32},{32,36}... | collective-permute-start | bytes 1572872 | tf_op jit(solution)/shard_map/ppermute | solution.py:30
  769.5 7.1 collective-permute-start.53
  774.1 6.9 collective-permute-start.52
  781.7 12.6 %collective-permute-start.54 = (f32[1,4,4,64,128]{4,3,2,1,0:T(8,128)S(1)}, f32[1,4,4,64,128]{4,3,2,1,0:T(8,128)S(1)}, u32[]{:S(2)}, u32[]{:S(2)}) collective-permute-start(f32[1,4,4,64,128]{4,3,2,1,0:T(8,128)S(1)} %fusion.189), channel_id=1, source_target_pairs={{0,4},{4,8},{8,12},{12,16},{16,20},{20,24},{24,28},{28,32},{32,36}... | collective-permute-start | bytes 1572872 | tf_op jit(solution)/shard_map/ppermute | solution.py:30
  783.7 6.1 collective-permute-start.56
  787.3 6.9 collective-permute-start.55
Sparse Core Ops, SparseCore 0:
  123.6 62.6 all-gather.4
  507.5 61.9 all-gather.6

commit v2 on v1

--- a/solution.py
+++ b/solution.py
@@ -1,6 +1,10 @@
+import functools
+
 import jax
 import jax.numpy as jnp
 from jax import lax
+from jax.experimental import pallas as pl
+from jax.experimental.pallas import tpu as pltpu
 from jax.sharding import PartitionSpec as P
 
 CYCLES = 2
@@ -93,23 +97,67 @@
     return spread.reshape(leading + (2 * depth_x, 2 * height_y, 2 * width_z))
 
 
+def coarse_kernel(src_ref, met_ref, out_ref, *, spacing, depth_x, height_y, width_z):
+    steps, rows, lanes = src_ref.shape
+    inverse_square = 1.0 / (spacing * spacing)
+    half_inverse = 0.5 / spacing
+    row = lax.broadcasted_iota(jnp.int32, (rows, lanes), 0)
+    lane = lax.broadcasted_iota(jnp.int32, (rows, lanes), 1)
+    plane = row % depth_x
+    part = row // depth_x
+    across_z = lane % width_z
+    across_y = lane // width_z
+    quarter = rows // 4
+    zero = jnp.zeros((rows, lanes), jnp.float32)
+
+    def shifted(v, shift, axis, edge):
+        size = v.shape[axis]
+        return jnp.where(edge, zero, pltpu.roll(v, shift % size, axis))
+
+    def apply(v, two_g):
+        ahead_x = shifted(v, -1, 0, plane == depth_x - 1)
+        behind_x = shifted(v, 1, 0, plane == 0)
+        ahead_y = shifted(v, -width_z, 1, across_y == height_y - 1)
+        behind_y = shifted(v, width_z, 1, across_y == 0)
+        ahead_z = shifted(v, -1, 1, across_z == width_z - 1)
+        behind_z = shifted(v, 1, 1, across_z == 0)
+        laplace = (6.0 * v - ahead_x - behind_x - ahead_y - behind_y - ahead_z - behind_z) * inverse_square
+        diff_x = ahead_x - behind_x
+        diff_y = ahead_y - behind_y
+        diff_z = ahead_z - behind_z
+        grad_x = pltpu.roll(diff_x, quarter, 0)
+        grad_y = pltpu.roll(diff_y, 2 * quarter, 0)
+        grad_z = pltpu.roll(diff_z, 3 * quarter, 0)
+        divergence = pltpu.roll(diff_x, 3 * quarter, 0) + pltpu.roll(diff_y, 2 * quarter, 0) + pltpu.roll(diff_z, quarter, 0)
+        coupling = jnp.where(part == 0, grad_x, jnp.where(part == 1, grad_y, jnp.where(part == 2, grad_z, divergence))) * half_inverse
+        return two_g * v + laplace + coupling
+
+    def advance(t, earlier):
+        g = met_ref[t]
+        two_g = 2.0 * g
+        diagonal = two_g + 6.0 / (spacing * spacing)
+        target = src_ref[t] + two_g * earlier
+        v = zero
+        for repeat in range(COARSE_SWEEPS):
+            v = v + (target - apply(v, two_g)) / diagonal
+        out_ref[t] = v
+        return v
+
+    lax.fori_loop(0, steps, advance, zero)
+
+
 def coarse_solve(source, metric, spacing):
-    diagonal = 2.0 * metric[:, None] + 6.0 / (spacing * spacing)
-
-    def advance(earlier, inputs):
-        source_now, metric_now, diagonal_now = inputs
-        target = source_now + 2.0 * metric_now[None] * earlier
-        iterate = jnp.zeros_like(source_now)
-        nothing = jnp.zeros_like(source_now)[None]
-        for repeat in range(COARSE_SWEEPS):
-            padded = jnp.pad(iterate[None], ((0, 0), (0, 0), (1, 1), (0, 0), (0, 0)))
-            applied = stencil_apply(padded, metric_now[None], nothing, spacing, None)[0]
-            iterate = iterate + (target - applied) / diagonal_now
-        return (iterate, iterate)
-
-    initial = jnp.zeros_like(source[0])
-    final_state, history = lax.scan(advance, initial, (source, metric, diagonal))
-    return history
+    steps, components, depth_x, height_y, width_z = source.shape
+    rows = components * depth_x
+    lanes = height_y * width_z
+    flat_source = source.reshape(steps, rows, lanes)
+    flat_metric = jnp.tile(metric.reshape(steps, depth_x, lanes), (1, components, 1))
+    kernel = functools.partial(coarse_kernel, spacing=spacing, depth_x=depth_x, height_y=height_y, width_z=width_z)
+    solved = pl.pallas_call(
+        kernel,
+        out_shape=jax.ShapeDtypeStruct(flat_source.shape, jnp.float32),
+    )(flat_source, flat_metric)
+    return solved.reshape(source.shape)
 
 
 def apply_local(values, metric, spacing, pinned):

time: 816 us -> 577 us (0.71); the launches traced: 803 us -> 575 us
  other arithmetic: 229 us -> 53.5 us
  local copies, waits for them, and re-layouts: 193 us -> 113 us
  Pallas kernels: 0 us -> 32.2 us
  waiting for transfers between devices: 226 us -> 213 us
  starting transfers between devices: 137 us -> 148 us
    broadcast_in_dim x64 -> x0, other arithmetic: 63.8 us -> none  [advance(): padded = jnp.pad(iterate[None], ((0, 0), (0, 0), (1, 1), (0, 0), (0, 0)))]
    mul x128 -> x0, other arithmetic: 53.9 us -> none  [the longest x64 49 us: advance(): target = source_now + 2.0 * metric_now[None] * earlier]
    div x64 -> x0, local copies, waits for them, and re-layouts: 48.6 us -> none  [advance(): iterate = iterate + (target - applied) / diagonal_now]
    ppermute x19, waiting for transfers between devices: 56.6 us -> 8.45 us  [with_halo(): lax.ppermute(lax.slice_in_dim(block, 0, width, axis=dim), axis, backward)]
    dynamic_update_slice x64 -> x0, local copies, waits for them, and re-layouts: 42.5 us -> none  [coarse_solve(): lax.scan(advance, initial, (source, metric, diagonal))]
    ppermute x19, waiting for transfers between devices: 36.8 us -> 71.9 us  [from_behind(): return lax.ppermute(array, axis, pairs)]
    pallas_call x0 -> x2, Pallas kernels: none -> 32.2 us  [coarse_solve(): pl.pallas_call(kernel, out_shape=jax.ShapeDtypeStruct(flat_source.shape,...]
    add x193 -> x0, other arithmetic: 31.8 us -> none  [the longest x192 31 us: advance(): iterate = iterate + (target - applied) / diagonal_now]
  transfers between devices with their start and end apart: 59 -> 59, of which waited for: 34 -> 33; matrix products, arithmetic and copies ran while one was open for 6% -> 8% of each run, Pallas kernels for 0% -> 0%
where the time goes in v2:
time: 577 us; the launch traced here: 575 us
  waiting for transfers between devices  213 us (37%)
  starting transfers between devices  148 us (26%)
  local copies, waits for them, and re-layouts  113 us (20%)
  other arithmetic  53.5 us (9%)
  Pallas kernels  32.2 us (6%)
  between operations  14.6 us (3%)
    ppermute x19, starting transfers between devices, with_halo(): lax.ppermute(lax.slice_in_dim(block, block.shape[dim] - width, None, axis...  86.7 us
    ppermute x19, waiting for transfers between devices, from_behind(): return lax.ppermute(array, axis, pairs)  71.9 us
    all_gather x1, waiting for transfers between devices, coarse_correction(): flat_both = lax.all_gather(both, ('tm', 'space'), axis=0, tiled=True)  62.2 us
    all_gather x1, waiting for transfers between devices, coarse_correction(): lax.all_gather(source_flat, ('tm', 'space'), axis=0, tiled=True)  59.8 us
    broadcast_in_dim x14, local copies, waits for them, and re-layouts, prolong(): jnp.broadcast_to(values.reshape(leading + (depth_x, 1, height_y, 1, width...  42.5 us
    ppermute x19, starting transfers between devices, from_behind(): return lax.ppermute(array, axis, pairs)  36.9 us
    pallas_call x2, Pallas kernels, coarse_solve(): pl.pallas_call(kernel, out_shape=jax.ShapeDtypeStruct(flat_source.shape,...  32.2 us
    reduce_sum x9, other arithmetic, restrict(): return jnp.sum(blocks, axis=(offset + 1, offset + 3, offset + 5)) * 0.125  30.2 us
  transfers between devices with their start and end apart: 59, of which 33 were waited for; matrix products, arithmetic and copies ran while one was open for 8% of the time, Pallas kernels for 0%

profile of v2, /device:TPU:2, one launch (start us, length us, event | category | flops | bytes accessed | tf_op | source)
XLA Modules:
  0.0 574.5 jit_solution(7398267916582283987)
XLA Ops:
  6.6 4.0 collective-permute-start.2
  11.9 2.1 collective-permute-start
  17.8 6.9 %collective-permute-done = f32[1,4,4,64,128]{4,3,2,1,0:T(8,128)S(1)} collective-permute-done((f32[1,4,4,64,128]{4,3,2,1,0:T(8,128)S(1)}, f32[1,4,4,64,128]{4,3,2,1,0:T(8,128)S(1)}, u32[]{:S(2)}, u32[]{:S(2)}) %collective-permute-start) | collective-permute-done | bytes 524320 | tf_op jit(solution)/shard_map/ppermute | solution.py:34
  28.4 5.2 collective-permute-start.5
  33.6 3.9 collective-permute-start.11
  38.8 9.8 %reshape.946 = f32[2,2,32,2,64,2]{5,4,3,2,1,0:T(8,128)} reshape(f32[1,4,64,128]{3,2,1,0:T(8,128)S(1)} %copy-done.7) | data formatting | bytes 262144 | tf_op jit(solution)/shard_map/reshape | solution.py:84
  48.6 4.0 reduce_sum.61
  53.4 1.9 collective-permute-start.6
  56.7 5.2 collective-permute-start.8
  67.5 8.8 %copy.380 = f32[1,4,4,64,128]{1,4,3,2,0:T(8,128)} copy(f32[1,4,4,64,128]{4,3,2,1,0:T(8,128)S(1)} %fusion.105) | data formatting | bytes 1048576 | tf_op jit(solution)/shard_map/sub | solution.py:234
  76.3 11.7 %reduce_sum.60 = f32[4,2,32,64]{0,3,2,1:T(8,128)S(1)} reduce(f32[4,2,2,32,2,64,2]{0,6,5,4,3,2,1:T(2,128)} %bitcast.70, f32[]{:T(128)} %constant.18.clone.1), dimensions={2,4,6}, to_apply=%region_0.0 | reduce | flops 114688 | bytes 589828 | tf_op jit(solution)/shard_map/reduce_sum | solution.py:86
  89.4 2.2 fusion.399
  92.9 4.5 collective-permute-start.14
  98.1 1.9 collective-permute-start.12
  100.2 6.3 %collective-permute-done.12 = f32[1,4,2,32,64]{4,3,2,1,0:T(8,128)S(1)} collective-permute-done((f32[1,4,2,32,64]{4,3,2,1,0:T(8,128)S(1)}, f32[1,4,2,32,64]{4,3,2,1,0:T(8,128)S(1)}, u32[]{:S(2)}, u32[]{:S(2)}) %collective-permute-start.12) | collective-permute-done | bytes 65568 | tf_op jit(solution)/shard_map/ppermute | solution.py:34
  108.0 4.5 collective-permute-start.17
  114.7 6.3 %collective-permute-done.15 = f32[1,4,2,32,64]{4,3,2,1,0:T(8,128)S(1)} collective-permute-done((f32[1,4,2,32,64]{4,3,2,1,0:T(8,128)S(1)}, f32[1,4,2,32,64]{4,3,2,1,0:T(8,128)S(1)}, u32[]{:S(2)}, u32[]{:S(2)}) %collective-permute-start.15) | collective-permute-done | bytes 65568 | tf_op jit(solution)/shard_map/ppermute | solution.py:34
  123.6 62.2 %all-gather.5.cloned.1.call-done = f32[128,1,2560]{2,1,0:T(1,128)} async-done(((f32[1,1,2560]{2,1,0:T(1,128)}), f32[128,1,2560]{2,1,0:T(1,128)}) %all-gather.5.cloned.1.call-update) | async-done | bytes 1310736 | tf_op jit(solution)/shard_map/all_gather | solution.py:201
  188.5 2.6 tile.16.met_ref
  191.1 2.8 reshape.947
  193.9 4.8 copy.384
  198.7 4.4 reshape_reshape.6.src_ref
  203.1 16.1 %shard_map.37 = f32[32,16,512]{2,1,0:T(8,128)} custom-call(f32[32,16,512]{2,1,0:T(8,128)} %reshape_reshape.6.src_ref, f32[32,16,512]{2,1,0:T(8,128)} %tile.16.met_ref), custom_call_target="tpu_custom_call" | custom-call | tf_op jit(solution)/shard_map/pallas_call | solution.py:156
  219.2 3.8 reshape.948
  226.1 4.5 collective-permute-start.20
  232.7 6.3 %collective-permute-done.18 = f32[1,4,2,32,64]{4,3,2,1,0:T(8,128)S(1)} collective-permute-done((f32[1,4,2,32,64]{4,3,2,1,0:T(8,128)S(1)}, f32[1,4,2,32,64]{4,3,2,1,0:T(8,128)S(1)}, u32[]{:S(2)}, u32[]{:S(2)}) %collective-permute-start.18) | collective-permute-done | bytes 65568 | tf_op jit(solution)/shard_map/ppermute | solution.py:34
  240.5 4.5 collective-permute-start.23
  247.2 6.3 %collective-permute-done.21 = f32[1,4,2,32,64]{4,3,2,1,0:T(8,128)S(1)} collective-permute-done((f32[1,4,2,32,64]{4,3,2,1,0:T(8,128)S(1)}, f32[1,4,2,32,64]{4,3,2,1,0:T(8,128)S(1)}, u32[]{:S(2)}, u32[]{:S(2)}) %collective-permute-start.21) | collective-permute-done | bytes 65568 | tf_op jit(solution)/shard_map/ppermute | solution.py:34
  255.9 7.9 %broadcast_in_dim.88 = f32[4,2,2,32,2,64,2]{0,6,5,4,3,2,1:T(2,128)} broadcast(f32[4,2,32,64]{0,3,2,1:T(8,128)S(1)} %copy.388), dimensions={0,1,3,5} | broadcast | bytes 589824 | tf_op jit(solution)/shard_map/broadcast_in_dim | solution.py:93
  263.8 10.0 %copy.389 = f32[1,4,4,64,128]{4,3,2,1,0:T(8,128)S(1)} copy(f32[1,4,4,64,128]{1,4,3,2,0:T(8,128)} %bitcast.71) | data formatting | bytes 1048576 | tf_op jit(solution)/shard_map/broadcast_in_dim | solution.py:93
  277.1 4.6 collective-permute-start.26
  284.4 2.1 collective-permute-done.24
  290.3 4.6 collective-permute-start.29
  297.5 2.1 collective-permute-done.27
  303.4 4.6 collective-permute-start.32
  310.7 2.1 collective-permute-done.30
  316.6 4.6 collective-permute-start.35
  323.9 2.1 collective-permute-done.33
  329.8 4.8 collective-permute-start.38
  337.0 2.1 collective-permute-done.36
  339.6 8.8 %copy.390 = f32[1,4,4,64,128]{1,4,3,2,0:T(8,128)} copy(f32[1,4,4,64,128]{4,3,2,1,0:T(8,128)S(1)} %fusion.37) | data formatting | bytes 1048576 | tf_op jit(solution)/shard_map/sub | solution.py:234
  348.4 11.7 %reduce_sum.83 = f32[4,2,32,64]{0,3,2,1:T(8,128)S(1)} reduce(f32[4,2,2,32,2,64,2]{0,6,5,4,3,2,1:T(2,128)} %bitcast.72, f32[]{:T(128)} %constant.18.clone.1), dimensions={2,4,6}, to_apply=%region_6.7 | reduce | flops 114688 | bytes 589828 | tf_op jit(solution)/shard_map/reduce_sum | solution.py:86
  363.8 4.5 collective-permute-start.41
  370.4 6.3 %collective-permute-done.39 = f32[1,4,2,32,64]{4,3,2,1,0:T(8,128)S(1)} collective-permute-done((f32[1,4,2,32,64]{4,3,2,1,0:T(8,128)S(1)}, f32[1,4,2,32,64]{4,3,2,1,0:T(8,128)S(1)}, u32[]{:S(2)}, u32[]{:S(2)}) %collective-permute-start.39) | collective-permute-done | bytes 65568 | tf_op jit(solution)/shard_map/ppermute | solution.py:34
  379.0 4.5 collective-permute-start.44
  385.7 6.3 %collective-permute-done.42 = f32[1,4,2,32,64]{4,3,2,1,0:T(8,128)S(1)} collective-permute-done((f32[1,4,2,32,64]{4,3,2,1,0:T(8,128)S(1)}, f32[1,4,2,32,64]{4,3,2,1,0:T(8,128)S(1)}, u32[]{:S(2)}, u32[]{:S(2)}) %collective-permute-start.42) | collective-permute-done | bytes 65568 | tf_op jit(solution)/shard_map/ppermute | solution.py:34
  394.3 59.8 %all-gather.7.cloned.1.call-done = f32[128,1,2048]{2,1,0:T(1,128)} async-done(((f32[1,1,2048]{2,1,0:T(1,128)}), f32[128,1,2048]{2,1,0:T(1,128)}) %all-gather.7.cloned.1.call-update) | async-done | bytes 1048592 | tf_op jit(solution)/shard_map/all_gather | solution.py:197
  454.1 3.7 reduce.14
  457.8 2.8 reshape.950
  460.6 4.8 copy.394
  465.4 4.4 reshape_reshape.7.src_ref
  469.8 16.1 %shard_map.38 = f32[32,16,512]{2,1,0:T(8,128)} custom-call(f32[32,16,512]{2,1,0:T(8,128)} %reshape_reshape.7.src_ref, f32[32,16,512]{2,1,0:T(8,128)} %tile.16.met_ref), custom_call_target="tpu_custom_call" | custom-call | tf_op jit(solution)/shard_map/pallas_call | solution.py:156
  485.9 3.8 reshape.951
  492.8 4.5 collective-permute-start.47
  499.4 6.3 %collective-permute-done.45 = f32[1,4,2,32,64]{4,3,2,1,0:T(8,128)S(1)} collective-permute-done((f32[1,4,2,32,64]{4,3,2,1,0:T(8,128)S(1)}, f32[1,4,2,32,64]{4,3,2,1,0:T(8,128)S(1)}, u32[]{:S(2)}, u32[]{:S(2)}) %collective-permute-start.45) | collective-permute-done | bytes 65568 | tf_op jit(solution)/shard_map/ppermute | solution.py:34
  507.3 4.5 collective-permute-start.50
  511.8 2.2 collective-permute-start.48
  514.1 6.1 %collective-permute-done.48 = f32[1,4,2,32,64]{4,3,2,1,0:T(8,128)S(1)} collective-permute-done((f32[1,4,2,32,64]{4,3,2,1,0:T(8,128)S(1)}, f32[1,4,2,32,64]{4,3,2,1,0:T(8,128)S(1)}, u32[]{:S(2)}, u32[]{:S(2)}) %collective-permute-start.48) | collective-permute-done | bytes 65568 | tf_op jit(solution)/shard_map/ppermute | solution.py:34
  522.7 7.9 %broadcast_in_dim.95 = f32[4,2,2,32,2,64,2]{0,6,5,4,3,2,1:T(2,128)} broadcast(f32[4,2,32,64]{0,3,2,1:T(8,128)S(1)} %copy.398), dimensions={0,1,3,5} | broadcast | bytes 589824 | tf_op jit(solution)/shard_map/broadcast_in_dim | solution.py:93
  530.5 10.0 %copy.399 = f32[1,4,4,64,128]{4,3,2,1,0:T(8,128)S(1)} copy(f32[1,4,4,64,128]{1,4,3,2,0:T(8,128)} %bitcast.73) | data formatting | bytes 1048576 | tf_op jit(solution)/shard_map/broadcast_in_dim | solution.py:93
  543.8 4.6 collective-permute-start.53
  551.1 2.1 collective-permute-done.51
  557.0 4.6 collective-permute-start.56
  564.3 2.1 collective-permute-done.54
  (199 shorter events, 108.5 us)
Async XLA Ops:
  6.5 179.3 %all-gather.5.cloned.1.call-start = ((), (), s32[]{:S(2)}) async-start(), calls=%async_computation | async-start | bytes 1320960 | tf_op jit(solution)/shard_map/all_gather | solution.py:201
  6.6 9.4 %collective-permute-start.2 = (f32[1,4,1,64,128]{4,3,2,1,0:T(8,128)S(1)}, f32[1,4,1,64,128]{4,3,2,1,0:T(8,128)S(1)}, u32[]{:S(2)}, u32[]{:S(2)}) collective-permute-start(f32[1,4,1,64,128]{4,3,2,1,0:T(8,128)S(1)} %broadcast.475), channel_id=1, source_target_pairs={{0,1},{1,2},{2,3},{4,5},{5,6},{6,7},{8,9},{9,10},{10,11},{12,13},{... | collective-permute-start | bytes 393224 | tf_op jit(solution)/shard_map/ppermute | solution.py:23
  10.5 7.0 %collective-permute-start.1 = (f32[1,4,1,64,128]{4,3,2,1,0:T(8,128)S(1)}, f32[1,4,1,64,128]{4,3,2,1,0:T(8,128)S(1)}, u32[]{:S(2)}, u32[]{:S(2)}) collective-permute-start(f32[1,4,1,64,128]{4,3,2,1,0:T(8,128)S(1)} %broadcast.475), channel_id=1, source_target_pairs={{1,0},{2,1},{3,2},{5,4},{6,5},{7,6},{9,8},{10,9},{11,10},{13,12},{... | collective-permute-start | bytes 393224 | tf_op jit(solution)/shard_map/ppermute | solution.py:26
  11.9 12.7 %collective-permute-start = (f32[1,4,4,64,128]{4,3,2,1,0:T(8,128)S(1)}, f32[1,4,4,64,128]{4,3,2,1,0:T(8,128)S(1)}, u32[]{:S(2)}, u32[]{:S(2)}) collective-permute-start(f32[1,4,4,64,128]{4,3,2,1,0:T(8,128)S(1)} %broadcast.473), channel_id=1, source_target_pairs={{0,4},{4,8},{8,12},{12,16},{16,20},{20,24},{24,28},{28,32},{32,36}... | collective-permute-start | bytes 1572872 | tf_op jit(solution)/shard_map/ppermute | solution.py:34
  25.1 27.7 %collective-permute-start.3 = (f32[1,4,4,64,128]{4,3,2,1,0:T(8,128)S(1)}, f32[1,4,4,64,128]{4,3,2,1,0:T(8,128)S(1)}, u32[]{:S(2)}, u32[]{:S(2)}) collective-permute-start(f32[1,4,4,64,128]{4,3,2,1,0:T(8,128)S(1)} %get-tuple-element.7), channel_id=1, source_target_pairs={{0,4},{4,8},{8,12},{12,16},{16,20},{20,24},{24,28},{28,32},{32,36}... | collective-permute-start | bytes 1572872 | tf_op jit(solution)/shard_map/ppermute | solution.py:34
  27.1 25.5 %collective-permute-start.4 = (f32[1,4,1,64,128]{4,3,2,1,0:T(8,128)S(1)}, f32[1,4,1,64,128]{4,3,2,1,0:T(8,128)S(1)}, u32[]{:S(2)}, u32[]{:S(2)}) collective-permute-start(f32[1,4,1,64,128]{4,3,2,1,0:T(8,128)S(1)} %get-tuple-element.61), channel_id=1, source_target_pairs={{1,0},{2,1},{3,2},{5,4},{6,5},{7,6},{9,8},{10,9},{11,10},{13,12},{... | collective-permute-start | bytes 393224 | tf_op jit(solution)/shard_map/ppermute | solution.py:26
  28.4 24.3 %collective-permute-start.5 = (f32[1,4,1,64,128]{4,3,2,1,0:T(8,128)S(1)}, f32[1,4,1,64,128]{4,3,2,1,0:T(8,128)S(1)}, u32[]{:S(2)}, u32[]{:S(2)}) collective-permute-start(f32[1,4,1,64,128]{4,3,2,1,0:T(8,128)S(1)} %get-tuple-element.62), channel_id=1, source_target_pairs={{0,1},{1,2},{2,3},{4,5},{5,6},{6,7},{8,9},{9,10},{10,11},{12,13},{... | collective-permute-start | bytes 393224 | tf_op jit(solution)/shard_map/ppermute | solution.py:23
  33.6 28.9 %collective-permute-start.11 = (f32[1,4,1,32,64]{4,3,2,1,0:T(8,128)S(1)}, f32[1,4,1,32,64]{4,3,2,1,0:T(8,128)S(1)}, u32[]{:S(2)}, u32[]{:S(2)}) collective-permute-start(f32[1,4,1,32,64]{4,3,2,1,0:T(8,128)S(1)} %broadcast.482), channel_id=1, source_target_pairs={{0,1},{1,2},{2,3},{4,5},{5,6},{6,7},{8,9},{9,10},{10,11},{12,13},{... | collective-permute-start | bytes 98312 | tf_op jit(solution)/shard_map/ppermute | solution.py:23
  37.5 27.6 %collective-permute-start.10 = (f32[1,4,1,32,64]{4,3,2,1,0:T(8,128)S(1)}, f32[1,4,1,32,64]{4,3,2,1,0:T(8,128)S(1)}, u32[]{:S(2)}, u32[]{:S(2)}) collective-permute-start(f32[1,4,1,32,64]{4,3,2,1,0:T(8,128)S(1)} %broadcast.482), channel_id=1, source_target_pairs={{1,0},{2,1},{3,2},{5,4},{6,5},{7,6},{9,8},{10,9},{11,10},{13,12},{... | collective-permute-start | bytes 98312 | tf_op jit(solution)/shard_map/ppermute | solution.py:26
  53.4 13.6 %collective-permute-start.6 = (f32[1,4,4,64,128]{4,3,2,1,0:T(8,128)S(1)}, f32[1,4,4,64,128]{4,3,2,1,0:T(8,128)S(1)}, u32[]{:S(2)}, u32[]{:S(2)}) collective-permute-start(f32[1,4,4,64,128]{4,3,2,1,0:T(8,128)S(1)} %fusion.119), channel_id=1, source_target_pairs={{0,4},{4,8},{8,12},{12,16},{16,20},{20,24},{24,28},{28,32},{32,36}... | collective-permute-start | bytes 1572872 | tf_op jit(solution)/shard_map/ppermute | solution.py:34
  55.4 11.4 %collective-permute-start.7 = (f32[1,4,1,64,128]{4,3,2,1,0:T(8,128)S(1)}, f32[1,4,1,64,128]{4,3,2,1,0:T(8,128)S(1)}, u32[]{:S(2)}, u32[]{:S(2)}) collective-permute-start(f32[1,4,1,64,128]{4,3,2,1,0:T(8,128)S(1)} %get-tuple-element.57), channel_id=1, source_target_pairs={{1,0},{2,1},{3,2},{5,4},{6,5},{7,6},{9,8},{10,9},{11,10},{13,12},{... | collective-permute-start | bytes 393224 | tf_op jit(solution)/shard_map/ppermute | solution.py:26
  56.7 10.1 %collective-permute-start.8 = (f32[1,4,1,64,128]{4,3,2,1,0:T(8,128)S(1)}, f32[1,4,1,64,128]{4,3,2,1,0:T(8,128)S(1)}, u32[]{:S(2)}, u32[]{:S(2)}) collective-permute-start(f32[1,4,1,64,128]{4,3,2,1,0:T(8,128)S(1)} %get-tuple-element.58), channel_id=1, source_target_pairs={{0,1},{1,2},{2,3},{4,5},{5,6},{6,7},{8,9},{9,10},{10,11},{12,13},{... | collective-permute-start | bytes 393224 | tf_op jit(solution)/shard_map/ppermute | solution.py:23
  63.2 26.2 %collective-permute-start.9 = (f32[1,4,2,32,64]{4,3,2,1,0:T(8,128)}, f32[1,4,2,32,64]{4,3,2,1,0:T(8,128)}, u32[]{:S(2)}, u32[]{:S(2)}) collective-permute-start(f32[1,4,2,32,64]{4,3,2,1,0:T(8,128)} %broadcast.481), channel_id=1, source_target_pairs={{0,4},{4,8},{8,12},{12,16},{16,20},{20,24},{24,28},{28,32},{32,36}... | collective-permute-start | bytes 196616 | tf_op jit(solution)/shard_map/ppermute | solution.py:34
  89.4 17.2 %copy-start.1 = (f32[4,2,32,64]{3,2,1,0:T(8,128)S(1)}, f32[4,2,32,64]{3,2,1,0:T(8,128)}, u32[]{:S(2)}) copy-start(f32[4,2,32,64]{3,2,1,0:T(8,128)} %copy.381) | copy-start | bytes 196612
  89.4 17.2 %copy-start.3 = (f32[2,32,64]{2,1,0:T(8,128)S(1)}, f32[2,32,64]{2,1,0:T(8,128)}, u32[]{:S(2)}) copy-start(f32[2,32,64]{2,1,0:T(8,128)} %get-tuple-element.123) | copy-start | bytes 49156
  89.4 17.2 %copy-start.5 = (f32[2,32,64]{2,1,0:T(8,128)S(1)}, f32[2,32,64]{2,1,0:T(8,128)}, u32[]{:S(2)}) copy-start(f32[2,32,64]{2,1,0:T(8,128)} %get-tuple-element.122) | copy-start | bytes 49156
  91.6 8.5 %collective-permute-start.13 = (f32[1,4,1,32,64]{4,3,2,1,0:T(8,128)S(1)}, f32[1,4,1,32,64]{4,3,2,1,0:T(8,128)S(1)}, u32[]{:S(2)}, u32[]{:S(2)}) collective-permute-start(f32[1,4,1,32,64]{4,3,2,1,0:T(8,128)S(1)} %get-tuple-element.113), channel_id=1, source_target_pairs={{1,0},{2,1},{3,2},{5,4},{6,5},{7,6},{9,8},{10,9},{11,10},{13,12},{... | collective-permute-start | bytes 98312 | tf_op jit(solution)/shard_map/ppermute | solution.py:26
  92.9 7.2 %collective-permute-start.14 = (f32[1,4,1,32,64]{4,3,2,1,0:T(8,128)S(1)}, f32[1,4,1,32,64]{4,3,2,1,0:T(8,128)S(1)}, u32[]{:S(2)}, u32[]{:S(2)}) collective-permute-start(f32[1,4,1,32,64]{4,3,2,1,0:T(8,128)S(1)} %get-tuple-element.114), channel_id=1, source_target_pairs={{0,1},{1,2},{2,3},{4,5},{5,6},{6,7},{8,9},{9,10},{10,11},{12,13},{... | collective-permute-start | bytes 98312 | tf_op jit(solution)/shard_map/ppermute | solution.py:23
  98.1 8.4 %collective-permute-start.12 = (f32[1,4,2,32,64]{4,3,2,1,0:T(8,128)S(1)}, f32[1,4,2,32,64]{4,3,2,1,0:T(8,128)S(1)}, u32[]{:S(2)}, u32[]{:S(2)}) collective-permute-start(f32[1,4,2,32,64]{4,3,2,1,0:T(8,128)S(1)} %get-tuple-element.5), channel_id=1, source_target_pairs={{0,4},{4,8},{8,12},{12,16},{16,20},{20,24},{24,28},{28,32},{32,36}... | collective-permute-start | bytes 196616 | tf_op jit(solution)/shard_map/ppermute | solution.py:34
  106.7 7.9 %collective-permute-start.16 = (f32[1,4,1,32,64]{4,3,2,1,0:T(8,128)S(1)}, f32[1,4,1,32,64]{4,3,2,1,0:T(8,128)S(1)}, u32[]{:S(2)}, u32[]{:S(2)}) collective-permute-start(f32[1,4,1,32,64]{4,3,2,1,0:T(8,128)S(1)} %get-tuple-element.109), channel_id=1, source_target_pairs={{1,0},{2,1},{3,2},{5,4},{6,5},{7,6},{9,8},{10,9},{11,10},{13,12},{... | collective-permute-start | bytes 98312 | tf_op jit(solution)/shard_map/ppermute | solution.py:26
  108.0 6.6 %collective-permute-start.17 = (f32[1,4,1,32,64]{4,3,2,1,0:T(8,128)S(1)}, f32[1,4,1,32,64]{4,3,2,1,0:T(8,128)S(1)}, u32[]{:S(2)}, u32[]{:S(2)}) collective-permute-start(f32[1,4,1,32,64]{4,3,2,1,0:T(8,128)S(1)} %get-tuple-element.110), channel_id=1, source_target_pairs={{0,1},{1,2},{2,3},{4,5},{5,6},{6,7},{8,9},{9,10},{10,11},{12,13},{... | collective-permute-start | bytes 98312 | tf_op jit(solution)/shard_map/ppermute | solution.py:23
  112.7 8.4 %collective-permute-start.15 = (f32[1,4,2,32,64]{4,3,2,1,0:T(8,128)S(1)}, f32[1,4,2,32,64]{4,3,2,1,0:T(8,128)S(1)}, u32[]{:S(2)}, u32[]{:S(2)}) collective-permute-start(f32[1,4,2,32,64]{4,3,2,1,0:T(8,128)S(1)} %fusion.255), channel_id=1, source_target_pairs={{0,4},{4,8},{8,12},{12,16},{16,20},{20,24},{24,28},{28,32},{32,36}... | collective-permute-start | bytes 196616 | tf_op jit(solution)/shard_map/ppermute | solution.py:34
  123.4 330.7 %all-gather.7.cloned.1.call-start = ((), (), s32[]{:S(2)}) async-start(), calls=%async_computation.1 | async-start | bytes 1056768 | tf_op jit(solution)/shard_map/all_gather | solution.py:197
  224.8 7.8 %collective-permute-start.19 = (f32[1,4,1,32,64]{4,3,2,1,0:T(8,128)S(1)}, f32[1,4,1,32,64]{4,3,2,1,0:T(8,128)S(1)}, u32[]{:S(2)}, u32[]{:S(2)}) collective-permute-start(f32[1,4,1,32,64]{4,3,2,1,0:T(8,128)S(1)} %get-tuple-element.105), channel_id=1, source_target_pairs={{1,0},{2,1},{3,2},{5,4},{6,5},{7,6},{9,8},{10,9},{11,10},{13,12},{... | collective-permute-start | bytes 98312 | tf_op jit(solution)/shard_map/ppermute | solution.py:26
  226.1 6.5 %collective-permute-start.20 = (f32[1,4,1,32,64]{4,3,2,1,0:T(8,128)S(1)}, f32[1,4,1,32,64]{4,3,2,1,0:T(8,128)S(1)}, u32[]{:S(2)}, u32[]{:S(2)}) collective-permute-start(f32[1,4,1,32,64]{4,3,2,1,0:T(8,128)S(1)} %get-tuple-element.106), channel_id=1, source_target_pairs={{0,1},{1,2},{2,3},{4,5},{5,6},{6,7},{8,9},{9,10},{10,11},{12,13},{... | collective-permute-start | bytes 98312 | tf_op jit(solution)/shard_map/ppermute | solution.py:23
  230.7 8.4 %collective-permute-start.18 = (f32[1,4,2,32,64]{4,3,2,1,0:T(8,128)S(1)}, f32[1,4,2,32,64]{4,3,2,1,0:T(8,128)S(1)}, u32[]{:S(2)}, u32[]{:S(2)}) collective-permute-start(f32[1,4,2,32,64]{4,3,2,1,0:T(8,128)S(1)} %broadcast_add_fusion.1), channel_id=1, source_target_pairs={{0,4},{4,8},{8,12},{12,16},{16,20},{20,24},{24,28},{28,32},{32,36}... | collective-permute-start | bytes 196616 | tf_op jit(solution)/shard_map/ppermute | solution.py:34
  239.2 7.8 %collective-permute-start.22 = (f32[1,4,1,32,64]{4,3,2,1,0:T(8,128)S(1)}, f32[1,4,1,32,64]{4,3,2,1,0:T(8,128)S(1)}, u32[]{:S(2)}, u32[]{:S(2)}) collective-permute-start(f32[1,4,1,32,64]{4,3,2,1,0:T(8,128)S(1)} %get-tuple-element.101), channel_id=1, source_target_pairs={{1,0},{2,1},{3,2},{5,4},{6,5},{7,6},{9,8},{10,9},{11,10},{13,12},{... | collective-permute-start | bytes 98312 | tf_op jit(solution)/shard_map/ppermute | solution.py:26
  240.5 6.5 %collective-permute-start.23 = (f32[1,4,1,32,64]{4,3,2,1,0:T(8,128)S(1)}, f32[1,4,1,32,64]{4,3,2,1,0:T(8,128)S(1)}, u32[]{:S(2)}, u32[]{:S(2)}) collective-permute-start(f32[1,4,1,32,64]{4,3,2,1,0:T(8,128)S(1)} %get-tuple-element.102), channel_id=1, source_target_pairs={{0,1},{1,2},{2,3},{4,5},{5,6},{6,7},{8,9},{9,10},{10,11},{12,13},{... | collective-permute-start | bytes 98312 | tf_op jit(solution)/shard_map/ppermute | solution.py:23
  245.1 8.4 %collective-permute-start.21 = (f32[1,4,2,32,64]{4,3,2,1,0:T(8,128)S(1)}, f32[1,4,2,32,64]{4,3,2,1,0:T(8,128)S(1)}, u32[]{:S(2)}, u32[]{:S(2)}) collective-permute-start(f32[1,4,2,32,64]{4,3,2,1,0:T(8,128)S(1)} %fusion.227), channel_id=1, source_target_pairs={{0,4},{4,8},{8,12},{12,16},{16,20},{20,24},{24,28},{28,32},{32,36}... | collective-permute-start | bytes 196616 | tf_op jit(solution)/shard_map/ppermute | solution.py:34
  273.9 12.6 %collective-permute-start.24 = (f32[1,4,4,64,128]{4,3,2,1,0:T(8,128)S(1)}, f32[1,4,4,64,128]{4,3,2,1,0:T(8,128)S(1)}, u32[]{:S(2)}, u32[]{:S(2)}) collective-permute-start(f32[1,4,4,64,128]{4,3,2,1,0:T(8,128)S(1)} %add.510), channel_id=1, source_target_pairs={{0,4},{4,8},{8,12},{12,16},{16,20},{20,24},{24,28},{28,32},{32,36}... | collective-permute-start | bytes 1572872 | tf_op jit(solution)/shard_map/ppermute | solution.py:34
  275.8 6.9 %collective-permute-start.25 = (f32[1,4,1,64,128]{4,3,2,1,0:T(8,128)S(1)}, f32[1,4,1,64,128]{4,3,2,1,0:T(8,128)S(1)}, u32[]{:S(2)}, u32[]{:S(2)}) collective-permute-start(f32[1,4,1,64,128]{4,3,2,1,0:T(8,128)S(1)} %get-tuple-element.53), channel_id=1, source_target_pairs={{1,0},{2,1},{3,2},{5,4},{6,5},{7,6},{9,8},{10,9},{11,10},{13,12},{... | collective-permute-start | bytes 393224 | tf_op jit(solution)/shard_map/ppermute | solution.py:26
  277.1 7.1 %collective-permute-start.26 = (f32[1,4,1,64,128]{4,3,2,1,0:T(8,128)S(1)}, f32[1,4,1,64,128]{4,3,2,1,0:T(8,128)S(1)}, u32[]{:S(2)}, u32[]{:S(2)}) collective-permute-start(f32[1,4,1,64,128]{4,3,2,1,0:T(8,128)S(1)} %get-tuple-element.54), channel_id=1, source_target_pairs={{0,1},{1,2},{2,3},{4,5},{5,6},{6,7},{8,9},{9,10},{10,11},{12,13},{... | collective-permute-start | bytes 393224 | tf_op jit(solution)/shard_map/ppermute | solution.py:23
  287.0 12.6 %collective-permute-start.27 = (f32[1,4,4,64,128]{4,3,2,1,0:T(8,128)S(1)}, f32[1,4,4,64,128]{4,3,2,1,0:T(8,128)S(1)}, u32[]{:S(2)}, u32[]{:S(2)}) collective-permute-start(f32[1,4,4,64,128]{4,3,2,1,0:T(8,128)S(1)} %fusion.93), channel_id=1, source_target_pairs={{0,4},{4,8},{8,12},{12,16},{16,20},{20,24},{24,28},{28,32},{32,36}... | collective-permute-start | bytes 1572872 | tf_op jit(solution)/shard_map/ppermute | solution.py:34
  289.0 6.9 %collective-permute-start.28 = (f32[1,4,1,64,128]{4,3,2,1,0:T(8,128)S(1)}, f32[1,4,1,64,128]{4,3,2,1,0:T(8,128)S(1)}, u32[]{:S(2)}, u32[]{:S(2)}) collective-permute-start(f32[1,4,1,64,128]{4,3,2,1,0:T(8,128)S(1)} %get-tuple-element.49), channel_id=1, source_target_pairs={{1,0},{2,1},{3,2},{5,4},{6,5},{7,6},{9,8},{10,9},{11,10},{13,12},{... | collective-permute-start | bytes 393224 | tf_op jit(solution)/shard_map/ppermute | solution.py:26
  290.3 7.1 %collective-permute-start.29 = (f32[1,4,1,64,128]{4,3,2,1,0:T(8,128)S(1)}, f32[1,4,1,64,128]{4,3,2,1,0:T(8,128)S(1)}, u32[]{:S(2)}, u32[]{:S(2)}) collective-permute-start(f32[1,4,1,64,128]{4,3,2,1,0:T(8,128)S(1)} %get-tuple-element.50), channel_id=1, source_target_pairs={{0,1},{1,2},{2,3},{4,5},{5,6},{6,7},{8,9},{9,10},{10,11},{12,13},{... | collective-permute-start | bytes 393224 | tf_op jit(solution)/shard_map/ppermute | solution.py:23
  300.2 12.6 %collective-permute-start.30 = (f32[1,4,4,64,128]{4,3,2,1,0:T(8,128)S(1)}, f32[1,4,4,64,128]{4,3,2,1,0:T(8,128)S(1)}, u32[]{:S(2)}, u32[]{:S(2)}) collective-permute-start(f32[1,4,4,64,128]{4,3,2,1,0:T(8,128)S(1)} %fusion.79), channel_id=1, source_target_pairs={{0,4},{4,8},{8,12},{12,16},{16,20},{20,24},{24,28},{28,32},{32,36}... | collective-permute-start | bytes 1572872 | tf_op jit(solution)/shard_map/ppermute | solution.py:34
  302.1 6.9 %collective-permute-start.31 = (f32[1,4,1,64,128]{4,3,2,1,0:T(8,128)S(1)}, f32[1,4,1,64,128]{4,3,2,1,0:T(8,128)S(1)}, u32[]{:S(2)}, u32[]{:S(2)}) collective-permute-start(f32[1,4,1,64,128]{4,3,2,1,0:T(8,128)S(1)} %get-tuple-element.45), channel_id=1, source_target_pairs={{1,0},{2,1},{3,2},{5,4},{6,5},{7,6},{9,8},{10,9},{11,10},{13,12},{... | collective-permute-start | bytes 393224 | tf_op jit(solution)/shard_map/ppermute | solution.py:26
  303.4 7.1 %collective-permute-start.32 = (f32[1,4,1,64,128]{4,3,2,1,0:T(8,128)S(1)}, f32[1,4,1,64,128]{4,3,2,1,0:T(8,128)S(1)}, u32[]{:S(2)}, u32[]{:S(2)}) collective-permute-start(f32[1,4,1,64,128]{4,3,2,1,0:T(8,128)S(1)} %get-tuple-element.46), channel_id=1, source_target_pairs={{0,1},{1,2},{2,3},{4,5},{5,6},{6,7},{8,9},{9,10},{10,11},{12,13},{... | collective-permute-start | bytes 393224 | tf_op jit(solution)/shard_map/ppermute | solution.py:23
  313.3 12.6 %collective-permute-start.33 = (f32[1,4,4,64,128]{4,3,2,1,0:T(8,128)S(1)}, f32[1,4,4,64,128]{4,3,2,1,0:T(8,128)S(1)}, u32[]{:S(2)}, u32[]{:S(2)}) collective-permute-start(f32[1,4,4,64,128]{4,3,2,1,0:T(8,128)S(1)} %fusion.65), channel_id=1, source_target_pairs={{0,4},{4,8},{8,12},{12,16},{16,20},{20,24},{24,28},{28,32},{32,36}... | collective-permute-start | bytes 1572872 | tf_op jit(solution)/shard_map/ppermute | solution.py:34
  315.3 6.9 %collective-permute-start.34 = (f32[1,4,1,64,128]{4,3,2,1,0:T(8,128)S(1)}, f32[1,4,1,64,128]{4,3,2,1,0:T(8,128)S(1)}, u32[]{:S(2)}, u32[]{:S(2)}) collective-permute-start(f32[1,4,1,64,128]{4,3,2,1,0:T(8,128)S(1)} %get-tuple-element.41), channel_id=1, source_target_pairs={{1,0},{2,1},{3,2},{5,4},{6,5},{7,6},{9,8},{10,9},{11,10},{13,12},{... | collective-permute-start | bytes 393224 | tf_op jit(solution)/shard_map/ppermute | solution.py:26
  316.6 7.1 %collective-permute-start.35 = (f32[1,4,1,64,128]{4,3,2,1,0:T(8,128)S(1)}, f32[1,4,1,64,128]{4,3,2,1,0:T(8,128)S(1)}, u32[]{:S(2)}, u32[]{:S(2)}) collective-permute-start(f32[1,4,1,64,128]{4,3,2,1,0:T(8,128)S(1)} %get-tuple-element.42), channel_id=1, source_target_pairs={{0,1},{1,2},{2,3},{4,5},{5,6},{6,7},{8,9},{9,10},{10,11},{12,13},{... | collective-permute-start | bytes 393224 | tf_op jit(solution)/shard_map/ppermute | solution.py:23
  326.5 12.6 %collective-permute-start.36 = (f32[1,4,4,64,128]{4,3,2,1,0:T(8,128)S(1)}, f32[1,4,4,64,128]{4,3,2,1,0:T(8,128)S(1)}, u32[]{:S(2)}, u32[]{:S(2)}) collective-permute-start(f32[1,4,4,64,128]{4,3,2,1,0:T(8,128)S(1)} %fusion.51), channel_id=1, source_target_pairs={{0,4},{4,8},{8,12},{12,16},{16,20},{20,24},{24,28},{28,32},{32,36}... | collective-permute-start | bytes 1572872 | tf_op jit(solution)/shard_map/ppermute | solution.py:34
  328.5 6.9 %collective-permute-start.37 = (f32[1,4,1,64,128]{4,3,2,1,0:T(8,128)S(1)}, f32[1,4,1,64,128]{4,3,2,1,0:T(8,128)S(1)}, u32[]{:S(2)}, u32[]{:S(2)}) collective-permute-start(f32[1,4,1,64,128]{4,3,2,1,0:T(8,128)S(1)} %get-tuple-element.37), channel_id=1, source_target_pairs={{1,0},{2,1},{3,2},{5,4},{6,5},{7,6},{9,8},{10,9},{11,10},{13,12},{... | collective-permute-start | bytes 393224 | tf_op jit(solution)/shard_map/ppermute | solution.py:26
  329.8 7.1 %collective-permute-start.38 = (f32[1,4,1,64,128]{4,3,2,1,0:T(8,128)S(1)}, f32[1,4,1,64,128]{4,3,2,1,0:T(8,128)S(1)}, u32[]{:S(2)}, u32[]{:S(2)}) collective-permute-start(f32[1,4,1,64,128]{4,3,2,1,0:T(8,128)S(1)} %get-tuple-element.38), channel_id=1, source_target_pairs={{0,1},{1,2},{2,3},{4,5},{5,6},{6,7},{8,9},{9,10},{10,11},{12,13},{... | collective-permute-start | bytes 393224 | tf_op jit(solution)/shard_map/ppermute | solution.py:23
  361.5 15.3 %copy-start.2 = (f32[4,2,32,64]{3,2,1,0:T(8,128)S(1)}, f32[4,2,32,64]{3,2,1,0:T(8,128)}, u32[]{:S(2)}) copy-start(f32[4,2,32,64]{3,2,1,0:T(8,128)} %copy.391) | copy-start | bytes 196612
  362.5 29.5 %copy-start.4 = (f32[2,32,64]{2,1,0:T(8,128)S(1)}, f32[2,32,64]{2,1,0:T(8,128)}, u32[]{:S(2)}) copy-start(f32[2,32,64]{2,1,0:T(8,128)} %get-tuple-element.123) | copy-start | bytes 49156
  362.5 7.8 %collective-permute-start.40 = (f32[1,4,1,32,64]{4,3,2,1,0:T(8,128)S(1)}, f32[1,4,1,32,64]{4,3,2,1,0:T(8,128)S(1)}, u32[]{:S(2)}, u32[]{:S(2)}) collective-permute-start(f32[1,4,1,32,64]{4,3,2,1,0:T(8,128)S(1)} %get-tuple-element.97), channel_id=1, source_target_pairs={{1,0},{2,1},{3,2},{5,4},{6,5},{7,6},{9,8},{10,9},{11,10},{13,12},{... | collective-permute-start | bytes 98312 | tf_op jit(solution)/shard_map/ppermute | solution.py:26
  363.8 6.5 %collective-permute-start.41 = (f32[1,4,1,32,64]{4,3,2,1,0:T(8,128)S(1)}, f32[1,4,1,32,64]{4,3,2,1,0:T(8,128)S(1)}, u32[]{:S(2)}, u32[]{:S(2)}) collective-permute-start(f32[1,4,1,32,64]{4,3,2,1,0:T(8,128)S(1)} %get-tuple-element.98), channel_id=1, source_target_pairs={{0,1},{1,2},{2,3},{4,5},{5,6},{6,7},{8,9},{9,10},{10,11},{12,13},{... | collective-permute-start | bytes 98312 | tf_op jit(solution)/shard_map/ppermute | solution.py:23
  368.4 8.4 %collective-permute-start.39 = (f32[1,4,2,32,64]{4,3,2,1,0:T(8,128)S(1)}, f32[1,4,2,32,64]{4,3,2,1,0:T(8,128)S(1)}, u32[]{:S(2)}, u32[]{:S(2)}) collective-permute-start(f32[1,4,2,32,64]{4,3,2,1,0:T(8,128)S(1)} %fusion.397), channel_id=1, source_target_pairs={{0,4},{4,8},{8,12},{12,16},{16,20},{20,24},{24,28},{28,32},{32,36}... | collective-permute-start | bytes 196616 | tf_op jit(solution)/shard_map/ppermute | solution.py:34
  377.7 7.8 %collective-permute-start.43 = (f32[1,4,1,32,64]{4,3,2,1,0:T(8,128)S(1)}, f32[1,4,1,32,64]{4,3,2,1,0:T(8,128)S(1)}, u32[]{:S(2)}, u32[]{:S(2)}) collective-permute-start(f32[1,4,1,32,64]{4,3,2,1,0:T(8,128)S(1)} %get-tuple-element.93), channel_id=1, source_target_pairs={{1,0},{2,1},{3,2},{5,4},{6,5},{7,6},{9,8},{10,9},{11,10},{13,12},{... | collective-permute-start | bytes 98312 | tf_op jit(solution)/shard_map/ppermute | solution.py:26
  379.0 6.5 %collective-permute-start.44 = (f32[1,4,1,32,64]{4,3,2,1,0:T(8,128)S(1)}, f32[1,4,1,32,64]{4,3,2,1,0:T(8,128)S(1)}, u32[]{:S(2)}, u32[]{:S(2)}) collective-permute-start(f32[1,4,1,32,64]{4,3,2,1,0:T(8,128)S(1)} %get-tuple-element.94), channel_id=1, source_target_pairs={{0,1},{1,2},{2,3},{4,5},{5,6},{6,7},{8,9},{9,10},{10,11},{12,13},{... | collective-permute-start | bytes 98312 | tf_op jit(solution)/shard_map/ppermute | solution.py:23
  383.6 8.4 %collective-permute-start.42 = (f32[1,4,2,32,64]{4,3,2,1,0:T(8,128)S(1)}, f32[1,4,2,32,64]{4,3,2,1,0:T(8,128)S(1)}, u32[]{:S(2)}, u32[]{:S(2)}) collective-permute-start(f32[1,4,2,32,64]{4,3,2,1,0:T(8,128)S(1)} %fusion.197), channel_id=1, source_target_pairs={{0,4},{4,8},{8,12},{12,16},{16,20},{20,24},{24,28},{28,32},{32,36}... | collective-permute-start | bytes 196616 | tf_op jit(solution)/shard_map/ppermute | solution.py:34
  491.5 7.8 %collective-permute-start.46 = (f32[1,4,1,32,64]{4,3,2,1,0:T(8,128)S(1)}, f32[1,4,1,32,64]{4,3,2,1,0:T(8,128)S(1)}, u32[]{:S(2)}, u32[]{:S(2)}) collective-permute-start(f32[1,4,1,32,64]{4,3,2,1,0:T(8,128)S(1)} %get-tuple-element.89), channel_id=1, source_target_pairs={{1,0},{2,1},{3,2},{5,4},{6,5},{7,6},{9,8},{10,9},{11,10},{13,12},{... | collective-permute-start | bytes 98312 | tf_op jit(solution)/shard_map/ppermute | solution.py:26
  492.8 6.5 %collective-permute-start.47 = (f32[1,4,1,32,64]{4,3,2,1,0:T(8,128)S(1)}, f32[1,4,1,32,64]{4,3,2,1,0:T(8,128)S(1)}, u32[]{:S(2)}, u32[]{:S(2)}) collective-permute-start(f32[1,4,1,32,64]{4,3,2,1,0:T(8,128)S(1)} %get-tuple-element.90), channel_id=1, source_target_pairs={{0,1},{1,2},{2,3},{4,5},{5,6},{6,7},{8,9},{9,10},{10,11},{12,13},{... | collective-permute-start | bytes 98312 | tf_op jit(solution)/shard_map/ppermute | solution.py:23
  497.4 8.4 %collective-permute-start.45 = (f32[1,4,2,32,64]{4,3,2,1,0:T(8,128)S(1)}, f32[1,4,2,32,64]{4,3,2,1,0:T(8,128)S(1)}, u32[]{:S(2)}, u32[]{:S(2)}) collective-permute-start(f32[1,4,2,32,64]{4,3,2,1,0:T(8,128)S(1)} %broadcast_add_fusion), channel_id=1, source_target_pairs={{0,4},{4,8},{8,12},{12,16},{16,20},{20,24},{24,28},{28,32},{32,36}... | collective-permute-start | bytes 196616 | tf_op jit(solution)/shard_map/ppermute | solution.py:34
  506.0 8.0 %collective-permute-start.49 = (f32[1,4,1,32,64]{4,3,2,1,0:T(8,128)S(1)}, f32[1,4,1,32,64]{4,3,2,1,0:T(8,128)S(1)}, u32[]{:S(2)}, u32[]{:S(2)}) collective-permute-start(f32[1,4,1,32,64]{4,3,2,1,0:T(8,128)S(1)} %get-tuple-element.85), channel_id=1, source_target_pairs={{1,0},{2,1},{3,2},{5,4},{6,5},{7,6},{9,8},{10,9},{11,10},{13,12},{... | collective-permute-start | bytes 98312 | tf_op jit(solution)/shard_map/ppermute | solution.py:26
  507.3 6.8 %collective-permute-start.50 = (f32[1,4,1,32,64]{4,3,2,1,0:T(8,128)S(1)}, f32[1,4,1,32,64]{4,3,2,1,0:T(8,128)S(1)}, u32[]{:S(2)}, u32[]{:S(2)}) collective-permute-start(f32[1,4,1,32,64]{4,3,2,1,0:T(8,128)S(1)} %get-tuple-element.86), channel_id=1, source_target_pairs={{0,1},{1,2},{2,3},{4,5},{5,6},{6,7},{8,9},{9,10},{10,11},{12,13},{... | collective-permute-start | bytes 98312 | tf_op jit(solution)/shard_map/ppermute | solution.py:23
  511.8 8.4 %collective-permute-start.48 = (f32[1,4,2,32,64]{4,3,2,1,0:T(8,128)S(1)}, f32[1,4,2,32,64]{4,3,2,1,0:T(8,128)S(1)}, u32[]{:S(2)}, u32[]{:S(2)}) collective-permute-start(f32[1,4,2,32,64]{4,3,2,1,0:T(8,128)S(1)} %fusion.169), channel_id=1, source_target_pairs={{0,4},{4,8},{8,12},{12,16},{16,20},{20,24},{24,28},{28,32},{32,36}... | collective-permute-start | bytes 196616 | tf_op jit(solution)/shard_map/ppermute | solution.py:34
  540.6 12.6 %collective-permute-start.51 = (f32[1,4,4,64,128]{4,3,2,1,0:T(8,128)S(1)}, f32[1,4,4,64,128]{4,3,2,1,0:T(8,128)S(1)}, u32[]{:S(2)}, u32[]{:S(2)}) collective-permute-start(f32[1,4,4,64,128]{4,3,2,1,0:T(8,128)S(1)} %add.555), channel_id=1, source_target_pairs={{0,4},{4,8},{8,12},{12,16},{16,20},{20,24},{24,28},{28,32},{32,36}... | collective-permute-start | bytes 1572872 | tf_op jit(solution)/shard_map/ppermute | solution.py:34
  542.5 6.9 %collective-permute-start.52 = (f32[1,4,1,64,128]{4,3,2,1,0:T(8,128)S(1)}, f32[1,4,1,64,128]{4,3,2,1,0:T(8,128)S(1)}, u32[]{:S(2)}, u32[]{:S(2)}) collective-permute-start(f32[1,4,1,64,128]{4,3,2,1,0:T(8,128)S(1)} %get-tuple-element.33), channel_id=1, source_target_pairs={{1,0},{2,1},{3,2},{5,4},{6,5},{7,6},{9,8},{10,9},{11,10},{13,12},{... | collective-permute-start | bytes 393224 | tf_op jit(solution)/shard_map/ppermute | solution.py:26
  543.8 7.1 %collective-permute-start.53 = (f32[1,4,1,64,128]{4,3,2,1,0:T(8,128)S(1)}, f32[1,4,1,64,128]{4,3,2,1,0:T(8,128)S(1)}, u32[]{:S(2)}, u32[]{:S(2)}) collective-permute-start(f32[1,4,1,64,128]{4,3,2,1,0:T(8,128)S(1)} %get-tuple-element.34), channel_id=1, source_target_pairs={{0,1},{1,2},{2,3},{4,5},{5,6},{6,7},{8,9},{9,10},{10,11},{12,13},{... | collective-permute-start | bytes 393224 | tf_op jit(solution)/shard_map/ppermute | solution.py:23
  553.7 12.6 %collective-permute-start.54 = (f32[1,4,4,64,128]{4,3,2,1,0:T(8,128)S(1)}, f32[1,4,4,64,128]{4,3,2,1,0:T(8,128)S(1)}, u32[]{:S(2)}, u32[]{:S(2)}) collective-permute-start(f32[1,4,4,64,128]{4,3,2,1,0:T(8,128)S(1)} %fusion.25), channel_id=1, source_target_pairs={{0,4},{4,8},{8,12},{12,16},{16,20},{20,24},{24,28},{28,32},{32,36}... | collective-permute-start | bytes 1572872 | tf_op jit(solution)/shard_map/ppermute | solution.py:34
  555.7 6.9 %collective-permute-start.55 = (f32[1,4,1,64,128]{4,3,2,1,0:T(8,128)S(1)}, f32[1,4,1,64,128]{4,3,2,1,0:T(8,128)S(1)}, u32[]{:S(2)}, u32[]{:S(2)}) collective-permute-start(f32[1,4,1,64,128]{4,3,2,1,0:T(8,128)S(1)} %get-tuple-element.29), channel_id=1, source_target_pairs={{1,0},{2,1},{3,2},{5,4},{6,5},{7,6},{9,8},{10,9},{11,10},{13,12},{... | collective-permute-start | bytes 393224 | tf_op jit(solution)/shard_map/ppermute | solution.py:26
  557.0 7.1 %collective-permute-start.56 = (f32[1,4,1,64,128]{4,3,2,1,0:T(8,128)S(1)}, f32[1,4,1,64,128]{4,3,2,1,0:T(8,128)S(1)}, u32[]{:S(2)}, u32[]{:S(2)}) collective-permute-start(f32[1,4,1,64,128]{4,3,2,1,0:T(8,128)S(1)} %get-tuple-element.30), channel_id=1, source_target_pairs={{0,1},{1,2},{2,3},{4,5},{5,6},{6,7},{8,9},{9,10},{10,11},{12,13},{... | collective-permute-start | bytes 393224 | tf_op jit(solution)/shard_map/ppermute | solution.py:23
  (5 other events, 44.2 us)
Sparse Core Ops, SparseCore 0:
  123.5 62.2 all-gather.4
  394.4 59.6 all-gather.6

commit v3 on v2

--- a/solution.py
+++ b/solution.py
@@ -184,6 +184,11 @@
     return (whole_source, whole_metric)
 
 
+def gather_all(flat):
+    within = lax.all_gather(flat, "space", axis=0, tiled=True)
+    return lax.all_gather(within, "tm", axis=0, tiled=True)
+
+
 def coarse_correction(source, metric_two, gathered):
     time_devs = lax.axis_size("tm")
     plane_devs = lax.axis_size("space")
@@ -194,11 +199,11 @@
     source_flat = source.reshape(1, -1)
     cut = source_flat.shape[1]
     if "metric" in gathered:
-        flat_source = lax.all_gather(source_flat, ("tm", "space"), axis=0, tiled=True)
+        flat_source = gather_all(source_flat)
         flat_metric = gathered["metric"]
     else:
         both = jnp.concatenate([source_flat, metric_two.reshape(1, -1)], axis=1)
-        flat_both = lax.all_gather(both, ("tm", "space"), axis=0, tiled=True)
+        flat_both = gather_all(both)
         flat_source = flat_both[:, :cut]
         flat_metric = flat_both[:, cut:]
         gathered["metric"] = flat_metric

time: 577 us -> 561 us (0.972)
  waiting for transfers between devices: 213 us -> 170 us
  blocking collectives: 0 us -> 25.6 us
    all_gather x2, waiting for transfers between devices: 122 us -> 78.7 us  [gather_all(): return lax.all_gather(within, 'tm', axis=0, tiled=True)]
    all_gather x0 -> x2, blocking collectives: none -> 25.6 us  [gather_all(): within = lax.all_gather(flat, 'space', axis=0, tiled=True)]
where the time goes in v3:
time: 561 us; the launch traced here: 558 us
  waiting for transfers between devices  170 us (30%)
  starting transfers between devices  148 us (26%)
  local copies, waits for them, and re-layouts  118 us (21%)
  other arithmetic  49.2 us (9%)
  Pallas kernels  32.2 us (6%)
  blocking collectives  25.6 us (5%)
  between operations  14.6 us (3%)
    ppermute x19, starting transfers between devices, with_halo(): lax.ppermute(lax.slice_in_dim(block, block.shape[dim] - width, None, axis...  86.7 us
    all_gather x2, waiting for transfers between devices, gather_all(): return lax.all_gather(within, 'tm', axis=0, tiled=True)  78.7 us
    ppermute x19, waiting for transfers between devices, from_behind(): return lax.ppermute(array, axis, pairs)  72.2 us
    broadcast_in_dim x14, local copies, waits for them, and re-layouts, prolong(): jnp.broadcast_to(values.reshape(leading + (depth_x, 1, height_y, 1, width...  42.5 us
    ppermute x19, starting transfers between devices, from_behind(): return lax.ppermute(array, axis, pairs)  36.6 us
    pallas_call x2, Pallas kernels, coarse_solve(): pl.pallas_call(kernel, out_shape=jax.ShapeDtypeStruct(flat_source.shape,...  32.2 us
    reduce_sum x9, other arithmetic, restrict(): return jnp.sum(blocks, axis=(offset + 1, offset + 3, offset + 5)) * 0.125  30.3 us
    all_gather x2, blocking collectives, gather_all(): within = lax.all_gather(flat, 'space', axis=0, tiled=True)  25.6 us
  transfers between devices with their start and end apart: 59, of which 33 were waited for; matrix products, arithmetic and copies ran while one was open for 8% of the time, Pallas kernels for 0%

profile of v3, /device:TPU:2, one launch (start us, length us, event | category | flops | bytes accessed | tf_op | source)
XLA Modules:
  0.0 557.9 jit_solution(10161748509739322301)
XLA Ops:
  6.6 4.0 collective-permute-start.2
  11.9 2.1 collective-permute-start
  17.8 6.9 %collective-permute-done = f32[1,4,4,64,128]{4,3,2,1,0:T(8,128)S(1)} collective-permute-done((f32[1,4,4,64,128]{4,3,2,1,0:T(8,128)S(1)}, f32[1,4,4,64,128]{4,3,2,1,0:T(8,128)S(1)}, u32[]{:S(2)}, u32[]{:S(2)}) %collective-permute-start) | collective-permute-done | bytes 524320 | tf_op jit(solution)/shard_map/ppermute | solution.py:34
  28.4 5.2 collective-permute-start.5
  33.6 3.9 collective-permute-start.11
  38.8 9.8 %reshape.946 = f32[2,2,32,2,64,2]{5,4,3,2,1,0:T(8,128)} reshape(f32[1,4,64,128]{3,2,1,0:T(8,128)S(1)} %copy-done.8) | data formatting | bytes 262144 | tf_op jit(solution)/shard_map/reshape | solution.py:84
  48.6 4.0 reduce_sum.61
  56.7 5.2 collective-permute-start.8
  67.6 8.8 %copy.392 = f32[1,4,4,64,128]{1,4,3,2,0:T(8,128)} copy(f32[1,4,4,64,128]{4,3,2,1,0:T(8,128)S(1)} %fusion.105) | data formatting | bytes 1048576 | tf_op jit(solution)/shard_map/sub | solution.py:239
  76.4 11.7 %reduce_sum.60 = f32[4,2,32,64]{0,3,2,1:T(8,128)S(1)} reduce(f32[4,2,2,32,2,64,2]{0,6,5,4,3,2,1:T(2,128)} %bitcast.71, f32[]{:T(128)} %constant.18.clone.1), dimensions={2,4,6}, to_apply=%region_0.0 | reduce | flops 114688 | bytes 589828 | tf_op jit(solution)/shard_map/reduce_sum | solution.py:86
  89.5 2.2 fusion.399
  93.1 4.5 collective-permute-start.14
  98.3 1.9 collective-permute-start.12
  100.4 6.3 %collective-permute-done.12 = f32[1,4,2,32,64]{4,3,2,1,0:T(8,128)S(1)} collective-permute-done((f32[1,4,2,32,64]{4,3,2,1,0:T(8,128)S(1)}, f32[1,4,2,32,64]{4,3,2,1,0:T(8,128)S(1)}, u32[]{:S(2)}, u32[]{:S(2)}) %collective-permute-start.12) | collective-permute-done | bytes 65568 | tf_op jit(solution)/shard_map/ppermute | solution.py:34
  108.2 4.5 collective-permute-start.17
  114.9 6.3 %collective-permute-done.15 = f32[1,4,2,32,64]{4,3,2,1,0:T(8,128)S(1)} collective-permute-done((f32[1,4,2,32,64]{4,3,2,1,0:T(8,128)S(1)}, f32[1,4,2,32,64]{4,3,2,1,0:T(8,128)S(1)}, u32[]{:S(2)}, u32[]{:S(2)}) %collective-permute-start.15) | collective-permute-done | bytes 65568 | tf_op jit(solution)/shard_map/ppermute | solution.py:34
  122.9 13.2 %all-gather = f32[4,1,2560]{2,1,0:T(1,128)S(1)} all-gather(f32[1,1,2560]{2,1,0:T(1,128)S(1)} %maximum_bitcast_fusion), channel_id=1, replica_groups=mesh['tm'=32,'space'=4] {'space'}, dimensions={0}, use_global_device_ids=true | all-gather | bytes 51200 | tf_op jit(solution)/shard_map/all_gather | solution.py:188
  137.0 39.3 %all-gather.7.cloned.1.call-done = f32[32,4,2560]{2,1,0:T(4,128)} async-done(((f32[1,4,2560]{2,1,0:T(4,128)}), f32[32,4,2560]{2,1,0:T(4,128)}) %all-gather.7.cloned.1.call-update) | async-done | bytes 1310736 | tf_op jit(solution)/shard_map/all_gather | solution.py:189
  181.4 2.6 tile.16.met_ref
  184.1 2.8 reshape.947
  186.9 4.9 copy.397
  191.7 4.4 reshape_reshape.6.src_ref
  196.1 16.1 %shard_map.37 = f32[32,16,512]{2,1,0:T(8,128)} custom-call(f32[32,16,512]{2,1,0:T(8,128)} %reshape_reshape.6.src_ref, f32[32,16,512]{2,1,0:T(8,128)} %tile.16.met_ref), custom_call_target="tpu_custom_call" | custom-call | tf_op jit(solution)/shard_map/pallas_call | solution.py:156
  212.2 3.8 reshape.948
  219.1 4.5 collective-permute-start.20
  225.8 6.3 %collective-permute-done.18 = f32[1,4,2,32,64]{4,3,2,1,0:T(8,128)S(1)} collective-permute-done((f32[1,4,2,32,64]{4,3,2,1,0:T(8,128)S(1)}, f32[1,4,2,32,64]{4,3,2,1,0:T(8,128)S(1)}, u32[]{:S(2)}, u32[]{:S(2)}) %collective-permute-start.18) | collective-permute-done | bytes 65568 | tf_op jit(solution)/shard_map/ppermute | solution.py:34
  233.6 4.5 collective-permute-start.23
  240.2 6.3 %collective-permute-done.21 = f32[1,4,2,32,64]{4,3,2,1,0:T(8,128)S(1)} collective-permute-done((f32[1,4,2,32,64]{4,3,2,1,0:T(8,128)S(1)}, f32[1,4,2,32,64]{4,3,2,1,0:T(8,128)S(1)}, u32[]{:S(2)}, u32[]{:S(2)}) %collective-permute-start.21) | collective-permute-done | bytes 65568 | tf_op jit(solution)/shard_map/ppermute | solution.py:34
  249.0 7.9 %broadcast_in_dim.88 = f32[4,2,2,32,2,64,2]{0,6,5,4,3,2,1:T(2,128)} broadcast(f32[4,2,32,64]{0,3,2,1:T(8,128)S(1)} %copy.401), dimensions={0,1,3,5} | broadcast | bytes 589824 | tf_op jit(solution)/shard_map/broadcast_in_dim | solution.py:93
  256.8 10.0 %copy.402 = f32[1,4,4,64,128]{4,3,2,1,0:T(8,128)S(1)} copy(f32[1,4,4,64,128]{1,4,3,2,0:T(8,128)} %bitcast.72) | data formatting | bytes 1048576 | tf_op jit(solution)/shard_map/broadcast_in_dim | solution.py:93
  266.9 1.9 collective-permute-start.24
  270.2 4.6 collective-permute-start.26
  277.4 2.1 collective-permute-done.24
  283.3 4.6 collective-permute-start.29
  290.6 2.1 collective-permute-done.27
  296.5 4.6 collective-permute-start.32
  303.7 2.1 collective-permute-done.30
  309.6 4.6 collective-permute-start.35
  316.9 2.1 collective-permute-done.33
  322.8 4.8 collective-permute-start.38
  330.1 2.1 collective-permute-done.36
  332.6 8.8 %copy.403 = f32[1,4,4,64,128]{1,4,3,2,0:T(8,128)} copy(f32[1,4,4,64,128]{4,3,2,1,0:T(8,128)S(1)} %fusion.37) | data formatting | bytes 1048576 | tf_op jit(solution)/shard_map/sub | solution.py:239
  341.5 11.7 %reduce_sum.83 = f32[4,2,32,64]{0,3,2,1:T(8,128)S(1)} reduce(f32[4,2,2,32,2,64,2]{0,6,5,4,3,2,1:T(2,128)} %bitcast.73, f32[]{:T(128)} %constant.18.clone.1), dimensions={2,4,6}, to_apply=%region_6.7 | reduce | flops 114688 | bytes 589828 | tf_op jit(solution)/shard_map/reduce_sum | solution.py:86
  356.9 4.5 collective-permute-start.41
  363.5 6.3 %collective-permute-done.39 = f32[1,4,2,32,64]{4,3,2,1,0:T(8,128)S(1)} collective-permute-done((f32[1,4,2,32,64]{4,3,2,1,0:T(8,128)S(1)}, f32[1,4,2,32,64]{4,3,2,1,0:T(8,128)S(1)}, u32[]{:S(2)}, u32[]{:S(2)}) %collective-permute-start.39) | collective-permute-done | bytes 65568 | tf_op jit(solution)/shard_map/ppermute | solution.py:34
  372.1 4.5 collective-permute-start.44
  378.8 6.3 %collective-permute-done.42 = f32[1,4,2,32,64]{4,3,2,1,0:T(8,128)S(1)} collective-permute-done((f32[1,4,2,32,64]{4,3,2,1,0:T(8,128)S(1)}, f32[1,4,2,32,64]{4,3,2,1,0:T(8,128)S(1)}, u32[]{:S(2)}, u32[]{:S(2)}) %collective-permute-start.42) | collective-permute-done | bytes 65568 | tf_op jit(solution)/shard_map/ppermute | solution.py:34
  386.8 12.4 %all-gather.2 = f32[4,1,2048]{2,1,0:T(1,128)S(1)} all-gather(f32[1,1,2048]{2,1,0:T(1,128)S(1)} %reshape.958), channel_id=1, replica_groups=mesh['tm'=32,'space'=4] {'space'}, dimensions={0}, use_global_device_ids=true | all-gather | bytes 40960 | tf_op jit(solution)/shard_map/all_gather | solution.py:188
  399.8 39.4 %all-gather.9.cloned.1.call-done = f32[32,4,2048]{2,1,0:T(4,128)} async-done(((f32[1,4,2048]{2,1,0:T(4,128)}), f32[32,4,2048]{2,1,0:T(4,128)}) %all-gather.9.cloned.1.call-update) | async-done | bytes 1048592 | tf_op jit(solution)/shard_map/all_gather | solution.py:189
  441.0 2.8 reshape.950
  443.9 4.9 copy.409
  448.7 4.4 reshape_reshape.7.src_ref
  453.1 16.1 %shard_map.38 = f32[32,16,512]{2,1,0:T(8,128)} custom-call(f32[32,16,512]{2,1,0:T(8,128)} %reshape_reshape.7.src_ref, f32[32,16,512]{2,1,0:T(8,128)} %tile.16.met_ref), custom_call_target="tpu_custom_call" | custom-call | tf_op jit(solution)/shard_map/pallas_call | solution.py:156
  469.2 3.8 reshape.951
  476.1 4.5 collective-permute-start.47
  482.8 6.3 %collective-permute-done.45 = f32[1,4,2,32,64]{4,3,2,1,0:T(8,128)S(1)} collective-permute-done((f32[1,4,2,32,64]{4,3,2,1,0:T(8,128)S(1)}, f32[1,4,2,32,64]{4,3,2,1,0:T(8,128)S(1)}, u32[]{:S(2)}, u32[]{:S(2)}) %collective-permute-start.45) | collective-permute-done | bytes 65568 | tf_op jit(solution)/shard_map/ppermute | solution.py:34
  490.6 4.5 collective-permute-start.50
  497.2 6.3 %collective-permute-done.48 = f32[1,4,2,32,64]{4,3,2,1,0:T(8,128)S(1)} collective-permute-done((f32[1,4,2,32,64]{4,3,2,1,0:T(8,128)S(1)}, f32[1,4,2,32,64]{4,3,2,1,0:T(8,128)S(1)}, u32[]{:S(2)}, u32[]{:S(2)}) %collective-permute-start.48) | collective-permute-done | bytes 65568 | tf_op jit(solution)/shard_map/ppermute | solution.py:34
  506.0 7.9 %broadcast_in_dim.95 = f32[4,2,2,32,2,64,2]{0,6,5,4,3,2,1:T(2,128)} broadcast(f32[4,2,32,64]{0,3,2,1:T(8,128)S(1)} %copy.413), dimensions={0,1,3,5} | broadcast | bytes 589824 | tf_op jit(solution)/shard_map/broadcast_in_dim | solution.py:93
  513.8 10.0 %copy.414 = f32[1,4,4,64,128]{4,3,2,1,0:T(8,128)S(1)} copy(f32[1,4,4,64,128]{1,4,3,2,0:T(8,128)} %bitcast.74) | data formatting | bytes 1048576 | tf_op jit(solution)/shard_map/broadcast_in_dim | solution.py:93
  527.2 4.6 collective-permute-start.53
  534.4 2.1 collective-permute-done.51
  540.3 4.6 collective-permute-start.56
  547.6 2.1 collective-permute-done.54
  (206 shorter events, 114.6 us)
Async XLA Ops:
  6.5 169.8 %all-gather.7.cloned.1.call-start = ((), (), s32[]{:S(2)}) async-start(), calls=%async_computation | async-start | bytes 1351680 | tf_op jit(solution)/shard_map/all_gather | solution.py:189
  6.6 9.4 %collective-permute-start.2 = (f32[1,4,1,64,128]{4,3,2,1,0:T(8,128)S(1)}, f32[1,4,1,64,128]{4,3,2,1,0:T(8,128)S(1)}, u32[]{:S(2)}, u32[]{:S(2)}) collective-permute-start(f32[1,4,1,64,128]{4,3,2,1,0:T(8,128)S(1)} %broadcast.475), channel_id=1, source_target_pairs={{0,1},{1,2},{2,3},{4,5},{5,6},{6,7},{8,9},{9,10},{10,11},{12,13},{... | collective-permute-start | bytes 393224 | tf_op jit(solution)/shard_map/ppermute | solution.py:23
  10.5 7.0 %collective-permute-start.1 = (f32[1,4,1,64,128]{4,3,2,1,0:T(8,128)S(1)}, f32[1,4,1,64,128]{4,3,2,1,0:T(8,128)S(1)}, u32[]{:S(2)}, u32[]{:S(2)}) collective-permute-start(f32[1,4,1,64,128]{4,3,2,1,0:T(8,128)S(1)} %broadcast.475), channel_id=1, source_target_pairs={{1,0},{2,1},{3,2},{5,4},{6,5},{7,6},{9,8},{10,9},{11,10},{13,12},{... | collective-permute-start | bytes 393224 | tf_op jit(solution)/shard_map/ppermute | solution.py:26
  11.9 12.7 %collective-permute-start = (f32[1,4,4,64,128]{4,3,2,1,0:T(8,128)S(1)}, f32[1,4,4,64,128]{4,3,2,1,0:T(8,128)S(1)}, u32[]{:S(2)}, u32[]{:S(2)}) collective-permute-start(f32[1,4,4,64,128]{4,3,2,1,0:T(8,128)S(1)} %broadcast.473), channel_id=1, source_target_pairs={{0,4},{4,8},{8,12},{12,16},{16,20},{20,24},{24,28},{28,32},{32,36}... | collective-permute-start | bytes 1572872 | tf_op jit(solution)/shard_map/ppermute | solution.py:34
  25.1 27.8 %collective-permute-start.3 = (f32[1,4,4,64,128]{4,3,2,1,0:T(8,128)S(1)}, f32[1,4,4,64,128]{4,3,2,1,0:T(8,128)S(1)}, u32[]{:S(2)}, u32[]{:S(2)}) collective-permute-start(f32[1,4,4,64,128]{4,3,2,1,0:T(8,128)S(1)} %get-tuple-element.7), channel_id=1, source_target_pairs={{0,4},{4,8},{8,12},{12,16},{16,20},{20,24},{24,28},{28,32},{32,36}... | collective-permute-start | bytes 1572872 | tf_op jit(solution)/shard_map/ppermute | solution.py:34
  27.1 25.6 %collective-permute-start.4 = (f32[1,4,1,64,128]{4,3,2,1,0:T(8,128)S(1)}, f32[1,4,1,64,128]{4,3,2,1,0:T(8,128)S(1)}, u32[]{:S(2)}, u32[]{:S(2)}) collective-permute-start(f32[1,4,1,64,128]{4,3,2,1,0:T(8,128)S(1)} %get-tuple-element.61), channel_id=1, source_target_pairs={{1,0},{2,1},{3,2},{5,4},{6,5},{7,6},{9,8},{10,9},{11,10},{13,12},{... | collective-permute-start | bytes 393224 | tf_op jit(solution)/shard_map/ppermute | solution.py:26
  28.4 24.3 %collective-permute-start.5 = (f32[1,4,1,64,128]{4,3,2,1,0:T(8,128)S(1)}, f32[1,4,1,64,128]{4,3,2,1,0:T(8,128)S(1)}, u32[]{:S(2)}, u32[]{:S(2)}) collective-permute-start(f32[1,4,1,64,128]{4,3,2,1,0:T(8,128)S(1)} %get-tuple-element.62), channel_id=1, source_target_pairs={{0,1},{1,2},{2,3},{4,5},{5,6},{6,7},{8,9},{9,10},{10,11},{12,13},{... | collective-permute-start | bytes 393224 | tf_op jit(solution)/shard_map/ppermute | solution.py:23
  33.6 28.9 %collective-permute-start.11 = (f32[1,4,1,32,64]{4,3,2,1,0:T(8,128)S(1)}, f32[1,4,1,32,64]{4,3,2,1,0:T(8,128)S(1)}, u32[]{:S(2)}, u32[]{:S(2)}) collective-permute-start(f32[1,4,1,32,64]{4,3,2,1,0:T(8,128)S(1)} %broadcast.482), channel_id=1, source_target_pairs={{0,1},{1,2},{2,3},{4,5},{5,6},{6,7},{8,9},{9,10},{10,11},{12,13},{... | collective-permute-start | bytes 98312 | tf_op jit(solution)/shard_map/ppermute | solution.py:23
  37.5 27.6 %collective-permute-start.10 = (f32[1,4,1,32,64]{4,3,2,1,0:T(8,128)S(1)}, f32[1,4,1,32,64]{4,3,2,1,0:T(8,128)S(1)}, u32[]{:S(2)}, u32[]{:S(2)}) collective-permute-start(f32[1,4,1,32,64]{4,3,2,1,0:T(8,128)S(1)} %broadcast.482), channel_id=1, source_target_pairs={{1,0},{2,1},{3,2},{5,4},{6,5},{7,6},{9,8},{10,9},{11,10},{13,12},{... | collective-permute-start | bytes 98312 | tf_op jit(solution)/shard_map/ppermute | solution.py:26
  53.5 13.6 %collective-permute-start.6 = (f32[1,4,4,64,128]{4,3,2,1,0:T(8,128)S(1)}, f32[1,4,4,64,128]{4,3,2,1,0:T(8,128)S(1)}, u32[]{:S(2)}, u32[]{:S(2)}) collective-permute-start(f32[1,4,4,64,128]{4,3,2,1,0:T(8,128)S(1)} %fusion.119), channel_id=1, source_target_pairs={{0,4},{4,8},{8,12},{12,16},{16,20},{20,24},{24,28},{28,32},{32,36}... | collective-permute-start | bytes 1572872 | tf_op jit(solution)/shard_map/ppermute | solution.py:34
  55.4 11.4 %collective-permute-start.7 = (f32[1,4,1,64,128]{4,3,2,1,0:T(8,128)S(1)}, f32[1,4,1,64,128]{4,3,2,1,0:T(8,128)S(1)}, u32[]{:S(2)}, u32[]{:S(2)}) collective-permute-start(f32[1,4,1,64,128]{4,3,2,1,0:T(8,128)S(1)} %get-tuple-element.57), channel_id=1, source_target_pairs={{1,0},{2,1},{3,2},{5,4},{6,5},{7,6},{9,8},{10,9},{11,10},{13,12},{... | collective-permute-start | bytes 393224 | tf_op jit(solution)/shard_map/ppermute | solution.py:26
  56.7 10.1 %collective-permute-start.8 = (f32[1,4,1,64,128]{4,3,2,1,0:T(8,128)S(1)}, f32[1,4,1,64,128]{4,3,2,1,0:T(8,128)S(1)}, u32[]{:S(2)}, u32[]{:S(2)}) collective-permute-start(f32[1,4,1,64,128]{4,3,2,1,0:T(8,128)S(1)} %get-tuple-element.58), channel_id=1, source_target_pairs={{0,1},{1,2},{2,3},{4,5},{5,6},{6,7},{8,9},{9,10},{10,11},{12,13},{... | collective-permute-start | bytes 393224 | tf_op jit(solution)/shard_map/ppermute | solution.py:23
  63.2 26.3 %collective-permute-start.9 = (f32[1,4,2,32,64]{4,3,2,1,0:T(8,128)}, f32[1,4,2,32,64]{4,3,2,1,0:T(8,128)}, u32[]{:S(2)}, u32[]{:S(2)}) collective-permute-start(f32[1,4,2,32,64]{4,3,2,1,0:T(8,128)} %broadcast.481), channel_id=1, source_target_pairs={{0,4},{4,8},{8,12},{12,16},{16,20},{20,24},{24,28},{28,32},{32,36}... | collective-permute-start | bytes 196616 | tf_op jit(solution)/shard_map/ppermute | solution.py:34
  89.5 17.2 %copy-start.2 = (f32[4,2,32,64]{3,2,1,0:T(8,128)S(1)}, f32[4,2,32,64]{3,2,1,0:T(8,128)}, u32[]{:S(2)}) copy-start(f32[4,2,32,64]{3,2,1,0:T(8,128)} %copy.393) | copy-start | bytes 196612
  89.5 17.2 %copy-start.4 = (f32[2,32,64]{2,1,0:T(8,128)S(1)}, f32[2,32,64]{2,1,0:T(8,128)}, u32[]{:S(2)}) copy-start(f32[2,32,64]{2,1,0:T(8,128)} %get-tuple-element.123) | copy-start | bytes 49156
  89.5 17.2 %copy-start.6 = (f32[2,32,64]{2,1,0:T(8,128)S(1)}, f32[2,32,64]{2,1,0:T(8,128)}, u32[]{:S(2)}) copy-start(f32[2,32,64]{2,1,0:T(8,128)} %get-tuple-element.122) | copy-start | bytes 49156
  91.8 8.5 %collective-permute-start.13 = (f32[1,4,1,32,64]{4,3,2,1,0:T(8,128)S(1)}, f32[1,4,1,32,64]{4,3,2,1,0:T(8,128)S(1)}, u32[]{:S(2)}, u32[]{:S(2)}) collective-permute-start(f32[1,4,1,32,64]{4,3,2,1,0:T(8,128)S(1)} %get-tuple-element.113), channel_id=1, source_target_pairs={{1,0},{2,1},{3,2},{5,4},{6,5},{7,6},{9,8},{10,9},{11,10},{13,12},{... | collective-permute-start | bytes 98312 | tf_op jit(solution)/shard_map/ppermute | solution.py:26
  93.1 7.2 %collective-permute-start.14 = (f32[1,4,1,32,64]{4,3,2,1,0:T(8,128)S(1)}, f32[1,4,1,32,64]{4,3,2,1,0:T(8,128)S(1)}, u32[]{:S(2)}, u32[]{:S(2)}) collective-permute-start(f32[1,4,1,32,64]{4,3,2,1,0:T(8,128)S(1)} %get-tuple-element.114), channel_id=1, source_target_pairs={{0,1},{1,2},{2,3},{4,5},{5,6},{6,7},{8,9},{9,10},{10,11},{12,13},{... | collective-permute-start | bytes 98312 | tf_op jit(solution)/shard_map/ppermute | solution.py:23
  98.3 8.4 %collective-permute-start.12 = (f32[1,4,2,32,64]{4,3,2,1,0:T(8,128)S(1)}, f32[1,4,2,32,64]{4,3,2,1,0:T(8,128)S(1)}, u32[]{:S(2)}, u32[]{:S(2)}) collective-permute-start(f32[1,4,2,32,64]{4,3,2,1,0:T(8,128)S(1)} %get-tuple-element.5), channel_id=1, source_target_pairs={{0,4},{4,8},{8,12},{12,16},{16,20},{20,24},{24,28},{28,32},{32,36}... | collective-permute-start | bytes 196616 | tf_op jit(solution)/shard_map/ppermute | solution.py:34
  106.9 7.9 %collective-permute-start.16 = (f32[1,4,1,32,64]{4,3,2,1,0:T(8,128)S(1)}, f32[1,4,1,32,64]{4,3,2,1,0:T(8,128)S(1)}, u32[]{:S(2)}, u32[]{:S(2)}) collective-permute-start(f32[1,4,1,32,64]{4,3,2,1,0:T(8,128)S(1)} %get-tuple-element.109), channel_id=1, source_target_pairs={{1,0},{2,1},{3,2},{5,4},{6,5},{7,6},{9,8},{10,9},{11,10},{13,12},{... | collective-permute-start | bytes 98312 | tf_op jit(solution)/shard_map/ppermute | solution.py:26
  108.2 6.6 %collective-permute-start.17 = (f32[1,4,1,32,64]{4,3,2,1,0:T(8,128)S(1)}, f32[1,4,1,32,64]{4,3,2,1,0:T(8,128)S(1)}, u32[]{:S(2)}, u32[]{:S(2)}) collective-permute-start(f32[1,4,1,32,64]{4,3,2,1,0:T(8,128)S(1)} %get-tuple-element.110), channel_id=1, source_target_pairs={{0,1},{1,2},{2,3},{4,5},{5,6},{6,7},{8,9},{9,10},{10,11},{12,13},{... | collective-permute-start | bytes 98312 | tf_op jit(solution)/shard_map/ppermute | solution.py:23
  112.8 8.4 %collective-permute-start.15 = (f32[1,4,2,32,64]{4,3,2,1,0:T(8,128)S(1)}, f32[1,4,2,32,64]{4,3,2,1,0:T(8,128)S(1)}, u32[]{:S(2)}, u32[]{:S(2)}) collective-permute-start(f32[1,4,2,32,64]{4,3,2,1,0:T(8,128)S(1)} %fusion.255), channel_id=1, source_target_pairs={{0,4},{4,8},{8,12},{12,16},{16,20},{20,24},{24,28},{28,32},{32,36}... | collective-permute-start | bytes 196616 | tf_op jit(solution)/shard_map/ppermute | solution.py:34
  136.8 302.4 %all-gather.9.cloned.1.call-start = ((), (), s32[]{:S(2)}) async-start(), calls=%async_computation.1 | async-start | bytes 1081344 | tf_op jit(solution)/shard_map/all_gather | solution.py:189
  217.8 7.8 %collective-permute-start.19 = (f32[1,4,1,32,64]{4,3,2,1,0:T(8,128)S(1)}, f32[1,4,1,32,64]{4,3,2,1,0:T(8,128)S(1)}, u32[]{:S(2)}, u32[]{:S(2)}) collective-permute-start(f32[1,4,1,32,64]{4,3,2,1,0:T(8,128)S(1)} %get-tuple-element.105), channel_id=1, source_target_pairs={{1,0},{2,1},{3,2},{5,4},{6,5},{7,6},{9,8},{10,9},{11,10},{13,12},{... | collective-permute-start | bytes 98312 | tf_op jit(solution)/shard_map/ppermute | solution.py:26
  219.1 6.5 %collective-permute-start.20 = (f32[1,4,1,32,64]{4,3,2,1,0:T(8,128)S(1)}, f32[1,4,1,32,64]{4,3,2,1,0:T(8,128)S(1)}, u32[]{:S(2)}, u32[]{:S(2)}) collective-permute-start(f32[1,4,1,32,64]{4,3,2,1,0:T(8,128)S(1)} %get-tuple-element.106), channel_id=1, source_target_pairs={{0,1},{1,2},{2,3},{4,5},{5,6},{6,7},{8,9},{9,10},{10,11},{12,13},{... | collective-permute-start | bytes 98312 | tf_op jit(solution)/shard_map/ppermute | solution.py:23
  223.7 8.4 %collective-permute-start.18 = (f32[1,4,2,32,64]{4,3,2,1,0:T(8,128)S(1)}, f32[1,4,2,32,64]{4,3,2,1,0:T(8,128)S(1)}, u32[]{:S(2)}, u32[]{:S(2)}) collective-permute-start(f32[1,4,2,32,64]{4,3,2,1,0:T(8,128)S(1)} %broadcast_add_fusion.1), channel_id=1, source_target_pairs={{0,4},{4,8},{8,12},{12,16},{16,20},{20,24},{24,28},{28,32},{32,36}... | collective-permute-start | bytes 196616 | tf_op jit(solution)/shard_map/ppermute | solution.py:34
  232.3 7.8 %collective-permute-start.22 = (f32[1,4,1,32,64]{4,3,2,1,0:T(8,128)S(1)}, f32[1,4,1,32,64]{4,3,2,1,0:T(8,128)S(1)}, u32[]{:S(2)}, u32[]{:S(2)}) collective-permute-start(f32[1,4,1,32,64]{4,3,2,1,0:T(8,128)S(1)} %get-tuple-element.101), channel_id=1, source_target_pairs={{1,0},{2,1},{3,2},{5,4},{6,5},{7,6},{9,8},{10,9},{11,10},{13,12},{... | collective-permute-start | bytes 98312 | tf_op jit(solution)/shard_map/ppermute | solution.py:26
  233.6 6.5 %collective-permute-start.23 = (f32[1,4,1,32,64]{4,3,2,1,0:T(8,128)S(1)}, f32[1,4,1,32,64]{4,3,2,1,0:T(8,128)S(1)}, u32[]{:S(2)}, u32[]{:S(2)}) collective-permute-start(f32[1,4,1,32,64]{4,3,2,1,0:T(8,128)S(1)} %get-tuple-element.102), channel_id=1, source_target_pairs={{0,1},{1,2},{2,3},{4,5},{5,6},{6,7},{8,9},{9,10},{10,11},{12,13},{... | collective-permute-start | bytes 98312 | tf_op jit(solution)/shard_map/ppermute | solution.py:23
  238.1 8.4 %collective-permute-start.21 = (f32[1,4,2,32,64]{4,3,2,1,0:T(8,128)S(1)}, f32[1,4,2,32,64]{4,3,2,1,0:T(8,128)S(1)}, u32[]{:S(2)}, u32[]{:S(2)}) collective-permute-start(f32[1,4,2,32,64]{4,3,2,1,0:T(8,128)S(1)} %fusion.227), channel_id=1, source_target_pairs={{0,4},{4,8},{8,12},{12,16},{16,20},{20,24},{24,28},{28,32},{32,36}... | collective-permute-start | bytes 196616 | tf_op jit(solution)/shard_map/ppermute | solution.py:34
  266.9 12.6 %collective-permute-start.24 = (f32[1,4,4,64,128]{4,3,2,1,0:T(8,128)S(1)}, f32[1,4,4,64,128]{4,3,2,1,0:T(8,128)S(1)}, u32[]{:S(2)}, u32[]{:S(2)}) collective-permute-start(f32[1,4,4,64,128]{4,3,2,1,0:T(8,128)S(1)} %add.510), channel_id=1, source_target_pairs={{0,4},{4,8},{8,12},{12,16},{16,20},{20,24},{24,28},{28,32},{32,36}... | collective-permute-start | bytes 1572872 | tf_op jit(solution)/shard_map/ppermute | solution.py:34
  268.9 6.9 %collective-permute-start.25 = (f32[1,4,1,64,128]{4,3,2,1,0:T(8,128)S(1)}, f32[1,4,1,64,128]{4,3,2,1,0:T(8,128)S(1)}, u32[]{:S(2)}, u32[]{:S(2)}) collective-permute-start(f32[1,4,1,64,128]{4,3,2,1,0:T(8,128)S(1)} %get-tuple-element.53), channel_id=1, source_target_pairs={{1,0},{2,1},{3,2},{5,4},{6,5},{7,6},{9,8},{10,9},{11,10},{13,12},{... | collective-permute-start | bytes 393224 | tf_op jit(solution)/shard_map/ppermute | solution.py:26
  270.2 7.1 %collective-permute-start.26 = (f32[1,4,1,64,128]{4,3,2,1,0:T(8,128)S(1)}, f32[1,4,1,64,128]{4,3,2,1,0:T(8,128)S(1)}, u32[]{:S(2)}, u32[]{:S(2)}) collective-permute-start(f32[1,4,1,64,128]{4,3,2,1,0:T(8,128)S(1)} %get-tuple-element.54), channel_id=1, source_target_pairs={{0,1},{1,2},{2,3},{4,5},{5,6},{6,7},{8,9},{9,10},{10,11},{12,13},{... | collective-permute-start | bytes 393224 | tf_op jit(solution)/shard_map/ppermute | solution.py:23
  280.1 12.6 %collective-permute-start.27 = (f32[1,4,4,64,128]{4,3,2,1,0:T(8,128)S(1)}, f32[1,4,4,64,128]{4,3,2,1,0:T(8,128)S(1)}, u32[]{:S(2)}, u32[]{:S(2)}) collective-permute-start(f32[1,4,4,64,128]{4,3,2,1,0:T(8,128)S(1)} %fusion.93), channel_id=1, source_target_pairs={{0,4},{4,8},{8,12},{12,16},{16,20},{20,24},{24,28},{28,32},{32,36}... | collective-permute-start | bytes 1572872 | tf_op jit(solution)/shard_map/ppermute | solution.py:34
  282.0 6.9 %collective-permute-start.28 = (f32[1,4,1,64,128]{4,3,2,1,0:T(8,128)S(1)}, f32[1,4,1,64,128]{4,3,2,1,0:T(8,128)S(1)}, u32[]{:S(2)}, u32[]{:S(2)}) collective-permute-start(f32[1,4,1,64,128]{4,3,2,1,0:T(8,128)S(1)} %get-tuple-element.49), channel_id=1, source_target_pairs={{1,0},{2,1},{3,2},{5,4},{6,5},{7,6},{9,8},{10,9},{11,10},{13,12},{... | collective-permute-start | bytes 393224 | tf_op jit(solution)/shard_map/ppermute | solution.py:26
  283.3 7.1 %collective-permute-start.29 = (f32[1,4,1,64,128]{4,3,2,1,0:T(8,128)S(1)}, f32[1,4,1,64,128]{4,3,2,1,0:T(8,128)S(1)}, u32[]{:S(2)}, u32[]{:S(2)}) collective-permute-start(f32[1,4,1,64,128]{4,3,2,1,0:T(8,128)S(1)} %get-tuple-element.50), channel_id=1, source_target_pairs={{0,1},{1,2},{2,3},{4,5},{5,6},{6,7},{8,9},{9,10},{10,11},{12,13},{... | collective-permute-start | bytes 393224 | tf_op jit(solution)/shard_map/ppermute | solution.py:23
  293.2 12.6 %collective-permute-start.30 = (f32[1,4,4,64,128]{4,3,2,1,0:T(8,128)S(1)}, f32[1,4,4,64,128]{4,3,2,1,0:T(8,128)S(1)}, u32[]{:S(2)}, u32[]{:S(2)}) collective-permute-start(f32[1,4,4,64,128]{4,3,2,1,0:T(8,128)S(1)} %fusion.79), channel_id=1, source_target_pairs={{0,4},{4,8},{8,12},{12,16},{16,20},{20,24},{24,28},{28,32},{32,36}... | collective-permute-start | bytes 1572872 | tf_op jit(solution)/shard_map/ppermute | solution.py:34
  295.2 6.9 %collective-permute-start.31 = (f32[1,4,1,64,128]{4,3,2,1,0:T(8,128)S(1)}, f32[1,4,1,64,128]{4,3,2,1,0:T(8,128)S(1)}, u32[]{:S(2)}, u32[]{:S(2)}) collective-permute-start(f32[1,4,1,64,128]{4,3,2,1,0:T(8,128)S(1)} %get-tuple-element.45), channel_id=1, source_target_pairs={{1,0},{2,1},{3,2},{5,4},{6,5},{7,6},{9,8},{10,9},{11,10},{13,12},{... | collective-permute-start | bytes 393224 | tf_op jit(solution)/shard_map/ppermute | solution.py:26
  296.5 7.1 %collective-permute-start.32 = (f32[1,4,1,64,128]{4,3,2,1,0:T(8,128)S(1)}, f32[1,4,1,64,128]{4,3,2,1,0:T(8,128)S(1)}, u32[]{:S(2)}, u32[]{:S(2)}) collective-permute-start(f32[1,4,1,64,128]{4,3,2,1,0:T(8,128)S(1)} %get-tuple-element.46), channel_id=1, source_target_pairs={{0,1},{1,2},{2,3},{4,5},{5,6},{6,7},{8,9},{9,10},{10,11},{12,13},{... | collective-permute-start | bytes 393224 | tf_op jit(solution)/shard_map/ppermute | solution.py:23
  306.4 12.6 %collective-permute-start.33 = (f32[1,4,4,64,128]{4,3,2,1,0:T(8,128)S(1)}, f32[1,4,4,64,128]{4,3,2,1,0:T(8,128)S(1)}, u32[]{:S(2)}, u32[]{:S(2)}) collective-permute-start(f32[1,4,4,64,128]{4,3,2,1,0:T(8,128)S(1)} %fusion.65), channel_id=1, source_target_pairs={{0,4},{4,8},{8,12},{12,16},{16,20},{20,24},{24,28},{28,32},{32,36}... | collective-permute-start | bytes 1572872 | tf_op jit(solution)/shard_map/ppermute | solution.py:34
  308.3 6.9 %collective-permute-start.34 = (f32[1,4,1,64,128]{4,3,2,1,0:T(8,128)S(1)}, f32[1,4,1,64,128]{4,3,2,1,0:T(8,128)S(1)}, u32[]{:S(2)}, u32[]{:S(2)}) collective-permute-start(f32[1,4,1,64,128]{4,3,2,1,0:T(8,128)S(1)} %get-tuple-element.41), channel_id=1, source_target_pairs={{1,0},{2,1},{3,2},{5,4},{6,5},{7,6},{9,8},{10,9},{11,10},{13,12},{... | collective-permute-start | bytes 393224 | tf_op jit(solution)/shard_map/ppermute | solution.py:26
  309.6 7.1 %collective-permute-start.35 = (f32[1,4,1,64,128]{4,3,2,1,0:T(8,128)S(1)}, f32[1,4,1,64,128]{4,3,2,1,0:T(8,128)S(1)}, u32[]{:S(2)}, u32[]{:S(2)}) collective-permute-start(f32[1,4,1,64,128]{4,3,2,1,0:T(8,128)S(1)} %get-tuple-element.42), channel_id=1, source_target_pairs={{0,1},{1,2},{2,3},{4,5},{5,6},{6,7},{8,9},{9,10},{10,11},{12,13},{... | collective-permute-start | bytes 393224 | tf_op jit(solution)/shard_map/ppermute | solution.py:23
  319.5 12.6 %collective-permute-start.36 = (f32[1,4,4,64,128]{4,3,2,1,0:T(8,128)S(1)}, f32[1,4,4,64,128]{4,3,2,1,0:T(8,128)S(1)}, u32[]{:S(2)}, u32[]{:S(2)}) collective-permute-start(f32[1,4,4,64,128]{4,3,2,1,0:T(8,128)S(1)} %fusion.51), channel_id=1, source_target_pairs={{0,4},{4,8},{8,12},{12,16},{16,20},{20,24},{24,28},{28,32},{32,36}... | collective-permute-start | bytes 1572872 | tf_op jit(solution)/shard_map/ppermute | solution.py:34
  321.5 6.9 %collective-permute-start.37 = (f32[1,4,1,64,128]{4,3,2,1,0:T(8,128)S(1)}, f32[1,4,1,64,128]{4,3,2,1,0:T(8,128)S(1)}, u32[]{:S(2)}, u32[]{:S(2)}) collective-permute-start(f32[1,4,1,64,128]{4,3,2,1,0:T(8,128)S(1)} %get-tuple-element.37), channel_id=1, source_target_pairs={{1,0},{2,1},{3,2},{5,4},{6,5},{7,6},{9,8},{10,9},{11,10},{13,12},{... | collective-permute-start | bytes 393224 | tf_op jit(solution)/shard_map/ppermute | solution.py:26
  322.8 7.1 %collective-permute-start.38 = (f32[1,4,1,64,128]{4,3,2,1,0:T(8,128)S(1)}, f32[1,4,1,64,128]{4,3,2,1,0:T(8,128)S(1)}, u32[]{:S(2)}, u32[]{:S(2)}) collective-permute-start(f32[1,4,1,64,128]{4,3,2,1,0:T(8,128)S(1)} %get-tuple-element.38), channel_id=1, source_target_pairs={{0,1},{1,2},{2,3},{4,5},{5,6},{6,7},{8,9},{9,10},{10,11},{12,13},{... | collective-permute-start | bytes 393224 | tf_op jit(solution)/shard_map/ppermute | solution.py:23
  354.6 15.3 %copy-start.3 = (f32[4,2,32,64]{3,2,1,0:T(8,128)S(1)}, f32[4,2,32,64]{3,2,1,0:T(8,128)}, u32[]{:S(2)}) copy-start(f32[4,2,32,64]{3,2,1,0:T(8,128)} %copy.404) | copy-start | bytes 196612
  355.6 29.5 %copy-start.5 = (f32[2,32,64]{2,1,0:T(8,128)S(1)}, f32[2,32,64]{2,1,0:T(8,128)}, u32[]{:S(2)}) copy-start(f32[2,32,64]{2,1,0:T(8,128)} %get-tuple-element.123) | copy-start | bytes 49156
  355.6 7.8 %collective-permute-start.40 = (f32[1,4,1,32,64]{4,3,2,1,0:T(8,128)S(1)}, f32[1,4,1,32,64]{4,3,2,1,0:T(8,128)S(1)}, u32[]{:S(2)}, u32[]{:S(2)}) collective-permute-start(f32[1,4,1,32,64]{4,3,2,1,0:T(8,128)S(1)} %get-tuple-element.97), channel_id=1, source_target_pairs={{1,0},{2,1},{3,2},{5,4},{6,5},{7,6},{9,8},{10,9},{11,10},{13,12},{... | collective-permute-start | bytes 98312 | tf_op jit(solution)/shard_map/ppermute | solution.py:26
  356.9 6.5 %collective-permute-start.41 = (f32[1,4,1,32,64]{4,3,2,1,0:T(8,128)S(1)}, f32[1,4,1,32,64]{4,3,2,1,0:T(8,128)S(1)}, u32[]{:S(2)}, u32[]{:S(2)}) collective-permute-start(f32[1,4,1,32,64]{4,3,2,1,0:T(8,128)S(1)} %get-tuple-element.98), channel_id=1, source_target_pairs={{0,1},{1,2},{2,3},{4,5},{5,6},{6,7},{8,9},{9,10},{10,11},{12,13},{... | collective-permute-start | bytes 98312 | tf_op jit(solution)/shard_map/ppermute | solution.py:23
  361.5 8.4 %collective-permute-start.39 = (f32[1,4,2,32,64]{4,3,2,1,0:T(8,128)S(1)}, f32[1,4,2,32,64]{4,3,2,1,0:T(8,128)S(1)}, u32[]{:S(2)}, u32[]{:S(2)}) collective-permute-start(f32[1,4,2,32,64]{4,3,2,1,0:T(8,128)S(1)} %fusion.397), channel_id=1, source_target_pairs={{0,4},{4,8},{8,12},{12,16},{16,20},{20,24},{24,28},{28,32},{32,36}... | collective-permute-start | bytes 196616 | tf_op jit(solution)/shard_map/ppermute | solution.py:34
  370.8 7.8 %collective-permute-start.43 = (f32[1,4,1,32,64]{4,3,2,1,0:T(8,128)S(1)}, f32[1,4,1,32,64]{4,3,2,1,0:T(8,128)S(1)}, u32[]{:S(2)}, u32[]{:S(2)}) collective-permute-start(f32[1,4,1,32,64]{4,3,2,1,0:T(8,128)S(1)} %get-tuple-element.93), channel_id=1, source_target_pairs={{1,0},{2,1},{3,2},{5,4},{6,5},{7,6},{9,8},{10,9},{11,10},{13,12},{... | collective-permute-start | bytes 98312 | tf_op jit(solution)/shard_map/ppermute | solution.py:26
  372.1 6.5 %collective-permute-start.44 = (f32[1,4,1,32,64]{4,3,2,1,0:T(8,128)S(1)}, f32[1,4,1,32,64]{4,3,2,1,0:T(8,128)S(1)}, u32[]{:S(2)}, u32[]{:S(2)}) collective-permute-start(f32[1,4,1,32,64]{4,3,2,1,0:T(8,128)S(1)} %get-tuple-element.94), channel_id=1, source_target_pairs={{0,1},{1,2},{2,3},{4,5},{5,6},{6,7},{8,9},{9,10},{10,11},{12,13},{... | collective-permute-start | bytes 98312 | tf_op jit(solution)/shard_map/ppermute | solution.py:23
  376.7 8.4 %collective-permute-start.42 = (f32[1,4,2,32,64]{4,3,2,1,0:T(8,128)S(1)}, f32[1,4,2,32,64]{4,3,2,1,0:T(8,128)S(1)}, u32[]{:S(2)}, u32[]{:S(2)}) collective-permute-start(f32[1,4,2,32,64]{4,3,2,1,0:T(8,128)S(1)} %fusion.197), channel_id=1, source_target_pairs={{0,4},{4,8},{8,12},{12,16},{16,20},{20,24},{24,28},{28,32},{32,36}... | collective-permute-start | bytes 196616 | tf_op jit(solution)/shard_map/ppermute | solution.py:34
  474.8 7.8 %collective-permute-start.46 = (f32[1,4,1,32,64]{4,3,2,1,0:T(8,128)S(1)}, f32[1,4,1,32,64]{4,3,2,1,0:T(8,128)S(1)}, u32[]{:S(2)}, u32[]{:S(2)}) collective-permute-start(f32[1,4,1,32,64]{4,3,2,1,0:T(8,128)S(1)} %get-tuple-element.89), channel_id=1, source_target_pairs={{1,0},{2,1},{3,2},{5,4},{6,5},{7,6},{9,8},{10,9},{11,10},{13,12},{... | collective-permute-start | bytes 98312 | tf_op jit(solution)/shard_map/ppermute | solution.py:26
  476.1 6.5 %collective-permute-start.47 = (f32[1,4,1,32,64]{4,3,2,1,0:T(8,128)S(1)}, f32[1,4,1,32,64]{4,3,2,1,0:T(8,128)S(1)}, u32[]{:S(2)}, u32[]{:S(2)}) collective-permute-start(f32[1,4,1,32,64]{4,3,2,1,0:T(8,128)S(1)} %get-tuple-element.90), channel_id=1, source_target_pairs={{0,1},{1,2},{2,3},{4,5},{5,6},{6,7},{8,9},{9,10},{10,11},{12,13},{... | collective-permute-start | bytes 98312 | tf_op jit(solution)/shard_map/ppermute | solution.py:23
  480.7 8.4 %collective-permute-start.45 = (f32[1,4,2,32,64]{4,3,2,1,0:T(8,128)S(1)}, f32[1,4,2,32,64]{4,3,2,1,0:T(8,128)S(1)}, u32[]{:S(2)}, u32[]{:S(2)}) collective-permute-start(f32[1,4,2,32,64]{4,3,2,1,0:T(8,128)S(1)} %broadcast_add_fusion), channel_id=1, source_target_pairs={{0,4},{4,8},{8,12},{12,16},{16,20},{20,24},{24,28},{28,32},{32,36}... | collective-permute-start | bytes 196616 | tf_op jit(solution)/shard_map/ppermute | solution.py:34
  489.3 7.8 %collective-permute-start.49 = (f32[1,4,1,32,64]{4,3,2,1,0:T(8,128)S(1)}, f32[1,4,1,32,64]{4,3,2,1,0:T(8,128)S(1)}, u32[]{:S(2)}, u32[]{:S(2)}) collective-permute-start(f32[1,4,1,32,64]{4,3,2,1,0:T(8,128)S(1)} %get-tuple-element.85), channel_id=1, source_target_pairs={{1,0},{2,1},{3,2},{5,4},{6,5},{7,6},{9,8},{10,9},{11,10},{13,12},{... | collective-permute-start | bytes 98312 | tf_op jit(solution)/shard_map/ppermute | solution.py:26
  490.6 6.5 %collective-permute-start.50 = (f32[1,4,1,32,64]{4,3,2,1,0:T(8,128)S(1)}, f32[1,4,1,32,64]{4,3,2,1,0:T(8,128)S(1)}, u32[]{:S(2)}, u32[]{:S(2)}) collective-permute-start(f32[1,4,1,32,64]{4,3,2,1,0:T(8,128)S(1)} %get-tuple-element.86), channel_id=1, source_target_pairs={{0,1},{1,2},{2,3},{4,5},{5,6},{6,7},{8,9},{9,10},{10,11},{12,13},{... | collective-permute-start | bytes 98312 | tf_op jit(solution)/shard_map/ppermute | solution.py:23
  495.1 8.4 %collective-permute-start.48 = (f32[1,4,2,32,64]{4,3,2,1,0:T(8,128)S(1)}, f32[1,4,2,32,64]{4,3,2,1,0:T(8,128)S(1)}, u32[]{:S(2)}, u32[]{:S(2)}) collective-permute-start(f32[1,4,2,32,64]{4,3,2,1,0:T(8,128)S(1)} %fusion.169), channel_id=1, source_target_pairs={{0,4},{4,8},{8,12},{12,16},{16,20},{20,24},{24,28},{28,32},{32,36}... | collective-permute-start | bytes 196616 | tf_op jit(solution)/shard_map/ppermute | solution.py:34
  523.9 12.6 %collective-permute-start.51 = (f32[1,4,4,64,128]{4,3,2,1,0:T(8,128)S(1)}, f32[1,4,4,64,128]{4,3,2,1,0:T(8,128)S(1)}, u32[]{:S(2)}, u32[]{:S(2)}) collective-permute-start(f32[1,4,4,64,128]{4,3,2,1,0:T(8,128)S(1)} %add.555), channel_id=1, source_target_pairs={{0,4},{4,8},{8,12},{12,16},{16,20},{20,24},{24,28},{28,32},{32,36}... | collective-permute-start | bytes 1572872 | tf_op jit(solution)/shard_map/ppermute | solution.py:34
  525.9 6.9 %collective-permute-start.52 = (f32[1,4,1,64,128]{4,3,2,1,0:T(8,128)S(1)}, f32[1,4,1,64,128]{4,3,2,1,0:T(8,128)S(1)}, u32[]{:S(2)}, u32[]{:S(2)}) collective-permute-start(f32[1,4,1,64,128]{4,3,2,1,0:T(8,128)S(1)} %get-tuple-element.33), channel_id=1, source_target_pairs={{1,0},{2,1},{3,2},{5,4},{6,5},{7,6},{9,8},{10,9},{11,10},{13,12},{... | collective-permute-start | bytes 393224 | tf_op jit(solution)/shard_map/ppermute | solution.py:26
  527.2 7.1 %collective-permute-start.53 = (f32[1,4,1,64,128]{4,3,2,1,0:T(8,128)S(1)}, f32[1,4,1,64,128]{4,3,2,1,0:T(8,128)S(1)}, u32[]{:S(2)}, u32[]{:S(2)}) collective-permute-start(f32[1,4,1,64,128]{4,3,2,1,0:T(8,128)S(1)} %get-tuple-element.34), channel_id=1, source_target_pairs={{0,1},{1,2},{2,3},{4,5},{5,6},{6,7},{8,9},{9,10},{10,11},{12,13},{... | collective-permute-start | bytes 393224 | tf_op jit(solution)/shard_map/ppermute | solution.py:23
  537.1 12.6 %collective-permute-start.54 = (f32[1,4,4,64,128]{4,3,2,1,0:T(8,128)S(1)}, f32[1,4,4,64,128]{4,3,2,1,0:T(8,128)S(1)}, u32[]{:S(2)}, u32[]{:S(2)}) collective-permute-start(f32[1,4,4,64,128]{4,3,2,1,0:T(8,128)S(1)} %fusion.25), channel_id=1, source_target_pairs={{0,4},{4,8},{8,12},{12,16},{16,20},{20,24},{24,28},{28,32},{32,36}... | collective-permute-start | bytes 1572872 | tf_op jit(solution)/shard_map/ppermute | solution.py:34
  539.0 6.9 %collective-permute-start.55 = (f32[1,4,1,64,128]{4,3,2,1,0:T(8,128)S(1)}, f32[1,4,1,64,128]{4,3,2,1,0:T(8,128)S(1)}, u32[]{:S(2)}, u32[]{:S(2)}) collective-permute-start(f32[1,4,1,64,128]{4,3,2,1,0:T(8,128)S(1)} %get-tuple-element.29), channel_id=1, source_target_pairs={{1,0},{2,1},{3,2},{5,4},{6,5},{7,6},{9,8},{10,9},{11,10},{13,12},{... | collective-permute-start | bytes 393224 | tf_op jit(solution)/shard_map/ppermute | solution.py:26
  540.3 7.1 %collective-permute-start.56 = (f32[1,4,1,64,128]{4,3,2,1,0:T(8,128)S(1)}, f32[1,4,1,64,128]{4,3,2,1,0:T(8,128)S(1)}, u32[]{:S(2)}, u32[]{:S(2)}) collective-permute-start(f32[1,4,1,64,128]{4,3,2,1,0:T(8,128)S(1)} %get-tuple-element.30), channel_id=1, source_target_pairs={{0,1},{1,2},{2,3},{4,5},{5,6},{6,7},{8,9},{9,10},{10,11},{12,13},{... | collective-permute-start | bytes 393224 | tf_op jit(solution)/shard_map/ppermute | solution.py:23
  (7 other events, 48.0 us)
Sparse Core Ops, SparseCore 0:
  136.9 39.3 all-gather.6
  400.0 39.2 all-gather.8

commit v4 on v3

--- a/solution.py
+++ b/solution.py
@@ -77,24 +77,30 @@
     return jnp.stack([moving, walled, walled, jnp.zeros_like(walled)], axis=0)[None]
 
 
+def pair_matrix(wide):
+    fine = lax.broadcasted_iota(jnp.int32, (wide, wide // 2), 0)
+    coarse = lax.broadcasted_iota(jnp.int32, (wide, wide // 2), 1)
+    return (fine // 2 == coarse).astype(jnp.float32)
+
+
 def restrict(values):
-    dims_all = values.shape
-    leading = dims_all[:-3]
-    depth_x, height_y, width_z = dims_all[-3:]
-    blocks = values.reshape(leading + (depth_x // 2, 2, height_y // 2, 2, width_z // 2, 2))
-    offset = len(leading)
-    return jnp.sum(blocks, axis=(offset + 1, offset + 3, offset + 5)) * 0.125
+    summed = values[..., 0::2, :, :] + values[..., 1::2, :, :]
+    summed = summed[..., 0::2, :] + summed[..., 1::2, :]
+    summed = jnp.einsum(
+        "...z,zw->...w", summed, pair_matrix(summed.shape[-1]), precision=lax.Precision.HIGHEST
+    )
+    return summed * 0.125
 
 
 def prolong(values):
-    dims_all = values.shape
-    leading = dims_all[:-3]
-    depth_x, height_y, width_z = dims_all[-3:]
-    spread = jnp.broadcast_to(
-        values.reshape(leading + (depth_x, 1, height_y, 1, width_z, 1)),
-        leading + (depth_x, 2, height_y, 2, width_z, 2),
-    )
-    return spread.reshape(leading + (2 * depth_x, 2 * height_y, 2 * width_z))
+    spread = jnp.einsum(
+        "...w,zw->...z",
+        values,
+        pair_matrix(2 * values.shape[-1]),
+        precision=lax.Precision.HIGHEST,
+    )
+    spread = jnp.repeat(spread, 2, axis=-2)
+    return jnp.repeat(spread, 2, axis=-3)
 
 
 def coarse_kernel(src_ref, met_ref, out_ref, *, spacing, depth_x, height_y, width_z):

time: 561 us -> 461 us (0.82)
  local copies, waits for them, and re-layouts: 118 us -> 43.1 us
  other arithmetic: 49.2 us -> 12 us
  waiting for transfers between devices: 170 us -> 179 us
    broadcast_in_dim x14 -> x6, local copies, waits for them, and re-layouts: 42.5 us -> 0.32 us  [the longest x4 0.23 us: prolong(): spread = jnp.repeat(spread, 2, axis=-2)]
    reduce_sum x9 -> x0, other arithmetic: 30.3 us -> none  [restrict(): return jnp.sum(blocks, axis=(offset + 1, offset + 3, offset + 5)) * 0.125]
    sub x2 -> x0, local copies, waits for them, and re-layouts: 17.7 us -> none  [cycle(): source - apply_local(values, metrics[depth], spacing, pinned_levels[depth])]
    reshape x1 -> x2, local copies, waits for them, and re-layouts: 9.82 us -> 0.17 us  [the longest x1 0.09 us: coarse_correction(): both = jnp.concatenate([source_flat, metric_two.reshape(1, -1)], axis=1)]
    ppermute x19, waiting for transfers between devices: 72.2 us -> 78.5 us  [from_behind(): return lax.ppermute(array, axis, pairs)]
  transfers between devices with their start and end apart: 59 -> 59, of which waited for: 33 -> 39; matrix products, arithmetic and copies ran while one was open for 8% -> 2% of each run, Pallas kernels for 0% -> 0%
where the time goes in v4:
time: 461 us; the launch traced here: 459 us
  waiting for transfers between devices  179 us (39%)
  starting transfers between devices  148 us (32%)
  local copies, waits for them, and re-layouts  43.1 us (9%)
  Pallas kernels  32.1 us (7%)
  blocking collectives  25.6 us (6%)
  between operations  14.8 us (3%)
  other arithmetic  12 us (3%)
    ppermute x19, starting transfers between devices, with_halo(): lax.ppermute(lax.slice_in_dim(block, block.shape[dim] - width, None, axis...  87.1 us
    all_gather x2, waiting for transfers between devices, gather_all(): return lax.all_gather(within, 'tm', axis=0, tiled=True)  78.8 us
    ppermute x19, waiting for transfers between devices, from_behind(): return lax.ppermute(array, axis, pairs)  78.5 us
    ppermute x19, starting transfers between devices, from_behind(): return lax.ppermute(array, axis, pairs)  36.7 us
    pallas_call x2, Pallas kernels, coarse_solve(): pl.pallas_call(kernel, out_shape=jax.ShapeDtypeStruct(flat_source.shape,...  32.1 us
    all_gather x2, blocking collectives, gather_all(): within = lax.all_gather(flat, 'space', axis=0, tiled=True)  25.6 us
    ppermute x19, starting transfers between devices, with_halo(): lax.ppermute(lax.slice_in_dim(block, 0, width, axis=dim), axis, backward)  24.6 us
    ppermute x19, waiting for transfers between devices, with_halo(): lax.ppermute(lax.slice_in_dim(block, block.shape[dim] - width, None, axis...  12.1 us
  transfers between devices with their start and end apart: 59, of which 39 were waited for; matrix products, arithmetic and copies ran while one was open for 2% of the time, Pallas kernels for 0%

profile of v4, /device:TPU:2, one launch (start us, length us, event | category | flops | bytes accessed | tf_op | source)
XLA Modules:
  0.0 459.3 jit_solution(12222075433451117610)
XLA Ops:
  6.5 4.0 collective-permute-start.11
  11.8 4.6 collective-permute-start.2
  17.7 1.9 collective-permute-start
  23.5 6.9 %collective-permute-done = f32[1,4,4,64,128]{4,3,2,1,0:T(8,128)S(1)} collective-permute-done((f32[1,4,4,64,128]{4,3,2,1,0:T(8,128)S(1)}, f32[1,4,4,64,128]{4,3,2,1,0:T(8,128)S(1)}, u32[]{:S(2)}, u32[]{:S(2)}) %collective-permute-start) | collective-permute-done | bytes 524320 | tf_op jit(solution)/shard_map/ppermute | solution.py:34
  30.8 1.9 collective-permute-start.3
  34.1 5.2 %collective-permute-start.5 = (f32[1,4,1,64,128]{4,3,2,1,0:T(8,128)S(1)}, f32[1,4,1,64,128]{4,3,2,1,0:T(8,128)S(1)}, u32[]{:S(2)}, u32[]{:S(2)}) collective-permute-start(f32[1,4,1,64,128]{4,3,2,1,0:T(8,128)S(1)} %get-tuple-element.62), channel_id=1, source_target_pairs={{0,1},{1,2},{2,3},{4,5},{5,6},{6,7},{8,9},{9,10},{10,11},{12,13},{... | collective-permute-start | bytes 393224 | tf_op jit(solution)/shard_map/ppermute | solution.py:23
  44.0 1.9 collective-permute-start.6
  47.3 5.2 %collective-permute-start.8 = (f32[1,4,1,64,128]{4,3,2,1,0:T(8,128)S(1)}, f32[1,4,1,64,128]{4,3,2,1,0:T(8,128)S(1)}, u32[]{:S(2)}, u32[]{:S(2)}) collective-permute-start(f32[1,4,1,64,128]{4,3,2,1,0:T(8,128)S(1)} %get-tuple-element.58), channel_id=1, source_target_pairs={{0,1},{1,2},{2,3},{4,5},{5,6},{6,7},{8,9},{9,10},{10,11},{12,13},{... | collective-permute-start | bytes 393224 | tf_op jit(solution)/shard_map/ppermute | solution.py:23
  52.5 1.9 collective-permute-start.9
  57.4 3.5 collective-permute-done.9
  63.1 4.5 collective-permute-start.14
  69.7 6.3 %collective-permute-done.12 = f32[1,4,2,32,64]{4,3,2,1,0:T(8,128)S(1)} collective-permute-done((f32[1,4,2,32,64]{4,3,2,1,0:T(8,128)S(1)}, f32[1,4,2,32,64]{4,3,2,1,0:T(8,128)S(1)}, u32[]{:S(2)}, u32[]{:S(2)}) %collective-permute-start.12) | collective-permute-done | bytes 65568 | tf_op jit(solution)/shard_map/ppermute | solution.py:34
  77.6 4.5 collective-permute-start.17
  82.3 1.9 collective-permute-start.15
  84.4 6.3 %collective-permute-done.15 = f32[1,4,2,32,64]{4,3,2,1,0:T(8,128)S(1)} collective-permute-done((f32[1,4,2,32,64]{4,3,2,1,0:T(8,128)S(1)}, f32[1,4,2,32,64]{4,3,2,1,0:T(8,128)S(1)}, u32[]{:S(2)}, u32[]{:S(2)}) %collective-permute-start.15) | collective-permute-done | bytes 65568 | tf_op jit(solution)/shard_map/ppermute | solution.py:34
  91.4 13.2 %all-gather = f32[4,1,2560]{2,1,0:T(1,128)S(1)} all-gather(f32[1,1,2560]{2,1,0:T(1,128)S(1)} %maximum_bitcast_fusion), channel_id=1, replica_groups=mesh['tm'=32,'space'=4] {'space'}, dimensions={0}, use_global_device_ids=true | all-gather | bytes 51200 | tf_op jit(solution)/shard_map/all_gather | solution.py:194
  105.3 39.5 %all-gather.7.cloned.1.call-done = f32[32,4,2560]{2,1,0:T(4,128)} async-done(((f32[1,4,2560]{2,1,0:T(4,128)}), f32[32,4,2560]{2,1,0:T(4,128)}) %all-gather.7.cloned.1.call-update) | async-done | bytes 1310736 | tf_op jit(solution)/shard_map/all_gather | solution.py:195
  150.9 2.8 reshape.914
  153.6 4.9 %copy.7 = f32[32,1,4,4,1,16,32]{6,5,3,2,0,4,1:T(8,128)} copy(f32[32,1,4,4,1,16,32]{6,5,2,3,0,4,1:T(8,128)} %bitcast.92) | data formatting | bytes 2097152 | tf_op jit(solution)/shard_map/transpose | solution.py:181
  158.5 4.4 reshape_reshape.6.src_ref
  162.9 16.1 %shard_map.37 = f32[32,16,512]{2,1,0:T(8,128)} custom-call(f32[32,16,512]{2,1,0:T(8,128)} %reshape_reshape.6.src_ref, f32[32,16,512]{2,1,0:T(8,128)} %tile.16.met_ref), custom_call_target="tpu_custom_call" | custom-call | tf_op jit(solution)/shard_map/pallas_call | solution.py:162
  178.9 3.8 reshape.915
  185.1 4.5 collective-permute-start.20
  189.7 1.9 collective-permute-start.18
  191.7 6.3 %collective-permute-done.18 = f32[1,4,2,32,64]{4,3,2,1,0:T(8,128)S(1)} collective-permute-done((f32[1,4,2,32,64]{4,3,2,1,0:T(8,128)S(1)}, f32[1,4,2,32,64]{4,3,2,1,0:T(8,128)S(1)}, u32[]{:S(2)}, u32[]{:S(2)}) %collective-permute-start.18) | collective-permute-done | bytes 65568 | tf_op jit(solution)/shard_map/ppermute | solution.py:34
  199.6 4.5 collective-permute-start.23
  204.1 1.9 collective-permute-start.21
  206.2 6.3 %collective-permute-done.21 = f32[1,4,2,32,64]{4,3,2,1,0:T(8,128)S(1)} collective-permute-done((f32[1,4,2,32,64]{4,3,2,1,0:T(8,128)S(1)}, f32[1,4,2,32,64]{4,3,2,1,0:T(8,128)S(1)}, u32[]{:S(2)}, u32[]{:S(2)}) %collective-permute-start.21) | collective-permute-done | bytes 65568 | tf_op jit(solution)/shard_map/ppermute | solution.py:34
  216.3 4.6 collective-permute-start.26
  223.6 2.1 collective-permute-done.24
  226.2 2.1 collective-permute-start.27
  229.7 4.6 collective-permute-start.29
  239.4 1.9 collective-permute-start.30
  242.6 4.6 collective-permute-start.32
  249.9 2.1 collective-permute-done.30
  252.5 1.9 collective-permute-start.33
  255.8 4.6 collective-permute-start.35
  263.0 2.1 collective-permute-done.33
  265.7 1.9 collective-permute-start.36
  268.9 4.6 collective-permute-start.38
  276.2 2.1 collective-permute-done.36
  281.0 4.5 collective-permute-start.41
  285.5 1.9 collective-permute-start.39
  287.6 6.3 %collective-permute-done.39 = f32[1,4,2,32,64]{4,3,2,1,0:T(8,128)S(1)} collective-permute-done((f32[1,4,2,32,64]{4,3,2,1,0:T(8,128)S(1)}, f32[1,4,2,32,64]{4,3,2,1,0:T(8,128)S(1)}, u32[]{:S(2)}, u32[]{:S(2)}) %collective-permute-start.39) | collective-permute-done | bytes 65568 | tf_op jit(solution)/shard_map/ppermute | solution.py:34
  295.4 4.5 collective-permute-start.44
  299.9 1.9 collective-permute-start.42
  302.0 6.3 %collective-permute-done.42 = f32[1,4,2,32,64]{4,3,2,1,0:T(8,128)S(1)} collective-permute-done((f32[1,4,2,32,64]{4,3,2,1,0:T(8,128)S(1)}, f32[1,4,2,32,64]{4,3,2,1,0:T(8,128)S(1)}, u32[]{:S(2)}, u32[]{:S(2)}) %collective-permute-start.42) | collective-permute-done | bytes 65568 | tf_op jit(solution)/shard_map/ppermute | solution.py:34
  309.0 12.4 %all-gather.2 = f32[4,1,2048]{2,1,0:T(1,128)S(1)} all-gather(f32[1,1,2048]{2,1,0:T(1,128)S(1)} %reshape.933), channel_id=1, replica_groups=mesh['tm'=32,'space'=4] {'space'}, dimensions={0}, use_global_device_ids=true | all-gather | bytes 40960 | tf_op jit(solution)/shard_map/all_gather | solution.py:194
  322.0 39.4 %all-gather.9.cloned.1.call-done = f32[32,4,2048]{2,1,0:T(4,128)} async-done(((f32[1,4,2048]{2,1,0:T(4,128)}), f32[32,4,2048]{2,1,0:T(4,128)}) %all-gather.9.cloned.1.call-update) | async-done | bytes 1048592 | tf_op jit(solution)/shard_map/all_gather | solution.py:195
  363.2 2.8 reshape.922
  366.0 4.9 %copy.10 = f32[32,1,4,4,1,16,32]{6,5,3,2,0,4,1:T(8,128)} copy(f32[32,1,4,4,1,16,32]{6,5,2,0,3,4,1:T(8,128)} %bitcast.93) | data formatting | bytes 2097152 | tf_op jit(solution)/shard_map/transpose | solution.py:181
  370.9 4.4 reshape_reshape.7.src_ref
  375.3 16.1 %shard_map.38 = f32[32,16,512]{2,1,0:T(8,128)} custom-call(f32[32,16,512]{2,1,0:T(8,128)} %reshape_reshape.7.src_ref, f32[32,16,512]{2,1,0:T(8,128)} %tile.16.met_ref), custom_call_target="tpu_custom_call" | custom-call | tf_op jit(solution)/shard_map/pallas_call | solution.py:162
  391.3 3.8 reshape.923
  397.4 4.5 collective-permute-start.47
  402.0 1.9 collective-permute-start.45
  404.0 6.3 %collective-permute-done.45 = f32[1,4,2,32,64]{4,3,2,1,0:T(8,128)S(1)} collective-permute-done((f32[1,4,2,32,64]{4,3,2,1,0:T(8,128)S(1)}, f32[1,4,2,32,64]{4,3,2,1,0:T(8,128)S(1)}, u32[]{:S(2)}, u32[]{:S(2)}) %collective-permute-start.45) | collective-permute-done | bytes 65568 | tf_op jit(solution)/shard_map/ppermute | solution.py:34
  411.8 4.5 collective-permute-start.50
  416.4 1.9 collective-permute-start.48
  418.5 6.3 %collective-permute-done.48 = f32[1,4,2,32,64]{4,3,2,1,0:T(8,128)S(1)} collective-permute-done((f32[1,4,2,32,64]{4,3,2,1,0:T(8,128)S(1)}, f32[1,4,2,32,64]{4,3,2,1,0:T(8,128)S(1)}, u32[]{:S(2)}, u32[]{:S(2)}) %collective-permute-start.48) | collective-permute-done | bytes 65568 | tf_op jit(solution)/shard_map/ppermute | solution.py:34
  428.6 4.6 collective-permute-start.53
  435.9 2.1 collective-permute-done.51
  441.8 4.6 collective-permute-start.56
  449.0 2.1 collective-permute-done.54
  (219 shorter events, 86.4 us)
Async XLA Ops:
  6.5 138.3 %all-gather.7.cloned.1.call-start = ((), (), s32[]{:S(2)}) async-start(), calls=%async_computation | async-start | bytes 1351680 | tf_op jit(solution)/shard_map/all_gather | solution.py:195
  6.5 45.9 %collective-permute-start.11 = (f32[1,4,1,32,64]{4,3,2,1,0:T(8,128)S(1)}, f32[1,4,1,32,64]{4,3,2,1,0:T(8,128)S(1)}, u32[]{:S(2)}, u32[]{:S(2)}) collective-permute-start(f32[1,4,1,32,64]{4,3,2,1,0:T(8,128)S(1)} %broadcast.483), channel_id=1, source_target_pairs={{0,1},{1,2},{2,3},{4,5},{5,6},{6,7},{8,9},{9,10},{10,11},{12,13},{... | collective-permute-start | bytes 98312 | tf_op jit(solution)/shard_map/ppermute | solution.py:23
  10.5 43.9 %collective-permute-start.10 = (f32[1,4,1,32,64]{4,3,2,1,0:T(8,128)S(1)}, f32[1,4,1,32,64]{4,3,2,1,0:T(8,128)S(1)}, u32[]{:S(2)}, u32[]{:S(2)}) collective-permute-start(f32[1,4,1,32,64]{4,3,2,1,0:T(8,128)S(1)} %broadcast.483), channel_id=1, source_target_pairs={{1,0},{2,1},{3,2},{5,4},{6,5},{7,6},{9,8},{10,9},{11,10},{13,12},{... | collective-permute-start | bytes 98312 | tf_op jit(solution)/shard_map/ppermute | solution.py:26
  11.8 10.1 %collective-permute-start.2 = (f32[1,4,1,64,128]{4,3,2,1,0:T(8,128)S(1)}, f32[1,4,1,64,128]{4,3,2,1,0:T(8,128)S(1)}, u32[]{:S(2)}, u32[]{:S(2)}) collective-permute-start(f32[1,4,1,64,128]{4,3,2,1,0:T(8,128)S(1)} %broadcast.475), channel_id=1, source_target_pairs={{0,1},{1,2},{2,3},{4,5},{5,6},{6,7},{8,9},{9,10},{10,11},{12,13},{... | collective-permute-start | bytes 393224 | tf_op jit(solution)/shard_map/ppermute | solution.py:23
  16.4 6.9 %collective-permute-start.1 = (f32[1,4,1,64,128]{4,3,2,1,0:T(8,128)S(1)}, f32[1,4,1,64,128]{4,3,2,1,0:T(8,128)S(1)}, u32[]{:S(2)}, u32[]{:S(2)}) collective-permute-start(f32[1,4,1,64,128]{4,3,2,1,0:T(8,128)S(1)} %broadcast.475), channel_id=1, source_target_pairs={{1,0},{2,1},{3,2},{5,4},{6,5},{7,6},{9,8},{10,9},{11,10},{13,12},{... | collective-permute-start | bytes 393224 | tf_op jit(solution)/shard_map/ppermute | solution.py:26
  17.7 12.6 %collective-permute-start = (f32[1,4,4,64,128]{4,3,2,1,0:T(8,128)S(1)}, f32[1,4,4,64,128]{4,3,2,1,0:T(8,128)S(1)}, u32[]{:S(2)}, u32[]{:S(2)}) collective-permute-start(f32[1,4,4,64,128]{4,3,2,1,0:T(8,128)S(1)} %broadcast.473), channel_id=1, source_target_pairs={{0,4},{4,8},{8,12},{12,16},{16,20},{20,24},{24,28},{28,32},{32,36}... | collective-permute-start | bytes 1572872 | tf_op jit(solution)/shard_map/ppermute | solution.py:34
  21.8 39.1 %copy-start.13 = (s32[128]{0:T(128)}, s32[128]{0:T(128)S(1)}, u32[]{:S(2)}) copy-start(s32[128]{0:T(128)S(1)} %get-tuple-element.125) | copy-start | bytes 1540
  21.8 39.1 %copy-start.15 = (s32[128]{0:T(128)}, s32[128]{0:T(128)S(1)}, u32[]{:S(2)}) copy-start(s32[128]{0:T(128)S(1)} %get-tuple-element.126) | copy-start | bytes 1540
  21.9 54.1 %copy-start.9 = (f32[2,32,64]{2,1,0:T(8,128)}, f32[2,32,64]{2,1,0:T(8,128)S(1)}, u32[]{:S(2)}) copy-start(f32[2,32,64]{2,1,0:T(8,128)S(1)} %get-tuple-element.122) | copy-start | bytes 49156
  22.0 68.8 %copy-start.4 = (f32[2,32,64]{2,1,0:T(8,128)}, f32[2,32,64]{2,1,0:T(8,128)S(1)}, u32[]{:S(2)}) copy-start(f32[2,32,64]{2,1,0:T(8,128)S(1)} %get-tuple-element.123) | copy-start | bytes 49156
  30.8 12.6 %collective-permute-start.3 = (f32[1,4,4,64,128]{4,3,2,1,0:T(8,128)S(1)}, f32[1,4,4,64,128]{4,3,2,1,0:T(8,128)S(1)}, u32[]{:S(2)}, u32[]{:S(2)}) collective-permute-start(f32[1,4,4,64,128]{4,3,2,1,0:T(8,128)S(1)} %get-tuple-element.7), channel_id=1, source_target_pairs={{0,4},{4,8},{8,12},{12,16},{16,20},{20,24},{24,28},{28,32},{32,36}... | collective-permute-start | bytes 1572872 | tf_op jit(solution)/shard_map/ppermute | solution.py:34
  32.8 7.8 %collective-permute-start.4 = (f32[1,4,1,64,128]{4,3,2,1,0:T(8,128)S(1)}, f32[1,4,1,64,128]{4,3,2,1,0:T(8,128)S(1)}, u32[]{:S(2)}, u32[]{:S(2)}) collective-permute-start(f32[1,4,1,64,128]{4,3,2,1,0:T(8,128)S(1)} %get-tuple-element.61), channel_id=1, source_target_pairs={{1,0},{2,1},{3,2},{5,4},{6,5},{7,6},{9,8},{10,9},{11,10},{13,12},{... | collective-permute-start | bytes 393224 | tf_op jit(solution)/shard_map/ppermute | solution.py:26
  34.1 7.7 %collective-permute-start.5 = (f32[1,4,1,64,128]{4,3,2,1,0:T(8,128)S(1)}, f32[1,4,1,64,128]{4,3,2,1,0:T(8,128)S(1)}, u32[]{:S(2)}, u32[]{:S(2)}) collective-permute-start(f32[1,4,1,64,128]{4,3,2,1,0:T(8,128)S(1)} %get-tuple-element.62), channel_id=1, source_target_pairs={{0,1},{1,2},{2,3},{4,5},{5,6},{6,7},{8,9},{9,10},{10,11},{12,13},{... | collective-permute-start | bytes 393224 | tf_op jit(solution)/shard_map/ppermute | solution.py:23
  44.0 12.6 %collective-permute-start.6 = (f32[1,4,4,64,128]{4,3,2,1,0:T(8,128)S(1)}, f32[1,4,4,64,128]{4,3,2,1,0:T(8,128)S(1)}, u32[]{:S(2)}, u32[]{:S(2)}) collective-permute-start(f32[1,4,4,64,128]{4,3,2,1,0:T(8,128)S(1)} %fusion.121), channel_id=1, source_target_pairs={{0,4},{4,8},{8,12},{12,16},{16,20},{20,24},{24,28},{28,32},{32,36}... | collective-permute-start | bytes 1572872 | tf_op jit(solution)/shard_map/ppermute | solution.py:34
  46.0 8.6 %collective-permute-start.7 = (f32[1,4,1,64,128]{4,3,2,1,0:T(8,128)S(1)}, f32[1,4,1,64,128]{4,3,2,1,0:T(8,128)S(1)}, u32[]{:S(2)}, u32[]{:S(2)}) collective-permute-start(f32[1,4,1,64,128]{4,3,2,1,0:T(8,128)S(1)} %get-tuple-element.57), channel_id=1, source_target_pairs={{1,0},{2,1},{3,2},{5,4},{6,5},{7,6},{9,8},{10,9},{11,10},{13,12},{... | collective-permute-start | bytes 393224 | tf_op jit(solution)/shard_map/ppermute | solution.py:26
  47.3 7.7 %collective-permute-start.8 = (f32[1,4,1,64,128]{4,3,2,1,0:T(8,128)S(1)}, f32[1,4,1,64,128]{4,3,2,1,0:T(8,128)S(1)}, u32[]{:S(2)}, u32[]{:S(2)}) collective-permute-start(f32[1,4,1,64,128]{4,3,2,1,0:T(8,128)S(1)} %get-tuple-element.58), channel_id=1, source_target_pairs={{0,1},{1,2},{2,3},{4,5},{5,6},{6,7},{8,9},{9,10},{10,11},{12,13},{... | collective-permute-start | bytes 393224 | tf_op jit(solution)/shard_map/ppermute | solution.py:23
  52.5 8.4 %collective-permute-start.9 = (f32[1,4,2,32,64]{4,3,2,1,0:T(8,128)S(1)}, f32[1,4,2,32,64]{4,3,2,1,0:T(8,128)S(1)}, u32[]{:S(2)}, u32[]{:S(2)}) collective-permute-start(f32[1,4,2,32,64]{4,3,2,1,0:T(8,128)S(1)} %broadcast.482), channel_id=1, source_target_pairs={{0,4},{4,8},{8,12},{12,16},{16,20},{20,24},{24,28},{28,32},{32,36}... | collective-permute-start | bytes 196616 | tf_op jit(solution)/shard_map/ppermute | solution.py:34
  61.8 29.1 %copy-start.7 = (f32[1,4,2,32,64]{4,3,2,1,0:T(8,128)}, f32[1,4,2,32,64]{4,3,2,1,0:T(8,128)S(1)}, u32[]{:S(2)}) copy-start(f32[1,4,2,32,64]{4,3,2,1,0:T(8,128)S(1)} %get-tuple-element.124) | copy-start | bytes 196612
  61.8 7.8 %collective-permute-start.13 = (f32[1,4,1,32,64]{4,3,2,1,0:T(8,128)S(1)}, f32[1,4,1,32,64]{4,3,2,1,0:T(8,128)S(1)}, u32[]{:S(2)}, u32[]{:S(2)}) collective-permute-start(f32[1,4,1,32,64]{4,3,2,1,0:T(8,128)S(1)} %get-tuple-element.113), channel_id=1, source_target_pairs={{1,0},{2,1},{3,2},{5,4},{6,5},{7,6},{9,8},{10,9},{11,10},{13,12},{... | collective-permute-start | bytes 98312 | tf_op jit(solution)/shard_map/ppermute | solution.py:26
  63.1 6.5 %collective-permute-start.14 = (f32[1,4,1,32,64]{4,3,2,1,0:T(8,128)S(1)}, f32[1,4,1,32,64]{4,3,2,1,0:T(8,128)S(1)}, u32[]{:S(2)}, u32[]{:S(2)}) collective-permute-start(f32[1,4,1,32,64]{4,3,2,1,0:T(8,128)S(1)} %get-tuple-element.114), channel_id=1, source_target_pairs={{0,1},{1,2},{2,3},{4,5},{5,6},{6,7},{8,9},{9,10},{10,11},{12,13},{... | collective-permute-start | bytes 98312 | tf_op jit(solution)/shard_map/ppermute | solution.py:23
  67.7 8.4 %collective-permute-start.12 = (f32[1,4,2,32,64]{4,3,2,1,0:T(8,128)S(1)}, f32[1,4,2,32,64]{4,3,2,1,0:T(8,128)S(1)}, u32[]{:S(2)}, u32[]{:S(2)}) collective-permute-start(f32[1,4,2,32,64]{4,3,2,1,0:T(8,128)S(1)} %get-tuple-element.5), channel_id=1, source_target_pairs={{0,4},{4,8},{8,12},{12,16},{16,20},{20,24},{24,28},{28,32},{32,36}... | collective-permute-start | bytes 196616 | tf_op jit(solution)/shard_map/ppermute | solution.py:34
  76.3 8.0 %collective-permute-start.16 = (f32[1,4,1,32,64]{4,3,2,1,0:T(8,128)S(1)}, f32[1,4,1,32,64]{4,3,2,1,0:T(8,128)S(1)}, u32[]{:S(2)}, u32[]{:S(2)}) collective-permute-start(f32[1,4,1,32,64]{4,3,2,1,0:T(8,128)S(1)} %get-tuple-element.109), channel_id=1, source_target_pairs={{1,0},{2,1},{3,2},{5,4},{6,5},{7,6},{9,8},{10,9},{11,10},{13,12},{... | collective-permute-start | bytes 98312 | tf_op jit(solution)/shard_map/ppermute | solution.py:26
  77.6 6.7 %collective-permute-start.17 = (f32[1,4,1,32,64]{4,3,2,1,0:T(8,128)S(1)}, f32[1,4,1,32,64]{4,3,2,1,0:T(8,128)S(1)}, u32[]{:S(2)}, u32[]{:S(2)}) collective-permute-start(f32[1,4,1,32,64]{4,3,2,1,0:T(8,128)S(1)} %get-tuple-element.110), channel_id=1, source_target_pairs={{0,1},{1,2},{2,3},{4,5},{5,6},{6,7},{8,9},{9,10},{10,11},{12,13},{... | collective-permute-start | bytes 98312 | tf_op jit(solution)/shard_map/ppermute | solution.py:23
  82.3 8.4 %collective-permute-start.15 = (f32[1,4,2,32,64]{4,3,2,1,0:T(8,128)S(1)}, f32[1,4,2,32,64]{4,3,2,1,0:T(8,128)S(1)}, u32[]{:S(2)}, u32[]{:S(2)}) collective-permute-start(f32[1,4,2,32,64]{4,3,2,1,0:T(8,128)S(1)} %fusion.255), channel_id=1, source_target_pairs={{0,4},{4,8},{8,12},{12,16},{16,20},{20,24},{24,28},{28,32},{32,36}... | collective-permute-start | bytes 196616 | tf_op jit(solution)/shard_map/ppermute | solution.py:34
  105.3 256.1 %all-gather.9.cloned.1.call-start = ((), (), s32[]{:S(2)}) async-start(), calls=%async_computation.1 | async-start | bytes 1081344 | tf_op jit(solution)/shard_map/all_gather | solution.py:195
  183.8 7.8 %collective-permute-start.19 = (f32[1,4,1,32,64]{4,3,2,1,0:T(8,128)S(1)}, f32[1,4,1,32,64]{4,3,2,1,0:T(8,128)S(1)}, u32[]{:S(2)}, u32[]{:S(2)}) collective-permute-start(f32[1,4,1,32,64]{4,3,2,1,0:T(8,128)S(1)} %get-tuple-element.105), channel_id=1, source_target_pairs={{1,0},{2,1},{3,2},{5,4},{6,5},{7,6},{9,8},{10,9},{11,10},{13,12},{... | collective-permute-start | bytes 98312 | tf_op jit(solution)/shard_map/ppermute | solution.py:26
  185.1 6.5 %collective-permute-start.20 = (f32[1,4,1,32,64]{4,3,2,1,0:T(8,128)S(1)}, f32[1,4,1,32,64]{4,3,2,1,0:T(8,128)S(1)}, u32[]{:S(2)}, u32[]{:S(2)}) collective-permute-start(f32[1,4,1,32,64]{4,3,2,1,0:T(8,128)S(1)} %get-tuple-element.106), channel_id=1, source_target_pairs={{0,1},{1,2},{2,3},{4,5},{5,6},{6,7},{8,9},{9,10},{10,11},{12,13},{... | collective-permute-start | bytes 98312 | tf_op jit(solution)/shard_map/ppermute | solution.py:23
  189.7 8.4 %collective-permute-start.18 = (f32[1,4,2,32,64]{4,3,2,1,0:T(8,128)S(1)}, f32[1,4,2,32,64]{4,3,2,1,0:T(8,128)S(1)}, u32[]{:S(2)}, u32[]{:S(2)}) collective-permute-start(f32[1,4,2,32,64]{4,3,2,1,0:T(8,128)S(1)} %broadcast_add_fusion.1), channel_id=1, source_target_pairs={{0,4},{4,8},{8,12},{12,16},{16,20},{20,24},{24,28},{28,32},{32,36}... | collective-permute-start | bytes 196616 | tf_op jit(solution)/shard_map/ppermute | solution.py:34
  198.3 7.8 %collective-permute-start.22 = (f32[1,4,1,32,64]{4,3,2,1,0:T(8,128)S(1)}, f32[1,4,1,32,64]{4,3,2,1,0:T(8,128)S(1)}, u32[]{:S(2)}, u32[]{:S(2)}) collective-permute-start(f32[1,4,1,32,64]{4,3,2,1,0:T(8,128)S(1)} %get-tuple-element.101), channel_id=1, source_target_pairs={{1,0},{2,1},{3,2},{5,4},{6,5},{7,6},{9,8},{10,9},{11,10},{13,12},{... | collective-permute-start | bytes 98312 | tf_op jit(solution)/shard_map/ppermute | solution.py:26
  199.6 6.5 %collective-permute-start.23 = (f32[1,4,1,32,64]{4,3,2,1,0:T(8,128)S(1)}, f32[1,4,1,32,64]{4,3,2,1,0:T(8,128)S(1)}, u32[]{:S(2)}, u32[]{:S(2)}) collective-permute-start(f32[1,4,1,32,64]{4,3,2,1,0:T(8,128)S(1)} %get-tuple-element.102), channel_id=1, source_target_pairs={{0,1},{1,2},{2,3},{4,5},{5,6},{6,7},{8,9},{9,10},{10,11},{12,13},{... | collective-permute-start | bytes 98312 | tf_op jit(solution)/shard_map/ppermute | solution.py:23
  204.1 8.4 %collective-permute-start.21 = (f32[1,4,2,32,64]{4,3,2,1,0:T(8,128)S(1)}, f32[1,4,2,32,64]{4,3,2,1,0:T(8,128)S(1)}, u32[]{:S(2)}, u32[]{:S(2)}) collective-permute-start(f32[1,4,2,32,64]{4,3,2,1,0:T(8,128)S(1)} %fusion.228), channel_id=1, source_target_pairs={{0,4},{4,8},{8,12},{12,16},{16,20},{20,24},{24,28},{28,32},{32,36}... | collective-permute-start | bytes 196616 | tf_op jit(solution)/shard_map/ppermute | solution.py:34
  213.1 12.6 %collective-permute-start.24 = (f32[1,4,4,64,128]{4,3,2,1,0:T(8,128)S(1)}, f32[1,4,4,64,128]{4,3,2,1,0:T(8,128)S(1)}, u32[]{:S(2)}, u32[]{:S(2)}) collective-permute-start(f32[1,4,4,64,128]{4,3,2,1,0:T(8,128)S(1)} %add.556), channel_id=1, source_target_pairs={{0,4},{4,8},{8,12},{12,16},{16,20},{20,24},{24,28},{28,32},{32,36}... | collective-permute-start | bytes 1572872 | tf_op jit(solution)/shard_map/ppermute | solution.py:34
  215.0 6.9 %collective-permute-start.25 = (f32[1,4,1,64,128]{4,3,2,1,0:T(8,128)S(1)}, f32[1,4,1,64,128]{4,3,2,1,0:T(8,128)S(1)}, u32[]{:S(2)}, u32[]{:S(2)}) collective-permute-start(f32[1,4,1,64,128]{4,3,2,1,0:T(8,128)S(1)} %get-tuple-element.53), channel_id=1, source_target_pairs={{1,0},{2,1},{3,2},{5,4},{6,5},{7,6},{9,8},{10,9},{11,10},{13,12},{... | collective-permute-start | bytes 393224 | tf_op jit(solution)/shard_map/ppermute | solution.py:26
  216.3 7.1 %collective-permute-start.26 = (f32[1,4,1,64,128]{4,3,2,1,0:T(8,128)S(1)}, f32[1,4,1,64,128]{4,3,2,1,0:T(8,128)S(1)}, u32[]{:S(2)}, u32[]{:S(2)}) collective-permute-start(f32[1,4,1,64,128]{4,3,2,1,0:T(8,128)S(1)} %get-tuple-element.54), channel_id=1, source_target_pairs={{0,1},{1,2},{2,3},{4,5},{5,6},{6,7},{8,9},{9,10},{10,11},{12,13},{... | collective-permute-start | bytes 393224 | tf_op jit(solution)/shard_map/ppermute | solution.py:23
  226.2 12.6 %collective-permute-start.27 = (f32[1,4,4,64,128]{4,3,2,1,0:T(8,128)S(1)}, f32[1,4,4,64,128]{4,3,2,1,0:T(8,128)S(1)}, u32[]{:S(2)}, u32[]{:S(2)}) collective-permute-start(f32[1,4,4,64,128]{4,3,2,1,0:T(8,128)S(1)} %fusion.95), channel_id=1, source_target_pairs={{0,4},{4,8},{8,12},{12,16},{16,20},{20,24},{24,28},{28,32},{32,36}... | collective-permute-start | bytes 1572872 | tf_op jit(solution)/shard_map/ppermute | solution.py:34
  228.4 6.9 %collective-permute-start.28 = (f32[1,4,1,64,128]{4,3,2,1,0:T(8,128)S(1)}, f32[1,4,1,64,128]{4,3,2,1,0:T(8,128)S(1)}, u32[]{:S(2)}, u32[]{:S(2)}) collective-permute-start(f32[1,4,1,64,128]{4,3,2,1,0:T(8,128)S(1)} %get-tuple-element.49), channel_id=1, source_target_pairs={{1,0},{2,1},{3,2},{5,4},{6,5},{7,6},{9,8},{10,9},{11,10},{13,12},{... | collective-permute-start | bytes 393224 | tf_op jit(solution)/shard_map/ppermute | solution.py:26
  229.7 7.1 %collective-permute-start.29 = (f32[1,4,1,64,128]{4,3,2,1,0:T(8,128)S(1)}, f32[1,4,1,64,128]{4,3,2,1,0:T(8,128)S(1)}, u32[]{:S(2)}, u32[]{:S(2)}) collective-permute-start(f32[1,4,1,64,128]{4,3,2,1,0:T(8,128)S(1)} %get-tuple-element.50), channel_id=1, source_target_pairs={{0,1},{1,2},{2,3},{4,5},{5,6},{6,7},{8,9},{9,10},{10,11},{12,13},{... | collective-permute-start | bytes 393224 | tf_op jit(solution)/shard_map/ppermute | solution.py:23
  239.4 12.6 %collective-permute-start.30 = (f32[1,4,4,64,128]{4,3,2,1,0:T(8,128)S(1)}, f32[1,4,4,64,128]{4,3,2,1,0:T(8,128)S(1)}, u32[]{:S(2)}, u32[]{:S(2)}) collective-permute-start(f32[1,4,4,64,128]{4,3,2,1,0:T(8,128)S(1)} %fusion.81), channel_id=1, source_target_pairs={{0,4},{4,8},{8,12},{12,16},{16,20},{20,24},{24,28},{28,32},{32,36}... | collective-permute-start | bytes 1572872 | tf_op jit(solution)/shard_map/ppermute | solution.py:34
  241.3 6.9 %collective-permute-start.31 = (f32[1,4,1,64,128]{4,3,2,1,0:T(8,128)S(1)}, f32[1,4,1,64,128]{4,3,2,1,0:T(8,128)S(1)}, u32[]{:S(2)}, u32[]{:S(2)}) collective-permute-start(f32[1,4,1,64,128]{4,3,2,1,0:T(8,128)S(1)} %get-tuple-element.45), channel_id=1, source_target_pairs={{1,0},{2,1},{3,2},{5,4},{6,5},{7,6},{9,8},{10,9},{11,10},{13,12},{... | collective-permute-start | bytes 393224 | tf_op jit(solution)/shard_map/ppermute | solution.py:26
  242.6 7.1 %collective-permute-start.32 = (f32[1,4,1,64,128]{4,3,2,1,0:T(8,128)S(1)}, f32[1,4,1,64,128]{4,3,2,1,0:T(8,128)S(1)}, u32[]{:S(2)}, u32[]{:S(2)}) collective-permute-start(f32[1,4,1,64,128]{4,3,2,1,0:T(8,128)S(1)} %get-tuple-element.46), channel_id=1, source_target_pairs={{0,1},{1,2},{2,3},{4,5},{5,6},{6,7},{8,9},{9,10},{10,11},{12,13},{... | collective-permute-start | bytes 393224 | tf_op jit(solution)/shard_map/ppermute | solution.py:23
  252.5 12.6 %collective-permute-start.33 = (f32[1,4,4,64,128]{4,3,2,1,0:T(8,128)S(1)}, f32[1,4,4,64,128]{4,3,2,1,0:T(8,128)S(1)}, u32[]{:S(2)}, u32[]{:S(2)}) collective-permute-start(f32[1,4,4,64,128]{4,3,2,1,0:T(8,128)S(1)} %fusion.67), channel_id=1, source_target_pairs={{0,4},{4,8},{8,12},{12,16},{16,20},{20,24},{24,28},{28,32},{32,36}... | collective-permute-start | bytes 1572872 | tf_op jit(solution)/shard_map/ppermute | solution.py:34
  254.5 6.9 %collective-permute-start.34 = (f32[1,4,1,64,128]{4,3,2,1,0:T(8,128)S(1)}, f32[1,4,1,64,128]{4,3,2,1,0:T(8,128)S(1)}, u32[]{:S(2)}, u32[]{:S(2)}) collective-permute-start(f32[1,4,1,64,128]{4,3,2,1,0:T(8,128)S(1)} %get-tuple-element.41), channel_id=1, source_target_pairs={{1,0},{2,1},{3,2},{5,4},{6,5},{7,6},{9,8},{10,9},{11,10},{13,12},{... | collective-permute-start | bytes 393224 | tf_op jit(solution)/shard_map/ppermute | solution.py:26
  255.8 7.1 %collective-permute-start.35 = (f32[1,4,1,64,128]{4,3,2,1,0:T(8,128)S(1)}, f32[1,4,1,64,128]{4,3,2,1,0:T(8,128)S(1)}, u32[]{:S(2)}, u32[]{:S(2)}) collective-permute-start(f32[1,4,1,64,128]{4,3,2,1,0:T(8,128)S(1)} %get-tuple-element.42), channel_id=1, source_target_pairs={{0,1},{1,2},{2,3},{4,5},{5,6},{6,7},{8,9},{9,10},{10,11},{12,13},{... | collective-permute-start | bytes 393224 | tf_op jit(solution)/shard_map/ppermute | solution.py:23
  265.7 12.6 %collective-permute-start.36 = (f32[1,4,4,64,128]{4,3,2,1,0:T(8,128)S(1)}, f32[1,4,4,64,128]{4,3,2,1,0:T(8,128)S(1)}, u32[]{:S(2)}, u32[]{:S(2)}) collective-permute-start(f32[1,4,4,64,128]{4,3,2,1,0:T(8,128)S(1)} %fusion.53), channel_id=1, source_target_pairs={{0,4},{4,8},{8,12},{12,16},{16,20},{20,24},{24,28},{28,32},{32,36}... | collective-permute-start | bytes 1572872 | tf_op jit(solution)/shard_map/ppermute | solution.py:34
  267.6 6.9 %collective-permute-start.37 = (f32[1,4,1,64,128]{4,3,2,1,0:T(8,128)S(1)}, f32[1,4,1,64,128]{4,3,2,1,0:T(8,128)S(1)}, u32[]{:S(2)}, u32[]{:S(2)}) collective-permute-start(f32[1,4,1,64,128]{4,3,2,1,0:T(8,128)S(1)} %get-tuple-element.37), channel_id=1, source_target_pairs={{1,0},{2,1},{3,2},{5,4},{6,5},{7,6},{9,8},{10,9},{11,10},{13,12},{... | collective-permute-start | bytes 393224 | tf_op jit(solution)/shard_map/ppermute | solution.py:26
  268.9 7.1 %collective-permute-start.38 = (f32[1,4,1,64,128]{4,3,2,1,0:T(8,128)S(1)}, f32[1,4,1,64,128]{4,3,2,1,0:T(8,128)S(1)}, u32[]{:S(2)}, u32[]{:S(2)}) collective-permute-start(f32[1,4,1,64,128]{4,3,2,1,0:T(8,128)S(1)} %get-tuple-element.38), channel_id=1, source_target_pairs={{0,1},{1,2},{2,3},{4,5},{5,6},{6,7},{8,9},{9,10},{10,11},{12,13},{... | collective-permute-start | bytes 393224 | tf_op jit(solution)/shard_map/ppermute | solution.py:23
  279.7 7.8 %collective-permute-start.40 = (f32[1,4,1,32,64]{4,3,2,1,0:T(8,128)S(1)}, f32[1,4,1,32,64]{4,3,2,1,0:T(8,128)S(1)}, u32[]{:S(2)}, u32[]{:S(2)}) collective-permute-start(f32[1,4,1,32,64]{4,3,2,1,0:T(8,128)S(1)} %get-tuple-element.97), channel_id=1, source_target_pairs={{1,0},{2,1},{3,2},{5,4},{6,5},{7,6},{9,8},{10,9},{11,10},{13,12},{... | collective-permute-start | bytes 98312 | tf_op jit(solution)/shard_map/ppermute | solution.py:26
  281.0 6.5 %collective-permute-start.41 = (f32[1,4,1,32,64]{4,3,2,1,0:T(8,128)S(1)}, f32[1,4,1,32,64]{4,3,2,1,0:T(8,128)S(1)}, u32[]{:S(2)}, u32[]{:S(2)}) collective-permute-start(f32[1,4,1,32,64]{4,3,2,1,0:T(8,128)S(1)} %get-tuple-element.98), channel_id=1, source_target_pairs={{0,1},{1,2},{2,3},{4,5},{5,6},{6,7},{8,9},{9,10},{10,11},{12,13},{... | collective-permute-start | bytes 98312 | tf_op jit(solution)/shard_map/ppermute | solution.py:23
  285.5 8.4 %collective-permute-start.39 = (f32[1,4,2,32,64]{4,3,2,1,0:T(8,128)S(1)}, f32[1,4,2,32,64]{4,3,2,1,0:T(8,128)S(1)}, u32[]{:S(2)}, u32[]{:S(2)}) collective-permute-start(f32[1,4,2,32,64]{4,3,2,1,0:T(8,128)S(1)} %multiply_divide_fusion), channel_id=1, source_target_pairs={{0,4},{4,8},{8,12},{12,16},{16,20},{20,24},{24,28},{28,32},{32,36}... | collective-permute-start | bytes 196616 | tf_op jit(solution)/shard_map/ppermute | solution.py:34
  294.1 7.8 %collective-permute-start.43 = (f32[1,4,1,32,64]{4,3,2,1,0:T(8,128)S(1)}, f32[1,4,1,32,64]{4,3,2,1,0:T(8,128)S(1)}, u32[]{:S(2)}, u32[]{:S(2)}) collective-permute-start(f32[1,4,1,32,64]{4,3,2,1,0:T(8,128)S(1)} %get-tuple-element.93), channel_id=1, source_target_pairs={{1,0},{2,1},{3,2},{5,4},{6,5},{7,6},{9,8},{10,9},{11,10},{13,12},{... | collective-permute-start | bytes 98312 | tf_op jit(solution)/shard_map/ppermute | solution.py:26
  295.4 6.5 %collective-permute-start.44 = (f32[1,4,1,32,64]{4,3,2,1,0:T(8,128)S(1)}, f32[1,4,1,32,64]{4,3,2,1,0:T(8,128)S(1)}, u32[]{:S(2)}, u32[]{:S(2)}) collective-permute-start(f32[1,4,1,32,64]{4,3,2,1,0:T(8,128)S(1)} %get-tuple-element.94), channel_id=1, source_target_pairs={{0,1},{1,2},{2,3},{4,5},{5,6},{6,7},{8,9},{9,10},{10,11},{12,13},{... | collective-permute-start | bytes 98312 | tf_op jit(solution)/shard_map/ppermute | solution.py:23
  299.9 8.4 %collective-permute-start.42 = (f32[1,4,2,32,64]{4,3,2,1,0:T(8,128)S(1)}, f32[1,4,2,32,64]{4,3,2,1,0:T(8,128)S(1)}, u32[]{:S(2)}, u32[]{:S(2)}) collective-permute-start(f32[1,4,2,32,64]{4,3,2,1,0:T(8,128)S(1)} %fusion.198), channel_id=1, source_target_pairs={{0,4},{4,8},{8,12},{12,16},{16,20},{20,24},{24,28},{28,32},{32,36}... | collective-permute-start | bytes 196616 | tf_op jit(solution)/shard_map/ppermute | solution.py:34
  396.1 7.8 %collective-permute-start.46 = (f32[1,4,1,32,64]{4,3,2,1,0:T(8,128)S(1)}, f32[1,4,1,32,64]{4,3,2,1,0:T(8,128)S(1)}, u32[]{:S(2)}, u32[]{:S(2)}) collective-permute-start(f32[1,4,1,32,64]{4,3,2,1,0:T(8,128)S(1)} %get-tuple-element.89), channel_id=1, source_target_pairs={{1,0},{2,1},{3,2},{5,4},{6,5},{7,6},{9,8},{10,9},{11,10},{13,12},{... | collective-permute-start | bytes 98312 | tf_op jit(solution)/shard_map/ppermute | solution.py:26
  397.4 6.5 %collective-permute-start.47 = (f32[1,4,1,32,64]{4,3,2,1,0:T(8,128)S(1)}, f32[1,4,1,32,64]{4,3,2,1,0:T(8,128)S(1)}, u32[]{:S(2)}, u32[]{:S(2)}) collective-permute-start(f32[1,4,1,32,64]{4,3,2,1,0:T(8,128)S(1)} %get-tuple-element.90), channel_id=1, source_target_pairs={{0,1},{1,2},{2,3},{4,5},{5,6},{6,7},{8,9},{9,10},{10,11},{12,13},{... | collective-permute-start | bytes 98312 | tf_op jit(solution)/shard_map/ppermute | solution.py:23
  402.0 8.4 %collective-permute-start.45 = (f32[1,4,2,32,64]{4,3,2,1,0:T(8,128)S(1)}, f32[1,4,2,32,64]{4,3,2,1,0:T(8,128)S(1)}, u32[]{:S(2)}, u32[]{:S(2)}) collective-permute-start(f32[1,4,2,32,64]{4,3,2,1,0:T(8,128)S(1)} %broadcast_add_fusion), channel_id=1, source_target_pairs={{0,4},{4,8},{8,12},{12,16},{16,20},{20,24},{24,28},{28,32},{32,36}... | collective-permute-start | bytes 196616 | tf_op jit(solution)/shard_map/ppermute | solution.py:34
  410.5 7.8 %collective-permute-start.49 = (f32[1,4,1,32,64]{4,3,2,1,0:T(8,128)S(1)}, f32[1,4,1,32,64]{4,3,2,1,0:T(8,128)S(1)}, u32[]{:S(2)}, u32[]{:S(2)}) collective-permute-start(f32[1,4,1,32,64]{4,3,2,1,0:T(8,128)S(1)} %get-tuple-element.85), channel_id=1, source_target_pairs={{1,0},{2,1},{3,2},{5,4},{6,5},{7,6},{9,8},{10,9},{11,10},{13,12},{... | collective-permute-start | bytes 98312 | tf_op jit(solution)/shard_map/ppermute | solution.py:26
  411.8 6.5 %collective-permute-start.50 = (f32[1,4,1,32,64]{4,3,2,1,0:T(8,128)S(1)}, f32[1,4,1,32,64]{4,3,2,1,0:T(8,128)S(1)}, u32[]{:S(2)}, u32[]{:S(2)}) collective-permute-start(f32[1,4,1,32,64]{4,3,2,1,0:T(8,128)S(1)} %get-tuple-element.86), channel_id=1, source_target_pairs={{0,1},{1,2},{2,3},{4,5},{5,6},{6,7},{8,9},{9,10},{10,11},{12,13},{... | collective-permute-start | bytes 98312 | tf_op jit(solution)/shard_map/ppermute | solution.py:23
  416.4 8.4 %collective-permute-start.48 = (f32[1,4,2,32,64]{4,3,2,1,0:T(8,128)S(1)}, f32[1,4,2,32,64]{4,3,2,1,0:T(8,128)S(1)}, u32[]{:S(2)}, u32[]{:S(2)}) collective-permute-start(f32[1,4,2,32,64]{4,3,2,1,0:T(8,128)S(1)} %fusion.171), channel_id=1, source_target_pairs={{0,4},{4,8},{8,12},{12,16},{16,20},{20,24},{24,28},{28,32},{32,36}... | collective-permute-start | bytes 196616 | tf_op jit(solution)/shard_map/ppermute | solution.py:34
  425.3 12.6 %collective-permute-start.51 = (f32[1,4,4,64,128]{4,3,2,1,0:T(8,128)S(1)}, f32[1,4,4,64,128]{4,3,2,1,0:T(8,128)S(1)}, u32[]{:S(2)}, u32[]{:S(2)}) collective-permute-start(f32[1,4,4,64,128]{4,3,2,1,0:T(8,128)S(1)} %add.605), channel_id=1, source_target_pairs={{0,4},{4,8},{8,12},{12,16},{16,20},{20,24},{24,28},{28,32},{32,36}... | collective-permute-start | bytes 1572872 | tf_op jit(solution)/shard_map/ppermute | solution.py:34
  427.3 6.9 %collective-permute-start.52 = (f32[1,4,1,64,128]{4,3,2,1,0:T(8,128)S(1)}, f32[1,4,1,64,128]{4,3,2,1,0:T(8,128)S(1)}, u32[]{:S(2)}, u32[]{:S(2)}) collective-permute-start(f32[1,4,1,64,128]{4,3,2,1,0:T(8,128)S(1)} %get-tuple-element.33), channel_id=1, source_target_pairs={{1,0},{2,1},{3,2},{5,4},{6,5},{7,6},{9,8},{10,9},{11,10},{13,12},{... | collective-permute-start | bytes 393224 | tf_op jit(solution)/shard_map/ppermute | solution.py:26
  428.6 7.1 %collective-permute-start.53 = (f32[1,4,1,64,128]{4,3,2,1,0:T(8,128)S(1)}, f32[1,4,1,64,128]{4,3,2,1,0:T(8,128)S(1)}, u32[]{:S(2)}, u32[]{:S(2)}) collective-permute-start(f32[1,4,1,64,128]{4,3,2,1,0:T(8,128)S(1)} %get-tuple-element.34), channel_id=1, source_target_pairs={{0,1},{1,2},{2,3},{4,5},{5,6},{6,7},{8,9},{9,10},{10,11},{12,13},{... | collective-permute-start | bytes 393224 | tf_op jit(solution)/shard_map/ppermute | solution.py:23
  438.5 12.6 %collective-permute-start.54 = (f32[1,4,4,64,128]{4,3,2,1,0:T(8,128)S(1)}, f32[1,4,4,64,128]{4,3,2,1,0:T(8,128)S(1)}, u32[]{:S(2)}, u32[]{:S(2)}) collective-permute-start(f32[1,4,4,64,128]{4,3,2,1,0:T(8,128)S(1)} %fusion.27), channel_id=1, source_target_pairs={{0,4},{4,8},{8,12},{12,16},{16,20},{20,24},{24,28},{28,32},{32,36}... | collective-permute-start | bytes 1572872 | tf_op jit(solution)/shard_map/ppermute | solution.py:34
  440.5 6.9 %collective-permute-start.55 = (f32[1,4,1,64,128]{4,3,2,1,0:T(8,128)S(1)}, f32[1,4,1,64,128]{4,3,2,1,0:T(8,128)S(1)}, u32[]{:S(2)}, u32[]{:S(2)}) collective-permute-start(f32[1,4,1,64,128]{4,3,2,1,0:T(8,128)S(1)} %get-tuple-element.29), channel_id=1, source_target_pairs={{1,0},{2,1},{3,2},{5,4},{6,5},{7,6},{9,8},{10,9},{11,10},{13,12},{... | collective-permute-start | bytes 393224 | tf_op jit(solution)/shard_map/ppermute | solution.py:26
  441.8 7.1 %collective-permute-start.56 = (f32[1,4,1,64,128]{4,3,2,1,0:T(8,128)S(1)}, f32[1,4,1,64,128]{4,3,2,1,0:T(8,128)S(1)}, u32[]{:S(2)}, u32[]{:S(2)}) collective-permute-start(f32[1,4,1,64,128]{4,3,2,1,0:T(8,128)S(1)} %get-tuple-element.30), channel_id=1, source_target_pairs={{0,1},{1,2},{2,3},{4,5},{5,6},{6,7},{8,9},{9,10},{10,11},{12,13},{... | collective-permute-start | bytes 393224 | tf_op jit(solution)/shard_map/ppermute | solution.py:23
  (13 other events, 180.7 us)
Sparse Core Ops, SparseCore 0:
  105.4 39.3 all-gather.6
  322.1 39.2 all-gather.8

commit v5 on v4

--- a/solution.py
+++ b/solution.py
@@ -103,26 +103,28 @@
     return jnp.repeat(spread, 2, axis=-3)
 
 
-def coarse_kernel(src_ref, met_ref, out_ref, *, spacing, depth_x, height_y, width_z):
+def coarse_kernel(src_ref, met_ref, out_ref, *, spacing, components, height_y, width_z):
     steps, rows, lanes = src_ref.shape
+    depth_x = rows // components
     inverse_square = 1.0 / (spacing * spacing)
     half_inverse = 0.5 / spacing
     row = lax.broadcasted_iota(jnp.int32, (rows, lanes), 0)
     lane = lax.broadcasted_iota(jnp.int32, (rows, lanes), 1)
-    plane = row % depth_x
-    part = row // depth_x
+    plane = row // components
+    part = row % components
     across_z = lane % width_z
     across_y = lane // width_z
-    quarter = rows // 4
     zero = jnp.zeros((rows, lanes), jnp.float32)
 
+    def rolled(v, shift, axis):
+        return pltpu.roll(v, shift % v.shape[axis], axis)
+
     def shifted(v, shift, axis, edge):
-        size = v.shape[axis]
-        return jnp.where(edge, zero, pltpu.roll(v, shift % size, axis))
+        return jnp.where(edge, zero, rolled(v, shift, axis))
 
     def apply(v, two_g):
-        ahead_x = shifted(v, -1, 0, plane == depth_x - 1)
-        behind_x = shifted(v, 1, 0, plane == 0)
+        ahead_x = shifted(v, -components, 0, plane == depth_x - 1)
+        behind_x = shifted(v, components, 0, plane == 0)
         ahead_y = shifted(v, -width_z, 1, across_y == height_y - 1)
         behind_y = shifted(v, width_z, 1, across_y == 0)
         ahead_z = shifted(v, -1, 1, across_z == width_z - 1)
@@ -131,10 +133,10 @@
         diff_x = ahead_x - behind_x
         diff_y = ahead_y - behind_y
         diff_z = ahead_z - behind_z
-        grad_x = pltpu.roll(diff_x, quarter, 0)
-        grad_y = pltpu.roll(diff_y, 2 * quarter, 0)
-        grad_z = pltpu.roll(diff_z, 3 * quarter, 0)
-        divergence = pltpu.roll(diff_x, 3 * quarter, 0) + pltpu.roll(diff_y, 2 * quarter, 0) + pltpu.roll(diff_z, quarter, 0)
+        grad_x = rolled(diff_x, -3, 0)
+        grad_y = rolled(diff_y, -2, 0)
+        grad_z = rolled(diff_z, -1, 0)
+        divergence = rolled(diff_x, 3, 0) + rolled(diff_y, 2, 0) + rolled(diff_z, 1, 0)
         coupling = jnp.where(part == 0, grad_x, jnp.where(part == 1, grad_y, jnp.where(part == 2, grad_z, divergence))) * half_inverse
         return two_g * v + laplace + coupling
 
@@ -152,18 +154,14 @@
     lax.fori_loop(0, steps, advance, zero)
 
 
-def coarse_solve(source, metric, spacing):
-    steps, components, depth_x, height_y, width_z = source.shape
-    rows = components * depth_x
-    lanes = height_y * width_z
-    flat_source = source.reshape(steps, rows, lanes)
-    flat_metric = jnp.tile(metric.reshape(steps, depth_x, lanes), (1, components, 1))
-    kernel = functools.partial(coarse_kernel, spacing=spacing, depth_x=depth_x, height_y=height_y, width_z=width_z)
-    solved = pl.pallas_call(
+def coarse_solve(flat_source, flat_metric, spacing, components, height_y, width_z):
+    kernel = functools.partial(
+        coarse_kernel, spacing=spacing, components=components, height_y=height_y, width_z=width_z
+    )
+    return pl.pallas_call(
         kernel,
         out_shape=jax.ShapeDtypeStruct(flat_source.shape, jnp.float32),
-    )(flat_source, flat_metric)
-    return solved.reshape(source.shape)
+    )(flat_source, jnp.repeat(flat_metric, components, axis=1))
 
 
 def apply_local(values, metric, spacing, pinned):
@@ -175,17 +173,16 @@
 
 def assemble(flat_source, flat_metric, time_devs, plane_devs, local_dims):
     local_steps, components, planes, height_y, width_z = local_dims
+    lanes = height_y * width_z
     whole_source = flat_source.reshape(
-        time_devs, plane_devs, local_steps, components, planes, height_y, width_z
-    )
-    whole_source = whole_source.transpose(0, 2, 3, 1, 4, 5, 6).reshape(
-        time_devs * local_steps, components, plane_devs * planes, height_y, width_z
-    )
-    whole_metric = flat_metric.reshape(
-        time_devs, plane_devs, local_steps, planes, height_y, width_z
-    )
-    whole_metric = whole_metric.transpose(0, 2, 1, 3, 4, 5).reshape(
-        time_devs * local_steps, plane_devs * planes, height_y, width_z
+        time_devs, plane_devs, local_steps, components, planes, lanes
+    )
+    whole_source = whole_source.transpose(0, 2, 1, 4, 3, 5).reshape(
+        time_devs * local_steps, plane_devs * planes * components, lanes
+    )
+    whole_metric = flat_metric.reshape(time_devs, plane_devs, local_steps, planes, lanes)
+    whole_metric = whole_metric.transpose(0, 2, 1, 3, 4).reshape(
+        time_devs * local_steps, plane_devs * planes, lanes
     )
     return (whole_source, whole_metric)
 
@@ -216,12 +213,14 @@
     whole_source, whole_metric = assemble(
         flat_source, flat_metric, time_devs, plane_devs, local_dims
     )
-    solved = coarse_solve(whole_source, whole_metric, 4.0)
-    return lax.dynamic_slice(
+    solved = coarse_solve(whole_source, whole_metric, 4.0, components, height_y, width_z)
+    mine = lax.dynamic_slice(
         solved,
-        (time_at * local_steps, 0, plane_at * planes, 0, 0),
-        (local_steps, components, planes, height_y, width_z),
-    )
+        (time_at * local_steps, plane_at * planes * components, 0),
+        (local_steps, planes * components, height_y * width_z),
+    )
+    mine = mine.reshape(local_steps, planes, components, height_y, width_z)
+    return mine.transpose(0, 2, 1, 3, 4)
 
 
 def per_device(right_side, metric, wall_mask):

time: 461 us -> 432 us (0.937)
  local copies, waits for them, and re-layouts: 43.1 us -> 14.6 us
    reshape x4 -> x1, local copies, waits for them, and re-layouts: 13.2 us -> 1.34 us  [coarse_solve(): jnp.repeat(flat_metric, components, axis=1)]
    transpose x2 -> x0, local copies, waits for them, and re-layouts: 9.71 us -> none  [assemble(): whole_source.transpose(0, 2, 3, 1, 4, 5, 6)]
    another operation x9, local copies, waits for them, and re-layouts: 12.1 us -> 5.58 us  [the longest x2 5.28 us: assemble(): whole_source.transpose(0, 2, 1, 4, 3, 5)]
where the time goes in v5:
time: 432 us; the launch traced here: 430 us
  waiting for transfers between devices  179 us (41%)
  starting transfers between devices  148 us (34%)
  Pallas kernels  33.1 us (8%)
  blocking collectives  25.6 us (6%)
  between operations  14.7 us (3%)
  local copies, waits for them, and re-layouts  14.6 us (3%)
  other arithmetic  12.1 us (3%)
    ppermute x19, starting transfers between devices, with_halo(): lax.ppermute(lax.slice_in_dim(block, block.shape[dim] - width, None, axis...  87.3 us
    all_gather x2, waiting for transfers between devices, gather_all(): return lax.all_gather(within, 'tm', axis=0, tiled=True)  78.9 us
    ppermute x19, waiting for transfers between devices, from_behind(): return lax.ppermute(array, axis, pairs)  78.7 us
    ppermute x19, starting transfers between devices, from_behind(): return lax.ppermute(array, axis, pairs)  36.5 us
    pallas_call x2, Pallas kernels, coarse_solve(): pl.pallas_call(kernel, out_shape=jax.ShapeDtypeStruct(flat_source.shape,...  33.1 us
    all_gather x2, blocking collectives, gather_all(): within = lax.all_gather(flat, 'space', axis=0, tiled=True)  25.6 us
    ppermute x19, starting transfers between devices, with_halo(): lax.ppermute(lax.slice_in_dim(block, 0, width, axis=dim), axis, backward)  24.5 us
    ppermute x19, waiting for transfers between devices, with_halo(): lax.ppermute(lax.slice_in_dim(block, block.shape[dim] - width, None, axis...  12.1 us
  transfers between devices with their start and end apart: 59, of which 39 were waited for; matrix products, arithmetic and copies ran while one was open for 2% of the time, Pallas kernels for 0%

profile of v5, /device:TPU:2, one launch (start us, length us, event | category | flops | bytes accessed | tf_op | source)
XLA Modules:
  0.0 429.6 jit_solution(4838588115160191894)
XLA Ops:
  6.5 4.0 collective-permute-start.11
  11.8 4.6 %collective-permute-start.2 = (f32[1,4,1,64,128]{4,3,2,1,0:T(8,128)S(1)}, f32[1,4,1,64,128]{4,3,2,1,0:T(8,128)S(1)}, u32[]{:S(2)}, u32[]{:S(2)}) collective-permute-start(f32[1,4,1,64,128]{4,3,2,1,0:T(8,128)S(1)} %broadcast.473), channel_id=1, source_target_pairs={{0,1},{1,2},{2,3},{4,5},{5,6},{6,7},{8,9},{9,10},{10,11},{12,13},{... | collective-permute-start | bytes 393224 | tf_op jit(solution)/shard_map/ppermute | solution.py:23
  17.7 1.9 collective-permute-start
  23.5 6.9 %collective-permute-done = f32[1,4,4,64,128]{4,3,2,1,0:T(8,128)S(1)} collective-permute-done((f32[1,4,4,64,128]{4,3,2,1,0:T(8,128)S(1)}, f32[1,4,4,64,128]{4,3,2,1,0:T(8,128)S(1)}, u32[]{:S(2)}, u32[]{:S(2)}) %collective-permute-start) | collective-permute-done | bytes 524320 | tf_op jit(solution)/shard_map/ppermute | solution.py:34
  30.8 1.9 collective-permute-start.3
  34.1 5.2 %collective-permute-start.5 = (f32[1,4,1,64,128]{4,3,2,1,0:T(8,128)S(1)}, f32[1,4,1,64,128]{4,3,2,1,0:T(8,128)S(1)}, u32[]{:S(2)}, u32[]{:S(2)}) collective-permute-start(f32[1,4,1,64,128]{4,3,2,1,0:T(8,128)S(1)} %get-tuple-element.62), channel_id=1, source_target_pairs={{0,1},{1,2},{2,3},{4,5},{5,6},{6,7},{8,9},{9,10},{10,11},{12,13},{... | collective-permute-start | bytes 393224 | tf_op jit(solution)/shard_map/ppermute | solution.py:23
  44.0 1.9 collective-permute-start.6
  47.3 5.2 %collective-permute-start.8 = (f32[1,4,1,64,128]{4,3,2,1,0:T(8,128)S(1)}, f32[1,4,1,64,128]{4,3,2,1,0:T(8,128)S(1)}, u32[]{:S(2)}, u32[]{:S(2)}) collective-permute-start(f32[1,4,1,64,128]{4,3,2,1,0:T(8,128)S(1)} %get-tuple-element.58), channel_id=1, source_target_pairs={{0,1},{1,2},{2,3},{4,5},{5,6},{6,7},{8,9},{9,10},{10,11},{12,13},{... | collective-permute-start | bytes 393224 | tf_op jit(solution)/shard_map/ppermute | solution.py:23
  52.5 1.9 collective-permute-start.9
  57.4 3.5 collective-permute-done.9
  62.4 4.5 %collective-permute-start.14 = (f32[1,4,1,32,64]{4,3,2,1,0:T(8,128)S(1)}, f32[1,4,1,32,64]{4,3,2,1,0:T(8,128)S(1)}, u32[]{:S(2)}, u32[]{:S(2)}) collective-permute-start(f32[1,4,1,32,64]{4,3,2,1,0:T(8,128)S(1)} %get-tuple-element.114), channel_id=1, source_target_pairs={{0,1},{1,2},{2,3},{4,5},{5,6},{6,7},{8,9},{9,10},{10,11},{12,13},{... | collective-permute-start | bytes 98312 | tf_op jit(solution)/shard_map/ppermute | solution.py:23
  67.0 1.9 collective-permute-start.12
  69.1 6.3 %collective-permute-done.12 = f32[1,4,2,32,64]{4,3,2,1,0:T(8,128)S(1)} collective-permute-done((f32[1,4,2,32,64]{4,3,2,1,0:T(8,128)S(1)}, f32[1,4,2,32,64]{4,3,2,1,0:T(8,128)S(1)}, u32[]{:S(2)}, u32[]{:S(2)}) %collective-permute-start.12) | collective-permute-done | bytes 65568 | tf_op jit(solution)/shard_map/ppermute | solution.py:34
  76.9 4.5 %collective-permute-start.17 = (f32[1,4,1,32,64]{4,3,2,1,0:T(8,128)S(1)}, f32[1,4,1,32,64]{4,3,2,1,0:T(8,128)S(1)}, u32[]{:S(2)}, u32[]{:S(2)}) collective-permute-start(f32[1,4,1,32,64]{4,3,2,1,0:T(8,128)S(1)} %get-tuple-element.110), channel_id=1, source_target_pairs={{0,1},{1,2},{2,3},{4,5},{5,6},{6,7},{8,9},{9,10},{10,11},{12,13},{... | collective-permute-start | bytes 98312 | tf_op jit(solution)/shard_map/ppermute | solution.py:23
  81.7 1.9 collective-permute-start.15
  83.7 6.3 %collective-permute-done.15 = f32[1,4,2,32,64]{4,3,2,1,0:T(8,128)S(1)} collective-permute-done((f32[1,4,2,32,64]{4,3,2,1,0:T(8,128)S(1)}, f32[1,4,2,32,64]{4,3,2,1,0:T(8,128)S(1)}, u32[]{:S(2)}, u32[]{:S(2)}) %collective-permute-start.15) | collective-permute-done | bytes 65568 | tf_op jit(solution)/shard_map/ppermute | solution.py:34
  90.7 13.2 %all-gather = f32[4,1,2560]{2,1,0:T(1,128)S(1)} all-gather(f32[1,1,2560]{2,1,0:T(1,128)S(1)} %maximum_bitcast_fusion), channel_id=1, replica_groups=mesh['tm'=32,'space'=4] {'space'}, dimensions={0}, use_global_device_ids=true | all-gather | bytes 51200 | tf_op jit(solution)/shard_map/all_gather | solution.py:191
  104.7 39.5 %all-gather.7.cloned.1.call-done = f32[32,4,2560]{2,1,0:T(4,128)} async-done(((f32[1,4,2560]{2,1,0:T(4,128)}), f32[32,4,2560]{2,1,0:T(4,128)}) %all-gather.7.cloned.1.call-update) | async-done | bytes 1310736 | tf_op jit(solution)/shard_map/all_gather | solution.py:192
  144.1 1.7 reshape.919
  146.9 2.5 reshape_transpose_reshape.10.src_ref
  151.2 16.6 %shard_map.37 = f32[32,16,512]{2,1,0:T(8,128)} custom-call(f32[32,16,512]{2,1,0:T(8,128)} %reshape_transpose_reshape.10.src_ref, f32[32,16,512]{2,1,0:T(8,128)} %reshape.904.met_ref), custom_call_target="tpu_custom_call" | custom-call | tf_op jit(solution)/shard_map/pallas_call | solution.py:161
  170.1 4.5 %collective-permute-start.20 = (f32[1,4,1,32,64]{4,3,2,1,0:T(8,128)S(1)}, f32[1,4,1,32,64]{4,3,2,1,0:T(8,128)S(1)}, u32[]{:S(2)}, u32[]{:S(2)}) collective-permute-start(f32[1,4,1,32,64]{4,3,2,1,0:T(8,128)S(1)} %get-tuple-element.106), channel_id=1, source_target_pairs={{0,1},{1,2},{2,3},{4,5},{5,6},{6,7},{8,9},{9,10},{10,11},{12,13},{... | collective-permute-start | bytes 98312 | tf_op jit(solution)/shard_map/ppermute | solution.py:23
  174.7 1.9 collective-permute-start.18
  176.7 6.3 %collective-permute-done.18 = f32[1,4,2,32,64]{4,3,2,1,0:T(8,128)S(1)} collective-permute-done((f32[1,4,2,32,64]{4,3,2,1,0:T(8,128)S(1)}, f32[1,4,2,32,64]{4,3,2,1,0:T(8,128)S(1)}, u32[]{:S(2)}, u32[]{:S(2)}) %collective-permute-start.18) | collective-permute-done | bytes 65568 | tf_op jit(solution)/shard_map/ppermute | solution.py:34
  184.5 4.5 %collective-permute-start.23 = (f32[1,4,1,32,64]{4,3,2,1,0:T(8,128)S(1)}, f32[1,4,1,32,64]{4,3,2,1,0:T(8,128)S(1)}, u32[]{:S(2)}, u32[]{:S(2)}) collective-permute-start(f32[1,4,1,32,64]{4,3,2,1,0:T(8,128)S(1)} %get-tuple-element.102), channel_id=1, source_target_pairs={{0,1},{1,2},{2,3},{4,5},{5,6},{6,7},{8,9},{9,10},{10,11},{12,13},{... | collective-permute-start | bytes 98312 | tf_op jit(solution)/shard_map/ppermute | solution.py:23
  189.1 1.9 collective-permute-start.21
  191.1 6.3 %collective-permute-done.21 = f32[1,4,2,32,64]{4,3,2,1,0:T(8,128)S(1)} collective-permute-done((f32[1,4,2,32,64]{4,3,2,1,0:T(8,128)S(1)}, f32[1,4,2,32,64]{4,3,2,1,0:T(8,128)S(1)}, u32[]{:S(2)}, u32[]{:S(2)}) %collective-permute-start.21) | collective-permute-done | bytes 65568 | tf_op jit(solution)/shard_map/ppermute | solution.py:34
  198.0 1.9 collective-permute-start.24
  201.3 4.6 %collective-permute-start.26 = (f32[1,4,1,64,128]{4,3,2,1,0:T(8,128)S(1)}, f32[1,4,1,64,128]{4,3,2,1,0:T(8,128)S(1)}, u32[]{:S(2)}, u32[]{:S(2)}) collective-permute-start(f32[1,4,1,64,128]{4,3,2,1,0:T(8,128)S(1)} %get-tuple-element.54), channel_id=1, source_target_pairs={{0,1},{1,2},{2,3},{4,5},{5,6},{6,7},{8,9},{9,10},{10,11},{12,13},{... | collective-permute-start | bytes 393224 | tf_op jit(solution)/shard_map/ppermute | solution.py:23
  208.6 2.1 collective-permute-done.24
  211.2 1.9 collective-permute-start.27
  214.5 4.6 %collective-permute-start.29 = (f32[1,4,1,64,128]{4,3,2,1,0:T(8,128)S(1)}, f32[1,4,1,64,128]{4,3,2,1,0:T(8,128)S(1)}, u32[]{:S(2)}, u32[]{:S(2)}) collective-permute-start(f32[1,4,1,64,128]{4,3,2,1,0:T(8,128)S(1)} %get-tuple-element.50), channel_id=1, source_target_pairs={{0,1},{1,2},{2,3},{4,5},{5,6},{6,7},{8,9},{9,10},{10,11},{12,13},{... | collective-permute-start | bytes 393224 | tf_op jit(solution)/shard_map/ppermute | solution.py:23
  221.7 2.1 collective-permute-done.27
  224.4 1.9 collective-permute-start.30
  227.6 4.6 %collective-permute-start.32 = (f32[1,4,1,64,128]{4,3,2,1,0:T(8,128)S(1)}, f32[1,4,1,64,128]{4,3,2,1,0:T(8,128)S(1)}, u32[]{:S(2)}, u32[]{:S(2)}) collective-permute-start(f32[1,4,1,64,128]{4,3,2,1,0:T(8,128)S(1)} %get-tuple-element.46), channel_id=1, source_target_pairs={{0,1},{1,2},{2,3},{4,5},{5,6},{6,7},{8,9},{9,10},{10,11},{12,13},{... | collective-permute-start | bytes 393224 | tf_op jit(solution)/shard_map/ppermute | solution.py:23
  234.9 2.1 collective-permute-done.30
  237.5 1.9 collective-permute-start.33
  240.8 4.7 %collective-permute-start.35 = (f32[1,4,1,64,128]{4,3,2,1,0:T(8,128)S(1)}, f32[1,4,1,64,128]{4,3,2,1,0:T(8,128)S(1)}, u32[]{:S(2)}, u32[]{:S(2)}) collective-permute-start(f32[1,4,1,64,128]{4,3,2,1,0:T(8,128)S(1)} %get-tuple-element.42), channel_id=1, source_target_pairs={{0,1},{1,2},{2,3},{4,5},{5,6},{6,7},{8,9},{9,10},{10,11},{12,13},{... | collective-permute-start | bytes 393224 | tf_op jit(solution)/shard_map/ppermute | solution.py:23
  248.0 2.1 collective-permute-done.33
  250.7 1.9 collective-permute-start.36
  253.9 4.6 %collective-permute-start.38 = (f32[1,4,1,64,128]{4,3,2,1,0:T(8,128)S(1)}, f32[1,4,1,64,128]{4,3,2,1,0:T(8,128)S(1)}, u32[]{:S(2)}, u32[]{:S(2)}) collective-permute-start(f32[1,4,1,64,128]{4,3,2,1,0:T(8,128)S(1)} %get-tuple-element.38), channel_id=1, source_target_pairs={{0,1},{1,2},{2,3},{4,5},{5,6},{6,7},{8,9},{9,10},{10,11},{12,13},{... | collective-permute-start | bytes 393224 | tf_op jit(solution)/shard_map/ppermute | solution.py:23
  261.2 2.1 collective-permute-done.36
  265.6 4.5 %collective-permute-start.41 = (f32[1,4,1,32,64]{4,3,2,1,0:T(8,128)S(1)}, f32[1,4,1,32,64]{4,3,2,1,0:T(8,128)S(1)}, u32[]{:S(2)}, u32[]{:S(2)}) collective-permute-start(f32[1,4,1,32,64]{4,3,2,1,0:T(8,128)S(1)} %get-tuple-element.98), channel_id=1, source_target_pairs={{0,1},{1,2},{2,3},{4,5},{5,6},{6,7},{8,9},{9,10},{10,11},{12,13},{... | collective-permute-start | bytes 98312 | tf_op jit(solution)/shard_map/ppermute | solution.py:23
  270.2 1.9 collective-permute-start.39
  272.2 6.3 %collective-permute-done.39 = f32[1,4,2,32,64]{4,3,2,1,0:T(8,128)S(1)} collective-permute-done((f32[1,4,2,32,64]{4,3,2,1,0:T(8,128)S(1)}, f32[1,4,2,32,64]{4,3,2,1,0:T(8,128)S(1)}, u32[]{:S(2)}, u32[]{:S(2)}) %collective-permute-start.39) | collective-permute-done | bytes 65568 | tf_op jit(solution)/shard_map/ppermute | solution.py:34
  280.0 4.5 %collective-permute-start.44 = (f32[1,4,1,32,64]{4,3,2,1,0:T(8,128)S(1)}, f32[1,4,1,32,64]{4,3,2,1,0:T(8,128)S(1)}, u32[]{:S(2)}, u32[]{:S(2)}) collective-permute-start(f32[1,4,1,32,64]{4,3,2,1,0:T(8,128)S(1)} %get-tuple-element.94), channel_id=1, source_target_pairs={{0,1},{1,2},{2,3},{4,5},{5,6},{6,7},{8,9},{9,10},{10,11},{12,13},{... | collective-permute-start | bytes 98312 | tf_op jit(solution)/shard_map/ppermute | solution.py:23
  284.6 1.9 collective-permute-start.42
  286.6 6.3 %collective-permute-done.42 = f32[1,4,2,32,64]{4,3,2,1,0:T(8,128)S(1)} collective-permute-done((f32[1,4,2,32,64]{4,3,2,1,0:T(8,128)S(1)}, f32[1,4,2,32,64]{4,3,2,1,0:T(8,128)S(1)}, u32[]{:S(2)}, u32[]{:S(2)}) %collective-permute-start.42) | collective-permute-done | bytes 65568 | tf_op jit(solution)/shard_map/ppermute | solution.py:34
  293.6 12.4 %all-gather.2 = f32[4,1,2048]{2,1,0:T(1,128)S(1)} all-gather(f32[1,1,2048]{2,1,0:T(1,128)S(1)} %reshape.920), channel_id=1, replica_groups=mesh['tm'=32,'space'=4] {'space'}, dimensions={0}, use_global_device_ids=true | all-gather | bytes 40960 | tf_op jit(solution)/shard_map/all_gather | solution.py:191
  306.7 39.4 %all-gather.9.cloned.1.call-done = f32[32,4,2048]{2,1,0:T(4,128)} async-done(((f32[1,4,2048]{2,1,0:T(4,128)}), f32[32,4,2048]{2,1,0:T(4,128)}) %all-gather.9.cloned.1.call-update) | async-done | bytes 1048592 | tf_op jit(solution)/shard_map/all_gather | solution.py:192
  346.0 2.8 reshape_transpose_reshape.12.src_ref
  348.8 16.6 %shard_map.38 = f32[32,16,512]{2,1,0:T(8,128)} custom-call(f32[32,16,512]{2,1,0:T(8,128)} %reshape_transpose_reshape.12.src_ref, f32[32,16,512]{2,1,0:T(8,128)} %reshape.904.met_ref), custom_call_target="tpu_custom_call" | custom-call | tf_op jit(solution)/shard_map/pallas_call | solution.py:161
  367.7 4.5 %collective-permute-start.47 = (f32[1,4,1,32,64]{4,3,2,1,0:T(8,128)S(1)}, f32[1,4,1,32,64]{4,3,2,1,0:T(8,128)S(1)}, u32[]{:S(2)}, u32[]{:S(2)}) collective-permute-start(f32[1,4,1,32,64]{4,3,2,1,0:T(8,128)S(1)} %get-tuple-element.90), channel_id=1, source_target_pairs={{0,1},{1,2},{2,3},{4,5},{5,6},{6,7},{8,9},{9,10},{10,11},{12,13},{... | collective-permute-start | bytes 98312 | tf_op jit(solution)/shard_map/ppermute | solution.py:23
  372.3 1.9 collective-permute-start.45
  374.3 6.3 %collective-permute-done.45 = f32[1,4,2,32,64]{4,3,2,1,0:T(8,128)S(1)} collective-permute-done((f32[1,4,2,32,64]{4,3,2,1,0:T(8,128)S(1)}, f32[1,4,2,32,64]{4,3,2,1,0:T(8,128)S(1)}, u32[]{:S(2)}, u32[]{:S(2)}) %collective-permute-start.45) | collective-permute-done | bytes 65568 | tf_op jit(solution)/shard_map/ppermute | solution.py:34
  382.1 4.5 %collective-permute-start.50 = (f32[1,4,1,32,64]{4,3,2,1,0:T(8,128)S(1)}, f32[1,4,1,32,64]{4,3,2,1,0:T(8,128)S(1)}, u32[]{:S(2)}, u32[]{:S(2)}) collective-permute-start(f32[1,4,1,32,64]{4,3,2,1,0:T(8,128)S(1)} %get-tuple-element.86), channel_id=1, source_target_pairs={{0,1},{1,2},{2,3},{4,5},{5,6},{6,7},{8,9},{9,10},{10,11},{12,13},{... | collective-permute-start | bytes 98312 | tf_op jit(solution)/shard_map/ppermute | solution.py:23
  386.7 1.9 collective-permute-start.48
  388.7 6.3 %collective-permute-done.48 = f32[1,4,2,32,64]{4,3,2,1,0:T(8,128)S(1)} collective-permute-done((f32[1,4,2,32,64]{4,3,2,1,0:T(8,128)S(1)}, f32[1,4,2,32,64]{4,3,2,1,0:T(8,128)S(1)}, u32[]{:S(2)}, u32[]{:S(2)}) %collective-permute-start.48) | collective-permute-done | bytes 65568 | tf_op jit(solution)/shard_map/ppermute | solution.py:34
  395.6 1.9 collective-permute-start.51
  398.9 4.6 %collective-permute-start.53 = (f32[1,4,1,64,128]{4,3,2,1,0:T(8,128)S(1)}, f32[1,4,1,64,128]{4,3,2,1,0:T(8,128)S(1)}, u32[]{:S(2)}, u32[]{:S(2)}) collective-permute-start(f32[1,4,1,64,128]{4,3,2,1,0:T(8,128)S(1)} %get-tuple-element.34), channel_id=1, source_target_pairs={{0,1},{1,2},{2,3},{4,5},{5,6},{6,7},{8,9},{9,10},{10,11},{12,13},{... | collective-permute-start | bytes 393224 | tf_op jit(solution)/shard_map/ppermute | solution.py:23
  406.2 2.1 collective-permute-done.51
  408.8 1.9 collective-permute-start.54
  412.1 4.6 %collective-permute-start.56 = (f32[1,4,1,64,128]{4,3,2,1,0:T(8,128)S(1)}, f32[1,4,1,64,128]{4,3,2,1,0:T(8,128)S(1)}, u32[]{:S(2)}, u32[]{:S(2)}) collective-permute-start(f32[1,4,1,64,128]{4,3,2,1,0:T(8,128)S(1)} %get-tuple-element.30), channel_id=1, source_target_pairs={{0,1},{1,2},{2,3},{4,5},{5,6},{6,7},{8,9},{9,10},{10,11},{12,13},{... | collective-permute-start | bytes 393224 | tf_op jit(solution)/shard_map/ppermute | solution.py:23
  419.3 2.1 collective-permute-done.54
  (187 shorter events, 70.7 us)
Async XLA Ops:
  6.5 15.1 %copy-start.1 = (f32[1,4,64,128]{3,2,1,0:T(8,128)S(1)}, f32[1,4,64,128]{3,2,1,0:T(8,128)}, u32[]{:S(2)}) copy-start(f32[1,4,64,128]{3,2,1,0:T(8,128)} %param.4) | copy-start | bytes 393220
  6.5 15.2 %copy-start.2 = (s32[4,64,128]{2,1,0:T(8,128)S(1)}, s32[4,64,128]{2,1,0:T(8,128)}, u32[]{:S(2)}) copy-start(s32[4,64,128]{2,1,0:T(8,128)} %param.5) | copy-start | bytes 393220
  6.5 137.6 %all-gather.7.cloned.1.call-start = ((), (), s32[]{:S(2)}) async-start(), calls=%async_computation | async-start | bytes 1351680 | tf_op jit(solution)/shard_map/all_gather | solution.py:192
  6.5 45.9 %collective-permute-start.11 = (f32[1,4,1,32,64]{4,3,2,1,0:T(8,128)S(1)}, f32[1,4,1,32,64]{4,3,2,1,0:T(8,128)S(1)}, u32[]{:S(2)}, u32[]{:S(2)}) collective-permute-start(f32[1,4,1,32,64]{4,3,2,1,0:T(8,128)S(1)} %broadcast.481), channel_id=1, source_target_pairs={{0,1},{1,2},{2,3},{4,5},{5,6},{6,7},{8,9},{9,10},{10,11},{12,13},{... | collective-permute-start | bytes 98312 | tf_op jit(solution)/shard_map/ppermute | solution.py:23
  10.5 43.9 %collective-permute-start.10 = (f32[1,4,1,32,64]{4,3,2,1,0:T(8,128)S(1)}, f32[1,4,1,32,64]{4,3,2,1,0:T(8,128)S(1)}, u32[]{:S(2)}, u32[]{:S(2)}) collective-permute-start(f32[1,4,1,32,64]{4,3,2,1,0:T(8,128)S(1)} %broadcast.481), channel_id=1, source_target_pairs={{1,0},{2,1},{3,2},{5,4},{6,5},{7,6},{9,8},{10,9},{11,10},{13,12},{... | collective-permute-start | bytes 98312 | tf_op jit(solution)/shard_map/ppermute | solution.py:26
  11.8 10.1 %collective-permute-start.2 = (f32[1,4,1,64,128]{4,3,2,1,0:T(8,128)S(1)}, f32[1,4,1,64,128]{4,3,2,1,0:T(8,128)S(1)}, u32[]{:S(2)}, u32[]{:S(2)}) collective-permute-start(f32[1,4,1,64,128]{4,3,2,1,0:T(8,128)S(1)} %broadcast.473), channel_id=1, source_target_pairs={{0,1},{1,2},{2,3},{4,5},{5,6},{6,7},{8,9},{9,10},{10,11},{12,13},{... | collective-permute-start | bytes 393224 | tf_op jit(solution)/shard_map/ppermute | solution.py:23
  16.4 6.9 %collective-permute-start.1 = (f32[1,4,1,64,128]{4,3,2,1,0:T(8,128)S(1)}, f32[1,4,1,64,128]{4,3,2,1,0:T(8,128)S(1)}, u32[]{:S(2)}, u32[]{:S(2)}) collective-permute-start(f32[1,4,1,64,128]{4,3,2,1,0:T(8,128)S(1)} %broadcast.473), channel_id=1, source_target_pairs={{1,0},{2,1},{3,2},{5,4},{6,5},{7,6},{9,8},{10,9},{11,10},{13,12},{... | collective-permute-start | bytes 393224 | tf_op jit(solution)/shard_map/ppermute | solution.py:26
  17.7 12.6 %collective-permute-start = (f32[1,4,4,64,128]{4,3,2,1,0:T(8,128)S(1)}, f32[1,4,4,64,128]{4,3,2,1,0:T(8,128)S(1)}, u32[]{:S(2)}, u32[]{:S(2)}) collective-permute-start(f32[1,4,4,64,128]{4,3,2,1,0:T(8,128)S(1)} %broadcast.471), channel_id=1, source_target_pairs={{0,4},{4,8},{8,12},{12,16},{16,20},{20,24},{24,28},{28,32},{32,36}... | collective-permute-start | bytes 1572872 | tf_op jit(solution)/shard_map/ppermute | solution.py:34
  20.6 9.8 %copy-start = (f32[1,4,4,64,128]{4,3,2,1,0:T(8,128)S(1)}, f32[1,4,4,64,128]{4,3,2,1,0:T(8,128)}, u32[]{:S(2)}) copy-start(f32[1,4,4,64,128]{4,3,2,1,0:T(8,128)} %param.3) | copy-start | bytes 1572868
  30.8 12.6 %collective-permute-start.3 = (f32[1,4,4,64,128]{4,3,2,1,0:T(8,128)S(1)}, f32[1,4,4,64,128]{4,3,2,1,0:T(8,128)S(1)}, u32[]{:S(2)}, u32[]{:S(2)}) collective-permute-start(f32[1,4,4,64,128]{4,3,2,1,0:T(8,128)S(1)} %get-tuple-element.7), channel_id=1, source_target_pairs={{0,4},{4,8},{8,12},{12,16},{16,20},{20,24},{24,28},{28,32},{32,36}... | collective-permute-start | bytes 1572872 | tf_op jit(solution)/shard_map/ppermute | solution.py:34
  32.8 7.8 %collective-permute-start.4 = (f32[1,4,1,64,128]{4,3,2,1,0:T(8,128)S(1)}, f32[1,4,1,64,128]{4,3,2,1,0:T(8,128)S(1)}, u32[]{:S(2)}, u32[]{:S(2)}) collective-permute-start(f32[1,4,1,64,128]{4,3,2,1,0:T(8,128)S(1)} %get-tuple-element.61), channel_id=1, source_target_pairs={{1,0},{2,1},{3,2},{5,4},{6,5},{7,6},{9,8},{10,9},{11,10},{13,12},{... | collective-permute-start | bytes 393224 | tf_op jit(solution)/shard_map/ppermute | solution.py:26
  34.1 7.7 %collective-permute-start.5 = (f32[1,4,1,64,128]{4,3,2,1,0:T(8,128)S(1)}, f32[1,4,1,64,128]{4,3,2,1,0:T(8,128)S(1)}, u32[]{:S(2)}, u32[]{:S(2)}) collective-permute-start(f32[1,4,1,64,128]{4,3,2,1,0:T(8,128)S(1)} %get-tuple-element.62), channel_id=1, source_target_pairs={{0,1},{1,2},{2,3},{4,5},{5,6},{6,7},{8,9},{9,10},{10,11},{12,13},{... | collective-permute-start | bytes 393224 | tf_op jit(solution)/shard_map/ppermute | solution.py:23
  44.0 12.6 %collective-permute-start.6 = (f32[1,4,4,64,128]{4,3,2,1,0:T(8,128)S(1)}, f32[1,4,4,64,128]{4,3,2,1,0:T(8,128)S(1)}, u32[]{:S(2)}, u32[]{:S(2)}) collective-permute-start(f32[1,4,4,64,128]{4,3,2,1,0:T(8,128)S(1)} %fusion.121), channel_id=1, source_target_pairs={{0,4},{4,8},{8,12},{12,16},{16,20},{20,24},{24,28},{28,32},{32,36}... | collective-permute-start | bytes 1572872 | tf_op jit(solution)/shard_map/ppermute | solution.py:34
  46.0 8.6 %collective-permute-start.7 = (f32[1,4,1,64,128]{4,3,2,1,0:T(8,128)S(1)}, f32[1,4,1,64,128]{4,3,2,1,0:T(8,128)S(1)}, u32[]{:S(2)}, u32[]{:S(2)}) collective-permute-start(f32[1,4,1,64,128]{4,3,2,1,0:T(8,128)S(1)} %get-tuple-element.57), channel_id=1, source_target_pairs={{1,0},{2,1},{3,2},{5,4},{6,5},{7,6},{9,8},{10,9},{11,10},{13,12},{... | collective-permute-start | bytes 393224 | tf_op jit(solution)/shard_map/ppermute | solution.py:26
  47.3 7.7 %collective-permute-start.8 = (f32[1,4,1,64,128]{4,3,2,1,0:T(8,128)S(1)}, f32[1,4,1,64,128]{4,3,2,1,0:T(8,128)S(1)}, u32[]{:S(2)}, u32[]{:S(2)}) collective-permute-start(f32[1,4,1,64,128]{4,3,2,1,0:T(8,128)S(1)} %get-tuple-element.58), channel_id=1, source_target_pairs={{0,1},{1,2},{2,3},{4,5},{5,6},{6,7},{8,9},{9,10},{10,11},{12,13},{... | collective-permute-start | bytes 393224 | tf_op jit(solution)/shard_map/ppermute | solution.py:23
  52.5 8.4 %collective-permute-start.9 = (f32[1,4,2,32,64]{4,3,2,1,0:T(8,128)S(1)}, f32[1,4,2,32,64]{4,3,2,1,0:T(8,128)S(1)}, u32[]{:S(2)}, u32[]{:S(2)}) collective-permute-start(f32[1,4,2,32,64]{4,3,2,1,0:T(8,128)S(1)} %broadcast.480), channel_id=1, source_target_pairs={{0,4},{4,8},{8,12},{12,16},{16,20},{20,24},{24,28},{28,32},{32,36}... | collective-permute-start | bytes 196616 | tf_op jit(solution)/shard_map/ppermute | solution.py:34
  61.1 7.8 %collective-permute-start.13 = (f32[1,4,1,32,64]{4,3,2,1,0:T(8,128)S(1)}, f32[1,4,1,32,64]{4,3,2,1,0:T(8,128)S(1)}, u32[]{:S(2)}, u32[]{:S(2)}) collective-permute-start(f32[1,4,1,32,64]{4,3,2,1,0:T(8,128)S(1)} %get-tuple-element.113), channel_id=1, source_target_pairs={{1,0},{2,1},{3,2},{5,4},{6,5},{7,6},{9,8},{10,9},{11,10},{13,12},{... | collective-permute-start | bytes 98312 | tf_op jit(solution)/shard_map/ppermute | solution.py:26
  62.4 6.5 %collective-permute-start.14 = (f32[1,4,1,32,64]{4,3,2,1,0:T(8,128)S(1)}, f32[1,4,1,32,64]{4,3,2,1,0:T(8,128)S(1)}, u32[]{:S(2)}, u32[]{:S(2)}) collective-permute-start(f32[1,4,1,32,64]{4,3,2,1,0:T(8,128)S(1)} %get-tuple-element.114), channel_id=1, source_target_pairs={{0,1},{1,2},{2,3},{4,5},{5,6},{6,7},{8,9},{9,10},{10,11},{12,13},{... | collective-permute-start | bytes 98312 | tf_op jit(solution)/shard_map/ppermute | solution.py:23
  67.0 8.4 %collective-permute-start.12 = (f32[1,4,2,32,64]{4,3,2,1,0:T(8,128)S(1)}, f32[1,4,2,32,64]{4,3,2,1,0:T(8,128)S(1)}, u32[]{:S(2)}, u32[]{:S(2)}) collective-permute-start(f32[1,4,2,32,64]{4,3,2,1,0:T(8,128)S(1)} %get-tuple-element.5), channel_id=1, source_target_pairs={{0,4},{4,8},{8,12},{12,16},{16,20},{20,24},{24,28},{28,32},{32,36}... | collective-permute-start | bytes 196616 | tf_op jit(solution)/shard_map/ppermute | solution.py:34
  75.6 8.0 %collective-permute-start.16 = (f32[1,4,1,32,64]{4,3,2,1,0:T(8,128)S(1)}, f32[1,4,1,32,64]{4,3,2,1,0:T(8,128)S(1)}, u32[]{:S(2)}, u32[]{:S(2)}) collective-permute-start(f32[1,4,1,32,64]{4,3,2,1,0:T(8,128)S(1)} %get-tuple-element.109), channel_id=1, source_target_pairs={{1,0},{2,1},{3,2},{5,4},{6,5},{7,6},{9,8},{10,9},{11,10},{13,12},{... | collective-permute-start | bytes 98312 | tf_op jit(solution)/shard_map/ppermute | solution.py:26
  76.9 6.7 %collective-permute-start.17 = (f32[1,4,1,32,64]{4,3,2,1,0:T(8,128)S(1)}, f32[1,4,1,32,64]{4,3,2,1,0:T(8,128)S(1)}, u32[]{:S(2)}, u32[]{:S(2)}) collective-permute-start(f32[1,4,1,32,64]{4,3,2,1,0:T(8,128)S(1)} %get-tuple-element.110), channel_id=1, source_target_pairs={{0,1},{1,2},{2,3},{4,5},{5,6},{6,7},{8,9},{9,10},{10,11},{12,13},{... | collective-permute-start | bytes 98312 | tf_op jit(solution)/shard_map/ppermute | solution.py:23
  81.7 8.4 %collective-permute-start.15 = (f32[1,4,2,32,64]{4,3,2,1,0:T(8,128)S(1)}, f32[1,4,2,32,64]{4,3,2,1,0:T(8,128)S(1)}, u32[]{:S(2)}, u32[]{:S(2)}) collective-permute-start(f32[1,4,2,32,64]{4,3,2,1,0:T(8,128)S(1)} %fusion.255), channel_id=1, source_target_pairs={{0,4},{4,8},{8,12},{12,16},{16,20},{20,24},{24,28},{28,32},{32,36}... | collective-permute-start | bytes 196616 | tf_op jit(solution)/shard_map/ppermute | solution.py:34
  104.6 241.4 %all-gather.9.cloned.1.call-start = ((), (), s32[]{:S(2)}) async-start(), calls=%async_computation.1 | async-start | bytes 1081344 | tf_op jit(solution)/shard_map/all_gather | solution.py:192
  168.8 7.8 %collective-permute-start.19 = (f32[1,4,1,32,64]{4,3,2,1,0:T(8,128)S(1)}, f32[1,4,1,32,64]{4,3,2,1,0:T(8,128)S(1)}, u32[]{:S(2)}, u32[]{:S(2)}) collective-permute-start(f32[1,4,1,32,64]{4,3,2,1,0:T(8,128)S(1)} %get-tuple-element.105), channel_id=1, source_target_pairs={{1,0},{2,1},{3,2},{5,4},{6,5},{7,6},{9,8},{10,9},{11,10},{13,12},{... | collective-permute-start | bytes 98312 | tf_op jit(solution)/shard_map/ppermute | solution.py:26
  170.1 6.5 %collective-permute-start.20 = (f32[1,4,1,32,64]{4,3,2,1,0:T(8,128)S(1)}, f32[1,4,1,32,64]{4,3,2,1,0:T(8,128)S(1)}, u32[]{:S(2)}, u32[]{:S(2)}) collective-permute-start(f32[1,4,1,32,64]{4,3,2,1,0:T(8,128)S(1)} %get-tuple-element.106), channel_id=1, source_target_pairs={{0,1},{1,2},{2,3},{4,5},{5,6},{6,7},{8,9},{9,10},{10,11},{12,13},{... | collective-permute-start | bytes 98312 | tf_op jit(solution)/shard_map/ppermute | solution.py:23
  174.7 8.4 %collective-permute-start.18 = (f32[1,4,2,32,64]{4,3,2,1,0:T(8,128)S(1)}, f32[1,4,2,32,64]{4,3,2,1,0:T(8,128)S(1)}, u32[]{:S(2)}, u32[]{:S(2)}) collective-permute-start(f32[1,4,2,32,64]{4,3,2,1,0:T(8,128)S(1)} %broadcast_add_fusion.1), channel_id=1, source_target_pairs={{0,4},{4,8},{8,12},{12,16},{16,20},{20,24},{24,28},{28,32},{32,36}... | collective-permute-start | bytes 196616 | tf_op jit(solution)/shard_map/ppermute | solution.py:34
  183.2 7.8 %collective-permute-start.22 = (f32[1,4,1,32,64]{4,3,2,1,0:T(8,128)S(1)}, f32[1,4,1,32,64]{4,3,2,1,0:T(8,128)S(1)}, u32[]{:S(2)}, u32[]{:S(2)}) collective-permute-start(f32[1,4,1,32,64]{4,3,2,1,0:T(8,128)S(1)} %get-tuple-element.101), channel_id=1, source_target_pairs={{1,0},{2,1},{3,2},{5,4},{6,5},{7,6},{9,8},{10,9},{11,10},{13,12},{... | collective-permute-start | bytes 98312 | tf_op jit(solution)/shard_map/ppermute | solution.py:26
  184.5 6.5 %collective-permute-start.23 = (f32[1,4,1,32,64]{4,3,2,1,0:T(8,128)S(1)}, f32[1,4,1,32,64]{4,3,2,1,0:T(8,128)S(1)}, u32[]{:S(2)}, u32[]{:S(2)}) collective-permute-start(f32[1,4,1,32,64]{4,3,2,1,0:T(8,128)S(1)} %get-tuple-element.102), channel_id=1, source_target_pairs={{0,1},{1,2},{2,3},{4,5},{5,6},{6,7},{8,9},{9,10},{10,11},{12,13},{... | collective-permute-start | bytes 98312 | tf_op jit(solution)/shard_map/ppermute | solution.py:23
  189.1 8.4 %collective-permute-start.21 = (f32[1,4,2,32,64]{4,3,2,1,0:T(8,128)S(1)}, f32[1,4,2,32,64]{4,3,2,1,0:T(8,128)S(1)}, u32[]{:S(2)}, u32[]{:S(2)}) collective-permute-start(f32[1,4,2,32,64]{4,3,2,1,0:T(8,128)S(1)} %fusion.228), channel_id=1, source_target_pairs={{0,4},{4,8},{8,12},{12,16},{16,20},{20,24},{24,28},{28,32},{32,36}... | collective-permute-start | bytes 196616 | tf_op jit(solution)/shard_map/ppermute | solution.py:34
  198.0 12.6 %collective-permute-start.24 = (f32[1,4,4,64,128]{4,3,2,1,0:T(8,128)S(1)}, f32[1,4,4,64,128]{4,3,2,1,0:T(8,128)S(1)}, u32[]{:S(2)}, u32[]{:S(2)}) collective-permute-start(f32[1,4,4,64,128]{4,3,2,1,0:T(8,128)S(1)} %add.556), channel_id=1, source_target_pairs={{0,4},{4,8},{8,12},{12,16},{16,20},{20,24},{24,28},{28,32},{32,36}... | collective-permute-start | bytes 1572872 | tf_op jit(solution)/shard_map/ppermute | solution.py:34
  200.0 6.9 %collective-permute-start.25 = (f32[1,4,1,64,128]{4,3,2,1,0:T(8,128)S(1)}, f32[1,4,1,64,128]{4,3,2,1,0:T(8,128)S(1)}, u32[]{:S(2)}, u32[]{:S(2)}) collective-permute-start(f32[1,4,1,64,128]{4,3,2,1,0:T(8,128)S(1)} %get-tuple-element.53), channel_id=1, source_target_pairs={{1,0},{2,1},{3,2},{5,4},{6,5},{7,6},{9,8},{10,9},{11,10},{13,12},{... | collective-permute-start | bytes 393224 | tf_op jit(solution)/shard_map/ppermute | solution.py:26
  201.3 7.1 %collective-permute-start.26 = (f32[1,4,1,64,128]{4,3,2,1,0:T(8,128)S(1)}, f32[1,4,1,64,128]{4,3,2,1,0:T(8,128)S(1)}, u32[]{:S(2)}, u32[]{:S(2)}) collective-permute-start(f32[1,4,1,64,128]{4,3,2,1,0:T(8,128)S(1)} %get-tuple-element.54), channel_id=1, source_target_pairs={{0,1},{1,2},{2,3},{4,5},{5,6},{6,7},{8,9},{9,10},{10,11},{12,13},{... | collective-permute-start | bytes 393224 | tf_op jit(solution)/shard_map/ppermute | solution.py:23
  211.2 12.6 %collective-permute-start.27 = (f32[1,4,4,64,128]{4,3,2,1,0:T(8,128)S(1)}, f32[1,4,4,64,128]{4,3,2,1,0:T(8,128)S(1)}, u32[]{:S(2)}, u32[]{:S(2)}) collective-permute-start(f32[1,4,4,64,128]{4,3,2,1,0:T(8,128)S(1)} %fusion.95), channel_id=1, source_target_pairs={{0,4},{4,8},{8,12},{12,16},{16,20},{20,24},{24,28},{28,32},{32,36}... | collective-permute-start | bytes 1572872 | tf_op jit(solution)/shard_map/ppermute | solution.py:34
  213.2 6.9 %collective-permute-start.28 = (f32[1,4,1,64,128]{4,3,2,1,0:T(8,128)S(1)}, f32[1,4,1,64,128]{4,3,2,1,0:T(8,128)S(1)}, u32[]{:S(2)}, u32[]{:S(2)}) collective-permute-start(f32[1,4,1,64,128]{4,3,2,1,0:T(8,128)S(1)} %get-tuple-element.49), channel_id=1, source_target_pairs={{1,0},{2,1},{3,2},{5,4},{6,5},{7,6},{9,8},{10,9},{11,10},{13,12},{... | collective-permute-start | bytes 393224 | tf_op jit(solution)/shard_map/ppermute | solution.py:26
  214.5 7.1 %collective-permute-start.29 = (f32[1,4,1,64,128]{4,3,2,1,0:T(8,128)S(1)}, f32[1,4,1,64,128]{4,3,2,1,0:T(8,128)S(1)}, u32[]{:S(2)}, u32[]{:S(2)}) collective-permute-start(f32[1,4,1,64,128]{4,3,2,1,0:T(8,128)S(1)} %get-tuple-element.50), channel_id=1, source_target_pairs={{0,1},{1,2},{2,3},{4,5},{5,6},{6,7},{8,9},{9,10},{10,11},{12,13},{... | collective-permute-start | bytes 393224 | tf_op jit(solution)/shard_map/ppermute | solution.py:23
  224.4 12.6 %collective-permute-start.30 = (f32[1,4,4,64,128]{4,3,2,1,0:T(8,128)S(1)}, f32[1,4,4,64,128]{4,3,2,1,0:T(8,128)S(1)}, u32[]{:S(2)}, u32[]{:S(2)}) collective-permute-start(f32[1,4,4,64,128]{4,3,2,1,0:T(8,128)S(1)} %fusion.81), channel_id=1, source_target_pairs={{0,4},{4,8},{8,12},{12,16},{16,20},{20,24},{24,28},{28,32},{32,36}... | collective-permute-start | bytes 1572872 | tf_op jit(solution)/shard_map/ppermute | solution.py:34
  226.3 6.9 %collective-permute-start.31 = (f32[1,4,1,64,128]{4,3,2,1,0:T(8,128)S(1)}, f32[1,4,1,64,128]{4,3,2,1,0:T(8,128)S(1)}, u32[]{:S(2)}, u32[]{:S(2)}) collective-permute-start(f32[1,4,1,64,128]{4,3,2,1,0:T(8,128)S(1)} %get-tuple-element.45), channel_id=1, source_target_pairs={{1,0},{2,1},{3,2},{5,4},{6,5},{7,6},{9,8},{10,9},{11,10},{13,12},{... | collective-permute-start | bytes 393224 | tf_op jit(solution)/shard_map/ppermute | solution.py:26
  227.6 7.1 %collective-permute-start.32 = (f32[1,4,1,64,128]{4,3,2,1,0:T(8,128)S(1)}, f32[1,4,1,64,128]{4,3,2,1,0:T(8,128)S(1)}, u32[]{:S(2)}, u32[]{:S(2)}) collective-permute-start(f32[1,4,1,64,128]{4,3,2,1,0:T(8,128)S(1)} %get-tuple-element.46), channel_id=1, source_target_pairs={{0,1},{1,2},{2,3},{4,5},{5,6},{6,7},{8,9},{9,10},{10,11},{12,13},{... | collective-permute-start | bytes 393224 | tf_op jit(solution)/shard_map/ppermute | solution.py:23
  237.5 12.6 %collective-permute-start.33 = (f32[1,4,4,64,128]{4,3,2,1,0:T(8,128)S(1)}, f32[1,4,4,64,128]{4,3,2,1,0:T(8,128)S(1)}, u32[]{:S(2)}, u32[]{:S(2)}) collective-permute-start(f32[1,4,4,64,128]{4,3,2,1,0:T(8,128)S(1)} %fusion.67), channel_id=1, source_target_pairs={{0,4},{4,8},{8,12},{12,16},{16,20},{20,24},{24,28},{28,32},{32,36}... | collective-permute-start | bytes 1572872 | tf_op jit(solution)/shard_map/ppermute | solution.py:34
  239.5 6.9 %collective-permute-start.34 = (f32[1,4,1,64,128]{4,3,2,1,0:T(8,128)S(1)}, f32[1,4,1,64,128]{4,3,2,1,0:T(8,128)S(1)}, u32[]{:S(2)}, u32[]{:S(2)}) collective-permute-start(f32[1,4,1,64,128]{4,3,2,1,0:T(8,128)S(1)} %get-tuple-element.41), channel_id=1, source_target_pairs={{1,0},{2,1},{3,2},{5,4},{6,5},{7,6},{9,8},{10,9},{11,10},{13,12},{... | collective-permute-start | bytes 393224 | tf_op jit(solution)/shard_map/ppermute | solution.py:26
  240.8 7.1 %collective-permute-start.35 = (f32[1,4,1,64,128]{4,3,2,1,0:T(8,128)S(1)}, f32[1,4,1,64,128]{4,3,2,1,0:T(8,128)S(1)}, u32[]{:S(2)}, u32[]{:S(2)}) collective-permute-start(f32[1,4,1,64,128]{4,3,2,1,0:T(8,128)S(1)} %get-tuple-element.42), channel_id=1, source_target_pairs={{0,1},{1,2},{2,3},{4,5},{5,6},{6,7},{8,9},{9,10},{10,11},{12,13},{... | collective-permute-start | bytes 393224 | tf_op jit(solution)/shard_map/ppermute | solution.py:23
  250.7 12.6 %collective-permute-start.36 = (f32[1,4,4,64,128]{4,3,2,1,0:T(8,128)S(1)}, f32[1,4,4,64,128]{4,3,2,1,0:T(8,128)S(1)}, u32[]{:S(2)}, u32[]{:S(2)}) collective-permute-start(f32[1,4,4,64,128]{4,3,2,1,0:T(8,128)S(1)} %fusion.53), channel_id=1, source_target_pairs={{0,4},{4,8},{8,12},{12,16},{16,20},{20,24},{24,28},{28,32},{32,36}... | collective-permute-start | bytes 1572872 | tf_op jit(solution)/shard_map/ppermute | solution.py:34
  252.6 6.9 %collective-permute-start.37 = (f32[1,4,1,64,128]{4,3,2,1,0:T(8,128)S(1)}, f32[1,4,1,64,128]{4,3,2,1,0:T(8,128)S(1)}, u32[]{:S(2)}, u32[]{:S(2)}) collective-permute-start(f32[1,4,1,64,128]{4,3,2,1,0:T(8,128)S(1)} %get-tuple-element.37), channel_id=1, source_target_pairs={{1,0},{2,1},{3,2},{5,4},{6,5},{7,6},{9,8},{10,9},{11,10},{13,12},{... | collective-permute-start | bytes 393224 | tf_op jit(solution)/shard_map/ppermute | solution.py:26
  253.9 7.1 %collective-permute-start.38 = (f32[1,4,1,64,128]{4,3,2,1,0:T(8,128)S(1)}, f32[1,4,1,64,128]{4,3,2,1,0:T(8,128)S(1)}, u32[]{:S(2)}, u32[]{:S(2)}) collective-permute-start(f32[1,4,1,64,128]{4,3,2,1,0:T(8,128)S(1)} %get-tuple-element.38), channel_id=1, source_target_pairs={{0,1},{1,2},{2,3},{4,5},{5,6},{6,7},{8,9},{9,10},{10,11},{12,13},{... | collective-permute-start | bytes 393224 | tf_op jit(solution)/shard_map/ppermute | solution.py:23
  264.3 7.8 %collective-permute-start.40 = (f32[1,4,1,32,64]{4,3,2,1,0:T(8,128)S(1)}, f32[1,4,1,32,64]{4,3,2,1,0:T(8,128)S(1)}, u32[]{:S(2)}, u32[]{:S(2)}) collective-permute-start(f32[1,4,1,32,64]{4,3,2,1,0:T(8,128)S(1)} %get-tuple-element.97), channel_id=1, source_target_pairs={{1,0},{2,1},{3,2},{5,4},{6,5},{7,6},{9,8},{10,9},{11,10},{13,12},{... | collective-permute-start | bytes 98312 | tf_op jit(solution)/shard_map/ppermute | solution.py:26
  265.6 6.5 %collective-permute-start.41 = (f32[1,4,1,32,64]{4,3,2,1,0:T(8,128)S(1)}, f32[1,4,1,32,64]{4,3,2,1,0:T(8,128)S(1)}, u32[]{:S(2)}, u32[]{:S(2)}) collective-permute-start(f32[1,4,1,32,64]{4,3,2,1,0:T(8,128)S(1)} %get-tuple-element.98), channel_id=1, source_target_pairs={{0,1},{1,2},{2,3},{4,5},{5,6},{6,7},{8,9},{9,10},{10,11},{12,13},{... | collective-permute-start | bytes 98312 | tf_op jit(solution)/shard_map/ppermute | solution.py:23
  270.2 8.4 %collective-permute-start.39 = (f32[1,4,2,32,64]{4,3,2,1,0:T(8,128)S(1)}, f32[1,4,2,32,64]{4,3,2,1,0:T(8,128)S(1)}, u32[]{:S(2)}, u32[]{:S(2)}) collective-permute-start(f32[1,4,2,32,64]{4,3,2,1,0:T(8,128)S(1)} %multiply_divide_fusion), channel_id=1, source_target_pairs={{0,4},{4,8},{8,12},{12,16},{16,20},{20,24},{24,28},{28,32},{32,36}... | collective-permute-start | bytes 196616 | tf_op jit(solution)/shard_map/ppermute | solution.py:34
  278.7 7.8 %collective-permute-start.43 = (f32[1,4,1,32,64]{4,3,2,1,0:T(8,128)S(1)}, f32[1,4,1,32,64]{4,3,2,1,0:T(8,128)S(1)}, u32[]{:S(2)}, u32[]{:S(2)}) collective-permute-start(f32[1,4,1,32,64]{4,3,2,1,0:T(8,128)S(1)} %get-tuple-element.93), channel_id=1, source_target_pairs={{1,0},{2,1},{3,2},{5,4},{6,5},{7,6},{9,8},{10,9},{11,10},{13,12},{... | collective-permute-start | bytes 98312 | tf_op jit(solution)/shard_map/ppermute | solution.py:26
  280.0 6.5 %collective-permute-start.44 = (f32[1,4,1,32,64]{4,3,2,1,0:T(8,128)S(1)}, f32[1,4,1,32,64]{4,3,2,1,0:T(8,128)S(1)}, u32[]{:S(2)}, u32[]{:S(2)}) collective-permute-start(f32[1,4,1,32,64]{4,3,2,1,0:T(8,128)S(1)} %get-tuple-element.94), channel_id=1, source_target_pairs={{0,1},{1,2},{2,3},{4,5},{5,6},{6,7},{8,9},{9,10},{10,11},{12,13},{... | collective-permute-start | bytes 98312 | tf_op jit(solution)/shard_map/ppermute | solution.py:23
  284.6 8.4 %collective-permute-start.42 = (f32[1,4,2,32,64]{4,3,2,1,0:T(8,128)S(1)}, f32[1,4,2,32,64]{4,3,2,1,0:T(8,128)S(1)}, u32[]{:S(2)}, u32[]{:S(2)}) collective-permute-start(f32[1,4,2,32,64]{4,3,2,1,0:T(8,128)S(1)} %fusion.198), channel_id=1, source_target_pairs={{0,4},{4,8},{8,12},{12,16},{16,20},{20,24},{24,28},{28,32},{32,36}... | collective-permute-start | bytes 196616 | tf_op jit(solution)/shard_map/ppermute | solution.py:34
  366.4 7.8 %collective-permute-start.46 = (f32[1,4,1,32,64]{4,3,2,1,0:T(8,128)S(1)}, f32[1,4,1,32,64]{4,3,2,1,0:T(8,128)S(1)}, u32[]{:S(2)}, u32[]{:S(2)}) collective-permute-start(f32[1,4,1,32,64]{4,3,2,1,0:T(8,128)S(1)} %get-tuple-element.89), channel_id=1, source_target_pairs={{1,0},{2,1},{3,2},{5,4},{6,5},{7,6},{9,8},{10,9},{11,10},{13,12},{... | collective-permute-start | bytes 98312 | tf_op jit(solution)/shard_map/ppermute | solution.py:26
  367.7 6.5 %collective-permute-start.47 = (f32[1,4,1,32,64]{4,3,2,1,0:T(8,128)S(1)}, f32[1,4,1,32,64]{4,3,2,1,0:T(8,128)S(1)}, u32[]{:S(2)}, u32[]{:S(2)}) collective-permute-start(f32[1,4,1,32,64]{4,3,2,1,0:T(8,128)S(1)} %get-tuple-element.90), channel_id=1, source_target_pairs={{0,1},{1,2},{2,3},{4,5},{5,6},{6,7},{8,9},{9,10},{10,11},{12,13},{... | collective-permute-start | bytes 98312 | tf_op jit(solution)/shard_map/ppermute | solution.py:23
  372.3 8.4 %collective-permute-start.45 = (f32[1,4,2,32,64]{4,3,2,1,0:T(8,128)S(1)}, f32[1,4,2,32,64]{4,3,2,1,0:T(8,128)S(1)}, u32[]{:S(2)}, u32[]{:S(2)}) collective-permute-start(f32[1,4,2,32,64]{4,3,2,1,0:T(8,128)S(1)} %broadcast_add_fusion), channel_id=1, source_target_pairs={{0,4},{4,8},{8,12},{12,16},{16,20},{20,24},{24,28},{28,32},{32,36}... | collective-permute-start | bytes 196616 | tf_op jit(solution)/shard_map/ppermute | solution.py:34
  380.8 7.8 %collective-permute-start.49 = (f32[1,4,1,32,64]{4,3,2,1,0:T(8,128)S(1)}, f32[1,4,1,32,64]{4,3,2,1,0:T(8,128)S(1)}, u32[]{:S(2)}, u32[]{:S(2)}) collective-permute-start(f32[1,4,1,32,64]{4,3,2,1,0:T(8,128)S(1)} %get-tuple-element.85), channel_id=1, source_target_pairs={{1,0},{2,1},{3,2},{5,4},{6,5},{7,6},{9,8},{10,9},{11,10},{13,12},{... | collective-permute-start | bytes 98312 | tf_op jit(solution)/shard_map/ppermute | solution.py:26
  382.1 6.5 %collective-permute-start.50 = (f32[1,4,1,32,64]{4,3,2,1,0:T(8,128)S(1)}, f32[1,4,1,32,64]{4,3,2,1,0:T(8,128)S(1)}, u32[]{:S(2)}, u32[]{:S(2)}) collective-permute-start(f32[1,4,1,32,64]{4,3,2,1,0:T(8,128)S(1)} %get-tuple-element.86), channel_id=1, source_target_pairs={{0,1},{1,2},{2,3},{4,5},{5,6},{6,7},{8,9},{9,10},{10,11},{12,13},{... | collective-permute-start | bytes 98312 | tf_op jit(solution)/shard_map/ppermute | solution.py:23
  386.7 8.4 %collective-permute-start.48 = (f32[1,4,2,32,64]{4,3,2,1,0:T(8,128)S(1)}, f32[1,4,2,32,64]{4,3,2,1,0:T(8,128)S(1)}, u32[]{:S(2)}, u32[]{:S(2)}) collective-permute-start(f32[1,4,2,32,64]{4,3,2,1,0:T(8,128)S(1)} %fusion.171), channel_id=1, source_target_pairs={{0,4},{4,8},{8,12},{12,16},{16,20},{20,24},{24,28},{28,32},{32,36}... | collective-permute-start | bytes 196616 | tf_op jit(solution)/shard_map/ppermute | solution.py:34
  395.6 12.6 %collective-permute-start.51 = (f32[1,4,4,64,128]{4,3,2,1,0:T(8,128)S(1)}, f32[1,4,4,64,128]{4,3,2,1,0:T(8,128)S(1)}, u32[]{:S(2)}, u32[]{:S(2)}) collective-permute-start(f32[1,4,4,64,128]{4,3,2,1,0:T(8,128)S(1)} %add.605), channel_id=1, source_target_pairs={{0,4},{4,8},{8,12},{12,16},{16,20},{20,24},{24,28},{28,32},{32,36}... | collective-permute-start | bytes 1572872 | tf_op jit(solution)/shard_map/ppermute | solution.py:34
  397.6 6.9 %collective-permute-start.52 = (f32[1,4,1,64,128]{4,3,2,1,0:T(8,128)S(1)}, f32[1,4,1,64,128]{4,3,2,1,0:T(8,128)S(1)}, u32[]{:S(2)}, u32[]{:S(2)}) collective-permute-start(f32[1,4,1,64,128]{4,3,2,1,0:T(8,128)S(1)} %get-tuple-element.33), channel_id=1, source_target_pairs={{1,0},{2,1},{3,2},{5,4},{6,5},{7,6},{9,8},{10,9},{11,10},{13,12},{... | collective-permute-start | bytes 393224 | tf_op jit(solution)/shard_map/ppermute | solution.py:26
  398.9 7.1 %collective-permute-start.53 = (f32[1,4,1,64,128]{4,3,2,1,0:T(8,128)S(1)}, f32[1,4,1,64,128]{4,3,2,1,0:T(8,128)S(1)}, u32[]{:S(2)}, u32[]{:S(2)}) collective-permute-start(f32[1,4,1,64,128]{4,3,2,1,0:T(8,128)S(1)} %get-tuple-element.34), channel_id=1, source_target_pairs={{0,1},{1,2},{2,3},{4,5},{5,6},{6,7},{8,9},{9,10},{10,11},{12,13},{... | collective-permute-start | bytes 393224 | tf_op jit(solution)/shard_map/ppermute | solution.py:23
  408.8 12.6 %collective-permute-start.54 = (f32[1,4,4,64,128]{4,3,2,1,0:T(8,128)S(1)}, f32[1,4,4,64,128]{4,3,2,1,0:T(8,128)S(1)}, u32[]{:S(2)}, u32[]{:S(2)}) collective-permute-start(f32[1,4,4,64,128]{4,3,2,1,0:T(8,128)S(1)} %fusion.27), channel_id=1, source_target_pairs={{0,4},{4,8},{8,12},{12,16},{16,20},{20,24},{24,28},{28,32},{32,36}... | collective-permute-start | bytes 1572872 | tf_op jit(solution)/shard_map/ppermute | solution.py:34
  410.8 6.9 %collective-permute-start.55 = (f32[1,4,1,64,128]{4,3,2,1,0:T(8,128)S(1)}, f32[1,4,1,64,128]{4,3,2,1,0:T(8,128)S(1)}, u32[]{:S(2)}, u32[]{:S(2)}) collective-permute-start(f32[1,4,1,64,128]{4,3,2,1,0:T(8,128)S(1)} %get-tuple-element.29), channel_id=1, source_target_pairs={{1,0},{2,1},{3,2},{5,4},{6,5},{7,6},{9,8},{10,9},{11,10},{13,12},{... | collective-permute-start | bytes 393224 | tf_op jit(solution)/shard_map/ppermute | solution.py:26
  412.1 7.1 %collective-permute-start.56 = (f32[1,4,1,64,128]{4,3,2,1,0:T(8,128)S(1)}, f32[1,4,1,64,128]{4,3,2,1,0:T(8,128)S(1)}, u32[]{:S(2)}, u32[]{:S(2)}) collective-permute-start(f32[1,4,1,64,128]{4,3,2,1,0:T(8,128)S(1)} %get-tuple-element.30), channel_id=1, source_target_pairs={{0,1},{1,2},{2,3},{4,5},{5,6},{6,7},{8,9},{9,10},{10,11},{12,13},{... | collective-permute-start | bytes 393224 | tf_op jit(solution)/shard_map/ppermute | solution.py:23
Sparse Core Ops, SparseCore 0:
  104.7 39.3 all-gather.6
  306.8 39.2 all-gather.8

commit v6 on v5

--- a/solution.py
+++ b/solution.py
@@ -231,33 +231,30 @@
     pinned_levels = (pinned, None)
     gathered = {}
 
+    def sweep(depth, values, source, diagonal):
+        if values is None:
+            return OMEGA * source / diagonal
+        spacing = 2.0**depth
+        applied = apply_local(values, metrics[depth], spacing, pinned_levels[depth])
+        return values + OMEGA * (source - applied) / diagonal
+
     def cycle(depth, values, source):
         spacing = 2.0**depth
         diagonal = diagonal_of(metrics[depth], spacing, pinned_levels[depth])
         for repeat in range(NU):
-            values = (
-                values
-                + OMEGA
-                * (source - apply_local(values, metrics[depth], spacing, pinned_levels[depth]))
-                / diagonal
-            )
+            values = sweep(depth, values, source, diagonal)
         residual = source - apply_local(values, metrics[depth], spacing, pinned_levels[depth])
         coarse_source = restrict(residual)
         if depth == 1:
             correction = coarse_correction(coarse_source, metric_two, gathered)
         else:
-            correction = cycle(1, jnp.zeros_like(coarse_source), coarse_source)
+            correction = cycle(1, None, coarse_source)
         values = values + prolong(correction)
         for repeat in range(NU):
-            values = (
-                values
-                + OMEGA
-                * (source - apply_local(values, metrics[depth], spacing, pinned_levels[depth]))
-                / diagonal
-            )
+            values = sweep(depth, values, source, diagonal)
         return values
 
-    solution = jnp.zeros_like(right_side)
+    solution = None
     for repeat in range(CYCLES):
         solution = cycle(0, solution, right_side)
     return solution

time: 432 us -> 407 us (0.942)
  starting transfers between devices: 148 us -> 132 us
  waiting for transfers between devices: 179 us -> 170 us
    ppermute x19 -> x17, waiting for transfers between devices: 78.7 us -> 67.5 us  [from_behind(): return lax.ppermute(array, axis, pairs)]
    ppermute x19 -> x17, starting transfers between devices: 87.3 us -> 77.6 us  [with_halo(): lax.ppermute(lax.slice_in_dim(block, block.shape[dim] - width, None, axis...]
    ppermute x19 -> x17, starting transfers between devices: 36.5 us -> 32.8 us  [from_behind(): return lax.ppermute(array, axis, pairs)]
    ppermute x19 -> x17, starting transfers between devices: 24.5 us -> 22 us  [with_halo(): lax.ppermute(lax.slice_in_dim(block, 0, width, axis=dim), axis, backward)]
    ppermute x19 -> x17, waiting for transfers between devices: 12.1 us -> 13.7 us  [with_halo(): lax.ppermute(lax.slice_in_dim(block, block.shape[dim] - width, None, axis...]
    ppermute x19 -> x17, waiting for transfers between devices: 9.43 us -> 10.3 us  [with_halo(): lax.ppermute(lax.slice_in_dim(block, 0, width, axis=dim), axis, backward)]
  transfers between devices with their start and end apart: 59 -> 53, of which waited for: 39 -> 37; matrix products, arithmetic and copies ran while one was open for 2% -> 1% of each run, Pallas kernels for 0% -> 0%
where the time goes in v6:
time: 407 us; the launch traced here: 405 us
  waiting for transfers between devices  170 us (42%)
  starting transfers between devices  132 us (32%)
  Pallas kernels  33.1 us (8%)
  blocking collectives  25.5 us (6%)
  between operations  14.6 us (4%)
  local copies, waits for them, and re-layouts  14.5 us (4%)
  other arithmetic  12.6 us (3%)
    all_gather x2, waiting for transfers between devices, gather_all(): return lax.all_gather(within, 'tm', axis=0, tiled=True)  78.8 us
    ppermute x17, starting transfers between devices, with_halo(): lax.ppermute(lax.slice_in_dim(block, block.shape[dim] - width, None, axis...  77.6 us
    ppermute x17, waiting for transfers between devices, from_behind(): return lax.ppermute(array, axis, pairs)  67.5 us
    pallas_call x2, Pallas kernels, coarse_solve(): pl.pallas_call(kernel, out_shape=jax.ShapeDtypeStruct(flat_source.shape,...  33.1 us
    ppermute x17, starting transfers between devices, from_behind(): return lax.ppermute(array, axis, pairs)  32.8 us
    all_gather x2, blocking collectives, gather_all(): within = lax.all_gather(flat, 'space', axis=0, tiled=True)  25.5 us
    ppermute x17, starting transfers between devices, with_halo(): lax.ppermute(lax.slice_in_dim(block, 0, width, axis=dim), axis, backward)  22 us
    ppermute x17, waiting for transfers between devices, with_halo(): lax.ppermute(lax.slice_in_dim(block, block.shape[dim] - width, None, axis...  13.7 us
  transfers between devices with their start and end apart: 53, of which 37 were waited for; matrix products, arithmetic and copies ran while one was open for 1% of the time, Pallas kernels for 0%

profile of v6, /device:TPU:2, one launch (start us, length us, event | category | flops | bytes accessed | tf_op | source)
XLA Modules:
  0.0 405.0 jit_solution(14881403258911320681)
XLA Ops:
  9.8 2.1 collective-permute-start
  13.2 4.6 %collective-permute-start.2 = (f32[1,4,1,64,128]{4,3,2,1,0:T(8,128)S(1)}, f32[1,4,1,64,128]{4,3,2,1,0:T(8,128)S(1)}, u32[]{:S(2)}, u32[]{:S(2)}) collective-permute-start(f32[1,4,1,64,128]{4,3,2,1,0:T(8,128)S(1)} %get-tuple-element.60), channel_id=1, source_target_pairs={{0,1},{1,2},{2,3},{4,5},{5,6},{6,7},{8,9},{9,10},{10,11},{12,13},{... | collective-permute-start | bytes 393224 | tf_op jit(solution)/shard_map/ppermute | solution.py:23
  19.2 1.7 collective-permute-done.2
  23.1 1.9 collective-permute-start.3
  26.3 4.6 %collective-permute-start.5 = (f32[1,4,1,64,128]{4,3,2,1,0:T(8,128)S(1)}, f32[1,4,1,64,128]{4,3,2,1,0:T(8,128)S(1)}, u32[]{:S(2)}, u32[]{:S(2)}) collective-permute-start(f32[1,4,1,64,128]{4,3,2,1,0:T(8,128)S(1)} %get-tuple-element.56), channel_id=1, source_target_pairs={{0,1},{1,2},{2,3},{4,5},{5,6},{6,7},{8,9},{9,10},{10,11},{12,13},{... | collective-permute-start | bytes 393224 | tf_op jit(solution)/shard_map/ppermute | solution.py:23
  30.9 2.2 collective-permute-done.4
  38.0 4.5 %collective-permute-start.8 = (f32[1,4,1,32,64]{4,3,2,1,0:T(8,128)S(1)}, f32[1,4,1,32,64]{4,3,2,1,0:T(8,128)S(1)}, u32[]{:S(2)}, u32[]{:S(2)}) collective-permute-start(f32[1,4,1,32,64]{4,3,2,1,0:T(8,128)S(1)} %get-tuple-element.108), channel_id=1, source_target_pairs={{0,1},{1,2},{2,3},{4,5},{5,6},{6,7},{8,9},{9,10},{10,11},{12,13},{... | collective-permute-start | bytes 98312 | tf_op jit(solution)/shard_map/ppermute | solution.py:23
  42.6 1.9 collective-permute-start.6
  44.6 6.3 %collective-permute-done.6 = f32[1,4,2,32,64]{4,3,2,1,0:T(8,128)S(1)} collective-permute-done((f32[1,4,2,32,64]{4,3,2,1,0:T(8,128)S(1)}, f32[1,4,2,32,64]{4,3,2,1,0:T(8,128)S(1)}, u32[]{:S(2)}, u32[]{:S(2)}) %collective-permute-start.6) | collective-permute-done | bytes 65568 | tf_op jit(solution)/shard_map/ppermute | solution.py:34
  52.4 4.5 %collective-permute-start.11 = (f32[1,4,1,32,64]{4,3,2,1,0:T(8,128)S(1)}, f32[1,4,1,32,64]{4,3,2,1,0:T(8,128)S(1)}, u32[]{:S(2)}, u32[]{:S(2)}) collective-permute-start(f32[1,4,1,32,64]{4,3,2,1,0:T(8,128)S(1)} %get-tuple-element.104), channel_id=1, source_target_pairs={{0,1},{1,2},{2,3},{4,5},{5,6},{6,7},{8,9},{9,10},{10,11},{12,13},{... | collective-permute-start | bytes 98312 | tf_op jit(solution)/shard_map/ppermute | solution.py:23
  57.2 1.9 collective-permute-start.9
  59.3 6.3 %collective-permute-done.9 = f32[1,4,2,32,64]{4,3,2,1,0:T(8,128)S(1)} collective-permute-done((f32[1,4,2,32,64]{4,3,2,1,0:T(8,128)S(1)}, f32[1,4,2,32,64]{4,3,2,1,0:T(8,128)S(1)}, u32[]{:S(2)}, u32[]{:S(2)}) %collective-permute-start.9) | collective-permute-done | bytes 65568 | tf_op jit(solution)/shard_map/ppermute | solution.py:34
  66.3 13.1 %all-gather = f32[4,1,2560]{2,1,0:T(1,128)S(1)} all-gather(f32[1,1,2560]{2,1,0:T(1,128)S(1)} %maximum_bitcast_fusion), channel_id=1, replica_groups=mesh['tm'=32,'space'=4] {'space'}, dimensions={0}, use_global_device_ids=true | all-gather | bytes 51200 | tf_op jit(solution)/shard_map/all_gather | solution.py:191
  80.1 39.5 %all-gather.7.cloned.1.call-done = f32[32,4,2560]{2,1,0:T(4,128)} async-done(((f32[1,4,2560]{2,1,0:T(4,128)}), f32[32,4,2560]{2,1,0:T(4,128)}) %all-gather.7.cloned.1.call-update) | async-done | bytes 1310736 | tf_op jit(solution)/shard_map/all_gather | solution.py:192
  119.6 1.7 reshape.853
  122.4 2.5 reshape_transpose_reshape.10.src_ref
  126.6 16.5 %shard_map.37 = f32[32,16,512]{2,1,0:T(8,128)} custom-call(f32[32,16,512]{2,1,0:T(8,128)} %reshape_transpose_reshape.10.src_ref, f32[32,16,512]{2,1,0:T(8,128)} %reshape.838.met_ref), custom_call_target="tpu_custom_call" | custom-call | tf_op jit(solution)/shard_map/pallas_call | solution.py:161
  145.5 4.5 %collective-permute-start.14 = (f32[1,4,1,32,64]{4,3,2,1,0:T(8,128)S(1)}, f32[1,4,1,32,64]{4,3,2,1,0:T(8,128)S(1)}, u32[]{:S(2)}, u32[]{:S(2)}) collective-permute-start(f32[1,4,1,32,64]{4,3,2,1,0:T(8,128)S(1)} %get-tuple-element.100), channel_id=1, source_target_pairs={{0,1},{1,2},{2,3},{4,5},{5,6},{6,7},{8,9},{9,10},{10,11},{12,13},{... | collective-permute-start | bytes 98312 | tf_op jit(solution)/shard_map/ppermute | solution.py:23
  150.1 1.9 collective-permute-start.12
  152.1 6.3 %collective-permute-done.12 = f32[1,4,2,32,64]{4,3,2,1,0:T(8,128)S(1)} collective-permute-done((f32[1,4,2,32,64]{4,3,2,1,0:T(8,128)S(1)}, f32[1,4,2,32,64]{4,3,2,1,0:T(8,128)S(1)}, u32[]{:S(2)}, u32[]{:S(2)}) %collective-permute-start.12) | collective-permute-done | bytes 65568 | tf_op jit(solution)/shard_map/ppermute | solution.py:34
  159.9 4.5 %collective-permute-start.17 = (f32[1,4,1,32,64]{4,3,2,1,0:T(8,128)S(1)}, f32[1,4,1,32,64]{4,3,2,1,0:T(8,128)S(1)}, u32[]{:S(2)}, u32[]{:S(2)}) collective-permute-start(f32[1,4,1,32,64]{4,3,2,1,0:T(8,128)S(1)} %get-tuple-element.96), channel_id=1, source_target_pairs={{0,1},{1,2},{2,3},{4,5},{5,6},{6,7},{8,9},{9,10},{10,11},{12,13},{... | collective-permute-start | bytes 98312 | tf_op jit(solution)/shard_map/ppermute | solution.py:23
  164.5 1.9 collective-permute-start.15
  166.5 6.3 %collective-permute-done.15 = f32[1,4,2,32,64]{4,3,2,1,0:T(8,128)S(1)} collective-permute-done((f32[1,4,2,32,64]{4,3,2,1,0:T(8,128)S(1)}, f32[1,4,2,32,64]{4,3,2,1,0:T(8,128)S(1)}, u32[]{:S(2)}, u32[]{:S(2)}) %collective-permute-start.15) | collective-permute-done | bytes 65568 | tf_op jit(solution)/shard_map/ppermute | solution.py:34
  173.4 1.9 collective-permute-start.18
  176.7 4.6 %collective-permute-start.20 = (f32[1,4,1,64,128]{4,3,2,1,0:T(8,128)S(1)}, f32[1,4,1,64,128]{4,3,2,1,0:T(8,128)S(1)}, u32[]{:S(2)}, u32[]{:S(2)}) collective-permute-start(f32[1,4,1,64,128]{4,3,2,1,0:T(8,128)S(1)} %get-tuple-element.52), channel_id=1, source_target_pairs={{0,1},{1,2},{2,3},{4,5},{5,6},{6,7},{8,9},{9,10},{10,11},{12,13},{... | collective-permute-start | bytes 393224 | tf_op jit(solution)/shard_map/ppermute | solution.py:23
  184.0 2.1 collective-permute-done.18
  186.6 1.9 collective-permute-start.21
  189.9 4.6 %collective-permute-start.23 = (f32[1,4,1,64,128]{4,3,2,1,0:T(8,128)S(1)}, f32[1,4,1,64,128]{4,3,2,1,0:T(8,128)S(1)}, u32[]{:S(2)}, u32[]{:S(2)}) collective-permute-start(f32[1,4,1,64,128]{4,3,2,1,0:T(8,128)S(1)} %get-tuple-element.48), channel_id=1, source_target_pairs={{0,1},{1,2},{2,3},{4,5},{5,6},{6,7},{8,9},{9,10},{10,11},{12,13},{... | collective-permute-start | bytes 393224 | tf_op jit(solution)/shard_map/ppermute | solution.py:23
  197.1 2.1 collective-permute-done.21
  199.8 1.9 collective-permute-start.24
  203.0 4.6 %collective-permute-start.26 = (f32[1,4,1,64,128]{4,3,2,1,0:T(8,128)S(1)}, f32[1,4,1,64,128]{4,3,2,1,0:T(8,128)S(1)}, u32[]{:S(2)}, u32[]{:S(2)}) collective-permute-start(f32[1,4,1,64,128]{4,3,2,1,0:T(8,128)S(1)} %get-tuple-element.44), channel_id=1, source_target_pairs={{0,1},{1,2},{2,3},{4,5},{5,6},{6,7},{8,9},{9,10},{10,11},{12,13},{... | collective-permute-start | bytes 393224 | tf_op jit(solution)/shard_map/ppermute | solution.py:23
  208.6 1.5 collective-permute-done.26
  210.3 2.1 collective-permute-done.24
  212.9 1.9 collective-permute-start.27
  216.2 4.6 %collective-permute-start.29 = (f32[1,4,1,64,128]{4,3,2,1,0:T(8,128)S(1)}, f32[1,4,1,64,128]{4,3,2,1,0:T(8,128)S(1)}, u32[]{:S(2)}, u32[]{:S(2)}) collective-permute-start(f32[1,4,1,64,128]{4,3,2,1,0:T(8,128)S(1)} %get-tuple-element.40), channel_id=1, source_target_pairs={{0,1},{1,2},{2,3},{4,5},{5,6},{6,7},{8,9},{9,10},{10,11},{12,13},{... | collective-permute-start | bytes 393224 | tf_op jit(solution)/shard_map/ppermute | solution.py:23
  223.4 2.1 collective-permute-done.27
  226.1 1.9 collective-permute-start.30
  229.3 4.7 %collective-permute-start.32 = (f32[1,4,1,64,128]{4,3,2,1,0:T(8,128)S(1)}, f32[1,4,1,64,128]{4,3,2,1,0:T(8,128)S(1)}, u32[]{:S(2)}, u32[]{:S(2)}) collective-permute-start(f32[1,4,1,64,128]{4,3,2,1,0:T(8,128)S(1)} %get-tuple-element.36), channel_id=1, source_target_pairs={{0,1},{1,2},{2,3},{4,5},{5,6},{6,7},{8,9},{9,10},{10,11},{12,13},{... | collective-permute-start | bytes 393224 | tf_op jit(solution)/shard_map/ppermute | solution.py:23
  234.9 1.5 collective-permute-done.32
  236.6 2.1 collective-permute-done.30
  241.0 4.5 %collective-permute-start.35 = (f32[1,4,1,32,64]{4,3,2,1,0:T(8,128)S(1)}, f32[1,4,1,32,64]{4,3,2,1,0:T(8,128)S(1)}, u32[]{:S(2)}, u32[]{:S(2)}) collective-permute-start(f32[1,4,1,32,64]{4,3,2,1,0:T(8,128)S(1)} %get-tuple-element.92), channel_id=1, source_target_pairs={{0,1},{1,2},{2,3},{4,5},{5,6},{6,7},{8,9},{9,10},{10,11},{12,13},{... | collective-permute-start | bytes 98312 | tf_op jit(solution)/shard_map/ppermute | solution.py:23
  245.6 1.9 collective-permute-start.33
  247.6 6.3 %collective-permute-done.33 = f32[1,4,2,32,64]{4,3,2,1,0:T(8,128)S(1)} collective-permute-done((f32[1,4,2,32,64]{4,3,2,1,0:T(8,128)S(1)}, f32[1,4,2,32,64]{4,3,2,1,0:T(8,128)S(1)}, u32[]{:S(2)}, u32[]{:S(2)}) %collective-permute-start.33) | collective-permute-done | bytes 65568 | tf_op jit(solution)/shard_map/ppermute | solution.py:34
  255.4 4.5 %collective-permute-start.38 = (f32[1,4,1,32,64]{4,3,2,1,0:T(8,128)S(1)}, f32[1,4,1,32,64]{4,3,2,1,0:T(8,128)S(1)}, u32[]{:S(2)}, u32[]{:S(2)}) collective-permute-start(f32[1,4,1,32,64]{4,3,2,1,0:T(8,128)S(1)} %get-tuple-element.88), channel_id=1, source_target_pairs={{0,1},{1,2},{2,3},{4,5},{5,6},{6,7},{8,9},{9,10},{10,11},{12,13},{... | collective-permute-start | bytes 98312 | tf_op jit(solution)/shard_map/ppermute | solution.py:23
  260.0 1.9 collective-permute-start.36
  262.0 6.3 %collective-permute-done.36 = f32[1,4,2,32,64]{4,3,2,1,0:T(8,128)S(1)} collective-permute-done((f32[1,4,2,32,64]{4,3,2,1,0:T(8,128)S(1)}, f32[1,4,2,32,64]{4,3,2,1,0:T(8,128)S(1)}, u32[]{:S(2)}, u32[]{:S(2)}) %collective-permute-start.36) | collective-permute-done | bytes 65568 | tf_op jit(solution)/shard_map/ppermute | solution.py:34
  269.0 12.4 %all-gather.2 = f32[4,1,2048]{2,1,0:T(1,128)S(1)} all-gather(f32[1,1,2048]{2,1,0:T(1,128)S(1)} %reshape.854), channel_id=1, replica_groups=mesh['tm'=32,'space'=4] {'space'}, dimensions={0}, use_global_device_ids=true | all-gather | bytes 40960 | tf_op jit(solution)/shard_map/all_gather | solution.py:191
  282.1 39.4 %all-gather.9.cloned.1.call-done = f32[32,4,2048]{2,1,0:T(4,128)} async-done(((f32[1,4,2048]{2,1,0:T(4,128)}), f32[32,4,2048]{2,1,0:T(4,128)}) %all-gather.9.cloned.1.call-update) | async-done | bytes 1048592 | tf_op jit(solution)/shard_map/all_gather | solution.py:192
  321.4 2.7 reshape_transpose_reshape.12.src_ref
  324.2 16.5 %shard_map.38 = f32[32,16,512]{2,1,0:T(8,128)} custom-call(f32[32,16,512]{2,1,0:T(8,128)} %reshape_transpose_reshape.12.src_ref, f32[32,16,512]{2,1,0:T(8,128)} %reshape.838.met_ref), custom_call_target="tpu_custom_call" | custom-call | tf_op jit(solution)/shard_map/pallas_call | solution.py:161
  343.1 4.5 %collective-permute-start.41 = (f32[1,4,1,32,64]{4,3,2,1,0:T(8,128)S(1)}, f32[1,4,1,32,64]{4,3,2,1,0:T(8,128)S(1)}, u32[]{:S(2)}, u32[]{:S(2)}) collective-permute-start(f32[1,4,1,32,64]{4,3,2,1,0:T(8,128)S(1)} %get-tuple-element.84), channel_id=1, source_target_pairs={{0,1},{1,2},{2,3},{4,5},{5,6},{6,7},{8,9},{9,10},{10,11},{12,13},{... | collective-permute-start | bytes 98312 | tf_op jit(solution)/shard_map/ppermute | solution.py:23
  347.6 1.9 collective-permute-start.39
  349.7 6.3 %collective-permute-done.39 = f32[1,4,2,32,64]{4,3,2,1,0:T(8,128)S(1)} collective-permute-done((f32[1,4,2,32,64]{4,3,2,1,0:T(8,128)S(1)}, f32[1,4,2,32,64]{4,3,2,1,0:T(8,128)S(1)}, u32[]{:S(2)}, u32[]{:S(2)}) %collective-permute-start.39) | collective-permute-done | bytes 65568 | tf_op jit(solution)/shard_map/ppermute | solution.py:34
  357.5 4.5 %collective-permute-start.44 = (f32[1,4,1,32,64]{4,3,2,1,0:T(8,128)S(1)}, f32[1,4,1,32,64]{4,3,2,1,0:T(8,128)S(1)}, u32[]{:S(2)}, u32[]{:S(2)}) collective-permute-start(f32[1,4,1,32,64]{4,3,2,1,0:T(8,128)S(1)} %get-tuple-element.80), channel_id=1, source_target_pairs={{0,1},{1,2},{2,3},{4,5},{5,6},{6,7},{8,9},{9,10},{10,11},{12,13},{... | collective-permute-start | bytes 98312 | tf_op jit(solution)/shard_map/ppermute | solution.py:23
  362.0 1.9 collective-permute-start.42
  364.1 6.3 %collective-permute-done.42 = f32[1,4,2,32,64]{4,3,2,1,0:T(8,128)S(1)} collective-permute-done((f32[1,4,2,32,64]{4,3,2,1,0:T(8,128)S(1)}, f32[1,4,2,32,64]{4,3,2,1,0:T(8,128)S(1)}, u32[]{:S(2)}, u32[]{:S(2)}) %collective-permute-start.42) | collective-permute-done | bytes 65568 | tf_op jit(solution)/shard_map/ppermute | solution.py:34
  371.0 1.9 collective-permute-start.45
  374.3 4.6 %collective-permute-start.47 = (f32[1,4,1,64,128]{4,3,2,1,0:T(8,128)S(1)}, f32[1,4,1,64,128]{4,3,2,1,0:T(8,128)S(1)}, u32[]{:S(2)}, u32[]{:S(2)}) collective-permute-start(f32[1,4,1,64,128]{4,3,2,1,0:T(8,128)S(1)} %get-tuple-element.32), channel_id=1, source_target_pairs={{0,1},{1,2},{2,3},{4,5},{5,6},{6,7},{8,9},{9,10},{10,11},{12,13},{... | collective-permute-start | bytes 393224 | tf_op jit(solution)/shard_map/ppermute | solution.py:23
  379.8 1.5 collective-permute-done.47
  381.5 2.1 collective-permute-done.45
  384.2 1.9 collective-permute-start.48
  387.4 4.6 %collective-permute-start.50 = (f32[1,4,1,64,128]{4,3,2,1,0:T(8,128)S(1)}, f32[1,4,1,64,128]{4,3,2,1,0:T(8,128)S(1)}, u32[]{:S(2)}, u32[]{:S(2)}) collective-permute-start(f32[1,4,1,64,128]{4,3,2,1,0:T(8,128)S(1)} %get-tuple-element.28), channel_id=1, source_target_pairs={{0,1},{1,2},{2,3},{4,5},{5,6},{6,7},{8,9},{9,10},{10,11},{12,13},{... | collective-permute-start | bytes 393224 | tf_op jit(solution)/shard_map/ppermute | solution.py:23
  393.0 1.5 collective-permute-done.50
  394.7 2.1 collective-permute-done.48
  (168 shorter events, 60.3 us)
Async XLA Ops:
  6.5 113.0 %all-gather.7.cloned.1.call-start = ((), (), s32[]{:S(2)}) async-start(), calls=%async_computation | async-start | bytes 1351680 | tf_op jit(solution)/shard_map/all_gather | solution.py:192
  7.5 10.2 %copy-start.1 = (f32[1,4,64,128]{3,2,1,0:T(8,128)S(1)}, f32[1,4,64,128]{3,2,1,0:T(8,128)}, u32[]{:S(2)}) copy-start(f32[1,4,64,128]{3,2,1,0:T(8,128)} %param.4) | copy-start | bytes 393220
  9.8 12.8 %copy-start = (f32[1,4,4,64,128]{4,3,2,1,0:T(8,128)S(1)}, f32[1,4,4,64,128]{4,3,2,1,0:T(8,128)}, u32[]{:S(2)}) copy-start(f32[1,4,4,64,128]{4,3,2,1,0:T(8,128)} %param.3) | copy-start | bytes 1572868
  9.8 12.7 %collective-permute-start = (f32[1,4,4,64,128]{4,3,2,1,0:T(8,128)S(1)}, f32[1,4,4,64,128]{4,3,2,1,0:T(8,128)S(1)}, u32[]{:S(2)}, u32[]{:S(2)}) collective-permute-start(f32[1,4,4,64,128]{4,3,2,1,0:T(8,128)S(1)} %get-tuple-element.5), channel_id=1, source_target_pairs={{0,4},{4,8},{8,12},{12,16},{16,20},{20,24},{24,28},{28,32},{32,36}... | collective-permute-start | bytes 1572872 | tf_op jit(solution)/shard_map/ppermute | solution.py:34
  11.9 7.4 %collective-permute-start.1 = (f32[1,4,1,64,128]{4,3,2,1,0:T(8,128)S(1)}, f32[1,4,1,64,128]{4,3,2,1,0:T(8,128)S(1)}, u32[]{:S(2)}, u32[]{:S(2)}) collective-permute-start(f32[1,4,1,64,128]{4,3,2,1,0:T(8,128)S(1)} %get-tuple-element.59), channel_id=1, source_target_pairs={{1,0},{2,1},{3,2},{5,4},{6,5},{7,6},{9,8},{10,9},{11,10},{13,12},{... | collective-permute-start | bytes 393224 | tf_op jit(solution)/shard_map/ppermute | solution.py:26
  13.2 7.8 %collective-permute-start.2 = (f32[1,4,1,64,128]{4,3,2,1,0:T(8,128)S(1)}, f32[1,4,1,64,128]{4,3,2,1,0:T(8,128)S(1)}, u32[]{:S(2)}, u32[]{:S(2)}) collective-permute-start(f32[1,4,1,64,128]{4,3,2,1,0:T(8,128)S(1)} %get-tuple-element.60), channel_id=1, source_target_pairs={{0,1},{1,2},{2,3},{4,5},{5,6},{6,7},{8,9},{9,10},{10,11},{12,13},{... | collective-permute-start | bytes 393224 | tf_op jit(solution)/shard_map/ppermute | solution.py:23
  23.1 12.6 %collective-permute-start.3 = (f32[1,4,4,64,128]{4,3,2,1,0:T(8,128)S(1)}, f32[1,4,4,64,128]{4,3,2,1,0:T(8,128)S(1)}, u32[]{:S(2)}, u32[]{:S(2)}) collective-permute-start(f32[1,4,4,64,128]{4,3,2,1,0:T(8,128)S(1)} %fusion.119), channel_id=1, source_target_pairs={{0,4},{4,8},{8,12},{12,16},{16,20},{20,24},{24,28},{28,32},{32,36}... | collective-permute-start | bytes 1572872 | tf_op jit(solution)/shard_map/ppermute | solution.py:34
  25.0 8.1 %collective-permute-start.4 = (f32[1,4,1,64,128]{4,3,2,1,0:T(8,128)S(1)}, f32[1,4,1,64,128]{4,3,2,1,0:T(8,128)S(1)}, u32[]{:S(2)}, u32[]{:S(2)}) collective-permute-start(f32[1,4,1,64,128]{4,3,2,1,0:T(8,128)S(1)} %get-tuple-element.55), channel_id=1, source_target_pairs={{1,0},{2,1},{3,2},{5,4},{6,5},{7,6},{9,8},{10,9},{11,10},{13,12},{... | collective-permute-start | bytes 393224 | tf_op jit(solution)/shard_map/ppermute | solution.py:26
  26.3 8.3 %collective-permute-start.5 = (f32[1,4,1,64,128]{4,3,2,1,0:T(8,128)S(1)}, f32[1,4,1,64,128]{4,3,2,1,0:T(8,128)S(1)}, u32[]{:S(2)}, u32[]{:S(2)}) collective-permute-start(f32[1,4,1,64,128]{4,3,2,1,0:T(8,128)S(1)} %get-tuple-element.56), channel_id=1, source_target_pairs={{0,1},{1,2},{2,3},{4,5},{5,6},{6,7},{8,9},{9,10},{10,11},{12,13},{... | collective-permute-start | bytes 393224 | tf_op jit(solution)/shard_map/ppermute | solution.py:23
  36.7 7.8 %collective-permute-start.7 = (f32[1,4,1,32,64]{4,3,2,1,0:T(8,128)S(1)}, f32[1,4,1,32,64]{4,3,2,1,0:T(8,128)S(1)}, u32[]{:S(2)}, u32[]{:S(2)}) collective-permute-start(f32[1,4,1,32,64]{4,3,2,1,0:T(8,128)S(1)} %get-tuple-element.107), channel_id=1, source_target_pairs={{1,0},{2,1},{3,2},{5,4},{6,5},{7,6},{9,8},{10,9},{11,10},{13,12},{... | collective-permute-start | bytes 98312 | tf_op jit(solution)/shard_map/ppermute | solution.py:26
  38.0 6.5 %collective-permute-start.8 = (f32[1,4,1,32,64]{4,3,2,1,0:T(8,128)S(1)}, f32[1,4,1,32,64]{4,3,2,1,0:T(8,128)S(1)}, u32[]{:S(2)}, u32[]{:S(2)}) collective-permute-start(f32[1,4,1,32,64]{4,3,2,1,0:T(8,128)S(1)} %get-tuple-element.108), channel_id=1, source_target_pairs={{0,1},{1,2},{2,3},{4,5},{5,6},{6,7},{8,9},{9,10},{10,11},{12,13},{... | collective-permute-start | bytes 98312 | tf_op jit(solution)/shard_map/ppermute | solution.py:23
  42.6 8.4 %collective-permute-start.6 = (f32[1,4,2,32,64]{4,3,2,1,0:T(8,128)S(1)}, f32[1,4,2,32,64]{4,3,2,1,0:T(8,128)S(1)}, u32[]{:S(2)}, u32[]{:S(2)}) collective-permute-start(f32[1,4,2,32,64]{4,3,2,1,0:T(8,128)S(1)} %fusion.388), channel_id=1, source_target_pairs={{0,4},{4,8},{8,12},{12,16},{16,20},{20,24},{24,28},{28,32},{32,36}... | collective-permute-start | bytes 196616 | tf_op jit(solution)/shard_map/ppermute | solution.py:34
  51.1 8.0 %collective-permute-start.10 = (f32[1,4,1,32,64]{4,3,2,1,0:T(8,128)S(1)}, f32[1,4,1,32,64]{4,3,2,1,0:T(8,128)S(1)}, u32[]{:S(2)}, u32[]{:S(2)}) collective-permute-start(f32[1,4,1,32,64]{4,3,2,1,0:T(8,128)S(1)} %get-tuple-element.103), channel_id=1, source_target_pairs={{1,0},{2,1},{3,2},{5,4},{6,5},{7,6},{9,8},{10,9},{11,10},{13,12},{... | collective-permute-start | bytes 98312 | tf_op jit(solution)/shard_map/ppermute | solution.py:26
  52.4 6.7 %collective-permute-start.11 = (f32[1,4,1,32,64]{4,3,2,1,0:T(8,128)S(1)}, f32[1,4,1,32,64]{4,3,2,1,0:T(8,128)S(1)}, u32[]{:S(2)}, u32[]{:S(2)}) collective-permute-start(f32[1,4,1,32,64]{4,3,2,1,0:T(8,128)S(1)} %get-tuple-element.104), channel_id=1, source_target_pairs={{0,1},{1,2},{2,3},{4,5},{5,6},{6,7},{8,9},{9,10},{10,11},{12,13},{... | collective-permute-start | bytes 98312 | tf_op jit(solution)/shard_map/ppermute | solution.py:23
  57.2 8.4 %collective-permute-start.9 = (f32[1,4,2,32,64]{4,3,2,1,0:T(8,128)S(1)}, f32[1,4,2,32,64]{4,3,2,1,0:T(8,128)S(1)}, u32[]{:S(2)}, u32[]{:S(2)}) collective-permute-start(f32[1,4,2,32,64]{4,3,2,1,0:T(8,128)S(1)} %fusion.233), channel_id=1, source_target_pairs={{0,4},{4,8},{8,12},{12,16},{16,20},{20,24},{24,28},{28,32},{32,36}... | collective-permute-start | bytes 196616 | tf_op jit(solution)/shard_map/ppermute | solution.py:34
  80.0 241.4 %all-gather.9.cloned.1.call-start = ((), (), s32[]{:S(2)}) async-start(), calls=%async_computation.1 | async-start | bytes 1081344 | tf_op jit(solution)/shard_map/all_gather | solution.py:192
  144.2 7.8 %collective-permute-start.13 = (f32[1,4,1,32,64]{4,3,2,1,0:T(8,128)S(1)}, f32[1,4,1,32,64]{4,3,2,1,0:T(8,128)S(1)}, u32[]{:S(2)}, u32[]{:S(2)}) collective-permute-start(f32[1,4,1,32,64]{4,3,2,1,0:T(8,128)S(1)} %get-tuple-element.99), channel_id=1, source_target_pairs={{1,0},{2,1},{3,2},{5,4},{6,5},{7,6},{9,8},{10,9},{11,10},{13,12},{... | collective-permute-start | bytes 98312 | tf_op jit(solution)/shard_map/ppermute | solution.py:26
  145.5 6.5 %collective-permute-start.14 = (f32[1,4,1,32,64]{4,3,2,1,0:T(8,128)S(1)}, f32[1,4,1,32,64]{4,3,2,1,0:T(8,128)S(1)}, u32[]{:S(2)}, u32[]{:S(2)}) collective-permute-start(f32[1,4,1,32,64]{4,3,2,1,0:T(8,128)S(1)} %get-tuple-element.100), channel_id=1, source_target_pairs={{0,1},{1,2},{2,3},{4,5},{5,6},{6,7},{8,9},{9,10},{10,11},{12,13},{... | collective-permute-start | bytes 98312 | tf_op jit(solution)/shard_map/ppermute | solution.py:23
  150.1 8.4 %collective-permute-start.12 = (f32[1,4,2,32,64]{4,3,2,1,0:T(8,128)S(1)}, f32[1,4,2,32,64]{4,3,2,1,0:T(8,128)S(1)}, u32[]{:S(2)}, u32[]{:S(2)}) collective-permute-start(f32[1,4,2,32,64]{4,3,2,1,0:T(8,128)S(1)} %broadcast_add_fusion.1), channel_id=1, source_target_pairs={{0,4},{4,8},{8,12},{12,16},{16,20},{20,24},{24,28},{28,32},{32,36}... | collective-permute-start | bytes 196616 | tf_op jit(solution)/shard_map/ppermute | solution.py:34
  158.6 7.8 %collective-permute-start.16 = (f32[1,4,1,32,64]{4,3,2,1,0:T(8,128)S(1)}, f32[1,4,1,32,64]{4,3,2,1,0:T(8,128)S(1)}, u32[]{:S(2)}, u32[]{:S(2)}) collective-permute-start(f32[1,4,1,32,64]{4,3,2,1,0:T(8,128)S(1)} %get-tuple-element.95), channel_id=1, source_target_pairs={{1,0},{2,1},{3,2},{5,4},{6,5},{7,6},{9,8},{10,9},{11,10},{13,12},{... | collective-permute-start | bytes 98312 | tf_op jit(solution)/shard_map/ppermute | solution.py:26
  159.9 6.5 %collective-permute-start.17 = (f32[1,4,1,32,64]{4,3,2,1,0:T(8,128)S(1)}, f32[1,4,1,32,64]{4,3,2,1,0:T(8,128)S(1)}, u32[]{:S(2)}, u32[]{:S(2)}) collective-permute-start(f32[1,4,1,32,64]{4,3,2,1,0:T(8,128)S(1)} %get-tuple-element.96), channel_id=1, source_target_pairs={{0,1},{1,2},{2,3},{4,5},{5,6},{6,7},{8,9},{9,10},{10,11},{12,13},{... | collective-permute-start | bytes 98312 | tf_op jit(solution)/shard_map/ppermute | solution.py:23
  164.5 8.4 %collective-permute-start.15 = (f32[1,4,2,32,64]{4,3,2,1,0:T(8,128)S(1)}, f32[1,4,2,32,64]{4,3,2,1,0:T(8,128)S(1)}, u32[]{:S(2)}, u32[]{:S(2)}) collective-permute-start(f32[1,4,2,32,64]{4,3,2,1,0:T(8,128)S(1)} %fusion.206), channel_id=1, source_target_pairs={{0,4},{4,8},{8,12},{12,16},{16,20},{20,24},{24,28},{28,32},{32,36}... | collective-permute-start | bytes 196616 | tf_op jit(solution)/shard_map/ppermute | solution.py:34
  173.4 12.6 %collective-permute-start.18 = (f32[1,4,4,64,128]{4,3,2,1,0:T(8,128)S(1)}, f32[1,4,4,64,128]{4,3,2,1,0:T(8,128)S(1)}, u32[]{:S(2)}, u32[]{:S(2)}) collective-permute-start(f32[1,4,4,64,128]{4,3,2,1,0:T(8,128)S(1)} %add.496), channel_id=1, source_target_pairs={{0,4},{4,8},{8,12},{12,16},{16,20},{20,24},{24,28},{28,32},{32,36}... | collective-permute-start | bytes 1572872 | tf_op jit(solution)/shard_map/ppermute | solution.py:34
  175.4 6.9 %collective-permute-start.19 = (f32[1,4,1,64,128]{4,3,2,1,0:T(8,128)S(1)}, f32[1,4,1,64,128]{4,3,2,1,0:T(8,128)S(1)}, u32[]{:S(2)}, u32[]{:S(2)}) collective-permute-start(f32[1,4,1,64,128]{4,3,2,1,0:T(8,128)S(1)} %get-tuple-element.51), channel_id=1, source_target_pairs={{1,0},{2,1},{3,2},{5,4},{6,5},{7,6},{9,8},{10,9},{11,10},{13,12},{... | collective-permute-start | bytes 393224 | tf_op jit(solution)/shard_map/ppermute | solution.py:26
  176.7 7.1 %collective-permute-start.20 = (f32[1,4,1,64,128]{4,3,2,1,0:T(8,128)S(1)}, f32[1,4,1,64,128]{4,3,2,1,0:T(8,128)S(1)}, u32[]{:S(2)}, u32[]{:S(2)}) collective-permute-start(f32[1,4,1,64,128]{4,3,2,1,0:T(8,128)S(1)} %get-tuple-element.52), channel_id=1, source_target_pairs={{0,1},{1,2},{2,3},{4,5},{5,6},{6,7},{8,9},{9,10},{10,11},{12,13},{... | collective-permute-start | bytes 393224 | tf_op jit(solution)/shard_map/ppermute | solution.py:23
  186.6 12.6 %collective-permute-start.21 = (f32[1,4,4,64,128]{4,3,2,1,0:T(8,128)S(1)}, f32[1,4,4,64,128]{4,3,2,1,0:T(8,128)S(1)}, u32[]{:S(2)}, u32[]{:S(2)}) collective-permute-start(f32[1,4,4,64,128]{4,3,2,1,0:T(8,128)S(1)} %fusion.93), channel_id=1, source_target_pairs={{0,4},{4,8},{8,12},{12,16},{16,20},{20,24},{24,28},{28,32},{32,36}... | collective-permute-start | bytes 1572872 | tf_op jit(solution)/shard_map/ppermute | solution.py:34
  188.6 6.9 %collective-permute-start.22 = (f32[1,4,1,64,128]{4,3,2,1,0:T(8,128)S(1)}, f32[1,4,1,64,128]{4,3,2,1,0:T(8,128)S(1)}, u32[]{:S(2)}, u32[]{:S(2)}) collective-permute-start(f32[1,4,1,64,128]{4,3,2,1,0:T(8,128)S(1)} %get-tuple-element.47), channel_id=1, source_target_pairs={{1,0},{2,1},{3,2},{5,4},{6,5},{7,6},{9,8},{10,9},{11,10},{13,12},{... | collective-permute-start | bytes 393224 | tf_op jit(solution)/shard_map/ppermute | solution.py:26
  189.9 7.1 %collective-permute-start.23 = (f32[1,4,1,64,128]{4,3,2,1,0:T(8,128)S(1)}, f32[1,4,1,64,128]{4,3,2,1,0:T(8,128)S(1)}, u32[]{:S(2)}, u32[]{:S(2)}) collective-permute-start(f32[1,4,1,64,128]{4,3,2,1,0:T(8,128)S(1)} %get-tuple-element.48), channel_id=1, source_target_pairs={{0,1},{1,2},{2,3},{4,5},{5,6},{6,7},{8,9},{9,10},{10,11},{12,13},{... | collective-permute-start | bytes 393224 | tf_op jit(solution)/shard_map/ppermute | solution.py:23
  199.8 12.6 %collective-permute-start.24 = (f32[1,4,4,64,128]{4,3,2,1,0:T(8,128)S(1)}, f32[1,4,4,64,128]{4,3,2,1,0:T(8,128)S(1)}, u32[]{:S(2)}, u32[]{:S(2)}) collective-permute-start(f32[1,4,4,64,128]{4,3,2,1,0:T(8,128)S(1)} %fusion.79), channel_id=1, source_target_pairs={{0,4},{4,8},{8,12},{12,16},{16,20},{20,24},{24,28},{28,32},{32,36}... | collective-permute-start | bytes 1572872 | tf_op jit(solution)/shard_map/ppermute | solution.py:34
  201.7 6.9 %collective-permute-start.25 = (f32[1,4,1,64,128]{4,3,2,1,0:T(8,128)S(1)}, f32[1,4,1,64,128]{4,3,2,1,0:T(8,128)S(1)}, u32[]{:S(2)}, u32[]{:S(2)}) collective-permute-start(f32[1,4,1,64,128]{4,3,2,1,0:T(8,128)S(1)} %get-tuple-element.43), channel_id=1, source_target_pairs={{1,0},{2,1},{3,2},{5,4},{6,5},{7,6},{9,8},{10,9},{11,10},{13,12},{... | collective-permute-start | bytes 393224 | tf_op jit(solution)/shard_map/ppermute | solution.py:26
  203.0 7.1 %collective-permute-start.26 = (f32[1,4,1,64,128]{4,3,2,1,0:T(8,128)S(1)}, f32[1,4,1,64,128]{4,3,2,1,0:T(8,128)S(1)}, u32[]{:S(2)}, u32[]{:S(2)}) collective-permute-start(f32[1,4,1,64,128]{4,3,2,1,0:T(8,128)S(1)} %get-tuple-element.44), channel_id=1, source_target_pairs={{0,1},{1,2},{2,3},{4,5},{5,6},{6,7},{8,9},{9,10},{10,11},{12,13},{... | collective-permute-start | bytes 393224 | tf_op jit(solution)/shard_map/ppermute | solution.py:23
  212.9 12.6 %collective-permute-start.27 = (f32[1,4,4,64,128]{4,3,2,1,0:T(8,128)S(1)}, f32[1,4,4,64,128]{4,3,2,1,0:T(8,128)S(1)}, u32[]{:S(2)}, u32[]{:S(2)}) collective-permute-start(f32[1,4,4,64,128]{4,3,2,1,0:T(8,128)S(1)} %fusion.65), channel_id=1, source_target_pairs={{0,4},{4,8},{8,12},{12,16},{16,20},{20,24},{24,28},{28,32},{32,36}... | collective-permute-start | bytes 1572872 | tf_op jit(solution)/shard_map/ppermute | solution.py:34
  214.9 6.9 %collective-permute-start.28 = (f32[1,4,1,64,128]{4,3,2,1,0:T(8,128)S(1)}, f32[1,4,1,64,128]{4,3,2,1,0:T(8,128)S(1)}, u32[]{:S(2)}, u32[]{:S(2)}) collective-permute-start(f32[1,4,1,64,128]{4,3,2,1,0:T(8,128)S(1)} %get-tuple-element.39), channel_id=1, source_target_pairs={{1,0},{2,1},{3,2},{5,4},{6,5},{7,6},{9,8},{10,9},{11,10},{13,12},{... | collective-permute-start | bytes 393224 | tf_op jit(solution)/shard_map/ppermute | solution.py:26
  216.2 7.1 %collective-permute-start.29 = (f32[1,4,1,64,128]{4,3,2,1,0:T(8,128)S(1)}, f32[1,4,1,64,128]{4,3,2,1,0:T(8,128)S(1)}, u32[]{:S(2)}, u32[]{:S(2)}) collective-permute-start(f32[1,4,1,64,128]{4,3,2,1,0:T(8,128)S(1)} %get-tuple-element.40), channel_id=1, source_target_pairs={{0,1},{1,2},{2,3},{4,5},{5,6},{6,7},{8,9},{9,10},{10,11},{12,13},{... | collective-permute-start | bytes 393224 | tf_op jit(solution)/shard_map/ppermute | solution.py:23
  226.1 12.6 %collective-permute-start.30 = (f32[1,4,4,64,128]{4,3,2,1,0:T(8,128)S(1)}, f32[1,4,4,64,128]{4,3,2,1,0:T(8,128)S(1)}, u32[]{:S(2)}, u32[]{:S(2)}) collective-permute-start(f32[1,4,4,64,128]{4,3,2,1,0:T(8,128)S(1)} %fusion.51), channel_id=1, source_target_pairs={{0,4},{4,8},{8,12},{12,16},{16,20},{20,24},{24,28},{28,32},{32,36}... | collective-permute-start | bytes 1572872 | tf_op jit(solution)/shard_map/ppermute | solution.py:34
  228.0 6.9 %collective-permute-start.31 = (f32[1,4,1,64,128]{4,3,2,1,0:T(8,128)S(1)}, f32[1,4,1,64,128]{4,3,2,1,0:T(8,128)S(1)}, u32[]{:S(2)}, u32[]{:S(2)}) collective-permute-start(f32[1,4,1,64,128]{4,3,2,1,0:T(8,128)S(1)} %get-tuple-element.35), channel_id=1, source_target_pairs={{1,0},{2,1},{3,2},{5,4},{6,5},{7,6},{9,8},{10,9},{11,10},{13,12},{... | collective-permute-start | bytes 393224 | tf_op jit(solution)/shard_map/ppermute | solution.py:26
  229.3 7.1 %collective-permute-start.32 = (f32[1,4,1,64,128]{4,3,2,1,0:T(8,128)S(1)}, f32[1,4,1,64,128]{4,3,2,1,0:T(8,128)S(1)}, u32[]{:S(2)}, u32[]{:S(2)}) collective-permute-start(f32[1,4,1,64,128]{4,3,2,1,0:T(8,128)S(1)} %get-tuple-element.36), channel_id=1, source_target_pairs={{0,1},{1,2},{2,3},{4,5},{5,6},{6,7},{8,9},{9,10},{10,11},{12,13},{... | collective-permute-start | bytes 393224 | tf_op jit(solution)/shard_map/ppermute | solution.py:23
  239.7 7.8 %collective-permute-start.34 = (f32[1,4,1,32,64]{4,3,2,1,0:T(8,128)S(1)}, f32[1,4,1,32,64]{4,3,2,1,0:T(8,128)S(1)}, u32[]{:S(2)}, u32[]{:S(2)}) collective-permute-start(f32[1,4,1,32,64]{4,3,2,1,0:T(8,128)S(1)} %get-tuple-element.91), channel_id=1, source_target_pairs={{1,0},{2,1},{3,2},{5,4},{6,5},{7,6},{9,8},{10,9},{11,10},{13,12},{... | collective-permute-start | bytes 98312 | tf_op jit(solution)/shard_map/ppermute | solution.py:26
  241.0 6.5 %collective-permute-start.35 = (f32[1,4,1,32,64]{4,3,2,1,0:T(8,128)S(1)}, f32[1,4,1,32,64]{4,3,2,1,0:T(8,128)S(1)}, u32[]{:S(2)}, u32[]{:S(2)}) collective-permute-start(f32[1,4,1,32,64]{4,3,2,1,0:T(8,128)S(1)} %get-tuple-element.92), channel_id=1, source_target_pairs={{0,1},{1,2},{2,3},{4,5},{5,6},{6,7},{8,9},{9,10},{10,11},{12,13},{... | collective-permute-start | bytes 98312 | tf_op jit(solution)/shard_map/ppermute | solution.py:23
  245.6 8.4 %collective-permute-start.33 = (f32[1,4,2,32,64]{4,3,2,1,0:T(8,128)S(1)}, f32[1,4,2,32,64]{4,3,2,1,0:T(8,128)S(1)}, u32[]{:S(2)}, u32[]{:S(2)}) collective-permute-start(f32[1,4,2,32,64]{4,3,2,1,0:T(8,128)S(1)} %fusion.389), channel_id=1, source_target_pairs={{0,4},{4,8},{8,12},{12,16},{16,20},{20,24},{24,28},{28,32},{32,36}... | collective-permute-start | bytes 196616 | tf_op jit(solution)/shard_map/ppermute | solution.py:34
  254.1 7.8 %collective-permute-start.37 = (f32[1,4,1,32,64]{4,3,2,1,0:T(8,128)S(1)}, f32[1,4,1,32,64]{4,3,2,1,0:T(8,128)S(1)}, u32[]{:S(2)}, u32[]{:S(2)}) collective-permute-start(f32[1,4,1,32,64]{4,3,2,1,0:T(8,128)S(1)} %get-tuple-element.87), channel_id=1, source_target_pairs={{1,0},{2,1},{3,2},{5,4},{6,5},{7,6},{9,8},{10,9},{11,10},{13,12},{... | collective-permute-start | bytes 98312 | tf_op jit(solution)/shard_map/ppermute | solution.py:26
  255.4 6.5 %collective-permute-start.38 = (f32[1,4,1,32,64]{4,3,2,1,0:T(8,128)S(1)}, f32[1,4,1,32,64]{4,3,2,1,0:T(8,128)S(1)}, u32[]{:S(2)}, u32[]{:S(2)}) collective-permute-start(f32[1,4,1,32,64]{4,3,2,1,0:T(8,128)S(1)} %get-tuple-element.88), channel_id=1, source_target_pairs={{0,1},{1,2},{2,3},{4,5},{5,6},{6,7},{8,9},{9,10},{10,11},{12,13},{... | collective-permute-start | bytes 98312 | tf_op jit(solution)/shard_map/ppermute | solution.py:23
  260.0 8.4 %collective-permute-start.36 = (f32[1,4,2,32,64]{4,3,2,1,0:T(8,128)S(1)}, f32[1,4,2,32,64]{4,3,2,1,0:T(8,128)S(1)}, u32[]{:S(2)}, u32[]{:S(2)}) collective-permute-start(f32[1,4,2,32,64]{4,3,2,1,0:T(8,128)S(1)} %fusion.176), channel_id=1, source_target_pairs={{0,4},{4,8},{8,12},{12,16},{16,20},{20,24},{24,28},{28,32},{32,36}... | collective-permute-start | bytes 196616 | tf_op jit(solution)/shard_map/ppermute | solution.py:34
  341.8 7.8 %collective-permute-start.40 = (f32[1,4,1,32,64]{4,3,2,1,0:T(8,128)S(1)}, f32[1,4,1,32,64]{4,3,2,1,0:T(8,128)S(1)}, u32[]{:S(2)}, u32[]{:S(2)}) collective-permute-start(f32[1,4,1,32,64]{4,3,2,1,0:T(8,128)S(1)} %get-tuple-element.83), channel_id=1, source_target_pairs={{1,0},{2,1},{3,2},{5,4},{6,5},{7,6},{9,8},{10,9},{11,10},{13,12},{... | collective-permute-start | bytes 98312 | tf_op jit(solution)/shard_map/ppermute | solution.py:26
  343.1 6.5 %collective-permute-start.41 = (f32[1,4,1,32,64]{4,3,2,1,0:T(8,128)S(1)}, f32[1,4,1,32,64]{4,3,2,1,0:T(8,128)S(1)}, u32[]{:S(2)}, u32[]{:S(2)}) collective-permute-start(f32[1,4,1,32,64]{4,3,2,1,0:T(8,128)S(1)} %get-tuple-element.84), channel_id=1, source_target_pairs={{0,1},{1,2},{2,3},{4,5},{5,6},{6,7},{8,9},{9,10},{10,11},{12,13},{... | collective-permute-start | bytes 98312 | tf_op jit(solution)/shard_map/ppermute | solution.py:23
  347.6 8.4 %collective-permute-start.39 = (f32[1,4,2,32,64]{4,3,2,1,0:T(8,128)S(1)}, f32[1,4,2,32,64]{4,3,2,1,0:T(8,128)S(1)}, u32[]{:S(2)}, u32[]{:S(2)}) collective-permute-start(f32[1,4,2,32,64]{4,3,2,1,0:T(8,128)S(1)} %broadcast_add_fusion), channel_id=1, source_target_pairs={{0,4},{4,8},{8,12},{12,16},{16,20},{20,24},{24,28},{28,32},{32,36}... | collective-permute-start | bytes 196616 | tf_op jit(solution)/shard_map/ppermute | solution.py:34
  356.2 7.8 %collective-permute-start.43 = (f32[1,4,1,32,64]{4,3,2,1,0:T(8,128)S(1)}, f32[1,4,1,32,64]{4,3,2,1,0:T(8,128)S(1)}, u32[]{:S(2)}, u32[]{:S(2)}) collective-permute-start(f32[1,4,1,32,64]{4,3,2,1,0:T(8,128)S(1)} %get-tuple-element.79), channel_id=1, source_target_pairs={{1,0},{2,1},{3,2},{5,4},{6,5},{7,6},{9,8},{10,9},{11,10},{13,12},{... | collective-permute-start | bytes 98312 | tf_op jit(solution)/shard_map/ppermute | solution.py:26
  357.5 6.5 %collective-permute-start.44 = (f32[1,4,1,32,64]{4,3,2,1,0:T(8,128)S(1)}, f32[1,4,1,32,64]{4,3,2,1,0:T(8,128)S(1)}, u32[]{:S(2)}, u32[]{:S(2)}) collective-permute-start(f32[1,4,1,32,64]{4,3,2,1,0:T(8,128)S(1)} %get-tuple-element.80), channel_id=1, source_target_pairs={{0,1},{1,2},{2,3},{4,5},{5,6},{6,7},{8,9},{9,10},{10,11},{12,13},{... | collective-permute-start | bytes 98312 | tf_op jit(solution)/shard_map/ppermute | solution.py:23
  362.0 8.4 %collective-permute-start.42 = (f32[1,4,2,32,64]{4,3,2,1,0:T(8,128)S(1)}, f32[1,4,2,32,64]{4,3,2,1,0:T(8,128)S(1)}, u32[]{:S(2)}, u32[]{:S(2)}) collective-permute-start(f32[1,4,2,32,64]{4,3,2,1,0:T(8,128)S(1)} %fusion.149), channel_id=1, source_target_pairs={{0,4},{4,8},{8,12},{12,16},{16,20},{20,24},{24,28},{28,32},{32,36}... | collective-permute-start | bytes 196616 | tf_op jit(solution)/shard_map/ppermute | solution.py:34
  371.0 12.6 %collective-permute-start.45 = (f32[1,4,4,64,128]{4,3,2,1,0:T(8,128)S(1)}, f32[1,4,4,64,128]{4,3,2,1,0:T(8,128)S(1)}, u32[]{:S(2)}, u32[]{:S(2)}) collective-permute-start(f32[1,4,4,64,128]{4,3,2,1,0:T(8,128)S(1)} %add.545), channel_id=1, source_target_pairs={{0,4},{4,8},{8,12},{12,16},{16,20},{20,24},{24,28},{28,32},{32,36}... | collective-permute-start | bytes 1572872 | tf_op jit(solution)/shard_map/ppermute | solution.py:34
  373.0 6.9 %collective-permute-start.46 = (f32[1,4,1,64,128]{4,3,2,1,0:T(8,128)S(1)}, f32[1,4,1,64,128]{4,3,2,1,0:T(8,128)S(1)}, u32[]{:S(2)}, u32[]{:S(2)}) collective-permute-start(f32[1,4,1,64,128]{4,3,2,1,0:T(8,128)S(1)} %get-tuple-element.31), channel_id=1, source_target_pairs={{1,0},{2,1},{3,2},{5,4},{6,5},{7,6},{9,8},{10,9},{11,10},{13,12},{... | collective-permute-start | bytes 393224 | tf_op jit(solution)/shard_map/ppermute | solution.py:26
  374.3 7.1 %collective-permute-start.47 = (f32[1,4,1,64,128]{4,3,2,1,0:T(8,128)S(1)}, f32[1,4,1,64,128]{4,3,2,1,0:T(8,128)S(1)}, u32[]{:S(2)}, u32[]{:S(2)}) collective-permute-start(f32[1,4,1,64,128]{4,3,2,1,0:T(8,128)S(1)} %get-tuple-element.32), channel_id=1, source_target_pairs={{0,1},{1,2},{2,3},{4,5},{5,6},{6,7},{8,9},{9,10},{10,11},{12,13},{... | collective-permute-start | bytes 393224 | tf_op jit(solution)/shard_map/ppermute | solution.py:23
  384.2 12.6 %collective-permute-start.48 = (f32[1,4,4,64,128]{4,3,2,1,0:T(8,128)S(1)}, f32[1,4,4,64,128]{4,3,2,1,0:T(8,128)S(1)}, u32[]{:S(2)}, u32[]{:S(2)}) collective-permute-start(f32[1,4,4,64,128]{4,3,2,1,0:T(8,128)S(1)} %fusion.25), channel_id=1, source_target_pairs={{0,4},{4,8},{8,12},{12,16},{16,20},{20,24},{24,28},{28,32},{32,36}... | collective-permute-start | bytes 1572872 | tf_op jit(solution)/shard_map/ppermute | solution.py:34
  386.1 6.9 %collective-permute-start.49 = (f32[1,4,1,64,128]{4,3,2,1,0:T(8,128)S(1)}, f32[1,4,1,64,128]{4,3,2,1,0:T(8,128)S(1)}, u32[]{:S(2)}, u32[]{:S(2)}) collective-permute-start(f32[1,4,1,64,128]{4,3,2,1,0:T(8,128)S(1)} %get-tuple-element.27), channel_id=1, source_target_pairs={{1,0},{2,1},{3,2},{5,4},{6,5},{7,6},{9,8},{10,9},{11,10},{13,12},{... | collective-permute-start | bytes 393224 | tf_op jit(solution)/shard_map/ppermute | solution.py:26
  387.4 7.1 %collective-permute-start.50 = (f32[1,4,1,64,128]{4,3,2,1,0:T(8,128)S(1)}, f32[1,4,1,64,128]{4,3,2,1,0:T(8,128)S(1)}, u32[]{:S(2)}, u32[]{:S(2)}) collective-permute-start(f32[1,4,1,64,128]{4,3,2,1,0:T(8,128)S(1)} %get-tuple-element.28), channel_id=1, source_target_pairs={{0,1},{1,2},{2,3},{4,5},{5,6},{6,7},{8,9},{9,10},{10,11},{12,13},{... | collective-permute-start | bytes 393224 | tf_op jit(solution)/shard_map/ppermute | solution.py:23
Sparse Core Ops, SparseCore 0:
  80.2 39.3 all-gather.6
  282.2 39.2 all-gather.8

commit v7 on v6

--- a/solution.py
+++ b/solution.py
@@ -220,7 +220,15 @@
         (local_steps, planes * components, height_y * width_z),
     )
     mine = mine.reshape(local_steps, planes, components, height_y, width_z)
-    return mine.transpose(0, 2, 1, 3, 4)
+    padded = jnp.pad(solved, ((1, 0), (components, components), (0, 0)))
+    around = lax.dynamic_slice(
+        padded,
+        (time_at * local_steps, plane_at * planes * components, 0),
+        (local_steps + 1, (planes + 2) * components, height_y * width_z),
+    )
+    around = around.reshape(local_steps + 1, planes + 2, components, height_y, width_z)
+    fine = prolong(around.transpose(0, 2, 1, 3, 4))[:, :, 1:-1]
+    return (mine.transpose(0, 2, 1, 3, 4), fine)
 
 
 def per_device(right_side, metric, wall_mask):
@@ -243,14 +251,22 @@
         diagonal = diagonal_of(metrics[depth], spacing, pinned_levels[depth])
         for repeat in range(NU):
             values = sweep(depth, values, source, diagonal)
-        residual = source - apply_local(values, metrics[depth], spacing, pinned_levels[depth])
+        applied = apply_local(values, metrics[depth], spacing, pinned_levels[depth])
+        residual = source - applied
         coarse_source = restrict(residual)
         if depth == 1:
-            correction = coarse_correction(coarse_source, metric_two, gathered)
+            correction, fine = coarse_correction(coarse_source, metric_two, gathered)
+            applied = applied + stencil_apply(
+                fine[1:], metrics[depth], fine[:-1, :, 1:-1], spacing, None
+            )
+            values = values + prolong(correction)
+            values = values + OMEGA * (source - applied) / diagonal
+            remaining = NU - 1
         else:
             correction = cycle(1, None, coarse_source)
-        values = values + prolong(correction)
-        for repeat in range(NU):
+            values = values + prolong(correction)
+            remaining = NU
+        for repeat in range(remaining):
             values = sweep(depth, values, source, diagonal)
         return values
 

time: 407 us -> 381 us (0.936)
  starting transfers between devices: 132 us -> 117 us
  waiting for transfers between devices: 170 us -> 158 us
    ppermute x17 -> x15, waiting for transfers between devices: 67.5 us -> 54.7 us  [from_behind(): return lax.ppermute(array, axis, pairs)]
    ppermute x17 -> x15, starting transfers between devices: 77.6 us -> 68.3 us  [with_halo(): lax.ppermute(lax.slice_in_dim(block, block.shape[dim] - width, None, axis...]
    ppermute x17 -> x15, starting transfers between devices: 32.8 us -> 28.9 us  [from_behind(): return lax.ppermute(array, axis, pairs)]
    ppermute x17 -> x15, starting transfers between devices: 22 us -> 19.6 us  [with_halo(): lax.ppermute(lax.slice_in_dim(block, 0, width, axis=dim), axis, backward)]
    ppermute x17 -> x15, waiting for transfers between devices: 13.7 us -> 13.9 us  [with_halo(): lax.ppermute(lax.slice_in_dim(block, block.shape[dim] - width, None, axis...]
    ppermute x17 -> x15, waiting for transfers between devices: 10.3 us -> 10.3 us  [with_halo(): lax.ppermute(lax.slice_in_dim(block, 0, width, axis=dim), axis, backward)]
  transfers between devices with their start and end apart: 53 -> 47, of which waited for: 37 -> 35; matrix products, arithmetic and copies ran while one was open for 1% -> 1% of each run, Pallas kernels for 0% -> 0%
where the time goes in v7:
time: 381 us; the launch traced here: 380 us
  waiting for transfers between devices  158 us (41%)
  starting transfers between devices  117 us (31%)
  Pallas kernels  33.1 us (9%)
  blocking collectives  25.5 us (7%)
  local copies, waits for them, and re-layouts  16.9 us (4%)
  between operations  14.6 us (4%)
  other arithmetic  12.6 us (3%)
    all_gather x2, waiting for transfers between devices, gather_all(): return lax.all_gather(within, 'tm', axis=0, tiled=True)  78.8 us
    ppermute x15, starting transfers between devices, with_halo(): lax.ppermute(lax.slice_in_dim(block, block.shape[dim] - width, None, axis...  68.3 us
    ppermute x15, waiting for transfers between devices, from_behind(): return lax.ppermute(array, axis, pairs)  54.7 us
    pallas_call x2, Pallas kernels, coarse_solve(): pl.pallas_call(kernel, out_shape=jax.ShapeDtypeStruct(flat_source.shape,...  33.1 us
    ppermute x15, starting transfers between devices, from_behind(): return lax.ppermute(array, axis, pairs)  28.9 us
    all_gather x2, blocking collectives, gather_all(): within = lax.all_gather(flat, 'space', axis=0, tiled=True)  25.5 us
    ppermute x15, starting transfers between devices, with_halo(): lax.ppermute(lax.slice_in_dim(block, 0, width, axis=dim), axis, backward)  19.6 us
    ppermute x15, waiting for transfers between devices, with_halo(): lax.ppermute(lax.slice_in_dim(block, block.shape[dim] - width, None, axis...  13.9 us
  transfers between devices with their start and end apart: 47, of which 35 were waited for; matrix products, arithmetic and copies ran while one was open for 1% of the time, Pallas kernels for 0%

profile of v7, /device:TPU:2, one launch (start us, length us, event | category | flops | bytes accessed | tf_op | source)
XLA Modules:
  0.0 379.6 jit_solution(5891378829642714763)
XLA Ops:
  9.8 2.1 collective-permute-start
  13.2 4.6 %collective-permute-start.2 = (f32[1,4,1,64,128]{4,3,2,1,0:T(8,128)S(1)}, f32[1,4,1,64,128]{4,3,2,1,0:T(8,128)S(1)}, u32[]{:S(2)}, u32[]{:S(2)}) collective-permute-start(f32[1,4,1,64,128]{4,3,2,1,0:T(8,128)S(1)} %get-tuple-element.68), channel_id=1, source_target_pairs={{0,1},{1,2},{2,3},{4,5},{5,6},{6,7},{8,9},{9,10},{10,11},{12,13},{... | collective-permute-start | bytes 393224 | tf_op jit(solution)/shard_map/ppermute | solution.py:23
  19.2 1.7 collective-permute-done.2
  23.1 1.9 collective-permute-start.3
  26.3 4.6 %collective-permute-start.5 = (f32[1,4,1,64,128]{4,3,2,1,0:T(8,128)S(1)}, f32[1,4,1,64,128]{4,3,2,1,0:T(8,128)S(1)}, u32[]{:S(2)}, u32[]{:S(2)}) collective-permute-start(f32[1,4,1,64,128]{4,3,2,1,0:T(8,128)S(1)} %get-tuple-element.64), channel_id=1, source_target_pairs={{0,1},{1,2},{2,3},{4,5},{5,6},{6,7},{8,9},{9,10},{10,11},{12,13},{... | collective-permute-start | bytes 393224 | tf_op jit(solution)/shard_map/ppermute | solution.py:23
  30.9 2.2 collective-permute-done.4
  33.1 1.5 collective-permute-done.5
  38.0 4.5 %collective-permute-start.8 = (f32[1,4,1,32,64]{4,3,2,1,0:T(8,128)S(1)}, f32[1,4,1,32,64]{4,3,2,1,0:T(8,128)S(1)}, u32[]{:S(2)}, u32[]{:S(2)}) collective-permute-start(f32[1,4,1,32,64]{4,3,2,1,0:T(8,128)S(1)} %get-tuple-element.108), channel_id=1, source_target_pairs={{0,1},{1,2},{2,3},{4,5},{5,6},{6,7},{8,9},{9,10},{10,11},{12,13},{... | collective-permute-start | bytes 98312 | tf_op jit(solution)/shard_map/ppermute | solution.py:23
  42.6 1.9 collective-permute-start.6
  44.6 6.3 %collective-permute-done.6 = f32[1,4,2,32,64]{4,3,2,1,0:T(8,128)S(1)} collective-permute-done((f32[1,4,2,32,64]{4,3,2,1,0:T(8,128)S(1)}, f32[1,4,2,32,64]{4,3,2,1,0:T(8,128)S(1)}, u32[]{:S(2)}, u32[]{:S(2)}) %collective-permute-start.6) | collective-permute-done | bytes 65568 | tf_op jit(solution)/shard_map/ppermute | solution.py:34
  52.4 4.5 %collective-permute-start.11 = (f32[1,4,1,32,64]{4,3,2,1,0:T(8,128)S(1)}, f32[1,4,1,32,64]{4,3,2,1,0:T(8,128)S(1)}, u32[]{:S(2)}, u32[]{:S(2)}) collective-permute-start(f32[1,4,1,32,64]{4,3,2,1,0:T(8,128)S(1)} %get-tuple-element.104), channel_id=1, source_target_pairs={{0,1},{1,2},{2,3},{4,5},{5,6},{6,7},{8,9},{9,10},{10,11},{12,13},{... | collective-permute-start | bytes 98312 | tf_op jit(solution)/shard_map/ppermute | solution.py:23
  57.2 1.9 collective-permute-start.9
  59.3 6.3 %collective-permute-done.9 = f32[1,4,2,32,64]{4,3,2,1,0:T(8,128)S(1)} collective-permute-done((f32[1,4,2,32,64]{4,3,2,1,0:T(8,128)S(1)}, f32[1,4,2,32,64]{4,3,2,1,0:T(8,128)S(1)}, u32[]{:S(2)}, u32[]{:S(2)}) %collective-permute-start.9) | collective-permute-done | bytes 65568 | tf_op jit(solution)/shard_map/ppermute | solution.py:34
  66.3 13.1 %all-gather = f32[4,1,2560]{2,1,0:T(1,128)S(1)} all-gather(f32[1,1,2560]{2,1,0:T(1,128)S(1)} %maximum_bitcast_fusion), channel_id=1, replica_groups=mesh['tm'=32,'space'=4] {'space'}, dimensions={0}, use_global_device_ids=true | all-gather | bytes 51200 | tf_op jit(solution)/shard_map/all_gather | solution.py:191
  80.1 39.5 %all-gather.7.cloned.1.call-done = f32[32,4,2560]{2,1,0:T(4,128)} async-done(((f32[1,4,2560]{2,1,0:T(4,128)}), f32[32,4,2560]{2,1,0:T(4,128)}) %all-gather.7.cloned.1.call-update) | async-done | bytes 1310736 | tf_op jit(solution)/shard_map/all_gather | solution.py:192
  119.6 1.7 reshape.877
  122.4 2.5 reshape_transpose_reshape.10.src_ref
  126.6 16.5 %shard_map.37 = f32[32,16,512]{2,1,0:T(8,128)} custom-call(f32[32,16,512]{2,1,0:T(8,128)} %reshape_transpose_reshape.10.src_ref, f32[32,16,512]{2,1,0:T(8,128)} %reshape.856.met_ref), custom_call_target="tpu_custom_call" | custom-call | tf_op jit(solution)/shard_map/pallas_call | solution.py:161
  147.2 4.5 %collective-permute-start.14 = (f32[1,4,1,32,64]{4,3,2,1,0:T(8,128)S(1)}, f32[1,4,1,32,64]{4,3,2,1,0:T(8,128)S(1)}, u32[]{:S(2)}, u32[]{:S(2)}) collective-permute-start(f32[1,4,1,32,64]{4,3,2,1,0:T(8,128)S(1)} %get-tuple-element.100), channel_id=1, source_target_pairs={{0,1},{1,2},{2,3},{4,5},{5,6},{6,7},{8,9},{9,10},{10,11},{12,13},{... | collective-permute-start | bytes 98312 | tf_op jit(solution)/shard_map/ppermute | solution.py:23
  151.8 1.9 collective-permute-start.12
  153.9 6.3 %collective-permute-done.12 = f32[1,4,2,32,64]{4,3,2,1,0:T(8,128)S(1)} collective-permute-done((f32[1,4,2,32,64]{4,3,2,1,0:T(8,128)S(1)}, f32[1,4,2,32,64]{4,3,2,1,0:T(8,128)S(1)}, u32[]{:S(2)}, u32[]{:S(2)}) %collective-permute-start.12) | collective-permute-done | bytes 65568 | tf_op jit(solution)/shard_map/ppermute | solution.py:34
  160.8 1.9 collective-permute-start.15
  164.0 4.6 %collective-permute-start.17 = (f32[1,4,1,64,128]{4,3,2,1,0:T(8,128)S(1)}, f32[1,4,1,64,128]{4,3,2,1,0:T(8,128)S(1)}, u32[]{:S(2)}, u32[]{:S(2)}) collective-permute-start(f32[1,4,1,64,128]{4,3,2,1,0:T(8,128)S(1)} %get-tuple-element.60), channel_id=1, source_target_pairs={{0,1},{1,2},{2,3},{4,5},{5,6},{6,7},{8,9},{9,10},{10,11},{12,13},{... | collective-permute-start | bytes 393224 | tf_op jit(solution)/shard_map/ppermute | solution.py:23
  169.6 1.5 collective-permute-done.17
  171.3 2.1 collective-permute-done.15
  173.9 1.9 collective-permute-start.18
  177.2 4.6 %collective-permute-start.20 = (f32[1,4,1,64,128]{4,3,2,1,0:T(8,128)S(1)}, f32[1,4,1,64,128]{4,3,2,1,0:T(8,128)S(1)}, u32[]{:S(2)}, u32[]{:S(2)}) collective-permute-start(f32[1,4,1,64,128]{4,3,2,1,0:T(8,128)S(1)} %get-tuple-element.56), channel_id=1, source_target_pairs={{0,1},{1,2},{2,3},{4,5},{5,6},{6,7},{8,9},{9,10},{10,11},{12,13},{... | collective-permute-start | bytes 393224 | tf_op jit(solution)/shard_map/ppermute | solution.py:23
  182.7 1.5 collective-permute-done.20
  184.4 2.1 collective-permute-done.18
  187.1 1.9 collective-permute-start.21
  190.3 4.6 %collective-permute-start.23 = (f32[1,4,1,64,128]{4,3,2,1,0:T(8,128)S(1)}, f32[1,4,1,64,128]{4,3,2,1,0:T(8,128)S(1)}, u32[]{:S(2)}, u32[]{:S(2)}) collective-permute-start(f32[1,4,1,64,128]{4,3,2,1,0:T(8,128)S(1)} %get-tuple-element.52), channel_id=1, source_target_pairs={{0,1},{1,2},{2,3},{4,5},{5,6},{6,7},{8,9},{9,10},{10,11},{12,13},{... | collective-permute-start | bytes 393224 | tf_op jit(solution)/shard_map/ppermute | solution.py:23
  195.9 1.5 collective-permute-done.23
  197.6 2.1 collective-permute-done.21
  200.2 1.9 collective-permute-start.24
  203.5 4.6 %collective-permute-start.26 = (f32[1,4,1,64,128]{4,3,2,1,0:T(8,128)S(1)}, f32[1,4,1,64,128]{4,3,2,1,0:T(8,128)S(1)}, u32[]{:S(2)}, u32[]{:S(2)}) collective-permute-start(f32[1,4,1,64,128]{4,3,2,1,0:T(8,128)S(1)} %get-tuple-element.48), channel_id=1, source_target_pairs={{0,1},{1,2},{2,3},{4,5},{5,6},{6,7},{8,9},{9,10},{10,11},{12,13},{... | collective-permute-start | bytes 393224 | tf_op jit(solution)/shard_map/ppermute | solution.py:23
  209.1 1.5 collective-permute-done.26
  210.8 2.1 collective-permute-done.24
  213.4 1.9 collective-permute-start.27
  215.4 1.5 collective-permute-start.28
  216.8 4.6 %collective-permute-start.29 = (f32[1,4,1,64,128]{4,3,2,1,0:T(8,128)S(1)}, f32[1,4,1,64,128]{4,3,2,1,0:T(8,128)S(1)}, u32[]{:S(2)}, u32[]{:S(2)}) collective-permute-start(f32[1,4,1,64,128]{4,3,2,1,0:T(8,128)S(1)} %get-tuple-element.44), channel_id=1, source_target_pairs={{0,1},{1,2},{2,3},{4,5},{5,6},{6,7},{8,9},{9,10},{10,11},{12,13},{... | collective-permute-start | bytes 393224 | tf_op jit(solution)/shard_map/ppermute | solution.py:23
  222.2 1.7 collective-permute-done.29
  224.1 1.9 collective-permute-done.27
  228.3 4.5 %collective-permute-start.32 = (f32[1,4,1,32,64]{4,3,2,1,0:T(8,128)S(1)}, f32[1,4,1,32,64]{4,3,2,1,0:T(8,128)S(1)}, u32[]{:S(2)}, u32[]{:S(2)}) collective-permute-start(f32[1,4,1,32,64]{4,3,2,1,0:T(8,128)S(1)} %get-tuple-element.96), channel_id=1, source_target_pairs={{0,1},{1,2},{2,3},{4,5},{5,6},{6,7},{8,9},{9,10},{10,11},{12,13},{... | collective-permute-start | bytes 98312 | tf_op jit(solution)/shard_map/ppermute | solution.py:23
  232.9 1.9 collective-permute-start.30
  234.9 6.3 %collective-permute-done.30 = f32[1,4,2,32,64]{4,3,2,1,0:T(8,128)S(1)} collective-permute-done((f32[1,4,2,32,64]{4,3,2,1,0:T(8,128)S(1)}, f32[1,4,2,32,64]{4,3,2,1,0:T(8,128)S(1)}, u32[]{:S(2)}, u32[]{:S(2)}) %collective-permute-start.30) | collective-permute-done | bytes 65568 | tf_op jit(solution)/shard_map/ppermute | solution.py:34
  242.7 4.5 %collective-permute-start.35 = (f32[1,4,1,32,64]{4,3,2,1,0:T(8,128)S(1)}, f32[1,4,1,32,64]{4,3,2,1,0:T(8,128)S(1)}, u32[]{:S(2)}, u32[]{:S(2)}) collective-permute-start(f32[1,4,1,32,64]{4,3,2,1,0:T(8,128)S(1)} %get-tuple-element.92), channel_id=1, source_target_pairs={{0,1},{1,2},{2,3},{4,5},{5,6},{6,7},{8,9},{9,10},{10,11},{12,13},{... | collective-permute-start | bytes 98312 | tf_op jit(solution)/shard_map/ppermute | solution.py:23
  247.3 1.9 collective-permute-start.33
  249.4 6.3 %collective-permute-done.33 = f32[1,4,2,32,64]{4,3,2,1,0:T(8,128)S(1)} collective-permute-done((f32[1,4,2,32,64]{4,3,2,1,0:T(8,128)S(1)}, f32[1,4,2,32,64]{4,3,2,1,0:T(8,128)S(1)}, u32[]{:S(2)}, u32[]{:S(2)}) %collective-permute-start.33) | collective-permute-done | bytes 65568 | tf_op jit(solution)/shard_map/ppermute | solution.py:34
  256.3 12.4 %all-gather.2 = f32[4,1,2048]{2,1,0:T(1,128)S(1)} all-gather(f32[1,1,2048]{2,1,0:T(1,128)S(1)} %reshape.878), channel_id=1, replica_groups=mesh['tm'=32,'space'=4] {'space'}, dimensions={0}, use_global_device_ids=true | all-gather | bytes 40960 | tf_op jit(solution)/shard_map/all_gather | solution.py:191
  269.4 39.4 %all-gather.9.cloned.1.call-done = f32[32,4,2048]{2,1,0:T(4,128)} async-done(((f32[1,4,2048]{2,1,0:T(4,128)}), f32[32,4,2048]{2,1,0:T(4,128)}) %all-gather.9.cloned.1.call-update) | async-done | bytes 1048592 | tf_op jit(solution)/shard_map/all_gather | solution.py:192
  308.8 2.8 reshape_transpose_reshape.12.src_ref
  311.5 16.5 %shard_map.38 = f32[32,16,512]{2,1,0:T(8,128)} custom-call(f32[32,16,512]{2,1,0:T(8,128)} %reshape_transpose_reshape.12.src_ref, f32[32,16,512]{2,1,0:T(8,128)} %reshape.856.met_ref), custom_call_target="tpu_custom_call" | custom-call | tf_op jit(solution)/shard_map/pallas_call | solution.py:161
  332.1 4.5 %collective-permute-start.38 = (f32[1,4,1,32,64]{4,3,2,1,0:T(8,128)S(1)}, f32[1,4,1,32,64]{4,3,2,1,0:T(8,128)S(1)}, u32[]{:S(2)}, u32[]{:S(2)}) collective-permute-start(f32[1,4,1,32,64]{4,3,2,1,0:T(8,128)S(1)} %get-tuple-element.88), channel_id=1, source_target_pairs={{0,1},{1,2},{2,3},{4,5},{5,6},{6,7},{8,9},{9,10},{10,11},{12,13},{... | collective-permute-start | bytes 98312 | tf_op jit(solution)/shard_map/ppermute | solution.py:23
  336.7 1.9 collective-permute-start.36
  338.8 6.3 %collective-permute-done.36 = f32[1,4,2,32,64]{4,3,2,1,0:T(8,128)S(1)} collective-permute-done((f32[1,4,2,32,64]{4,3,2,1,0:T(8,128)S(1)}, f32[1,4,2,32,64]{4,3,2,1,0:T(8,128)S(1)}, u32[]{:S(2)}, u32[]{:S(2)}) %collective-permute-start.36) | collective-permute-done | bytes 65568 | tf_op jit(solution)/shard_map/ppermute | solution.py:34
  345.7 1.9 collective-permute-start.39
  348.9 4.6 %collective-permute-start.41 = (f32[1,4,1,64,128]{4,3,2,1,0:T(8,128)S(1)}, f32[1,4,1,64,128]{4,3,2,1,0:T(8,128)S(1)}, u32[]{:S(2)}, u32[]{:S(2)}) collective-permute-start(f32[1,4,1,64,128]{4,3,2,1,0:T(8,128)S(1)} %get-tuple-element.40), channel_id=1, source_target_pairs={{0,1},{1,2},{2,3},{4,5},{5,6},{6,7},{8,9},{9,10},{10,11},{12,13},{... | collective-permute-start | bytes 393224 | tf_op jit(solution)/shard_map/ppermute | solution.py:23
  354.5 1.5 collective-permute-done.41
  356.2 2.1 collective-permute-done.39
  358.8 1.9 collective-permute-start.42
  362.1 4.6 %collective-permute-start.44 = (f32[1,4,1,64,128]{4,3,2,1,0:T(8,128)S(1)}, f32[1,4,1,64,128]{4,3,2,1,0:T(8,128)S(1)}, u32[]{:S(2)}, u32[]{:S(2)}) collective-permute-start(f32[1,4,1,64,128]{4,3,2,1,0:T(8,128)S(1)} %get-tuple-element.36), channel_id=1, source_target_pairs={{0,1},{1,2},{2,3},{4,5},{5,6},{6,7},{8,9},{9,10},{10,11},{12,13},{... | collective-permute-start | bytes 393224 | tf_op jit(solution)/shard_map/ppermute | solution.py:23
  367.6 1.5 collective-permute-done.44
  369.4 2.1 collective-permute-done.42
  371.4 1.3 fusion.11
  (164 shorter events, 52.0 us)
Async XLA Ops:
  6.5 113.0 %all-gather.7.cloned.1.call-start = ((), (), s32[]{:S(2)}) async-start(), calls=%async_computation | async-start | bytes 1351680 | tf_op jit(solution)/shard_map/all_gather | solution.py:192
  7.5 10.2 %copy-start.1 = (f32[1,4,64,128]{3,2,1,0:T(8,128)S(1)}, f32[1,4,64,128]{3,2,1,0:T(8,128)}, u32[]{:S(2)}) copy-start(f32[1,4,64,128]{3,2,1,0:T(8,128)} %param.4) | copy-start | bytes 393220
  9.8 12.8 %copy-start = (f32[1,4,4,64,128]{4,3,2,1,0:T(8,128)S(1)}, f32[1,4,4,64,128]{4,3,2,1,0:T(8,128)}, u32[]{:S(2)}) copy-start(f32[1,4,4,64,128]{4,3,2,1,0:T(8,128)} %param.3) | copy-start | bytes 1572868
  9.8 12.7 %collective-permute-start = (f32[1,4,4,64,128]{4,3,2,1,0:T(8,128)S(1)}, f32[1,4,4,64,128]{4,3,2,1,0:T(8,128)S(1)}, u32[]{:S(2)}, u32[]{:S(2)}) collective-permute-start(f32[1,4,4,64,128]{4,3,2,1,0:T(8,128)S(1)} %get-tuple-element.9), channel_id=1, source_target_pairs={{0,4},{4,8},{8,12},{12,16},{16,20},{20,24},{24,28},{28,32},{32,36}... | collective-permute-start | bytes 1572872 | tf_op jit(solution)/shard_map/ppermute | solution.py:34
  11.9 7.4 %collective-permute-start.1 = (f32[1,4,1,64,128]{4,3,2,1,0:T(8,128)S(1)}, f32[1,4,1,64,128]{4,3,2,1,0:T(8,128)S(1)}, u32[]{:S(2)}, u32[]{:S(2)}) collective-permute-start(f32[1,4,1,64,128]{4,3,2,1,0:T(8,128)S(1)} %get-tuple-element.67), channel_id=1, source_target_pairs={{1,0},{2,1},{3,2},{5,4},{6,5},{7,6},{9,8},{10,9},{11,10},{13,12},{... | collective-permute-start | bytes 393224 | tf_op jit(solution)/shard_map/ppermute | solution.py:26
  13.2 7.8 %collective-permute-start.2 = (f32[1,4,1,64,128]{4,3,2,1,0:T(8,128)S(1)}, f32[1,4,1,64,128]{4,3,2,1,0:T(8,128)S(1)}, u32[]{:S(2)}, u32[]{:S(2)}) collective-permute-start(f32[1,4,1,64,128]{4,3,2,1,0:T(8,128)S(1)} %get-tuple-element.68), channel_id=1, source_target_pairs={{0,1},{1,2},{2,3},{4,5},{5,6},{6,7},{8,9},{9,10},{10,11},{12,13},{... | collective-permute-start | bytes 393224 | tf_op jit(solution)/shard_map/ppermute | solution.py:23
  23.1 12.6 %collective-permute-start.3 = (f32[1,4,4,64,128]{4,3,2,1,0:T(8,128)S(1)}, f32[1,4,4,64,128]{4,3,2,1,0:T(8,128)S(1)}, u32[]{:S(2)}, u32[]{:S(2)}) collective-permute-start(f32[1,4,4,64,128]{4,3,2,1,0:T(8,128)S(1)} %fusion.119), channel_id=1, source_target_pairs={{0,4},{4,8},{8,12},{12,16},{16,20},{20,24},{24,28},{28,32},{32,36}... | collective-permute-start | bytes 1572872 | tf_op jit(solution)/shard_map/ppermute | solution.py:34
  25.0 8.1 %collective-permute-start.4 = (f32[1,4,1,64,128]{4,3,2,1,0:T(8,128)S(1)}, f32[1,4,1,64,128]{4,3,2,1,0:T(8,128)S(1)}, u32[]{:S(2)}, u32[]{:S(2)}) collective-permute-start(f32[1,4,1,64,128]{4,3,2,1,0:T(8,128)S(1)} %get-tuple-element.63), channel_id=1, source_target_pairs={{1,0},{2,1},{3,2},{5,4},{6,5},{7,6},{9,8},{10,9},{11,10},{13,12},{... | collective-permute-start | bytes 393224 | tf_op jit(solution)/shard_map/ppermute | solution.py:26
  26.3 8.3 %collective-permute-start.5 = (f32[1,4,1,64,128]{4,3,2,1,0:T(8,128)S(1)}, f32[1,4,1,64,128]{4,3,2,1,0:T(8,128)S(1)}, u32[]{:S(2)}, u32[]{:S(2)}) collective-permute-start(f32[1,4,1,64,128]{4,3,2,1,0:T(8,128)S(1)} %get-tuple-element.64), channel_id=1, source_target_pairs={{0,1},{1,2},{2,3},{4,5},{5,6},{6,7},{8,9},{9,10},{10,11},{12,13},{... | collective-permute-start | bytes 393224 | tf_op jit(solution)/shard_map/ppermute | solution.py:23
  36.7 7.8 %collective-permute-start.7 = (f32[1,4,1,32,64]{4,3,2,1,0:T(8,128)S(1)}, f32[1,4,1,32,64]{4,3,2,1,0:T(8,128)S(1)}, u32[]{:S(2)}, u32[]{:S(2)}) collective-permute-start(f32[1,4,1,32,64]{4,3,2,1,0:T(8,128)S(1)} %get-tuple-element.107), channel_id=1, source_target_pairs={{1,0},{2,1},{3,2},{5,4},{6,5},{7,6},{9,8},{10,9},{11,10},{13,12},{... | collective-permute-start | bytes 98312 | tf_op jit(solution)/shard_map/ppermute | solution.py:26
  38.0 6.5 %collective-permute-start.8 = (f32[1,4,1,32,64]{4,3,2,1,0:T(8,128)S(1)}, f32[1,4,1,32,64]{4,3,2,1,0:T(8,128)S(1)}, u32[]{:S(2)}, u32[]{:S(2)}) collective-permute-start(f32[1,4,1,32,64]{4,3,2,1,0:T(8,128)S(1)} %get-tuple-element.108), channel_id=1, source_target_pairs={{0,1},{1,2},{2,3},{4,5},{5,6},{6,7},{8,9},{9,10},{10,11},{12,13},{... | collective-permute-start | bytes 98312 | tf_op jit(solution)/shard_map/ppermute | solution.py:23
  42.6 8.4 %collective-permute-start.6 = (f32[1,4,2,32,64]{4,3,2,1,0:T(8,128)S(1)}, f32[1,4,2,32,64]{4,3,2,1,0:T(8,128)S(1)}, u32[]{:S(2)}, u32[]{:S(2)}) collective-permute-start(f32[1,4,2,32,64]{4,3,2,1,0:T(8,128)S(1)} %fusion.388), channel_id=1, source_target_pairs={{0,4},{4,8},{8,12},{12,16},{16,20},{20,24},{24,28},{28,32},{32,36}... | collective-permute-start | bytes 196616 | tf_op jit(solution)/shard_map/ppermute | solution.py:34
  51.1 8.0 %collective-permute-start.10 = (f32[1,4,1,32,64]{4,3,2,1,0:T(8,128)S(1)}, f32[1,4,1,32,64]{4,3,2,1,0:T(8,128)S(1)}, u32[]{:S(2)}, u32[]{:S(2)}) collective-permute-start(f32[1,4,1,32,64]{4,3,2,1,0:T(8,128)S(1)} %get-tuple-element.103), channel_id=1, source_target_pairs={{1,0},{2,1},{3,2},{5,4},{6,5},{7,6},{9,8},{10,9},{11,10},{13,12},{... | collective-permute-start | bytes 98312 | tf_op jit(solution)/shard_map/ppermute | solution.py:26
  52.4 6.7 %collective-permute-start.11 = (f32[1,4,1,32,64]{4,3,2,1,0:T(8,128)S(1)}, f32[1,4,1,32,64]{4,3,2,1,0:T(8,128)S(1)}, u32[]{:S(2)}, u32[]{:S(2)}) collective-permute-start(f32[1,4,1,32,64]{4,3,2,1,0:T(8,128)S(1)} %get-tuple-element.104), channel_id=1, source_target_pairs={{0,1},{1,2},{2,3},{4,5},{5,6},{6,7},{8,9},{9,10},{10,11},{12,13},{... | collective-permute-start | bytes 98312 | tf_op jit(solution)/shard_map/ppermute | solution.py:23
  57.2 8.4 %collective-permute-start.9 = (f32[1,4,2,32,64]{4,3,2,1,0:T(8,128)S(1)}, f32[1,4,2,32,64]{4,3,2,1,0:T(8,128)S(1)}, u32[]{:S(2)}, u32[]{:S(2)}) collective-permute-start(f32[1,4,2,32,64]{4,3,2,1,0:T(8,128)S(1)} %fusion.207), channel_id=1, source_target_pairs={{0,4},{4,8},{8,12},{12,16},{16,20},{20,24},{24,28},{28,32},{32,36}... | collective-permute-start | bytes 196616 | tf_op jit(solution)/shard_map/ppermute | solution.py:34
  80.0 228.7 %all-gather.9.cloned.1.call-start = ((), (), s32[]{:S(2)}) async-start(), calls=%async_computation.1 | async-start | bytes 1081344 | tf_op jit(solution)/shard_map/all_gather | solution.py:192
  145.9 7.8 %collective-permute-start.13 = (f32[1,4,1,32,64]{4,3,2,1,0:T(8,128)S(1)}, f32[1,4,1,32,64]{4,3,2,1,0:T(8,128)S(1)}, u32[]{:S(2)}, u32[]{:S(2)}) collective-permute-start(f32[1,4,1,32,64]{4,3,2,1,0:T(8,128)S(1)} %get-tuple-element.99), channel_id=1, source_target_pairs={{1,0},{2,1},{3,2},{5,4},{6,5},{7,6},{9,8},{10,9},{11,10},{13,12},{... | collective-permute-start | bytes 98312 | tf_op jit(solution)/shard_map/ppermute | solution.py:26
  147.2 6.5 %collective-permute-start.14 = (f32[1,4,1,32,64]{4,3,2,1,0:T(8,128)S(1)}, f32[1,4,1,32,64]{4,3,2,1,0:T(8,128)S(1)}, u32[]{:S(2)}, u32[]{:S(2)}) collective-permute-start(f32[1,4,1,32,64]{4,3,2,1,0:T(8,128)S(1)} %get-tuple-element.100), channel_id=1, source_target_pairs={{0,1},{1,2},{2,3},{4,5},{5,6},{6,7},{8,9},{9,10},{10,11},{12,13},{... | collective-permute-start | bytes 98312 | tf_op jit(solution)/shard_map/ppermute | solution.py:23
  151.8 8.4 %collective-permute-start.12 = (f32[1,4,2,32,64]{4,3,2,1,0:T(8,128)S(1)}, f32[1,4,2,32,64]{4,3,2,1,0:T(8,128)S(1)}, u32[]{:S(2)}, u32[]{:S(2)}) collective-permute-start(f32[1,4,2,32,64]{4,3,2,1,0:T(8,128)S(1)} %fusion.221), channel_id=1, source_target_pairs={{0,4},{4,8},{8,12},{12,16},{16,20},{20,24},{24,28},{28,32},{32,36}... | collective-permute-start | bytes 196616 | tf_op jit(solution)/shard_map/ppermute | solution.py:34
  160.8 12.6 %collective-permute-start.15 = (f32[1,4,4,64,128]{4,3,2,1,0:T(8,128)S(1)}, f32[1,4,4,64,128]{4,3,2,1,0:T(8,128)S(1)}, u32[]{:S(2)}, u32[]{:S(2)}) collective-permute-start(f32[1,4,4,64,128]{4,3,2,1,0:T(8,128)S(1)} %add.517), channel_id=1, source_target_pairs={{0,4},{4,8},{8,12},{12,16},{16,20},{20,24},{24,28},{28,32},{32,36}... | collective-permute-start | bytes 1572872 | tf_op jit(solution)/shard_map/ppermute | solution.py:34
  162.7 6.9 %collective-permute-start.16 = (f32[1,4,1,64,128]{4,3,2,1,0:T(8,128)S(1)}, f32[1,4,1,64,128]{4,3,2,1,0:T(8,128)S(1)}, u32[]{:S(2)}, u32[]{:S(2)}) collective-permute-start(f32[1,4,1,64,128]{4,3,2,1,0:T(8,128)S(1)} %get-tuple-element.59), channel_id=1, source_target_pairs={{1,0},{2,1},{3,2},{5,4},{6,5},{7,6},{9,8},{10,9},{11,10},{13,12},{... | collective-permute-start | bytes 393224 | tf_op jit(solution)/shard_map/ppermute | solution.py:26
  164.0 7.1 %collective-permute-start.17 = (f32[1,4,1,64,128]{4,3,2,1,0:T(8,128)S(1)}, f32[1,4,1,64,128]{4,3,2,1,0:T(8,128)S(1)}, u32[]{:S(2)}, u32[]{:S(2)}) collective-permute-start(f32[1,4,1,64,128]{4,3,2,1,0:T(8,128)S(1)} %get-tuple-element.60), channel_id=1, source_target_pairs={{0,1},{1,2},{2,3},{4,5},{5,6},{6,7},{8,9},{9,10},{10,11},{12,13},{... | collective-permute-start | bytes 393224 | tf_op jit(solution)/shard_map/ppermute | solution.py:23
  173.9 12.6 %collective-permute-start.18 = (f32[1,4,4,64,128]{4,3,2,1,0:T(8,128)S(1)}, f32[1,4,4,64,128]{4,3,2,1,0:T(8,128)S(1)}, u32[]{:S(2)}, u32[]{:S(2)}) collective-permute-start(f32[1,4,4,64,128]{4,3,2,1,0:T(8,128)S(1)} %fusion.93), channel_id=1, source_target_pairs={{0,4},{4,8},{8,12},{12,16},{16,20},{20,24},{24,28},{28,32},{32,36}... | collective-permute-start | bytes 1572872 | tf_op jit(solution)/shard_map/ppermute | solution.py:34
  175.9 6.9 %collective-permute-start.19 = (f32[1,4,1,64,128]{4,3,2,1,0:T(8,128)S(1)}, f32[1,4,1,64,128]{4,3,2,1,0:T(8,128)S(1)}, u32[]{:S(2)}, u32[]{:S(2)}) collective-permute-start(f32[1,4,1,64,128]{4,3,2,1,0:T(8,128)S(1)} %get-tuple-element.55), channel_id=1, source_target_pairs={{1,0},{2,1},{3,2},{5,4},{6,5},{7,6},{9,8},{10,9},{11,10},{13,12},{... | collective-permute-start | bytes 393224 | tf_op jit(solution)/shard_map/ppermute | solution.py:26
  177.2 7.1 %collective-permute-start.20 = (f32[1,4,1,64,128]{4,3,2,1,0:T(8,128)S(1)}, f32[1,4,1,64,128]{4,3,2,1,0:T(8,128)S(1)}, u32[]{:S(2)}, u32[]{:S(2)}) collective-permute-start(f32[1,4,1,64,128]{4,3,2,1,0:T(8,128)S(1)} %get-tuple-element.56), channel_id=1, source_target_pairs={{0,1},{1,2},{2,3},{4,5},{5,6},{6,7},{8,9},{9,10},{10,11},{12,13},{... | collective-permute-start | bytes 393224 | tf_op jit(solution)/shard_map/ppermute | solution.py:23
  187.1 12.6 %collective-permute-start.21 = (f32[1,4,4,64,128]{4,3,2,1,0:T(8,128)S(1)}, f32[1,4,4,64,128]{4,3,2,1,0:T(8,128)S(1)}, u32[]{:S(2)}, u32[]{:S(2)}) collective-permute-start(f32[1,4,4,64,128]{4,3,2,1,0:T(8,128)S(1)} %fusion.79), channel_id=1, source_target_pairs={{0,4},{4,8},{8,12},{12,16},{16,20},{20,24},{24,28},{28,32},{32,36}... | collective-permute-start | bytes 1572872 | tf_op jit(solution)/shard_map/ppermute | solution.py:34
  189.0 6.9 %collective-permute-start.22 = (f32[1,4,1,64,128]{4,3,2,1,0:T(8,128)S(1)}, f32[1,4,1,64,128]{4,3,2,1,0:T(8,128)S(1)}, u32[]{:S(2)}, u32[]{:S(2)}) collective-permute-start(f32[1,4,1,64,128]{4,3,2,1,0:T(8,128)S(1)} %get-tuple-element.51), channel_id=1, source_target_pairs={{1,0},{2,1},{3,2},{5,4},{6,5},{7,6},{9,8},{10,9},{11,10},{13,12},{... | collective-permute-start | bytes 393224 | tf_op jit(solution)/shard_map/ppermute | solution.py:26
  190.3 7.1 %collective-permute-start.23 = (f32[1,4,1,64,128]{4,3,2,1,0:T(8,128)S(1)}, f32[1,4,1,64,128]{4,3,2,1,0:T(8,128)S(1)}, u32[]{:S(2)}, u32[]{:S(2)}) collective-permute-start(f32[1,4,1,64,128]{4,3,2,1,0:T(8,128)S(1)} %get-tuple-element.52), channel_id=1, source_target_pairs={{0,1},{1,2},{2,3},{4,5},{5,6},{6,7},{8,9},{9,10},{10,11},{12,13},{... | collective-permute-start | bytes 393224 | tf_op jit(solution)/shard_map/ppermute | solution.py:23
  200.2 12.6 %collective-permute-start.24 = (f32[1,4,4,64,128]{4,3,2,1,0:T(8,128)S(1)}, f32[1,4,4,64,128]{4,3,2,1,0:T(8,128)S(1)}, u32[]{:S(2)}, u32[]{:S(2)}) collective-permute-start(f32[1,4,4,64,128]{4,3,2,1,0:T(8,128)S(1)} %fusion.65), channel_id=1, source_target_pairs={{0,4},{4,8},{8,12},{12,16},{16,20},{20,24},{24,28},{28,32},{32,36}... | collective-permute-start | bytes 1572872 | tf_op jit(solution)/shard_map/ppermute | solution.py:34
  202.2 6.9 %collective-permute-start.25 = (f32[1,4,1,64,128]{4,3,2,1,0:T(8,128)S(1)}, f32[1,4,1,64,128]{4,3,2,1,0:T(8,128)S(1)}, u32[]{:S(2)}, u32[]{:S(2)}) collective-permute-start(f32[1,4,1,64,128]{4,3,2,1,0:T(8,128)S(1)} %get-tuple-element.47), channel_id=1, source_target_pairs={{1,0},{2,1},{3,2},{5,4},{6,5},{7,6},{9,8},{10,9},{11,10},{13,12},{... | collective-permute-start | bytes 393224 | tf_op jit(solution)/shard_map/ppermute | solution.py:26
  203.5 7.1 %collective-permute-start.26 = (f32[1,4,1,64,128]{4,3,2,1,0:T(8,128)S(1)}, f32[1,4,1,64,128]{4,3,2,1,0:T(8,128)S(1)}, u32[]{:S(2)}, u32[]{:S(2)}) collective-permute-start(f32[1,4,1,64,128]{4,3,2,1,0:T(8,128)S(1)} %get-tuple-element.48), channel_id=1, source_target_pairs={{0,1},{1,2},{2,3},{4,5},{5,6},{6,7},{8,9},{9,10},{10,11},{12,13},{... | collective-permute-start | bytes 393224 | tf_op jit(solution)/shard_map/ppermute | solution.py:23
  213.4 12.6 %collective-permute-start.27 = (f32[1,4,4,64,128]{4,3,2,1,0:T(8,128)S(1)}, f32[1,4,4,64,128]{4,3,2,1,0:T(8,128)S(1)}, u32[]{:S(2)}, u32[]{:S(2)}) collective-permute-start(f32[1,4,4,64,128]{4,3,2,1,0:T(8,128)S(1)} %fusion.51), channel_id=1, source_target_pairs={{0,4},{4,8},{8,12},{12,16},{16,20},{20,24},{24,28},{28,32},{32,36}... | collective-permute-start | bytes 1572872 | tf_op jit(solution)/shard_map/ppermute | solution.py:34
  215.4 6.9 %collective-permute-start.28 = (f32[1,4,1,64,128]{4,3,2,1,0:T(8,128)S(1)}, f32[1,4,1,64,128]{4,3,2,1,0:T(8,128)S(1)}, u32[]{:S(2)}, u32[]{:S(2)}) collective-permute-start(f32[1,4,1,64,128]{4,3,2,1,0:T(8,128)S(1)} %get-tuple-element.43), channel_id=1, source_target_pairs={{1,0},{2,1},{3,2},{5,4},{6,5},{7,6},{9,8},{10,9},{11,10},{13,12},{... | collective-permute-start | bytes 393224 | tf_op jit(solution)/shard_map/ppermute | solution.py:26
  216.8 7.1 %collective-permute-start.29 = (f32[1,4,1,64,128]{4,3,2,1,0:T(8,128)S(1)}, f32[1,4,1,64,128]{4,3,2,1,0:T(8,128)S(1)}, u32[]{:S(2)}, u32[]{:S(2)}) collective-permute-start(f32[1,4,1,64,128]{4,3,2,1,0:T(8,128)S(1)} %get-tuple-element.44), channel_id=1, source_target_pairs={{0,1},{1,2},{2,3},{4,5},{5,6},{6,7},{8,9},{9,10},{10,11},{12,13},{... | collective-permute-start | bytes 393224 | tf_op jit(solution)/shard_map/ppermute | solution.py:23
  227.0 7.8 %collective-permute-start.31 = (f32[1,4,1,32,64]{4,3,2,1,0:T(8,128)S(1)}, f32[1,4,1,32,64]{4,3,2,1,0:T(8,128)S(1)}, u32[]{:S(2)}, u32[]{:S(2)}) collective-permute-start(f32[1,4,1,32,64]{4,3,2,1,0:T(8,128)S(1)} %get-tuple-element.95), channel_id=1, source_target_pairs={{1,0},{2,1},{3,2},{5,4},{6,5},{7,6},{9,8},{10,9},{11,10},{13,12},{... | collective-permute-start | bytes 98312 | tf_op jit(solution)/shard_map/ppermute | solution.py:26
  228.3 6.5 %collective-permute-start.32 = (f32[1,4,1,32,64]{4,3,2,1,0:T(8,128)S(1)}, f32[1,4,1,32,64]{4,3,2,1,0:T(8,128)S(1)}, u32[]{:S(2)}, u32[]{:S(2)}) collective-permute-start(f32[1,4,1,32,64]{4,3,2,1,0:T(8,128)S(1)} %get-tuple-element.96), channel_id=1, source_target_pairs={{0,1},{1,2},{2,3},{4,5},{5,6},{6,7},{8,9},{9,10},{10,11},{12,13},{... | collective-permute-start | bytes 98312 | tf_op jit(solution)/shard_map/ppermute | solution.py:23
  232.9 8.4 %collective-permute-start.30 = (f32[1,4,2,32,64]{4,3,2,1,0:T(8,128)S(1)}, f32[1,4,2,32,64]{4,3,2,1,0:T(8,128)S(1)}, u32[]{:S(2)}, u32[]{:S(2)}) collective-permute-start(f32[1,4,2,32,64]{4,3,2,1,0:T(8,128)S(1)} %fusion.389), channel_id=1, source_target_pairs={{0,4},{4,8},{8,12},{12,16},{16,20},{20,24},{24,28},{28,32},{32,36}... | collective-permute-start | bytes 196616 | tf_op jit(solution)/shard_map/ppermute | solution.py:34
  241.4 7.8 %collective-permute-start.34 = (f32[1,4,1,32,64]{4,3,2,1,0:T(8,128)S(1)}, f32[1,4,1,32,64]{4,3,2,1,0:T(8,128)S(1)}, u32[]{:S(2)}, u32[]{:S(2)}) collective-permute-start(f32[1,4,1,32,64]{4,3,2,1,0:T(8,128)S(1)} %get-tuple-element.91), channel_id=1, source_target_pairs={{1,0},{2,1},{3,2},{5,4},{6,5},{7,6},{9,8},{10,9},{11,10},{13,12},{... | collective-permute-start | bytes 98312 | tf_op jit(solution)/shard_map/ppermute | solution.py:26
  242.7 6.5 %collective-permute-start.35 = (f32[1,4,1,32,64]{4,3,2,1,0:T(8,128)S(1)}, f32[1,4,1,32,64]{4,3,2,1,0:T(8,128)S(1)}, u32[]{:S(2)}, u32[]{:S(2)}) collective-permute-start(f32[1,4,1,32,64]{4,3,2,1,0:T(8,128)S(1)} %get-tuple-element.92), channel_id=1, source_target_pairs={{0,1},{1,2},{2,3},{4,5},{5,6},{6,7},{8,9},{9,10},{10,11},{12,13},{... | collective-permute-start | bytes 98312 | tf_op jit(solution)/shard_map/ppermute | solution.py:23
  247.3 8.4 %collective-permute-start.33 = (f32[1,4,2,32,64]{4,3,2,1,0:T(8,128)S(1)}, f32[1,4,2,32,64]{4,3,2,1,0:T(8,128)S(1)}, u32[]{:S(2)}, u32[]{:S(2)}) collective-permute-start(f32[1,4,2,32,64]{4,3,2,1,0:T(8,128)S(1)} %fusion.166), channel_id=1, source_target_pairs={{0,4},{4,8},{8,12},{12,16},{16,20},{20,24},{24,28},{28,32},{32,36}... | collective-permute-start | bytes 196616 | tf_op jit(solution)/shard_map/ppermute | solution.py:34
  330.8 7.8 %collective-permute-start.37 = (f32[1,4,1,32,64]{4,3,2,1,0:T(8,128)S(1)}, f32[1,4,1,32,64]{4,3,2,1,0:T(8,128)S(1)}, u32[]{:S(2)}, u32[]{:S(2)}) collective-permute-start(f32[1,4,1,32,64]{4,3,2,1,0:T(8,128)S(1)} %get-tuple-element.87), channel_id=1, source_target_pairs={{1,0},{2,1},{3,2},{5,4},{6,5},{7,6},{9,8},{10,9},{11,10},{13,12},{... | collective-permute-start | bytes 98312 | tf_op jit(solution)/shard_map/ppermute | solution.py:26
  332.1 6.5 %collective-permute-start.38 = (f32[1,4,1,32,64]{4,3,2,1,0:T(8,128)S(1)}, f32[1,4,1,32,64]{4,3,2,1,0:T(8,128)S(1)}, u32[]{:S(2)}, u32[]{:S(2)}) collective-permute-start(f32[1,4,1,32,64]{4,3,2,1,0:T(8,128)S(1)} %get-tuple-element.88), channel_id=1, source_target_pairs={{0,1},{1,2},{2,3},{4,5},{5,6},{6,7},{8,9},{9,10},{10,11},{12,13},{... | collective-permute-start | bytes 98312 | tf_op jit(solution)/shard_map/ppermute | solution.py:23
  336.7 8.4 %collective-permute-start.36 = (f32[1,4,2,32,64]{4,3,2,1,0:T(8,128)S(1)}, f32[1,4,2,32,64]{4,3,2,1,0:T(8,128)S(1)}, u32[]{:S(2)}, u32[]{:S(2)}) collective-permute-start(f32[1,4,2,32,64]{4,3,2,1,0:T(8,128)S(1)} %fusion.233), channel_id=1, source_target_pairs={{0,4},{4,8},{8,12},{12,16},{16,20},{20,24},{24,28},{28,32},{32,36}... | collective-permute-start | bytes 196616 | tf_op jit(solution)/shard_map/ppermute | solution.py:34
  345.7 12.6 %collective-permute-start.39 = (f32[1,4,4,64,128]{4,3,2,1,0:T(8,128)S(1)}, f32[1,4,4,64,128]{4,3,2,1,0:T(8,128)S(1)}, u32[]{:S(2)}, u32[]{:S(2)}) collective-permute-start(f32[1,4,4,64,128]{4,3,2,1,0:T(8,128)S(1)} %add.567), channel_id=1, source_target_pairs={{0,4},{4,8},{8,12},{12,16},{16,20},{20,24},{24,28},{28,32},{32,36}... | collective-permute-start | bytes 1572872 | tf_op jit(solution)/shard_map/ppermute | solution.py:34
  347.6 6.9 %collective-permute-start.40 = (f32[1,4,1,64,128]{4,3,2,1,0:T(8,128)S(1)}, f32[1,4,1,64,128]{4,3,2,1,0:T(8,128)S(1)}, u32[]{:S(2)}, u32[]{:S(2)}) collective-permute-start(f32[1,4,1,64,128]{4,3,2,1,0:T(8,128)S(1)} %get-tuple-element.39), channel_id=1, source_target_pairs={{1,0},{2,1},{3,2},{5,4},{6,5},{7,6},{9,8},{10,9},{11,10},{13,12},{... | collective-permute-start | bytes 393224 | tf_op jit(solution)/shard_map/ppermute | solution.py:26
  348.9 7.1 %collective-permute-start.41 = (f32[1,4,1,64,128]{4,3,2,1,0:T(8,128)S(1)}, f32[1,4,1,64,128]{4,3,2,1,0:T(8,128)S(1)}, u32[]{:S(2)}, u32[]{:S(2)}) collective-permute-start(f32[1,4,1,64,128]{4,3,2,1,0:T(8,128)S(1)} %get-tuple-element.40), channel_id=1, source_target_pairs={{0,1},{1,2},{2,3},{4,5},{5,6},{6,7},{8,9},{9,10},{10,11},{12,13},{... | collective-permute-start | bytes 393224 | tf_op jit(solution)/shard_map/ppermute | solution.py:23
  358.8 12.6 %collective-permute-start.42 = (f32[1,4,4,64,128]{4,3,2,1,0:T(8,128)S(1)}, f32[1,4,4,64,128]{4,3,2,1,0:T(8,128)S(1)}, u32[]{:S(2)}, u32[]{:S(2)}) collective-permute-start(f32[1,4,4,64,128]{4,3,2,1,0:T(8,128)S(1)} %fusion.25), channel_id=1, source_target_pairs={{0,4},{4,8},{8,12},{12,16},{16,20},{20,24},{24,28},{28,32},{32,36}... | collective-permute-start | bytes 1572872 | tf_op jit(solution)/shard_map/ppermute | solution.py:34
  360.8 6.9 %collective-permute-start.43 = (f32[1,4,1,64,128]{4,3,2,1,0:T(8,128)S(1)}, f32[1,4,1,64,128]{4,3,2,1,0:T(8,128)S(1)}, u32[]{:S(2)}, u32[]{:S(2)}) collective-permute-start(f32[1,4,1,64,128]{4,3,2,1,0:T(8,128)S(1)} %get-tuple-element.35), channel_id=1, source_target_pairs={{1,0},{2,1},{3,2},{5,4},{6,5},{7,6},{9,8},{10,9},{11,10},{13,12},{... | collective-permute-start | bytes 393224 | tf_op jit(solution)/shard_map/ppermute | solution.py:26
  362.1 7.1 %collective-permute-start.44 = (f32[1,4,1,64,128]{4,3,2,1,0:T(8,128)S(1)}, f32[1,4,1,64,128]{4,3,2,1,0:T(8,128)S(1)}, u32[]{:S(2)}, u32[]{:S(2)}) collective-permute-start(f32[1,4,1,64,128]{4,3,2,1,0:T(8,128)S(1)} %get-tuple-element.36), channel_id=1, source_target_pairs={{0,1},{1,2},{2,3},{4,5},{5,6},{6,7},{8,9},{9,10},{10,11},{12,13},{... | collective-permute-start | bytes 393224 | tf_op jit(solution)/shard_map/ppermute | solution.py:23
Sparse Core Ops, SparseCore 0:
  80.2 39.3 all-gather.6
  269.5 39.2 all-gather.8

commit v8 on v7

--- a/solution.py
+++ b/solution.py
@@ -188,8 +188,9 @@
 
 
 def gather_all(flat):
-    within = lax.all_gather(flat, "space", axis=0, tiled=True)
-    return lax.all_gather(within, "tm", axis=0, tiled=True)
+    across = lax.all_gather(flat, "tm", axis=0, tiled=True)
+    whole = lax.all_gather(across, "space", axis=1, tiled=True)
+    return whole.reshape(-1, flat.shape[1])
 
 
 def coarse_correction(source, metric_two, gathered):

time: 381 us -> 373 us (0.979)
  waiting for transfers between devices: 158 us -> 128 us
  blocking collectives: 25.5 us -> 46.5 us
    all_gather x2, waiting for transfers between devices: 78.8 us -> 49.2 us  [gather_all(): whole = lax.all_gather(across, 'space', axis=1, tiled=True)]
    all_gather x2, blocking collectives: 25.5 us -> 46.5 us  [gather_all(): across = lax.all_gather(flat, 'tm', axis=0, tiled=True)]
where the time goes in v8:
time: 373 us; the launch traced here: 371 us
  waiting for transfers between devices  128 us (34%)
  starting transfers between devices  117 us (31%)
  blocking collectives  46.5 us (12%)
  Pallas kernels  33.1 us (9%)
  local copies, waits for them, and re-layouts  17.3 us (5%)
  between operations  14.6 us (4%)
  other arithmetic  12.6 us (3%)
    ppermute x15, starting transfers between devices, with_halo(): lax.ppermute(lax.slice_in_dim(block, block.shape[dim] - width, None, axis...  68.5 us
    ppermute x15, waiting for transfers between devices, from_behind(): return lax.ppermute(array, axis, pairs)  54.8 us
    all_gather x2, waiting for transfers between devices, gather_all(): whole = lax.all_gather(across, 'space', axis=1, tiled=True)  49.2 us
    all_gather x2, blocking collectives, gather_all(): across = lax.all_gather(flat, 'tm', axis=0, tiled=True)  46.5 us
    pallas_call x2, Pallas kernels, coarse_solve(): pl.pallas_call(kernel, out_shape=jax.ShapeDtypeStruct(flat_source.shape,...  33.1 us
    ppermute x15, starting transfers between devices, from_behind(): return lax.ppermute(array, axis, pairs)  28.9 us
    ppermute x15, starting transfers between devices, with_halo(): lax.ppermute(lax.slice_in_dim(block, 0, width, axis=dim), axis, backward)  19.4 us
    ppermute x15, waiting for transfers between devices, with_halo(): lax.ppermute(lax.slice_in_dim(block, block.shape[dim] - width, None, axis...  13.7 us
  transfers between devices with their start and end apart: 47, of which 35 were waited for; matrix products, arithmetic and copies ran while one was open for 1% of the time, Pallas kernels for 0%

profile of v8, /device:TPU:2, one launch (start us, length us, event | category | flops | bytes accessed | tf_op | source)
XLA Modules:
  0.0 371.3 jit_solution(5980680469242040398)
XLA Ops:
  9.8 2.1 collective-permute-start
  13.2 4.6 %collective-permute-start.2 = (f32[1,4,1,64,128]{4,3,2,1,0:T(8,128)S(1)}, f32[1,4,1,64,128]{4,3,2,1,0:T(8,128)S(1)}, u32[]{:S(2)}, u32[]{:S(2)}) collective-permute-start(f32[1,4,1,64,128]{4,3,2,1,0:T(8,128)S(1)} %get-tuple-element.68), channel_id=1, source_target_pairs={{0,1},{1,2},{2,3},{4,5},{5,6},{6,7},{8,9},{9,10},{10,11},{12,13},{... | collective-permute-start | bytes 393224 | tf_op jit(solution)/shard_map/ppermute | solution.py:23
  19.2 1.7 collective-permute-done.2
  21.2 1.3 collective-permute-done
  23.1 1.9 collective-permute-start.3
  26.3 4.6 %collective-permute-start.5 = (f32[1,4,1,64,128]{4,3,2,1,0:T(8,128)S(1)}, f32[1,4,1,64,128]{4,3,2,1,0:T(8,128)S(1)}, u32[]{:S(2)}, u32[]{:S(2)}) collective-permute-start(f32[1,4,1,64,128]{4,3,2,1,0:T(8,128)S(1)} %get-tuple-element.64), channel_id=1, source_target_pairs={{0,1},{1,2},{2,3},{4,5},{5,6},{6,7},{8,9},{9,10},{10,11},{12,13},{... | collective-permute-start | bytes 393224 | tf_op jit(solution)/shard_map/ppermute | solution.py:23
  30.9 2.2 collective-permute-done.4
  33.1 1.5 collective-permute-done.5
  38.0 4.5 %collective-permute-start.8 = (f32[1,4,1,32,64]{4,3,2,1,0:T(8,128)S(1)}, f32[1,4,1,32,64]{4,3,2,1,0:T(8,128)S(1)}, u32[]{:S(2)}, u32[]{:S(2)}) collective-permute-start(f32[1,4,1,32,64]{4,3,2,1,0:T(8,128)S(1)} %get-tuple-element.108), channel_id=1, source_target_pairs={{0,1},{1,2},{2,3},{4,5},{5,6},{6,7},{8,9},{9,10},{10,11},{12,13},{... | collective-permute-start | bytes 98312 | tf_op jit(solution)/shard_map/ppermute | solution.py:23
  42.6 1.9 collective-permute-start.6
  44.6 6.3 %collective-permute-done.6 = f32[1,4,2,32,64]{4,3,2,1,0:T(8,128)S(1)} collective-permute-done((f32[1,4,2,32,64]{4,3,2,1,0:T(8,128)S(1)}, f32[1,4,2,32,64]{4,3,2,1,0:T(8,128)S(1)}, u32[]{:S(2)}, u32[]{:S(2)}) %collective-permute-start.6) | collective-permute-done | bytes 65568 | tf_op jit(solution)/shard_map/ppermute | solution.py:34
  52.4 4.5 %collective-permute-start.11 = (f32[1,4,1,32,64]{4,3,2,1,0:T(8,128)S(1)}, f32[1,4,1,32,64]{4,3,2,1,0:T(8,128)S(1)}, u32[]{:S(2)}, u32[]{:S(2)}) collective-permute-start(f32[1,4,1,32,64]{4,3,2,1,0:T(8,128)S(1)} %get-tuple-element.104), channel_id=1, source_target_pairs={{0,1},{1,2},{2,3},{4,5},{5,6},{6,7},{8,9},{9,10},{10,11},{12,13},{... | collective-permute-start | bytes 98312 | tf_op jit(solution)/shard_map/ppermute | solution.py:23
  57.2 1.9 collective-permute-start.9
  59.3 6.3 %collective-permute-done.9 = f32[1,4,2,32,64]{4,3,2,1,0:T(8,128)S(1)} collective-permute-done((f32[1,4,2,32,64]{4,3,2,1,0:T(8,128)S(1)}, f32[1,4,2,32,64]{4,3,2,1,0:T(8,128)S(1)}, u32[]{:S(2)}, u32[]{:S(2)}) %collective-permute-start.9) | collective-permute-done | bytes 65568 | tf_op jit(solution)/shard_map/ppermute | solution.py:34
  66.3 23.3 %all-gather = f32[32,1,2560]{2,1,0:T(1,128)S(1)} all-gather(f32[1,1,2560]{2,1,0:T(1,128)S(1)} %maximum_bitcast_fusion), channel_id=1, replica_groups=mesh['tm'=32,'space'=4] {'tm'}, dimensions={0}, use_global_device_ids=true | all-gather | bytes 337920 | tf_op jit(solution)/shard_map/all_gather | solution.py:191
  90.4 25.6 %all-gather.5.cloned.1.call-done = f32[32,10240]{1,0:T(8,128)} async-done(((f32[32,2560]{1,0:T(8,128)}), f32[32,10240]{1,0:T(8,128)}) %all-gather.5.cloned.1.call-update) | async-done | bytes 1310736 | tf_op jit(solution)/shard_map/all_gather | solution.py:192
  116.0 1.7 reshape.859
  118.7 2.5 reshape_transpose_reshape.7.src_ref
  122.9 16.5 %shard_map.37 = f32[32,16,512]{2,1,0:T(8,128)} custom-call(f32[32,16,512]{2,1,0:T(8,128)} %reshape_transpose_reshape.7.src_ref, f32[32,16,512]{2,1,0:T(8,128)} %reshape.860.met_ref), custom_call_target="tpu_custom_call" | custom-call | tf_op jit(solution)/shard_map/pallas_call | solution.py:161
  143.6 4.5 %collective-permute-start.14 = (f32[1,4,1,32,64]{4,3,2,1,0:T(8,128)S(1)}, f32[1,4,1,32,64]{4,3,2,1,0:T(8,128)S(1)}, u32[]{:S(2)}, u32[]{:S(2)}) collective-permute-start(f32[1,4,1,32,64]{4,3,2,1,0:T(8,128)S(1)} %get-tuple-element.100), channel_id=1, source_target_pairs={{0,1},{1,2},{2,3},{4,5},{5,6},{6,7},{8,9},{9,10},{10,11},{12,13},{... | collective-permute-start | bytes 98312 | tf_op jit(solution)/shard_map/ppermute | solution.py:23
  148.2 1.9 collective-permute-start.12
  150.2 6.3 %collective-permute-done.12 = f32[1,4,2,32,64]{4,3,2,1,0:T(8,128)S(1)} collective-permute-done((f32[1,4,2,32,64]{4,3,2,1,0:T(8,128)S(1)}, f32[1,4,2,32,64]{4,3,2,1,0:T(8,128)S(1)}, u32[]{:S(2)}, u32[]{:S(2)}) %collective-permute-start.12) | collective-permute-done | bytes 65568 | tf_op jit(solution)/shard_map/ppermute | solution.py:34
  157.1 1.9 collective-permute-start.15
  160.4 4.6 %collective-permute-start.17 = (f32[1,4,1,64,128]{4,3,2,1,0:T(8,128)S(1)}, f32[1,4,1,64,128]{4,3,2,1,0:T(8,128)S(1)}, u32[]{:S(2)}, u32[]{:S(2)}) collective-permute-start(f32[1,4,1,64,128]{4,3,2,1,0:T(8,128)S(1)} %get-tuple-element.60), channel_id=1, source_target_pairs={{0,1},{1,2},{2,3},{4,5},{5,6},{6,7},{8,9},{9,10},{10,11},{12,13},{... | collective-permute-start | bytes 393224 | tf_op jit(solution)/shard_map/ppermute | solution.py:23
  165.9 1.5 collective-permute-done.17
  167.6 2.1 collective-permute-done.15
  170.3 1.9 collective-permute-start.18
  173.5 4.6 %collective-permute-start.20 = (f32[1,4,1,64,128]{4,3,2,1,0:T(8,128)S(1)}, f32[1,4,1,64,128]{4,3,2,1,0:T(8,128)S(1)}, u32[]{:S(2)}, u32[]{:S(2)}) collective-permute-start(f32[1,4,1,64,128]{4,3,2,1,0:T(8,128)S(1)} %get-tuple-element.56), channel_id=1, source_target_pairs={{0,1},{1,2},{2,3},{4,5},{5,6},{6,7},{8,9},{9,10},{10,11},{12,13},{... | collective-permute-start | bytes 393224 | tf_op jit(solution)/shard_map/ppermute | solution.py:23
  179.1 1.5 collective-permute-done.20
  180.8 2.1 collective-permute-done.18
  183.4 1.9 collective-permute-start.21
  186.7 4.7 %collective-permute-start.23 = (f32[1,4,1,64,128]{4,3,2,1,0:T(8,128)S(1)}, f32[1,4,1,64,128]{4,3,2,1,0:T(8,128)S(1)}, u32[]{:S(2)}, u32[]{:S(2)}) collective-permute-start(f32[1,4,1,64,128]{4,3,2,1,0:T(8,128)S(1)} %get-tuple-element.52), channel_id=1, source_target_pairs={{0,1},{1,2},{2,3},{4,5},{5,6},{6,7},{8,9},{9,10},{10,11},{12,13},{... | collective-permute-start | bytes 393224 | tf_op jit(solution)/shard_map/ppermute | solution.py:23
  192.3 1.5 collective-permute-done.23
  194.0 2.1 collective-permute-done.21
  196.6 1.9 collective-permute-start.24
  199.9 4.6 %collective-permute-start.26 = (f32[1,4,1,64,128]{4,3,2,1,0:T(8,128)S(1)}, f32[1,4,1,64,128]{4,3,2,1,0:T(8,128)S(1)}, u32[]{:S(2)}, u32[]{:S(2)}) collective-permute-start(f32[1,4,1,64,128]{4,3,2,1,0:T(8,128)S(1)} %get-tuple-element.48), channel_id=1, source_target_pairs={{0,1},{1,2},{2,3},{4,5},{5,6},{6,7},{8,9},{9,10},{10,11},{12,13},{... | collective-permute-start | bytes 393224 | tf_op jit(solution)/shard_map/ppermute | solution.py:23
  205.4 1.5 collective-permute-done.26
  207.1 2.1 collective-permute-done.24
  209.8 1.9 collective-permute-start.27
  213.0 4.6 %collective-permute-start.29 = (f32[1,4,1,64,128]{4,3,2,1,0:T(8,128)S(1)}, f32[1,4,1,64,128]{4,3,2,1,0:T(8,128)S(1)}, u32[]{:S(2)}, u32[]{:S(2)}) collective-permute-start(f32[1,4,1,64,128]{4,3,2,1,0:T(8,128)S(1)} %get-tuple-element.44), channel_id=1, source_target_pairs={{0,1},{1,2},{2,3},{4,5},{5,6},{6,7},{8,9},{9,10},{10,11},{12,13},{... | collective-permute-start | bytes 393224 | tf_op jit(solution)/shard_map/ppermute | solution.py:23
  218.6 1.5 collective-permute-done.29
  220.3 2.1 collective-permute-done.27
  224.7 4.5 %collective-permute-start.32 = (f32[1,4,1,32,64]{4,3,2,1,0:T(8,128)S(1)}, f32[1,4,1,32,64]{4,3,2,1,0:T(8,128)S(1)}, u32[]{:S(2)}, u32[]{:S(2)}) collective-permute-start(f32[1,4,1,32,64]{4,3,2,1,0:T(8,128)S(1)} %get-tuple-element.96), channel_id=1, source_target_pairs={{0,1},{1,2},{2,3},{4,5},{5,6},{6,7},{8,9},{9,10},{10,11},{12,13},{... | collective-permute-start | bytes 98312 | tf_op jit(solution)/shard_map/ppermute | solution.py:23
  229.2 1.9 collective-permute-start.30
  231.3 6.3 %collective-permute-done.30 = f32[1,4,2,32,64]{4,3,2,1,0:T(8,128)S(1)} collective-permute-done((f32[1,4,2,32,64]{4,3,2,1,0:T(8,128)S(1)}, f32[1,4,2,32,64]{4,3,2,1,0:T(8,128)S(1)}, u32[]{:S(2)}, u32[]{:S(2)}) %collective-permute-start.30) | collective-permute-done | bytes 65568 | tf_op jit(solution)/shard_map/ppermute | solution.py:34
  239.1 4.5 %collective-permute-start.35 = (f32[1,4,1,32,64]{4,3,2,1,0:T(8,128)S(1)}, f32[1,4,1,32,64]{4,3,2,1,0:T(8,128)S(1)}, u32[]{:S(2)}, u32[]{:S(2)}) collective-permute-start(f32[1,4,1,32,64]{4,3,2,1,0:T(8,128)S(1)} %get-tuple-element.92), channel_id=1, source_target_pairs={{0,1},{1,2},{2,3},{4,5},{5,6},{6,7},{8,9},{9,10},{10,11},{12,13},{... | collective-permute-start | bytes 98312 | tf_op jit(solution)/shard_map/ppermute | solution.py:23
  243.7 1.9 collective-permute-start.33
  245.7 6.3 %collective-permute-done.33 = f32[1,4,2,32,64]{4,3,2,1,0:T(8,128)S(1)} collective-permute-done((f32[1,4,2,32,64]{4,3,2,1,0:T(8,128)S(1)}, f32[1,4,2,32,64]{4,3,2,1,0:T(8,128)S(1)}, u32[]{:S(2)}, u32[]{:S(2)}) %collective-permute-start.33) | collective-permute-done | bytes 65568 | tf_op jit(solution)/shard_map/ppermute | solution.py:34
  252.7 23.3 %all-gather.1 = f32[32,1,2048]{2,1,0:T(1,128)S(1)} all-gather(f32[1,1,2048]{2,1,0:T(1,128)S(1)} %reshape.880), channel_id=1, replica_groups=mesh['tm'=32,'space'=4] {'tm'}, dimensions={0}, use_global_device_ids=true | all-gather | bytes 270336 | tf_op jit(solution)/shard_map/all_gather | solution.py:191
  276.8 23.6 %all-gather.7.cloned.1.call-done = f32[32,8192]{1,0:T(8,128)} async-done(((f32[32,2048]{1,0:T(8,128)}), f32[32,8192]{1,0:T(8,128)}) %all-gather.7.cloned.1.call-update) | async-done | bytes 1048592 | tf_op jit(solution)/shard_map/all_gather | solution.py:192
  300.4 2.8 copy.22
  303.2 16.5 %shard_map.38 = f32[32,16,512]{2,1,0:T(8,128)} custom-call(f32[32,16,512]{2,1,0:T(8,128)} %bitcast.114, f32[32,16,512]{2,1,0:T(8,128)} %reshape.860.met_ref), custom_call_target="tpu_custom_call" | custom-call | tf_op jit(solution)/shard_map/pallas_call | solution.py:161
  323.9 4.5 %collective-permute-start.38 = (f32[1,4,1,32,64]{4,3,2,1,0:T(8,128)S(1)}, f32[1,4,1,32,64]{4,3,2,1,0:T(8,128)S(1)}, u32[]{:S(2)}, u32[]{:S(2)}) collective-permute-start(f32[1,4,1,32,64]{4,3,2,1,0:T(8,128)S(1)} %get-tuple-element.88), channel_id=1, source_target_pairs={{0,1},{1,2},{2,3},{4,5},{5,6},{6,7},{8,9},{9,10},{10,11},{12,13},{... | collective-permute-start | bytes 98312 | tf_op jit(solution)/shard_map/ppermute | solution.py:23
  328.4 1.9 collective-permute-start.36
  330.5 6.3 %collective-permute-done.36 = f32[1,4,2,32,64]{4,3,2,1,0:T(8,128)S(1)} collective-permute-done((f32[1,4,2,32,64]{4,3,2,1,0:T(8,128)S(1)}, f32[1,4,2,32,64]{4,3,2,1,0:T(8,128)S(1)}, u32[]{:S(2)}, u32[]{:S(2)}) %collective-permute-start.36) | collective-permute-done | bytes 65568 | tf_op jit(solution)/shard_map/ppermute | solution.py:34
  337.4 1.9 collective-permute-start.39
  340.6 4.6 %collective-permute-start.41 = (f32[1,4,1,64,128]{4,3,2,1,0:T(8,128)S(1)}, f32[1,4,1,64,128]{4,3,2,1,0:T(8,128)S(1)}, u32[]{:S(2)}, u32[]{:S(2)}) collective-permute-start(f32[1,4,1,64,128]{4,3,2,1,0:T(8,128)S(1)} %get-tuple-element.40), channel_id=1, source_target_pairs={{0,1},{1,2},{2,3},{4,5},{5,6},{6,7},{8,9},{9,10},{10,11},{12,13},{... | collective-permute-start | bytes 393224 | tf_op jit(solution)/shard_map/ppermute | solution.py:23
  346.2 1.5 collective-permute-done.41
  347.9 2.1 collective-permute-done.39
  350.6 1.9 collective-permute-start.42
  353.8 4.6 %collective-permute-start.44 = (f32[1,4,1,64,128]{4,3,2,1,0:T(8,128)S(1)}, f32[1,4,1,64,128]{4,3,2,1,0:T(8,128)S(1)}, u32[]{:S(2)}, u32[]{:S(2)}) collective-permute-start(f32[1,4,1,64,128]{4,3,2,1,0:T(8,128)S(1)} %get-tuple-element.36), channel_id=1, source_target_pairs={{0,1},{1,2},{2,3},{4,5},{5,6},{6,7},{8,9},{9,10},{10,11},{12,13},{... | collective-permute-start | bytes 393224 | tf_op jit(solution)/shard_map/ppermute | solution.py:23
  359.4 1.5 collective-permute-done.44
  361.1 2.1 collective-permute-done.42
  363.2 1.3 fusion.11
  (164 shorter events, 52.2 us)
Async XLA Ops:
  6.5 109.4 %all-gather.5.cloned.1.call-start = ((), (), s32[]{:S(2)}) async-start(), calls=%async_computation | async-start | bytes 1638400 | tf_op jit(solution)/shard_map/all_gather | solution.py:192
  7.5 10.2 %copy-start.1 = (f32[1,4,64,128]{3,2,1,0:T(8,128)S(1)}, f32[1,4,64,128]{3,2,1,0:T(8,128)}, u32[]{:S(2)}) copy-start(f32[1,4,64,128]{3,2,1,0:T(8,128)} %param.4) | copy-start | bytes 393220
  9.8 12.8 %copy-start = (f32[1,4,4,64,128]{4,3,2,1,0:T(8,128)S(1)}, f32[1,4,4,64,128]{4,3,2,1,0:T(8,128)}, u32[]{:S(2)}) copy-start(f32[1,4,4,64,128]{4,3,2,1,0:T(8,128)} %param.3) | copy-start | bytes 1572868
  9.8 12.7 %collective-permute-start = (f32[1,4,4,64,128]{4,3,2,1,0:T(8,128)S(1)}, f32[1,4,4,64,128]{4,3,2,1,0:T(8,128)S(1)}, u32[]{:S(2)}, u32[]{:S(2)}) collective-permute-start(f32[1,4,4,64,128]{4,3,2,1,0:T(8,128)S(1)} %get-tuple-element.9), channel_id=1, source_target_pairs={{0,4},{4,8},{8,12},{12,16},{16,20},{20,24},{24,28},{28,32},{32,36}... | collective-permute-start | bytes 1572872 | tf_op jit(solution)/shard_map/ppermute | solution.py:34
  11.9 7.4 %collective-permute-start.1 = (f32[1,4,1,64,128]{4,3,2,1,0:T(8,128)S(1)}, f32[1,4,1,64,128]{4,3,2,1,0:T(8,128)S(1)}, u32[]{:S(2)}, u32[]{:S(2)}) collective-permute-start(f32[1,4,1,64,128]{4,3,2,1,0:T(8,128)S(1)} %get-tuple-element.67), channel_id=1, source_target_pairs={{1,0},{2,1},{3,2},{5,4},{6,5},{7,6},{9,8},{10,9},{11,10},{13,12},{... | collective-permute-start | bytes 393224 | tf_op jit(solution)/shard_map/ppermute | solution.py:26
  13.2 7.8 %collective-permute-start.2 = (f32[1,4,1,64,128]{4,3,2,1,0:T(8,128)S(1)}, f32[1,4,1,64,128]{4,3,2,1,0:T(8,128)S(1)}, u32[]{:S(2)}, u32[]{:S(2)}) collective-permute-start(f32[1,4,1,64,128]{4,3,2,1,0:T(8,128)S(1)} %get-tuple-element.68), channel_id=1, source_target_pairs={{0,1},{1,2},{2,3},{4,5},{5,6},{6,7},{8,9},{9,10},{10,11},{12,13},{... | collective-permute-start | bytes 393224 | tf_op jit(solution)/shard_map/ppermute | solution.py:23
  23.1 12.6 %collective-permute-start.3 = (f32[1,4,4,64,128]{4,3,2,1,0:T(8,128)S(1)}, f32[1,4,4,64,128]{4,3,2,1,0:T(8,128)S(1)}, u32[]{:S(2)}, u32[]{:S(2)}) collective-permute-start(f32[1,4,4,64,128]{4,3,2,1,0:T(8,128)S(1)} %fusion.119), channel_id=1, source_target_pairs={{0,4},{4,8},{8,12},{12,16},{16,20},{20,24},{24,28},{28,32},{32,36}... | collective-permute-start | bytes 1572872 | tf_op jit(solution)/shard_map/ppermute | solution.py:34
  25.0 8.1 %collective-permute-start.4 = (f32[1,4,1,64,128]{4,3,2,1,0:T(8,128)S(1)}, f32[1,4,1,64,128]{4,3,2,1,0:T(8,128)S(1)}, u32[]{:S(2)}, u32[]{:S(2)}) collective-permute-start(f32[1,4,1,64,128]{4,3,2,1,0:T(8,128)S(1)} %get-tuple-element.63), channel_id=1, source_target_pairs={{1,0},{2,1},{3,2},{5,4},{6,5},{7,6},{9,8},{10,9},{11,10},{13,12},{... | collective-permute-start | bytes 393224 | tf_op jit(solution)/shard_map/ppermute | solution.py:26
  26.3 8.3 %collective-permute-start.5 = (f32[1,4,1,64,128]{4,3,2,1,0:T(8,128)S(1)}, f32[1,4,1,64,128]{4,3,2,1,0:T(8,128)S(1)}, u32[]{:S(2)}, u32[]{:S(2)}) collective-permute-start(f32[1,4,1,64,128]{4,3,2,1,0:T(8,128)S(1)} %get-tuple-element.64), channel_id=1, source_target_pairs={{0,1},{1,2},{2,3},{4,5},{5,6},{6,7},{8,9},{9,10},{10,11},{12,13},{... | collective-permute-start | bytes 393224 | tf_op jit(solution)/shard_map/ppermute | solution.py:23
  36.7 7.8 %collective-permute-start.7 = (f32[1,4,1,32,64]{4,3,2,1,0:T(8,128)S(1)}, f32[1,4,1,32,64]{4,3,2,1,0:T(8,128)S(1)}, u32[]{:S(2)}, u32[]{:S(2)}) collective-permute-start(f32[1,4,1,32,64]{4,3,2,1,0:T(8,128)S(1)} %get-tuple-element.107), channel_id=1, source_target_pairs={{1,0},{2,1},{3,2},{5,4},{6,5},{7,6},{9,8},{10,9},{11,10},{13,12},{... | collective-permute-start | bytes 98312 | tf_op jit(solution)/shard_map/ppermute | solution.py:26
  38.0 6.5 %collective-permute-start.8 = (f32[1,4,1,32,64]{4,3,2,1,0:T(8,128)S(1)}, f32[1,4,1,32,64]{4,3,2,1,0:T(8,128)S(1)}, u32[]{:S(2)}, u32[]{:S(2)}) collective-permute-start(f32[1,4,1,32,64]{4,3,2,1,0:T(8,128)S(1)} %get-tuple-element.108), channel_id=1, source_target_pairs={{0,1},{1,2},{2,3},{4,5},{5,6},{6,7},{8,9},{9,10},{10,11},{12,13},{... | collective-permute-start | bytes 98312 | tf_op jit(solution)/shard_map/ppermute | solution.py:23
  42.6 8.4 %collective-permute-start.6 = (f32[1,4,2,32,64]{4,3,2,1,0:T(8,128)S(1)}, f32[1,4,2,32,64]{4,3,2,1,0:T(8,128)S(1)}, u32[]{:S(2)}, u32[]{:S(2)}) collective-permute-start(f32[1,4,2,32,64]{4,3,2,1,0:T(8,128)S(1)} %fusion.388), channel_id=1, source_target_pairs={{0,4},{4,8},{8,12},{12,16},{16,20},{20,24},{24,28},{28,32},{32,36}... | collective-permute-start | bytes 196616 | tf_op jit(solution)/shard_map/ppermute | solution.py:34
  51.1 8.0 %collective-permute-start.10 = (f32[1,4,1,32,64]{4,3,2,1,0:T(8,128)S(1)}, f32[1,4,1,32,64]{4,3,2,1,0:T(8,128)S(1)}, u32[]{:S(2)}, u32[]{:S(2)}) collective-permute-start(f32[1,4,1,32,64]{4,3,2,1,0:T(8,128)S(1)} %get-tuple-element.103), channel_id=1, source_target_pairs={{1,0},{2,1},{3,2},{5,4},{6,5},{7,6},{9,8},{10,9},{11,10},{13,12},{... | collective-permute-start | bytes 98312 | tf_op jit(solution)/shard_map/ppermute | solution.py:26
  52.4 6.7 %collective-permute-start.11 = (f32[1,4,1,32,64]{4,3,2,1,0:T(8,128)S(1)}, f32[1,4,1,32,64]{4,3,2,1,0:T(8,128)S(1)}, u32[]{:S(2)}, u32[]{:S(2)}) collective-permute-start(f32[1,4,1,32,64]{4,3,2,1,0:T(8,128)S(1)} %get-tuple-element.104), channel_id=1, source_target_pairs={{0,1},{1,2},{2,3},{4,5},{5,6},{6,7},{8,9},{9,10},{10,11},{12,13},{... | collective-permute-start | bytes 98312 | tf_op jit(solution)/shard_map/ppermute | solution.py:23
  57.2 8.4 %collective-permute-start.9 = (f32[1,4,2,32,64]{4,3,2,1,0:T(8,128)S(1)}, f32[1,4,2,32,64]{4,3,2,1,0:T(8,128)S(1)}, u32[]{:S(2)}, u32[]{:S(2)}) collective-permute-start(f32[1,4,2,32,64]{4,3,2,1,0:T(8,128)S(1)} %fusion.207), channel_id=1, source_target_pairs={{0,4},{4,8},{8,12},{12,16},{16,20},{20,24},{24,28},{28,32},{32,36}... | collective-permute-start | bytes 196616 | tf_op jit(solution)/shard_map/ppermute | solution.py:34
  90.3 210.1 %all-gather.7.cloned.1.call-start = ((), (), s32[]{:S(2)}) async-start(), calls=%async_computation.1 | async-start | bytes 1310720 | tf_op jit(solution)/shard_map/all_gather | solution.py:192
  142.3 7.8 %collective-permute-start.13 = (f32[1,4,1,32,64]{4,3,2,1,0:T(8,128)S(1)}, f32[1,4,1,32,64]{4,3,2,1,0:T(8,128)S(1)}, u32[]{:S(2)}, u32[]{:S(2)}) collective-permute-start(f32[1,4,1,32,64]{4,3,2,1,0:T(8,128)S(1)} %get-tuple-element.99), channel_id=1, source_target_pairs={{1,0},{2,1},{3,2},{5,4},{6,5},{7,6},{9,8},{10,9},{11,10},{13,12},{... | collective-permute-start | bytes 98312 | tf_op jit(solution)/shard_map/ppermute | solution.py:26
  143.6 6.5 %collective-permute-start.14 = (f32[1,4,1,32,64]{4,3,2,1,0:T(8,128)S(1)}, f32[1,4,1,32,64]{4,3,2,1,0:T(8,128)S(1)}, u32[]{:S(2)}, u32[]{:S(2)}) collective-permute-start(f32[1,4,1,32,64]{4,3,2,1,0:T(8,128)S(1)} %get-tuple-element.100), channel_id=1, source_target_pairs={{0,1},{1,2},{2,3},{4,5},{5,6},{6,7},{8,9},{9,10},{10,11},{12,13},{... | collective-permute-start | bytes 98312 | tf_op jit(solution)/shard_map/ppermute | solution.py:23
  148.2 8.4 %collective-permute-start.12 = (f32[1,4,2,32,64]{4,3,2,1,0:T(8,128)S(1)}, f32[1,4,2,32,64]{4,3,2,1,0:T(8,128)S(1)}, u32[]{:S(2)}, u32[]{:S(2)}) collective-permute-start(f32[1,4,2,32,64]{4,3,2,1,0:T(8,128)S(1)} %fusion.221), channel_id=1, source_target_pairs={{0,4},{4,8},{8,12},{12,16},{16,20},{20,24},{24,28},{28,32},{32,36}... | collective-permute-start | bytes 196616 | tf_op jit(solution)/shard_map/ppermute | solution.py:34
  157.1 12.6 %collective-permute-start.15 = (f32[1,4,4,64,128]{4,3,2,1,0:T(8,128)S(1)}, f32[1,4,4,64,128]{4,3,2,1,0:T(8,128)S(1)}, u32[]{:S(2)}, u32[]{:S(2)}) collective-permute-start(f32[1,4,4,64,128]{4,3,2,1,0:T(8,128)S(1)} %add.517), channel_id=1, source_target_pairs={{0,4},{4,8},{8,12},{12,16},{16,20},{20,24},{24,28},{28,32},{32,36}... | collective-permute-start | bytes 1572872 | tf_op jit(solution)/shard_map/ppermute | solution.py:34
  159.1 6.9 %collective-permute-start.16 = (f32[1,4,1,64,128]{4,3,2,1,0:T(8,128)S(1)}, f32[1,4,1,64,128]{4,3,2,1,0:T(8,128)S(1)}, u32[]{:S(2)}, u32[]{:S(2)}) collective-permute-start(f32[1,4,1,64,128]{4,3,2,1,0:T(8,128)S(1)} %get-tuple-element.59), channel_id=1, source_target_pairs={{1,0},{2,1},{3,2},{5,4},{6,5},{7,6},{9,8},{10,9},{11,10},{13,12},{... | collective-permute-start | bytes 393224 | tf_op jit(solution)/shard_map/ppermute | solution.py:26
  160.4 7.1 %collective-permute-start.17 = (f32[1,4,1,64,128]{4,3,2,1,0:T(8,128)S(1)}, f32[1,4,1,64,128]{4,3,2,1,0:T(8,128)S(1)}, u32[]{:S(2)}, u32[]{:S(2)}) collective-permute-start(f32[1,4,1,64,128]{4,3,2,1,0:T(8,128)S(1)} %get-tuple-element.60), channel_id=1, source_target_pairs={{0,1},{1,2},{2,3},{4,5},{5,6},{6,7},{8,9},{9,10},{10,11},{12,13},{... | collective-permute-start | bytes 393224 | tf_op jit(solution)/shard_map/ppermute | solution.py:23
  170.3 12.6 %collective-permute-start.18 = (f32[1,4,4,64,128]{4,3,2,1,0:T(8,128)S(1)}, f32[1,4,4,64,128]{4,3,2,1,0:T(8,128)S(1)}, u32[]{:S(2)}, u32[]{:S(2)}) collective-permute-start(f32[1,4,4,64,128]{4,3,2,1,0:T(8,128)S(1)} %fusion.93), channel_id=1, source_target_pairs={{0,4},{4,8},{8,12},{12,16},{16,20},{20,24},{24,28},{28,32},{32,36}... | collective-permute-start | bytes 1572872 | tf_op jit(solution)/shard_map/ppermute | solution.py:34
  172.2 6.9 %collective-permute-start.19 = (f32[1,4,1,64,128]{4,3,2,1,0:T(8,128)S(1)}, f32[1,4,1,64,128]{4,3,2,1,0:T(8,128)S(1)}, u32[]{:S(2)}, u32[]{:S(2)}) collective-permute-start(f32[1,4,1,64,128]{4,3,2,1,0:T(8,128)S(1)} %get-tuple-element.55), channel_id=1, source_target_pairs={{1,0},{2,1},{3,2},{5,4},{6,5},{7,6},{9,8},{10,9},{11,10},{13,12},{... | collective-permute-start | bytes 393224 | tf_op jit(solution)/shard_map/ppermute | solution.py:26
  173.5 7.1 %collective-permute-start.20 = (f32[1,4,1,64,128]{4,3,2,1,0:T(8,128)S(1)}, f32[1,4,1,64,128]{4,3,2,1,0:T(8,128)S(1)}, u32[]{:S(2)}, u32[]{:S(2)}) collective-permute-start(f32[1,4,1,64,128]{4,3,2,1,0:T(8,128)S(1)} %get-tuple-element.56), channel_id=1, source_target_pairs={{0,1},{1,2},{2,3},{4,5},{5,6},{6,7},{8,9},{9,10},{10,11},{12,13},{... | collective-permute-start | bytes 393224 | tf_op jit(solution)/shard_map/ppermute | solution.py:23
  183.4 12.6 %collective-permute-start.21 = (f32[1,4,4,64,128]{4,3,2,1,0:T(8,128)S(1)}, f32[1,4,4,64,128]{4,3,2,1,0:T(8,128)S(1)}, u32[]{:S(2)}, u32[]{:S(2)}) collective-permute-start(f32[1,4,4,64,128]{4,3,2,1,0:T(8,128)S(1)} %fusion.79), channel_id=1, source_target_pairs={{0,4},{4,8},{8,12},{12,16},{16,20},{20,24},{24,28},{28,32},{32,36}... | collective-permute-start | bytes 1572872 | tf_op jit(solution)/shard_map/ppermute | solution.py:34
  185.4 6.9 %collective-permute-start.22 = (f32[1,4,1,64,128]{4,3,2,1,0:T(8,128)S(1)}, f32[1,4,1,64,128]{4,3,2,1,0:T(8,128)S(1)}, u32[]{:S(2)}, u32[]{:S(2)}) collective-permute-start(f32[1,4,1,64,128]{4,3,2,1,0:T(8,128)S(1)} %get-tuple-element.51), channel_id=1, source_target_pairs={{1,0},{2,1},{3,2},{5,4},{6,5},{7,6},{9,8},{10,9},{11,10},{13,12},{... | collective-permute-start | bytes 393224 | tf_op jit(solution)/shard_map/ppermute | solution.py:26
  186.7 7.1 %collective-permute-start.23 = (f32[1,4,1,64,128]{4,3,2,1,0:T(8,128)S(1)}, f32[1,4,1,64,128]{4,3,2,1,0:T(8,128)S(1)}, u32[]{:S(2)}, u32[]{:S(2)}) collective-permute-start(f32[1,4,1,64,128]{4,3,2,1,0:T(8,128)S(1)} %get-tuple-element.52), channel_id=1, source_target_pairs={{0,1},{1,2},{2,3},{4,5},{5,6},{6,7},{8,9},{9,10},{10,11},{12,13},{... | collective-permute-start | bytes 393224 | tf_op jit(solution)/shard_map/ppermute | solution.py:23
  196.6 12.6 %collective-permute-start.24 = (f32[1,4,4,64,128]{4,3,2,1,0:T(8,128)S(1)}, f32[1,4,4,64,128]{4,3,2,1,0:T(8,128)S(1)}, u32[]{:S(2)}, u32[]{:S(2)}) collective-permute-start(f32[1,4,4,64,128]{4,3,2,1,0:T(8,128)S(1)} %fusion.65), channel_id=1, source_target_pairs={{0,4},{4,8},{8,12},{12,16},{16,20},{20,24},{24,28},{28,32},{32,36}... | collective-permute-start | bytes 1572872 | tf_op jit(solution)/shard_map/ppermute | solution.py:34
  198.6 6.9 %collective-permute-start.25 = (f32[1,4,1,64,128]{4,3,2,1,0:T(8,128)S(1)}, f32[1,4,1,64,128]{4,3,2,1,0:T(8,128)S(1)}, u32[]{:S(2)}, u32[]{:S(2)}) collective-permute-start(f32[1,4,1,64,128]{4,3,2,1,0:T(8,128)S(1)} %get-tuple-element.47), channel_id=1, source_target_pairs={{1,0},{2,1},{3,2},{5,4},{6,5},{7,6},{9,8},{10,9},{11,10},{13,12},{... | collective-permute-start | bytes 393224 | tf_op jit(solution)/shard_map/ppermute | solution.py:26
  199.9 7.1 %collective-permute-start.26 = (f32[1,4,1,64,128]{4,3,2,1,0:T(8,128)S(1)}, f32[1,4,1,64,128]{4,3,2,1,0:T(8,128)S(1)}, u32[]{:S(2)}, u32[]{:S(2)}) collective-permute-start(f32[1,4,1,64,128]{4,3,2,1,0:T(8,128)S(1)} %get-tuple-element.48), channel_id=1, source_target_pairs={{0,1},{1,2},{2,3},{4,5},{5,6},{6,7},{8,9},{9,10},{10,11},{12,13},{... | collective-permute-start | bytes 393224 | tf_op jit(solution)/shard_map/ppermute | solution.py:23
  209.8 12.6 %collective-permute-start.27 = (f32[1,4,4,64,128]{4,3,2,1,0:T(8,128)S(1)}, f32[1,4,4,64,128]{4,3,2,1,0:T(8,128)S(1)}, u32[]{:S(2)}, u32[]{:S(2)}) collective-permute-start(f32[1,4,4,64,128]{4,3,2,1,0:T(8,128)S(1)} %fusion.51), channel_id=1, source_target_pairs={{0,4},{4,8},{8,12},{12,16},{16,20},{20,24},{24,28},{28,32},{32,36}... | collective-permute-start | bytes 1572872 | tf_op jit(solution)/shard_map/ppermute | solution.py:34
  211.7 6.9 %collective-permute-start.28 = (f32[1,4,1,64,128]{4,3,2,1,0:T(8,128)S(1)}, f32[1,4,1,64,128]{4,3,2,1,0:T(8,128)S(1)}, u32[]{:S(2)}, u32[]{:S(2)}) collective-permute-start(f32[1,4,1,64,128]{4,3,2,1,0:T(8,128)S(1)} %get-tuple-element.43), channel_id=1, source_target_pairs={{1,0},{2,1},{3,2},{5,4},{6,5},{7,6},{9,8},{10,9},{11,10},{13,12},{... | collective-permute-start | bytes 393224 | tf_op jit(solution)/shard_map/ppermute | solution.py:26
  213.0 7.1 %collective-permute-start.29 = (f32[1,4,1,64,128]{4,3,2,1,0:T(8,128)S(1)}, f32[1,4,1,64,128]{4,3,2,1,0:T(8,128)S(1)}, u32[]{:S(2)}, u32[]{:S(2)}) collective-permute-start(f32[1,4,1,64,128]{4,3,2,1,0:T(8,128)S(1)} %get-tuple-element.44), channel_id=1, source_target_pairs={{0,1},{1,2},{2,3},{4,5},{5,6},{6,7},{8,9},{9,10},{10,11},{12,13},{... | collective-permute-start | bytes 393224 | tf_op jit(solution)/shard_map/ppermute | solution.py:23
  223.4 7.8 %collective-permute-start.31 = (f32[1,4,1,32,64]{4,3,2,1,0:T(8,128)S(1)}, f32[1,4,1,32,64]{4,3,2,1,0:T(8,128)S(1)}, u32[]{:S(2)}, u32[]{:S(2)}) collective-permute-start(f32[1,4,1,32,64]{4,3,2,1,0:T(8,128)S(1)} %get-tuple-element.95), channel_id=1, source_target_pairs={{1,0},{2,1},{3,2},{5,4},{6,5},{7,6},{9,8},{10,9},{11,10},{13,12},{... | collective-permute-start | bytes 98312 | tf_op jit(solution)/shard_map/ppermute | solution.py:26
  224.7 6.5 %collective-permute-start.32 = (f32[1,4,1,32,64]{4,3,2,1,0:T(8,128)S(1)}, f32[1,4,1,32,64]{4,3,2,1,0:T(8,128)S(1)}, u32[]{:S(2)}, u32[]{:S(2)}) collective-permute-start(f32[1,4,1,32,64]{4,3,2,1,0:T(8,128)S(1)} %get-tuple-element.96), channel_id=1, source_target_pairs={{0,1},{1,2},{2,3},{4,5},{5,6},{6,7},{8,9},{9,10},{10,11},{12,13},{... | collective-permute-start | bytes 98312 | tf_op jit(solution)/shard_map/ppermute | solution.py:23
  229.2 8.4 %collective-permute-start.30 = (f32[1,4,2,32,64]{4,3,2,1,0:T(8,128)S(1)}, f32[1,4,2,32,64]{4,3,2,1,0:T(8,128)S(1)}, u32[]{:S(2)}, u32[]{:S(2)}) collective-permute-start(f32[1,4,2,32,64]{4,3,2,1,0:T(8,128)S(1)} %fusion.389), channel_id=1, source_target_pairs={{0,4},{4,8},{8,12},{12,16},{16,20},{20,24},{24,28},{28,32},{32,36}... | collective-permute-start | bytes 196616 | tf_op jit(solution)/shard_map/ppermute | solution.py:34
  237.8 7.8 %collective-permute-start.34 = (f32[1,4,1,32,64]{4,3,2,1,0:T(8,128)S(1)}, f32[1,4,1,32,64]{4,3,2,1,0:T(8,128)S(1)}, u32[]{:S(2)}, u32[]{:S(2)}) collective-permute-start(f32[1,4,1,32,64]{4,3,2,1,0:T(8,128)S(1)} %get-tuple-element.91), channel_id=1, source_target_pairs={{1,0},{2,1},{3,2},{5,4},{6,5},{7,6},{9,8},{10,9},{11,10},{13,12},{... | collective-permute-start | bytes 98312 | tf_op jit(solution)/shard_map/ppermute | solution.py:26
  239.1 6.5 %collective-permute-start.35 = (f32[1,4,1,32,64]{4,3,2,1,0:T(8,128)S(1)}, f32[1,4,1,32,64]{4,3,2,1,0:T(8,128)S(1)}, u32[]{:S(2)}, u32[]{:S(2)}) collective-permute-start(f32[1,4,1,32,64]{4,3,2,1,0:T(8,128)S(1)} %get-tuple-element.92), channel_id=1, source_target_pairs={{0,1},{1,2},{2,3},{4,5},{5,6},{6,7},{8,9},{9,10},{10,11},{12,13},{... | collective-permute-start | bytes 98312 | tf_op jit(solution)/shard_map/ppermute | solution.py:23
  243.7 8.4 %collective-permute-start.33 = (f32[1,4,2,32,64]{4,3,2,1,0:T(8,128)S(1)}, f32[1,4,2,32,64]{4,3,2,1,0:T(8,128)S(1)}, u32[]{:S(2)}, u32[]{:S(2)}) collective-permute-start(f32[1,4,2,32,64]{4,3,2,1,0:T(8,128)S(1)} %fusion.166), channel_id=1, source_target_pairs={{0,4},{4,8},{8,12},{12,16},{16,20},{20,24},{24,28},{28,32},{32,36}... | collective-permute-start | bytes 196616 | tf_op jit(solution)/shard_map/ppermute | solution.py:34
  322.6 7.8 %collective-permute-start.37 = (f32[1,4,1,32,64]{4,3,2,1,0:T(8,128)S(1)}, f32[1,4,1,32,64]{4,3,2,1,0:T(8,128)S(1)}, u32[]{:S(2)}, u32[]{:S(2)}) collective-permute-start(f32[1,4,1,32,64]{4,3,2,1,0:T(8,128)S(1)} %get-tuple-element.87), channel_id=1, source_target_pairs={{1,0},{2,1},{3,2},{5,4},{6,5},{7,6},{9,8},{10,9},{11,10},{13,12},{... | collective-permute-start | bytes 98312 | tf_op jit(solution)/shard_map/ppermute | solution.py:26
  323.9 6.5 %collective-permute-start.38 = (f32[1,4,1,32,64]{4,3,2,1,0:T(8,128)S(1)}, f32[1,4,1,32,64]{4,3,2,1,0:T(8,128)S(1)}, u32[]{:S(2)}, u32[]{:S(2)}) collective-permute-start(f32[1,4,1,32,64]{4,3,2,1,0:T(8,128)S(1)} %get-tuple-element.88), channel_id=1, source_target_pairs={{0,1},{1,2},{2,3},{4,5},{5,6},{6,7},{8,9},{9,10},{10,11},{12,13},{... | collective-permute-start | bytes 98312 | tf_op jit(solution)/shard_map/ppermute | solution.py:23
  328.4 8.4 %collective-permute-start.36 = (f32[1,4,2,32,64]{4,3,2,1,0:T(8,128)S(1)}, f32[1,4,2,32,64]{4,3,2,1,0:T(8,128)S(1)}, u32[]{:S(2)}, u32[]{:S(2)}) collective-permute-start(f32[1,4,2,32,64]{4,3,2,1,0:T(8,128)S(1)} %fusion.233), channel_id=1, source_target_pairs={{0,4},{4,8},{8,12},{12,16},{16,20},{20,24},{24,28},{28,32},{32,36}... | collective-permute-start | bytes 196616 | tf_op jit(solution)/shard_map/ppermute | solution.py:34
  337.4 12.6 %collective-permute-start.39 = (f32[1,4,4,64,128]{4,3,2,1,0:T(8,128)S(1)}, f32[1,4,4,64,128]{4,3,2,1,0:T(8,128)S(1)}, u32[]{:S(2)}, u32[]{:S(2)}) collective-permute-start(f32[1,4,4,64,128]{4,3,2,1,0:T(8,128)S(1)} %add.567), channel_id=1, source_target_pairs={{0,4},{4,8},{8,12},{12,16},{16,20},{20,24},{24,28},{28,32},{32,36}... | collective-permute-start | bytes 1572872 | tf_op jit(solution)/shard_map/ppermute | solution.py:34
  339.3 6.9 %collective-permute-start.40 = (f32[1,4,1,64,128]{4,3,2,1,0:T(8,128)S(1)}, f32[1,4,1,64,128]{4,3,2,1,0:T(8,128)S(1)}, u32[]{:S(2)}, u32[]{:S(2)}) collective-permute-start(f32[1,4,1,64,128]{4,3,2,1,0:T(8,128)S(1)} %get-tuple-element.39), channel_id=1, source_target_pairs={{1,0},{2,1},{3,2},{5,4},{6,5},{7,6},{9,8},{10,9},{11,10},{13,12},{... | collective-permute-start | bytes 393224 | tf_op jit(solution)/shard_map/ppermute | solution.py:26
  340.6 7.1 %collective-permute-start.41 = (f32[1,4,1,64,128]{4,3,2,1,0:T(8,128)S(1)}, f32[1,4,1,64,128]{4,3,2,1,0:T(8,128)S(1)}, u32[]{:S(2)}, u32[]{:S(2)}) collective-permute-start(f32[1,4,1,64,128]{4,3,2,1,0:T(8,128)S(1)} %get-tuple-element.40), channel_id=1, source_target_pairs={{0,1},{1,2},{2,3},{4,5},{5,6},{6,7},{8,9},{9,10},{10,11},{12,13},{... | collective-permute-start | bytes 393224 | tf_op jit(solution)/shard_map/ppermute | solution.py:23
  350.6 12.6 %collective-permute-start.42 = (f32[1,4,4,64,128]{4,3,2,1,0:T(8,128)S(1)}, f32[1,4,4,64,128]{4,3,2,1,0:T(8,128)S(1)}, u32[]{:S(2)}, u32[]{:S(2)}) collective-permute-start(f32[1,4,4,64,128]{4,3,2,1,0:T(8,128)S(1)} %fusion.25), channel_id=1, source_target_pairs={{0,4},{4,8},{8,12},{12,16},{16,20},{20,24},{24,28},{28,32},{32,36}... | collective-permute-start | bytes 1572872 | tf_op jit(solution)/shard_map/ppermute | solution.py:34
  352.5 6.9 %collective-permute-start.43 = (f32[1,4,1,64,128]{4,3,2,1,0:T(8,128)S(1)}, f32[1,4,1,64,128]{4,3,2,1,0:T(8,128)S(1)}, u32[]{:S(2)}, u32[]{:S(2)}) collective-permute-start(f32[1,4,1,64,128]{4,3,2,1,0:T(8,128)S(1)} %get-tuple-element.35), channel_id=1, source_target_pairs={{1,0},{2,1},{3,2},{5,4},{6,5},{7,6},{9,8},{10,9},{11,10},{13,12},{... | collective-permute-start | bytes 393224 | tf_op jit(solution)/shard_map/ppermute | solution.py:26
  353.8 7.1 %collective-permute-start.44 = (f32[1,4,1,64,128]{4,3,2,1,0:T(8,128)S(1)}, f32[1,4,1,64,128]{4,3,2,1,0:T(8,128)S(1)}, u32[]{:S(2)}, u32[]{:S(2)}) collective-permute-start(f32[1,4,1,64,128]{4,3,2,1,0:T(8,128)S(1)} %get-tuple-element.36), channel_id=1, source_target_pairs={{0,1},{1,2},{2,3},{4,5},{5,6},{6,7},{8,9},{9,10},{10,11},{12,13},{... | collective-permute-start | bytes 393224 | tf_op jit(solution)/shard_map/ppermute | solution.py:23
Sparse Core Ops, SparseCore 0:
  90.4 25.4 all-gather.4
  276.9 23.4 all-gather.6

commit v9 on v8

--- a/solution.py
+++ b/solution.py
@@ -145,8 +145,8 @@
         two_g = 2.0 * g
         diagonal = two_g + 6.0 / (spacing * spacing)
         target = src_ref[t] + two_g * earlier
-        v = zero
-        for repeat in range(COARSE_SWEEPS):
+        v = target / diagonal
+        for repeat in range(COARSE_SWEEPS - 1):
             v = v + (target - apply(v, two_g)) / diagonal
         out_ref[t] = v
         return v

time: 373 us -> 368 us (0.987)
  Pallas kernels: 33.1 us -> 28.4 us
    pallas_call x2, Pallas kernels: 33.1 us -> 28.4 us  [coarse_solve(): pl.pallas_call(kernel, out_shape=jax.ShapeDtypeStruct(flat_source.shape,...]
where the time goes in v9:
time: 368 us; the launch traced here: 367 us
  waiting for transfers between devices  128 us (35%)
  starting transfers between devices  117 us (32%)
  blocking collectives  46.5 us (13%)
  Pallas kernels  28.4 us (8%)
  local copies, waits for them, and re-layouts  17.3 us (5%)
  between operations  14.6 us (4%)
  other arithmetic  12.6 us (3%)
    ppermute x15, starting transfers between devices, with_halo(): lax.ppermute(lax.slice_in_dim(block, block.shape[dim] - width, None, axis...  68.5 us
    ppermute x15, waiting for transfers between devices, from_behind(): return lax.ppermute(array, axis, pairs)  54.8 us
    all_gather x2, waiting for transfers between devices, gather_all(): whole = lax.all_gather(across, 'space', axis=1, tiled=True)  49.2 us
    all_gather x2, blocking collectives, gather_all(): across = lax.all_gather(flat, 'tm', axis=0, tiled=True)  46.5 us
    ppermute x15, starting transfers between devices, from_behind(): return lax.ppermute(array, axis, pairs)  28.9 us
    pallas_call x2, Pallas kernels, coarse_solve(): pl.pallas_call(kernel, out_shape=jax.ShapeDtypeStruct(flat_source.shape,...  28.4 us
    ppermute x15, starting transfers between devices, with_halo(): lax.ppermute(lax.slice_in_dim(block, 0, width, axis=dim), axis, backward)  19.4 us
    ppermute x15, waiting for transfers between devices, with_halo(): lax.ppermute(lax.slice_in_dim(block, block.shape[dim] - width, None, axis...  13.7 us
  transfers between devices with their start and end apart: 47, of which 35 were waited for; matrix products, arithmetic and copies ran while one was open for 1% of the time, Pallas kernels for 0%

profile of v9, /device:TPU:2, one launch (start us, length us, event | category | flops | bytes accessed | tf_op | source)
XLA Modules:
  0.0 366.7 jit_solution(6067072588194643543)
XLA Ops:
  9.8 2.1 collective-permute-start
  13.2 4.6 %collective-permute-start.2 = (f32[1,4,1,64,128]{4,3,2,1,0:T(8,128)S(1)}, f32[1,4,1,64,128]{4,3,2,1,0:T(8,128)S(1)}, u32[]{:S(2)}, u32[]{:S(2)}) collective-permute-start(f32[1,4,1,64,128]{4,3,2,1,0:T(8,128)S(1)} %get-tuple-element.68), channel_id=1, source_target_pairs={{0,1},{1,2},{2,3},{4,5},{5,6},{6,7},{8,9},{9,10},{10,11},{12,13},{... | collective-permute-start | bytes 393224 | tf_op jit(solution)/shard_map/ppermute | solution.py:23
  19.2 1.7 collective-permute-done.2
  21.2 1.3 collective-permute-done
  23.1 1.9 collective-permute-start.3
  26.3 4.6 %collective-permute-start.5 = (f32[1,4,1,64,128]{4,3,2,1,0:T(8,128)S(1)}, f32[1,4,1,64,128]{4,3,2,1,0:T(8,128)S(1)}, u32[]{:S(2)}, u32[]{:S(2)}) collective-permute-start(f32[1,4,1,64,128]{4,3,2,1,0:T(8,128)S(1)} %get-tuple-element.64), channel_id=1, source_target_pairs={{0,1},{1,2},{2,3},{4,5},{5,6},{6,7},{8,9},{9,10},{10,11},{12,13},{... | collective-permute-start | bytes 393224 | tf_op jit(solution)/shard_map/ppermute | solution.py:23
  30.9 2.2 collective-permute-done.4
  33.1 1.5 collective-permute-done.5
  38.0 4.5 %collective-permute-start.8 = (f32[1,4,1,32,64]{4,3,2,1,0:T(8,128)S(1)}, f32[1,4,1,32,64]{4,3,2,1,0:T(8,128)S(1)}, u32[]{:S(2)}, u32[]{:S(2)}) collective-permute-start(f32[1,4,1,32,64]{4,3,2,1,0:T(8,128)S(1)} %get-tuple-element.108), channel_id=1, source_target_pairs={{0,1},{1,2},{2,3},{4,5},{5,6},{6,7},{8,9},{9,10},{10,11},{12,13},{... | collective-permute-start | bytes 98312 | tf_op jit(solution)/shard_map/ppermute | solution.py:23
  42.6 1.9 collective-permute-start.6
  44.6 6.3 %collective-permute-done.6 = f32[1,4,2,32,64]{4,3,2,1,0:T(8,128)S(1)} collective-permute-done((f32[1,4,2,32,64]{4,3,2,1,0:T(8,128)S(1)}, f32[1,4,2,32,64]{4,3,2,1,0:T(8,128)S(1)}, u32[]{:S(2)}, u32[]{:S(2)}) %collective-permute-start.6) | collective-permute-done | bytes 65568 | tf_op jit(solution)/shard_map/ppermute | solution.py:34
  52.4 4.5 %collective-permute-start.11 = (f32[1,4,1,32,64]{4,3,2,1,0:T(8,128)S(1)}, f32[1,4,1,32,64]{4,3,2,1,0:T(8,128)S(1)}, u32[]{:S(2)}, u32[]{:S(2)}) collective-permute-start(f32[1,4,1,32,64]{4,3,2,1,0:T(8,128)S(1)} %get-tuple-element.104), channel_id=1, source_target_pairs={{0,1},{1,2},{2,3},{4,5},{5,6},{6,7},{8,9},{9,10},{10,11},{12,13},{... | collective-permute-start | bytes 98312 | tf_op jit(solution)/shard_map/ppermute | solution.py:23
  57.2 1.9 collective-permute-start.9
  59.3 6.3 %collective-permute-done.9 = f32[1,4,2,32,64]{4,3,2,1,0:T(8,128)S(1)} collective-permute-done((f32[1,4,2,32,64]{4,3,2,1,0:T(8,128)S(1)}, f32[1,4,2,32,64]{4,3,2,1,0:T(8,128)S(1)}, u32[]{:S(2)}, u32[]{:S(2)}) %collective-permute-start.9) | collective-permute-done | bytes 65568 | tf_op jit(solution)/shard_map/ppermute | solution.py:34
  66.3 23.3 %all-gather = f32[32,1,2560]{2,1,0:T(1,128)S(1)} all-gather(f32[1,1,2560]{2,1,0:T(1,128)S(1)} %maximum_bitcast_fusion), channel_id=1, replica_groups=mesh['tm'=32,'space'=4] {'tm'}, dimensions={0}, use_global_device_ids=true | all-gather | bytes 337920 | tf_op jit(solution)/shard_map/all_gather | solution.py:191
  90.4 25.6 %all-gather.5.cloned.1.call-done = f32[32,10240]{1,0:T(8,128)} async-done(((f32[32,2560]{1,0:T(8,128)}), f32[32,10240]{1,0:T(8,128)}) %all-gather.5.cloned.1.call-update) | async-done | bytes 1310736 | tf_op jit(solution)/shard_map/all_gather | solution.py:192
  116.0 1.7 reshape.859
  118.7 2.5 reshape_transpose_reshape.7.src_ref
  122.9 14.2 %shard_map.37 = f32[32,16,512]{2,1,0:T(8,128)} custom-call(f32[32,16,512]{2,1,0:T(8,128)} %reshape_transpose_reshape.7.src_ref, f32[32,16,512]{2,1,0:T(8,128)} %reshape.860.met_ref), custom_call_target="tpu_custom_call" | custom-call | tf_op jit(solution)/shard_map/pallas_call | solution.py:161
  141.3 4.5 %collective-permute-start.14 = (f32[1,4,1,32,64]{4,3,2,1,0:T(8,128)S(1)}, f32[1,4,1,32,64]{4,3,2,1,0:T(8,128)S(1)}, u32[]{:S(2)}, u32[]{:S(2)}) collective-permute-start(f32[1,4,1,32,64]{4,3,2,1,0:T(8,128)S(1)} %get-tuple-element.100), channel_id=1, source_target_pairs={{0,1},{1,2},{2,3},{4,5},{5,6},{6,7},{8,9},{9,10},{10,11},{12,13},{... | collective-permute-start | bytes 98312 | tf_op jit(solution)/shard_map/ppermute | solution.py:23
  145.8 1.9 collective-permute-start.12
  147.9 6.3 %collective-permute-done.12 = f32[1,4,2,32,64]{4,3,2,1,0:T(8,128)S(1)} collective-permute-done((f32[1,4,2,32,64]{4,3,2,1,0:T(8,128)S(1)}, f32[1,4,2,32,64]{4,3,2,1,0:T(8,128)S(1)}, u32[]{:S(2)}, u32[]{:S(2)}) %collective-permute-start.12) | collective-permute-done | bytes 65568 | tf_op jit(solution)/shard_map/ppermute | solution.py:34
  154.8 1.9 collective-permute-start.15
  158.1 4.6 %collective-permute-start.17 = (f32[1,4,1,64,128]{4,3,2,1,0:T(8,128)S(1)}, f32[1,4,1,64,128]{4,3,2,1,0:T(8,128)S(1)}, u32[]{:S(2)}, u32[]{:S(2)}) collective-permute-start(f32[1,4,1,64,128]{4,3,2,1,0:T(8,128)S(1)} %get-tuple-element.60), channel_id=1, source_target_pairs={{0,1},{1,2},{2,3},{4,5},{5,6},{6,7},{8,9},{9,10},{10,11},{12,13},{... | collective-permute-start | bytes 393224 | tf_op jit(solution)/shard_map/ppermute | solution.py:23
  163.6 1.5 collective-permute-done.17
  165.3 2.1 collective-permute-done.15
  168.0 1.9 collective-permute-start.18
  171.2 4.6 %collective-permute-start.20 = (f32[1,4,1,64,128]{4,3,2,1,0:T(8,128)S(1)}, f32[1,4,1,64,128]{4,3,2,1,0:T(8,128)S(1)}, u32[]{:S(2)}, u32[]{:S(2)}) collective-permute-start(f32[1,4,1,64,128]{4,3,2,1,0:T(8,128)S(1)} %get-tuple-element.56), channel_id=1, source_target_pairs={{0,1},{1,2},{2,3},{4,5},{5,6},{6,7},{8,9},{9,10},{10,11},{12,13},{... | collective-permute-start | bytes 393224 | tf_op jit(solution)/shard_map/ppermute | solution.py:23
  176.8 1.5 collective-permute-done.20
  178.5 2.1 collective-permute-done.18
  181.1 1.9 collective-permute-start.21
  184.4 4.7 %collective-permute-start.23 = (f32[1,4,1,64,128]{4,3,2,1,0:T(8,128)S(1)}, f32[1,4,1,64,128]{4,3,2,1,0:T(8,128)S(1)}, u32[]{:S(2)}, u32[]{:S(2)}) collective-permute-start(f32[1,4,1,64,128]{4,3,2,1,0:T(8,128)S(1)} %get-tuple-element.52), channel_id=1, source_target_pairs={{0,1},{1,2},{2,3},{4,5},{5,6},{6,7},{8,9},{9,10},{10,11},{12,13},{... | collective-permute-start | bytes 393224 | tf_op jit(solution)/shard_map/ppermute | solution.py:23
  189.9 1.5 collective-permute-done.23
  191.6 2.1 collective-permute-done.21
  194.3 1.9 collective-permute-start.24
  197.5 4.6 %collective-permute-start.26 = (f32[1,4,1,64,128]{4,3,2,1,0:T(8,128)S(1)}, f32[1,4,1,64,128]{4,3,2,1,0:T(8,128)S(1)}, u32[]{:S(2)}, u32[]{:S(2)}) collective-permute-start(f32[1,4,1,64,128]{4,3,2,1,0:T(8,128)S(1)} %get-tuple-element.48), channel_id=1, source_target_pairs={{0,1},{1,2},{2,3},{4,5},{5,6},{6,7},{8,9},{9,10},{10,11},{12,13},{... | collective-permute-start | bytes 393224 | tf_op jit(solution)/shard_map/ppermute | solution.py:23
  203.1 1.5 collective-permute-done.26
  204.8 2.1 collective-permute-done.24
  207.4 1.9 collective-permute-start.27
  210.7 4.6 %collective-permute-start.29 = (f32[1,4,1,64,128]{4,3,2,1,0:T(8,128)S(1)}, f32[1,4,1,64,128]{4,3,2,1,0:T(8,128)S(1)}, u32[]{:S(2)}, u32[]{:S(2)}) collective-permute-start(f32[1,4,1,64,128]{4,3,2,1,0:T(8,128)S(1)} %get-tuple-element.44), channel_id=1, source_target_pairs={{0,1},{1,2},{2,3},{4,5},{5,6},{6,7},{8,9},{9,10},{10,11},{12,13},{... | collective-permute-start | bytes 393224 | tf_op jit(solution)/shard_map/ppermute | solution.py:23
  216.3 1.5 collective-permute-done.29
  218.0 2.1 collective-permute-done.27
  222.4 4.5 %collective-permute-start.32 = (f32[1,4,1,32,64]{4,3,2,1,0:T(8,128)S(1)}, f32[1,4,1,32,64]{4,3,2,1,0:T(8,128)S(1)}, u32[]{:S(2)}, u32[]{:S(2)}) collective-permute-start(f32[1,4,1,32,64]{4,3,2,1,0:T(8,128)S(1)} %get-tuple-element.96), channel_id=1, source_target_pairs={{0,1},{1,2},{2,3},{4,5},{5,6},{6,7},{8,9},{9,10},{10,11},{12,13},{... | collective-permute-start | bytes 98312 | tf_op jit(solution)/shard_map/ppermute | solution.py:23
  226.9 1.9 collective-permute-start.30
  229.0 6.3 %collective-permute-done.30 = f32[1,4,2,32,64]{4,3,2,1,0:T(8,128)S(1)} collective-permute-done((f32[1,4,2,32,64]{4,3,2,1,0:T(8,128)S(1)}, f32[1,4,2,32,64]{4,3,2,1,0:T(8,128)S(1)}, u32[]{:S(2)}, u32[]{:S(2)}) %collective-permute-start.30) | collective-permute-done | bytes 65568 | tf_op jit(solution)/shard_map/ppermute | solution.py:34
  236.8 4.5 %collective-permute-start.35 = (f32[1,4,1,32,64]{4,3,2,1,0:T(8,128)S(1)}, f32[1,4,1,32,64]{4,3,2,1,0:T(8,128)S(1)}, u32[]{:S(2)}, u32[]{:S(2)}) collective-permute-start(f32[1,4,1,32,64]{4,3,2,1,0:T(8,128)S(1)} %get-tuple-element.92), channel_id=1, source_target_pairs={{0,1},{1,2},{2,3},{4,5},{5,6},{6,7},{8,9},{9,10},{10,11},{12,13},{... | collective-permute-start | bytes 98312 | tf_op jit(solution)/shard_map/ppermute | solution.py:23
  241.3 1.9 collective-permute-start.33
  243.4 6.3 %collective-permute-done.33 = f32[1,4,2,32,64]{4,3,2,1,0:T(8,128)S(1)} collective-permute-done((f32[1,4,2,32,64]{4,3,2,1,0:T(8,128)S(1)}, f32[1,4,2,32,64]{4,3,2,1,0:T(8,128)S(1)}, u32[]{:S(2)}, u32[]{:S(2)}) %collective-permute-start.33) | collective-permute-done | bytes 65568 | tf_op jit(solution)/shard_map/ppermute | solution.py:34
  250.4 23.3 %all-gather.1 = f32[32,1,2048]{2,1,0:T(1,128)S(1)} all-gather(f32[1,1,2048]{2,1,0:T(1,128)S(1)} %reshape.880), channel_id=1, replica_groups=mesh['tm'=32,'space'=4] {'tm'}, dimensions={0}, use_global_device_ids=true | all-gather | bytes 270336 | tf_op jit(solution)/shard_map/all_gather | solution.py:191
  274.4 23.6 %all-gather.7.cloned.1.call-done = f32[32,8192]{1,0:T(8,128)} async-done(((f32[32,2048]{1,0:T(8,128)}), f32[32,8192]{1,0:T(8,128)}) %all-gather.7.cloned.1.call-update) | async-done | bytes 1048592 | tf_op jit(solution)/shard_map/all_gather | solution.py:192
  298.1 2.8 copy.22
  300.9 14.2 %shard_map.38 = f32[32,16,512]{2,1,0:T(8,128)} custom-call(f32[32,16,512]{2,1,0:T(8,128)} %bitcast.114, f32[32,16,512]{2,1,0:T(8,128)} %reshape.860.met_ref), custom_call_target="tpu_custom_call" | custom-call | tf_op jit(solution)/shard_map/pallas_call | solution.py:161
  319.2 4.5 %collective-permute-start.38 = (f32[1,4,1,32,64]{4,3,2,1,0:T(8,128)S(1)}, f32[1,4,1,32,64]{4,3,2,1,0:T(8,128)S(1)}, u32[]{:S(2)}, u32[]{:S(2)}) collective-permute-start(f32[1,4,1,32,64]{4,3,2,1,0:T(8,128)S(1)} %get-tuple-element.88), channel_id=1, source_target_pairs={{0,1},{1,2},{2,3},{4,5},{5,6},{6,7},{8,9},{9,10},{10,11},{12,13},{... | collective-permute-start | bytes 98312 | tf_op jit(solution)/shard_map/ppermute | solution.py:23
  323.8 1.9 collective-permute-start.36
  325.8 6.3 %collective-permute-done.36 = f32[1,4,2,32,64]{4,3,2,1,0:T(8,128)S(1)} collective-permute-done((f32[1,4,2,32,64]{4,3,2,1,0:T(8,128)S(1)}, f32[1,4,2,32,64]{4,3,2,1,0:T(8,128)S(1)}, u32[]{:S(2)}, u32[]{:S(2)}) %collective-permute-start.36) | collective-permute-done | bytes 65568 | tf_op jit(solution)/shard_map/ppermute | solution.py:34
  332.7 1.9 collective-permute-start.39
  336.0 4.6 %collective-permute-start.41 = (f32[1,4,1,64,128]{4,3,2,1,0:T(8,128)S(1)}, f32[1,4,1,64,128]{4,3,2,1,0:T(8,128)S(1)}, u32[]{:S(2)}, u32[]{:S(2)}) collective-permute-start(f32[1,4,1,64,128]{4,3,2,1,0:T(8,128)S(1)} %get-tuple-element.40), channel_id=1, source_target_pairs={{0,1},{1,2},{2,3},{4,5},{5,6},{6,7},{8,9},{9,10},{10,11},{12,13},{... | collective-permute-start | bytes 393224 | tf_op jit(solution)/shard_map/ppermute | solution.py:23
  341.6 1.5 collective-permute-done.41
  343.3 2.1 collective-permute-done.39
  345.9 1.9 collective-permute-start.42
  349.2 4.6 %collective-permute-start.44 = (f32[1,4,1,64,128]{4,3,2,1,0:T(8,128)S(1)}, f32[1,4,1,64,128]{4,3,2,1,0:T(8,128)S(1)}, u32[]{:S(2)}, u32[]{:S(2)}) collective-permute-start(f32[1,4,1,64,128]{4,3,2,1,0:T(8,128)S(1)} %get-tuple-element.36), channel_id=1, source_target_pairs={{0,1},{1,2},{2,3},{4,5},{5,6},{6,7},{8,9},{9,10},{10,11},{12,13},{... | collective-permute-start | bytes 393224 | tf_op jit(solution)/shard_map/ppermute | solution.py:23
  354.7 1.5 collective-permute-done.44
  356.4 2.1 collective-permute-done.42
  358.5 1.3 fusion.11
  (164 shorter events, 52.2 us)
Async XLA Ops:
  6.5 109.4 %all-gather.5.cloned.1.call-start = ((), (), s32[]{:S(2)}) async-start(), calls=%async_computation | async-start | bytes 1638400 | tf_op jit(solution)/shard_map/all_gather | solution.py:192
  7.5 10.2 %copy-start.1 = (f32[1,4,64,128]{3,2,1,0:T(8,128)S(1)}, f32[1,4,64,128]{3,2,1,0:T(8,128)}, u32[]{:S(2)}) copy-start(f32[1,4,64,128]{3,2,1,0:T(8,128)} %param.4) | copy-start | bytes 393220
  9.8 12.8 %copy-start = (f32[1,4,4,64,128]{4,3,2,1,0:T(8,128)S(1)}, f32[1,4,4,64,128]{4,3,2,1,0:T(8,128)}, u32[]{:S(2)}) copy-start(f32[1,4,4,64,128]{4,3,2,1,0:T(8,128)} %param.3) | copy-start | bytes 1572868
  9.8 12.7 %collective-permute-start = (f32[1,4,4,64,128]{4,3,2,1,0:T(8,128)S(1)}, f32[1,4,4,64,128]{4,3,2,1,0:T(8,128)S(1)}, u32[]{:S(2)}, u32[]{:S(2)}) collective-permute-start(f32[1,4,4,64,128]{4,3,2,1,0:T(8,128)S(1)} %get-tuple-element.9), channel_id=1, source_target_pairs={{0,4},{4,8},{8,12},{12,16},{16,20},{20,24},{24,28},{28,32},{32,36}... | collective-permute-start | bytes 1572872 | tf_op jit(solution)/shard_map/ppermute | solution.py:34
  11.9 7.4 %collective-permute-start.1 = (f32[1,4,1,64,128]{4,3,2,1,0:T(8,128)S(1)}, f32[1,4,1,64,128]{4,3,2,1,0:T(8,128)S(1)}, u32[]{:S(2)}, u32[]{:S(2)}) collective-permute-start(f32[1,4,1,64,128]{4,3,2,1,0:T(8,128)S(1)} %get-tuple-element.67), channel_id=1, source_target_pairs={{1,0},{2,1},{3,2},{5,4},{6,5},{7,6},{9,8},{10,9},{11,10},{13,12},{... | collective-permute-start | bytes 393224 | tf_op jit(solution)/shard_map/ppermute | solution.py:26
  13.2 7.8 %collective-permute-start.2 = (f32[1,4,1,64,128]{4,3,2,1,0:T(8,128)S(1)}, f32[1,4,1,64,128]{4,3,2,1,0:T(8,128)S(1)}, u32[]{:S(2)}, u32[]{:S(2)}) collective-permute-start(f32[1,4,1,64,128]{4,3,2,1,0:T(8,128)S(1)} %get-tuple-element.68), channel_id=1, source_target_pairs={{0,1},{1,2},{2,3},{4,5},{5,6},{6,7},{8,9},{9,10},{10,11},{12,13},{... | collective-permute-start | bytes 393224 | tf_op jit(solution)/shard_map/ppermute | solution.py:23
  23.1 12.6 %collective-permute-start.3 = (f32[1,4,4,64,128]{4,3,2,1,0:T(8,128)S(1)}, f32[1,4,4,64,128]{4,3,2,1,0:T(8,128)S(1)}, u32[]{:S(2)}, u32[]{:S(2)}) collective-permute-start(f32[1,4,4,64,128]{4,3,2,1,0:T(8,128)S(1)} %fusion.119), channel_id=1, source_target_pairs={{0,4},{4,8},{8,12},{12,16},{16,20},{20,24},{24,28},{28,32},{32,36}... | collective-permute-start | bytes 1572872 | tf_op jit(solution)/shard_map/ppermute | solution.py:34
  25.0 8.1 %collective-permute-start.4 = (f32[1,4,1,64,128]{4,3,2,1,0:T(8,128)S(1)}, f32[1,4,1,64,128]{4,3,2,1,0:T(8,128)S(1)}, u32[]{:S(2)}, u32[]{:S(2)}) collective-permute-start(f32[1,4,1,64,128]{4,3,2,1,0:T(8,128)S(1)} %get-tuple-element.63), channel_id=1, source_target_pairs={{1,0},{2,1},{3,2},{5,4},{6,5},{7,6},{9,8},{10,9},{11,10},{13,12},{... | collective-permute-start | bytes 393224 | tf_op jit(solution)/shard_map/ppermute | solution.py:26
  26.3 8.3 %collective-permute-start.5 = (f32[1,4,1,64,128]{4,3,2,1,0:T(8,128)S(1)}, f32[1,4,1,64,128]{4,3,2,1,0:T(8,128)S(1)}, u32[]{:S(2)}, u32[]{:S(2)}) collective-permute-start(f32[1,4,1,64,128]{4,3,2,1,0:T(8,128)S(1)} %get-tuple-element.64), channel_id=1, source_target_pairs={{0,1},{1,2},{2,3},{4,5},{5,6},{6,7},{8,9},{9,10},{10,11},{12,13},{... | collective-permute-start | bytes 393224 | tf_op jit(solution)/shard_map/ppermute | solution.py:23
  36.7 7.8 %collective-permute-start.7 = (f32[1,4,1,32,64]{4,3,2,1,0:T(8,128)S(1)}, f32[1,4,1,32,64]{4,3,2,1,0:T(8,128)S(1)}, u32[]{:S(2)}, u32[]{:S(2)}) collective-permute-start(f32[1,4,1,32,64]{4,3,2,1,0:T(8,128)S(1)} %get-tuple-element.107), channel_id=1, source_target_pairs={{1,0},{2,1},{3,2},{5,4},{6,5},{7,6},{9,8},{10,9},{11,10},{13,12},{... | collective-permute-start | bytes 98312 | tf_op jit(solution)/shard_map/ppermute | solution.py:26
  38.0 6.5 %collective-permute-start.8 = (f32[1,4,1,32,64]{4,3,2,1,0:T(8,128)S(1)}, f32[1,4,1,32,64]{4,3,2,1,0:T(8,128)S(1)}, u32[]{:S(2)}, u32[]{:S(2)}) collective-permute-start(f32[1,4,1,32,64]{4,3,2,1,0:T(8,128)S(1)} %get-tuple-element.108), channel_id=1, source_target_pairs={{0,1},{1,2},{2,3},{4,5},{5,6},{6,7},{8,9},{9,10},{10,11},{12,13},{... | collective-permute-start | bytes 98312 | tf_op jit(solution)/shard_map/ppermute | solution.py:23
  42.6 8.4 %collective-permute-start.6 = (f32[1,4,2,32,64]{4,3,2,1,0:T(8,128)S(1)}, f32[1,4,2,32,64]{4,3,2,1,0:T(8,128)S(1)}, u32[]{:S(2)}, u32[]{:S(2)}) collective-permute-start(f32[1,4,2,32,64]{4,3,2,1,0:T(8,128)S(1)} %fusion.388), channel_id=1, source_target_pairs={{0,4},{4,8},{8,12},{12,16},{16,20},{20,24},{24,28},{28,32},{32,36}... | collective-permute-start | bytes 196616 | tf_op jit(solution)/shard_map/ppermute | solution.py:34
  51.1 8.0 %collective-permute-start.10 = (f32[1,4,1,32,64]{4,3,2,1,0:T(8,128)S(1)}, f32[1,4,1,32,64]{4,3,2,1,0:T(8,128)S(1)}, u32[]{:S(2)}, u32[]{:S(2)}) collective-permute-start(f32[1,4,1,32,64]{4,3,2,1,0:T(8,128)S(1)} %get-tuple-element.103), channel_id=1, source_target_pairs={{1,0},{2,1},{3,2},{5,4},{6,5},{7,6},{9,8},{10,9},{11,10},{13,12},{... | collective-permute-start | bytes 98312 | tf_op jit(solution)/shard_map/ppermute | solution.py:26
  52.4 6.7 %collective-permute-start.11 = (f32[1,4,1,32,64]{4,3,2,1,0:T(8,128)S(1)}, f32[1,4,1,32,64]{4,3,2,1,0:T(8,128)S(1)}, u32[]{:S(2)}, u32[]{:S(2)}) collective-permute-start(f32[1,4,1,32,64]{4,3,2,1,0:T(8,128)S(1)} %get-tuple-element.104), channel_id=1, source_target_pairs={{0,1},{1,2},{2,3},{4,5},{5,6},{6,7},{8,9},{9,10},{10,11},{12,13},{... | collective-permute-start | bytes 98312 | tf_op jit(solution)/shard_map/ppermute | solution.py:23
  57.2 8.4 %collective-permute-start.9 = (f32[1,4,2,32,64]{4,3,2,1,0:T(8,128)S(1)}, f32[1,4,2,32,64]{4,3,2,1,0:T(8,128)S(1)}, u32[]{:S(2)}, u32[]{:S(2)}) collective-permute-start(f32[1,4,2,32,64]{4,3,2,1,0:T(8,128)S(1)} %fusion.207), channel_id=1, source_target_pairs={{0,4},{4,8},{8,12},{12,16},{16,20},{20,24},{24,28},{28,32},{32,36}... | collective-permute-start | bytes 196616 | tf_op jit(solution)/shard_map/ppermute | solution.py:34
  90.3 207.8 %all-gather.7.cloned.1.call-start = ((), (), s32[]{:S(2)}) async-start(), calls=%async_computation.1 | async-start | bytes 1310720 | tf_op jit(solution)/shard_map/all_gather | solution.py:192
  140.0 7.8 %collective-permute-start.13 = (f32[1,4,1,32,64]{4,3,2,1,0:T(8,128)S(1)}, f32[1,4,1,32,64]{4,3,2,1,0:T(8,128)S(1)}, u32[]{:S(2)}, u32[]{:S(2)}) collective-permute-start(f32[1,4,1,32,64]{4,3,2,1,0:T(8,128)S(1)} %get-tuple-element.99), channel_id=1, source_target_pairs={{1,0},{2,1},{3,2},{5,4},{6,5},{7,6},{9,8},{10,9},{11,10},{13,12},{... | collective-permute-start | bytes 98312 | tf_op jit(solution)/shard_map/ppermute | solution.py:26
  141.3 6.5 %collective-permute-start.14 = (f32[1,4,1,32,64]{4,3,2,1,0:T(8,128)S(1)}, f32[1,4,1,32,64]{4,3,2,1,0:T(8,128)S(1)}, u32[]{:S(2)}, u32[]{:S(2)}) collective-permute-start(f32[1,4,1,32,64]{4,3,2,1,0:T(8,128)S(1)} %get-tuple-element.100), channel_id=1, source_target_pairs={{0,1},{1,2},{2,3},{4,5},{5,6},{6,7},{8,9},{9,10},{10,11},{12,13},{... | collective-permute-start | bytes 98312 | tf_op jit(solution)/shard_map/ppermute | solution.py:23
  145.8 8.4 %collective-permute-start.12 = (f32[1,4,2,32,64]{4,3,2,1,0:T(8,128)S(1)}, f32[1,4,2,32,64]{4,3,2,1,0:T(8,128)S(1)}, u32[]{:S(2)}, u32[]{:S(2)}) collective-permute-start(f32[1,4,2,32,64]{4,3,2,1,0:T(8,128)S(1)} %fusion.221), channel_id=1, source_target_pairs={{0,4},{4,8},{8,12},{12,16},{16,20},{20,24},{24,28},{28,32},{32,36}... | collective-permute-start | bytes 196616 | tf_op jit(solution)/shard_map/ppermute | solution.py:34
  154.8 12.6 %collective-permute-start.15 = (f32[1,4,4,64,128]{4,3,2,1,0:T(8,128)S(1)}, f32[1,4,4,64,128]{4,3,2,1,0:T(8,128)S(1)}, u32[]{:S(2)}, u32[]{:S(2)}) collective-permute-start(f32[1,4,4,64,128]{4,3,2,1,0:T(8,128)S(1)} %add.517), channel_id=1, source_target_pairs={{0,4},{4,8},{8,12},{12,16},{16,20},{20,24},{24,28},{28,32},{32,36}... | collective-permute-start | bytes 1572872 | tf_op jit(solution)/shard_map/ppermute | solution.py:34
  156.8 6.9 %collective-permute-start.16 = (f32[1,4,1,64,128]{4,3,2,1,0:T(8,128)S(1)}, f32[1,4,1,64,128]{4,3,2,1,0:T(8,128)S(1)}, u32[]{:S(2)}, u32[]{:S(2)}) collective-permute-start(f32[1,4,1,64,128]{4,3,2,1,0:T(8,128)S(1)} %get-tuple-element.59), channel_id=1, source_target_pairs={{1,0},{2,1},{3,2},{5,4},{6,5},{7,6},{9,8},{10,9},{11,10},{13,12},{... | collective-permute-start | bytes 393224 | tf_op jit(solution)/shard_map/ppermute | solution.py:26
  158.1 7.1 %collective-permute-start.17 = (f32[1,4,1,64,128]{4,3,2,1,0:T(8,128)S(1)}, f32[1,4,1,64,128]{4,3,2,1,0:T(8,128)S(1)}, u32[]{:S(2)}, u32[]{:S(2)}) collective-permute-start(f32[1,4,1,64,128]{4,3,2,1,0:T(8,128)S(1)} %get-tuple-element.60), channel_id=1, source_target_pairs={{0,1},{1,2},{2,3},{4,5},{5,6},{6,7},{8,9},{9,10},{10,11},{12,13},{... | collective-permute-start | bytes 393224 | tf_op jit(solution)/shard_map/ppermute | solution.py:23
  168.0 12.6 %collective-permute-start.18 = (f32[1,4,4,64,128]{4,3,2,1,0:T(8,128)S(1)}, f32[1,4,4,64,128]{4,3,2,1,0:T(8,128)S(1)}, u32[]{:S(2)}, u32[]{:S(2)}) collective-permute-start(f32[1,4,4,64,128]{4,3,2,1,0:T(8,128)S(1)} %fusion.93), channel_id=1, source_target_pairs={{0,4},{4,8},{8,12},{12,16},{16,20},{20,24},{24,28},{28,32},{32,36}... | collective-permute-start | bytes 1572872 | tf_op jit(solution)/shard_map/ppermute | solution.py:34
  169.9 6.9 %collective-permute-start.19 = (f32[1,4,1,64,128]{4,3,2,1,0:T(8,128)S(1)}, f32[1,4,1,64,128]{4,3,2,1,0:T(8,128)S(1)}, u32[]{:S(2)}, u32[]{:S(2)}) collective-permute-start(f32[1,4,1,64,128]{4,3,2,1,0:T(8,128)S(1)} %get-tuple-element.55), channel_id=1, source_target_pairs={{1,0},{2,1},{3,2},{5,4},{6,5},{7,6},{9,8},{10,9},{11,10},{13,12},{... | collective-permute-start | bytes 393224 | tf_op jit(solution)/shard_map/ppermute | solution.py:26
  171.2 7.1 %collective-permute-start.20 = (f32[1,4,1,64,128]{4,3,2,1,0:T(8,128)S(1)}, f32[1,4,1,64,128]{4,3,2,1,0:T(8,128)S(1)}, u32[]{:S(2)}, u32[]{:S(2)}) collective-permute-start(f32[1,4,1,64,128]{4,3,2,1,0:T(8,128)S(1)} %get-tuple-element.56), channel_id=1, source_target_pairs={{0,1},{1,2},{2,3},{4,5},{5,6},{6,7},{8,9},{9,10},{10,11},{12,13},{... | collective-permute-start | bytes 393224 | tf_op jit(solution)/shard_map/ppermute | solution.py:23
  181.1 12.6 %collective-permute-start.21 = (f32[1,4,4,64,128]{4,3,2,1,0:T(8,128)S(1)}, f32[1,4,4,64,128]{4,3,2,1,0:T(8,128)S(1)}, u32[]{:S(2)}, u32[]{:S(2)}) collective-permute-start(f32[1,4,4,64,128]{4,3,2,1,0:T(8,128)S(1)} %fusion.79), channel_id=1, source_target_pairs={{0,4},{4,8},{8,12},{12,16},{16,20},{20,24},{24,28},{28,32},{32,36}... | collective-permute-start | bytes 1572872 | tf_op jit(solution)/shard_map/ppermute | solution.py:34
  183.1 6.9 %collective-permute-start.22 = (f32[1,4,1,64,128]{4,3,2,1,0:T(8,128)S(1)}, f32[1,4,1,64,128]{4,3,2,1,0:T(8,128)S(1)}, u32[]{:S(2)}, u32[]{:S(2)}) collective-permute-start(f32[1,4,1,64,128]{4,3,2,1,0:T(8,128)S(1)} %get-tuple-element.51), channel_id=1, source_target_pairs={{1,0},{2,1},{3,2},{5,4},{6,5},{7,6},{9,8},{10,9},{11,10},{13,12},{... | collective-permute-start | bytes 393224 | tf_op jit(solution)/shard_map/ppermute | solution.py:26
  184.4 7.1 %collective-permute-start.23 = (f32[1,4,1,64,128]{4,3,2,1,0:T(8,128)S(1)}, f32[1,4,1,64,128]{4,3,2,1,0:T(8,128)S(1)}, u32[]{:S(2)}, u32[]{:S(2)}) collective-permute-start(f32[1,4,1,64,128]{4,3,2,1,0:T(8,128)S(1)} %get-tuple-element.52), channel_id=1, source_target_pairs={{0,1},{1,2},{2,3},{4,5},{5,6},{6,7},{8,9},{9,10},{10,11},{12,13},{... | collective-permute-start | bytes 393224 | tf_op jit(solution)/shard_map/ppermute | solution.py:23
  194.3 12.6 %collective-permute-start.24 = (f32[1,4,4,64,128]{4,3,2,1,0:T(8,128)S(1)}, f32[1,4,4,64,128]{4,3,2,1,0:T(8,128)S(1)}, u32[]{:S(2)}, u32[]{:S(2)}) collective-permute-start(f32[1,4,4,64,128]{4,3,2,1,0:T(8,128)S(1)} %fusion.65), channel_id=1, source_target_pairs={{0,4},{4,8},{8,12},{12,16},{16,20},{20,24},{24,28},{28,32},{32,36}... | collective-permute-start | bytes 1572872 | tf_op jit(solution)/shard_map/ppermute | solution.py:34
  196.2 6.9 %collective-permute-start.25 = (f32[1,4,1,64,128]{4,3,2,1,0:T(8,128)S(1)}, f32[1,4,1,64,128]{4,3,2,1,0:T(8,128)S(1)}, u32[]{:S(2)}, u32[]{:S(2)}) collective-permute-start(f32[1,4,1,64,128]{4,3,2,1,0:T(8,128)S(1)} %get-tuple-element.47), channel_id=1, source_target_pairs={{1,0},{2,1},{3,2},{5,4},{6,5},{7,6},{9,8},{10,9},{11,10},{13,12},{... | collective-permute-start | bytes 393224 | tf_op jit(solution)/shard_map/ppermute | solution.py:26
  197.5 7.1 %collective-permute-start.26 = (f32[1,4,1,64,128]{4,3,2,1,0:T(8,128)S(1)}, f32[1,4,1,64,128]{4,3,2,1,0:T(8,128)S(1)}, u32[]{:S(2)}, u32[]{:S(2)}) collective-permute-start(f32[1,4,1,64,128]{4,3,2,1,0:T(8,128)S(1)} %get-tuple-element.48), channel_id=1, source_target_pairs={{0,1},{1,2},{2,3},{4,5},{5,6},{6,7},{8,9},{9,10},{10,11},{12,13},{... | collective-permute-start | bytes 393224 | tf_op jit(solution)/shard_map/ppermute | solution.py:23
  207.4 12.6 %collective-permute-start.27 = (f32[1,4,4,64,128]{4,3,2,1,0:T(8,128)S(1)}, f32[1,4,4,64,128]{4,3,2,1,0:T(8,128)S(1)}, u32[]{:S(2)}, u32[]{:S(2)}) collective-permute-start(f32[1,4,4,64,128]{4,3,2,1,0:T(8,128)S(1)} %fusion.51), channel_id=1, source_target_pairs={{0,4},{4,8},{8,12},{12,16},{16,20},{20,24},{24,28},{28,32},{32,36}... | collective-permute-start | bytes 1572872 | tf_op jit(solution)/shard_map/ppermute | solution.py:34
  209.4 6.9 %collective-permute-start.28 = (f32[1,4,1,64,128]{4,3,2,1,0:T(8,128)S(1)}, f32[1,4,1,64,128]{4,3,2,1,0:T(8,128)S(1)}, u32[]{:S(2)}, u32[]{:S(2)}) collective-permute-start(f32[1,4,1,64,128]{4,3,2,1,0:T(8,128)S(1)} %get-tuple-element.43), channel_id=1, source_target_pairs={{1,0},{2,1},{3,2},{5,4},{6,5},{7,6},{9,8},{10,9},{11,10},{13,12},{... | collective-permute-start | bytes 393224 | tf_op jit(solution)/shard_map/ppermute | solution.py:26
  210.7 7.1 %collective-permute-start.29 = (f32[1,4,1,64,128]{4,3,2,1,0:T(8,128)S(1)}, f32[1,4,1,64,128]{4,3,2,1,0:T(8,128)S(1)}, u32[]{:S(2)}, u32[]{:S(2)}) collective-permute-start(f32[1,4,1,64,128]{4,3,2,1,0:T(8,128)S(1)} %get-tuple-element.44), channel_id=1, source_target_pairs={{0,1},{1,2},{2,3},{4,5},{5,6},{6,7},{8,9},{9,10},{10,11},{12,13},{... | collective-permute-start | bytes 393224 | tf_op jit(solution)/shard_map/ppermute | solution.py:23
  221.1 7.8 %collective-permute-start.31 = (f32[1,4,1,32,64]{4,3,2,1,0:T(8,128)S(1)}, f32[1,4,1,32,64]{4,3,2,1,0:T(8,128)S(1)}, u32[]{:S(2)}, u32[]{:S(2)}) collective-permute-start(f32[1,4,1,32,64]{4,3,2,1,0:T(8,128)S(1)} %get-tuple-element.95), channel_id=1, source_target_pairs={{1,0},{2,1},{3,2},{5,4},{6,5},{7,6},{9,8},{10,9},{11,10},{13,12},{... | collective-permute-start | bytes 98312 | tf_op jit(solution)/shard_map/ppermute | solution.py:26
  222.4 6.5 %collective-permute-start.32 = (f32[1,4,1,32,64]{4,3,2,1,0:T(8,128)S(1)}, f32[1,4,1,32,64]{4,3,2,1,0:T(8,128)S(1)}, u32[]{:S(2)}, u32[]{:S(2)}) collective-permute-start(f32[1,4,1,32,64]{4,3,2,1,0:T(8,128)S(1)} %get-tuple-element.96), channel_id=1, source_target_pairs={{0,1},{1,2},{2,3},{4,5},{5,6},{6,7},{8,9},{9,10},{10,11},{12,13},{... | collective-permute-start | bytes 98312 | tf_op jit(solution)/shard_map/ppermute | solution.py:23
  226.9 8.4 %collective-permute-start.30 = (f32[1,4,2,32,64]{4,3,2,1,0:T(8,128)S(1)}, f32[1,4,2,32,64]{4,3,2,1,0:T(8,128)S(1)}, u32[]{:S(2)}, u32[]{:S(2)}) collective-permute-start(f32[1,4,2,32,64]{4,3,2,1,0:T(8,128)S(1)} %fusion.389), channel_id=1, source_target_pairs={{0,4},{4,8},{8,12},{12,16},{16,20},{20,24},{24,28},{28,32},{32,36}... | collective-permute-start | bytes 196616 | tf_op jit(solution)/shard_map/ppermute | solution.py:34
  235.5 7.8 %collective-permute-start.34 = (f32[1,4,1,32,64]{4,3,2,1,0:T(8,128)S(1)}, f32[1,4,1,32,64]{4,3,2,1,0:T(8,128)S(1)}, u32[]{:S(2)}, u32[]{:S(2)}) collective-permute-start(f32[1,4,1,32,64]{4,3,2,1,0:T(8,128)S(1)} %get-tuple-element.91), channel_id=1, source_target_pairs={{1,0},{2,1},{3,2},{5,4},{6,5},{7,6},{9,8},{10,9},{11,10},{13,12},{... | collective-permute-start | bytes 98312 | tf_op jit(solution)/shard_map/ppermute | solution.py:26
  236.8 6.5 %collective-permute-start.35 = (f32[1,4,1,32,64]{4,3,2,1,0:T(8,128)S(1)}, f32[1,4,1,32,64]{4,3,2,1,0:T(8,128)S(1)}, u32[]{:S(2)}, u32[]{:S(2)}) collective-permute-start(f32[1,4,1,32,64]{4,3,2,1,0:T(8,128)S(1)} %get-tuple-element.92), channel_id=1, source_target_pairs={{0,1},{1,2},{2,3},{4,5},{5,6},{6,7},{8,9},{9,10},{10,11},{12,13},{... | collective-permute-start | bytes 98312 | tf_op jit(solution)/shard_map/ppermute | solution.py:23
  241.3 8.4 %collective-permute-start.33 = (f32[1,4,2,32,64]{4,3,2,1,0:T(8,128)S(1)}, f32[1,4,2,32,64]{4,3,2,1,0:T(8,128)S(1)}, u32[]{:S(2)}, u32[]{:S(2)}) collective-permute-start(f32[1,4,2,32,64]{4,3,2,1,0:T(8,128)S(1)} %fusion.166), channel_id=1, source_target_pairs={{0,4},{4,8},{8,12},{12,16},{16,20},{20,24},{24,28},{28,32},{32,36}... | collective-permute-start | bytes 196616 | tf_op jit(solution)/shard_map/ppermute | solution.py:34
  317.9 7.8 %collective-permute-start.37 = (f32[1,4,1,32,64]{4,3,2,1,0:T(8,128)S(1)}, f32[1,4,1,32,64]{4,3,2,1,0:T(8,128)S(1)}, u32[]{:S(2)}, u32[]{:S(2)}) collective-permute-start(f32[1,4,1,32,64]{4,3,2,1,0:T(8,128)S(1)} %get-tuple-element.87), channel_id=1, source_target_pairs={{1,0},{2,1},{3,2},{5,4},{6,5},{7,6},{9,8},{10,9},{11,10},{13,12},{... | collective-permute-start | bytes 98312 | tf_op jit(solution)/shard_map/ppermute | solution.py:26
  319.2 6.5 %collective-permute-start.38 = (f32[1,4,1,32,64]{4,3,2,1,0:T(8,128)S(1)}, f32[1,4,1,32,64]{4,3,2,1,0:T(8,128)S(1)}, u32[]{:S(2)}, u32[]{:S(2)}) collective-permute-start(f32[1,4,1,32,64]{4,3,2,1,0:T(8,128)S(1)} %get-tuple-element.88), channel_id=1, source_target_pairs={{0,1},{1,2},{2,3},{4,5},{5,6},{6,7},{8,9},{9,10},{10,11},{12,13},{... | collective-permute-start | bytes 98312 | tf_op jit(solution)/shard_map/ppermute | solution.py:23
  323.8 8.4 %collective-permute-start.36 = (f32[1,4,2,32,64]{4,3,2,1,0:T(8,128)S(1)}, f32[1,4,2,32,64]{4,3,2,1,0:T(8,128)S(1)}, u32[]{:S(2)}, u32[]{:S(2)}) collective-permute-start(f32[1,4,2,32,64]{4,3,2,1,0:T(8,128)S(1)} %fusion.233), channel_id=1, source_target_pairs={{0,4},{4,8},{8,12},{12,16},{16,20},{20,24},{24,28},{28,32},{32,36}... | collective-permute-start | bytes 196616 | tf_op jit(solution)/shard_map/ppermute | solution.py:34
  332.7 12.6 %collective-permute-start.39 = (f32[1,4,4,64,128]{4,3,2,1,0:T(8,128)S(1)}, f32[1,4,4,64,128]{4,3,2,1,0:T(8,128)S(1)}, u32[]{:S(2)}, u32[]{:S(2)}) collective-permute-start(f32[1,4,4,64,128]{4,3,2,1,0:T(8,128)S(1)} %add.567), channel_id=1, source_target_pairs={{0,4},{4,8},{8,12},{12,16},{16,20},{20,24},{24,28},{28,32},{32,36}... | collective-permute-start | bytes 1572872 | tf_op jit(solution)/shard_map/ppermute | solution.py:34
  334.7 6.9 %collective-permute-start.40 = (f32[1,4,1,64,128]{4,3,2,1,0:T(8,128)S(1)}, f32[1,4,1,64,128]{4,3,2,1,0:T(8,128)S(1)}, u32[]{:S(2)}, u32[]{:S(2)}) collective-permute-start(f32[1,4,1,64,128]{4,3,2,1,0:T(8,128)S(1)} %get-tuple-element.39), channel_id=1, source_target_pairs={{1,0},{2,1},{3,2},{5,4},{6,5},{7,6},{9,8},{10,9},{11,10},{13,12},{... | collective-permute-start | bytes 393224 | tf_op jit(solution)/shard_map/ppermute | solution.py:26
  336.0 7.1 %collective-permute-start.41 = (f32[1,4,1,64,128]{4,3,2,1,0:T(8,128)S(1)}, f32[1,4,1,64,128]{4,3,2,1,0:T(8,128)S(1)}, u32[]{:S(2)}, u32[]{:S(2)}) collective-permute-start(f32[1,4,1,64,128]{4,3,2,1,0:T(8,128)S(1)} %get-tuple-element.40), channel_id=1, source_target_pairs={{0,1},{1,2},{2,3},{4,5},{5,6},{6,7},{8,9},{9,10},{10,11},{12,13},{... | collective-permute-start | bytes 393224 | tf_op jit(solution)/shard_map/ppermute | solution.py:23
  345.9 12.6 %collective-permute-start.42 = (f32[1,4,4,64,128]{4,3,2,1,0:T(8,128)S(1)}, f32[1,4,4,64,128]{4,3,2,1,0:T(8,128)S(1)}, u32[]{:S(2)}, u32[]{:S(2)}) collective-permute-start(f32[1,4,4,64,128]{4,3,2,1,0:T(8,128)S(1)} %fusion.25), channel_id=1, source_target_pairs={{0,4},{4,8},{8,12},{12,16},{16,20},{20,24},{24,28},{28,32},{32,36}... | collective-permute-start | bytes 1572872 | tf_op jit(solution)/shard_map/ppermute | solution.py:34
  347.9 6.9 %collective-permute-start.43 = (f32[1,4,1,64,128]{4,3,2,1,0:T(8,128)S(1)}, f32[1,4,1,64,128]{4,3,2,1,0:T(8,128)S(1)}, u32[]{:S(2)}, u32[]{:S(2)}) collective-permute-start(f32[1,4,1,64,128]{4,3,2,1,0:T(8,128)S(1)} %get-tuple-element.35), channel_id=1, source_target_pairs={{1,0},{2,1},{3,2},{5,4},{6,5},{7,6},{9,8},{10,9},{11,10},{13,12},{... | collective-permute-start | bytes 393224 | tf_op jit(solution)/shard_map/ppermute | solution.py:26
  349.2 7.1 %collective-permute-start.44 = (f32[1,4,1,64,128]{4,3,2,1,0:T(8,128)S(1)}, f32[1,4,1,64,128]{4,3,2,1,0:T(8,128)S(1)}, u32[]{:S(2)}, u32[]{:S(2)}) collective-permute-start(f32[1,4,1,64,128]{4,3,2,1,0:T(8,128)S(1)} %get-tuple-element.36), channel_id=1, source_target_pairs={{0,1},{1,2},{2,3},{4,5},{5,6},{6,7},{8,9},{9,10},{10,11},{12,13},{... | collective-permute-start | bytes 393224 | tf_op jit(solution)/shard_map/ppermute | solution.py:23
Sparse Core Ops, SparseCore 0:
  90.4 25.4 all-gather.4
  274.6 23.4 all-gather.6

commit v10 on v9

--- a/solution.py
+++ b/solution.py
@@ -265,8 +265,15 @@
             remaining = NU - 1
         else:
             correction = cycle(1, None, coarse_source)
-            values = values + prolong(correction)
-            remaining = NU
+            around = with_halo(correction, (("space", 2),), 1)
+            earlier = prolong(from_behind(correction, "tm", 1))
+            fine = prolong(around)[:, :, 1:-1]
+            applied = applied + stencil_apply(
+                fine, metrics[depth], earlier, spacing, pinned_levels[depth]
+            )
+            values = values + fine[:, :, 1:-1]
+            values = values + OMEGA * (source - applied) / diagonal
+            remaining = NU - 1
         for repeat in range(remaining):
             values = sweep(depth, values, source, diagonal)
         return values

time: 368 us -> 372 us (1.011)
    ppermute x15, waiting for transfers between devices: 10.3 us -> 14.1 us  [with_halo(): lax.ppermute(lax.slice_in_dim(block, 0, width, axis=dim), axis, backward)]
  transfers between devices with their start and end apart: 47 -> 47, of which waited for: 35 -> 33; matrix products, arithmetic and copies ran while one was open for 1% -> 1% of each run, Pallas kernels for 0% -> 0%
where the time goes in v10:
time: 372 us; the launch traced here: 369 us
  waiting for transfers between devices  128 us (34%)
  starting transfers between devices  116 us (31%)
  blocking collectives  46.5 us (12%)
  Pallas kernels  28.4 us (8%)
  local copies, waits for them, and re-layouts  18 us (5%)
  between operations  14.7 us (4%)
  other arithmetic  14.6 us (4%)
    ppermute x15, starting transfers between devices, with_halo(): lax.ppermute(lax.slice_in_dim(block, block.shape[dim] - width, None, axis...  68 us
    ppermute x15, waiting for transfers between devices, from_behind(): return lax.ppermute(array, axis, pairs)  52.9 us
    all_gather x2, waiting for transfers between devices, gather_all(): whole = lax.all_gather(across, 'space', axis=1, tiled=True)  50.4 us
    all_gather x2, blocking collectives, gather_all(): across = lax.all_gather(flat, 'tm', axis=0, tiled=True)  46.5 us
    ppermute x15, starting transfers between devices, from_behind(): return lax.ppermute(array, axis, pairs)  28.9 us
    pallas_call x2, Pallas kernels, coarse_solve(): pl.pallas_call(kernel, out_shape=jax.ShapeDtypeStruct(flat_source.shape,...  28.4 us
    ppermute x15, starting transfers between devices, with_halo(): lax.ppermute(lax.slice_in_dim(block, 0, width, axis=dim), axis, backward)  19.4 us
    ppermute x15, waiting for transfers between devices, with_halo(): lax.ppermute(lax.slice_in_dim(block, 0, width, axis=dim), axis, backward)  14.1 us
  transfers between devices with their start and end apart: 47, of which 33 were waited for; matrix products, arithmetic and copies ran while one was open for 1% of the time, Pallas kernels for 0%

profile of v10, /device:TPU:2, one launch (start us, length us, event | category | flops | bytes accessed | tf_op | source)
XLA Modules:
  0.0 369.4 jit_solution(9937040443591087256)
XLA Ops:
  9.8 2.1 collective-permute-start
  13.2 4.6 %collective-permute-start.2 = (f32[1,4,1,64,128]{4,3,2,1,0:T(8,128)S(1)}, f32[1,4,1,64,128]{4,3,2,1,0:T(8,128)S(1)}, u32[]{:S(2)}, u32[]{:S(2)}) collective-permute-start(f32[1,4,1,64,128]{4,3,2,1,0:T(8,128)S(1)} %get-tuple-element.68), channel_id=1, source_target_pairs={{0,1},{1,2},{2,3},{4,5},{5,6},{6,7},{8,9},{9,10},{10,11},{12,13},{... | collective-permute-start | bytes 393224 | tf_op jit(solution)/shard_map/ppermute | solution.py:23
  19.2 1.7 collective-permute-done.2
  21.2 1.3 collective-permute-done
  23.1 1.9 collective-permute-start.3
  26.3 4.6 %collective-permute-start.5 = (f32[1,4,1,64,128]{4,3,2,1,0:T(8,128)S(1)}, f32[1,4,1,64,128]{4,3,2,1,0:T(8,128)S(1)}, u32[]{:S(2)}, u32[]{:S(2)}) collective-permute-start(f32[1,4,1,64,128]{4,3,2,1,0:T(8,128)S(1)} %get-tuple-element.64), channel_id=1, source_target_pairs={{0,1},{1,2},{2,3},{4,5},{5,6},{6,7},{8,9},{9,10},{10,11},{12,13},{... | collective-permute-start | bytes 393224 | tf_op jit(solution)/shard_map/ppermute | solution.py:23
  30.9 2.2 collective-permute-done.4
  33.1 1.5 collective-permute-done.5
  38.8 4.5 %collective-permute-start.8 = (f32[1,4,1,32,64]{4,3,2,1,0:T(8,128)S(1)}, f32[1,4,1,32,64]{4,3,2,1,0:T(8,128)S(1)}, u32[]{:S(2)}, u32[]{:S(2)}) collective-permute-start(f32[1,4,1,32,64]{4,3,2,1,0:T(8,128)S(1)} %get-tuple-element.112), channel_id=1, source_target_pairs={{0,1},{1,2},{2,3},{4,5},{5,6},{6,7},{8,9},{9,10},{10,11},{12,13},{... | collective-permute-start | bytes 98312 | tf_op jit(solution)/shard_map/ppermute | solution.py:23
  43.4 1.9 collective-permute-start.6
  45.4 6.3 %collective-permute-done.6 = f32[1,4,2,32,64]{4,3,2,1,0:T(8,128)S(1)} collective-permute-done((f32[1,4,2,32,64]{4,3,2,1,0:T(8,128)S(1)}, f32[1,4,2,32,64]{4,3,2,1,0:T(8,128)S(1)}, u32[]{:S(2)}, u32[]{:S(2)}) %collective-permute-start.6) | collective-permute-done | bytes 65568 | tf_op jit(solution)/shard_map/ppermute | solution.py:34
  53.2 4.5 %collective-permute-start.11 = (f32[1,4,1,32,64]{4,3,2,1,0:T(8,128)S(1)}, f32[1,4,1,32,64]{4,3,2,1,0:T(8,128)S(1)}, u32[]{:S(2)}, u32[]{:S(2)}) collective-permute-start(f32[1,4,1,32,64]{4,3,2,1,0:T(8,128)S(1)} %get-tuple-element.108), channel_id=1, source_target_pairs={{0,1},{1,2},{2,3},{4,5},{5,6},{6,7},{8,9},{9,10},{10,11},{12,13},{... | collective-permute-start | bytes 98312 | tf_op jit(solution)/shard_map/ppermute | solution.py:23
  58.0 1.9 collective-permute-start.9
  60.1 6.3 %collective-permute-done.9 = f32[1,4,2,32,64]{4,3,2,1,0:T(8,128)S(1)} collective-permute-done((f32[1,4,2,32,64]{4,3,2,1,0:T(8,128)S(1)}, f32[1,4,2,32,64]{4,3,2,1,0:T(8,128)S(1)}, u32[]{:S(2)}, u32[]{:S(2)}) %collective-permute-start.9) | collective-permute-done | bytes 65568 | tf_op jit(solution)/shard_map/ppermute | solution.py:34
  67.0 23.3 %all-gather = f32[32,1,2560]{2,1,0:T(1,128)S(1)} all-gather(f32[1,1,2560]{2,1,0:T(1,128)S(1)} %maximum_bitcast_fusion.4), channel_id=1, replica_groups=mesh['tm'=32,'space'=4] {'tm'}, dimensions={0}, use_global_device_ids=true | all-gather | bytes 337920 | tf_op jit(solution)/shard_map/all_gather | solution.py:191
  91.2 25.6 %all-gather.5.cloned.1.call-done = f32[32,10240]{1,0:T(8,128)} async-done(((f32[32,2560]{1,0:T(8,128)}), f32[32,10240]{1,0:T(8,128)}) %all-gather.5.cloned.1.call-update) | async-done | bytes 1310736 | tf_op jit(solution)/shard_map/all_gather | solution.py:192
  116.8 1.7 reshape.883
  119.6 2.5 reshape_transpose_reshape.7.src_ref
  123.8 14.2 %shard_map.37 = f32[32,16,512]{2,1,0:T(8,128)} custom-call(f32[32,16,512]{2,1,0:T(8,128)} %reshape_transpose_reshape.7.src_ref, f32[32,16,512]{2,1,0:T(8,128)} %reshape.884.met_ref), custom_call_target="tpu_custom_call" | custom-call | tf_op jit(solution)/shard_map/pallas_call | solution.py:161
  142.1 4.5 %collective-permute-start.14 = (f32[1,4,1,32,64]{4,3,2,1,0:T(8,128)S(1)}, f32[1,4,1,32,64]{4,3,2,1,0:T(8,128)S(1)}, u32[]{:S(2)}, u32[]{:S(2)}) collective-permute-start(f32[1,4,1,32,64]{4,3,2,1,0:T(8,128)S(1)} %get-tuple-element.104), channel_id=1, source_target_pairs={{0,1},{1,2},{2,3},{4,5},{5,6},{6,7},{8,9},{9,10},{10,11},{12,13},{... | collective-permute-start | bytes 98312 | tf_op jit(solution)/shard_map/ppermute | solution.py:23
  146.7 1.9 collective-permute-start.12
  148.7 6.3 %collective-permute-done.12 = f32[1,4,2,32,64]{4,3,2,1,0:T(8,128)S(1)} collective-permute-done((f32[1,4,2,32,64]{4,3,2,1,0:T(8,128)S(1)}, f32[1,4,2,32,64]{4,3,2,1,0:T(8,128)S(1)}, u32[]{:S(2)}, u32[]{:S(2)}) %collective-permute-start.12) | collective-permute-done | bytes 65568 | tf_op jit(solution)/shard_map/ppermute | solution.py:34
  155.3 2.7 collective-permute-start.15
  159.3 1.9 collective-permute-start.17
  161.2 2.9 collective-permute-done.16
  165.0 2.7 collective-permute-done.17
  168.7 1.9 collective-permute-start.18
  172.0 5.2 %collective-permute-start.20 = (f32[1,4,1,64,128]{4,3,2,1,0:T(8,128)S(1)}, f32[1,4,1,64,128]{4,3,2,1,0:T(8,128)S(1)}, u32[]{:S(2)}, u32[]{:S(2)}) collective-permute-start(f32[1,4,1,64,128]{4,3,2,1,0:T(8,128)S(1)} %get-tuple-element.60), channel_id=1, source_target_pairs={{0,1},{1,2},{2,3},{4,5},{5,6},{6,7},{8,9},{9,10},{10,11},{12,13},{... | collective-permute-start | bytes 393224 | tf_op jit(solution)/shard_map/ppermute | solution.py:23
  178.2 1.5 collective-permute-done.20
  179.9 1.5 collective-permute-done.18
  181.9 1.9 collective-permute-start.21
  185.2 5.4 %collective-permute-start.23 = (f32[1,4,1,64,128]{4,3,2,1,0:T(8,128)S(1)}, f32[1,4,1,64,128]{4,3,2,1,0:T(8,128)S(1)}, u32[]{:S(2)}, u32[]{:S(2)}) collective-permute-start(f32[1,4,1,64,128]{4,3,2,1,0:T(8,128)S(1)} %get-tuple-element.56), channel_id=1, source_target_pairs={{0,1},{1,2},{2,3},{4,5},{5,6},{6,7},{8,9},{9,10},{10,11},{12,13},{... | collective-permute-start | bytes 393224 | tf_op jit(solution)/shard_map/ppermute | solution.py:23
  191.3 1.5 collective-permute-done.23
  193.0 1.5 collective-permute-done.21
  195.1 1.9 collective-permute-start.24
  198.3 5.2 %collective-permute-start.26 = (f32[1,4,1,64,128]{4,3,2,1,0:T(8,128)S(1)}, f32[1,4,1,64,128]{4,3,2,1,0:T(8,128)S(1)}, u32[]{:S(2)}, u32[]{:S(2)}) collective-permute-start(f32[1,4,1,64,128]{4,3,2,1,0:T(8,128)S(1)} %get-tuple-element.52), channel_id=1, source_target_pairs={{0,1},{1,2},{2,3},{4,5},{5,6},{6,7},{8,9},{9,10},{10,11},{12,13},{... | collective-permute-start | bytes 393224 | tf_op jit(solution)/shard_map/ppermute | solution.py:23
  204.5 1.5 collective-permute-done.26
  206.2 1.5 collective-permute-done.24
  208.2 1.9 collective-permute-start.27
  211.5 5.2 %collective-permute-start.29 = (f32[1,4,1,64,128]{4,3,2,1,0:T(8,128)S(1)}, f32[1,4,1,64,128]{4,3,2,1,0:T(8,128)S(1)}, u32[]{:S(2)}, u32[]{:S(2)}) collective-permute-start(f32[1,4,1,64,128]{4,3,2,1,0:T(8,128)S(1)} %get-tuple-element.48), channel_id=1, source_target_pairs={{0,1},{1,2},{2,3},{4,5},{5,6},{6,7},{8,9},{9,10},{10,11},{12,13},{... | collective-permute-start | bytes 393224 | tf_op jit(solution)/shard_map/ppermute | solution.py:23
  217.7 1.5 collective-permute-done.29
  219.4 1.5 collective-permute-done.27
  223.9 5.2 %collective-permute-start.32 = (f32[1,4,1,32,64]{4,3,2,1,0:T(8,128)S(1)}, f32[1,4,1,32,64]{4,3,2,1,0:T(8,128)S(1)}, u32[]{:S(2)}, u32[]{:S(2)}) collective-permute-start(f32[1,4,1,32,64]{4,3,2,1,0:T(8,128)S(1)} %get-tuple-element.98), channel_id=1, source_target_pairs={{0,1},{1,2},{2,3},{4,5},{5,6},{6,7},{8,9},{9,10},{10,11},{12,13},{... | collective-permute-start | bytes 98312 | tf_op jit(solution)/shard_map/ppermute | solution.py:23
  229.1 1.9 collective-permute-start.30
  231.2 6.3 %collective-permute-done.30 = f32[1,4,2,32,64]{4,3,2,1,0:T(8,128)S(1)} collective-permute-done((f32[1,4,2,32,64]{4,3,2,1,0:T(8,128)S(1)}, f32[1,4,2,32,64]{4,3,2,1,0:T(8,128)S(1)}, u32[]{:S(2)}, u32[]{:S(2)}) %collective-permute-start.30) | collective-permute-done | bytes 65568 | tf_op jit(solution)/shard_map/ppermute | solution.py:34
  239.0 4.6 %collective-permute-start.35 = (f32[1,4,1,32,64]{4,3,2,1,0:T(8,128)S(1)}, f32[1,4,1,32,64]{4,3,2,1,0:T(8,128)S(1)}, u32[]{:S(2)}, u32[]{:S(2)}) collective-permute-start(f32[1,4,1,32,64]{4,3,2,1,0:T(8,128)S(1)} %get-tuple-element.94), channel_id=1, source_target_pairs={{0,1},{1,2},{2,3},{4,5},{5,6},{6,7},{8,9},{9,10},{10,11},{12,13},{... | collective-permute-start | bytes 98312 | tf_op jit(solution)/shard_map/ppermute | solution.py:23
  243.5 1.9 collective-permute-start.33
  245.6 6.3 %collective-permute-done.33 = f32[1,4,2,32,64]{4,3,2,1,0:T(8,128)S(1)} collective-permute-done((f32[1,4,2,32,64]{4,3,2,1,0:T(8,128)S(1)}, f32[1,4,2,32,64]{4,3,2,1,0:T(8,128)S(1)}, u32[]{:S(2)}, u32[]{:S(2)}) %collective-permute-start.33) | collective-permute-done | bytes 65568 | tf_op jit(solution)/shard_map/ppermute | solution.py:34
  252.6 23.3 %all-gather.1 = f32[32,1,2048]{2,1,0:T(1,128)S(1)} all-gather(f32[1,1,2048]{2,1,0:T(1,128)S(1)} %reshape.906), channel_id=1, replica_groups=mesh['tm'=32,'space'=4] {'tm'}, dimensions={0}, use_global_device_ids=true | all-gather | bytes 270336 | tf_op jit(solution)/shard_map/all_gather | solution.py:191
  276.6 24.8 %all-gather.7.cloned.1.call-done = f32[32,8192]{1,0:T(8,128)} async-done(((f32[32,2048]{1,0:T(8,128)}), f32[32,8192]{1,0:T(8,128)}) %all-gather.7.cloned.1.call-update) | async-done | bytes 1048592 | tf_op jit(solution)/shard_map/all_gather | solution.py:192
  301.5 2.8 copy.22
  304.3 14.2 %shard_map.38 = f32[32,16,512]{2,1,0:T(8,128)} custom-call(f32[32,16,512]{2,1,0:T(8,128)} %bitcast.126, f32[32,16,512]{2,1,0:T(8,128)} %reshape.884.met_ref), custom_call_target="tpu_custom_call" | custom-call | tf_op jit(solution)/shard_map/pallas_call | solution.py:161
  322.6 4.5 %collective-permute-start.38 = (f32[1,4,1,32,64]{4,3,2,1,0:T(8,128)S(1)}, f32[1,4,1,32,64]{4,3,2,1,0:T(8,128)S(1)}, u32[]{:S(2)}, u32[]{:S(2)}) collective-permute-start(f32[1,4,1,32,64]{4,3,2,1,0:T(8,128)S(1)} %get-tuple-element.90), channel_id=1, source_target_pairs={{0,1},{1,2},{2,3},{4,5},{5,6},{6,7},{8,9},{9,10},{10,11},{12,13},{... | collective-permute-start | bytes 98312 | tf_op jit(solution)/shard_map/ppermute | solution.py:23
  327.2 1.9 collective-permute-start.36
  329.2 6.3 %collective-permute-done.36 = f32[1,4,2,32,64]{4,3,2,1,0:T(8,128)S(1)} collective-permute-done((f32[1,4,2,32,64]{4,3,2,1,0:T(8,128)S(1)}, f32[1,4,2,32,64]{4,3,2,1,0:T(8,128)S(1)}, u32[]{:S(2)}, u32[]{:S(2)}) %collective-permute-start.36) | collective-permute-done | bytes 65568 | tf_op jit(solution)/shard_map/ppermute | solution.py:34
  335.7 2.1 collective-permute-start.39
  339.2 1.9 collective-permute-start.41
  341.1 2.9 collective-permute-done.40
  344.9 2.7 collective-permute-done.41
  348.6 1.9 collective-permute-start.42
  351.9 5.2 %collective-permute-start.44 = (f32[1,4,1,64,128]{4,3,2,1,0:T(8,128)S(1)}, f32[1,4,1,64,128]{4,3,2,1,0:T(8,128)S(1)}, u32[]{:S(2)}, u32[]{:S(2)}) collective-permute-start(f32[1,4,1,64,128]{4,3,2,1,0:T(8,128)S(1)} %get-tuple-element.44), channel_id=1, source_target_pairs={{0,1},{1,2},{2,3},{4,5},{5,6},{6,7},{8,9},{9,10},{10,11},{12,13},{... | collective-permute-start | bytes 393224 | tf_op jit(solution)/shard_map/ppermute | solution.py:23
  358.1 1.5 collective-permute-done.44
  359.8 1.5 collective-permute-done.42
  361.2 1.3 fusion.11
  (176 shorter events, 53.3 us)
Async XLA Ops:
  6.5 110.2 %all-gather.5.cloned.1.call-start = ((), (), s32[]{:S(2)}) async-start(), calls=%async_computation | async-start | bytes 1638400 | tf_op jit(solution)/shard_map/all_gather | solution.py:192
  7.5 10.2 %copy-start.3 = (f32[1,4,64,128]{3,2,1,0:T(8,128)S(1)}, f32[1,4,64,128]{3,2,1,0:T(8,128)}, u32[]{:S(2)}) copy-start(f32[1,4,64,128]{3,2,1,0:T(8,128)} %param.4) | copy-start | bytes 393220
  9.8 12.8 %copy-start = (f32[1,4,4,64,128]{4,3,2,1,0:T(8,128)S(1)}, f32[1,4,4,64,128]{4,3,2,1,0:T(8,128)}, u32[]{:S(2)}) copy-start(f32[1,4,4,64,128]{4,3,2,1,0:T(8,128)} %param.3) | copy-start | bytes 1572868
  9.8 12.7 %collective-permute-start = (f32[1,4,4,64,128]{4,3,2,1,0:T(8,128)S(1)}, f32[1,4,4,64,128]{4,3,2,1,0:T(8,128)S(1)}, u32[]{:S(2)}, u32[]{:S(2)}) collective-permute-start(f32[1,4,4,64,128]{4,3,2,1,0:T(8,128)S(1)} %get-tuple-element.13), channel_id=1, source_target_pairs={{0,4},{4,8},{8,12},{12,16},{16,20},{20,24},{24,28},{28,32},{32,36}... | collective-permute-start | bytes 1572872 | tf_op jit(solution)/shard_map/ppermute | solution.py:34
  11.9 7.4 %collective-permute-start.1 = (f32[1,4,1,64,128]{4,3,2,1,0:T(8,128)S(1)}, f32[1,4,1,64,128]{4,3,2,1,0:T(8,128)S(1)}, u32[]{:S(2)}, u32[]{:S(2)}) collective-permute-start(f32[1,4,1,64,128]{4,3,2,1,0:T(8,128)S(1)} %get-tuple-element.67), channel_id=1, source_target_pairs={{1,0},{2,1},{3,2},{5,4},{6,5},{7,6},{9,8},{10,9},{11,10},{13,12},{... | collective-permute-start | bytes 393224 | tf_op jit(solution)/shard_map/ppermute | solution.py:26
  13.2 7.8 %collective-permute-start.2 = (f32[1,4,1,64,128]{4,3,2,1,0:T(8,128)S(1)}, f32[1,4,1,64,128]{4,3,2,1,0:T(8,128)S(1)}, u32[]{:S(2)}, u32[]{:S(2)}) collective-permute-start(f32[1,4,1,64,128]{4,3,2,1,0:T(8,128)S(1)} %get-tuple-element.68), channel_id=1, source_target_pairs={{0,1},{1,2},{2,3},{4,5},{5,6},{6,7},{8,9},{9,10},{10,11},{12,13},{... | collective-permute-start | bytes 393224 | tf_op jit(solution)/shard_map/ppermute | solution.py:23
  23.1 12.6 %collective-permute-start.3 = (f32[1,4,4,64,128]{4,3,2,1,0:T(8,128)S(1)}, f32[1,4,4,64,128]{4,3,2,1,0:T(8,128)S(1)}, u32[]{:S(2)}, u32[]{:S(2)}) collective-permute-start(f32[1,4,4,64,128]{4,3,2,1,0:T(8,128)S(1)} %fusion.89), channel_id=1, source_target_pairs={{0,4},{4,8},{8,12},{12,16},{16,20},{20,24},{24,28},{28,32},{32,36}... | collective-permute-start | bytes 1572872 | tf_op jit(solution)/shard_map/ppermute | solution.py:34
  25.0 8.1 %collective-permute-start.4 = (f32[1,4,1,64,128]{4,3,2,1,0:T(8,128)S(1)}, f32[1,4,1,64,128]{4,3,2,1,0:T(8,128)S(1)}, u32[]{:S(2)}, u32[]{:S(2)}) collective-permute-start(f32[1,4,1,64,128]{4,3,2,1,0:T(8,128)S(1)} %get-tuple-element.63), channel_id=1, source_target_pairs={{1,0},{2,1},{3,2},{5,4},{6,5},{7,6},{9,8},{10,9},{11,10},{13,12},{... | collective-permute-start | bytes 393224 | tf_op jit(solution)/shard_map/ppermute | solution.py:26
  26.3 8.3 %collective-permute-start.5 = (f32[1,4,1,64,128]{4,3,2,1,0:T(8,128)S(1)}, f32[1,4,1,64,128]{4,3,2,1,0:T(8,128)S(1)}, u32[]{:S(2)}, u32[]{:S(2)}) collective-permute-start(f32[1,4,1,64,128]{4,3,2,1,0:T(8,128)S(1)} %get-tuple-element.64), channel_id=1, source_target_pairs={{0,1},{1,2},{2,3},{4,5},{5,6},{6,7},{8,9},{9,10},{10,11},{12,13},{... | collective-permute-start | bytes 393224 | tf_op jit(solution)/shard_map/ppermute | solution.py:23
  37.5 7.8 %collective-permute-start.7 = (f32[1,4,1,32,64]{4,3,2,1,0:T(8,128)S(1)}, f32[1,4,1,32,64]{4,3,2,1,0:T(8,128)S(1)}, u32[]{:S(2)}, u32[]{:S(2)}) collective-permute-start(f32[1,4,1,32,64]{4,3,2,1,0:T(8,128)S(1)} %get-tuple-element.111), channel_id=1, source_target_pairs={{1,0},{2,1},{3,2},{5,4},{6,5},{7,6},{9,8},{10,9},{11,10},{13,12},{... | collective-permute-start | bytes 98312 | tf_op jit(solution)/shard_map/ppermute | solution.py:26
  38.8 6.5 %collective-permute-start.8 = (f32[1,4,1,32,64]{4,3,2,1,0:T(8,128)S(1)}, f32[1,4,1,32,64]{4,3,2,1,0:T(8,128)S(1)}, u32[]{:S(2)}, u32[]{:S(2)}) collective-permute-start(f32[1,4,1,32,64]{4,3,2,1,0:T(8,128)S(1)} %get-tuple-element.112), channel_id=1, source_target_pairs={{0,1},{1,2},{2,3},{4,5},{5,6},{6,7},{8,9},{9,10},{10,11},{12,13},{... | collective-permute-start | bytes 98312 | tf_op jit(solution)/shard_map/ppermute | solution.py:23
  43.4 8.4 %collective-permute-start.6 = (f32[1,4,2,32,64]{4,3,2,1,0:T(8,128)S(1)}, f32[1,4,2,32,64]{4,3,2,1,0:T(8,128)S(1)}, u32[]{:S(2)}, u32[]{:S(2)}) collective-permute-start(f32[1,4,2,32,64]{4,3,2,1,0:T(8,128)S(1)} %fusion.366), channel_id=1, source_target_pairs={{0,4},{4,8},{8,12},{12,16},{16,20},{20,24},{24,28},{28,32},{32,36}... | collective-permute-start | bytes 196616 | tf_op jit(solution)/shard_map/ppermute | solution.py:34
  51.9 8.0 %collective-permute-start.10 = (f32[1,4,1,32,64]{4,3,2,1,0:T(8,128)S(1)}, f32[1,4,1,32,64]{4,3,2,1,0:T(8,128)S(1)}, u32[]{:S(2)}, u32[]{:S(2)}) collective-permute-start(f32[1,4,1,32,64]{4,3,2,1,0:T(8,128)S(1)} %get-tuple-element.107), channel_id=1, source_target_pairs={{1,0},{2,1},{3,2},{5,4},{6,5},{7,6},{9,8},{10,9},{11,10},{13,12},{... | collective-permute-start | bytes 98312 | tf_op jit(solution)/shard_map/ppermute | solution.py:26
  53.2 6.7 %collective-permute-start.11 = (f32[1,4,1,32,64]{4,3,2,1,0:T(8,128)S(1)}, f32[1,4,1,32,64]{4,3,2,1,0:T(8,128)S(1)}, u32[]{:S(2)}, u32[]{:S(2)}) collective-permute-start(f32[1,4,1,32,64]{4,3,2,1,0:T(8,128)S(1)} %get-tuple-element.108), channel_id=1, source_target_pairs={{0,1},{1,2},{2,3},{4,5},{5,6},{6,7},{8,9},{9,10},{10,11},{12,13},{... | collective-permute-start | bytes 98312 | tf_op jit(solution)/shard_map/ppermute | solution.py:23
  58.0 8.4 %collective-permute-start.9 = (f32[1,4,2,32,64]{4,3,2,1,0:T(8,128)S(1)}, f32[1,4,2,32,64]{4,3,2,1,0:T(8,128)S(1)}, u32[]{:S(2)}, u32[]{:S(2)}) collective-permute-start(f32[1,4,2,32,64]{4,3,2,1,0:T(8,128)S(1)} %fusion.209), channel_id=1, source_target_pairs={{0,4},{4,8},{8,12},{12,16},{16,20},{20,24},{24,28},{28,32},{32,36}... | collective-permute-start | bytes 196616 | tf_op jit(solution)/shard_map/ppermute | solution.py:34
  91.1 210.3 %all-gather.7.cloned.1.call-start = ((), (), s32[]{:S(2)}) async-start(), calls=%async_computation.1 | async-start | bytes 1310720 | tf_op jit(solution)/shard_map/all_gather | solution.py:192
  140.8 7.8 %collective-permute-start.13 = (f32[1,4,1,32,64]{4,3,2,1,0:T(8,128)S(1)}, f32[1,4,1,32,64]{4,3,2,1,0:T(8,128)S(1)}, u32[]{:S(2)}, u32[]{:S(2)}) collective-permute-start(f32[1,4,1,32,64]{4,3,2,1,0:T(8,128)S(1)} %get-tuple-element.103), channel_id=1, source_target_pairs={{1,0},{2,1},{3,2},{5,4},{6,5},{7,6},{9,8},{10,9},{11,10},{13,12},{... | collective-permute-start | bytes 98312 | tf_op jit(solution)/shard_map/ppermute | solution.py:26
  142.1 6.5 %collective-permute-start.14 = (f32[1,4,1,32,64]{4,3,2,1,0:T(8,128)S(1)}, f32[1,4,1,32,64]{4,3,2,1,0:T(8,128)S(1)}, u32[]{:S(2)}, u32[]{:S(2)}) collective-permute-start(f32[1,4,1,32,64]{4,3,2,1,0:T(8,128)S(1)} %get-tuple-element.104), channel_id=1, source_target_pairs={{0,1},{1,2},{2,3},{4,5},{5,6},{6,7},{8,9},{9,10},{10,11},{12,13},{... | collective-permute-start | bytes 98312 | tf_op jit(solution)/shard_map/ppermute | solution.py:23
  146.7 8.4 %collective-permute-start.12 = (f32[1,4,2,32,64]{4,3,2,1,0:T(8,128)S(1)}, f32[1,4,2,32,64]{4,3,2,1,0:T(8,128)S(1)}, u32[]{:S(2)}, u32[]{:S(2)}) collective-permute-start(f32[1,4,2,32,64]{4,3,2,1,0:T(8,128)S(1)} %fusion.223), channel_id=1, source_target_pairs={{0,4},{4,8},{8,12},{12,16},{16,20},{20,24},{24,28},{28,32},{32,36}... | collective-permute-start | bytes 196616 | tf_op jit(solution)/shard_map/ppermute | solution.py:34
  155.3 6.0 %collective-permute-start.15 = (f32[1,4,1,32,64]{4,3,2,1,0:T(8,128)S(1)}, f32[1,4,1,32,64]{4,3,2,1,0:T(8,128)S(1)}, u32[]{:S(2)}, u32[]{:S(2)}) collective-permute-start(f32[1,4,1,32,64]{4,3,2,1,0:T(8,128)S(1)} %get-tuple-element.99), channel_id=1, source_target_pairs={{0,1},{1,2},{2,3},{4,5},{5,6},{6,7},{8,9},{9,10},{10,11},{12,13},{... | collective-permute-start | bytes 98312 | tf_op jit(solution)/shard_map/ppermute | solution.py:23
  158.0 6.2 %collective-permute-start.16 = (f32[1,4,1,32,64]{4,3,2,1,0:T(8,128)S(1)}, f32[1,4,1,32,64]{4,3,2,1,0:T(8,128)S(1)}, u32[]{:S(2)}, u32[]{:S(2)}) collective-permute-start(f32[1,4,1,32,64]{4,3,2,1,0:T(8,128)S(1)} %get-tuple-element.100), channel_id=1, source_target_pairs={{1,0},{2,1},{3,2},{5,4},{6,5},{7,6},{9,8},{10,9},{11,10},{13,12},{... | collective-permute-start | bytes 98312 | tf_op jit(solution)/shard_map/ppermute | solution.py:26
  159.3 8.4 %collective-permute-start.17 = (f32[1,4,2,32,64]{4,3,2,1,0:T(8,128)S(1)}, f32[1,4,2,32,64]{4,3,2,1,0:T(8,128)S(1)}, u32[]{:S(2)}, u32[]{:S(2)}) collective-permute-start(f32[1,4,2,32,64]{4,3,2,1,0:T(8,128)S(1)} %fusion.183), channel_id=1, source_target_pairs={{0,4},{4,8},{8,12},{12,16},{16,20},{20,24},{24,28},{28,32},{32,36}... | collective-permute-start | bytes 196616 | tf_op jit(solution)/shard_map/ppermute | solution.py:34
  164.8 3.3 copy-start.1
  168.7 12.6 %collective-permute-start.18 = (f32[1,4,4,64,128]{4,3,2,1,0:T(8,128)S(1)}, f32[1,4,4,64,128]{4,3,2,1,0:T(8,128)S(1)}, u32[]{:S(2)}, u32[]{:S(2)}) collective-permute-start(f32[1,4,4,64,128]{4,3,2,1,0:T(8,128)S(1)} %fusion.92), channel_id=1, source_target_pairs={{0,4},{4,8},{8,12},{12,16},{16,20},{20,24},{24,28},{28,32},{32,36}... | collective-permute-start | bytes 1572872 | tf_op jit(solution)/shard_map/ppermute | solution.py:34
  170.7 7.5 %collective-permute-start.19 = (f32[1,4,1,64,128]{4,3,2,1,0:T(8,128)S(1)}, f32[1,4,1,64,128]{4,3,2,1,0:T(8,128)S(1)}, u32[]{:S(2)}, u32[]{:S(2)}) collective-permute-start(f32[1,4,1,64,128]{4,3,2,1,0:T(8,128)S(1)} %get-tuple-element.59), channel_id=1, source_target_pairs={{1,0},{2,1},{3,2},{5,4},{6,5},{7,6},{9,8},{10,9},{11,10},{13,12},{... | collective-permute-start | bytes 393224 | tf_op jit(solution)/shard_map/ppermute | solution.py:26
  172.0 7.7 %collective-permute-start.20 = (f32[1,4,1,64,128]{4,3,2,1,0:T(8,128)S(1)}, f32[1,4,1,64,128]{4,3,2,1,0:T(8,128)S(1)}, u32[]{:S(2)}, u32[]{:S(2)}) collective-permute-start(f32[1,4,1,64,128]{4,3,2,1,0:T(8,128)S(1)} %get-tuple-element.60), channel_id=1, source_target_pairs={{0,1},{1,2},{2,3},{4,5},{5,6},{6,7},{8,9},{9,10},{10,11},{12,13},{... | collective-permute-start | bytes 393224 | tf_op jit(solution)/shard_map/ppermute | solution.py:23
  181.9 12.6 %collective-permute-start.21 = (f32[1,4,4,64,128]{4,3,2,1,0:T(8,128)S(1)}, f32[1,4,4,64,128]{4,3,2,1,0:T(8,128)S(1)}, u32[]{:S(2)}, u32[]{:S(2)}) collective-permute-start(f32[1,4,4,64,128]{4,3,2,1,0:T(8,128)S(1)} %fusion.64), channel_id=1, source_target_pairs={{0,4},{4,8},{8,12},{12,16},{16,20},{20,24},{24,28},{28,32},{32,36}... | collective-permute-start | bytes 1572872 | tf_op jit(solution)/shard_map/ppermute | solution.py:34
  183.9 7.5 %collective-permute-start.22 = (f32[1,4,1,64,128]{4,3,2,1,0:T(8,128)S(1)}, f32[1,4,1,64,128]{4,3,2,1,0:T(8,128)S(1)}, u32[]{:S(2)}, u32[]{:S(2)}) collective-permute-start(f32[1,4,1,64,128]{4,3,2,1,0:T(8,128)S(1)} %get-tuple-element.55), channel_id=1, source_target_pairs={{1,0},{2,1},{3,2},{5,4},{6,5},{7,6},{9,8},{10,9},{11,10},{13,12},{... | collective-permute-start | bytes 393224 | tf_op jit(solution)/shard_map/ppermute | solution.py:26
  185.2 7.7 %collective-permute-start.23 = (f32[1,4,1,64,128]{4,3,2,1,0:T(8,128)S(1)}, f32[1,4,1,64,128]{4,3,2,1,0:T(8,128)S(1)}, u32[]{:S(2)}, u32[]{:S(2)}) collective-permute-start(f32[1,4,1,64,128]{4,3,2,1,0:T(8,128)S(1)} %get-tuple-element.56), channel_id=1, source_target_pairs={{0,1},{1,2},{2,3},{4,5},{5,6},{6,7},{8,9},{9,10},{10,11},{12,13},{... | collective-permute-start | bytes 393224 | tf_op jit(solution)/shard_map/ppermute | solution.py:23
  195.1 12.6 %collective-permute-start.24 = (f32[1,4,4,64,128]{4,3,2,1,0:T(8,128)S(1)}, f32[1,4,4,64,128]{4,3,2,1,0:T(8,128)S(1)}, u32[]{:S(2)}, u32[]{:S(2)}) collective-permute-start(f32[1,4,4,64,128]{4,3,2,1,0:T(8,128)S(1)} %fusion.50), channel_id=1, source_target_pairs={{0,4},{4,8},{8,12},{12,16},{16,20},{20,24},{24,28},{28,32},{32,36}... | collective-permute-start | bytes 1572872 | tf_op jit(solution)/shard_map/ppermute | solution.py:34
  197.0 7.5 %collective-permute-start.25 = (f32[1,4,1,64,128]{4,3,2,1,0:T(8,128)S(1)}, f32[1,4,1,64,128]{4,3,2,1,0:T(8,128)S(1)}, u32[]{:S(2)}, u32[]{:S(2)}) collective-permute-start(f32[1,4,1,64,128]{4,3,2,1,0:T(8,128)S(1)} %get-tuple-element.51), channel_id=1, source_target_pairs={{1,0},{2,1},{3,2},{5,4},{6,5},{7,6},{9,8},{10,9},{11,10},{13,12},{... | collective-permute-start | bytes 393224 | tf_op jit(solution)/shard_map/ppermute | solution.py:26
  198.3 7.7 %collective-permute-start.26 = (f32[1,4,1,64,128]{4,3,2,1,0:T(8,128)S(1)}, f32[1,4,1,64,128]{4,3,2,1,0:T(8,128)S(1)}, u32[]{:S(2)}, u32[]{:S(2)}) collective-permute-start(f32[1,4,1,64,128]{4,3,2,1,0:T(8,128)S(1)} %get-tuple-element.52), channel_id=1, source_target_pairs={{0,1},{1,2},{2,3},{4,5},{5,6},{6,7},{8,9},{9,10},{10,11},{12,13},{... | collective-permute-start | bytes 393224 | tf_op jit(solution)/shard_map/ppermute | solution.py:23
  208.2 12.6 %collective-permute-start.27 = (f32[1,4,4,64,128]{4,3,2,1,0:T(8,128)S(1)}, f32[1,4,4,64,128]{4,3,2,1,0:T(8,128)S(1)}, u32[]{:S(2)}, u32[]{:S(2)}) collective-permute-start(f32[1,4,4,64,128]{4,3,2,1,0:T(8,128)S(1)} %fusion.36), channel_id=1, source_target_pairs={{0,4},{4,8},{8,12},{12,16},{16,20},{20,24},{24,28},{28,32},{32,36}... | collective-permute-start | bytes 1572872 | tf_op jit(solution)/shard_map/ppermute | solution.py:34
  210.2 7.5 %collective-permute-start.28 = (f32[1,4,1,64,128]{4,3,2,1,0:T(8,128)S(1)}, f32[1,4,1,64,128]{4,3,2,1,0:T(8,128)S(1)}, u32[]{:S(2)}, u32[]{:S(2)}) collective-permute-start(f32[1,4,1,64,128]{4,3,2,1,0:T(8,128)S(1)} %get-tuple-element.47), channel_id=1, source_target_pairs={{1,0},{2,1},{3,2},{5,4},{6,5},{7,6},{9,8},{10,9},{11,10},{13,12},{... | collective-permute-start | bytes 393224 | tf_op jit(solution)/shard_map/ppermute | solution.py:26
  211.5 7.7 %collective-permute-start.29 = (f32[1,4,1,64,128]{4,3,2,1,0:T(8,128)S(1)}, f32[1,4,1,64,128]{4,3,2,1,0:T(8,128)S(1)}, u32[]{:S(2)}, u32[]{:S(2)}) collective-permute-start(f32[1,4,1,64,128]{4,3,2,1,0:T(8,128)S(1)} %get-tuple-element.48), channel_id=1, source_target_pairs={{0,1},{1,2},{2,3},{4,5},{5,6},{6,7},{8,9},{9,10},{10,11},{12,13},{... | collective-permute-start | bytes 393224 | tf_op jit(solution)/shard_map/ppermute | solution.py:23
  222.6 8.4 %collective-permute-start.31 = (f32[1,4,1,32,64]{4,3,2,1,0:T(8,128)S(1)}, f32[1,4,1,32,64]{4,3,2,1,0:T(8,128)S(1)}, u32[]{:S(2)}, u32[]{:S(2)}) collective-permute-start(f32[1,4,1,32,64]{4,3,2,1,0:T(8,128)S(1)} %get-tuple-element.97), channel_id=1, source_target_pairs={{1,0},{2,1},{3,2},{5,4},{6,5},{7,6},{9,8},{10,9},{11,10},{13,12},{... | collective-permute-start | bytes 98312 | tf_op jit(solution)/shard_map/ppermute | solution.py:26
  223.9 7.1 %collective-permute-start.32 = (f32[1,4,1,32,64]{4,3,2,1,0:T(8,128)S(1)}, f32[1,4,1,32,64]{4,3,2,1,0:T(8,128)S(1)}, u32[]{:S(2)}, u32[]{:S(2)}) collective-permute-start(f32[1,4,1,32,64]{4,3,2,1,0:T(8,128)S(1)} %get-tuple-element.98), channel_id=1, source_target_pairs={{0,1},{1,2},{2,3},{4,5},{5,6},{6,7},{8,9},{9,10},{10,11},{12,13},{... | collective-permute-start | bytes 98312 | tf_op jit(solution)/shard_map/ppermute | solution.py:23
  229.1 8.4 %collective-permute-start.30 = (f32[1,4,2,32,64]{4,3,2,1,0:T(8,128)S(1)}, f32[1,4,2,32,64]{4,3,2,1,0:T(8,128)S(1)}, u32[]{:S(2)}, u32[]{:S(2)}) collective-permute-start(f32[1,4,2,32,64]{4,3,2,1,0:T(8,128)S(1)} %fusion.367), channel_id=1, source_target_pairs={{0,4},{4,8},{8,12},{12,16},{16,20},{20,24},{24,28},{28,32},{32,36}... | collective-permute-start | bytes 196616 | tf_op jit(solution)/shard_map/ppermute | solution.py:34
  237.7 7.8 %collective-permute-start.34 = (f32[1,4,1,32,64]{4,3,2,1,0:T(8,128)S(1)}, f32[1,4,1,32,64]{4,3,2,1,0:T(8,128)S(1)}, u32[]{:S(2)}, u32[]{:S(2)}) collective-permute-start(f32[1,4,1,32,64]{4,3,2,1,0:T(8,128)S(1)} %get-tuple-element.93), channel_id=1, source_target_pairs={{1,0},{2,1},{3,2},{5,4},{6,5},{7,6},{9,8},{10,9},{11,10},{13,12},{... | collective-permute-start | bytes 98312 | tf_op jit(solution)/shard_map/ppermute | solution.py:26
  239.0 6.5 %collective-permute-start.35 = (f32[1,4,1,32,64]{4,3,2,1,0:T(8,128)S(1)}, f32[1,4,1,32,64]{4,3,2,1,0:T(8,128)S(1)}, u32[]{:S(2)}, u32[]{:S(2)}) collective-permute-start(f32[1,4,1,32,64]{4,3,2,1,0:T(8,128)S(1)} %get-tuple-element.94), channel_id=1, source_target_pairs={{0,1},{1,2},{2,3},{4,5},{5,6},{6,7},{8,9},{9,10},{10,11},{12,13},{... | collective-permute-start | bytes 98312 | tf_op jit(solution)/shard_map/ppermute | solution.py:23
  243.5 8.4 %collective-permute-start.33 = (f32[1,4,2,32,64]{4,3,2,1,0:T(8,128)S(1)}, f32[1,4,2,32,64]{4,3,2,1,0:T(8,128)S(1)}, u32[]{:S(2)}, u32[]{:S(2)}) collective-permute-start(f32[1,4,2,32,64]{4,3,2,1,0:T(8,128)S(1)} %fusion.168), channel_id=1, source_target_pairs={{0,4},{4,8},{8,12},{12,16},{16,20},{20,24},{24,28},{28,32},{32,36}... | collective-permute-start | bytes 196616 | tf_op jit(solution)/shard_map/ppermute | solution.py:34
  321.3 7.8 %collective-permute-start.37 = (f32[1,4,1,32,64]{4,3,2,1,0:T(8,128)S(1)}, f32[1,4,1,32,64]{4,3,2,1,0:T(8,128)S(1)}, u32[]{:S(2)}, u32[]{:S(2)}) collective-permute-start(f32[1,4,1,32,64]{4,3,2,1,0:T(8,128)S(1)} %get-tuple-element.89), channel_id=1, source_target_pairs={{1,0},{2,1},{3,2},{5,4},{6,5},{7,6},{9,8},{10,9},{11,10},{13,12},{... | collective-permute-start | bytes 98312 | tf_op jit(solution)/shard_map/ppermute | solution.py:26
  322.6 6.5 %collective-permute-start.38 = (f32[1,4,1,32,64]{4,3,2,1,0:T(8,128)S(1)}, f32[1,4,1,32,64]{4,3,2,1,0:T(8,128)S(1)}, u32[]{:S(2)}, u32[]{:S(2)}) collective-permute-start(f32[1,4,1,32,64]{4,3,2,1,0:T(8,128)S(1)} %get-tuple-element.90), channel_id=1, source_target_pairs={{0,1},{1,2},{2,3},{4,5},{5,6},{6,7},{8,9},{9,10},{10,11},{12,13},{... | collective-permute-start | bytes 98312 | tf_op jit(solution)/shard_map/ppermute | solution.py:23
  327.2 8.4 %collective-permute-start.36 = (f32[1,4,2,32,64]{4,3,2,1,0:T(8,128)S(1)}, f32[1,4,2,32,64]{4,3,2,1,0:T(8,128)S(1)}, u32[]{:S(2)}, u32[]{:S(2)}) collective-permute-start(f32[1,4,2,32,64]{4,3,2,1,0:T(8,128)S(1)} %fusion.235), channel_id=1, source_target_pairs={{0,4},{4,8},{8,12},{12,16},{16,20},{20,24},{24,28},{28,32},{32,36}... | collective-permute-start | bytes 196616 | tf_op jit(solution)/shard_map/ppermute | solution.py:34
  335.7 5.4 %collective-permute-start.39 = (f32[1,4,1,32,64]{4,3,2,1,0:T(8,128)S(1)}, f32[1,4,1,32,64]{4,3,2,1,0:T(8,128)S(1)}, u32[]{:S(2)}, u32[]{:S(2)}) collective-permute-start(f32[1,4,1,32,64]{4,3,2,1,0:T(8,128)S(1)} %get-tuple-element.85), channel_id=1, source_target_pairs={{0,1},{1,2},{2,3},{4,5},{5,6},{6,7},{8,9},{9,10},{10,11},{12,13},{... | collective-permute-start | bytes 98312 | tf_op jit(solution)/shard_map/ppermute | solution.py:23
  337.9 6.2 %collective-permute-start.40 = (f32[1,4,1,32,64]{4,3,2,1,0:T(8,128)S(1)}, f32[1,4,1,32,64]{4,3,2,1,0:T(8,128)S(1)}, u32[]{:S(2)}, u32[]{:S(2)}) collective-permute-start(f32[1,4,1,32,64]{4,3,2,1,0:T(8,128)S(1)} %get-tuple-element.86), channel_id=1, source_target_pairs={{1,0},{2,1},{3,2},{5,4},{6,5},{7,6},{9,8},{10,9},{11,10},{13,12},{... | collective-permute-start | bytes 98312 | tf_op jit(solution)/shard_map/ppermute | solution.py:26
  339.2 8.4 %collective-permute-start.41 = (f32[1,4,2,32,64]{4,3,2,1,0:T(8,128)S(1)}, f32[1,4,2,32,64]{4,3,2,1,0:T(8,128)S(1)}, u32[]{:S(2)}, u32[]{:S(2)}) collective-permute-start(f32[1,4,2,32,64]{4,3,2,1,0:T(8,128)S(1)} %fusion.142), channel_id=1, source_target_pairs={{0,4},{4,8},{8,12},{12,16},{16,20},{20,24},{24,28},{28,32},{32,36}... | collective-permute-start | bytes 196616 | tf_op jit(solution)/shard_map/ppermute | solution.py:34
  344.7 3.3 copy-start.2
  348.6 12.6 %collective-permute-start.42 = (f32[1,4,4,64,128]{4,3,2,1,0:T(8,128)S(1)}, f32[1,4,4,64,128]{4,3,2,1,0:T(8,128)S(1)}, u32[]{:S(2)}, u32[]{:S(2)}) collective-permute-start(f32[1,4,4,64,128]{4,3,2,1,0:T(8,128)S(1)} %fusion.93), channel_id=1, source_target_pairs={{0,4},{4,8},{8,12},{12,16},{16,20},{20,24},{24,28},{28,32},{32,36}... | collective-permute-start | bytes 1572872 | tf_op jit(solution)/shard_map/ppermute | solution.py:34
  350.6 7.5 %collective-permute-start.43 = (f32[1,4,1,64,128]{4,3,2,1,0:T(8,128)S(1)}, f32[1,4,1,64,128]{4,3,2,1,0:T(8,128)S(1)}, u32[]{:S(2)}, u32[]{:S(2)}) collective-permute-start(f32[1,4,1,64,128]{4,3,2,1,0:T(8,128)S(1)} %get-tuple-element.43), channel_id=1, source_target_pairs={{1,0},{2,1},{3,2},{5,4},{6,5},{7,6},{9,8},{10,9},{11,10},{13,12},{... | collective-permute-start | bytes 393224 | tf_op jit(solution)/shard_map/ppermute | solution.py:26
  351.9 7.7 %collective-permute-start.44 = (f32[1,4,1,64,128]{4,3,2,1,0:T(8,128)S(1)}, f32[1,4,1,64,128]{4,3,2,1,0:T(8,128)S(1)}, u32[]{:S(2)}, u32[]{:S(2)}) collective-permute-start(f32[1,4,1,64,128]{4,3,2,1,0:T(8,128)S(1)} %get-tuple-element.44), channel_id=1, source_target_pairs={{0,1},{1,2},{2,3},{4,5},{5,6},{6,7},{8,9},{9,10},{10,11},{12,13},{... | collective-permute-start | bytes 393224 | tf_op jit(solution)/shard_map/ppermute | solution.py:23
Sparse Core Ops, SparseCore 0:
  91.2 25.4 all-gather.4
  276.8 24.6 all-gather.6

commit v11 on v9

--- a/solution.py
+++ b/solution.py
@@ -164,11 +164,14 @@
     )(flat_source, jnp.repeat(flat_metric, components, axis=1))
 
 
+def earlier_of(values):
+    arrived = from_behind(values[-1:], "tm", 1)
+    return jnp.concatenate([arrived, values[:-1]], axis=0)
+
+
 def apply_local(values, metric, spacing, pinned):
     padded = with_halo(values, (("space", 2),), 1)
-    arrived = from_behind(values, "tm", 1)
-    earlier = jnp.concatenate([arrived, values[:-1]], axis=0)
-    return stencil_apply(padded, metric, earlier, spacing, pinned)
+    return stencil_apply(padded, metric, earlier_of(values), spacing, pinned)
 
 
 def assemble(flat_source, flat_metric, time_devs, plane_devs, local_dims):
@@ -247,12 +250,33 @@
         applied = apply_local(values, metrics[depth], spacing, pinned_levels[depth])
         return values + OMEGA * (source - applied) / diagonal
 
+    def smooth_from_zero(depth, source):
+        spacing = 2.0**depth
+        metric_wide = with_halo(metrics[depth], (("space", 1),), 2)
+        source_wide = with_halo(source, (("space", 2),), 2)
+        diagonal_wide = diagonal_of(metric_wide, spacing, None)
+        first = OMEGA * source_wide / diagonal_wide
+        inner = first[:, :, 1:-1]
+        earlier = earlier_of(inner)
+        applied = stencil_apply(first, metric_wide[:, 1:-1], earlier, spacing, None)
+        second = inner + OMEGA * (source_wide[:, :, 1:-1] - applied) / diagonal_wide[:, :, 1:-1]
+        planes = source.shape[2]
+        inside = lax.axis_index("space") * planes - 1 + lax.broadcasted_iota(jnp.int32, (planes + 2,), 0)
+        inside = jnp.logical_and(inside >= 0, inside < planes * lax.axis_size("space"))
+        second = jnp.where(inside[None, None, :, None, None], second, 0.0)
+        values = second[:, :, 1:-1]
+        applied = stencil_apply(second, metrics[depth], earlier_of(values), spacing, None)
+        return (values, applied)
+
     def cycle(depth, values, source):
         spacing = 2.0**depth
         diagonal = diagonal_of(metrics[depth], spacing, pinned_levels[depth])
-        for repeat in range(NU):
-            values = sweep(depth, values, source, diagonal)
-        applied = apply_local(values, metrics[depth], spacing, pinned_levels[depth])
+        if values is None and depth == 1 and NU == 2:
+            values, applied = smooth_from_zero(depth, source)
+        else:
+            for repeat in range(NU):
+                values = sweep(depth, values, source, diagonal)
+            applied = apply_local(values, metrics[depth], spacing, pinned_levels[depth])
         residual = source - applied
         coarse_source = restrict(residual)
         if depth == 1:

time: 368 us -> 375 us (1.019)
  waiting for transfers between devices: 128 us -> 137 us
  starting transfers between devices: 117 us -> 111 us
    ppermute x15 -> x14, starting transfers between devices: 68.5 us -> 63.9 us  [with_halo(): lax.ppermute(lax.slice_in_dim(block, block.shape[dim] - width, None, axis...]
    ppermute x15 -> x14, waiting for transfers between devices: 13.7 us -> 16.4 us  [with_halo(): lax.ppermute(lax.slice_in_dim(block, block.shape[dim] - width, None, axis...]
    ppermute x15 -> x14, waiting for transfers between devices: 10.3 us -> 11.9 us  [with_halo(): lax.ppermute(lax.slice_in_dim(block, 0, width, axis=dim), axis, backward)]
    ppermute x15 -> x14, starting transfers between devices: 19.4 us -> 18.2 us  [with_halo(): lax.ppermute(lax.slice_in_dim(block, 0, width, axis=dim), axis, backward)]
  transfers between devices with their start and end apart: 47 -> 45, of which waited for: 35 -> 39; matrix products, arithmetic and copies ran while one was open for 1% -> 2% of each run, Pallas kernels for 0% -> 0%
where the time goes in v11:
time: 375 us; the launch traced here: 373 us
  waiting for transfers between devices  137 us (37%)
  starting transfers between devices  111 us (30%)
  blocking collectives  46.5 us (12%)
  Pallas kernels  28.5 us (8%)
  local copies, waits for them, and re-layouts  18.1 us (5%)
  between operations  14.6 us (4%)
  other arithmetic  14 us (4%)
    ppermute x14, starting transfers between devices, with_halo(): lax.ppermute(lax.slice_in_dim(block, block.shape[dim] - width, None, axis...  63.9 us
    ppermute x15, waiting for transfers between devices, from_behind(): return lax.ppermute(array, axis, pairs)  57.7 us
    all_gather x2, waiting for transfers between devices, gather_all(): whole = lax.all_gather(across, 'space', axis=1, tiled=True)  51.2 us
    all_gather x2, blocking collectives, gather_all(): across = lax.all_gather(flat, 'tm', axis=0, tiled=True)  46.5 us
    ppermute x15, starting transfers between devices, from_behind(): return lax.ppermute(array, axis, pairs)  28.8 us
    pallas_call x2, Pallas kernels, coarse_solve(): pl.pallas_call(kernel, out_shape=jax.ShapeDtypeStruct(flat_source.shape,...  28.5 us
    ppermute x14, starting transfers between devices, with_halo(): lax.ppermute(lax.slice_in_dim(block, 0, width, axis=dim), axis, backward)  18.2 us
    ppermute x14, waiting for transfers between devices, with_halo(): lax.ppermute(lax.slice_in_dim(block, block.shape[dim] - width, None, axis...  16.4 us
  transfers between devices with their start and end apart: 45, of which 39 were waited for; matrix products, arithmetic and copies ran while one was open for 2% of the time, Pallas kernels for 0%

profile of v11, /device:TPU:2, one launch (start us, length us, event | category | flops | bytes accessed | tf_op | source)
XLA Modules:
  0.0 373.1 jit_solution(15996609192131764067)
XLA Ops:
  9.6 4.5 %collective-permute-start.8 = (f32[1,2,32,64]{3,2,1,0:T(8,128)S(1)}, f32[1,2,32,64]{3,2,1,0:T(8,128)S(1)}, u32[]{:S(2)}, u32[]{:S(2)}) collective-permute-start(f32[1,2,32,64]{3,2,1,0:T(8,128)S(1)} %get-tuple-element.112), channel_id=1, source_target_pairs={{0,1},{1,2},{2,3},{4,5},{5,6},{6,7},{8,9},{9,10},{10,11},{12,13},{... | collective-permute-start | bytes 49160 | tf_op jit(solution)/shard_map/ppermute | solution.py:23
  16.4 1.9 collective-permute-start
  19.6 4.6 %collective-permute-start.2 = (f32[1,4,1,64,128]{4,3,2,1,0:T(8,128)S(1)}, f32[1,4,1,64,128]{4,3,2,1,0:T(8,128)S(1)}, u32[]{:S(2)}, u32[]{:S(2)}) collective-permute-start(f32[1,4,1,64,128]{4,3,2,1,0:T(8,128)S(1)} %get-tuple-element.68), channel_id=1, source_target_pairs={{0,1},{1,2},{2,3},{4,5},{5,6},{6,7},{8,9},{9,10},{10,11},{12,13},{... | collective-permute-start | bytes 393224 | tf_op jit(solution)/shard_map/ppermute | solution.py:23
  25.7 1.7 collective-permute-done.2
  29.5 1.9 collective-permute-start.3
  32.7 4.6 %collective-permute-start.5 = (f32[1,4,1,64,128]{4,3,2,1,0:T(8,128)S(1)}, f32[1,4,1,64,128]{4,3,2,1,0:T(8,128)S(1)}, u32[]{:S(2)}, u32[]{:S(2)}) collective-permute-start(f32[1,4,1,64,128]{4,3,2,1,0:T(8,128)S(1)} %get-tuple-element.64), channel_id=1, source_target_pairs={{0,1},{1,2},{2,3},{4,5},{5,6},{6,7},{8,9},{9,10},{10,11},{12,13},{... | collective-permute-start | bytes 393224 | tf_op jit(solution)/shard_map/ppermute | solution.py:23
  37.3 2.2 collective-permute-done.4
  39.6 1.5 collective-permute-done.5
  44.7 4.6 %collective-permute-start.6 = (f32[1,4,2,32,64]{4,3,2,1,0:T(8,128)S(1)}, f32[1,4,2,32,64]{4,3,2,1,0:T(8,128)S(1)}, u32[]{:S(2)}, u32[]{:S(2)}) collective-permute-start(f32[1,4,2,32,64]{4,3,2,1,0:T(8,128)S(1)} %fusion.1), channel_id=1, source_target_pairs={{0,1},{1,2},{2,3},{4,5},{5,6},{6,7},{8,9},{9,10},{10,11},{12,13},{... | collective-permute-start | bytes 196616 | tf_op jit(solution)/shard_map/ppermute | solution.py:23
  51.9 1.9 collective-permute-start.10
  54.0 7.7 %collective-permute-done.10 = f32[1,4,4,32,64]{4,3,2,1,0:T(8,128)S(1)} collective-permute-done((f32[1,4,4,32,64]{4,3,2,1,0:T(8,128)S(1)}, f32[1,4,4,32,64]{4,3,2,1,0:T(8,128)S(1)}, u32[]{:S(2)}, u32[]{:S(2)}) %collective-permute-start.10) | collective-permute-done | bytes 131104 | tf_op jit(solution)/shard_map/ppermute | solution.py:34
  62.0 1.9 collective-permute-start.11
  64.1 6.4 %collective-permute-done.11 = f32[1,4,2,32,64]{4,3,2,1,0:T(8,128)S(1)} collective-permute-done((f32[1,4,2,32,64]{4,3,2,1,0:T(8,128)S(1)}, f32[1,4,2,32,64]{4,3,2,1,0:T(8,128)S(1)}, u32[]{:S(2)}, u32[]{:S(2)}) %collective-permute-start.11) | collective-permute-done | bytes 65568 | tf_op jit(solution)/shard_map/ppermute | solution.py:34
  71.7 23.3 %all-gather = f32[32,1,2560]{2,1,0:T(1,128)S(1)} all-gather(f32[1,1,2560]{2,1,0:T(1,128)S(1)} %maximum_bitcast_fusion), channel_id=1, replica_groups=mesh['tm'=32,'space'=4] {'tm'}, dimensions={0}, use_global_device_ids=true | all-gather | bytes 337920 | tf_op jit(solution)/shard_map/all_gather | solution.py:194
  95.8 26.6 %all-gather.5.cloned.1.call-done = f32[32,10240]{1,0:T(8,128)} async-done(((f32[32,2560]{1,0:T(8,128)}), f32[32,10240]{1,0:T(8,128)}) %all-gather.5.cloned.1.call-update) | async-done | bytes 1310736 | tf_op jit(solution)/shard_map/all_gather | solution.py:195
  122.4 1.7 reshape.998
  125.2 2.5 reshape_transpose_reshape.7.src_ref
  129.4 14.3 %shard_map.37 = f32[32,16,512]{2,1,0:T(8,128)} custom-call(f32[32,16,512]{2,1,0:T(8,128)} %reshape_transpose_reshape.7.src_ref, f32[32,16,512]{2,1,0:T(8,128)} %reshape.999.met_ref), custom_call_target="tpu_custom_call" | custom-call | tf_op jit(solution)/shard_map/pallas_call | solution.py:161
  148.2 4.5 %collective-permute-start.14 = (f32[1,4,1,32,64]{4,3,2,1,0:T(8,128)S(1)}, f32[1,4,1,32,64]{4,3,2,1,0:T(8,128)S(1)}, u32[]{:S(2)}, u32[]{:S(2)}) collective-permute-start(f32[1,4,1,32,64]{4,3,2,1,0:T(8,128)S(1)} %get-tuple-element.104), channel_id=1, source_target_pairs={{0,1},{1,2},{2,3},{4,5},{5,6},{6,7},{8,9},{9,10},{10,11},{12,13},{... | collective-permute-start | bytes 98312 | tf_op jit(solution)/shard_map/ppermute | solution.py:23
  152.8 1.9 collective-permute-start.12
  154.8 6.3 %collective-permute-done.12 = f32[1,4,2,32,64]{4,3,2,1,0:T(8,128)S(1)} collective-permute-done((f32[1,4,2,32,64]{4,3,2,1,0:T(8,128)S(1)}, f32[1,4,2,32,64]{4,3,2,1,0:T(8,128)S(1)}, u32[]{:S(2)}, u32[]{:S(2)}) %collective-permute-start.12) | collective-permute-done | bytes 65568 | tf_op jit(solution)/shard_map/ppermute | solution.py:34
  161.7 1.9 collective-permute-start.15
  165.0 4.6 %collective-permute-start.17 = (f32[1,4,1,64,128]{4,3,2,1,0:T(8,128)S(1)}, f32[1,4,1,64,128]{4,3,2,1,0:T(8,128)S(1)}, u32[]{:S(2)}, u32[]{:S(2)}) collective-permute-start(f32[1,4,1,64,128]{4,3,2,1,0:T(8,128)S(1)} %get-tuple-element.60), channel_id=1, source_target_pairs={{0,1},{1,2},{2,3},{4,5},{5,6},{6,7},{8,9},{9,10},{10,11},{12,13},{... | collective-permute-start | bytes 393224 | tf_op jit(solution)/shard_map/ppermute | solution.py:23
  170.6 1.5 collective-permute-done.17
  172.3 2.1 collective-permute-done.15
  174.9 1.9 collective-permute-start.18
  178.2 4.6 %collective-permute-start.20 = (f32[1,4,1,64,128]{4,3,2,1,0:T(8,128)S(1)}, f32[1,4,1,64,128]{4,3,2,1,0:T(8,128)S(1)}, u32[]{:S(2)}, u32[]{:S(2)}) collective-permute-start(f32[1,4,1,64,128]{4,3,2,1,0:T(8,128)S(1)} %get-tuple-element.56), channel_id=1, source_target_pairs={{0,1},{1,2},{2,3},{4,5},{5,6},{6,7},{8,9},{9,10},{10,11},{12,13},{... | collective-permute-start | bytes 393224 | tf_op jit(solution)/shard_map/ppermute | solution.py:23
  183.7 1.5 collective-permute-done.20
  185.4 2.1 collective-permute-done.18
  188.1 1.9 collective-permute-start.21
  191.3 4.7 %collective-permute-start.23 = (f32[1,4,1,64,128]{4,3,2,1,0:T(8,128)S(1)}, f32[1,4,1,64,128]{4,3,2,1,0:T(8,128)S(1)}, u32[]{:S(2)}, u32[]{:S(2)}) collective-permute-start(f32[1,4,1,64,128]{4,3,2,1,0:T(8,128)S(1)} %get-tuple-element.52), channel_id=1, source_target_pairs={{0,1},{1,2},{2,3},{4,5},{5,6},{6,7},{8,9},{9,10},{10,11},{12,13},{... | collective-permute-start | bytes 393224 | tf_op jit(solution)/shard_map/ppermute | solution.py:23
  196.9 1.5 collective-permute-done.23
  198.6 2.1 collective-permute-done.21
  201.2 1.9 collective-permute-start.24
  204.5 4.6 %collective-permute-start.26 = (f32[1,4,1,64,128]{4,3,2,1,0:T(8,128)S(1)}, f32[1,4,1,64,128]{4,3,2,1,0:T(8,128)S(1)}, u32[]{:S(2)}, u32[]{:S(2)}) collective-permute-start(f32[1,4,1,64,128]{4,3,2,1,0:T(8,128)S(1)} %get-tuple-element.48), channel_id=1, source_target_pairs={{0,1},{1,2},{2,3},{4,5},{5,6},{6,7},{8,9},{9,10},{10,11},{12,13},{... | collective-permute-start | bytes 393224 | tf_op jit(solution)/shard_map/ppermute | solution.py:23
  210.0 1.5 collective-permute-done.26
  211.7 2.1 collective-permute-done.24
  214.4 1.9 collective-permute-start.27
  217.6 4.6 %collective-permute-start.29 = (f32[1,4,1,64,128]{4,3,2,1,0:T(8,128)S(1)}, f32[1,4,1,64,128]{4,3,2,1,0:T(8,128)S(1)}, u32[]{:S(2)}, u32[]{:S(2)}) collective-permute-start(f32[1,4,1,64,128]{4,3,2,1,0:T(8,128)S(1)} %get-tuple-element.44), channel_id=1, source_target_pairs={{0,1},{1,2},{2,3},{4,5},{5,6},{6,7},{8,9},{9,10},{10,11},{12,13},{... | collective-permute-start | bytes 393224 | tf_op jit(solution)/shard_map/ppermute | solution.py:23
  223.2 1.5 collective-permute-done.29
  224.9 2.1 collective-permute-done.27
  227.9 1.4 collective-permute-start.31
  229.4 4.6 %collective-permute-start.30 = (f32[1,4,2,32,64]{4,3,2,1,0:T(8,128)S(1)}, f32[1,4,2,32,64]{4,3,2,1,0:T(8,128)S(1)}, u32[]{:S(2)}, u32[]{:S(2)}) collective-permute-start(f32[1,4,2,32,64]{4,3,2,1,0:T(8,128)S(1)} %fusion), channel_id=1, source_target_pairs={{0,1},{1,2},{2,3},{4,5},{5,6},{6,7},{8,9},{9,10},{10,11},{12,13},{... | collective-permute-start | bytes 196616 | tf_op jit(solution)/shard_map/ppermute | solution.py:23
  234.9 1.5 collective-permute-done.30
  236.5 1.9 collective-permute-start.32
  238.6 7.7 %collective-permute-done.32 = f32[1,4,4,32,64]{4,3,2,1,0:T(8,128)S(1)} collective-permute-done((f32[1,4,4,32,64]{4,3,2,1,0:T(8,128)S(1)}, f32[1,4,4,32,64]{4,3,2,1,0:T(8,128)S(1)}, u32[]{:S(2)}, u32[]{:S(2)}) %collective-permute-start.32) | collective-permute-done | bytes 131104 | tf_op jit(solution)/shard_map/ppermute | solution.py:34
  246.7 1.9 collective-permute-start.33
  248.7 6.4 %collective-permute-done.33 = f32[1,4,2,32,64]{4,3,2,1,0:T(8,128)S(1)} collective-permute-done((f32[1,4,2,32,64]{4,3,2,1,0:T(8,128)S(1)}, f32[1,4,2,32,64]{4,3,2,1,0:T(8,128)S(1)}, u32[]{:S(2)}, u32[]{:S(2)}) %collective-permute-start.33) | collective-permute-done | bytes 65568 | tf_op jit(solution)/shard_map/ppermute | solution.py:34
  255.7 23.3 %all-gather.1 = f32[32,1,2048]{2,1,0:T(1,128)S(1)} all-gather(f32[1,1,2048]{2,1,0:T(1,128)S(1)} %reshape.1019), channel_id=1, replica_groups=mesh['tm'=32,'space'=4] {'tm'}, dimensions={0}, use_global_device_ids=true | all-gather | bytes 270336 | tf_op jit(solution)/shard_map/all_gather | solution.py:194
  279.8 24.6 %all-gather.7.cloned.1.call-done = f32[32,8192]{1,0:T(8,128)} async-done(((f32[32,2048]{1,0:T(8,128)}), f32[32,8192]{1,0:T(8,128)}) %all-gather.7.cloned.1.call-update) | async-done | bytes 1048592 | tf_op jit(solution)/shard_map/all_gather | solution.py:195
  304.4 2.8 copy.22
  307.2 14.3 %shard_map.38 = f32[32,16,512]{2,1,0:T(8,128)} custom-call(f32[32,16,512]{2,1,0:T(8,128)} %bitcast.102, f32[32,16,512]{2,1,0:T(8,128)} %reshape.999.met_ref), custom_call_target="tpu_custom_call" | custom-call | tf_op jit(solution)/shard_map/pallas_call | solution.py:161
  325.6 4.5 %collective-permute-start.36 = (f32[1,4,1,32,64]{4,3,2,1,0:T(8,128)S(1)}, f32[1,4,1,32,64]{4,3,2,1,0:T(8,128)S(1)}, u32[]{:S(2)}, u32[]{:S(2)}) collective-permute-start(f32[1,4,1,32,64]{4,3,2,1,0:T(8,128)S(1)} %get-tuple-element.100), channel_id=1, source_target_pairs={{0,1},{1,2},{2,3},{4,5},{5,6},{6,7},{8,9},{9,10},{10,11},{12,13},{... | collective-permute-start | bytes 98312 | tf_op jit(solution)/shard_map/ppermute | solution.py:23
  330.2 1.9 collective-permute-start.34
  332.2 6.3 %collective-permute-done.34 = f32[1,4,2,32,64]{4,3,2,1,0:T(8,128)S(1)} collective-permute-done((f32[1,4,2,32,64]{4,3,2,1,0:T(8,128)S(1)}, f32[1,4,2,32,64]{4,3,2,1,0:T(8,128)S(1)}, u32[]{:S(2)}, u32[]{:S(2)}) %collective-permute-start.34) | collective-permute-done | bytes 65568 | tf_op jit(solution)/shard_map/ppermute | solution.py:34
  339.1 1.9 collective-permute-start.37
  342.4 4.6 %collective-permute-start.39 = (f32[1,4,1,64,128]{4,3,2,1,0:T(8,128)S(1)}, f32[1,4,1,64,128]{4,3,2,1,0:T(8,128)S(1)}, u32[]{:S(2)}, u32[]{:S(2)}) collective-permute-start(f32[1,4,1,64,128]{4,3,2,1,0:T(8,128)S(1)} %get-tuple-element.40), channel_id=1, source_target_pairs={{0,1},{1,2},{2,3},{4,5},{5,6},{6,7},{8,9},{9,10},{10,11},{12,13},{... | collective-permute-start | bytes 393224 | tf_op jit(solution)/shard_map/ppermute | solution.py:23
  347.9 1.5 collective-permute-done.39
  349.6 2.1 collective-permute-done.37
  352.3 1.9 collective-permute-start.40
  355.5 4.6 %collective-permute-start.42 = (f32[1,4,1,64,128]{4,3,2,1,0:T(8,128)S(1)}, f32[1,4,1,64,128]{4,3,2,1,0:T(8,128)S(1)}, u32[]{:S(2)}, u32[]{:S(2)}) collective-permute-start(f32[1,4,1,64,128]{4,3,2,1,0:T(8,128)S(1)} %get-tuple-element.36), channel_id=1, source_target_pairs={{0,1},{1,2},{2,3},{4,5},{5,6},{6,7},{8,9},{9,10},{10,11},{12,13},{... | collective-permute-start | bytes 393224 | tf_op jit(solution)/shard_map/ppermute | solution.py:23
  361.1 1.5 collective-permute-done.42
  362.8 2.1 collective-permute-done.40
  364.9 1.3 fusion.13
  (198 shorter events, 56.7 us)
Async XLA Ops:
  6.5 9.6 %copy-start = (f32[1,4,4,64,128]{4,3,2,1,0:T(8,128)S(1)}, f32[1,4,4,64,128]{4,3,2,1,0:T(8,128)}, u32[]{:S(2)}) copy-start(f32[1,4,4,64,128]{4,3,2,1,0:T(8,128)} %param.3) | copy-start | bytes 1572868
  6.5 115.9 %all-gather.5.cloned.1.call-start = ((), (), s32[]{:S(2)}) async-start(), calls=%async_computation | async-start | bytes 1638400 | tf_op jit(solution)/shard_map/all_gather | solution.py:195
  6.5 8.6 %copy-start.8 = (pred[128]{0:T(512)(128)(4,1)}, pred[128]{0:T(512)(128)(4,1)S(1)}, u32[]{:S(2)}) copy-start(pred[128]{0:T(512)(128)(4,1)S(1)} %compare_and_fusion.1) | copy-start | bytes 388
  6.6 8.6 %copy-start.11 = (s32[128]{0:T(128)}, s32[128]{0:T(128)S(1)}, u32[]{:S(2)}) copy-start(s32[128]{0:T(128)S(1)} %get-tuple-element.113) | copy-start | bytes 1540
  6.6 8.6 %copy-start.14 = (s32[128]{0:T(128)}, s32[128]{0:T(128)S(1)}, u32[]{:S(2)}) copy-start(s32[128]{0:T(128)S(1)} %get-tuple-element.114) | copy-start | bytes 1540
  8.3 16.7 %collective-permute-start.9 = (f32[1,2,32,64]{3,2,1,0:T(8,128)S(1)}, f32[1,2,32,64]{3,2,1,0:T(8,128)S(1)}, u32[]{:S(2)}, u32[]{:S(2)}) collective-permute-start(f32[1,2,32,64]{3,2,1,0:T(8,128)S(1)} %get-tuple-element.112), channel_id=1, source_target_pairs={{1,0},{2,1},{3,2},{5,4},{6,5},{7,6},{9,8},{10,9},{11,10},{13,12},{... | collective-permute-start | bytes 49160 | tf_op jit(solution)/shard_map/ppermute | solution.py:26
  9.6 15.4 %collective-permute-start.8 = (f32[1,2,32,64]{3,2,1,0:T(8,128)S(1)}, f32[1,2,32,64]{3,2,1,0:T(8,128)S(1)}, u32[]{:S(2)}, u32[]{:S(2)}) collective-permute-start(f32[1,2,32,64]{3,2,1,0:T(8,128)S(1)} %get-tuple-element.112), channel_id=1, source_target_pairs={{0,1},{1,2},{2,3},{4,5},{5,6},{6,7},{8,9},{9,10},{10,11},{12,13},{... | collective-permute-start | bytes 49160 | tf_op jit(solution)/shard_map/ppermute | solution.py:23
  16.1 8.1 %copy-start.1 = (f32[1,4,64,128]{3,2,1,0:T(8,128)S(1)}, f32[1,4,64,128]{3,2,1,0:T(8,128)}, u32[]{:S(2)}) copy-start(f32[1,4,64,128]{3,2,1,0:T(8,128)} %param.4) | copy-start | bytes 393220
  16.4 12.6 %collective-permute-start = (f32[1,4,4,64,128]{4,3,2,1,0:T(8,128)S(1)}, f32[1,4,4,64,128]{4,3,2,1,0:T(8,128)S(1)}, u32[]{:S(2)}, u32[]{:S(2)}) collective-permute-start(f32[1,4,4,64,128]{4,3,2,1,0:T(8,128)S(1)} %get-tuple-element.9), channel_id=1, source_target_pairs={{0,4},{4,8},{8,12},{12,16},{16,20},{20,24},{24,28},{28,32},{32,36}... | collective-permute-start | bytes 1572872 | tf_op jit(solution)/shard_map/ppermute | solution.py:34
  18.3 7.4 %collective-permute-start.1 = (f32[1,4,1,64,128]{4,3,2,1,0:T(8,128)S(1)}, f32[1,4,1,64,128]{4,3,2,1,0:T(8,128)S(1)}, u32[]{:S(2)}, u32[]{:S(2)}) collective-permute-start(f32[1,4,1,64,128]{4,3,2,1,0:T(8,128)S(1)} %get-tuple-element.67), channel_id=1, source_target_pairs={{1,0},{2,1},{3,2},{5,4},{6,5},{7,6},{9,8},{10,9},{11,10},{13,12},{... | collective-permute-start | bytes 393224 | tf_op jit(solution)/shard_map/ppermute | solution.py:26
  19.6 7.8 %collective-permute-start.2 = (f32[1,4,1,64,128]{4,3,2,1,0:T(8,128)S(1)}, f32[1,4,1,64,128]{4,3,2,1,0:T(8,128)S(1)}, u32[]{:S(2)}, u32[]{:S(2)}) collective-permute-start(f32[1,4,1,64,128]{4,3,2,1,0:T(8,128)S(1)} %get-tuple-element.68), channel_id=1, source_target_pairs={{0,1},{1,2},{2,3},{4,5},{5,6},{6,7},{8,9},{9,10},{10,11},{12,13},{... | collective-permute-start | bytes 393224 | tf_op jit(solution)/shard_map/ppermute | solution.py:23
  29.5 12.6 %collective-permute-start.3 = (f32[1,4,4,64,128]{4,3,2,1,0:T(8,128)S(1)}, f32[1,4,4,64,128]{4,3,2,1,0:T(8,128)S(1)}, u32[]{:S(2)}, u32[]{:S(2)}) collective-permute-start(f32[1,4,4,64,128]{4,3,2,1,0:T(8,128)S(1)} %fusion.121), channel_id=1, source_target_pairs={{0,4},{4,8},{8,12},{12,16},{16,20},{20,24},{24,28},{28,32},{32,36}... | collective-permute-start | bytes 1572872 | tf_op jit(solution)/shard_map/ppermute | solution.py:34
  31.4 8.1 %collective-permute-start.4 = (f32[1,4,1,64,128]{4,3,2,1,0:T(8,128)S(1)}, f32[1,4,1,64,128]{4,3,2,1,0:T(8,128)S(1)}, u32[]{:S(2)}, u32[]{:S(2)}) collective-permute-start(f32[1,4,1,64,128]{4,3,2,1,0:T(8,128)S(1)} %get-tuple-element.63), channel_id=1, source_target_pairs={{1,0},{2,1},{3,2},{5,4},{6,5},{7,6},{9,8},{10,9},{11,10},{13,12},{... | collective-permute-start | bytes 393224 | tf_op jit(solution)/shard_map/ppermute | solution.py:26
  32.7 8.3 %collective-permute-start.5 = (f32[1,4,1,64,128]{4,3,2,1,0:T(8,128)S(1)}, f32[1,4,1,64,128]{4,3,2,1,0:T(8,128)S(1)}, u32[]{:S(2)}, u32[]{:S(2)}) collective-permute-start(f32[1,4,1,64,128]{4,3,2,1,0:T(8,128)S(1)} %get-tuple-element.64), channel_id=1, source_target_pairs={{0,1},{1,2},{2,3},{4,5},{5,6},{6,7},{8,9},{9,10},{10,11},{12,13},{... | collective-permute-start | bytes 393224 | tf_op jit(solution)/shard_map/ppermute | solution.py:23
  37.3 24.4 %copy-start.2 = (f32[4,32,64]{2,1,0:T(8,128)}, f32[4,32,64]{2,1,0:T(8,128)S(1)}, u32[]{:S(2)}) copy-start(f32[4,32,64]{2,1,0:T(8,128)S(1)} %fusion.382) | copy-start | bytes 98308
  42.5 0.6 copy-start.9
  42.5 0.7 copy-start.12
  42.5 0.7 copy-start.15
  43.4 7.2 %collective-permute-start.7 = (f32[1,4,2,32,64]{4,3,2,1,0:T(8,128)S(1)}, f32[1,4,2,32,64]{4,3,2,1,0:T(8,128)S(1)}, u32[]{:S(2)}, u32[]{:S(2)}) collective-permute-start(f32[1,4,2,32,64]{4,3,2,1,0:T(8,128)S(1)} %fusion.1), channel_id=1, source_target_pairs={{1,0},{2,1},{3,2},{5,4},{6,5},{7,6},{9,8},{10,9},{11,10},{13,12},{... | collective-permute-start | bytes 196616 | tf_op jit(solution)/shard_map/ppermute | solution.py:26
  44.7 7.1 %collective-permute-start.6 = (f32[1,4,2,32,64]{4,3,2,1,0:T(8,128)S(1)}, f32[1,4,2,32,64]{4,3,2,1,0:T(8,128)S(1)}, u32[]{:S(2)}, u32[]{:S(2)}) collective-permute-start(f32[1,4,2,32,64]{4,3,2,1,0:T(8,128)S(1)} %fusion.1), channel_id=1, source_target_pairs={{0,1},{1,2},{2,3},{4,5},{5,6},{6,7},{8,9},{9,10},{10,11},{12,13},{... | collective-permute-start | bytes 196616 | tf_op jit(solution)/shard_map/ppermute | solution.py:23
  49.3 12.4 %copy-start.4 = (f32[4,32,64]{2,1,0:T(8,128)}, f32[4,32,64]{2,1,0:T(8,128)S(1)}, u32[]{:S(2)}) copy-start(f32[4,32,64]{2,1,0:T(8,128)S(1)} %slice_bitcast_fusion) | copy-start | bytes 98308
  51.8 9.9 %copy-start.17 = (pred[4]{0:T(512)(128)(4,1)S(1)}, pred[4]{0:T(512)(128)(4,1)}, u32[]{:S(2)}) copy-start(pred[4]{0:T(512)(128)(4,1)} %compare_and_fusion.2) | copy-start | bytes 16
  51.9 9.8 %collective-permute-start.10 = (f32[1,4,4,32,64]{4,3,2,1,0:T(8,128)S(1)}, f32[1,4,4,32,64]{4,3,2,1,0:T(8,128)S(1)}, u32[]{:S(2)}, u32[]{:S(2)}) collective-permute-start(f32[1,4,4,32,64]{4,3,2,1,0:T(8,128)S(1)} %slice.1736), channel_id=1, source_target_pairs={{0,4},{4,8},{8,12},{12,16},{16,20},{20,24},{24,28},{28,32},{32,36}... | collective-permute-start | bytes 393224 | tf_op jit(solution)/shard_map/ppermute | solution.py:34
  62.0 8.4 %collective-permute-start.11 = (f32[1,4,2,32,64]{4,3,2,1,0:T(8,128)S(1)}, f32[1,4,2,32,64]{4,3,2,1,0:T(8,128)S(1)}, u32[]{:S(2)}, u32[]{:S(2)}) collective-permute-start(f32[1,4,2,32,64]{4,3,2,1,0:T(8,128)S(1)} %slice.1746), channel_id=1, source_target_pairs={{0,4},{4,8},{8,12},{12,16},{16,20},{20,24},{24,28},{28,32},{32,36}... | collective-permute-start | bytes 196616 | tf_op jit(solution)/shard_map/ppermute | solution.py:34
  95.8 208.7 %all-gather.7.cloned.1.call-start = ((), (), s32[]{:S(2)}) async-start(), calls=%async_computation.1 | async-start | bytes 1310720 | tf_op jit(solution)/shard_map/all_gather | solution.py:195
  145.8 0.9 copy-start.6
  145.8 0.9 copy-start.7
  146.2 15.0 %copy-start.10 = (pred[128]{0:T(512)(128)(4,1)S(1)}, pred[128]{0:T(512)(128)(4,1)}, u32[]{:S(2)}) copy-start(pred[128]{0:T(512)(128)(4,1)} %copy-done.8) | copy-start | bytes 388
  146.2 15.0 %copy-start.13 = (s32[128]{0:T(128)S(1)}, s32[128]{0:T(128)}, u32[]{:S(2)}) copy-start(s32[128]{0:T(128)} %copy-done.11) | copy-start | bytes 1540
  146.2 15.0 %copy-start.16 = (s32[128]{0:T(128)S(1)}, s32[128]{0:T(128)}, u32[]{:S(2)}) copy-start(s32[128]{0:T(128)} %copy-done.14) | copy-start | bytes 1540
  146.9 7.8 %collective-permute-start.13 = (f32[1,4,1,32,64]{4,3,2,1,0:T(8,128)S(1)}, f32[1,4,1,32,64]{4,3,2,1,0:T(8,128)S(1)}, u32[]{:S(2)}, u32[]{:S(2)}) collective-permute-start(f32[1,4,1,32,64]{4,3,2,1,0:T(8,128)S(1)} %get-tuple-element.103), channel_id=1, source_target_pairs={{1,0},{2,1},{3,2},{5,4},{6,5},{7,6},{9,8},{10,9},{11,10},{13,12},{... | collective-permute-start | bytes 98312 | tf_op jit(solution)/shard_map/ppermute | solution.py:26
  148.2 6.5 %collective-permute-start.14 = (f32[1,4,1,32,64]{4,3,2,1,0:T(8,128)S(1)}, f32[1,4,1,32,64]{4,3,2,1,0:T(8,128)S(1)}, u32[]{:S(2)}, u32[]{:S(2)}) collective-permute-start(f32[1,4,1,32,64]{4,3,2,1,0:T(8,128)S(1)} %get-tuple-element.104), channel_id=1, source_target_pairs={{0,1},{1,2},{2,3},{4,5},{5,6},{6,7},{8,9},{9,10},{10,11},{12,13},{... | collective-permute-start | bytes 98312 | tf_op jit(solution)/shard_map/ppermute | solution.py:23
  152.8 8.4 %collective-permute-start.12 = (f32[1,4,2,32,64]{4,3,2,1,0:T(8,128)S(1)}, f32[1,4,2,32,64]{4,3,2,1,0:T(8,128)S(1)}, u32[]{:S(2)}, u32[]{:S(2)}) collective-permute-start(f32[1,4,2,32,64]{4,3,2,1,0:T(8,128)S(1)} %fusion.202), channel_id=1, source_target_pairs={{0,4},{4,8},{8,12},{12,16},{16,20},{20,24},{24,28},{28,32},{32,36}... | collective-permute-start | bytes 196616 | tf_op jit(solution)/shard_map/ppermute | solution.py:34
  161.7 12.6 %collective-permute-start.15 = (f32[1,4,4,64,128]{4,3,2,1,0:T(8,128)S(1)}, f32[1,4,4,64,128]{4,3,2,1,0:T(8,128)S(1)}, u32[]{:S(2)}, u32[]{:S(2)}) collective-permute-start(f32[1,4,4,64,128]{4,3,2,1,0:T(8,128)S(1)} %add.554), channel_id=1, source_target_pairs={{0,4},{4,8},{8,12},{12,16},{16,20},{20,24},{24,28},{28,32},{32,36}... | collective-permute-start | bytes 1572872 | tf_op jit(solution)/shard_map/ppermute | solution.py:34
  163.7 6.9 %collective-permute-start.16 = (f32[1,4,1,64,128]{4,3,2,1,0:T(8,128)S(1)}, f32[1,4,1,64,128]{4,3,2,1,0:T(8,128)S(1)}, u32[]{:S(2)}, u32[]{:S(2)}) collective-permute-start(f32[1,4,1,64,128]{4,3,2,1,0:T(8,128)S(1)} %get-tuple-element.59), channel_id=1, source_target_pairs={{1,0},{2,1},{3,2},{5,4},{6,5},{7,6},{9,8},{10,9},{11,10},{13,12},{... | collective-permute-start | bytes 393224 | tf_op jit(solution)/shard_map/ppermute | solution.py:26
  165.0 7.1 %collective-permute-start.17 = (f32[1,4,1,64,128]{4,3,2,1,0:T(8,128)S(1)}, f32[1,4,1,64,128]{4,3,2,1,0:T(8,128)S(1)}, u32[]{:S(2)}, u32[]{:S(2)}) collective-permute-start(f32[1,4,1,64,128]{4,3,2,1,0:T(8,128)S(1)} %get-tuple-element.60), channel_id=1, source_target_pairs={{0,1},{1,2},{2,3},{4,5},{5,6},{6,7},{8,9},{9,10},{10,11},{12,13},{... | collective-permute-start | bytes 393224 | tf_op jit(solution)/shard_map/ppermute | solution.py:23
  174.9 12.6 %collective-permute-start.18 = (f32[1,4,4,64,128]{4,3,2,1,0:T(8,128)S(1)}, f32[1,4,4,64,128]{4,3,2,1,0:T(8,128)S(1)}, u32[]{:S(2)}, u32[]{:S(2)}) collective-permute-start(f32[1,4,4,64,128]{4,3,2,1,0:T(8,128)S(1)} %fusion.95), channel_id=1, source_target_pairs={{0,4},{4,8},{8,12},{12,16},{16,20},{20,24},{24,28},{28,32},{32,36}... | collective-permute-start | bytes 1572872 | tf_op jit(solution)/shard_map/ppermute | solution.py:34
  176.9 6.9 %collective-permute-start.19 = (f32[1,4,1,64,128]{4,3,2,1,0:T(8,128)S(1)}, f32[1,4,1,64,128]{4,3,2,1,0:T(8,128)S(1)}, u32[]{:S(2)}, u32[]{:S(2)}) collective-permute-start(f32[1,4,1,64,128]{4,3,2,1,0:T(8,128)S(1)} %get-tuple-element.55), channel_id=1, source_target_pairs={{1,0},{2,1},{3,2},{5,4},{6,5},{7,6},{9,8},{10,9},{11,10},{13,12},{... | collective-permute-start | bytes 393224 | tf_op jit(solution)/shard_map/ppermute | solution.py:26
  178.2 7.1 %collective-permute-start.20 = (f32[1,4,1,64,128]{4,3,2,1,0:T(8,128)S(1)}, f32[1,4,1,64,128]{4,3,2,1,0:T(8,128)S(1)}, u32[]{:S(2)}, u32[]{:S(2)}) collective-permute-start(f32[1,4,1,64,128]{4,3,2,1,0:T(8,128)S(1)} %get-tuple-element.56), channel_id=1, source_target_pairs={{0,1},{1,2},{2,3},{4,5},{5,6},{6,7},{8,9},{9,10},{10,11},{12,13},{... | collective-permute-start | bytes 393224 | tf_op jit(solution)/shard_map/ppermute | solution.py:23
  188.1 12.6 %collective-permute-start.21 = (f32[1,4,4,64,128]{4,3,2,1,0:T(8,128)S(1)}, f32[1,4,4,64,128]{4,3,2,1,0:T(8,128)S(1)}, u32[]{:S(2)}, u32[]{:S(2)}) collective-permute-start(f32[1,4,4,64,128]{4,3,2,1,0:T(8,128)S(1)} %fusion.81), channel_id=1, source_target_pairs={{0,4},{4,8},{8,12},{12,16},{16,20},{20,24},{24,28},{28,32},{32,36}... | collective-permute-start | bytes 1572872 | tf_op jit(solution)/shard_map/ppermute | solution.py:34
  190.0 6.9 %collective-permute-start.22 = (f32[1,4,1,64,128]{4,3,2,1,0:T(8,128)S(1)}, f32[1,4,1,64,128]{4,3,2,1,0:T(8,128)S(1)}, u32[]{:S(2)}, u32[]{:S(2)}) collective-permute-start(f32[1,4,1,64,128]{4,3,2,1,0:T(8,128)S(1)} %get-tuple-element.51), channel_id=1, source_target_pairs={{1,0},{2,1},{3,2},{5,4},{6,5},{7,6},{9,8},{10,9},{11,10},{13,12},{... | collective-permute-start | bytes 393224 | tf_op jit(solution)/shard_map/ppermute | solution.py:26
  191.3 7.1 %collective-permute-start.23 = (f32[1,4,1,64,128]{4,3,2,1,0:T(8,128)S(1)}, f32[1,4,1,64,128]{4,3,2,1,0:T(8,128)S(1)}, u32[]{:S(2)}, u32[]{:S(2)}) collective-permute-start(f32[1,4,1,64,128]{4,3,2,1,0:T(8,128)S(1)} %get-tuple-element.52), channel_id=1, source_target_pairs={{0,1},{1,2},{2,3},{4,5},{5,6},{6,7},{8,9},{9,10},{10,11},{12,13},{... | collective-permute-start | bytes 393224 | tf_op jit(solution)/shard_map/ppermute | solution.py:23
  201.2 12.6 %collective-permute-start.24 = (f32[1,4,4,64,128]{4,3,2,1,0:T(8,128)S(1)}, f32[1,4,4,64,128]{4,3,2,1,0:T(8,128)S(1)}, u32[]{:S(2)}, u32[]{:S(2)}) collective-permute-start(f32[1,4,4,64,128]{4,3,2,1,0:T(8,128)S(1)} %fusion.67), channel_id=1, source_target_pairs={{0,4},{4,8},{8,12},{12,16},{16,20},{20,24},{24,28},{28,32},{32,36}... | collective-permute-start | bytes 1572872 | tf_op jit(solution)/shard_map/ppermute | solution.py:34
  203.2 6.9 %collective-permute-start.25 = (f32[1,4,1,64,128]{4,3,2,1,0:T(8,128)S(1)}, f32[1,4,1,64,128]{4,3,2,1,0:T(8,128)S(1)}, u32[]{:S(2)}, u32[]{:S(2)}) collective-permute-start(f32[1,4,1,64,128]{4,3,2,1,0:T(8,128)S(1)} %get-tuple-element.47), channel_id=1, source_target_pairs={{1,0},{2,1},{3,2},{5,4},{6,5},{7,6},{9,8},{10,9},{11,10},{13,12},{... | collective-permute-start | bytes 393224 | tf_op jit(solution)/shard_map/ppermute | solution.py:26
  204.5 7.1 %collective-permute-start.26 = (f32[1,4,1,64,128]{4,3,2,1,0:T(8,128)S(1)}, f32[1,4,1,64,128]{4,3,2,1,0:T(8,128)S(1)}, u32[]{:S(2)}, u32[]{:S(2)}) collective-permute-start(f32[1,4,1,64,128]{4,3,2,1,0:T(8,128)S(1)} %get-tuple-element.48), channel_id=1, source_target_pairs={{0,1},{1,2},{2,3},{4,5},{5,6},{6,7},{8,9},{9,10},{10,11},{12,13},{... | collective-permute-start | bytes 393224 | tf_op jit(solution)/shard_map/ppermute | solution.py:23
  214.4 12.6 %collective-permute-start.27 = (f32[1,4,4,64,128]{4,3,2,1,0:T(8,128)S(1)}, f32[1,4,4,64,128]{4,3,2,1,0:T(8,128)S(1)}, u32[]{:S(2)}, u32[]{:S(2)}) collective-permute-start(f32[1,4,4,64,128]{4,3,2,1,0:T(8,128)S(1)} %fusion.53), channel_id=1, source_target_pairs={{0,4},{4,8},{8,12},{12,16},{16,20},{20,24},{24,28},{28,32},{32,36}... | collective-permute-start | bytes 1572872 | tf_op jit(solution)/shard_map/ppermute | solution.py:34
  216.3 6.9 %collective-permute-start.28 = (f32[1,4,1,64,128]{4,3,2,1,0:T(8,128)S(1)}, f32[1,4,1,64,128]{4,3,2,1,0:T(8,128)S(1)}, u32[]{:S(2)}, u32[]{:S(2)}) collective-permute-start(f32[1,4,1,64,128]{4,3,2,1,0:T(8,128)S(1)} %get-tuple-element.43), channel_id=1, source_target_pairs={{1,0},{2,1},{3,2},{5,4},{6,5},{7,6},{9,8},{10,9},{11,10},{13,12},{... | collective-permute-start | bytes 393224 | tf_op jit(solution)/shard_map/ppermute | solution.py:26
  217.6 7.1 %collective-permute-start.29 = (f32[1,4,1,64,128]{4,3,2,1,0:T(8,128)S(1)}, f32[1,4,1,64,128]{4,3,2,1,0:T(8,128)S(1)}, u32[]{:S(2)}, u32[]{:S(2)}) collective-permute-start(f32[1,4,1,64,128]{4,3,2,1,0:T(8,128)S(1)} %get-tuple-element.44), channel_id=1, source_target_pairs={{0,1},{1,2},{2,3},{4,5},{5,6},{6,7},{8,9},{9,10},{10,11},{12,13},{... | collective-permute-start | bytes 393224 | tf_op jit(solution)/shard_map/ppermute | solution.py:23
  227.9 18.4 %copy-start.3 = (f32[4,32,64]{2,1,0:T(8,128)S(1)}, f32[4,32,64]{2,1,0:T(8,128)}, u32[]{:S(2)}) copy-start(f32[4,32,64]{2,1,0:T(8,128)} %copy-done.2) | copy-start | bytes 98308
  227.9 18.4 %copy-start.5 = (f32[4,32,64]{2,1,0:T(8,128)S(1)}, f32[4,32,64]{2,1,0:T(8,128)}, u32[]{:S(2)}) copy-start(f32[4,32,64]{2,1,0:T(8,128)} %copy-done.4) | copy-start | bytes 98308
  227.9 18.4 %copy-start.18 = (pred[4]{0:T(512)(128)(4,1)S(1)}, pred[4]{0:T(512)(128)(4,1)}, u32[]{:S(2)}) copy-start(pred[4]{0:T(512)(128)(4,1)} %compare_and_fusion.2) | copy-start | bytes 16
  227.9 7.0 %collective-permute-start.31 = (f32[1,4,2,32,64]{4,3,2,1,0:T(8,128)S(1)}, f32[1,4,2,32,64]{4,3,2,1,0:T(8,128)S(1)}, u32[]{:S(2)}, u32[]{:S(2)}) collective-permute-start(f32[1,4,2,32,64]{4,3,2,1,0:T(8,128)S(1)} %fusion), channel_id=1, source_target_pairs={{1,0},{2,1},{3,2},{5,4},{6,5},{7,6},{9,8},{10,9},{11,10},{13,12},{... | collective-permute-start | bytes 196616 | tf_op jit(solution)/shard_map/ppermute | solution.py:26
  229.4 7.1 %collective-permute-start.30 = (f32[1,4,2,32,64]{4,3,2,1,0:T(8,128)S(1)}, f32[1,4,2,32,64]{4,3,2,1,0:T(8,128)S(1)}, u32[]{:S(2)}, u32[]{:S(2)}) collective-permute-start(f32[1,4,2,32,64]{4,3,2,1,0:T(8,128)S(1)} %fusion), channel_id=1, source_target_pairs={{0,1},{1,2},{2,3},{4,5},{5,6},{6,7},{8,9},{9,10},{10,11},{12,13},{... | collective-permute-start | bytes 196616 | tf_op jit(solution)/shard_map/ppermute | solution.py:23
  236.5 9.8 %collective-permute-start.32 = (f32[1,4,4,32,64]{4,3,2,1,0:T(8,128)S(1)}, f32[1,4,4,32,64]{4,3,2,1,0:T(8,128)S(1)}, u32[]{:S(2)}, u32[]{:S(2)}) collective-permute-start(f32[1,4,4,32,64]{4,3,2,1,0:T(8,128)S(1)} %slice.1827), channel_id=1, source_target_pairs={{0,4},{4,8},{8,12},{12,16},{16,20},{20,24},{24,28},{28,32},{32,36}... | collective-permute-start | bytes 393224 | tf_op jit(solution)/shard_map/ppermute | solution.py:34
  246.7 8.4 %collective-permute-start.33 = (f32[1,4,2,32,64]{4,3,2,1,0:T(8,128)S(1)}, f32[1,4,2,32,64]{4,3,2,1,0:T(8,128)S(1)}, u32[]{:S(2)}, u32[]{:S(2)}) collective-permute-start(f32[1,4,2,32,64]{4,3,2,1,0:T(8,128)S(1)} %slice.1835), channel_id=1, source_target_pairs={{0,4},{4,8},{8,12},{12,16},{16,20},{20,24},{24,28},{28,32},{32,36}... | collective-permute-start | bytes 196616 | tf_op jit(solution)/shard_map/ppermute | solution.py:34
  324.3 7.8 %collective-permute-start.35 = (f32[1,4,1,32,64]{4,3,2,1,0:T(8,128)S(1)}, f32[1,4,1,32,64]{4,3,2,1,0:T(8,128)S(1)}, u32[]{:S(2)}, u32[]{:S(2)}) collective-permute-start(f32[1,4,1,32,64]{4,3,2,1,0:T(8,128)S(1)} %get-tuple-element.99), channel_id=1, source_target_pairs={{1,0},{2,1},{3,2},{5,4},{6,5},{7,6},{9,8},{10,9},{11,10},{13,12},{... | collective-permute-start | bytes 98312 | tf_op jit(solution)/shard_map/ppermute | solution.py:26
  325.6 6.5 %collective-permute-start.36 = (f32[1,4,1,32,64]{4,3,2,1,0:T(8,128)S(1)}, f32[1,4,1,32,64]{4,3,2,1,0:T(8,128)S(1)}, u32[]{:S(2)}, u32[]{:S(2)}) collective-permute-start(f32[1,4,1,32,64]{4,3,2,1,0:T(8,128)S(1)} %get-tuple-element.100), channel_id=1, source_target_pairs={{0,1},{1,2},{2,3},{4,5},{5,6},{6,7},{8,9},{9,10},{10,11},{12,13},{... | collective-permute-start | bytes 98312 | tf_op jit(solution)/shard_map/ppermute | solution.py:23
  330.2 8.4 %collective-permute-start.34 = (f32[1,4,2,32,64]{4,3,2,1,0:T(8,128)S(1)}, f32[1,4,2,32,64]{4,3,2,1,0:T(8,128)S(1)}, u32[]{:S(2)}, u32[]{:S(2)}) collective-permute-start(f32[1,4,2,32,64]{4,3,2,1,0:T(8,128)S(1)} %fusion.221), channel_id=1, source_target_pairs={{0,4},{4,8},{8,12},{12,16},{16,20},{20,24},{24,28},{28,32},{32,36}... | collective-permute-start | bytes 196616 | tf_op jit(solution)/shard_map/ppermute | solution.py:34
  339.1 12.6 %collective-permute-start.37 = (f32[1,4,4,64,128]{4,3,2,1,0:T(8,128)S(1)}, f32[1,4,4,64,128]{4,3,2,1,0:T(8,128)S(1)}, u32[]{:S(2)}, u32[]{:S(2)}) collective-permute-start(f32[1,4,4,64,128]{4,3,2,1,0:T(8,128)S(1)} %add.604), channel_id=1, source_target_pairs={{0,4},{4,8},{8,12},{12,16},{16,20},{20,24},{24,28},{28,32},{32,36}... | collective-permute-start | bytes 1572872 | tf_op jit(solution)/shard_map/ppermute | solution.py:34
  341.1 6.9 %collective-permute-start.38 = (f32[1,4,1,64,128]{4,3,2,1,0:T(8,128)S(1)}, f32[1,4,1,64,128]{4,3,2,1,0:T(8,128)S(1)}, u32[]{:S(2)}, u32[]{:S(2)}) collective-permute-start(f32[1,4,1,64,128]{4,3,2,1,0:T(8,128)S(1)} %get-tuple-element.39), channel_id=1, source_target_pairs={{1,0},{2,1},{3,2},{5,4},{6,5},{7,6},{9,8},{10,9},{11,10},{13,12},{... | collective-permute-start | bytes 393224 | tf_op jit(solution)/shard_map/ppermute | solution.py:26
  342.4 7.1 %collective-permute-start.39 = (f32[1,4,1,64,128]{4,3,2,1,0:T(8,128)S(1)}, f32[1,4,1,64,128]{4,3,2,1,0:T(8,128)S(1)}, u32[]{:S(2)}, u32[]{:S(2)}) collective-permute-start(f32[1,4,1,64,128]{4,3,2,1,0:T(8,128)S(1)} %get-tuple-element.40), channel_id=1, source_target_pairs={{0,1},{1,2},{2,3},{4,5},{5,6},{6,7},{8,9},{9,10},{10,11},{12,13},{... | collective-permute-start | bytes 393224 | tf_op jit(solution)/shard_map/ppermute | solution.py:23
  352.3 12.6 %collective-permute-start.40 = (f32[1,4,4,64,128]{4,3,2,1,0:T(8,128)S(1)}, f32[1,4,4,64,128]{4,3,2,1,0:T(8,128)S(1)}, u32[]{:S(2)}, u32[]{:S(2)}) collective-permute-start(f32[1,4,4,64,128]{4,3,2,1,0:T(8,128)S(1)} %fusion.27), channel_id=1, source_target_pairs={{0,4},{4,8},{8,12},{12,16},{16,20},{20,24},{24,28},{28,32},{32,36}... | collective-permute-start | bytes 1572872 | tf_op jit(solution)/shard_map/ppermute | solution.py:34
  354.2 6.9 %collective-permute-start.41 = (f32[1,4,1,64,128]{4,3,2,1,0:T(8,128)S(1)}, f32[1,4,1,64,128]{4,3,2,1,0:T(8,128)S(1)}, u32[]{:S(2)}, u32[]{:S(2)}) collective-permute-start(f32[1,4,1,64,128]{4,3,2,1,0:T(8,128)S(1)} %get-tuple-element.35), channel_id=1, source_target_pairs={{1,0},{2,1},{3,2},{5,4},{6,5},{7,6},{9,8},{10,9},{11,10},{13,12},{... | collective-permute-start | bytes 393224 | tf_op jit(solution)/shard_map/ppermute | solution.py:26
  355.5 7.1 %collective-permute-start.42 = (f32[1,4,1,64,128]{4,3,2,1,0:T(8,128)S(1)}, f32[1,4,1,64,128]{4,3,2,1,0:T(8,128)S(1)}, u32[]{:S(2)}, u32[]{:S(2)}) collective-permute-start(f32[1,4,1,64,128]{4,3,2,1,0:T(8,128)S(1)} %get-tuple-element.36), channel_id=1, source_target_pairs={{0,1},{1,2},{2,3},{4,5},{5,6},{6,7},{8,9},{9,10},{10,11},{12,13},{... | collective-permute-start | bytes 393224 | tf_op jit(solution)/shard_map/ppermute | solution.py:23
Sparse Core Ops, SparseCore 0:
  95.9 26.4 all-gather.4
  279.9 24.4 all-gather.6

commit v12 on v9

--- a/solution.py
+++ b/solution.py
@@ -189,8 +189,9 @@
 
 def gather_all(flat):
     across = lax.all_gather(flat, "tm", axis=0, tiled=True)
-    whole = lax.all_gather(across, "space", axis=1, tiled=True)
-    return whole.reshape(-1, flat.shape[1])
+    whole = lax.all_gather(across.reshape(1, -1), "space", axis=0, tiled=True)
+    whole = whole.reshape(lax.axis_size("space"), lax.axis_size("tm"), flat.shape[1])
+    return whole.transpose(1, 0, 2).reshape(-1, flat.shape[1])
 
 
 def coarse_correction(source, metric_two, gathered):

time: 368 us -> 382 us (1.038)
  other arithmetic: 12.6 us -> 21.2 us
  blocking collectives: 46.5 us -> 50.8 us
    all_gather x0 -> x2, other arithmetic: none -> 8.7 us  [gather_all(): whole = lax.all_gather(across.reshape(1, -1), 'space', axis=0, tiled=True)]
    all_gather x2, blocking collectives: 46.5 us -> 50.8 us  [gather_all(): across = lax.all_gather(flat, 'tm', axis=0, tiled=True)]
where the time goes in v12:
time: 382 us; the launch traced here: 380 us
  waiting for transfers between devices  128 us (34%)
  starting transfers between devices  117 us (31%)
  blocking collectives  50.8 us (13%)
  Pallas kernels  28.5 us (7%)
  other arithmetic  21.2 us (6%)
  local copies, waits for them, and re-layouts  18.1 us (5%)
  between operations  14.6 us (4%)
    ppermute x15, starting transfers between devices, with_halo(): lax.ppermute(lax.slice_in_dim(block, block.shape[dim] - width, None, axis...  68.5 us
    ppermute x15, waiting for transfers between devices, from_behind(): return lax.ppermute(array, axis, pairs)  54.8 us
    all_gather x2, blocking collectives, gather_all(): across = lax.all_gather(flat, 'tm', axis=0, tiled=True)  50.8 us
    all_gather x2, waiting for transfers between devices, gather_all(): whole = lax.all_gather(across.reshape(1, -1), 'space', axis=0, tiled=True)  49.1 us
    ppermute x15, starting transfers between devices, from_behind(): return lax.ppermute(array, axis, pairs)  28.9 us
    pallas_call x2, Pallas kernels, coarse_solve(): pl.pallas_call(kernel, out_shape=jax.ShapeDtypeStruct(flat_source.shape,...  28.5 us
    ppermute x15, starting transfers between devices, with_halo(): lax.ppermute(lax.slice_in_dim(block, 0, width, axis=dim), axis, backward)  19.4 us
    ppermute x15, waiting for transfers between devices, with_halo(): lax.ppermute(lax.slice_in_dim(block, block.shape[dim] - width, None, axis...  13.7 us
  transfers between devices with their start and end apart: 47, of which 35 were waited for; matrix products, arithmetic and copies ran while one was open for 1% of the time, Pallas kernels for 0%

profile of v12, /device:TPU:2, one launch (start us, length us, event | category | flops | bytes accessed | tf_op | source)
XLA Modules:
  0.0 380.5 jit_solution(18091788298405216269)
XLA Ops:
  9.8 2.1 collective-permute-start
  13.2 4.6 %collective-permute-start.2 = (f32[1,4,1,64,128]{4,3,2,1,0:T(8,128)S(1)}, f32[1,4,1,64,128]{4,3,2,1,0:T(8,128)S(1)}, u32[]{:S(2)}, u32[]{:S(2)}) collective-permute-start(f32[1,4,1,64,128]{4,3,2,1,0:T(8,128)S(1)} %get-tuple-element.68), channel_id=1, source_target_pairs={{0,1},{1,2},{2,3},{4,5},{5,6},{6,7},{8,9},{9,10},{10,11},{12,13},{... | collective-permute-start | bytes 393224 | tf_op jit(solution)/shard_map/ppermute | solution.py:23
  19.2 1.7 collective-permute-done.2
  23.0 1.9 collective-permute-start.3
  26.3 4.6 %collective-permute-start.5 = (f32[1,4,1,64,128]{4,3,2,1,0:T(8,128)S(1)}, f32[1,4,1,64,128]{4,3,2,1,0:T(8,128)S(1)}, u32[]{:S(2)}, u32[]{:S(2)}) collective-permute-start(f32[1,4,1,64,128]{4,3,2,1,0:T(8,128)S(1)} %get-tuple-element.64), channel_id=1, source_target_pairs={{0,1},{1,2},{2,3},{4,5},{5,6},{6,7},{8,9},{9,10},{10,11},{12,13},{... | collective-permute-start | bytes 393224 | tf_op jit(solution)/shard_map/ppermute | solution.py:23
  30.9 2.2 collective-permute-done.4
  37.9 4.5 %collective-permute-start.8 = (f32[1,4,1,32,64]{4,3,2,1,0:T(8,128)S(1)}, f32[1,4,1,32,64]{4,3,2,1,0:T(8,128)S(1)}, u32[]{:S(2)}, u32[]{:S(2)}) collective-permute-start(f32[1,4,1,32,64]{4,3,2,1,0:T(8,128)S(1)} %get-tuple-element.108), channel_id=1, source_target_pairs={{0,1},{1,2},{2,3},{4,5},{5,6},{6,7},{8,9},{9,10},{10,11},{12,13},{... | collective-permute-start | bytes 98312 | tf_op jit(solution)/shard_map/ppermute | solution.py:23
  42.5 1.9 collective-permute-start.6
  44.6 6.3 %collective-permute-done.6 = f32[1,4,2,32,64]{4,3,2,1,0:T(8,128)S(1)} collective-permute-done((f32[1,4,2,32,64]{4,3,2,1,0:T(8,128)S(1)}, f32[1,4,2,32,64]{4,3,2,1,0:T(8,128)S(1)}, u32[]{:S(2)}, u32[]{:S(2)}) %collective-permute-start.6) | collective-permute-done | bytes 65568 | tf_op jit(solution)/shard_map/ppermute | solution.py:34
  52.4 4.5 %collective-permute-start.11 = (f32[1,4,1,32,64]{4,3,2,1,0:T(8,128)S(1)}, f32[1,4,1,32,64]{4,3,2,1,0:T(8,128)S(1)}, u32[]{:S(2)}, u32[]{:S(2)}) collective-permute-start(f32[1,4,1,32,64]{4,3,2,1,0:T(8,128)S(1)} %get-tuple-element.104), channel_id=1, source_target_pairs={{0,1},{1,2},{2,3},{4,5},{5,6},{6,7},{8,9},{9,10},{10,11},{12,13},{... | collective-permute-start | bytes 98312 | tf_op jit(solution)/shard_map/ppermute | solution.py:23
  57.2 1.9 collective-permute-start.9
  59.2 6.3 %collective-permute-done.9 = f32[1,4,2,32,64]{4,3,2,1,0:T(8,128)S(1)} collective-permute-done((f32[1,4,2,32,64]{4,3,2,1,0:T(8,128)S(1)}, f32[1,4,2,32,64]{4,3,2,1,0:T(8,128)S(1)}, u32[]{:S(2)}, u32[]{:S(2)}) %collective-permute-start.9) | collective-permute-done | bytes 65568 | tf_op jit(solution)/shard_map/ppermute | solution.py:34
  66.2 25.5 %all-gather = f32[32,1,2560]{2,1,0:T(1,128)} all-gather(f32[1,1,2560]{2,1,0:T(1,128)S(1)} %maximum_bitcast_fusion), channel_id=1, replica_groups=mesh['tm'=32,'space'=4] {'tm'}, dimensions={0}, use_global_device_ids=true | all-gather | bytes 337920 | tf_op jit(solution)/shard_map/all_gather | solution.py:191
  91.9 25.5 %all-gather.7.cloned.1.call-done = f32[4,1,81920]{2,1,0:T(1,128)} async-done(((f32[1,1,81920]{2,1,0:T(1,128)}), f32[4,1,81920]{2,1,0:T(1,128)}) %all-gather.7.cloned.1.call-update) | async-done | bytes 1310736 | tf_op jit(solution)/shard_map/all_gather | solution.py:192
  117.4 4.7 %reduce = f32[4,81920]{1,0:T(4,128)S(1)} reduce(f32[4,1,81920]{2,1,0:T(1,128)} %all-gather.7.cloned.1.call-done, f32[]{:T(128)} %constant.145), dimensions={1}, to_apply=%all-gather.1.reduce_sub_computation | reduce | bytes 2621444 | tf_op jit(solution)/shard_map/all_gather | solution.py:192
  122.6 1.9 copy.15
  124.5 1.7 reshape.873
  127.3 2.5 reshape_transpose_reshape.7.src_ref
  131.5 14.2 %shard_map.37 = f32[32,16,512]{2,1,0:T(8,128)} custom-call(f32[32,16,512]{2,1,0:T(8,128)} %reshape_transpose_reshape.7.src_ref, f32[32,16,512]{2,1,0:T(8,128)} %reshape.874.met_ref), custom_call_target="tpu_custom_call" | custom-call | tf_op jit(solution)/shard_map/pallas_call | solution.py:161
  149.9 4.5 %collective-permute-start.14 = (f32[1,4,1,32,64]{4,3,2,1,0:T(8,128)S(1)}, f32[1,4,1,32,64]{4,3,2,1,0:T(8,128)S(1)}, u32[]{:S(2)}, u32[]{:S(2)}) collective-permute-start(f32[1,4,1,32,64]{4,3,2,1,0:T(8,128)S(1)} %get-tuple-element.100), channel_id=1, source_target_pairs={{0,1},{1,2},{2,3},{4,5},{5,6},{6,7},{8,9},{9,10},{10,11},{12,13},{... | collective-permute-start | bytes 98312 | tf_op jit(solution)/shard_map/ppermute | solution.py:23
  154.4 1.9 collective-permute-start.12
  156.5 6.3 %collective-permute-done.12 = f32[1,4,2,32,64]{4,3,2,1,0:T(8,128)S(1)} collective-permute-done((f32[1,4,2,32,64]{4,3,2,1,0:T(8,128)S(1)}, f32[1,4,2,32,64]{4,3,2,1,0:T(8,128)S(1)}, u32[]{:S(2)}, u32[]{:S(2)}) %collective-permute-start.12) | collective-permute-done | bytes 65568 | tf_op jit(solution)/shard_map/ppermute | solution.py:34
  163.4 1.9 collective-permute-start.15
  166.6 4.6 %collective-permute-start.17 = (f32[1,4,1,64,128]{4,3,2,1,0:T(8,128)S(1)}, f32[1,4,1,64,128]{4,3,2,1,0:T(8,128)S(1)}, u32[]{:S(2)}, u32[]{:S(2)}) collective-permute-start(f32[1,4,1,64,128]{4,3,2,1,0:T(8,128)S(1)} %get-tuple-element.60), channel_id=1, source_target_pairs={{0,1},{1,2},{2,3},{4,5},{5,6},{6,7},{8,9},{9,10},{10,11},{12,13},{... | collective-permute-start | bytes 393224 | tf_op jit(solution)/shard_map/ppermute | solution.py:23
  172.2 1.5 collective-permute-done.17
  173.9 2.1 collective-permute-done.15
  176.5 1.9 collective-permute-start.18
  179.8 4.6 %collective-permute-start.20 = (f32[1,4,1,64,128]{4,3,2,1,0:T(8,128)S(1)}, f32[1,4,1,64,128]{4,3,2,1,0:T(8,128)S(1)}, u32[]{:S(2)}, u32[]{:S(2)}) collective-permute-start(f32[1,4,1,64,128]{4,3,2,1,0:T(8,128)S(1)} %get-tuple-element.56), channel_id=1, source_target_pairs={{0,1},{1,2},{2,3},{4,5},{5,6},{6,7},{8,9},{9,10},{10,11},{12,13},{... | collective-permute-start | bytes 393224 | tf_op jit(solution)/shard_map/ppermute | solution.py:23
  185.4 1.5 collective-permute-done.20
  187.1 2.1 collective-permute-done.18
  189.7 1.9 collective-permute-start.21
  193.0 4.6 %collective-permute-start.23 = (f32[1,4,1,64,128]{4,3,2,1,0:T(8,128)S(1)}, f32[1,4,1,64,128]{4,3,2,1,0:T(8,128)S(1)}, u32[]{:S(2)}, u32[]{:S(2)}) collective-permute-start(f32[1,4,1,64,128]{4,3,2,1,0:T(8,128)S(1)} %get-tuple-element.52), channel_id=1, source_target_pairs={{0,1},{1,2},{2,3},{4,5},{5,6},{6,7},{8,9},{9,10},{10,11},{12,13},{... | collective-permute-start | bytes 393224 | tf_op jit(solution)/shard_map/ppermute | solution.py:23
  198.5 1.5 collective-permute-done.23
  200.2 2.1 collective-permute-done.21
  202.9 1.9 collective-permute-start.24
  206.1 4.8 %collective-permute-start.26 = (f32[1,4,1,64,128]{4,3,2,1,0:T(8,128)S(1)}, f32[1,4,1,64,128]{4,3,2,1,0:T(8,128)S(1)}, u32[]{:S(2)}, u32[]{:S(2)}) collective-permute-start(f32[1,4,1,64,128]{4,3,2,1,0:T(8,128)S(1)} %get-tuple-element.48), channel_id=1, source_target_pairs={{0,1},{1,2},{2,3},{4,5},{5,6},{6,7},{8,9},{9,10},{10,11},{12,13},{... | collective-permute-start | bytes 393224 | tf_op jit(solution)/shard_map/ppermute | solution.py:23
  211.7 1.5 collective-permute-done.26
  213.4 2.1 collective-permute-done.24
  216.0 1.9 collective-permute-start.27
  219.3 4.6 %collective-permute-start.29 = (f32[1,4,1,64,128]{4,3,2,1,0:T(8,128)S(1)}, f32[1,4,1,64,128]{4,3,2,1,0:T(8,128)S(1)}, u32[]{:S(2)}, u32[]{:S(2)}) collective-permute-start(f32[1,4,1,64,128]{4,3,2,1,0:T(8,128)S(1)} %get-tuple-element.44), channel_id=1, source_target_pairs={{0,1},{1,2},{2,3},{4,5},{5,6},{6,7},{8,9},{9,10},{10,11},{12,13},{... | collective-permute-start | bytes 393224 | tf_op jit(solution)/shard_map/ppermute | solution.py:23
  224.8 1.5 collective-permute-done.29
  226.5 2.1 collective-permute-done.27
  230.9 4.5 %collective-permute-start.32 = (f32[1,4,1,32,64]{4,3,2,1,0:T(8,128)S(1)}, f32[1,4,1,32,64]{4,3,2,1,0:T(8,128)S(1)}, u32[]{:S(2)}, u32[]{:S(2)}) collective-permute-start(f32[1,4,1,32,64]{4,3,2,1,0:T(8,128)S(1)} %get-tuple-element.96), channel_id=1, source_target_pairs={{0,1},{1,2},{2,3},{4,5},{5,6},{6,7},{8,9},{9,10},{10,11},{12,13},{... | collective-permute-start | bytes 98312 | tf_op jit(solution)/shard_map/ppermute | solution.py:23
  235.5 1.9 collective-permute-start.30
  237.5 6.3 %collective-permute-done.30 = f32[1,4,2,32,64]{4,3,2,1,0:T(8,128)S(1)} collective-permute-done((f32[1,4,2,32,64]{4,3,2,1,0:T(8,128)S(1)}, f32[1,4,2,32,64]{4,3,2,1,0:T(8,128)S(1)}, u32[]{:S(2)}, u32[]{:S(2)}) %collective-permute-start.30) | collective-permute-done | bytes 65568 | tf_op jit(solution)/shard_map/ppermute | solution.py:34
  245.3 4.5 %collective-permute-start.35 = (f32[1,4,1,32,64]{4,3,2,1,0:T(8,128)S(1)}, f32[1,4,1,32,64]{4,3,2,1,0:T(8,128)S(1)}, u32[]{:S(2)}, u32[]{:S(2)}) collective-permute-start(f32[1,4,1,32,64]{4,3,2,1,0:T(8,128)S(1)} %get-tuple-element.92), channel_id=1, source_target_pairs={{0,1},{1,2},{2,3},{4,5},{5,6},{6,7},{8,9},{9,10},{10,11},{12,13},{... | collective-permute-start | bytes 98312 | tf_op jit(solution)/shard_map/ppermute | solution.py:23
  249.9 1.9 collective-permute-start.33
  252.0 6.3 %collective-permute-done.33 = f32[1,4,2,32,64]{4,3,2,1,0:T(8,128)S(1)} collective-permute-done((f32[1,4,2,32,64]{4,3,2,1,0:T(8,128)S(1)}, f32[1,4,2,32,64]{4,3,2,1,0:T(8,128)S(1)}, u32[]{:S(2)}, u32[]{:S(2)}) %collective-permute-start.33) | collective-permute-done | bytes 65568 | tf_op jit(solution)/shard_map/ppermute | solution.py:34
  258.9 25.3 %all-gather.2 = f32[32,1,2048]{2,1,0:T(1,128)} all-gather(f32[1,1,2048]{2,1,0:T(1,128)S(1)} %reshape.898), channel_id=1, replica_groups=mesh['tm'=32,'space'=4] {'tm'}, dimensions={0}, use_global_device_ids=true | all-gather | bytes 270336 | tf_op jit(solution)/shard_map/all_gather | solution.py:191
  284.3 23.6 %all-gather.9.cloned.1.call-done = f32[4,1,65536]{2,1,0:T(1,128)} async-done(((f32[1,1,65536]{2,1,0:T(1,128)}), f32[4,1,65536]{2,1,0:T(1,128)}) %all-gather.9.cloned.1.call-update) | async-done | bytes 1048592 | tf_op jit(solution)/shard_map/all_gather | solution.py:192
  307.9 4.0 %reduce.1 = f32[4,65536]{1,0:T(4,128)S(1)} reduce(f32[4,1,65536]{2,1,0:T(1,128)} %all-gather.9.cloned.1.call-done, f32[]{:T(128)} %constant.145), dimensions={1}, to_apply=%all-gather.3.reduce_sub_computation | reduce | bytes 2097156 | tf_op jit(solution)/shard_map/all_gather | solution.py:192
  313.2 1.5 reshape_transpose_reshape_reshape.3.src_ref
  314.7 14.2 %shard_map.38 = f32[32,16,512]{2,1,0:T(8,128)} custom-call(f32[32,16,512]{2,1,0:T(8,128)} %reshape_transpose_reshape_reshape.3.src_ref, f32[32,16,512]{2,1,0:T(8,128)} %reshape.874.met_ref), custom_call_target="tpu_custom_call" | custom-call | tf_op jit(solution)/shard_map/pallas_call | solution.py:161
  333.0 4.5 %collective-permute-start.38 = (f32[1,4,1,32,64]{4,3,2,1,0:T(8,128)S(1)}, f32[1,4,1,32,64]{4,3,2,1,0:T(8,128)S(1)}, u32[]{:S(2)}, u32[]{:S(2)}) collective-permute-start(f32[1,4,1,32,64]{4,3,2,1,0:T(8,128)S(1)} %get-tuple-element.88), channel_id=1, source_target_pairs={{0,1},{1,2},{2,3},{4,5},{5,6},{6,7},{8,9},{9,10},{10,11},{12,13},{... | collective-permute-start | bytes 98312 | tf_op jit(solution)/shard_map/ppermute | solution.py:23
  337.6 1.9 collective-permute-start.36
  339.6 6.3 %collective-permute-done.36 = f32[1,4,2,32,64]{4,3,2,1,0:T(8,128)S(1)} collective-permute-done((f32[1,4,2,32,64]{4,3,2,1,0:T(8,128)S(1)}, f32[1,4,2,32,64]{4,3,2,1,0:T(8,128)S(1)}, u32[]{:S(2)}, u32[]{:S(2)}) %collective-permute-start.36) | collective-permute-done | bytes 65568 | tf_op jit(solution)/shard_map/ppermute | solution.py:34
  346.5 1.9 collective-permute-start.39
  349.8 4.6 %collective-permute-start.41 = (f32[1,4,1,64,128]{4,3,2,1,0:T(8,128)S(1)}, f32[1,4,1,64,128]{4,3,2,1,0:T(8,128)S(1)}, u32[]{:S(2)}, u32[]{:S(2)}) collective-permute-start(f32[1,4,1,64,128]{4,3,2,1,0:T(8,128)S(1)} %get-tuple-element.40), channel_id=1, source_target_pairs={{0,1},{1,2},{2,3},{4,5},{5,6},{6,7},{8,9},{9,10},{10,11},{12,13},{... | collective-permute-start | bytes 393224 | tf_op jit(solution)/shard_map/ppermute | solution.py:23
  355.3 1.5 collective-permute-done.41
  357.0 2.1 collective-permute-done.39
  359.7 1.9 collective-permute-start.42
  362.9 4.6 %collective-permute-start.44 = (f32[1,4,1,64,128]{4,3,2,1,0:T(8,128)S(1)}, f32[1,4,1,64,128]{4,3,2,1,0:T(8,128)S(1)}, u32[]{:S(2)}, u32[]{:S(2)}) collective-permute-start(f32[1,4,1,64,128]{4,3,2,1,0:T(8,128)S(1)} %get-tuple-element.36), channel_id=1, source_target_pairs={{0,1},{1,2},{2,3},{4,5},{5,6},{6,7},{8,9},{9,10},{10,11},{12,13},{... | collective-permute-start | bytes 393224 | tf_op jit(solution)/shard_map/ppermute | solution.py:23
  368.5 1.5 collective-permute-done.44
  370.2 2.1 collective-permute-done.42
  (168 shorter events, 56.6 us)
Async XLA Ops:
  6.5 110.9 %all-gather.7.cloned.1.call-start = ((), (), s32[]{:S(2)}) async-start(), calls=%async_computation | async-start | bytes 1638400 | tf_op jit(solution)/shard_map/all_gather | solution.py:192
  7.5 10.2 %copy-start.1 = (f32[1,4,64,128]{3,2,1,0:T(8,128)S(1)}, f32[1,4,64,128]{3,2,1,0:T(8,128)}, u32[]{:S(2)}) copy-start(f32[1,4,64,128]{3,2,1,0:T(8,128)} %param.4) | copy-start | bytes 393220
  9.8 12.8 %copy-start = (f32[1,4,4,64,128]{4,3,2,1,0:T(8,128)S(1)}, f32[1,4,4,64,128]{4,3,2,1,0:T(8,128)}, u32[]{:S(2)}) copy-start(f32[1,4,4,64,128]{4,3,2,1,0:T(8,128)} %param.3) | copy-start | bytes 1572868
  9.8 12.7 %collective-permute-start = (f32[1,4,4,64,128]{4,3,2,1,0:T(8,128)S(1)}, f32[1,4,4,64,128]{4,3,2,1,0:T(8,128)S(1)}, u32[]{:S(2)}, u32[]{:S(2)}) collective-permute-start(f32[1,4,4,64,128]{4,3,2,1,0:T(8,128)S(1)} %get-tuple-element.9), channel_id=1, source_target_pairs={{0,4},{4,8},{8,12},{12,16},{16,20},{20,24},{24,28},{28,32},{32,36}... | collective-permute-start | bytes 1572872 | tf_op jit(solution)/shard_map/ppermute | solution.py:34
  11.9 7.4 %collective-permute-start.1 = (f32[1,4,1,64,128]{4,3,2,1,0:T(8,128)S(1)}, f32[1,4,1,64,128]{4,3,2,1,0:T(8,128)S(1)}, u32[]{:S(2)}, u32[]{:S(2)}) collective-permute-start(f32[1,4,1,64,128]{4,3,2,1,0:T(8,128)S(1)} %get-tuple-element.67), channel_id=1, source_target_pairs={{1,0},{2,1},{3,2},{5,4},{6,5},{7,6},{9,8},{10,9},{11,10},{13,12},{... | collective-permute-start | bytes 393224 | tf_op jit(solution)/shard_map/ppermute | solution.py:26
  13.2 7.8 %collective-permute-start.2 = (f32[1,4,1,64,128]{4,3,2,1,0:T(8,128)S(1)}, f32[1,4,1,64,128]{4,3,2,1,0:T(8,128)S(1)}, u32[]{:S(2)}, u32[]{:S(2)}) collective-permute-start(f32[1,4,1,64,128]{4,3,2,1,0:T(8,128)S(1)} %get-tuple-element.68), channel_id=1, source_target_pairs={{0,1},{1,2},{2,3},{4,5},{5,6},{6,7},{8,9},{9,10},{10,11},{12,13},{... | collective-permute-start | bytes 393224 | tf_op jit(solution)/shard_map/ppermute | solution.py:23
  23.0 12.6 %collective-permute-start.3 = (f32[1,4,4,64,128]{4,3,2,1,0:T(8,128)S(1)}, f32[1,4,4,64,128]{4,3,2,1,0:T(8,128)S(1)}, u32[]{:S(2)}, u32[]{:S(2)}) collective-permute-start(f32[1,4,4,64,128]{4,3,2,1,0:T(8,128)S(1)} %fusion.119), channel_id=1, source_target_pairs={{0,4},{4,8},{8,12},{12,16},{16,20},{20,24},{24,28},{28,32},{32,36}... | collective-permute-start | bytes 1572872 | tf_op jit(solution)/shard_map/ppermute | solution.py:34
  25.0 8.1 %collective-permute-start.4 = (f32[1,4,1,64,128]{4,3,2,1,0:T(8,128)S(1)}, f32[1,4,1,64,128]{4,3,2,1,0:T(8,128)S(1)}, u32[]{:S(2)}, u32[]{:S(2)}) collective-permute-start(f32[1,4,1,64,128]{4,3,2,1,0:T(8,128)S(1)} %get-tuple-element.63), channel_id=1, source_target_pairs={{1,0},{2,1},{3,2},{5,4},{6,5},{7,6},{9,8},{10,9},{11,10},{13,12},{... | collective-permute-start | bytes 393224 | tf_op jit(solution)/shard_map/ppermute | solution.py:26
  26.3 8.3 %collective-permute-start.5 = (f32[1,4,1,64,128]{4,3,2,1,0:T(8,128)S(1)}, f32[1,4,1,64,128]{4,3,2,1,0:T(8,128)S(1)}, u32[]{:S(2)}, u32[]{:S(2)}) collective-permute-start(f32[1,4,1,64,128]{4,3,2,1,0:T(8,128)S(1)} %get-tuple-element.64), channel_id=1, source_target_pairs={{0,1},{1,2},{2,3},{4,5},{5,6},{6,7},{8,9},{9,10},{10,11},{12,13},{... | collective-permute-start | bytes 393224 | tf_op jit(solution)/shard_map/ppermute | solution.py:23
  36.6 7.8 %collective-permute-start.7 = (f32[1,4,1,32,64]{4,3,2,1,0:T(8,128)S(1)}, f32[1,4,1,32,64]{4,3,2,1,0:T(8,128)S(1)}, u32[]{:S(2)}, u32[]{:S(2)}) collective-permute-start(f32[1,4,1,32,64]{4,3,2,1,0:T(8,128)S(1)} %get-tuple-element.107), channel_id=1, source_target_pairs={{1,0},{2,1},{3,2},{5,4},{6,5},{7,6},{9,8},{10,9},{11,10},{13,12},{... | collective-permute-start | bytes 98312 | tf_op jit(solution)/shard_map/ppermute | solution.py:26
  37.9 6.5 %collective-permute-start.8 = (f32[1,4,1,32,64]{4,3,2,1,0:T(8,128)S(1)}, f32[1,4,1,32,64]{4,3,2,1,0:T(8,128)S(1)}, u32[]{:S(2)}, u32[]{:S(2)}) collective-permute-start(f32[1,4,1,32,64]{4,3,2,1,0:T(8,128)S(1)} %get-tuple-element.108), channel_id=1, source_target_pairs={{0,1},{1,2},{2,3},{4,5},{5,6},{6,7},{8,9},{9,10},{10,11},{12,13},{... | collective-permute-start | bytes 98312 | tf_op jit(solution)/shard_map/ppermute | solution.py:23
  42.5 8.4 %collective-permute-start.6 = (f32[1,4,2,32,64]{4,3,2,1,0:T(8,128)S(1)}, f32[1,4,2,32,64]{4,3,2,1,0:T(8,128)S(1)}, u32[]{:S(2)}, u32[]{:S(2)}) collective-permute-start(f32[1,4,2,32,64]{4,3,2,1,0:T(8,128)S(1)} %fusion.388), channel_id=1, source_target_pairs={{0,4},{4,8},{8,12},{12,16},{16,20},{20,24},{24,28},{28,32},{32,36}... | collective-permute-start | bytes 196616 | tf_op jit(solution)/shard_map/ppermute | solution.py:34
  51.1 8.0 %collective-permute-start.10 = (f32[1,4,1,32,64]{4,3,2,1,0:T(8,128)S(1)}, f32[1,4,1,32,64]{4,3,2,1,0:T(8,128)S(1)}, u32[]{:S(2)}, u32[]{:S(2)}) collective-permute-start(f32[1,4,1,32,64]{4,3,2,1,0:T(8,128)S(1)} %get-tuple-element.103), channel_id=1, source_target_pairs={{1,0},{2,1},{3,2},{5,4},{6,5},{7,6},{9,8},{10,9},{11,10},{13,12},{... | collective-permute-start | bytes 98312 | tf_op jit(solution)/shard_map/ppermute | solution.py:26
  52.4 6.7 %collective-permute-start.11 = (f32[1,4,1,32,64]{4,3,2,1,0:T(8,128)S(1)}, f32[1,4,1,32,64]{4,3,2,1,0:T(8,128)S(1)}, u32[]{:S(2)}, u32[]{:S(2)}) collective-permute-start(f32[1,4,1,32,64]{4,3,2,1,0:T(8,128)S(1)} %get-tuple-element.104), channel_id=1, source_target_pairs={{0,1},{1,2},{2,3},{4,5},{5,6},{6,7},{8,9},{9,10},{10,11},{12,13},{... | collective-permute-start | bytes 98312 | tf_op jit(solution)/shard_map/ppermute | solution.py:23
  57.2 8.4 %collective-permute-start.9 = (f32[1,4,2,32,64]{4,3,2,1,0:T(8,128)S(1)}, f32[1,4,2,32,64]{4,3,2,1,0:T(8,128)S(1)}, u32[]{:S(2)}, u32[]{:S(2)}) collective-permute-start(f32[1,4,2,32,64]{4,3,2,1,0:T(8,128)S(1)} %fusion.207), channel_id=1, source_target_pairs={{0,4},{4,8},{8,12},{12,16},{16,20},{20,24},{24,28},{28,32},{32,36}... | collective-permute-start | bytes 196616 | tf_op jit(solution)/shard_map/ppermute | solution.py:34
  91.7 216.2 %all-gather.9.cloned.1.call-start = ((), (), s32[]{:S(2)}) async-start(), calls=%async_computation.1 | async-start | bytes 1310720 | tf_op jit(solution)/shard_map/all_gather | solution.py:192
  148.6 7.8 %collective-permute-start.13 = (f32[1,4,1,32,64]{4,3,2,1,0:T(8,128)S(1)}, f32[1,4,1,32,64]{4,3,2,1,0:T(8,128)S(1)}, u32[]{:S(2)}, u32[]{:S(2)}) collective-permute-start(f32[1,4,1,32,64]{4,3,2,1,0:T(8,128)S(1)} %get-tuple-element.99), channel_id=1, source_target_pairs={{1,0},{2,1},{3,2},{5,4},{6,5},{7,6},{9,8},{10,9},{11,10},{13,12},{... | collective-permute-start | bytes 98312 | tf_op jit(solution)/shard_map/ppermute | solution.py:26
  149.9 6.5 %collective-permute-start.14 = (f32[1,4,1,32,64]{4,3,2,1,0:T(8,128)S(1)}, f32[1,4,1,32,64]{4,3,2,1,0:T(8,128)S(1)}, u32[]{:S(2)}, u32[]{:S(2)}) collective-permute-start(f32[1,4,1,32,64]{4,3,2,1,0:T(8,128)S(1)} %get-tuple-element.100), channel_id=1, source_target_pairs={{0,1},{1,2},{2,3},{4,5},{5,6},{6,7},{8,9},{9,10},{10,11},{12,13},{... | collective-permute-start | bytes 98312 | tf_op jit(solution)/shard_map/ppermute | solution.py:23
  154.4 8.4 %collective-permute-start.12 = (f32[1,4,2,32,64]{4,3,2,1,0:T(8,128)S(1)}, f32[1,4,2,32,64]{4,3,2,1,0:T(8,128)S(1)}, u32[]{:S(2)}, u32[]{:S(2)}) collective-permute-start(f32[1,4,2,32,64]{4,3,2,1,0:T(8,128)S(1)} %fusion.221), channel_id=1, source_target_pairs={{0,4},{4,8},{8,12},{12,16},{16,20},{20,24},{24,28},{28,32},{32,36}... | collective-permute-start | bytes 196616 | tf_op jit(solution)/shard_map/ppermute | solution.py:34
  163.4 12.6 %collective-permute-start.15 = (f32[1,4,4,64,128]{4,3,2,1,0:T(8,128)S(1)}, f32[1,4,4,64,128]{4,3,2,1,0:T(8,128)S(1)}, u32[]{:S(2)}, u32[]{:S(2)}) collective-permute-start(f32[1,4,4,64,128]{4,3,2,1,0:T(8,128)S(1)} %add.517), channel_id=1, source_target_pairs={{0,4},{4,8},{8,12},{12,16},{16,20},{20,24},{24,28},{28,32},{32,36}... | collective-permute-start | bytes 1572872 | tf_op jit(solution)/shard_map/ppermute | solution.py:34
  165.3 6.9 %collective-permute-start.16 = (f32[1,4,1,64,128]{4,3,2,1,0:T(8,128)S(1)}, f32[1,4,1,64,128]{4,3,2,1,0:T(8,128)S(1)}, u32[]{:S(2)}, u32[]{:S(2)}) collective-permute-start(f32[1,4,1,64,128]{4,3,2,1,0:T(8,128)S(1)} %get-tuple-element.59), channel_id=1, source_target_pairs={{1,0},{2,1},{3,2},{5,4},{6,5},{7,6},{9,8},{10,9},{11,10},{13,12},{... | collective-permute-start | bytes 393224 | tf_op jit(solution)/shard_map/ppermute | solution.py:26
  166.6 7.1 %collective-permute-start.17 = (f32[1,4,1,64,128]{4,3,2,1,0:T(8,128)S(1)}, f32[1,4,1,64,128]{4,3,2,1,0:T(8,128)S(1)}, u32[]{:S(2)}, u32[]{:S(2)}) collective-permute-start(f32[1,4,1,64,128]{4,3,2,1,0:T(8,128)S(1)} %get-tuple-element.60), channel_id=1, source_target_pairs={{0,1},{1,2},{2,3},{4,5},{5,6},{6,7},{8,9},{9,10},{10,11},{12,13},{... | collective-permute-start | bytes 393224 | tf_op jit(solution)/shard_map/ppermute | solution.py:23
  176.5 12.6 %collective-permute-start.18 = (f32[1,4,4,64,128]{4,3,2,1,0:T(8,128)S(1)}, f32[1,4,4,64,128]{4,3,2,1,0:T(8,128)S(1)}, u32[]{:S(2)}, u32[]{:S(2)}) collective-permute-start(f32[1,4,4,64,128]{4,3,2,1,0:T(8,128)S(1)} %fusion.93), channel_id=1, source_target_pairs={{0,4},{4,8},{8,12},{12,16},{16,20},{20,24},{24,28},{28,32},{32,36}... | collective-permute-start | bytes 1572872 | tf_op jit(solution)/shard_map/ppermute | solution.py:34
  178.5 6.9 %collective-permute-start.19 = (f32[1,4,1,64,128]{4,3,2,1,0:T(8,128)S(1)}, f32[1,4,1,64,128]{4,3,2,1,0:T(8,128)S(1)}, u32[]{:S(2)}, u32[]{:S(2)}) collective-permute-start(f32[1,4,1,64,128]{4,3,2,1,0:T(8,128)S(1)} %get-tuple-element.55), channel_id=1, source_target_pairs={{1,0},{2,1},{3,2},{5,4},{6,5},{7,6},{9,8},{10,9},{11,10},{13,12},{... | collective-permute-start | bytes 393224 | tf_op jit(solution)/shard_map/ppermute | solution.py:26
  179.8 7.1 %collective-permute-start.20 = (f32[1,4,1,64,128]{4,3,2,1,0:T(8,128)S(1)}, f32[1,4,1,64,128]{4,3,2,1,0:T(8,128)S(1)}, u32[]{:S(2)}, u32[]{:S(2)}) collective-permute-start(f32[1,4,1,64,128]{4,3,2,1,0:T(8,128)S(1)} %get-tuple-element.56), channel_id=1, source_target_pairs={{0,1},{1,2},{2,3},{4,5},{5,6},{6,7},{8,9},{9,10},{10,11},{12,13},{... | collective-permute-start | bytes 393224 | tf_op jit(solution)/shard_map/ppermute | solution.py:23
  189.7 12.6 %collective-permute-start.21 = (f32[1,4,4,64,128]{4,3,2,1,0:T(8,128)S(1)}, f32[1,4,4,64,128]{4,3,2,1,0:T(8,128)S(1)}, u32[]{:S(2)}, u32[]{:S(2)}) collective-permute-start(f32[1,4,4,64,128]{4,3,2,1,0:T(8,128)S(1)} %fusion.79), channel_id=1, source_target_pairs={{0,4},{4,8},{8,12},{12,16},{16,20},{20,24},{24,28},{28,32},{32,36}... | collective-permute-start | bytes 1572872 | tf_op jit(solution)/shard_map/ppermute | solution.py:34
  191.7 6.9 %collective-permute-start.22 = (f32[1,4,1,64,128]{4,3,2,1,0:T(8,128)S(1)}, f32[1,4,1,64,128]{4,3,2,1,0:T(8,128)S(1)}, u32[]{:S(2)}, u32[]{:S(2)}) collective-permute-start(f32[1,4,1,64,128]{4,3,2,1,0:T(8,128)S(1)} %get-tuple-element.51), channel_id=1, source_target_pairs={{1,0},{2,1},{3,2},{5,4},{6,5},{7,6},{9,8},{10,9},{11,10},{13,12},{... | collective-permute-start | bytes 393224 | tf_op jit(solution)/shard_map/ppermute | solution.py:26
  193.0 7.1 %collective-permute-start.23 = (f32[1,4,1,64,128]{4,3,2,1,0:T(8,128)S(1)}, f32[1,4,1,64,128]{4,3,2,1,0:T(8,128)S(1)}, u32[]{:S(2)}, u32[]{:S(2)}) collective-permute-start(f32[1,4,1,64,128]{4,3,2,1,0:T(8,128)S(1)} %get-tuple-element.52), channel_id=1, source_target_pairs={{0,1},{1,2},{2,3},{4,5},{5,6},{6,7},{8,9},{9,10},{10,11},{12,13},{... | collective-permute-start | bytes 393224 | tf_op jit(solution)/shard_map/ppermute | solution.py:23
  202.9 12.6 %collective-permute-start.24 = (f32[1,4,4,64,128]{4,3,2,1,0:T(8,128)S(1)}, f32[1,4,4,64,128]{4,3,2,1,0:T(8,128)S(1)}, u32[]{:S(2)}, u32[]{:S(2)}) collective-permute-start(f32[1,4,4,64,128]{4,3,2,1,0:T(8,128)S(1)} %fusion.65), channel_id=1, source_target_pairs={{0,4},{4,8},{8,12},{12,16},{16,20},{20,24},{24,28},{28,32},{32,36}... | collective-permute-start | bytes 1572872 | tf_op jit(solution)/shard_map/ppermute | solution.py:34
  204.8 6.9 %collective-permute-start.25 = (f32[1,4,1,64,128]{4,3,2,1,0:T(8,128)S(1)}, f32[1,4,1,64,128]{4,3,2,1,0:T(8,128)S(1)}, u32[]{:S(2)}, u32[]{:S(2)}) collective-permute-start(f32[1,4,1,64,128]{4,3,2,1,0:T(8,128)S(1)} %get-tuple-element.47), channel_id=1, source_target_pairs={{1,0},{2,1},{3,2},{5,4},{6,5},{7,6},{9,8},{10,9},{11,10},{13,12},{... | collective-permute-start | bytes 393224 | tf_op jit(solution)/shard_map/ppermute | solution.py:26
  206.1 7.1 %collective-permute-start.26 = (f32[1,4,1,64,128]{4,3,2,1,0:T(8,128)S(1)}, f32[1,4,1,64,128]{4,3,2,1,0:T(8,128)S(1)}, u32[]{:S(2)}, u32[]{:S(2)}) collective-permute-start(f32[1,4,1,64,128]{4,3,2,1,0:T(8,128)S(1)} %get-tuple-element.48), channel_id=1, source_target_pairs={{0,1},{1,2},{2,3},{4,5},{5,6},{6,7},{8,9},{9,10},{10,11},{12,13},{... | collective-permute-start | bytes 393224 | tf_op jit(solution)/shard_map/ppermute | solution.py:23
  216.0 12.6 %collective-permute-start.27 = (f32[1,4,4,64,128]{4,3,2,1,0:T(8,128)S(1)}, f32[1,4,4,64,128]{4,3,2,1,0:T(8,128)S(1)}, u32[]{:S(2)}, u32[]{:S(2)}) collective-permute-start(f32[1,4,4,64,128]{4,3,2,1,0:T(8,128)S(1)} %fusion.51), channel_id=1, source_target_pairs={{0,4},{4,8},{8,12},{12,16},{16,20},{20,24},{24,28},{28,32},{32,36}... | collective-permute-start | bytes 1572872 | tf_op jit(solution)/shard_map/ppermute | solution.py:34
  218.0 6.9 %collective-permute-start.28 = (f32[1,4,1,64,128]{4,3,2,1,0:T(8,128)S(1)}, f32[1,4,1,64,128]{4,3,2,1,0:T(8,128)S(1)}, u32[]{:S(2)}, u32[]{:S(2)}) collective-permute-start(f32[1,4,1,64,128]{4,3,2,1,0:T(8,128)S(1)} %get-tuple-element.43), channel_id=1, source_target_pairs={{1,0},{2,1},{3,2},{5,4},{6,5},{7,6},{9,8},{10,9},{11,10},{13,12},{... | collective-permute-start | bytes 393224 | tf_op jit(solution)/shard_map/ppermute | solution.py:26
  219.3 7.1 %collective-permute-start.29 = (f32[1,4,1,64,128]{4,3,2,1,0:T(8,128)S(1)}, f32[1,4,1,64,128]{4,3,2,1,0:T(8,128)S(1)}, u32[]{:S(2)}, u32[]{:S(2)}) collective-permute-start(f32[1,4,1,64,128]{4,3,2,1,0:T(8,128)S(1)} %get-tuple-element.44), channel_id=1, source_target_pairs={{0,1},{1,2},{2,3},{4,5},{5,6},{6,7},{8,9},{9,10},{10,11},{12,13},{... | collective-permute-start | bytes 393224 | tf_op jit(solution)/shard_map/ppermute | solution.py:23
  229.6 7.8 %collective-permute-start.31 = (f32[1,4,1,32,64]{4,3,2,1,0:T(8,128)S(1)}, f32[1,4,1,32,64]{4,3,2,1,0:T(8,128)S(1)}, u32[]{:S(2)}, u32[]{:S(2)}) collective-permute-start(f32[1,4,1,32,64]{4,3,2,1,0:T(8,128)S(1)} %get-tuple-element.95), channel_id=1, source_target_pairs={{1,0},{2,1},{3,2},{5,4},{6,5},{7,6},{9,8},{10,9},{11,10},{13,12},{... | collective-permute-start | bytes 98312 | tf_op jit(solution)/shard_map/ppermute | solution.py:26
  230.9 6.5 %collective-permute-start.32 = (f32[1,4,1,32,64]{4,3,2,1,0:T(8,128)S(1)}, f32[1,4,1,32,64]{4,3,2,1,0:T(8,128)S(1)}, u32[]{:S(2)}, u32[]{:S(2)}) collective-permute-start(f32[1,4,1,32,64]{4,3,2,1,0:T(8,128)S(1)} %get-tuple-element.96), channel_id=1, source_target_pairs={{0,1},{1,2},{2,3},{4,5},{5,6},{6,7},{8,9},{9,10},{10,11},{12,13},{... | collective-permute-start | bytes 98312 | tf_op jit(solution)/shard_map/ppermute | solution.py:23
  235.5 8.4 %collective-permute-start.30 = (f32[1,4,2,32,64]{4,3,2,1,0:T(8,128)S(1)}, f32[1,4,2,32,64]{4,3,2,1,0:T(8,128)S(1)}, u32[]{:S(2)}, u32[]{:S(2)}) collective-permute-start(f32[1,4,2,32,64]{4,3,2,1,0:T(8,128)S(1)} %fusion.389), channel_id=1, source_target_pairs={{0,4},{4,8},{8,12},{12,16},{16,20},{20,24},{24,28},{28,32},{32,36}... | collective-permute-start | bytes 196616 | tf_op jit(solution)/shard_map/ppermute | solution.py:34
  244.0 7.8 %collective-permute-start.34 = (f32[1,4,1,32,64]{4,3,2,1,0:T(8,128)S(1)}, f32[1,4,1,32,64]{4,3,2,1,0:T(8,128)S(1)}, u32[]{:S(2)}, u32[]{:S(2)}) collective-permute-start(f32[1,4,1,32,64]{4,3,2,1,0:T(8,128)S(1)} %get-tuple-element.91), channel_id=1, source_target_pairs={{1,0},{2,1},{3,2},{5,4},{6,5},{7,6},{9,8},{10,9},{11,10},{13,12},{... | collective-permute-start | bytes 98312 | tf_op jit(solution)/shard_map/ppermute | solution.py:26
  245.3 6.5 %collective-permute-start.35 = (f32[1,4,1,32,64]{4,3,2,1,0:T(8,128)S(1)}, f32[1,4,1,32,64]{4,3,2,1,0:T(8,128)S(1)}, u32[]{:S(2)}, u32[]{:S(2)}) collective-permute-start(f32[1,4,1,32,64]{4,3,2,1,0:T(8,128)S(1)} %get-tuple-element.92), channel_id=1, source_target_pairs={{0,1},{1,2},{2,3},{4,5},{5,6},{6,7},{8,9},{9,10},{10,11},{12,13},{... | collective-permute-start | bytes 98312 | tf_op jit(solution)/shard_map/ppermute | solution.py:23
  249.9 8.4 %collective-permute-start.33 = (f32[1,4,2,32,64]{4,3,2,1,0:T(8,128)S(1)}, f32[1,4,2,32,64]{4,3,2,1,0:T(8,128)S(1)}, u32[]{:S(2)}, u32[]{:S(2)}) collective-permute-start(f32[1,4,2,32,64]{4,3,2,1,0:T(8,128)S(1)} %fusion.166), channel_id=1, source_target_pairs={{0,4},{4,8},{8,12},{12,16},{16,20},{20,24},{24,28},{28,32},{32,36}... | collective-permute-start | bytes 196616 | tf_op jit(solution)/shard_map/ppermute | solution.py:34
  331.7 7.8 %collective-permute-start.37 = (f32[1,4,1,32,64]{4,3,2,1,0:T(8,128)S(1)}, f32[1,4,1,32,64]{4,3,2,1,0:T(8,128)S(1)}, u32[]{:S(2)}, u32[]{:S(2)}) collective-permute-start(f32[1,4,1,32,64]{4,3,2,1,0:T(8,128)S(1)} %get-tuple-element.87), channel_id=1, source_target_pairs={{1,0},{2,1},{3,2},{5,4},{6,5},{7,6},{9,8},{10,9},{11,10},{13,12},{... | collective-permute-start | bytes 98312 | tf_op jit(solution)/shard_map/ppermute | solution.py:26
  333.0 6.5 %collective-permute-start.38 = (f32[1,4,1,32,64]{4,3,2,1,0:T(8,128)S(1)}, f32[1,4,1,32,64]{4,3,2,1,0:T(8,128)S(1)}, u32[]{:S(2)}, u32[]{:S(2)}) collective-permute-start(f32[1,4,1,32,64]{4,3,2,1,0:T(8,128)S(1)} %get-tuple-element.88), channel_id=1, source_target_pairs={{0,1},{1,2},{2,3},{4,5},{5,6},{6,7},{8,9},{9,10},{10,11},{12,13},{... | collective-permute-start | bytes 98312 | tf_op jit(solution)/shard_map/ppermute | solution.py:23
  337.6 8.4 %collective-permute-start.36 = (f32[1,4,2,32,64]{4,3,2,1,0:T(8,128)S(1)}, f32[1,4,2,32,64]{4,3,2,1,0:T(8,128)S(1)}, u32[]{:S(2)}, u32[]{:S(2)}) collective-permute-start(f32[1,4,2,32,64]{4,3,2,1,0:T(8,128)S(1)} %fusion.233), channel_id=1, source_target_pairs={{0,4},{4,8},{8,12},{12,16},{16,20},{20,24},{24,28},{28,32},{32,36}... | collective-permute-start | bytes 196616 | tf_op jit(solution)/shard_map/ppermute | solution.py:34
  346.5 12.6 %collective-permute-start.39 = (f32[1,4,4,64,128]{4,3,2,1,0:T(8,128)S(1)}, f32[1,4,4,64,128]{4,3,2,1,0:T(8,128)S(1)}, u32[]{:S(2)}, u32[]{:S(2)}) collective-permute-start(f32[1,4,4,64,128]{4,3,2,1,0:T(8,128)S(1)} %add.567), channel_id=1, source_target_pairs={{0,4},{4,8},{8,12},{12,16},{16,20},{20,24},{24,28},{28,32},{32,36}... | collective-permute-start | bytes 1572872 | tf_op jit(solution)/shard_map/ppermute | solution.py:34
  348.5 6.9 %collective-permute-start.40 = (f32[1,4,1,64,128]{4,3,2,1,0:T(8,128)S(1)}, f32[1,4,1,64,128]{4,3,2,1,0:T(8,128)S(1)}, u32[]{:S(2)}, u32[]{:S(2)}) collective-permute-start(f32[1,4,1,64,128]{4,3,2,1,0:T(8,128)S(1)} %get-tuple-element.39), channel_id=1, source_target_pairs={{1,0},{2,1},{3,2},{5,4},{6,5},{7,6},{9,8},{10,9},{11,10},{13,12},{... | collective-permute-start | bytes 393224 | tf_op jit(solution)/shard_map/ppermute | solution.py:26
  349.8 7.1 %collective-permute-start.41 = (f32[1,4,1,64,128]{4,3,2,1,0:T(8,128)S(1)}, f32[1,4,1,64,128]{4,3,2,1,0:T(8,128)S(1)}, u32[]{:S(2)}, u32[]{:S(2)}) collective-permute-start(f32[1,4,1,64,128]{4,3,2,1,0:T(8,128)S(1)} %get-tuple-element.40), channel_id=1, source_target_pairs={{0,1},{1,2},{2,3},{4,5},{5,6},{6,7},{8,9},{9,10},{10,11},{12,13},{... | collective-permute-start | bytes 393224 | tf_op jit(solution)/shard_map/ppermute | solution.py:23
  359.7 12.6 %collective-permute-start.42 = (f32[1,4,4,64,128]{4,3,2,1,0:T(8,128)S(1)}, f32[1,4,4,64,128]{4,3,2,1,0:T(8,128)S(1)}, u32[]{:S(2)}, u32[]{:S(2)}) collective-permute-start(f32[1,4,4,64,128]{4,3,2,1,0:T(8,128)S(1)} %fusion.25), channel_id=1, source_target_pairs={{0,4},{4,8},{8,12},{12,16},{16,20},{20,24},{24,28},{28,32},{32,36}... | collective-permute-start | bytes 1572872 | tf_op jit(solution)/shard_map/ppermute | solution.py:34
  361.6 6.9 %collective-permute-start.43 = (f32[1,4,1,64,128]{4,3,2,1,0:T(8,128)S(1)}, f32[1,4,1,64,128]{4,3,2,1,0:T(8,128)S(1)}, u32[]{:S(2)}, u32[]{:S(2)}) collective-permute-start(f32[1,4,1,64,128]{4,3,2,1,0:T(8,128)S(1)} %get-tuple-element.35), channel_id=1, source_target_pairs={{1,0},{2,1},{3,2},{5,4},{6,5},{7,6},{9,8},{10,9},{11,10},{13,12},{... | collective-permute-start | bytes 393224 | tf_op jit(solution)/shard_map/ppermute | solution.py:26
  362.9 7.1 %collective-permute-start.44 = (f32[1,4,1,64,128]{4,3,2,1,0:T(8,128)S(1)}, f32[1,4,1,64,128]{4,3,2,1,0:T(8,128)S(1)}, u32[]{:S(2)}, u32[]{:S(2)}) collective-permute-start(f32[1,4,1,64,128]{4,3,2,1,0:T(8,128)S(1)} %get-tuple-element.36), channel_id=1, source_target_pairs={{0,1},{1,2},{2,3},{4,5},{5,6},{6,7},{8,9},{9,10},{10,11},{12,13},{... | collective-permute-start | bytes 393224 | tf_op jit(solution)/shard_map/ppermute | solution.py:23
Sparse Core Ops, SparseCore 0:
  91.8 25.5 all-gather.6
  284.4 23.4 all-gather.8

commit v13 on v9

--- a/solution.py
+++ b/solution.py
@@ -187,8 +187,25 @@
     return (whole_source, whole_metric)
 
 
+def gather_doubling(flat, axis):
+    size = lax.axis_size(axis)
+    position = lax.axis_index(axis)
+    gathered = flat
+    step = 1
+    while step < size:
+        other = lax.ppermute(gathered, axis, [(i, i ^ step) for i in range(size)])
+        lower = (position & step) == 0
+        gathered = jnp.where(
+            lower,
+            jnp.concatenate([gathered, other], axis=0),
+            jnp.concatenate([other, gathered], axis=0),
+        )
+        step *= 2
+    return gathered
+
+
 def gather_all(flat):
-    across = lax.all_gather(flat, "tm", axis=0, tiled=True)
+    across = gather_doubling(flat, "tm")
     whole = lax.all_gather(across, "space", axis=1, tiled=True)
     return whole.reshape(-1, flat.shape[1])
 

time: 368 us -> 364 us (0.989)
  blocking collectives: 46.5 us -> 0 us
  waiting for transfers between devices: 128 us -> 164 us
  starting transfers between devices: 117 us -> 123 us
    all_gather x2 -> x0, blocking collectives: 46.5 us -> none  [gather_all(): across = lax.all_gather(flat, 'tm', axis=0, tiled=True)]
    ppermute x0 -> x10, waiting for transfers between devices: none -> 37 us  [gather_doubling(): other = lax.ppermute(gathered, axis, [(i, i ^ step) for i in range(size)])]
    ppermute x0 -> x10, starting transfers between devices: none -> 6.55 us  [gather_doubling(): other = lax.ppermute(gathered, axis, [(i, i ^ step) for i in range(size)])]
  transfers between devices with their start and end apart: 47 -> 57, of which waited for: 35 -> 45; matrix products, arithmetic and copies ran while one was open for 1% -> 1% of each run, Pallas kernels for 0% -> 0%
where the time goes in v13:
time: 364 us; the launch traced here: 363 us
  waiting for transfers between devices  164 us (45%)
  starting transfers between devices  123 us (34%)
  Pallas kernels  28.5 us (8%)
  local copies, waits for them, and re-layouts  15.8 us (4%)
  between operations  14.7 us (4%)
  other arithmetic  14.3 us (4%)
    ppermute x15, starting transfers between devices, with_halo(): lax.ppermute(lax.slice_in_dim(block, block.shape[dim] - width, None, axis...  68.5 us
    ppermute x15, waiting for transfers between devices, from_behind(): return lax.ppermute(array, axis, pairs)  54.8 us
    all_gather x2, waiting for transfers between devices, gather_all(): whole = lax.all_gather(across, 'space', axis=1, tiled=True)  47.9 us
    ppermute x10, waiting for transfers between devices, gather_doubling(): other = lax.ppermute(gathered, axis, [(i, i ^ step) for i in range(size)])  37 us
    ppermute x15, starting transfers between devices, from_behind(): return lax.ppermute(array, axis, pairs)  28.9 us
    pallas_call x2, Pallas kernels, coarse_solve(): pl.pallas_call(kernel, out_shape=jax.ShapeDtypeStruct(flat_source.shape,...  28.5 us
    ppermute x15, starting transfers between devices, with_halo(): lax.ppermute(lax.slice_in_dim(block, 0, width, axis=dim), axis, backward)  19.4 us
    ppermute x15, waiting for transfers between devices, with_halo(): lax.ppermute(lax.slice_in_dim(block, block.shape[dim] - width, None, axis...  13.7 us
  transfers between devices with their start and end apart: 57, of which 45 were waited for; matrix products, arithmetic and copies ran while one was open for 1% of the time, Pallas kernels for 0%

profile of v13, /device:TPU:2, one launch (start us, length us, event | category | flops | bytes accessed | tf_op | source)
XLA Modules:
  0.0 362.7 jit_solution(17691812267971976091)
XLA Ops:
  9.8 2.1 collective-permute-start
  13.2 4.6 %collective-permute-start.2 = (f32[1,4,1,64,128]{4,3,2,1,0:T(8,128)S(1)}, f32[1,4,1,64,128]{4,3,2,1,0:T(8,128)S(1)}, u32[]{:S(2)}, u32[]{:S(2)}) collective-permute-start(f32[1,4,1,64,128]{4,3,2,1,0:T(8,128)S(1)} %get-tuple-element.68), channel_id=1, source_target_pairs={{0,1},{1,2},{2,3},{4,5},{5,6},{6,7},{8,9},{9,10},{10,11},{12,13},{... | collective-permute-start | bytes 393224 | tf_op jit(solution)/shard_map/ppermute | solution.py:23
  19.2 1.7 collective-permute-done.2
  23.1 1.9 collective-permute-start.3
  26.3 4.6 %collective-permute-start.5 = (f32[1,4,1,64,128]{4,3,2,1,0:T(8,128)S(1)}, f32[1,4,1,64,128]{4,3,2,1,0:T(8,128)S(1)}, u32[]{:S(2)}, u32[]{:S(2)}) collective-permute-start(f32[1,4,1,64,128]{4,3,2,1,0:T(8,128)S(1)} %get-tuple-element.64), channel_id=1, source_target_pairs={{0,1},{1,2},{2,3},{4,5},{5,6},{6,7},{8,9},{9,10},{10,11},{12,13},{... | collective-permute-start | bytes 393224 | tf_op jit(solution)/shard_map/ppermute | solution.py:23
  30.9 2.2 collective-permute-done.4
  38.0 4.5 %collective-permute-start.8 = (f32[1,4,1,32,64]{4,3,2,1,0:T(8,128)S(1)}, f32[1,4,1,32,64]{4,3,2,1,0:T(8,128)S(1)}, u32[]{:S(2)}, u32[]{:S(2)}) collective-permute-start(f32[1,4,1,32,64]{4,3,2,1,0:T(8,128)S(1)} %get-tuple-element.108), channel_id=1, source_target_pairs={{0,1},{1,2},{2,3},{4,5},{5,6},{6,7},{8,9},{9,10},{10,11},{12,13},{... | collective-permute-start | bytes 98312 | tf_op jit(solution)/shard_map/ppermute | solution.py:23
  42.6 1.9 collective-permute-start.6
  44.6 6.3 %collective-permute-done.6 = f32[1,4,2,32,64]{4,3,2,1,0:T(8,128)S(1)} collective-permute-done((f32[1,4,2,32,64]{4,3,2,1,0:T(8,128)S(1)}, f32[1,4,2,32,64]{4,3,2,1,0:T(8,128)S(1)}, u32[]{:S(2)}, u32[]{:S(2)}) %collective-permute-start.6) | collective-permute-done | bytes 65568 | tf_op jit(solution)/shard_map/ppermute | solution.py:34
  52.4 4.5 %collective-permute-start.11 = (f32[1,4,1,32,64]{4,3,2,1,0:T(8,128)S(1)}, f32[1,4,1,32,64]{4,3,2,1,0:T(8,128)S(1)}, u32[]{:S(2)}, u32[]{:S(2)}) collective-permute-start(f32[1,4,1,32,64]{4,3,2,1,0:T(8,128)S(1)} %get-tuple-element.104), channel_id=1, source_target_pairs={{0,1},{1,2},{2,3},{4,5},{5,6},{6,7},{8,9},{9,10},{10,11},{12,13},{... | collective-permute-start | bytes 98312 | tf_op jit(solution)/shard_map/ppermute | solution.py:23
  57.2 1.9 collective-permute-start.9
  59.3 6.3 %collective-permute-done.9 = f32[1,4,2,32,64]{4,3,2,1,0:T(8,128)S(1)} collective-permute-done((f32[1,4,2,32,64]{4,3,2,1,0:T(8,128)S(1)}, f32[1,4,2,32,64]{4,3,2,1,0:T(8,128)S(1)}, u32[]{:S(2)}, u32[]{:S(2)}) %collective-permute-start.9) | collective-permute-done | bytes 65568 | tf_op jit(solution)/shard_map/ppermute | solution.py:34
  67.7 3.8 %collective-permute-done.13 = f32[2,2560]{1,0:T(2,128)S(1)} collective-permute-done((f32[2,2560]{1,0:T(2,128)S(1)}, f32[2,2560]{1,0:T(2,128)S(1)}, u32[]{:S(2)}, u32[]{:S(2)}) %collective-permute-start.13) | collective-permute-done | bytes 20512 | tf_op jit(solution)/shard_map/ppermute | solution.py:196
  71.6 5.5 %collective-permute-done.14 = f32[4,2560]{1,0:T(4,128)S(1)} collective-permute-done((f32[4,2560]{1,0:T(4,128)S(1)}, f32[4,2560]{1,0:T(4,128)S(1)}, u32[]{:S(2)}, u32[]{:S(2)}) %collective-permute-start.14) | collective-permute-done | bytes 40992 | tf_op jit(solution)/shard_map/ppermute | solution.py:196
  77.2 4.4 %collective-permute-done.15 = f32[8,2560]{1,0:T(8,128)S(1)} collective-permute-done((f32[8,2560]{1,0:T(8,128)S(1)}, f32[8,2560]{1,0:T(8,128)S(1)}, u32[]{:S(2)}, u32[]{:S(2)}) %collective-permute-start.15) | collective-permute-done | bytes 81952 | tf_op jit(solution)/shard_map/ppermute | solution.py:196
  81.6 3.1 collective-permute-start.16
  84.7 3.8 %collective-permute-done.16 = f32[16,2560]{1,0:T(8,128)S(1)} collective-permute-done((f32[16,2560]{1,0:T(8,128)S(1)}, f32[16,2560]{1,0:T(8,128)S(1)}, u32[]{:S(2)}, u32[]{:S(2)}) %collective-permute-start.16) | collective-permute-done | bytes 163872 | tf_op jit(solution)/shard_map/ppermute | solution.py:196
  89.4 25.1 %all-gather.3.cloned.1.call-done = f32[32,10240]{1,0:T(8,128)} async-done(((f32[32,2560]{1,0:T(8,128)}), f32[32,10240]{1,0:T(8,128)}) %all-gather.3.cloned.1.call-update) | async-done | bytes 1310736 | tf_op jit(solution)/shard_map/all_gather | solution.py:209
  114.4 1.7 reshape.859
  117.2 2.5 reshape_transpose_reshape.7.src_ref
  121.5 14.2 %shard_map.37 = f32[32,16,512]{2,1,0:T(8,128)} custom-call(f32[32,16,512]{2,1,0:T(8,128)} %reshape_transpose_reshape.7.src_ref, f32[32,16,512]{2,1,0:T(8,128)} %reshape.860.met_ref), custom_call_target="tpu_custom_call" | custom-call | tf_op jit(solution)/shard_map/pallas_call | solution.py:161
  139.8 4.5 %collective-permute-start.19 = (f32[1,4,1,32,64]{4,3,2,1,0:T(8,128)S(1)}, f32[1,4,1,32,64]{4,3,2,1,0:T(8,128)S(1)}, u32[]{:S(2)}, u32[]{:S(2)}) collective-permute-start(f32[1,4,1,32,64]{4,3,2,1,0:T(8,128)S(1)} %get-tuple-element.100), channel_id=1, source_target_pairs={{0,1},{1,2},{2,3},{4,5},{5,6},{6,7},{8,9},{9,10},{10,11},{12,13},{... | collective-permute-start | bytes 98312 | tf_op jit(solution)/shard_map/ppermute | solution.py:23
  144.4 1.9 collective-permute-start.17
  146.4 6.3 %collective-permute-done.17 = f32[1,4,2,32,64]{4,3,2,1,0:T(8,128)S(1)} collective-permute-done((f32[1,4,2,32,64]{4,3,2,1,0:T(8,128)S(1)}, f32[1,4,2,32,64]{4,3,2,1,0:T(8,128)S(1)}, u32[]{:S(2)}, u32[]{:S(2)}) %collective-permute-start.17) | collective-permute-done | bytes 65568 | tf_op jit(solution)/shard_map/ppermute | solution.py:34
  153.4 1.9 collective-permute-start.20
  156.6 4.6 %collective-permute-start.22 = (f32[1,4,1,64,128]{4,3,2,1,0:T(8,128)S(1)}, f32[1,4,1,64,128]{4,3,2,1,0:T(8,128)S(1)}, u32[]{:S(2)}, u32[]{:S(2)}) collective-permute-start(f32[1,4,1,64,128]{4,3,2,1,0:T(8,128)S(1)} %get-tuple-element.60), channel_id=1, source_target_pairs={{0,1},{1,2},{2,3},{4,5},{5,6},{6,7},{8,9},{9,10},{10,11},{12,13},{... | collective-permute-start | bytes 393224 | tf_op jit(solution)/shard_map/ppermute | solution.py:23
  162.2 1.5 collective-permute-done.22
  163.9 2.1 collective-permute-done.20
  166.5 1.9 collective-permute-start.23
  169.8 4.6 %collective-permute-start.25 = (f32[1,4,1,64,128]{4,3,2,1,0:T(8,128)S(1)}, f32[1,4,1,64,128]{4,3,2,1,0:T(8,128)S(1)}, u32[]{:S(2)}, u32[]{:S(2)}) collective-permute-start(f32[1,4,1,64,128]{4,3,2,1,0:T(8,128)S(1)} %get-tuple-element.56), channel_id=1, source_target_pairs={{0,1},{1,2},{2,3},{4,5},{5,6},{6,7},{8,9},{9,10},{10,11},{12,13},{... | collective-permute-start | bytes 393224 | tf_op jit(solution)/shard_map/ppermute | solution.py:23
  177.0 2.1 collective-permute-done.23
  179.7 1.9 collective-permute-start.26
  182.9 4.7 %collective-permute-start.28 = (f32[1,4,1,64,128]{4,3,2,1,0:T(8,128)S(1)}, f32[1,4,1,64,128]{4,3,2,1,0:T(8,128)S(1)}, u32[]{:S(2)}, u32[]{:S(2)}) collective-permute-start(f32[1,4,1,64,128]{4,3,2,1,0:T(8,128)S(1)} %get-tuple-element.52), channel_id=1, source_target_pairs={{0,1},{1,2},{2,3},{4,5},{5,6},{6,7},{8,9},{9,10},{10,11},{12,13},{... | collective-permute-start | bytes 393224 | tf_op jit(solution)/shard_map/ppermute | solution.py:23
  188.5 1.5 collective-permute-done.28
  190.2 2.1 collective-permute-done.26
  192.8 1.9 collective-permute-start.29
  196.1 4.6 %collective-permute-start.31 = (f32[1,4,1,64,128]{4,3,2,1,0:T(8,128)S(1)}, f32[1,4,1,64,128]{4,3,2,1,0:T(8,128)S(1)}, u32[]{:S(2)}, u32[]{:S(2)}) collective-permute-start(f32[1,4,1,64,128]{4,3,2,1,0:T(8,128)S(1)} %get-tuple-element.48), channel_id=1, source_target_pairs={{0,1},{1,2},{2,3},{4,5},{5,6},{6,7},{8,9},{9,10},{10,11},{12,13},{... | collective-permute-start | bytes 393224 | tf_op jit(solution)/shard_map/ppermute | solution.py:23
  203.3 2.1 collective-permute-done.29
  206.0 1.9 collective-permute-start.32
  209.2 4.6 %collective-permute-start.34 = (f32[1,4,1,64,128]{4,3,2,1,0:T(8,128)S(1)}, f32[1,4,1,64,128]{4,3,2,1,0:T(8,128)S(1)}, u32[]{:S(2)}, u32[]{:S(2)}) collective-permute-start(f32[1,4,1,64,128]{4,3,2,1,0:T(8,128)S(1)} %get-tuple-element.44), channel_id=1, source_target_pairs={{0,1},{1,2},{2,3},{4,5},{5,6},{6,7},{8,9},{9,10},{10,11},{12,13},{... | collective-permute-start | bytes 393224 | tf_op jit(solution)/shard_map/ppermute | solution.py:23
  216.5 2.1 collective-permute-done.32
  220.9 4.5 %collective-permute-start.37 = (f32[1,4,1,32,64]{4,3,2,1,0:T(8,128)S(1)}, f32[1,4,1,32,64]{4,3,2,1,0:T(8,128)S(1)}, u32[]{:S(2)}, u32[]{:S(2)}) collective-permute-start(f32[1,4,1,32,64]{4,3,2,1,0:T(8,128)S(1)} %get-tuple-element.96), channel_id=1, source_target_pairs={{0,1},{1,2},{2,3},{4,5},{5,6},{6,7},{8,9},{9,10},{10,11},{12,13},{... | collective-permute-start | bytes 98312 | tf_op jit(solution)/shard_map/ppermute | solution.py:23
  225.5 1.9 collective-permute-start.35
  227.5 6.3 %collective-permute-done.35 = f32[1,4,2,32,64]{4,3,2,1,0:T(8,128)S(1)} collective-permute-done((f32[1,4,2,32,64]{4,3,2,1,0:T(8,128)S(1)}, f32[1,4,2,32,64]{4,3,2,1,0:T(8,128)S(1)}, u32[]{:S(2)}, u32[]{:S(2)}) %collective-permute-start.35) | collective-permute-done | bytes 65568 | tf_op jit(solution)/shard_map/ppermute | solution.py:34
  235.3 4.5 %collective-permute-start.40 = (f32[1,4,1,32,64]{4,3,2,1,0:T(8,128)S(1)}, f32[1,4,1,32,64]{4,3,2,1,0:T(8,128)S(1)}, u32[]{:S(2)}, u32[]{:S(2)}) collective-permute-start(f32[1,4,1,32,64]{4,3,2,1,0:T(8,128)S(1)} %get-tuple-element.92), channel_id=1, source_target_pairs={{0,1},{1,2},{2,3},{4,5},{5,6},{6,7},{8,9},{9,10},{10,11},{12,13},{... | collective-permute-start | bytes 98312 | tf_op jit(solution)/shard_map/ppermute | solution.py:23
  239.9 1.9 collective-permute-start.38
  241.9 6.3 %collective-permute-done.38 = f32[1,4,2,32,64]{4,3,2,1,0:T(8,128)S(1)} collective-permute-done((f32[1,4,2,32,64]{4,3,2,1,0:T(8,128)S(1)}, f32[1,4,2,32,64]{4,3,2,1,0:T(8,128)S(1)}, u32[]{:S(2)}, u32[]{:S(2)}) %collective-permute-start.38) | collective-permute-done | bytes 65568 | tf_op jit(solution)/shard_map/ppermute | solution.py:34
  250.3 3.7 %collective-permute-done.42 = f32[2,2048]{1,0:T(2,128)S(1)} collective-permute-done((f32[2,2048]{1,0:T(2,128)S(1)}, f32[2,2048]{1,0:T(2,128)S(1)}, u32[]{:S(2)}, u32[]{:S(2)}) %collective-permute-start.42) | collective-permute-done | bytes 16416 | tf_op jit(solution)/shard_map/ppermute | solution.py:196
  254.1 5.4 %collective-permute-done.43 = f32[4,2048]{1,0:T(4,128)S(1)} collective-permute-done((f32[4,2048]{1,0:T(4,128)S(1)}, f32[4,2048]{1,0:T(4,128)S(1)}, u32[]{:S(2)}, u32[]{:S(2)}) %collective-permute-start.43) | collective-permute-done | bytes 32800 | tf_op jit(solution)/shard_map/ppermute | solution.py:196
  259.7 4.3 %collective-permute-done.44 = f32[8,2048]{1,0:T(8,128)S(1)} collective-permute-done((f32[8,2048]{1,0:T(8,128)S(1)}, f32[8,2048]{1,0:T(8,128)S(1)}, u32[]{:S(2)}, u32[]{:S(2)}) %collective-permute-start.44) | collective-permute-done | bytes 65568 | tf_op jit(solution)/shard_map/ppermute | solution.py:196
  263.9 2.8 collective-permute-start.45
  266.7 3.8 %collective-permute-done.45 = f32[16,2048]{1,0:T(8,128)S(1)} collective-permute-done((f32[16,2048]{1,0:T(8,128)S(1)}, f32[16,2048]{1,0:T(8,128)S(1)}, u32[]{:S(2)}, u32[]{:S(2)}) %collective-permute-start.45) | collective-permute-done | bytes 131104 | tf_op jit(solution)/shard_map/ppermute | solution.py:196
  271.2 22.8 %all-gather.5.cloned.1.call-done = f32[32,8192]{1,0:T(8,128)} async-done(((f32[32,2048]{1,0:T(8,128)}), f32[32,8192]{1,0:T(8,128)}) %all-gather.5.cloned.1.call-update) | async-done | bytes 1048592 | tf_op jit(solution)/shard_map/all_gather | solution.py:209
  294.0 2.8 copy.14
  296.9 14.2 %shard_map.38 = f32[32,16,512]{2,1,0:T(8,128)} custom-call(f32[32,16,512]{2,1,0:T(8,128)} %bitcast.106, f32[32,16,512]{2,1,0:T(8,128)} %reshape.860.met_ref), custom_call_target="tpu_custom_call" | custom-call | tf_op jit(solution)/shard_map/pallas_call | solution.py:161
  315.2 4.5 %collective-permute-start.48 = (f32[1,4,1,32,64]{4,3,2,1,0:T(8,128)S(1)}, f32[1,4,1,32,64]{4,3,2,1,0:T(8,128)S(1)}, u32[]{:S(2)}, u32[]{:S(2)}) collective-permute-start(f32[1,4,1,32,64]{4,3,2,1,0:T(8,128)S(1)} %get-tuple-element.88), channel_id=1, source_target_pairs={{0,1},{1,2},{2,3},{4,5},{5,6},{6,7},{8,9},{9,10},{10,11},{12,13},{... | collective-permute-start | bytes 98312 | tf_op jit(solution)/shard_map/ppermute | solution.py:23
  319.8 1.9 collective-permute-start.46
  321.8 6.3 %collective-permute-done.46 = f32[1,4,2,32,64]{4,3,2,1,0:T(8,128)S(1)} collective-permute-done((f32[1,4,2,32,64]{4,3,2,1,0:T(8,128)S(1)}, f32[1,4,2,32,64]{4,3,2,1,0:T(8,128)S(1)}, u32[]{:S(2)}, u32[]{:S(2)}) %collective-permute-start.46) | collective-permute-done | bytes 65568 | tf_op jit(solution)/shard_map/ppermute | solution.py:34
  328.7 1.9 collective-permute-start.49
  332.0 4.6 %collective-permute-start.51 = (f32[1,4,1,64,128]{4,3,2,1,0:T(8,128)S(1)}, f32[1,4,1,64,128]{4,3,2,1,0:T(8,128)S(1)}, u32[]{:S(2)}, u32[]{:S(2)}) collective-permute-start(f32[1,4,1,64,128]{4,3,2,1,0:T(8,128)S(1)} %get-tuple-element.40), channel_id=1, source_target_pairs={{0,1},{1,2},{2,3},{4,5},{5,6},{6,7},{8,9},{9,10},{10,11},{12,13},{... | collective-permute-start | bytes 393224 | tf_op jit(solution)/shard_map/ppermute | solution.py:23
  339.2 2.1 collective-permute-done.49
  341.9 1.9 collective-permute-start.52
  345.1 4.6 %collective-permute-start.54 = (f32[1,4,1,64,128]{4,3,2,1,0:T(8,128)S(1)}, f32[1,4,1,64,128]{4,3,2,1,0:T(8,128)S(1)}, u32[]{:S(2)}, u32[]{:S(2)}) collective-permute-start(f32[1,4,1,64,128]{4,3,2,1,0:T(8,128)S(1)} %get-tuple-element.36), channel_id=1, source_target_pairs={{0,1},{1,2},{2,3},{4,5},{5,6},{6,7},{8,9},{9,10},{10,11},{12,13},{... | collective-permute-start | bytes 393224 | tf_op jit(solution)/shard_map/ppermute | solution.py:23
  352.4 2.1 collective-permute-done.52
  (191 shorter events, 67.1 us)
Async XLA Ops:
  6.5 107.9 %all-gather.3.cloned.1.call-start = ((), (), s32[]{:S(2)}) async-start(), calls=%async_computation | async-start | bytes 1638400 | tf_op jit(solution)/shard_map/all_gather | solution.py:209
  7.5 10.2 %copy-start.1 = (f32[1,4,64,128]{3,2,1,0:T(8,128)S(1)}, f32[1,4,64,128]{3,2,1,0:T(8,128)}, u32[]{:S(2)}) copy-start(f32[1,4,64,128]{3,2,1,0:T(8,128)} %param.4) | copy-start | bytes 393220
  9.8 12.8 %copy-start = (f32[1,4,4,64,128]{4,3,2,1,0:T(8,128)S(1)}, f32[1,4,4,64,128]{4,3,2,1,0:T(8,128)}, u32[]{:S(2)}) copy-start(f32[1,4,4,64,128]{4,3,2,1,0:T(8,128)} %param.3) | copy-start | bytes 1572868
  9.8 12.7 %collective-permute-start = (f32[1,4,4,64,128]{4,3,2,1,0:T(8,128)S(1)}, f32[1,4,4,64,128]{4,3,2,1,0:T(8,128)S(1)}, u32[]{:S(2)}, u32[]{:S(2)}) collective-permute-start(f32[1,4,4,64,128]{4,3,2,1,0:T(8,128)S(1)} %get-tuple-element.9), channel_id=1, source_target_pairs={{0,4},{4,8},{8,12},{12,16},{16,20},{20,24},{24,28},{28,32},{32,36}... | collective-permute-start | bytes 1572872 | tf_op jit(solution)/shard_map/ppermute | solution.py:34
  11.9 7.4 %collective-permute-start.1 = (f32[1,4,1,64,128]{4,3,2,1,0:T(8,128)S(1)}, f32[1,4,1,64,128]{4,3,2,1,0:T(8,128)S(1)}, u32[]{:S(2)}, u32[]{:S(2)}) collective-permute-start(f32[1,4,1,64,128]{4,3,2,1,0:T(8,128)S(1)} %get-tuple-element.67), channel_id=1, source_target_pairs={{1,0},{2,1},{3,2},{5,4},{6,5},{7,6},{9,8},{10,9},{11,10},{13,12},{... | collective-permute-start | bytes 393224 | tf_op jit(solution)/shard_map/ppermute | solution.py:26
  13.2 7.8 %collective-permute-start.2 = (f32[1,4,1,64,128]{4,3,2,1,0:T(8,128)S(1)}, f32[1,4,1,64,128]{4,3,2,1,0:T(8,128)S(1)}, u32[]{:S(2)}, u32[]{:S(2)}) collective-permute-start(f32[1,4,1,64,128]{4,3,2,1,0:T(8,128)S(1)} %get-tuple-element.68), channel_id=1, source_target_pairs={{0,1},{1,2},{2,3},{4,5},{5,6},{6,7},{8,9},{9,10},{10,11},{12,13},{... | collective-permute-start | bytes 393224 | tf_op jit(solution)/shard_map/ppermute | solution.py:23
  23.1 12.6 %collective-permute-start.3 = (f32[1,4,4,64,128]{4,3,2,1,0:T(8,128)S(1)}, f32[1,4,4,64,128]{4,3,2,1,0:T(8,128)S(1)}, u32[]{:S(2)}, u32[]{:S(2)}) collective-permute-start(f32[1,4,4,64,128]{4,3,2,1,0:T(8,128)S(1)} %fusion.119), channel_id=1, source_target_pairs={{0,4},{4,8},{8,12},{12,16},{16,20},{20,24},{24,28},{28,32},{32,36}... | collective-permute-start | bytes 1572872 | tf_op jit(solution)/shard_map/ppermute | solution.py:34
  25.0 8.1 %collective-permute-start.4 = (f32[1,4,1,64,128]{4,3,2,1,0:T(8,128)S(1)}, f32[1,4,1,64,128]{4,3,2,1,0:T(8,128)S(1)}, u32[]{:S(2)}, u32[]{:S(2)}) collective-permute-start(f32[1,4,1,64,128]{4,3,2,1,0:T(8,128)S(1)} %get-tuple-element.63), channel_id=1, source_target_pairs={{1,0},{2,1},{3,2},{5,4},{6,5},{7,6},{9,8},{10,9},{11,10},{13,12},{... | collective-permute-start | bytes 393224 | tf_op jit(solution)/shard_map/ppermute | solution.py:26
  26.3 8.3 %collective-permute-start.5 = (f32[1,4,1,64,128]{4,3,2,1,0:T(8,128)S(1)}, f32[1,4,1,64,128]{4,3,2,1,0:T(8,128)S(1)}, u32[]{:S(2)}, u32[]{:S(2)}) collective-permute-start(f32[1,4,1,64,128]{4,3,2,1,0:T(8,128)S(1)} %get-tuple-element.64), channel_id=1, source_target_pairs={{0,1},{1,2},{2,3},{4,5},{5,6},{6,7},{8,9},{9,10},{10,11},{12,13},{... | collective-permute-start | bytes 393224 | tf_op jit(solution)/shard_map/ppermute | solution.py:23
  36.7 7.8 %collective-permute-start.7 = (f32[1,4,1,32,64]{4,3,2,1,0:T(8,128)S(1)}, f32[1,4,1,32,64]{4,3,2,1,0:T(8,128)S(1)}, u32[]{:S(2)}, u32[]{:S(2)}) collective-permute-start(f32[1,4,1,32,64]{4,3,2,1,0:T(8,128)S(1)} %get-tuple-element.107), channel_id=1, source_target_pairs={{1,0},{2,1},{3,2},{5,4},{6,5},{7,6},{9,8},{10,9},{11,10},{13,12},{... | collective-permute-start | bytes 98312 | tf_op jit(solution)/shard_map/ppermute | solution.py:26
  38.0 6.5 %collective-permute-start.8 = (f32[1,4,1,32,64]{4,3,2,1,0:T(8,128)S(1)}, f32[1,4,1,32,64]{4,3,2,1,0:T(8,128)S(1)}, u32[]{:S(2)}, u32[]{:S(2)}) collective-permute-start(f32[1,4,1,32,64]{4,3,2,1,0:T(8,128)S(1)} %get-tuple-element.108), channel_id=1, source_target_pairs={{0,1},{1,2},{2,3},{4,5},{5,6},{6,7},{8,9},{9,10},{10,11},{12,13},{... | collective-permute-start | bytes 98312 | tf_op jit(solution)/shard_map/ppermute | solution.py:23
  42.6 8.4 %collective-permute-start.6 = (f32[1,4,2,32,64]{4,3,2,1,0:T(8,128)S(1)}, f32[1,4,2,32,64]{4,3,2,1,0:T(8,128)S(1)}, u32[]{:S(2)}, u32[]{:S(2)}) collective-permute-start(f32[1,4,2,32,64]{4,3,2,1,0:T(8,128)S(1)} %fusion.388), channel_id=1, source_target_pairs={{0,4},{4,8},{8,12},{12,16},{16,20},{20,24},{24,28},{28,32},{32,36}... | collective-permute-start | bytes 196616 | tf_op jit(solution)/shard_map/ppermute | solution.py:34
  51.1 8.0 %collective-permute-start.10 = (f32[1,4,1,32,64]{4,3,2,1,0:T(8,128)S(1)}, f32[1,4,1,32,64]{4,3,2,1,0:T(8,128)S(1)}, u32[]{:S(2)}, u32[]{:S(2)}) collective-permute-start(f32[1,4,1,32,64]{4,3,2,1,0:T(8,128)S(1)} %get-tuple-element.103), channel_id=1, source_target_pairs={{1,0},{2,1},{3,2},{5,4},{6,5},{7,6},{9,8},{10,9},{11,10},{13,12},{... | collective-permute-start | bytes 98312 | tf_op jit(solution)/shard_map/ppermute | solution.py:26
  52.4 6.7 %collective-permute-start.11 = (f32[1,4,1,32,64]{4,3,2,1,0:T(8,128)S(1)}, f32[1,4,1,32,64]{4,3,2,1,0:T(8,128)S(1)}, u32[]{:S(2)}, u32[]{:S(2)}) collective-permute-start(f32[1,4,1,32,64]{4,3,2,1,0:T(8,128)S(1)} %get-tuple-element.104), channel_id=1, source_target_pairs={{0,1},{1,2},{2,3},{4,5},{5,6},{6,7},{8,9},{9,10},{10,11},{12,13},{... | collective-permute-start | bytes 98312 | tf_op jit(solution)/shard_map/ppermute | solution.py:23
  57.2 8.4 %collective-permute-start.9 = (f32[1,4,2,32,64]{4,3,2,1,0:T(8,128)S(1)}, f32[1,4,2,32,64]{4,3,2,1,0:T(8,128)S(1)}, u32[]{:S(2)}, u32[]{:S(2)}) collective-permute-start(f32[1,4,2,32,64]{4,3,2,1,0:T(8,128)S(1)} %fusion.207), channel_id=1, source_target_pairs={{0,4},{4,8},{8,12},{12,16},{16,20},{20,24},{24,28},{28,32},{32,36}... | collective-permute-start | bytes 196616 | tf_op jit(solution)/shard_map/ppermute | solution.py:34
  66.3 1.3 collective-permute-start.12
  67.6 3.9 %collective-permute-start.13 = (f32[2,2560]{1,0:T(2,128)S(1)}, f32[2,2560]{1,0:T(2,128)S(1)}, u32[]{:S(2)}, u32[]{:S(2)}) collective-permute-start(f32[2,2560]{1,0:T(2,128)S(1)} %maximum_select_fusion.8), channel_id=1, source_target_pairs={{0,8},{4,12},{8,0},{12,4},{16,24},{20,28},{24,16},{28,20},{32,40},... | collective-permute-start | bytes 61448 | tf_op jit(solution)/shard_map/ppermute | solution.py:196
  71.5 5.6 %collective-permute-start.14 = (f32[4,2560]{1,0:T(4,128)S(1)}, f32[4,2560]{1,0:T(4,128)S(1)}, u32[]{:S(2)}, u32[]{:S(2)}) collective-permute-start(f32[4,2560]{1,0:T(4,128)S(1)} %maximum_select_fusion.6), channel_id=1, source_target_pairs={{0,16},{4,20},{8,24},{12,28},{16,0},{20,4},{24,8},{28,12},{32,48},... | collective-permute-start | bytes 122888 | tf_op jit(solution)/shard_map/ppermute | solution.py:196
  77.1 4.5 %collective-permute-start.15 = (f32[8,2560]{1,0:T(8,128)S(1)}, f32[8,2560]{1,0:T(8,128)S(1)}, u32[]{:S(2)}, u32[]{:S(2)}) collective-permute-start(f32[8,2560]{1,0:T(8,128)S(1)} %maximum_select_fusion.4), channel_id=1, source_target_pairs={{0,32},{4,36},{8,40},{12,44},{16,48},{20,52},{24,56},{28,60},{32,0... | collective-permute-start | bytes 245768 | tf_op jit(solution)/shard_map/ppermute | solution.py:196
  81.6 6.9 %collective-permute-start.16 = (f32[16,2560]{1,0:T(8,128)S(1)}, f32[16,2560]{1,0:T(8,128)S(1)}, u32[]{:S(2)}, u32[]{:S(2)}) collective-permute-start(f32[16,2560]{1,0:T(8,128)S(1)} %maximum_select_fusion.2), channel_id=1, source_target_pairs={{0,64},{4,68},{8,72},{12,76},{16,80},{20,84},{24,88},{28,92},{32,9... | collective-permute-start | bytes 491528 | tf_op jit(solution)/shard_map/ppermute | solution.py:196
  89.3 204.7 %all-gather.5.cloned.1.call-start = ((), (), s32[]{:S(2)}) async-start(), calls=%async_computation.1 | async-start | bytes 1310720 | tf_op jit(solution)/shard_map/all_gather | solution.py:209
  138.5 7.8 %collective-permute-start.18 = (f32[1,4,1,32,64]{4,3,2,1,0:T(8,128)S(1)}, f32[1,4,1,32,64]{4,3,2,1,0:T(8,128)S(1)}, u32[]{:S(2)}, u32[]{:S(2)}) collective-permute-start(f32[1,4,1,32,64]{4,3,2,1,0:T(8,128)S(1)} %get-tuple-element.99), channel_id=1, source_target_pairs={{1,0},{2,1},{3,2},{5,4},{6,5},{7,6},{9,8},{10,9},{11,10},{13,12},{... | collective-permute-start | bytes 98312 | tf_op jit(solution)/shard_map/ppermute | solution.py:26
  139.8 6.5 %collective-permute-start.19 = (f32[1,4,1,32,64]{4,3,2,1,0:T(8,128)S(1)}, f32[1,4,1,32,64]{4,3,2,1,0:T(8,128)S(1)}, u32[]{:S(2)}, u32[]{:S(2)}) collective-permute-start(f32[1,4,1,32,64]{4,3,2,1,0:T(8,128)S(1)} %get-tuple-element.100), channel_id=1, source_target_pairs={{0,1},{1,2},{2,3},{4,5},{5,6},{6,7},{8,9},{9,10},{10,11},{12,13},{... | collective-permute-start | bytes 98312 | tf_op jit(solution)/shard_map/ppermute | solution.py:23
  144.4 8.4 %collective-permute-start.17 = (f32[1,4,2,32,64]{4,3,2,1,0:T(8,128)S(1)}, f32[1,4,2,32,64]{4,3,2,1,0:T(8,128)S(1)}, u32[]{:S(2)}, u32[]{:S(2)}) collective-permute-start(f32[1,4,2,32,64]{4,3,2,1,0:T(8,128)S(1)} %fusion.221), channel_id=1, source_target_pairs={{0,4},{4,8},{8,12},{12,16},{16,20},{20,24},{24,28},{28,32},{32,36}... | collective-permute-start | bytes 196616 | tf_op jit(solution)/shard_map/ppermute | solution.py:34
  153.4 12.6 %collective-permute-start.20 = (f32[1,4,4,64,128]{4,3,2,1,0:T(8,128)S(1)}, f32[1,4,4,64,128]{4,3,2,1,0:T(8,128)S(1)}, u32[]{:S(2)}, u32[]{:S(2)}) collective-permute-start(f32[1,4,4,64,128]{4,3,2,1,0:T(8,128)S(1)} %add.517), channel_id=1, source_target_pairs={{0,4},{4,8},{8,12},{12,16},{16,20},{20,24},{24,28},{28,32},{32,36}... | collective-permute-start | bytes 1572872 | tf_op jit(solution)/shard_map/ppermute | solution.py:34
  155.3 6.9 %collective-permute-start.21 = (f32[1,4,1,64,128]{4,3,2,1,0:T(8,128)S(1)}, f32[1,4,1,64,128]{4,3,2,1,0:T(8,128)S(1)}, u32[]{:S(2)}, u32[]{:S(2)}) collective-permute-start(f32[1,4,1,64,128]{4,3,2,1,0:T(8,128)S(1)} %get-tuple-element.59), channel_id=1, source_target_pairs={{1,0},{2,1},{3,2},{5,4},{6,5},{7,6},{9,8},{10,9},{11,10},{13,12},{... | collective-permute-start | bytes 393224 | tf_op jit(solution)/shard_map/ppermute | solution.py:26
  156.6 7.1 %collective-permute-start.22 = (f32[1,4,1,64,128]{4,3,2,1,0:T(8,128)S(1)}, f32[1,4,1,64,128]{4,3,2,1,0:T(8,128)S(1)}, u32[]{:S(2)}, u32[]{:S(2)}) collective-permute-start(f32[1,4,1,64,128]{4,3,2,1,0:T(8,128)S(1)} %get-tuple-element.60), channel_id=1, source_target_pairs={{0,1},{1,2},{2,3},{4,5},{5,6},{6,7},{8,9},{9,10},{10,11},{12,13},{... | collective-permute-start | bytes 393224 | tf_op jit(solution)/shard_map/ppermute | solution.py:23
  166.5 12.6 %collective-permute-start.23 = (f32[1,4,4,64,128]{4,3,2,1,0:T(8,128)S(1)}, f32[1,4,4,64,128]{4,3,2,1,0:T(8,128)S(1)}, u32[]{:S(2)}, u32[]{:S(2)}) collective-permute-start(f32[1,4,4,64,128]{4,3,2,1,0:T(8,128)S(1)} %fusion.93), channel_id=1, source_target_pairs={{0,4},{4,8},{8,12},{12,16},{16,20},{20,24},{24,28},{28,32},{32,36}... | collective-permute-start | bytes 1572872 | tf_op jit(solution)/shard_map/ppermute | solution.py:34
  168.5 6.9 %collective-permute-start.24 = (f32[1,4,1,64,128]{4,3,2,1,0:T(8,128)S(1)}, f32[1,4,1,64,128]{4,3,2,1,0:T(8,128)S(1)}, u32[]{:S(2)}, u32[]{:S(2)}) collective-permute-start(f32[1,4,1,64,128]{4,3,2,1,0:T(8,128)S(1)} %get-tuple-element.55), channel_id=1, source_target_pairs={{1,0},{2,1},{3,2},{5,4},{6,5},{7,6},{9,8},{10,9},{11,10},{13,12},{... | collective-permute-start | bytes 393224 | tf_op jit(solution)/shard_map/ppermute | solution.py:26
  169.8 7.1 %collective-permute-start.25 = (f32[1,4,1,64,128]{4,3,2,1,0:T(8,128)S(1)}, f32[1,4,1,64,128]{4,3,2,1,0:T(8,128)S(1)}, u32[]{:S(2)}, u32[]{:S(2)}) collective-permute-start(f32[1,4,1,64,128]{4,3,2,1,0:T(8,128)S(1)} %get-tuple-element.56), channel_id=1, source_target_pairs={{0,1},{1,2},{2,3},{4,5},{5,6},{6,7},{8,9},{9,10},{10,11},{12,13},{... | collective-permute-start | bytes 393224 | tf_op jit(solution)/shard_map/ppermute | solution.py:23
  179.7 12.6 %collective-permute-start.26 = (f32[1,4,4,64,128]{4,3,2,1,0:T(8,128)S(1)}, f32[1,4,4,64,128]{4,3,2,1,0:T(8,128)S(1)}, u32[]{:S(2)}, u32[]{:S(2)}) collective-permute-start(f32[1,4,4,64,128]{4,3,2,1,0:T(8,128)S(1)} %fusion.79), channel_id=1, source_target_pairs={{0,4},{4,8},{8,12},{12,16},{16,20},{20,24},{24,28},{28,32},{32,36}... | collective-permute-start | bytes 1572872 | tf_op jit(solution)/shard_map/ppermute | solution.py:34
  181.6 6.9 %collective-permute-start.27 = (f32[1,4,1,64,128]{4,3,2,1,0:T(8,128)S(1)}, f32[1,4,1,64,128]{4,3,2,1,0:T(8,128)S(1)}, u32[]{:S(2)}, u32[]{:S(2)}) collective-permute-start(f32[1,4,1,64,128]{4,3,2,1,0:T(8,128)S(1)} %get-tuple-element.51), channel_id=1, source_target_pairs={{1,0},{2,1},{3,2},{5,4},{6,5},{7,6},{9,8},{10,9},{11,10},{13,12},{... | collective-permute-start | bytes 393224 | tf_op jit(solution)/shard_map/ppermute | solution.py:26
  182.9 7.1 %collective-permute-start.28 = (f32[1,4,1,64,128]{4,3,2,1,0:T(8,128)S(1)}, f32[1,4,1,64,128]{4,3,2,1,0:T(8,128)S(1)}, u32[]{:S(2)}, u32[]{:S(2)}) collective-permute-start(f32[1,4,1,64,128]{4,3,2,1,0:T(8,128)S(1)} %get-tuple-element.52), channel_id=1, source_target_pairs={{0,1},{1,2},{2,3},{4,5},{5,6},{6,7},{8,9},{9,10},{10,11},{12,13},{... | collective-permute-start | bytes 393224 | tf_op jit(solution)/shard_map/ppermute | solution.py:23
  192.8 12.6 %collective-permute-start.29 = (f32[1,4,4,64,128]{4,3,2,1,0:T(8,128)S(1)}, f32[1,4,4,64,128]{4,3,2,1,0:T(8,128)S(1)}, u32[]{:S(2)}, u32[]{:S(2)}) collective-permute-start(f32[1,4,4,64,128]{4,3,2,1,0:T(8,128)S(1)} %fusion.65), channel_id=1, source_target_pairs={{0,4},{4,8},{8,12},{12,16},{16,20},{20,24},{24,28},{28,32},{32,36}... | collective-permute-start | bytes 1572872 | tf_op jit(solution)/shard_map/ppermute | solution.py:34
  194.8 6.9 %collective-permute-start.30 = (f32[1,4,1,64,128]{4,3,2,1,0:T(8,128)S(1)}, f32[1,4,1,64,128]{4,3,2,1,0:T(8,128)S(1)}, u32[]{:S(2)}, u32[]{:S(2)}) collective-permute-start(f32[1,4,1,64,128]{4,3,2,1,0:T(8,128)S(1)} %get-tuple-element.47), channel_id=1, source_target_pairs={{1,0},{2,1},{3,2},{5,4},{6,5},{7,6},{9,8},{10,9},{11,10},{13,12},{... | collective-permute-start | bytes 393224 | tf_op jit(solution)/shard_map/ppermute | solution.py:26
  196.1 7.1 %collective-permute-start.31 = (f32[1,4,1,64,128]{4,3,2,1,0:T(8,128)S(1)}, f32[1,4,1,64,128]{4,3,2,1,0:T(8,128)S(1)}, u32[]{:S(2)}, u32[]{:S(2)}) collective-permute-start(f32[1,4,1,64,128]{4,3,2,1,0:T(8,128)S(1)} %get-tuple-element.48), channel_id=1, source_target_pairs={{0,1},{1,2},{2,3},{4,5},{5,6},{6,7},{8,9},{9,10},{10,11},{12,13},{... | collective-permute-start | bytes 393224 | tf_op jit(solution)/shard_map/ppermute | solution.py:23
  206.0 12.6 %collective-permute-start.32 = (f32[1,4,4,64,128]{4,3,2,1,0:T(8,128)S(1)}, f32[1,4,4,64,128]{4,3,2,1,0:T(8,128)S(1)}, u32[]{:S(2)}, u32[]{:S(2)}) collective-permute-start(f32[1,4,4,64,128]{4,3,2,1,0:T(8,128)S(1)} %fusion.51), channel_id=1, source_target_pairs={{0,4},{4,8},{8,12},{12,16},{16,20},{20,24},{24,28},{28,32},{32,36}... | collective-permute-start | bytes 1572872 | tf_op jit(solution)/shard_map/ppermute | solution.py:34
  207.9 6.9 %collective-permute-start.33 = (f32[1,4,1,64,128]{4,3,2,1,0:T(8,128)S(1)}, f32[1,4,1,64,128]{4,3,2,1,0:T(8,128)S(1)}, u32[]{:S(2)}, u32[]{:S(2)}) collective-permute-start(f32[1,4,1,64,128]{4,3,2,1,0:T(8,128)S(1)} %get-tuple-element.43), channel_id=1, source_target_pairs={{1,0},{2,1},{3,2},{5,4},{6,5},{7,6},{9,8},{10,9},{11,10},{13,12},{... | collective-permute-start | bytes 393224 | tf_op jit(solution)/shard_map/ppermute | solution.py:26
  209.2 7.1 %collective-permute-start.34 = (f32[1,4,1,64,128]{4,3,2,1,0:T(8,128)S(1)}, f32[1,4,1,64,128]{4,3,2,1,0:T(8,128)S(1)}, u32[]{:S(2)}, u32[]{:S(2)}) collective-permute-start(f32[1,4,1,64,128]{4,3,2,1,0:T(8,128)S(1)} %get-tuple-element.44), channel_id=1, source_target_pairs={{0,1},{1,2},{2,3},{4,5},{5,6},{6,7},{8,9},{9,10},{10,11},{12,13},{... | collective-permute-start | bytes 393224 | tf_op jit(solution)/shard_map/ppermute | solution.py:23
  219.6 7.8 %collective-permute-start.36 = (f32[1,4,1,32,64]{4,3,2,1,0:T(8,128)S(1)}, f32[1,4,1,32,64]{4,3,2,1,0:T(8,128)S(1)}, u32[]{:S(2)}, u32[]{:S(2)}) collective-permute-start(f32[1,4,1,32,64]{4,3,2,1,0:T(8,128)S(1)} %get-tuple-element.95), channel_id=1, source_target_pairs={{1,0},{2,1},{3,2},{5,4},{6,5},{7,6},{9,8},{10,9},{11,10},{13,12},{... | collective-permute-start | bytes 98312 | tf_op jit(solution)/shard_map/ppermute | solution.py:26
  220.9 6.5 %collective-permute-start.37 = (f32[1,4,1,32,64]{4,3,2,1,0:T(8,128)S(1)}, f32[1,4,1,32,64]{4,3,2,1,0:T(8,128)S(1)}, u32[]{:S(2)}, u32[]{:S(2)}) collective-permute-start(f32[1,4,1,32,64]{4,3,2,1,0:T(8,128)S(1)} %get-tuple-element.96), channel_id=1, source_target_pairs={{0,1},{1,2},{2,3},{4,5},{5,6},{6,7},{8,9},{9,10},{10,11},{12,13},{... | collective-permute-start | bytes 98312 | tf_op jit(solution)/shard_map/ppermute | solution.py:23
  225.5 8.4 %collective-permute-start.35 = (f32[1,4,2,32,64]{4,3,2,1,0:T(8,128)S(1)}, f32[1,4,2,32,64]{4,3,2,1,0:T(8,128)S(1)}, u32[]{:S(2)}, u32[]{:S(2)}) collective-permute-start(f32[1,4,2,32,64]{4,3,2,1,0:T(8,128)S(1)} %fusion.389), channel_id=1, source_target_pairs={{0,4},{4,8},{8,12},{12,16},{16,20},{20,24},{24,28},{28,32},{32,36}... | collective-permute-start | bytes 196616 | tf_op jit(solution)/shard_map/ppermute | solution.py:34
  234.0 7.8 %collective-permute-start.39 = (f32[1,4,1,32,64]{4,3,2,1,0:T(8,128)S(1)}, f32[1,4,1,32,64]{4,3,2,1,0:T(8,128)S(1)}, u32[]{:S(2)}, u32[]{:S(2)}) collective-permute-start(f32[1,4,1,32,64]{4,3,2,1,0:T(8,128)S(1)} %get-tuple-element.91), channel_id=1, source_target_pairs={{1,0},{2,1},{3,2},{5,4},{6,5},{7,6},{9,8},{10,9},{11,10},{13,12},{... | collective-permute-start | bytes 98312 | tf_op jit(solution)/shard_map/ppermute | solution.py:26
  235.3 6.5 %collective-permute-start.40 = (f32[1,4,1,32,64]{4,3,2,1,0:T(8,128)S(1)}, f32[1,4,1,32,64]{4,3,2,1,0:T(8,128)S(1)}, u32[]{:S(2)}, u32[]{:S(2)}) collective-permute-start(f32[1,4,1,32,64]{4,3,2,1,0:T(8,128)S(1)} %get-tuple-element.92), channel_id=1, source_target_pairs={{0,1},{1,2},{2,3},{4,5},{5,6},{6,7},{8,9},{9,10},{10,11},{12,13},{... | collective-permute-start | bytes 98312 | tf_op jit(solution)/shard_map/ppermute | solution.py:23
  239.9 8.4 %collective-permute-start.38 = (f32[1,4,2,32,64]{4,3,2,1,0:T(8,128)S(1)}, f32[1,4,2,32,64]{4,3,2,1,0:T(8,128)S(1)}, u32[]{:S(2)}, u32[]{:S(2)}) collective-permute-start(f32[1,4,2,32,64]{4,3,2,1,0:T(8,128)S(1)} %fusion.166), channel_id=1, source_target_pairs={{0,4},{4,8},{8,12},{12,16},{16,20},{20,24},{24,28},{28,32},{32,36}... | collective-permute-start | bytes 196616 | tf_op jit(solution)/shard_map/ppermute | solution.py:34
  248.9 1.3 collective-permute-start.41
  250.2 3.8 %collective-permute-start.42 = (f32[2,2048]{1,0:T(2,128)S(1)}, f32[2,2048]{1,0:T(2,128)S(1)}, u32[]{:S(2)}, u32[]{:S(2)}) collective-permute-start(f32[2,2048]{1,0:T(2,128)S(1)} %maximum_select_fusion.9), channel_id=1, source_target_pairs={{0,8},{4,12},{8,0},{12,4},{16,24},{20,28},{24,16},{28,20},{32,40},... | collective-permute-start | bytes 49160 | tf_op jit(solution)/shard_map/ppermute | solution.py:196
  254.1 5.5 %collective-permute-start.43 = (f32[4,2048]{1,0:T(4,128)S(1)}, f32[4,2048]{1,0:T(4,128)S(1)}, u32[]{:S(2)}, u32[]{:S(2)}) collective-permute-start(f32[4,2048]{1,0:T(4,128)S(1)} %maximum_select_fusion.7), channel_id=1, source_target_pairs={{0,16},{4,20},{8,24},{12,28},{16,0},{20,4},{24,8},{28,12},{32,48},... | collective-permute-start | bytes 98312 | tf_op jit(solution)/shard_map/ppermute | solution.py:196
  259.6 4.3 %collective-permute-start.44 = (f32[8,2048]{1,0:T(8,128)S(1)}, f32[8,2048]{1,0:T(8,128)S(1)}, u32[]{:S(2)}, u32[]{:S(2)}) collective-permute-start(f32[8,2048]{1,0:T(8,128)S(1)} %maximum_select_fusion.5), channel_id=1, source_target_pairs={{0,32},{4,36},{8,40},{12,44},{16,48},{20,52},{24,56},{28,60},{32,0... | collective-permute-start | bytes 196616 | tf_op jit(solution)/shard_map/ppermute | solution.py:196
  263.9 6.6 %collective-permute-start.45 = (f32[16,2048]{1,0:T(8,128)S(1)}, f32[16,2048]{1,0:T(8,128)S(1)}, u32[]{:S(2)}, u32[]{:S(2)}) collective-permute-start(f32[16,2048]{1,0:T(8,128)S(1)} %maximum_select_fusion.3), channel_id=1, source_target_pairs={{0,64},{4,68},{8,72},{12,76},{16,80},{20,84},{24,88},{28,92},{32,9... | collective-permute-start | bytes 393224 | tf_op jit(solution)/shard_map/ppermute | solution.py:196
  313.9 7.8 %collective-permute-start.47 = (f32[1,4,1,32,64]{4,3,2,1,0:T(8,128)S(1)}, f32[1,4,1,32,64]{4,3,2,1,0:T(8,128)S(1)}, u32[]{:S(2)}, u32[]{:S(2)}) collective-permute-start(f32[1,4,1,32,64]{4,3,2,1,0:T(8,128)S(1)} %get-tuple-element.87), channel_id=1, source_target_pairs={{1,0},{2,1},{3,2},{5,4},{6,5},{7,6},{9,8},{10,9},{11,10},{13,12},{... | collective-permute-start | bytes 98312 | tf_op jit(solution)/shard_map/ppermute | solution.py:26
  315.2 6.5 %collective-permute-start.48 = (f32[1,4,1,32,64]{4,3,2,1,0:T(8,128)S(1)}, f32[1,4,1,32,64]{4,3,2,1,0:T(8,128)S(1)}, u32[]{:S(2)}, u32[]{:S(2)}) collective-permute-start(f32[1,4,1,32,64]{4,3,2,1,0:T(8,128)S(1)} %get-tuple-element.88), channel_id=1, source_target_pairs={{0,1},{1,2},{2,3},{4,5},{5,6},{6,7},{8,9},{9,10},{10,11},{12,13},{... | collective-permute-start | bytes 98312 | tf_op jit(solution)/shard_map/ppermute | solution.py:23
  319.8 8.4 %collective-permute-start.46 = (f32[1,4,2,32,64]{4,3,2,1,0:T(8,128)S(1)}, f32[1,4,2,32,64]{4,3,2,1,0:T(8,128)S(1)}, u32[]{:S(2)}, u32[]{:S(2)}) collective-permute-start(f32[1,4,2,32,64]{4,3,2,1,0:T(8,128)S(1)} %fusion.233), channel_id=1, source_target_pairs={{0,4},{4,8},{8,12},{12,16},{16,20},{20,24},{24,28},{28,32},{32,36}... | collective-permute-start | bytes 196616 | tf_op jit(solution)/shard_map/ppermute | solution.py:34
  328.7 12.6 %collective-permute-start.49 = (f32[1,4,4,64,128]{4,3,2,1,0:T(8,128)S(1)}, f32[1,4,4,64,128]{4,3,2,1,0:T(8,128)S(1)}, u32[]{:S(2)}, u32[]{:S(2)}) collective-permute-start(f32[1,4,4,64,128]{4,3,2,1,0:T(8,128)S(1)} %add.567), channel_id=1, source_target_pairs={{0,4},{4,8},{8,12},{12,16},{16,20},{20,24},{24,28},{28,32},{32,36}... | collective-permute-start | bytes 1572872 | tf_op jit(solution)/shard_map/ppermute | solution.py:34
  330.7 6.9 %collective-permute-start.50 = (f32[1,4,1,64,128]{4,3,2,1,0:T(8,128)S(1)}, f32[1,4,1,64,128]{4,3,2,1,0:T(8,128)S(1)}, u32[]{:S(2)}, u32[]{:S(2)}) collective-permute-start(f32[1,4,1,64,128]{4,3,2,1,0:T(8,128)S(1)} %get-tuple-element.39), channel_id=1, source_target_pairs={{1,0},{2,1},{3,2},{5,4},{6,5},{7,6},{9,8},{10,9},{11,10},{13,12},{... | collective-permute-start | bytes 393224 | tf_op jit(solution)/shard_map/ppermute | solution.py:26
  332.0 7.1 %collective-permute-start.51 = (f32[1,4,1,64,128]{4,3,2,1,0:T(8,128)S(1)}, f32[1,4,1,64,128]{4,3,2,1,0:T(8,128)S(1)}, u32[]{:S(2)}, u32[]{:S(2)}) collective-permute-start(f32[1,4,1,64,128]{4,3,2,1,0:T(8,128)S(1)} %get-tuple-element.40), channel_id=1, source_target_pairs={{0,1},{1,2},{2,3},{4,5},{5,6},{6,7},{8,9},{9,10},{10,11},{12,13},{... | collective-permute-start | bytes 393224 | tf_op jit(solution)/shard_map/ppermute | solution.py:23
  341.9 12.6 %collective-permute-start.52 = (f32[1,4,4,64,128]{4,3,2,1,0:T(8,128)S(1)}, f32[1,4,4,64,128]{4,3,2,1,0:T(8,128)S(1)}, u32[]{:S(2)}, u32[]{:S(2)}) collective-permute-start(f32[1,4,4,64,128]{4,3,2,1,0:T(8,128)S(1)} %fusion.25), channel_id=1, source_target_pairs={{0,4},{4,8},{8,12},{12,16},{16,20},{20,24},{24,28},{28,32},{32,36}... | collective-permute-start | bytes 1572872 | tf_op jit(solution)/shard_map/ppermute | solution.py:34
  343.8 6.9 %collective-permute-start.53 = (f32[1,4,1,64,128]{4,3,2,1,0:T(8,128)S(1)}, f32[1,4,1,64,128]{4,3,2,1,0:T(8,128)S(1)}, u32[]{:S(2)}, u32[]{:S(2)}) collective-permute-start(f32[1,4,1,64,128]{4,3,2,1,0:T(8,128)S(1)} %get-tuple-element.35), channel_id=1, source_target_pairs={{1,0},{2,1},{3,2},{5,4},{6,5},{7,6},{9,8},{10,9},{11,10},{13,12},{... | collective-permute-start | bytes 393224 | tf_op jit(solution)/shard_map/ppermute | solution.py:26
  345.1 7.1 %collective-permute-start.54 = (f32[1,4,1,64,128]{4,3,2,1,0:T(8,128)S(1)}, f32[1,4,1,64,128]{4,3,2,1,0:T(8,128)S(1)}, u32[]{:S(2)}, u32[]{:S(2)}) collective-permute-start(f32[1,4,1,64,128]{4,3,2,1,0:T(8,128)S(1)} %get-tuple-element.36), channel_id=1, source_target_pairs={{0,1},{1,2},{2,3},{4,5},{5,6},{6,7},{8,9},{9,10},{10,11},{12,13},{... | collective-permute-start | bytes 393224 | tf_op jit(solution)/shard_map/ppermute | solution.py:23
Sparse Core Ops, SparseCore 0:
  89.4 24.9 all-gather.2
  271.4 22.6 all-gather.4

commit v14 on v13

--- a/solution.py
+++ b/solution.py
@@ -187,7 +187,7 @@
     return (whole_source, whole_metric)
 
 
-def gather_doubling(flat, axis):
+def gather_doubling(flat, axis, dim):
     size = lax.axis_size(axis)
     position = lax.axis_index(axis)
     gathered = flat
@@ -197,16 +197,16 @@
         lower = (position & step) == 0
         gathered = jnp.where(
             lower,
-            jnp.concatenate([gathered, other], axis=0),
-            jnp.concatenate([other, gathered], axis=0),
+            jnp.concatenate([gathered, other], axis=dim),
+            jnp.concatenate([other, gathered], axis=dim),
         )
         step *= 2
     return gathered
 
 
 def gather_all(flat):
-    across = gather_doubling(flat, "tm")
-    whole = lax.all_gather(across, "space", axis=1, tiled=True)
+    across = gather_doubling(flat, "tm", 0)
+    whole = gather_doubling(across, "space", 1)
     return whole.reshape(-1, flat.shape[1])
 
 

time: 364 us -> 346 us (0.951)
  waiting for transfers between devices: 164 us -> 143 us
  starting transfers between devices: 123 us -> 137 us
  between operations: 14.7 us -> 1.35 us
    all_gather x2 -> x0, waiting for transfers between devices: 47.9 us -> none  [gather_all(): whole = lax.all_gather(across, 'space', axis=1, tiled=True)]
    ppermute x10 -> x14, waiting for transfers between devices: 37 us -> 64.4 us  [gather_doubling(): other = lax.ppermute(gathered, axis, [(i, i ^ step) for i in range(size)])]
    ppermute x10 -> x14, starting transfers between devices: 6.55 us -> 20 us  [gather_doubling(): other = lax.ppermute(gathered, axis, [(i, i ^ step) for i in range(size)])]
  transfers between devices with their start and end apart: 57 -> 59, of which waited for: 45 -> 47; matrix products, arithmetic and copies ran while one was open for 1% -> 1% of each run, Pallas kernels for 0% -> 0%
where the time goes in v14:
time: 346 us; the launch traced here: 342 us
  waiting for transfers between devices  143 us (41%)
  starting transfers between devices  137 us (40%)
  Pallas kernels  28.5 us (8%)
  other arithmetic  16.8 us (5%)
  local copies, waits for them, and re-layouts  13.3 us (4%)
    ppermute x15, starting transfers between devices, with_halo(): lax.ppermute(lax.slice_in_dim(block, block.shape[dim] - width, None, axis...  68.5 us
    ppermute x14, waiting for transfers between devices, gather_doubling(): other = lax.ppermute(gathered, axis, [(i, i ^ step) for i in range(size)])  64.4 us
    ppermute x15, waiting for transfers between devices, from_behind(): return lax.ppermute(array, axis, pairs)  54.8 us
    ppermute x15, starting transfers between devices, from_behind(): return lax.ppermute(array, axis, pairs)  28.9 us
    pallas_call x2, Pallas kernels, coarse_solve(): pl.pallas_call(kernel, out_shape=jax.ShapeDtypeStruct(flat_source.shape,...  28.5 us
    ppermute x14, starting transfers between devices, gather_doubling(): other = lax.ppermute(gathered, axis, [(i, i ^ step) for i in range(size)])  20 us
    ppermute x15, starting transfers between devices, with_halo(): lax.ppermute(lax.slice_in_dim(block, 0, width, axis=dim), axis, backward)  19.4 us
    ppermute x15, waiting for transfers between devices, with_halo(): lax.ppermute(lax.slice_in_dim(block, block.shape[dim] - width, None, axis...  13.7 us
  transfers between devices with their start and end apart: 59, of which 47 were waited for; matrix products, arithmetic and copies ran while one was open for 1% of the time, Pallas kernels for 0%

profile of v14, /device:TPU:2, one launch (start us, length us, event | category | flops | bytes accessed | tf_op | source)
XLA Modules:
  0.0 342.4 jit_solution(14530969627387623815)
XLA Ops:
  3.2 2.1 collective-permute-start
  6.6 4.6 %collective-permute-start.2 = (f32[1,4,1,64,128]{4,3,2,1,0:T(8,128)S(1)}, f32[1,4,1,64,128]{4,3,2,1,0:T(8,128)S(1)}, u32[]{:S(2)}, u32[]{:S(2)}) collective-permute-start(f32[1,4,1,64,128]{4,3,2,1,0:T(8,128)S(1)} %get-tuple-element.68), channel_id=1, source_target_pairs={{0,1},{1,2},{2,3},{4,5},{5,6},{6,7},{8,9},{9,10},{10,11},{12,13},{... | collective-permute-start | bytes 393224 | tf_op jit(solution)/shard_map/ppermute | solution.py:23
  16.5 1.9 collective-permute-start.3
  19.8 4.6 %collective-permute-start.5 = (f32[1,4,1,64,128]{4,3,2,1,0:T(8,128)S(1)}, f32[1,4,1,64,128]{4,3,2,1,0:T(8,128)S(1)}, u32[]{:S(2)}, u32[]{:S(2)}) collective-permute-start(f32[1,4,1,64,128]{4,3,2,1,0:T(8,128)S(1)} %get-tuple-element.64), channel_id=1, source_target_pairs={{0,1},{1,2},{2,3},{4,5},{5,6},{6,7},{8,9},{9,10},{10,11},{12,13},{... | collective-permute-start | bytes 393224 | tf_op jit(solution)/shard_map/ppermute | solution.py:23
  24.4 2.2 collective-permute-done.4
  31.4 4.5 %collective-permute-start.8 = (f32[1,4,1,32,64]{4,3,2,1,0:T(8,128)S(1)}, f32[1,4,1,32,64]{4,3,2,1,0:T(8,128)S(1)}, u32[]{:S(2)}, u32[]{:S(2)}) collective-permute-start(f32[1,4,1,32,64]{4,3,2,1,0:T(8,128)S(1)} %get-tuple-element.108), channel_id=1, source_target_pairs={{0,1},{1,2},{2,3},{4,5},{5,6},{6,7},{8,9},{9,10},{10,11},{12,13},{... | collective-permute-start | bytes 98312 | tf_op jit(solution)/shard_map/ppermute | solution.py:23
  36.0 1.9 collective-permute-start.6
  38.1 6.3 %collective-permute-done.6 = f32[1,4,2,32,64]{4,3,2,1,0:T(8,128)S(1)} collective-permute-done((f32[1,4,2,32,64]{4,3,2,1,0:T(8,128)S(1)}, f32[1,4,2,32,64]{4,3,2,1,0:T(8,128)S(1)}, u32[]{:S(2)}, u32[]{:S(2)}) %collective-permute-start.6) | collective-permute-done | bytes 65568 | tf_op jit(solution)/shard_map/ppermute | solution.py:34
  45.9 4.5 %collective-permute-start.11 = (f32[1,4,1,32,64]{4,3,2,1,0:T(8,128)S(1)}, f32[1,4,1,32,64]{4,3,2,1,0:T(8,128)S(1)}, u32[]{:S(2)}, u32[]{:S(2)}) collective-permute-start(f32[1,4,1,32,64]{4,3,2,1,0:T(8,128)S(1)} %get-tuple-element.104), channel_id=1, source_target_pairs={{0,1},{1,2},{2,3},{4,5},{5,6},{6,7},{8,9},{9,10},{10,11},{12,13},{... | collective-permute-start | bytes 98312 | tf_op jit(solution)/shard_map/ppermute | solution.py:23
  50.6 1.9 collective-permute-start.9
  52.7 6.3 %collective-permute-done.9 = f32[1,4,2,32,64]{4,3,2,1,0:T(8,128)S(1)} collective-permute-done((f32[1,4,2,32,64]{4,3,2,1,0:T(8,128)S(1)}, f32[1,4,2,32,64]{4,3,2,1,0:T(8,128)S(1)}, u32[]{:S(2)}, u32[]{:S(2)}) %collective-permute-start.9) | collective-permute-done | bytes 65568 | tf_op jit(solution)/shard_map/ppermute | solution.py:34
  61.1 3.8 %collective-permute-done.13 = f32[2,2560]{1,0:T(2,128)S(1)} collective-permute-done((f32[2,2560]{1,0:T(2,128)S(1)}, f32[2,2560]{1,0:T(2,128)S(1)}, u32[]{:S(2)}, u32[]{:S(2)}) %collective-permute-start.13) | collective-permute-done | bytes 20512 | tf_op jit(solution)/shard_map/ppermute | solution.py:196
  65.0 5.5 %collective-permute-done.14 = f32[4,2560]{1,0:T(4,128)S(1)} collective-permute-done((f32[4,2560]{1,0:T(4,128)S(1)}, f32[4,2560]{1,0:T(4,128)S(1)}, u32[]{:S(2)}, u32[]{:S(2)}) %collective-permute-start.14) | collective-permute-done | bytes 40992 | tf_op jit(solution)/shard_map/ppermute | solution.py:196
  70.6 4.4 %collective-permute-done.15 = f32[8,2560]{1,0:T(8,128)S(1)} collective-permute-done((f32[8,2560]{1,0:T(8,128)S(1)}, f32[8,2560]{1,0:T(8,128)S(1)}, u32[]{:S(2)}, u32[]{:S(2)}) %collective-permute-start.15) | collective-permute-done | bytes 81952 | tf_op jit(solution)/shard_map/ppermute | solution.py:196
  75.0 3.1 collective-permute-start.16
  78.1 3.8 %collective-permute-done.16 = f32[16,2560]{1,0:T(8,128)S(1)} collective-permute-done((f32[16,2560]{1,0:T(8,128)S(1)}, f32[16,2560]{1,0:T(8,128)S(1)}, u32[]{:S(2)}, u32[]{:S(2)}) %collective-permute-start.16) | collective-permute-done | bytes 163872 | tf_op jit(solution)/shard_map/ppermute | solution.py:196
  82.0 2.0 collective-permute-start.17
  84.0 6.4 %collective-permute-done.17 = f32[32,2560]{1,0:T(8,128)S(1)} collective-permute-done((f32[32,2560]{1,0:T(8,128)S(1)}, f32[32,2560]{1,0:T(8,128)S(1)}, u32[]{:S(2)}, u32[]{:S(2)}) %collective-permute-start.17) | collective-permute-done | bytes 327712 | tf_op jit(solution)/shard_map/ppermute | solution.py:196
  90.5 5.3 %collective-permute-start.18 = (f32[32,5120]{1,0:T(8,128)S(1)}, f32[32,5120]{1,0:T(8,128)}, u32[]{:S(2)}, u32[]{:S(2)}) collective-permute-start(f32[32,5120]{1,0:T(8,128)S(1)} %maximum_select_fusion.2), channel_id=1, source_target_pairs={{0,2},{1,3},{2,0},{3,1},{4,6},{5,7},{6,4},{7,5},{8,10},{9,11},{10,... | collective-permute-start | bytes 1966088 | tf_op jit(solution)/shard_map/ppermute | solution.py:196
  95.8 9.3 %collective-permute-done.18 = f32[32,5120]{1,0:T(8,128)} collective-permute-done((f32[32,5120]{1,0:T(8,128)S(1)}, f32[32,5120]{1,0:T(8,128)}, u32[]{:S(2)}, u32[]{:S(2)}) %collective-permute-start.18) | collective-permute-done | bytes 655392 | tf_op jit(solution)/shard_map/ppermute | solution.py:196
  105.1 1.8 maximum_select_fusion
  112.6 14.2 %shard_map.37 = f32[32,16,512]{2,1,0:T(8,128)} custom-call(f32[32,16,512]{2,1,0:T(8,128)} %reshape_transpose_reshape.7.src_ref, f32[32,16,512]{2,1,0:T(8,128)} %reshape.877.met_ref), custom_call_target="tpu_custom_call" | custom-call | tf_op jit(solution)/shard_map/pallas_call | solution.py:161
  131.0 4.5 %collective-permute-start.21 = (f32[1,4,1,32,64]{4,3,2,1,0:T(8,128)S(1)}, f32[1,4,1,32,64]{4,3,2,1,0:T(8,128)S(1)}, u32[]{:S(2)}, u32[]{:S(2)}) collective-permute-start(f32[1,4,1,32,64]{4,3,2,1,0:T(8,128)S(1)} %get-tuple-element.100), channel_id=1, source_target_pairs={{0,1},{1,2},{2,3},{4,5},{5,6},{6,7},{8,9},{9,10},{10,11},{12,13},{... | collective-permute-start | bytes 98312 | tf_op jit(solution)/shard_map/ppermute | solution.py:23
  135.6 1.9 collective-permute-start.19
  137.6 6.3 %collective-permute-done.19 = f32[1,4,2,32,64]{4,3,2,1,0:T(8,128)S(1)} collective-permute-done((f32[1,4,2,32,64]{4,3,2,1,0:T(8,128)S(1)}, f32[1,4,2,32,64]{4,3,2,1,0:T(8,128)S(1)}, u32[]{:S(2)}, u32[]{:S(2)}) %collective-permute-start.19) | collective-permute-done | bytes 65568 | tf_op jit(solution)/shard_map/ppermute | solution.py:34
  144.5 1.9 collective-permute-start.22
  147.7 4.6 %collective-permute-start.24 = (f32[1,4,1,64,128]{4,3,2,1,0:T(8,128)S(1)}, f32[1,4,1,64,128]{4,3,2,1,0:T(8,128)S(1)}, u32[]{:S(2)}, u32[]{:S(2)}) collective-permute-start(f32[1,4,1,64,128]{4,3,2,1,0:T(8,128)S(1)} %get-tuple-element.60), channel_id=1, source_target_pairs={{0,1},{1,2},{2,3},{4,5},{5,6},{6,7},{8,9},{9,10},{10,11},{12,13},{... | collective-permute-start | bytes 393224 | tf_op jit(solution)/shard_map/ppermute | solution.py:23
  155.0 2.1 collective-permute-done.22
  157.7 1.9 collective-permute-start.25
  160.9 4.6 %collective-permute-start.27 = (f32[1,4,1,64,128]{4,3,2,1,0:T(8,128)S(1)}, f32[1,4,1,64,128]{4,3,2,1,0:T(8,128)S(1)}, u32[]{:S(2)}, u32[]{:S(2)}) collective-permute-start(f32[1,4,1,64,128]{4,3,2,1,0:T(8,128)S(1)} %get-tuple-element.56), channel_id=1, source_target_pairs={{0,1},{1,2},{2,3},{4,5},{5,6},{6,7},{8,9},{9,10},{10,11},{12,13},{... | collective-permute-start | bytes 393224 | tf_op jit(solution)/shard_map/ppermute | solution.py:23
  168.2 2.1 collective-permute-done.25
  170.8 1.9 collective-permute-start.28
  174.1 4.7 %collective-permute-start.30 = (f32[1,4,1,64,128]{4,3,2,1,0:T(8,128)S(1)}, f32[1,4,1,64,128]{4,3,2,1,0:T(8,128)S(1)}, u32[]{:S(2)}, u32[]{:S(2)}) collective-permute-start(f32[1,4,1,64,128]{4,3,2,1,0:T(8,128)S(1)} %get-tuple-element.52), channel_id=1, source_target_pairs={{0,1},{1,2},{2,3},{4,5},{5,6},{6,7},{8,9},{9,10},{10,11},{12,13},{... | collective-permute-start | bytes 393224 | tf_op jit(solution)/shard_map/ppermute | solution.py:23
  181.3 2.1 collective-permute-done.28
  184.0 1.9 collective-permute-start.31
  187.2 4.6 %collective-permute-start.33 = (f32[1,4,1,64,128]{4,3,2,1,0:T(8,128)S(1)}, f32[1,4,1,64,128]{4,3,2,1,0:T(8,128)S(1)}, u32[]{:S(2)}, u32[]{:S(2)}) collective-permute-start(f32[1,4,1,64,128]{4,3,2,1,0:T(8,128)S(1)} %get-tuple-element.48), channel_id=1, source_target_pairs={{0,1},{1,2},{2,3},{4,5},{5,6},{6,7},{8,9},{9,10},{10,11},{12,13},{... | collective-permute-start | bytes 393224 | tf_op jit(solution)/shard_map/ppermute | solution.py:23
  194.5 2.1 collective-permute-done.31
  197.1 1.9 collective-permute-start.34
  200.4 4.6 %collective-permute-start.36 = (f32[1,4,1,64,128]{4,3,2,1,0:T(8,128)S(1)}, f32[1,4,1,64,128]{4,3,2,1,0:T(8,128)S(1)}, u32[]{:S(2)}, u32[]{:S(2)}) collective-permute-start(f32[1,4,1,64,128]{4,3,2,1,0:T(8,128)S(1)} %get-tuple-element.44), channel_id=1, source_target_pairs={{0,1},{1,2},{2,3},{4,5},{5,6},{6,7},{8,9},{9,10},{10,11},{12,13},{... | collective-permute-start | bytes 393224 | tf_op jit(solution)/shard_map/ppermute | solution.py:23
  207.7 2.1 collective-permute-done.34
  212.0 4.5 %collective-permute-start.39 = (f32[1,4,1,32,64]{4,3,2,1,0:T(8,128)S(1)}, f32[1,4,1,32,64]{4,3,2,1,0:T(8,128)S(1)}, u32[]{:S(2)}, u32[]{:S(2)}) collective-permute-start(f32[1,4,1,32,64]{4,3,2,1,0:T(8,128)S(1)} %get-tuple-element.96), channel_id=1, source_target_pairs={{0,1},{1,2},{2,3},{4,5},{5,6},{6,7},{8,9},{9,10},{10,11},{12,13},{... | collective-permute-start | bytes 98312 | tf_op jit(solution)/shard_map/ppermute | solution.py:23
  216.6 1.9 collective-permute-start.37
  218.6 6.3 %collective-permute-done.37 = f32[1,4,2,32,64]{4,3,2,1,0:T(8,128)S(1)} collective-permute-done((f32[1,4,2,32,64]{4,3,2,1,0:T(8,128)S(1)}, f32[1,4,2,32,64]{4,3,2,1,0:T(8,128)S(1)}, u32[]{:S(2)}, u32[]{:S(2)}) %collective-permute-start.37) | collective-permute-done | bytes 65568 | tf_op jit(solution)/shard_map/ppermute | solution.py:34
  226.4 4.5 %collective-permute-start.42 = (f32[1,4,1,32,64]{4,3,2,1,0:T(8,128)S(1)}, f32[1,4,1,32,64]{4,3,2,1,0:T(8,128)S(1)}, u32[]{:S(2)}, u32[]{:S(2)}) collective-permute-start(f32[1,4,1,32,64]{4,3,2,1,0:T(8,128)S(1)} %get-tuple-element.92), channel_id=1, source_target_pairs={{0,1},{1,2},{2,3},{4,5},{5,6},{6,7},{8,9},{9,10},{10,11},{12,13},{... | collective-permute-start | bytes 98312 | tf_op jit(solution)/shard_map/ppermute | solution.py:23
  231.0 1.9 collective-permute-start.40
  233.1 6.3 %collective-permute-done.40 = f32[1,4,2,32,64]{4,3,2,1,0:T(8,128)S(1)} collective-permute-done((f32[1,4,2,32,64]{4,3,2,1,0:T(8,128)S(1)}, f32[1,4,2,32,64]{4,3,2,1,0:T(8,128)S(1)}, u32[]{:S(2)}, u32[]{:S(2)}) %collective-permute-start.40) | collective-permute-done | bytes 65568 | tf_op jit(solution)/shard_map/ppermute | solution.py:34
  241.4 3.7 %collective-permute-done.44 = f32[2,2048]{1,0:T(2,128)S(1)} collective-permute-done((f32[2,2048]{1,0:T(2,128)S(1)}, f32[2,2048]{1,0:T(2,128)S(1)}, u32[]{:S(2)}, u32[]{:S(2)}) %collective-permute-start.44) | collective-permute-done | bytes 16416 | tf_op jit(solution)/shard_map/ppermute | solution.py:196
  245.3 5.4 %collective-permute-done.45 = f32[4,2048]{1,0:T(4,128)S(1)} collective-permute-done((f32[4,2048]{1,0:T(4,128)S(1)}, f32[4,2048]{1,0:T(4,128)S(1)}, u32[]{:S(2)}, u32[]{:S(2)}) %collective-permute-start.45) | collective-permute-done | bytes 32800 | tf_op jit(solution)/shard_map/ppermute | solution.py:196
  250.8 4.3 %collective-permute-done.46 = f32[8,2048]{1,0:T(8,128)S(1)} collective-permute-done((f32[8,2048]{1,0:T(8,128)S(1)}, f32[8,2048]{1,0:T(8,128)S(1)}, u32[]{:S(2)}, u32[]{:S(2)}) %collective-permute-start.46) | collective-permute-done | bytes 65568 | tf_op jit(solution)/shard_map/ppermute | solution.py:196
  255.1 3.3 collective-permute-start.47
  258.4 3.2 collective-permute-done.47
  263.1 5.5 %collective-permute-done.48 = f32[32,2048]{1,0:T(8,128)S(1)} collective-permute-done((f32[32,2048]{1,0:T(8,128)S(1)}, f32[32,2048]{1,0:T(8,128)S(1)}, u32[]{:S(2)}, u32[]{:S(2)}) %collective-permute-start.48) | collective-permute-done | bytes 262176 | tf_op jit(solution)/shard_map/ppermute | solution.py:196
  269.4 4.1 %collective-permute-start.49 = (f32[32,4096]{1,0:T(8,128)}, f32[32,4096]{1,0:T(8,128)}, u32[]{:S(2)}, u32[]{:S(2)}) collective-permute-start(f32[32,4096]{1,0:T(8,128)} %maximum_select_fusion.4), channel_id=1, source_target_pairs={{0,2},{1,3},{2,0},{3,1},{4,6},{5,7},{6,4},{7,5},{8,10},{9,11},{10,... | collective-permute-start | bytes 1572872 | tf_op jit(solution)/shard_map/ppermute | solution.py:196
  274.2 6.8 %collective-permute-done.49 = f32[32,4096]{1,0:T(8,128)} collective-permute-done((f32[32,4096]{1,0:T(8,128)}, f32[32,4096]{1,0:T(8,128)}, u32[]{:S(2)}, u32[]{:S(2)}) %collective-permute-start.49) | collective-permute-done | bytes 524320 | tf_op jit(solution)/shard_map/ppermute | solution.py:196
  283.4 14.3 %shard_map.38 = f32[32,16,512]{2,1,0:T(8,128)} custom-call(f32[32,16,512]{2,1,0:T(8,128)} %maximum_select_fusion.1.src_ref, f32[32,16,512]{2,1,0:T(8,128)} %reshape.877.met_ref), custom_call_target="tpu_custom_call" | custom-call | tf_op jit(solution)/shard_map/pallas_call | solution.py:161
  301.8 4.5 %collective-permute-start.52 = (f32[1,4,1,32,64]{4,3,2,1,0:T(8,128)S(1)}, f32[1,4,1,32,64]{4,3,2,1,0:T(8,128)S(1)}, u32[]{:S(2)}, u32[]{:S(2)}) collective-permute-start(f32[1,4,1,32,64]{4,3,2,1,0:T(8,128)S(1)} %get-tuple-element.88), channel_id=1, source_target_pairs={{0,1},{1,2},{2,3},{4,5},{5,6},{6,7},{8,9},{9,10},{10,11},{12,13},{... | collective-permute-start | bytes 98312 | tf_op jit(solution)/shard_map/ppermute | solution.py:23
  306.4 1.9 collective-permute-start.50
  308.4 6.3 %collective-permute-done.50 = f32[1,4,2,32,64]{4,3,2,1,0:T(8,128)S(1)} collective-permute-done((f32[1,4,2,32,64]{4,3,2,1,0:T(8,128)S(1)}, f32[1,4,2,32,64]{4,3,2,1,0:T(8,128)S(1)}, u32[]{:S(2)}, u32[]{:S(2)}) %collective-permute-start.50) | collective-permute-done | bytes 65568 | tf_op jit(solution)/shard_map/ppermute | solution.py:34
  315.3 1.9 collective-permute-start.53
  318.6 4.6 %collective-permute-start.55 = (f32[1,4,1,64,128]{4,3,2,1,0:T(8,128)S(1)}, f32[1,4,1,64,128]{4,3,2,1,0:T(8,128)S(1)}, u32[]{:S(2)}, u32[]{:S(2)}) collective-permute-start(f32[1,4,1,64,128]{4,3,2,1,0:T(8,128)S(1)} %get-tuple-element.40), channel_id=1, source_target_pairs={{0,1},{1,2},{2,3},{4,5},{5,6},{6,7},{8,9},{9,10},{10,11},{12,13},{... | collective-permute-start | bytes 393224 | tf_op jit(solution)/shard_map/ppermute | solution.py:23
  325.8 2.1 collective-permute-done.53
  328.5 1.9 collective-permute-start.56
  331.7 4.6 %collective-permute-start.58 = (f32[1,4,1,64,128]{4,3,2,1,0:T(8,128)S(1)}, f32[1,4,1,64,128]{4,3,2,1,0:T(8,128)S(1)}, u32[]{:S(2)}, u32[]{:S(2)}) collective-permute-start(f32[1,4,1,64,128]{4,3,2,1,0:T(8,128)S(1)} %get-tuple-element.36), channel_id=1, source_target_pairs={{0,1},{1,2},{2,3},{4,5},{5,6},{6,7},{8,9},{9,10},{10,11},{12,13},{... | collective-permute-start | bytes 393224 | tf_op jit(solution)/shard_map/ppermute | solution.py:23
  339.0 2.1 collective-permute-done.56
  (208 shorter events, 78.5 us)
Async XLA Ops:
  1.0 10.2 %copy-start.2 = (f32[1,4,64,128]{3,2,1,0:T(8,128)S(1)}, f32[1,4,64,128]{3,2,1,0:T(8,128)}, u32[]{:S(2)}) copy-start(f32[1,4,64,128]{3,2,1,0:T(8,128)} %param.4) | copy-start | bytes 393220
  3.2 12.8 %copy-start = (f32[1,4,4,64,128]{4,3,2,1,0:T(8,128)S(1)}, f32[1,4,4,64,128]{4,3,2,1,0:T(8,128)}, u32[]{:S(2)}) copy-start(f32[1,4,4,64,128]{4,3,2,1,0:T(8,128)} %param.3) | copy-start | bytes 1572868
  3.2 12.7 %collective-permute-start = (f32[1,4,4,64,128]{4,3,2,1,0:T(8,128)S(1)}, f32[1,4,4,64,128]{4,3,2,1,0:T(8,128)S(1)}, u32[]{:S(2)}, u32[]{:S(2)}) collective-permute-start(f32[1,4,4,64,128]{4,3,2,1,0:T(8,128)S(1)} %get-tuple-element.9), channel_id=1, source_target_pairs={{0,4},{4,8},{8,12},{12,16},{16,20},{20,24},{24,28},{28,32},{32,36}... | collective-permute-start | bytes 1572872 | tf_op jit(solution)/shard_map/ppermute | solution.py:34
  5.3 7.4 %collective-permute-start.1 = (f32[1,4,1,64,128]{4,3,2,1,0:T(8,128)S(1)}, f32[1,4,1,64,128]{4,3,2,1,0:T(8,128)S(1)}, u32[]{:S(2)}, u32[]{:S(2)}) collective-permute-start(f32[1,4,1,64,128]{4,3,2,1,0:T(8,128)S(1)} %get-tuple-element.67), channel_id=1, source_target_pairs={{1,0},{2,1},{3,2},{5,4},{6,5},{7,6},{9,8},{10,9},{11,10},{13,12},{... | collective-permute-start | bytes 393224 | tf_op jit(solution)/shard_map/ppermute | solution.py:26
  6.6 7.8 %collective-permute-start.2 = (f32[1,4,1,64,128]{4,3,2,1,0:T(8,128)S(1)}, f32[1,4,1,64,128]{4,3,2,1,0:T(8,128)S(1)}, u32[]{:S(2)}, u32[]{:S(2)}) collective-permute-start(f32[1,4,1,64,128]{4,3,2,1,0:T(8,128)S(1)} %get-tuple-element.68), channel_id=1, source_target_pairs={{0,1},{1,2},{2,3},{4,5},{5,6},{6,7},{8,9},{9,10},{10,11},{12,13},{... | collective-permute-start | bytes 393224 | tf_op jit(solution)/shard_map/ppermute | solution.py:23
  16.5 12.6 %collective-permute-start.3 = (f32[1,4,4,64,128]{4,3,2,1,0:T(8,128)S(1)}, f32[1,4,4,64,128]{4,3,2,1,0:T(8,128)S(1)}, u32[]{:S(2)}, u32[]{:S(2)}) collective-permute-start(f32[1,4,4,64,128]{4,3,2,1,0:T(8,128)S(1)} %fusion.119), channel_id=1, source_target_pairs={{0,4},{4,8},{8,12},{12,16},{16,20},{20,24},{24,28},{28,32},{32,36}... | collective-permute-start | bytes 1572872 | tf_op jit(solution)/shard_map/ppermute | solution.py:34
  18.5 8.1 %collective-permute-start.4 = (f32[1,4,1,64,128]{4,3,2,1,0:T(8,128)S(1)}, f32[1,4,1,64,128]{4,3,2,1,0:T(8,128)S(1)}, u32[]{:S(2)}, u32[]{:S(2)}) collective-permute-start(f32[1,4,1,64,128]{4,3,2,1,0:T(8,128)S(1)} %get-tuple-element.63), channel_id=1, source_target_pairs={{1,0},{2,1},{3,2},{5,4},{6,5},{7,6},{9,8},{10,9},{11,10},{13,12},{... | collective-permute-start | bytes 393224 | tf_op jit(solution)/shard_map/ppermute | solution.py:26
  19.8 8.3 %collective-permute-start.5 = (f32[1,4,1,64,128]{4,3,2,1,0:T(8,128)S(1)}, f32[1,4,1,64,128]{4,3,2,1,0:T(8,128)S(1)}, u32[]{:S(2)}, u32[]{:S(2)}) collective-permute-start(f32[1,4,1,64,128]{4,3,2,1,0:T(8,128)S(1)} %get-tuple-element.64), channel_id=1, source_target_pairs={{0,1},{1,2},{2,3},{4,5},{5,6},{6,7},{8,9},{9,10},{10,11},{12,13},{... | collective-permute-start | bytes 393224 | tf_op jit(solution)/shard_map/ppermute | solution.py:23
  30.1 7.8 %collective-permute-start.7 = (f32[1,4,1,32,64]{4,3,2,1,0:T(8,128)S(1)}, f32[1,4,1,32,64]{4,3,2,1,0:T(8,128)S(1)}, u32[]{:S(2)}, u32[]{:S(2)}) collective-permute-start(f32[1,4,1,32,64]{4,3,2,1,0:T(8,128)S(1)} %get-tuple-element.107), channel_id=1, source_target_pairs={{1,0},{2,1},{3,2},{5,4},{6,5},{7,6},{9,8},{10,9},{11,10},{13,12},{... | collective-permute-start | bytes 98312 | tf_op jit(solution)/shard_map/ppermute | solution.py:26
  31.4 6.5 %collective-permute-start.8 = (f32[1,4,1,32,64]{4,3,2,1,0:T(8,128)S(1)}, f32[1,4,1,32,64]{4,3,2,1,0:T(8,128)S(1)}, u32[]{:S(2)}, u32[]{:S(2)}) collective-permute-start(f32[1,4,1,32,64]{4,3,2,1,0:T(8,128)S(1)} %get-tuple-element.108), channel_id=1, source_target_pairs={{0,1},{1,2},{2,3},{4,5},{5,6},{6,7},{8,9},{9,10},{10,11},{12,13},{... | collective-permute-start | bytes 98312 | tf_op jit(solution)/shard_map/ppermute | solution.py:23
  36.0 8.4 %collective-permute-start.6 = (f32[1,4,2,32,64]{4,3,2,1,0:T(8,128)S(1)}, f32[1,4,2,32,64]{4,3,2,1,0:T(8,128)S(1)}, u32[]{:S(2)}, u32[]{:S(2)}) collective-permute-start(f32[1,4,2,32,64]{4,3,2,1,0:T(8,128)S(1)} %fusion.388), channel_id=1, source_target_pairs={{0,4},{4,8},{8,12},{12,16},{16,20},{20,24},{24,28},{28,32},{32,36}... | collective-permute-start | bytes 196616 | tf_op jit(solution)/shard_map/ppermute | solution.py:34
  44.6 8.0 %collective-permute-start.10 = (f32[1,4,1,32,64]{4,3,2,1,0:T(8,128)S(1)}, f32[1,4,1,32,64]{4,3,2,1,0:T(8,128)S(1)}, u32[]{:S(2)}, u32[]{:S(2)}) collective-permute-start(f32[1,4,1,32,64]{4,3,2,1,0:T(8,128)S(1)} %get-tuple-element.103), channel_id=1, source_target_pairs={{1,0},{2,1},{3,2},{5,4},{6,5},{7,6},{9,8},{10,9},{11,10},{13,12},{... | collective-permute-start | bytes 98312 | tf_op jit(solution)/shard_map/ppermute | solution.py:26
  45.9 6.7 %collective-permute-start.11 = (f32[1,4,1,32,64]{4,3,2,1,0:T(8,128)S(1)}, f32[1,4,1,32,64]{4,3,2,1,0:T(8,128)S(1)}, u32[]{:S(2)}, u32[]{:S(2)}) collective-permute-start(f32[1,4,1,32,64]{4,3,2,1,0:T(8,128)S(1)} %get-tuple-element.104), channel_id=1, source_target_pairs={{0,1},{1,2},{2,3},{4,5},{5,6},{6,7},{8,9},{9,10},{10,11},{12,13},{... | collective-permute-start | bytes 98312 | tf_op jit(solution)/shard_map/ppermute | solution.py:23
  50.6 8.4 %collective-permute-start.9 = (f32[1,4,2,32,64]{4,3,2,1,0:T(8,128)S(1)}, f32[1,4,2,32,64]{4,3,2,1,0:T(8,128)S(1)}, u32[]{:S(2)}, u32[]{:S(2)}) collective-permute-start(f32[1,4,2,32,64]{4,3,2,1,0:T(8,128)S(1)} %fusion.207), channel_id=1, source_target_pairs={{0,4},{4,8},{8,12},{12,16},{16,20},{20,24},{24,28},{28,32},{32,36}... | collective-permute-start | bytes 196616 | tf_op jit(solution)/shard_map/ppermute | solution.py:34
  59.7 1.3 collective-permute-start.12
  61.0 3.9 %collective-permute-start.13 = (f32[2,2560]{1,0:T(2,128)S(1)}, f32[2,2560]{1,0:T(2,128)S(1)}, u32[]{:S(2)}, u32[]{:S(2)}) collective-permute-start(f32[2,2560]{1,0:T(2,128)S(1)} %maximum_select_fusion.15), channel_id=1, source_target_pairs={{0,8},{4,12},{8,0},{12,4},{16,24},{20,28},{24,16},{28,20},{32,40},... | collective-permute-start | bytes 61448 | tf_op jit(solution)/shard_map/ppermute | solution.py:196
  64.9 5.6 %collective-permute-start.14 = (f32[4,2560]{1,0:T(4,128)S(1)}, f32[4,2560]{1,0:T(4,128)S(1)}, u32[]{:S(2)}, u32[]{:S(2)}) collective-permute-start(f32[4,2560]{1,0:T(4,128)S(1)} %maximum_select_fusion.13), channel_id=1, source_target_pairs={{0,16},{4,20},{8,24},{12,28},{16,0},{20,4},{24,8},{28,12},{32,48},... | collective-permute-start | bytes 122888 | tf_op jit(solution)/shard_map/ppermute | solution.py:196
  70.5 4.5 %collective-permute-start.15 = (f32[8,2560]{1,0:T(8,128)S(1)}, f32[8,2560]{1,0:T(8,128)S(1)}, u32[]{:S(2)}, u32[]{:S(2)}) collective-permute-start(f32[8,2560]{1,0:T(8,128)S(1)} %maximum_select_fusion.11), channel_id=1, source_target_pairs={{0,32},{4,36},{8,40},{12,44},{16,48},{20,52},{24,56},{28,60},{32,0... | collective-permute-start | bytes 245768 | tf_op jit(solution)/shard_map/ppermute | solution.py:196
  75.0 6.9 %collective-permute-start.16 = (f32[16,2560]{1,0:T(8,128)S(1)}, f32[16,2560]{1,0:T(8,128)S(1)}, u32[]{:S(2)}, u32[]{:S(2)}) collective-permute-start(f32[16,2560]{1,0:T(8,128)S(1)} %maximum_select_fusion.8), channel_id=1, source_target_pairs={{0,64},{4,68},{8,72},{12,76},{16,80},{20,84},{24,88},{28,92},{32,9... | collective-permute-start | bytes 491528 | tf_op jit(solution)/shard_map/ppermute | solution.py:196
  82.0 8.4 %collective-permute-start.17 = (f32[32,2560]{1,0:T(8,128)S(1)}, f32[32,2560]{1,0:T(8,128)S(1)}, u32[]{:S(2)}, u32[]{:S(2)}) collective-permute-start(f32[32,2560]{1,0:T(8,128)S(1)} %maximum_select_fusion.5), channel_id=1, source_target_pairs={{0,1},{1,0},{2,3},{3,2},{4,5},{5,4},{6,7},{7,6},{8,9},{9,8},{10,11... | collective-permute-start | bytes 983048 | tf_op jit(solution)/shard_map/ppermute | solution.py:196
  90.5 5.4 %copy-start.1 = (f32[32,5120]{1,0:T(8,128)}, f32[32,5120]{1,0:T(8,128)S(1)}, u32[]{:S(2)}) copy-start(f32[32,5120]{1,0:T(8,128)S(1)} %maximum_select_fusion.2) | copy-start | bytes 1966084
  90.5 14.7 %collective-permute-start.18 = (f32[32,5120]{1,0:T(8,128)S(1)}, f32[32,5120]{1,0:T(8,128)}, u32[]{:S(2)}, u32[]{:S(2)}) collective-permute-start(f32[32,5120]{1,0:T(8,128)S(1)} %maximum_select_fusion.2), channel_id=1, source_target_pairs={{0,2},{1,3},{2,0},{3,1},{4,6},{5,7},{6,4},{7,5},{8,10},{9,11},{10,... | collective-permute-start | bytes 1966088 | tf_op jit(solution)/shard_map/ppermute | solution.py:196
  108.4 1.2 slice-start.1
  109.6 1.3 slice-start
  129.7 7.8 %collective-permute-start.20 = (f32[1,4,1,32,64]{4,3,2,1,0:T(8,128)S(1)}, f32[1,4,1,32,64]{4,3,2,1,0:T(8,128)S(1)}, u32[]{:S(2)}, u32[]{:S(2)}) collective-permute-start(f32[1,4,1,32,64]{4,3,2,1,0:T(8,128)S(1)} %get-tuple-element.99), channel_id=1, source_target_pairs={{1,0},{2,1},{3,2},{5,4},{6,5},{7,6},{9,8},{10,9},{11,10},{13,12},{... | collective-permute-start | bytes 98312 | tf_op jit(solution)/shard_map/ppermute | solution.py:26
  131.0 6.5 %collective-permute-start.21 = (f32[1,4,1,32,64]{4,3,2,1,0:T(8,128)S(1)}, f32[1,4,1,32,64]{4,3,2,1,0:T(8,128)S(1)}, u32[]{:S(2)}, u32[]{:S(2)}) collective-permute-start(f32[1,4,1,32,64]{4,3,2,1,0:T(8,128)S(1)} %get-tuple-element.100), channel_id=1, source_target_pairs={{0,1},{1,2},{2,3},{4,5},{5,6},{6,7},{8,9},{9,10},{10,11},{12,13},{... | collective-permute-start | bytes 98312 | tf_op jit(solution)/shard_map/ppermute | solution.py:23
  135.6 8.4 %collective-permute-start.19 = (f32[1,4,2,32,64]{4,3,2,1,0:T(8,128)S(1)}, f32[1,4,2,32,64]{4,3,2,1,0:T(8,128)S(1)}, u32[]{:S(2)}, u32[]{:S(2)}) collective-permute-start(f32[1,4,2,32,64]{4,3,2,1,0:T(8,128)S(1)} %fusion.221), channel_id=1, source_target_pairs={{0,4},{4,8},{8,12},{12,16},{16,20},{20,24},{24,28},{28,32},{32,36}... | collective-permute-start | bytes 196616 | tf_op jit(solution)/shard_map/ppermute | solution.py:34
  144.5 12.6 %collective-permute-start.22 = (f32[1,4,4,64,128]{4,3,2,1,0:T(8,128)S(1)}, f32[1,4,4,64,128]{4,3,2,1,0:T(8,128)S(1)}, u32[]{:S(2)}, u32[]{:S(2)}) collective-permute-start(f32[1,4,4,64,128]{4,3,2,1,0:T(8,128)S(1)} %add.517), channel_id=1, source_target_pairs={{0,4},{4,8},{8,12},{12,16},{16,20},{20,24},{24,28},{28,32},{32,36}... | collective-permute-start | bytes 1572872 | tf_op jit(solution)/shard_map/ppermute | solution.py:34
  146.4 6.9 %collective-permute-start.23 = (f32[1,4,1,64,128]{4,3,2,1,0:T(8,128)S(1)}, f32[1,4,1,64,128]{4,3,2,1,0:T(8,128)S(1)}, u32[]{:S(2)}, u32[]{:S(2)}) collective-permute-start(f32[1,4,1,64,128]{4,3,2,1,0:T(8,128)S(1)} %get-tuple-element.59), channel_id=1, source_target_pairs={{1,0},{2,1},{3,2},{5,4},{6,5},{7,6},{9,8},{10,9},{11,10},{13,12},{... | collective-permute-start | bytes 393224 | tf_op jit(solution)/shard_map/ppermute | solution.py:26
  147.7 7.1 %collective-permute-start.24 = (f32[1,4,1,64,128]{4,3,2,1,0:T(8,128)S(1)}, f32[1,4,1,64,128]{4,3,2,1,0:T(8,128)S(1)}, u32[]{:S(2)}, u32[]{:S(2)}) collective-permute-start(f32[1,4,1,64,128]{4,3,2,1,0:T(8,128)S(1)} %get-tuple-element.60), channel_id=1, source_target_pairs={{0,1},{1,2},{2,3},{4,5},{5,6},{6,7},{8,9},{9,10},{10,11},{12,13},{... | collective-permute-start | bytes 393224 | tf_op jit(solution)/shard_map/ppermute | solution.py:23
  157.7 12.6 %collective-permute-start.25 = (f32[1,4,4,64,128]{4,3,2,1,0:T(8,128)S(1)}, f32[1,4,4,64,128]{4,3,2,1,0:T(8,128)S(1)}, u32[]{:S(2)}, u32[]{:S(2)}) collective-permute-start(f32[1,4,4,64,128]{4,3,2,1,0:T(8,128)S(1)} %fusion.93), channel_id=1, source_target_pairs={{0,4},{4,8},{8,12},{12,16},{16,20},{20,24},{24,28},{28,32},{32,36}... | collective-permute-start | bytes 1572872 | tf_op jit(solution)/shard_map/ppermute | solution.py:34
  159.6 6.9 %collective-permute-start.26 = (f32[1,4,1,64,128]{4,3,2,1,0:T(8,128)S(1)}, f32[1,4,1,64,128]{4,3,2,1,0:T(8,128)S(1)}, u32[]{:S(2)}, u32[]{:S(2)}) collective-permute-start(f32[1,4,1,64,128]{4,3,2,1,0:T(8,128)S(1)} %get-tuple-element.55), channel_id=1, source_target_pairs={{1,0},{2,1},{3,2},{5,4},{6,5},{7,6},{9,8},{10,9},{11,10},{13,12},{... | collective-permute-start | bytes 393224 | tf_op jit(solution)/shard_map/ppermute | solution.py:26
  160.9 7.1 %collective-permute-start.27 = (f32[1,4,1,64,128]{4,3,2,1,0:T(8,128)S(1)}, f32[1,4,1,64,128]{4,3,2,1,0:T(8,128)S(1)}, u32[]{:S(2)}, u32[]{:S(2)}) collective-permute-start(f32[1,4,1,64,128]{4,3,2,1,0:T(8,128)S(1)} %get-tuple-element.56), channel_id=1, source_target_pairs={{0,1},{1,2},{2,3},{4,5},{5,6},{6,7},{8,9},{9,10},{10,11},{12,13},{... | collective-permute-start | bytes 393224 | tf_op jit(solution)/shard_map/ppermute | solution.py:23
  170.8 12.6 %collective-permute-start.28 = (f32[1,4,4,64,128]{4,3,2,1,0:T(8,128)S(1)}, f32[1,4,4,64,128]{4,3,2,1,0:T(8,128)S(1)}, u32[]{:S(2)}, u32[]{:S(2)}) collective-permute-start(f32[1,4,4,64,128]{4,3,2,1,0:T(8,128)S(1)} %fusion.79), channel_id=1, source_target_pairs={{0,4},{4,8},{8,12},{12,16},{16,20},{20,24},{24,28},{28,32},{32,36}... | collective-permute-start | bytes 1572872 | tf_op jit(solution)/shard_map/ppermute | solution.py:34
  172.8 6.9 %collective-permute-start.29 = (f32[1,4,1,64,128]{4,3,2,1,0:T(8,128)S(1)}, f32[1,4,1,64,128]{4,3,2,1,0:T(8,128)S(1)}, u32[]{:S(2)}, u32[]{:S(2)}) collective-permute-start(f32[1,4,1,64,128]{4,3,2,1,0:T(8,128)S(1)} %get-tuple-element.51), channel_id=1, source_target_pairs={{1,0},{2,1},{3,2},{5,4},{6,5},{7,6},{9,8},{10,9},{11,10},{13,12},{... | collective-permute-start | bytes 393224 | tf_op jit(solution)/shard_map/ppermute | solution.py:26
  174.1 7.1 %collective-permute-start.30 = (f32[1,4,1,64,128]{4,3,2,1,0:T(8,128)S(1)}, f32[1,4,1,64,128]{4,3,2,1,0:T(8,128)S(1)}, u32[]{:S(2)}, u32[]{:S(2)}) collective-permute-start(f32[1,4,1,64,128]{4,3,2,1,0:T(8,128)S(1)} %get-tuple-element.52), channel_id=1, source_target_pairs={{0,1},{1,2},{2,3},{4,5},{5,6},{6,7},{8,9},{9,10},{10,11},{12,13},{... | collective-permute-start | bytes 393224 | tf_op jit(solution)/shard_map/ppermute | solution.py:23
  184.0 12.6 %collective-permute-start.31 = (f32[1,4,4,64,128]{4,3,2,1,0:T(8,128)S(1)}, f32[1,4,4,64,128]{4,3,2,1,0:T(8,128)S(1)}, u32[]{:S(2)}, u32[]{:S(2)}) collective-permute-start(f32[1,4,4,64,128]{4,3,2,1,0:T(8,128)S(1)} %fusion.65), channel_id=1, source_target_pairs={{0,4},{4,8},{8,12},{12,16},{16,20},{20,24},{24,28},{28,32},{32,36}... | collective-permute-start | bytes 1572872 | tf_op jit(solution)/shard_map/ppermute | solution.py:34
  185.9 6.9 %collective-permute-start.32 = (f32[1,4,1,64,128]{4,3,2,1,0:T(8,128)S(1)}, f32[1,4,1,64,128]{4,3,2,1,0:T(8,128)S(1)}, u32[]{:S(2)}, u32[]{:S(2)}) collective-permute-start(f32[1,4,1,64,128]{4,3,2,1,0:T(8,128)S(1)} %get-tuple-element.47), channel_id=1, source_target_pairs={{1,0},{2,1},{3,2},{5,4},{6,5},{7,6},{9,8},{10,9},{11,10},{13,12},{... | collective-permute-start | bytes 393224 | tf_op jit(solution)/shard_map/ppermute | solution.py:26
  187.2 7.1 %collective-permute-start.33 = (f32[1,4,1,64,128]{4,3,2,1,0:T(8,128)S(1)}, f32[1,4,1,64,128]{4,3,2,1,0:T(8,128)S(1)}, u32[]{:S(2)}, u32[]{:S(2)}) collective-permute-start(f32[1,4,1,64,128]{4,3,2,1,0:T(8,128)S(1)} %get-tuple-element.48), channel_id=1, source_target_pairs={{0,1},{1,2},{2,3},{4,5},{5,6},{6,7},{8,9},{9,10},{10,11},{12,13},{... | collective-permute-start | bytes 393224 | tf_op jit(solution)/shard_map/ppermute | solution.py:23
  197.1 12.6 %collective-permute-start.34 = (f32[1,4,4,64,128]{4,3,2,1,0:T(8,128)S(1)}, f32[1,4,4,64,128]{4,3,2,1,0:T(8,128)S(1)}, u32[]{:S(2)}, u32[]{:S(2)}) collective-permute-start(f32[1,4,4,64,128]{4,3,2,1,0:T(8,128)S(1)} %fusion.51), channel_id=1, source_target_pairs={{0,4},{4,8},{8,12},{12,16},{16,20},{20,24},{24,28},{28,32},{32,36}... | collective-permute-start | bytes 1572872 | tf_op jit(solution)/shard_map/ppermute | solution.py:34
  199.1 6.9 %collective-permute-start.35 = (f32[1,4,1,64,128]{4,3,2,1,0:T(8,128)S(1)}, f32[1,4,1,64,128]{4,3,2,1,0:T(8,128)S(1)}, u32[]{:S(2)}, u32[]{:S(2)}) collective-permute-start(f32[1,4,1,64,128]{4,3,2,1,0:T(8,128)S(1)} %get-tuple-element.43), channel_id=1, source_target_pairs={{1,0},{2,1},{3,2},{5,4},{6,5},{7,6},{9,8},{10,9},{11,10},{13,12},{... | collective-permute-start | bytes 393224 | tf_op jit(solution)/shard_map/ppermute | solution.py:26
  200.4 7.1 %collective-permute-start.36 = (f32[1,4,1,64,128]{4,3,2,1,0:T(8,128)S(1)}, f32[1,4,1,64,128]{4,3,2,1,0:T(8,128)S(1)}, u32[]{:S(2)}, u32[]{:S(2)}) collective-permute-start(f32[1,4,1,64,128]{4,3,2,1,0:T(8,128)S(1)} %get-tuple-element.44), channel_id=1, source_target_pairs={{0,1},{1,2},{2,3},{4,5},{5,6},{6,7},{8,9},{9,10},{10,11},{12,13},{... | collective-permute-start | bytes 393224 | tf_op jit(solution)/shard_map/ppermute | solution.py:23
  210.7 7.8 %collective-permute-start.38 = (f32[1,4,1,32,64]{4,3,2,1,0:T(8,128)S(1)}, f32[1,4,1,32,64]{4,3,2,1,0:T(8,128)S(1)}, u32[]{:S(2)}, u32[]{:S(2)}) collective-permute-start(f32[1,4,1,32,64]{4,3,2,1,0:T(8,128)S(1)} %get-tuple-element.95), channel_id=1, source_target_pairs={{1,0},{2,1},{3,2},{5,4},{6,5},{7,6},{9,8},{10,9},{11,10},{13,12},{... | collective-permute-start | bytes 98312 | tf_op jit(solution)/shard_map/ppermute | solution.py:26
  212.0 6.5 %collective-permute-start.39 = (f32[1,4,1,32,64]{4,3,2,1,0:T(8,128)S(1)}, f32[1,4,1,32,64]{4,3,2,1,0:T(8,128)S(1)}, u32[]{:S(2)}, u32[]{:S(2)}) collective-permute-start(f32[1,4,1,32,64]{4,3,2,1,0:T(8,128)S(1)} %get-tuple-element.96), channel_id=1, source_target_pairs={{0,1},{1,2},{2,3},{4,5},{5,6},{6,7},{8,9},{9,10},{10,11},{12,13},{... | collective-permute-start | bytes 98312 | tf_op jit(solution)/shard_map/ppermute | solution.py:23
  216.6 8.4 %collective-permute-start.37 = (f32[1,4,2,32,64]{4,3,2,1,0:T(8,128)S(1)}, f32[1,4,2,32,64]{4,3,2,1,0:T(8,128)S(1)}, u32[]{:S(2)}, u32[]{:S(2)}) collective-permute-start(f32[1,4,2,32,64]{4,3,2,1,0:T(8,128)S(1)} %fusion.389), channel_id=1, source_target_pairs={{0,4},{4,8},{8,12},{12,16},{16,20},{20,24},{24,28},{28,32},{32,36}... | collective-permute-start | bytes 196616 | tf_op jit(solution)/shard_map/ppermute | solution.py:34
  225.1 7.8 %collective-permute-start.41 = (f32[1,4,1,32,64]{4,3,2,1,0:T(8,128)S(1)}, f32[1,4,1,32,64]{4,3,2,1,0:T(8,128)S(1)}, u32[]{:S(2)}, u32[]{:S(2)}) collective-permute-start(f32[1,4,1,32,64]{4,3,2,1,0:T(8,128)S(1)} %get-tuple-element.91), channel_id=1, source_target_pairs={{1,0},{2,1},{3,2},{5,4},{6,5},{7,6},{9,8},{10,9},{11,10},{13,12},{... | collective-permute-start | bytes 98312 | tf_op jit(solution)/shard_map/ppermute | solution.py:26
  226.4 6.5 %collective-permute-start.42 = (f32[1,4,1,32,64]{4,3,2,1,0:T(8,128)S(1)}, f32[1,4,1,32,64]{4,3,2,1,0:T(8,128)S(1)}, u32[]{:S(2)}, u32[]{:S(2)}) collective-permute-start(f32[1,4,1,32,64]{4,3,2,1,0:T(8,128)S(1)} %get-tuple-element.92), channel_id=1, source_target_pairs={{0,1},{1,2},{2,3},{4,5},{5,6},{6,7},{8,9},{9,10},{10,11},{12,13},{... | collective-permute-start | bytes 98312 | tf_op jit(solution)/shard_map/ppermute | solution.py:23
  231.0 8.4 %collective-permute-start.40 = (f32[1,4,2,32,64]{4,3,2,1,0:T(8,128)S(1)}, f32[1,4,2,32,64]{4,3,2,1,0:T(8,128)S(1)}, u32[]{:S(2)}, u32[]{:S(2)}) collective-permute-start(f32[1,4,2,32,64]{4,3,2,1,0:T(8,128)S(1)} %fusion.166), channel_id=1, source_target_pairs={{0,4},{4,8},{8,12},{12,16},{16,20},{20,24},{24,28},{28,32},{32,36}... | collective-permute-start | bytes 196616 | tf_op jit(solution)/shard_map/ppermute | solution.py:34
  240.0 1.3 collective-permute-start.43
  241.3 3.8 %collective-permute-start.44 = (f32[2,2048]{1,0:T(2,128)S(1)}, f32[2,2048]{1,0:T(2,128)S(1)}, u32[]{:S(2)}, u32[]{:S(2)}) collective-permute-start(f32[2,2048]{1,0:T(2,128)S(1)} %maximum_select_fusion.16), channel_id=1, source_target_pairs={{0,8},{4,12},{8,0},{12,4},{16,24},{20,28},{24,16},{28,20},{32,40},... | collective-permute-start | bytes 49160 | tf_op jit(solution)/shard_map/ppermute | solution.py:196
  245.2 5.5 %collective-permute-start.45 = (f32[4,2048]{1,0:T(4,128)S(1)}, f32[4,2048]{1,0:T(4,128)S(1)}, u32[]{:S(2)}, u32[]{:S(2)}) collective-permute-start(f32[4,2048]{1,0:T(4,128)S(1)} %maximum_select_fusion.14), channel_id=1, source_target_pairs={{0,16},{4,20},{8,24},{12,28},{16,0},{20,4},{24,8},{28,12},{32,48},... | collective-permute-start | bytes 98312 | tf_op jit(solution)/shard_map/ppermute | solution.py:196
  250.7 4.3 %collective-permute-start.46 = (f32[8,2048]{1,0:T(8,128)S(1)}, f32[8,2048]{1,0:T(8,128)S(1)}, u32[]{:S(2)}, u32[]{:S(2)}) collective-permute-start(f32[8,2048]{1,0:T(8,128)S(1)} %maximum_select_fusion.12), channel_id=1, source_target_pairs={{0,32},{4,36},{8,40},{12,44},{16,48},{20,52},{24,56},{28,60},{32,0... | collective-permute-start | bytes 196616 | tf_op jit(solution)/shard_map/ppermute | solution.py:196
  255.1 6.6 %collective-permute-start.47 = (f32[16,2048]{1,0:T(8,128)S(1)}, f32[16,2048]{1,0:T(8,128)S(1)}, u32[]{:S(2)}, u32[]{:S(2)}) collective-permute-start(f32[16,2048]{1,0:T(8,128)S(1)} %maximum_select_fusion.10), channel_id=1, source_target_pairs={{0,64},{4,68},{8,72},{12,76},{16,80},{20,84},{24,88},{28,92},{32,9... | collective-permute-start | bytes 393224 | tf_op jit(solution)/shard_map/ppermute | solution.py:196
  261.6 7.0 %collective-permute-start.48 = (f32[32,2048]{1,0:T(8,128)S(1)}, f32[32,2048]{1,0:T(8,128)S(1)}, u32[]{:S(2)}, u32[]{:S(2)}) collective-permute-start(f32[32,2048]{1,0:T(8,128)S(1)} %maximum_select_fusion.7), channel_id=1, source_target_pairs={{0,1},{1,0},{2,3},{3,2},{4,5},{5,4},{6,7},{7,6},{8,9},{9,8},{10,11... | collective-permute-start | bytes 786440 | tf_op jit(solution)/shard_map/ppermute | solution.py:196
  269.4 11.6 %collective-permute-start.49 = (f32[32,4096]{1,0:T(8,128)}, f32[32,4096]{1,0:T(8,128)}, u32[]{:S(2)}, u32[]{:S(2)}) collective-permute-start(f32[32,4096]{1,0:T(8,128)} %maximum_select_fusion.4), channel_id=1, source_target_pairs={{0,2},{1,3},{2,0},{3,1},{4,6},{5,7},{6,4},{7,5},{8,10},{9,11},{10,... | collective-permute-start | bytes 1572872 | tf_op jit(solution)/shard_map/ppermute | solution.py:196
  300.5 7.8 %collective-permute-start.51 = (f32[1,4,1,32,64]{4,3,2,1,0:T(8,128)S(1)}, f32[1,4,1,32,64]{4,3,2,1,0:T(8,128)S(1)}, u32[]{:S(2)}, u32[]{:S(2)}) collective-permute-start(f32[1,4,1,32,64]{4,3,2,1,0:T(8,128)S(1)} %get-tuple-element.87), channel_id=1, source_target_pairs={{1,0},{2,1},{3,2},{5,4},{6,5},{7,6},{9,8},{10,9},{11,10},{13,12},{... | collective-permute-start | bytes 98312 | tf_op jit(solution)/shard_map/ppermute | solution.py:26
  301.8 6.5 %collective-permute-start.52 = (f32[1,4,1,32,64]{4,3,2,1,0:T(8,128)S(1)}, f32[1,4,1,32,64]{4,3,2,1,0:T(8,128)S(1)}, u32[]{:S(2)}, u32[]{:S(2)}) collective-permute-start(f32[1,4,1,32,64]{4,3,2,1,0:T(8,128)S(1)} %get-tuple-element.88), channel_id=1, source_target_pairs={{0,1},{1,2},{2,3},{4,5},{5,6},{6,7},{8,9},{9,10},{10,11},{12,13},{... | collective-permute-start | bytes 98312 | tf_op jit(solution)/shard_map/ppermute | solution.py:23
  306.4 8.4 %collective-permute-start.50 = (f32[1,4,2,32,64]{4,3,2,1,0:T(8,128)S(1)}, f32[1,4,2,32,64]{4,3,2,1,0:T(8,128)S(1)}, u32[]{:S(2)}, u32[]{:S(2)}) collective-permute-start(f32[1,4,2,32,64]{4,3,2,1,0:T(8,128)S(1)} %fusion.233), channel_id=1, source_target_pairs={{0,4},{4,8},{8,12},{12,16},{16,20},{20,24},{24,28},{28,32},{32,36}... | collective-permute-start | bytes 196616 | tf_op jit(solution)/shard_map/ppermute | solution.py:34
  315.3 12.6 %collective-permute-start.53 = (f32[1,4,4,64,128]{4,3,2,1,0:T(8,128)S(1)}, f32[1,4,4,64,128]{4,3,2,1,0:T(8,128)S(1)}, u32[]{:S(2)}, u32[]{:S(2)}) collective-permute-start(f32[1,4,4,64,128]{4,3,2,1,0:T(8,128)S(1)} %add.567), channel_id=1, source_target_pairs={{0,4},{4,8},{8,12},{12,16},{16,20},{20,24},{24,28},{28,32},{32,36}... | collective-permute-start | bytes 1572872 | tf_op jit(solution)/shard_map/ppermute | solution.py:34
  317.3 6.9 %collective-permute-start.54 = (f32[1,4,1,64,128]{4,3,2,1,0:T(8,128)S(1)}, f32[1,4,1,64,128]{4,3,2,1,0:T(8,128)S(1)}, u32[]{:S(2)}, u32[]{:S(2)}) collective-permute-start(f32[1,4,1,64,128]{4,3,2,1,0:T(8,128)S(1)} %get-tuple-element.39), channel_id=1, source_target_pairs={{1,0},{2,1},{3,2},{5,4},{6,5},{7,6},{9,8},{10,9},{11,10},{13,12},{... | collective-permute-start | bytes 393224 | tf_op jit(solution)/shard_map/ppermute | solution.py:26
  318.6 7.1 %collective-permute-start.55 = (f32[1,4,1,64,128]{4,3,2,1,0:T(8,128)S(1)}, f32[1,4,1,64,128]{4,3,2,1,0:T(8,128)S(1)}, u32[]{:S(2)}, u32[]{:S(2)}) collective-permute-start(f32[1,4,1,64,128]{4,3,2,1,0:T(8,128)S(1)} %get-tuple-element.40), channel_id=1, source_target_pairs={{0,1},{1,2},{2,3},{4,5},{5,6},{6,7},{8,9},{9,10},{10,11},{12,13},{... | collective-permute-start | bytes 393224 | tf_op jit(solution)/shard_map/ppermute | solution.py:23
  328.5 12.6 %collective-permute-start.56 = (f32[1,4,4,64,128]{4,3,2,1,0:T(8,128)S(1)}, f32[1,4,4,64,128]{4,3,2,1,0:T(8,128)S(1)}, u32[]{:S(2)}, u32[]{:S(2)}) collective-permute-start(f32[1,4,4,64,128]{4,3,2,1,0:T(8,128)S(1)} %fusion.25), channel_id=1, source_target_pairs={{0,4},{4,8},{8,12},{12,16},{16,20},{20,24},{24,28},{28,32},{32,36}... | collective-permute-start | bytes 1572872 | tf_op jit(solution)/shard_map/ppermute | solution.py:34
  330.4 6.9 %collective-permute-start.57 = (f32[1,4,1,64,128]{4,3,2,1,0:T(8,128)S(1)}, f32[1,4,1,64,128]{4,3,2,1,0:T(8,128)S(1)}, u32[]{:S(2)}, u32[]{:S(2)}) collective-permute-start(f32[1,4,1,64,128]{4,3,2,1,0:T(8,128)S(1)} %get-tuple-element.35), channel_id=1, source_target_pairs={{1,0},{2,1},{3,2},{5,4},{6,5},{7,6},{9,8},{10,9},{11,10},{13,12},{... | collective-permute-start | bytes 393224 | tf_op jit(solution)/shard_map/ppermute | solution.py:26
  331.7 7.1 %collective-permute-start.58 = (f32[1,4,1,64,128]{4,3,2,1,0:T(8,128)S(1)}, f32[1,4,1,64,128]{4,3,2,1,0:T(8,128)S(1)}, u32[]{:S(2)}, u32[]{:S(2)}) collective-permute-start(f32[1,4,1,64,128]{4,3,2,1,0:T(8,128)S(1)} %get-tuple-element.36), channel_id=1, source_target_pairs={{0,1},{1,2},{2,3},{4,5},{5,6},{6,7},{8,9},{9,10},{10,11},{12,13},{... | collective-permute-start | bytes 393224 | tf_op jit(solution)/shard_map/ppermute | solution.py:23

commit v15 on v14

--- a/solution.py
+++ b/solution.py
@@ -205,8 +205,8 @@
 
 
 def gather_all(flat):
-    across = gather_doubling(flat, "tm", 0)
-    whole = gather_doubling(across, "space", 1)
+    across = gather_doubling(flat, "space", 1)
+    whole = gather_doubling(across, "tm", 0)
     return whole.reshape(-1, flat.shape[1])
 
 

time: 346 us -> 344 us (level)
  no operation moved by 1% of the time
where the time goes in v15:
time: 344 us; the launch traced here: 342 us
  waiting for transfers between devices  146 us (42%)
  starting transfers between devices  135 us (39%)
  Pallas kernels  28.5 us (8%)
  other arithmetic  16.4 us (5%)
  local copies, waits for them, and re-layouts  12.3 us (4%)
    ppermute x15, starting transfers between devices, with_halo(): lax.ppermute(lax.slice_in_dim(block, block.shape[dim] - width, None, axis...  68.3 us
    ppermute x14, waiting for transfers between devices, gather_doubling(): other = lax.ppermute(gathered, axis, [(i, i ^ step) for i in range(size)])  67.4 us
    ppermute x15, waiting for transfers between devices, from_behind(): return lax.ppermute(array, axis, pairs)  54.6 us
    ppermute x15, starting transfers between devices, from_behind(): return lax.ppermute(array, axis, pairs)  29.1 us
    pallas_call x2, Pallas kernels, coarse_solve(): pl.pallas_call(kernel, out_shape=jax.ShapeDtypeStruct(flat_source.shape,...  28.5 us
    ppermute x15, starting transfers between devices, with_halo(): lax.ppermute(lax.slice_in_dim(block, 0, width, axis=dim), axis, backward)  19.4 us
    ppermute x14, starting transfers between devices, gather_doubling(): other = lax.ppermute(gathered, axis, [(i, i ^ step) for i in range(size)])  18.1 us
    ppermute x15, waiting for transfers between devices, with_halo(): lax.ppermute(lax.slice_in_dim(block, block.shape[dim] - width, None, axis...  13.4 us
  transfers between devices with their start and end apart: 59, of which 47 were waited for; matrix products, arithmetic and copies ran while one was open for 1% of the time, Pallas kernels for 0%

profile of v15, /device:TPU:2, one launch (start us, length us, event | category | flops | bytes accessed | tf_op | source)
XLA Modules:
  0.0 342.1 jit_solution(2535762562262571286)
XLA Ops:
  3.2 2.1 collective-permute-start
  6.6 4.6 %collective-permute-start.2 = (f32[1,4,1,64,128]{4,3,2,1,0:T(8,128)S(1)}, f32[1,4,1,64,128]{4,3,2,1,0:T(8,128)S(1)}, u32[]{:S(2)}, u32[]{:S(2)}) collective-permute-start(f32[1,4,1,64,128]{4,3,2,1,0:T(8,128)S(1)} %get-tuple-element.68), channel_id=1, source_target_pairs={{0,1},{1,2},{2,3},{4,5},{5,6},{6,7},{8,9},{9,10},{10,11},{12,13},{... | collective-permute-start | bytes 393224 | tf_op jit(solution)/shard_map/ppermute | solution.py:23
  12.7 1.7 collective-permute-done.2
  16.5 1.9 collective-permute-start.3
  19.8 4.6 %collective-permute-start.5 = (f32[1,4,1,64,128]{4,3,2,1,0:T(8,128)S(1)}, f32[1,4,1,64,128]{4,3,2,1,0:T(8,128)S(1)}, u32[]{:S(2)}, u32[]{:S(2)}) collective-permute-start(f32[1,4,1,64,128]{4,3,2,1,0:T(8,128)S(1)} %get-tuple-element.64), channel_id=1, source_target_pairs={{0,1},{1,2},{2,3},{4,5},{5,6},{6,7},{8,9},{9,10},{10,11},{12,13},{... | collective-permute-start | bytes 393224 | tf_op jit(solution)/shard_map/ppermute | solution.py:23
  24.4 2.2 collective-permute-done.4
  31.4 4.5 %collective-permute-start.8 = (f32[1,4,1,32,64]{4,3,2,1,0:T(8,128)S(1)}, f32[1,4,1,32,64]{4,3,2,1,0:T(8,128)S(1)}, u32[]{:S(2)}, u32[]{:S(2)}) collective-permute-start(f32[1,4,1,32,64]{4,3,2,1,0:T(8,128)S(1)} %get-tuple-element.108), channel_id=1, source_target_pairs={{0,1},{1,2},{2,3},{4,5},{5,6},{6,7},{8,9},{9,10},{10,11},{12,13},{... | collective-permute-start | bytes 98312 | tf_op jit(solution)/shard_map/ppermute | solution.py:23
  36.0 1.9 collective-permute-start.6
  38.1 6.3 %collective-permute-done.6 = f32[1,4,2,32,64]{4,3,2,1,0:T(8,128)S(1)} collective-permute-done((f32[1,4,2,32,64]{4,3,2,1,0:T(8,128)S(1)}, f32[1,4,2,32,64]{4,3,2,1,0:T(8,128)S(1)}, u32[]{:S(2)}, u32[]{:S(2)}) %collective-permute-start.6) | collective-permute-done | bytes 65568 | tf_op jit(solution)/shard_map/ppermute | solution.py:34
  45.9 4.5 %collective-permute-start.11 = (f32[1,4,1,32,64]{4,3,2,1,0:T(8,128)S(1)}, f32[1,4,1,32,64]{4,3,2,1,0:T(8,128)S(1)}, u32[]{:S(2)}, u32[]{:S(2)}) collective-permute-start(f32[1,4,1,32,64]{4,3,2,1,0:T(8,128)S(1)} %get-tuple-element.104), channel_id=1, source_target_pairs={{0,1},{1,2},{2,3},{4,5},{5,6},{6,7},{8,9},{9,10},{10,11},{12,13},{... | collective-permute-start | bytes 98312 | tf_op jit(solution)/shard_map/ppermute | solution.py:23
  50.6 1.9 collective-permute-start.9
  52.7 6.3 %collective-permute-done.9 = f32[1,4,2,32,64]{4,3,2,1,0:T(8,128)S(1)} collective-permute-done((f32[1,4,2,32,64]{4,3,2,1,0:T(8,128)S(1)}, f32[1,4,2,32,64]{4,3,2,1,0:T(8,128)S(1)}, u32[]{:S(2)}, u32[]{:S(2)}) %collective-permute-start.9) | collective-permute-done | bytes 65568 | tf_op jit(solution)/shard_map/ppermute | solution.py:34
  59.7 2.0 collective-permute-start.12
  63.5 4.0 %collective-permute-start.13 = (f32[1,5120]{1,0:T(1,128)S(1)}, f32[1,5120]{1,0:T(1,128)S(1)}, u32[]{:S(2)}, u32[]{:S(2)}) collective-permute-start(f32[1,5120]{1,0:T(1,128)S(1)} %broadcast_select_fusion.2), channel_id=1, source_target_pairs={{0,2},{1,3},{2,0},{3,1},{4,6},{5,7},{6,4},{7,5},{8,10},{9,11},{10,... | collective-permute-start | bytes 61448 | tf_op jit(solution)/shard_map/ppermute | solution.py:196
  67.5 1.7 collective-permute-done.13
  70.8 4.5 %collective-permute-done.15 = f32[2,10240]{1,0:T(2,128)S(1)} collective-permute-done((f32[2,10240]{1,0:T(2,128)S(1)}, f32[2,10240]{1,0:T(2,128)S(1)}, u32[]{:S(2)}, u32[]{:S(2)}) %collective-permute-start.15) | collective-permute-done | bytes 81952 | tf_op jit(solution)/shard_map/ppermute | solution.py:196
  75.5 6.9 %collective-permute-done.16 = f32[4,10240]{1,0:T(4,128)S(1)} collective-permute-done((f32[4,10240]{1,0:T(4,128)S(1)}, f32[4,10240]{1,0:T(4,128)S(1)}, u32[]{:S(2)}, u32[]{:S(2)}) %collective-permute-start.16) | collective-permute-done | bytes 163872 | tf_op jit(solution)/shard_map/ppermute | solution.py:196
  82.6 8.0 %collective-permute-done.17 = f32[8,10240]{1,0:T(8,128)S(1)} collective-permute-done((f32[8,10240]{1,0:T(8,128)S(1)}, f32[8,10240]{1,0:T(8,128)S(1)}, u32[]{:S(2)}, u32[]{:S(2)}) %collective-permute-start.17) | collective-permute-done | bytes 327712 | tf_op jit(solution)/shard_map/ppermute | solution.py:196
  90.7 2.5 collective-permute-start.18
  93.2 13.4 %collective-permute-done.18 = f32[16,10240]{1,0:T(8,128)} collective-permute-done((f32[16,10240]{1,0:T(8,128)S(1)}, f32[16,10240]{1,0:T(8,128)}, u32[]{:S(2)}, u32[]{:S(2)}) %collective-permute-start.18) | collective-permute-done | bytes 655392 | tf_op jit(solution)/shard_map/ppermute | solution.py:196
  106.6 1.8 maximum_select_fusion
  114.1 14.2 %shard_map.37 = f32[32,16,512]{2,1,0:T(8,128)} custom-call(f32[32,16,512]{2,1,0:T(8,128)} %reshape_transpose_reshape.7.src_ref, f32[32,16,512]{2,1,0:T(8,128)} %reshape.1321.met_ref), custom_call_target="tpu_custom_call" | custom-call | tf_op jit(solution)/shard_map/pallas_call | solution.py:161
  132.4 4.5 %collective-permute-start.21 = (f32[1,4,1,32,64]{4,3,2,1,0:T(8,128)S(1)}, f32[1,4,1,32,64]{4,3,2,1,0:T(8,128)S(1)}, u32[]{:S(2)}, u32[]{:S(2)}) collective-permute-start(f32[1,4,1,32,64]{4,3,2,1,0:T(8,128)S(1)} %get-tuple-element.100), channel_id=1, source_target_pairs={{0,1},{1,2},{2,3},{4,5},{5,6},{6,7},{8,9},{9,10},{10,11},{12,13},{... | collective-permute-start | bytes 98312 | tf_op jit(solution)/shard_map/ppermute | solution.py:23
  137.0 1.9 collective-permute-start.19
  139.0 6.3 %collective-permute-done.19 = f32[1,4,2,32,64]{4,3,2,1,0:T(8,128)S(1)} collective-permute-done((f32[1,4,2,32,64]{4,3,2,1,0:T(8,128)S(1)}, f32[1,4,2,32,64]{4,3,2,1,0:T(8,128)S(1)}, u32[]{:S(2)}, u32[]{:S(2)}) %collective-permute-start.19) | collective-permute-done | bytes 65568 | tf_op jit(solution)/shard_map/ppermute | solution.py:34
  145.9 1.9 collective-permute-start.22
  149.2 4.6 %collective-permute-start.24 = (f32[1,4,1,64,128]{4,3,2,1,0:T(8,128)S(1)}, f32[1,4,1,64,128]{4,3,2,1,0:T(8,128)S(1)}, u32[]{:S(2)}, u32[]{:S(2)}) collective-permute-start(f32[1,4,1,64,128]{4,3,2,1,0:T(8,128)S(1)} %get-tuple-element.60), channel_id=1, source_target_pairs={{0,1},{1,2},{2,3},{4,5},{5,6},{6,7},{8,9},{9,10},{10,11},{12,13},{... | collective-permute-start | bytes 393224 | tf_op jit(solution)/shard_map/ppermute | solution.py:23
  156.4 2.1 collective-permute-done.22
  159.1 1.9 collective-permute-start.25
  162.3 4.6 %collective-permute-start.27 = (f32[1,4,1,64,128]{4,3,2,1,0:T(8,128)S(1)}, f32[1,4,1,64,128]{4,3,2,1,0:T(8,128)S(1)}, u32[]{:S(2)}, u32[]{:S(2)}) collective-permute-start(f32[1,4,1,64,128]{4,3,2,1,0:T(8,128)S(1)} %get-tuple-element.56), channel_id=1, source_target_pairs={{0,1},{1,2},{2,3},{4,5},{5,6},{6,7},{8,9},{9,10},{10,11},{12,13},{... | collective-permute-start | bytes 393224 | tf_op jit(solution)/shard_map/ppermute | solution.py:23
  169.6 2.1 collective-permute-done.25
  172.2 2.1 collective-permute-start.28
  175.7 4.6 %collective-permute-start.30 = (f32[1,4,1,64,128]{4,3,2,1,0:T(8,128)S(1)}, f32[1,4,1,64,128]{4,3,2,1,0:T(8,128)S(1)}, u32[]{:S(2)}, u32[]{:S(2)}) collective-permute-start(f32[1,4,1,64,128]{4,3,2,1,0:T(8,128)S(1)} %get-tuple-element.52), channel_id=1, source_target_pairs={{0,1},{1,2},{2,3},{4,5},{5,6},{6,7},{8,9},{9,10},{10,11},{12,13},{... | collective-permute-start | bytes 393224 | tf_op jit(solution)/shard_map/ppermute | solution.py:23
  182.9 1.9 collective-permute-done.28
  185.4 1.9 collective-permute-start.31
  188.7 4.6 %collective-permute-start.33 = (f32[1,4,1,64,128]{4,3,2,1,0:T(8,128)S(1)}, f32[1,4,1,64,128]{4,3,2,1,0:T(8,128)S(1)}, u32[]{:S(2)}, u32[]{:S(2)}) collective-permute-start(f32[1,4,1,64,128]{4,3,2,1,0:T(8,128)S(1)} %get-tuple-element.48), channel_id=1, source_target_pairs={{0,1},{1,2},{2,3},{4,5},{5,6},{6,7},{8,9},{9,10},{10,11},{12,13},{... | collective-permute-start | bytes 393224 | tf_op jit(solution)/shard_map/ppermute | solution.py:23
  195.9 2.1 collective-permute-done.31
  198.6 1.9 collective-permute-start.34
  201.8 4.6 %collective-permute-start.36 = (f32[1,4,1,64,128]{4,3,2,1,0:T(8,128)S(1)}, f32[1,4,1,64,128]{4,3,2,1,0:T(8,128)S(1)}, u32[]{:S(2)}, u32[]{:S(2)}) collective-permute-start(f32[1,4,1,64,128]{4,3,2,1,0:T(8,128)S(1)} %get-tuple-element.44), channel_id=1, source_target_pairs={{0,1},{1,2},{2,3},{4,5},{5,6},{6,7},{8,9},{9,10},{10,11},{12,13},{... | collective-permute-start | bytes 393224 | tf_op jit(solution)/shard_map/ppermute | solution.py:23
  209.1 2.1 collective-permute-done.34
  213.4 4.5 %collective-permute-start.39 = (f32[1,4,1,32,64]{4,3,2,1,0:T(8,128)S(1)}, f32[1,4,1,32,64]{4,3,2,1,0:T(8,128)S(1)}, u32[]{:S(2)}, u32[]{:S(2)}) collective-permute-start(f32[1,4,1,32,64]{4,3,2,1,0:T(8,128)S(1)} %get-tuple-element.96), channel_id=1, source_target_pairs={{0,1},{1,2},{2,3},{4,5},{5,6},{6,7},{8,9},{9,10},{10,11},{12,13},{... | collective-permute-start | bytes 98312 | tf_op jit(solution)/shard_map/ppermute | solution.py:23
  218.0 1.9 collective-permute-start.37
  220.1 6.3 %collective-permute-done.37 = f32[1,4,2,32,64]{4,3,2,1,0:T(8,128)S(1)} collective-permute-done((f32[1,4,2,32,64]{4,3,2,1,0:T(8,128)S(1)}, f32[1,4,2,32,64]{4,3,2,1,0:T(8,128)S(1)}, u32[]{:S(2)}, u32[]{:S(2)}) %collective-permute-start.37) | collective-permute-done | bytes 65568 | tf_op jit(solution)/shard_map/ppermute | solution.py:34
  227.9 4.5 %collective-permute-start.42 = (f32[1,4,1,32,64]{4,3,2,1,0:T(8,128)S(1)}, f32[1,4,1,32,64]{4,3,2,1,0:T(8,128)S(1)}, u32[]{:S(2)}, u32[]{:S(2)}) collective-permute-start(f32[1,4,1,32,64]{4,3,2,1,0:T(8,128)S(1)} %get-tuple-element.92), channel_id=1, source_target_pairs={{0,1},{1,2},{2,3},{4,5},{5,6},{6,7},{8,9},{9,10},{10,11},{12,13},{... | collective-permute-start | bytes 98312 | tf_op jit(solution)/shard_map/ppermute | solution.py:23
  232.4 1.9 collective-permute-start.40
  234.5 6.3 %collective-permute-done.40 = f32[1,4,2,32,64]{4,3,2,1,0:T(8,128)S(1)} collective-permute-done((f32[1,4,2,32,64]{4,3,2,1,0:T(8,128)S(1)}, f32[1,4,2,32,64]{4,3,2,1,0:T(8,128)S(1)}, u32[]{:S(2)}, u32[]{:S(2)}) %collective-permute-start.40) | collective-permute-done | bytes 65568 | tf_op jit(solution)/shard_map/ppermute | solution.py:34
  243.2 2.0 collective-permute-done.43
  245.2 3.6 %collective-permute-start.44 = (f32[1,4096]{1,0:T(1,128)S(1)}, f32[1,4096]{1,0:T(1,128)S(1)}, u32[]{:S(2)}, u32[]{:S(2)}) collective-permute-start(f32[1,4096]{1,0:T(1,128)S(1)} %broadcast_select_fusion.3), channel_id=1, source_target_pairs={{0,2},{1,3},{2,0},{3,1},{4,6},{5,7},{6,4},{7,5},{8,10},{9,11},{10,... | collective-permute-start | bytes 49160 | tf_op jit(solution)/shard_map/ppermute | solution.py:196
  248.8 1.7 collective-permute-done.44
  252.1 4.3 %collective-permute-done.46 = f32[2,8192]{1,0:T(2,128)S(1)} collective-permute-done((f32[2,8192]{1,0:T(2,128)S(1)}, f32[2,8192]{1,0:T(2,128)S(1)}, u32[]{:S(2)}, u32[]{:S(2)}) %collective-permute-start.46) | collective-permute-done | bytes 65568 | tf_op jit(solution)/shard_map/ppermute | solution.py:196
  256.5 6.5 %collective-permute-done.47 = f32[4,8192]{1,0:T(4,128)S(1)} collective-permute-done((f32[4,8192]{1,0:T(4,128)S(1)}, f32[4,8192]{1,0:T(4,128)S(1)}, u32[]{:S(2)}, u32[]{:S(2)}) %collective-permute-start.47) | collective-permute-done | bytes 131104 | tf_op jit(solution)/shard_map/ppermute | solution.py:196
  263.2 6.4 %collective-permute-done.48 = f32[8,8192]{1,0:T(8,128)S(1)} collective-permute-done((f32[8,8192]{1,0:T(8,128)S(1)}, f32[8,8192]{1,0:T(8,128)S(1)}, u32[]{:S(2)}, u32[]{:S(2)}) %collective-permute-start.48) | collective-permute-done | bytes 262176 | tf_op jit(solution)/shard_map/ppermute | solution.py:196
  269.6 3.7 %collective-permute-start.49 = (f32[16,8192]{1,0:T(8,128)S(1)}, f32[16,8192]{1,0:T(8,128)S(1)}, u32[]{:S(2)}, u32[]{:S(2)}) collective-permute-start(f32[16,8192]{1,0:T(8,128)S(1)} %maximum_select_fusion.4), channel_id=1, source_target_pairs={{0,64},{4,68},{8,72},{12,76},{16,80},{20,84},{24,88},{28,92},{32,9... | collective-permute-start | bytes 1572872 | tf_op jit(solution)/shard_map/ppermute | solution.py:196
  273.6 8.1 %collective-permute-done.49 = f32[16,8192]{1,0:T(8,128)S(1)} collective-permute-done((f32[16,8192]{1,0:T(8,128)S(1)}, f32[16,8192]{1,0:T(8,128)S(1)}, u32[]{:S(2)}, u32[]{:S(2)}) %collective-permute-start.49) | collective-permute-done | bytes 524320 | tf_op jit(solution)/shard_map/ppermute | solution.py:196
  283.1 14.2 %shard_map.38 = f32[32,16,512]{2,1,0:T(8,128)} custom-call(f32[32,16,512]{2,1,0:T(8,128)} %maximum_select_fusion.1.src_ref, f32[32,16,512]{2,1,0:T(8,128)} %reshape.1321.met_ref), custom_call_target="tpu_custom_call" | custom-call | tf_op jit(solution)/shard_map/pallas_call | solution.py:161
  301.4 4.5 %collective-permute-start.52 = (f32[1,4,1,32,64]{4,3,2,1,0:T(8,128)S(1)}, f32[1,4,1,32,64]{4,3,2,1,0:T(8,128)S(1)}, u32[]{:S(2)}, u32[]{:S(2)}) collective-permute-start(f32[1,4,1,32,64]{4,3,2,1,0:T(8,128)S(1)} %get-tuple-element.88), channel_id=1, source_target_pairs={{0,1},{1,2},{2,3},{4,5},{5,6},{6,7},{8,9},{9,10},{10,11},{12,13},{... | collective-permute-start | bytes 98312 | tf_op jit(solution)/shard_map/ppermute | solution.py:23
  306.0 1.9 collective-permute-start.50
  308.1 6.3 %collective-permute-done.50 = f32[1,4,2,32,64]{4,3,2,1,0:T(8,128)S(1)} collective-permute-done((f32[1,4,2,32,64]{4,3,2,1,0:T(8,128)S(1)}, f32[1,4,2,32,64]{4,3,2,1,0:T(8,128)S(1)}, u32[]{:S(2)}, u32[]{:S(2)}) %collective-permute-start.50) | collective-permute-done | bytes 65568 | tf_op jit(solution)/shard_map/ppermute | solution.py:34
  314.9 1.9 collective-permute-start.53
  318.2 4.6 %collective-permute-start.55 = (f32[1,4,1,64,128]{4,3,2,1,0:T(8,128)S(1)}, f32[1,4,1,64,128]{4,3,2,1,0:T(8,128)S(1)}, u32[]{:S(2)}, u32[]{:S(2)}) collective-permute-start(f32[1,4,1,64,128]{4,3,2,1,0:T(8,128)S(1)} %get-tuple-element.40), channel_id=1, source_target_pairs={{0,1},{1,2},{2,3},{4,5},{5,6},{6,7},{8,9},{9,10},{10,11},{12,13},{... | collective-permute-start | bytes 393224 | tf_op jit(solution)/shard_map/ppermute | solution.py:23
  325.5 2.1 collective-permute-done.53
  328.1 1.9 collective-permute-start.56
  331.4 4.6 %collective-permute-start.58 = (f32[1,4,1,64,128]{4,3,2,1,0:T(8,128)S(1)}, f32[1,4,1,64,128]{4,3,2,1,0:T(8,128)S(1)}, u32[]{:S(2)}, u32[]{:S(2)}) collective-permute-start(f32[1,4,1,64,128]{4,3,2,1,0:T(8,128)S(1)} %get-tuple-element.36), channel_id=1, source_target_pairs={{0,1},{1,2},{2,3},{4,5},{5,6},{6,7},{8,9},{9,10},{10,11},{12,13},{... | collective-permute-start | bytes 393224 | tf_op jit(solution)/shard_map/ppermute | solution.py:23
  338.6 2.1 collective-permute-done.56
  (213 shorter events, 77.4 us)
Async XLA Ops:
  1.0 10.2 %copy-start.2 = (f32[1,4,64,128]{3,2,1,0:T(8,128)S(1)}, f32[1,4,64,128]{3,2,1,0:T(8,128)}, u32[]{:S(2)}) copy-start(f32[1,4,64,128]{3,2,1,0:T(8,128)} %param.4) | copy-start | bytes 393220
  3.2 12.8 %copy-start = (f32[1,4,4,64,128]{4,3,2,1,0:T(8,128)S(1)}, f32[1,4,4,64,128]{4,3,2,1,0:T(8,128)}, u32[]{:S(2)}) copy-start(f32[1,4,4,64,128]{4,3,2,1,0:T(8,128)} %param.3) | copy-start | bytes 1572868
  3.2 12.7 %collective-permute-start = (f32[1,4,4,64,128]{4,3,2,1,0:T(8,128)S(1)}, f32[1,4,4,64,128]{4,3,2,1,0:T(8,128)S(1)}, u32[]{:S(2)}, u32[]{:S(2)}) collective-permute-start(f32[1,4,4,64,128]{4,3,2,1,0:T(8,128)S(1)} %get-tuple-element.9), channel_id=1, source_target_pairs={{0,4},{4,8},{8,12},{12,16},{16,20},{20,24},{24,28},{28,32},{32,36}... | collective-permute-start | bytes 1572872 | tf_op jit(solution)/shard_map/ppermute | solution.py:34
  5.3 7.4 %collective-permute-start.1 = (f32[1,4,1,64,128]{4,3,2,1,0:T(8,128)S(1)}, f32[1,4,1,64,128]{4,3,2,1,0:T(8,128)S(1)}, u32[]{:S(2)}, u32[]{:S(2)}) collective-permute-start(f32[1,4,1,64,128]{4,3,2,1,0:T(8,128)S(1)} %get-tuple-element.67), channel_id=1, source_target_pairs={{1,0},{2,1},{3,2},{5,4},{6,5},{7,6},{9,8},{10,9},{11,10},{13,12},{... | collective-permute-start | bytes 393224 | tf_op jit(solution)/shard_map/ppermute | solution.py:26
  6.6 7.8 %collective-permute-start.2 = (f32[1,4,1,64,128]{4,3,2,1,0:T(8,128)S(1)}, f32[1,4,1,64,128]{4,3,2,1,0:T(8,128)S(1)}, u32[]{:S(2)}, u32[]{:S(2)}) collective-permute-start(f32[1,4,1,64,128]{4,3,2,1,0:T(8,128)S(1)} %get-tuple-element.68), channel_id=1, source_target_pairs={{0,1},{1,2},{2,3},{4,5},{5,6},{6,7},{8,9},{9,10},{10,11},{12,13},{... | collective-permute-start | bytes 393224 | tf_op jit(solution)/shard_map/ppermute | solution.py:23
  16.5 12.6 %collective-permute-start.3 = (f32[1,4,4,64,128]{4,3,2,1,0:T(8,128)S(1)}, f32[1,4,4,64,128]{4,3,2,1,0:T(8,128)S(1)}, u32[]{:S(2)}, u32[]{:S(2)}) collective-permute-start(f32[1,4,4,64,128]{4,3,2,1,0:T(8,128)S(1)} %fusion.119), channel_id=1, source_target_pairs={{0,4},{4,8},{8,12},{12,16},{16,20},{20,24},{24,28},{28,32},{32,36}... | collective-permute-start | bytes 1572872 | tf_op jit(solution)/shard_map/ppermute | solution.py:34
  18.5 8.1 %collective-permute-start.4 = (f32[1,4,1,64,128]{4,3,2,1,0:T(8,128)S(1)}, f32[1,4,1,64,128]{4,3,2,1,0:T(8,128)S(1)}, u32[]{:S(2)}, u32[]{:S(2)}) collective-permute-start(f32[1,4,1,64,128]{4,3,2,1,0:T(8,128)S(1)} %get-tuple-element.63), channel_id=1, source_target_pairs={{1,0},{2,1},{3,2},{5,4},{6,5},{7,6},{9,8},{10,9},{11,10},{13,12},{... | collective-permute-start | bytes 393224 | tf_op jit(solution)/shard_map/ppermute | solution.py:26
  19.8 8.3 %collective-permute-start.5 = (f32[1,4,1,64,128]{4,3,2,1,0:T(8,128)S(1)}, f32[1,4,1,64,128]{4,3,2,1,0:T(8,128)S(1)}, u32[]{:S(2)}, u32[]{:S(2)}) collective-permute-start(f32[1,4,1,64,128]{4,3,2,1,0:T(8,128)S(1)} %get-tuple-element.64), channel_id=1, source_target_pairs={{0,1},{1,2},{2,3},{4,5},{5,6},{6,7},{8,9},{9,10},{10,11},{12,13},{... | collective-permute-start | bytes 393224 | tf_op jit(solution)/shard_map/ppermute | solution.py:23
  30.1 7.8 %collective-permute-start.7 = (f32[1,4,1,32,64]{4,3,2,1,0:T(8,128)S(1)}, f32[1,4,1,32,64]{4,3,2,1,0:T(8,128)S(1)}, u32[]{:S(2)}, u32[]{:S(2)}) collective-permute-start(f32[1,4,1,32,64]{4,3,2,1,0:T(8,128)S(1)} %get-tuple-element.107), channel_id=1, source_target_pairs={{1,0},{2,1},{3,2},{5,4},{6,5},{7,6},{9,8},{10,9},{11,10},{13,12},{... | collective-permute-start | bytes 98312 | tf_op jit(solution)/shard_map/ppermute | solution.py:26
  31.4 6.5 %collective-permute-start.8 = (f32[1,4,1,32,64]{4,3,2,1,0:T(8,128)S(1)}, f32[1,4,1,32,64]{4,3,2,1,0:T(8,128)S(1)}, u32[]{:S(2)}, u32[]{:S(2)}) collective-permute-start(f32[1,4,1,32,64]{4,3,2,1,0:T(8,128)S(1)} %get-tuple-element.108), channel_id=1, source_target_pairs={{0,1},{1,2},{2,3},{4,5},{5,6},{6,7},{8,9},{9,10},{10,11},{12,13},{... | collective-permute-start | bytes 98312 | tf_op jit(solution)/shard_map/ppermute | solution.py:23
  36.0 8.4 %collective-permute-start.6 = (f32[1,4,2,32,64]{4,3,2,1,0:T(8,128)S(1)}, f32[1,4,2,32,64]{4,3,2,1,0:T(8,128)S(1)}, u32[]{:S(2)}, u32[]{:S(2)}) collective-permute-start(f32[1,4,2,32,64]{4,3,2,1,0:T(8,128)S(1)} %fusion.388), channel_id=1, source_target_pairs={{0,4},{4,8},{8,12},{12,16},{16,20},{20,24},{24,28},{28,32},{32,36}... | collective-permute-start | bytes 196616 | tf_op jit(solution)/shard_map/ppermute | solution.py:34
  44.6 8.0 %collective-permute-start.10 = (f32[1,4,1,32,64]{4,3,2,1,0:T(8,128)S(1)}, f32[1,4,1,32,64]{4,3,2,1,0:T(8,128)S(1)}, u32[]{:S(2)}, u32[]{:S(2)}) collective-permute-start(f32[1,4,1,32,64]{4,3,2,1,0:T(8,128)S(1)} %get-tuple-element.103), channel_id=1, source_target_pairs={{1,0},{2,1},{3,2},{5,4},{6,5},{7,6},{9,8},{10,9},{11,10},{13,12},{... | collective-permute-start | bytes 98312 | tf_op jit(solution)/shard_map/ppermute | solution.py:26
  45.9 6.7 %collective-permute-start.11 = (f32[1,4,1,32,64]{4,3,2,1,0:T(8,128)S(1)}, f32[1,4,1,32,64]{4,3,2,1,0:T(8,128)S(1)}, u32[]{:S(2)}, u32[]{:S(2)}) collective-permute-start(f32[1,4,1,32,64]{4,3,2,1,0:T(8,128)S(1)} %get-tuple-element.104), channel_id=1, source_target_pairs={{0,1},{1,2},{2,3},{4,5},{5,6},{6,7},{8,9},{9,10},{10,11},{12,13},{... | collective-permute-start | bytes 98312 | tf_op jit(solution)/shard_map/ppermute | solution.py:23
  50.6 8.4 %collective-permute-start.9 = (f32[1,4,2,32,64]{4,3,2,1,0:T(8,128)S(1)}, f32[1,4,2,32,64]{4,3,2,1,0:T(8,128)S(1)}, u32[]{:S(2)}, u32[]{:S(2)}) collective-permute-start(f32[1,4,2,32,64]{4,3,2,1,0:T(8,128)S(1)} %fusion.207), channel_id=1, source_target_pairs={{0,4},{4,8},{8,12},{12,16},{16,20},{20,24},{24,28},{28,32},{32,36}... | collective-permute-start | bytes 196616 | tf_op jit(solution)/shard_map/ppermute | solution.py:34
  59.7 3.8 %collective-permute-start.12 = (f32[1,2560]{1,0:T(1,128)S(1)}, f32[1,2560]{1,0:T(1,128)S(1)}, u32[]{:S(2)}, u32[]{:S(2)}) collective-permute-start(f32[1,2560]{1,0:T(1,128)S(1)} %pad_maximum_fusion.30), channel_id=1, source_target_pairs={{0,1},{1,0},{2,3},{3,2},{4,5},{5,4},{6,7},{7,6},{8,9},{9,8},{10,11... | collective-permute-start | bytes 30728 | tf_op jit(solution)/shard_map/ppermute | solution.py:196
  63.5 5.7 %collective-permute-start.13 = (f32[1,5120]{1,0:T(1,128)S(1)}, f32[1,5120]{1,0:T(1,128)S(1)}, u32[]{:S(2)}, u32[]{:S(2)}) collective-permute-start(f32[1,5120]{1,0:T(1,128)S(1)} %broadcast_select_fusion.2), channel_id=1, source_target_pairs={{0,2},{1,3},{2,0},{3,1},{4,6},{5,7},{6,4},{7,5},{8,10},{9,11},{10,... | collective-permute-start | bytes 61448 | tf_op jit(solution)/shard_map/ppermute | solution.py:196
  69.2 1.3 collective-permute-start.14
  70.7 4.6 %collective-permute-start.15 = (f32[2,10240]{1,0:T(2,128)S(1)}, f32[2,10240]{1,0:T(2,128)S(1)}, u32[]{:S(2)}, u32[]{:S(2)}) collective-permute-start(f32[2,10240]{1,0:T(2,128)S(1)} %maximum_select_fusion.11), channel_id=1, source_target_pairs={{0,8},{4,12},{8,0},{12,4},{16,24},{20,28},{24,16},{28,20},{32,40},... | collective-permute-start | bytes 245768 | tf_op jit(solution)/shard_map/ppermute | solution.py:196
  75.4 7.0 %collective-permute-start.16 = (f32[4,10240]{1,0:T(4,128)S(1)}, f32[4,10240]{1,0:T(4,128)S(1)}, u32[]{:S(2)}, u32[]{:S(2)}) collective-permute-start(f32[4,10240]{1,0:T(4,128)S(1)} %maximum_select_fusion.8), channel_id=1, source_target_pairs={{0,16},{4,20},{8,24},{12,28},{16,0},{20,4},{24,8},{28,12},{32,48},... | collective-permute-start | bytes 491528 | tf_op jit(solution)/shard_map/ppermute | solution.py:196
  82.5 8.1 %collective-permute-start.17 = (f32[8,10240]{1,0:T(8,128)S(1)}, f32[8,10240]{1,0:T(8,128)S(1)}, u32[]{:S(2)}, u32[]{:S(2)}) collective-permute-start(f32[8,10240]{1,0:T(8,128)S(1)} %maximum_select_fusion.5), channel_id=1, source_target_pairs={{0,32},{4,36},{8,40},{12,44},{16,48},{20,52},{24,56},{28,60},{32,0... | collective-permute-start | bytes 983048 | tf_op jit(solution)/shard_map/ppermute | solution.py:196
  90.7 2.6 copy-start.1
  90.7 15.9 %collective-permute-start.18 = (f32[16,10240]{1,0:T(8,128)S(1)}, f32[16,10240]{1,0:T(8,128)}, u32[]{:S(2)}, u32[]{:S(2)}) collective-permute-start(f32[16,10240]{1,0:T(8,128)S(1)} %maximum_select_fusion.2), channel_id=1, source_target_pairs={{0,64},{4,68},{8,72},{12,76},{16,80},{20,84},{24,88},{28,92},{32,9... | collective-permute-start | bytes 1966088 | tf_op jit(solution)/shard_map/ppermute | solution.py:196
  109.8 1.2 slice-start.1
  111.1 1.3 slice-start
  131.1 7.8 %collective-permute-start.20 = (f32[1,4,1,32,64]{4,3,2,1,0:T(8,128)S(1)}, f32[1,4,1,32,64]{4,3,2,1,0:T(8,128)S(1)}, u32[]{:S(2)}, u32[]{:S(2)}) collective-permute-start(f32[1,4,1,32,64]{4,3,2,1,0:T(8,128)S(1)} %get-tuple-element.99), channel_id=1, source_target_pairs={{1,0},{2,1},{3,2},{5,4},{6,5},{7,6},{9,8},{10,9},{11,10},{13,12},{... | collective-permute-start | bytes 98312 | tf_op jit(solution)/shard_map/ppermute | solution.py:26
  132.4 6.5 %collective-permute-start.21 = (f32[1,4,1,32,64]{4,3,2,1,0:T(8,128)S(1)}, f32[1,4,1,32,64]{4,3,2,1,0:T(8,128)S(1)}, u32[]{:S(2)}, u32[]{:S(2)}) collective-permute-start(f32[1,4,1,32,64]{4,3,2,1,0:T(8,128)S(1)} %get-tuple-element.100), channel_id=1, source_target_pairs={{0,1},{1,2},{2,3},{4,5},{5,6},{6,7},{8,9},{9,10},{10,11},{12,13},{... | collective-permute-start | bytes 98312 | tf_op jit(solution)/shard_map/ppermute | solution.py:23
  137.0 8.4 %collective-permute-start.19 = (f32[1,4,2,32,64]{4,3,2,1,0:T(8,128)S(1)}, f32[1,4,2,32,64]{4,3,2,1,0:T(8,128)S(1)}, u32[]{:S(2)}, u32[]{:S(2)}) collective-permute-start(f32[1,4,2,32,64]{4,3,2,1,0:T(8,128)S(1)} %fusion.221), channel_id=1, source_target_pairs={{0,4},{4,8},{8,12},{12,16},{16,20},{20,24},{24,28},{28,32},{32,36}... | collective-permute-start | bytes 196616 | tf_op jit(solution)/shard_map/ppermute | solution.py:34
  145.9 12.6 %collective-permute-start.22 = (f32[1,4,4,64,128]{4,3,2,1,0:T(8,128)S(1)}, f32[1,4,4,64,128]{4,3,2,1,0:T(8,128)S(1)}, u32[]{:S(2)}, u32[]{:S(2)}) collective-permute-start(f32[1,4,4,64,128]{4,3,2,1,0:T(8,128)S(1)} %add.517), channel_id=1, source_target_pairs={{0,4},{4,8},{8,12},{12,16},{16,20},{20,24},{24,28},{28,32},{32,36}... | collective-permute-start | bytes 1572872 | tf_op jit(solution)/shard_map/ppermute | solution.py:34
  147.9 6.9 %collective-permute-start.23 = (f32[1,4,1,64,128]{4,3,2,1,0:T(8,128)S(1)}, f32[1,4,1,64,128]{4,3,2,1,0:T(8,128)S(1)}, u32[]{:S(2)}, u32[]{:S(2)}) collective-permute-start(f32[1,4,1,64,128]{4,3,2,1,0:T(8,128)S(1)} %get-tuple-element.59), channel_id=1, source_target_pairs={{1,0},{2,1},{3,2},{5,4},{6,5},{7,6},{9,8},{10,9},{11,10},{13,12},{... | collective-permute-start | bytes 393224 | tf_op jit(solution)/shard_map/ppermute | solution.py:26
  149.2 7.1 %collective-permute-start.24 = (f32[1,4,1,64,128]{4,3,2,1,0:T(8,128)S(1)}, f32[1,4,1,64,128]{4,3,2,1,0:T(8,128)S(1)}, u32[]{:S(2)}, u32[]{:S(2)}) collective-permute-start(f32[1,4,1,64,128]{4,3,2,1,0:T(8,128)S(1)} %get-tuple-element.60), channel_id=1, source_target_pairs={{0,1},{1,2},{2,3},{4,5},{5,6},{6,7},{8,9},{9,10},{10,11},{12,13},{... | collective-permute-start | bytes 393224 | tf_op jit(solution)/shard_map/ppermute | solution.py:23
  159.1 12.6 %collective-permute-start.25 = (f32[1,4,4,64,128]{4,3,2,1,0:T(8,128)S(1)}, f32[1,4,4,64,128]{4,3,2,1,0:T(8,128)S(1)}, u32[]{:S(2)}, u32[]{:S(2)}) collective-permute-start(f32[1,4,4,64,128]{4,3,2,1,0:T(8,128)S(1)} %fusion.93), channel_id=1, source_target_pairs={{0,4},{4,8},{8,12},{12,16},{16,20},{20,24},{24,28},{28,32},{32,36}... | collective-permute-start | bytes 1572872 | tf_op jit(solution)/shard_map/ppermute | solution.py:34
  161.0 6.9 %collective-permute-start.26 = (f32[1,4,1,64,128]{4,3,2,1,0:T(8,128)S(1)}, f32[1,4,1,64,128]{4,3,2,1,0:T(8,128)S(1)}, u32[]{:S(2)}, u32[]{:S(2)}) collective-permute-start(f32[1,4,1,64,128]{4,3,2,1,0:T(8,128)S(1)} %get-tuple-element.55), channel_id=1, source_target_pairs={{1,0},{2,1},{3,2},{5,4},{6,5},{7,6},{9,8},{10,9},{11,10},{13,12},{... | collective-permute-start | bytes 393224 | tf_op jit(solution)/shard_map/ppermute | solution.py:26
  162.3 7.1 %collective-permute-start.27 = (f32[1,4,1,64,128]{4,3,2,1,0:T(8,128)S(1)}, f32[1,4,1,64,128]{4,3,2,1,0:T(8,128)S(1)}, u32[]{:S(2)}, u32[]{:S(2)}) collective-permute-start(f32[1,4,1,64,128]{4,3,2,1,0:T(8,128)S(1)} %get-tuple-element.56), channel_id=1, source_target_pairs={{0,1},{1,2},{2,3},{4,5},{5,6},{6,7},{8,9},{9,10},{10,11},{12,13},{... | collective-permute-start | bytes 393224 | tf_op jit(solution)/shard_map/ppermute | solution.py:23
  172.2 12.6 %collective-permute-start.28 = (f32[1,4,4,64,128]{4,3,2,1,0:T(8,128)S(1)}, f32[1,4,4,64,128]{4,3,2,1,0:T(8,128)S(1)}, u32[]{:S(2)}, u32[]{:S(2)}) collective-permute-start(f32[1,4,4,64,128]{4,3,2,1,0:T(8,128)S(1)} %fusion.79), channel_id=1, source_target_pairs={{0,4},{4,8},{8,12},{12,16},{16,20},{20,24},{24,28},{28,32},{32,36}... | collective-permute-start | bytes 1572872 | tf_op jit(solution)/shard_map/ppermute | solution.py:34
  174.4 6.9 %collective-permute-start.29 = (f32[1,4,1,64,128]{4,3,2,1,0:T(8,128)S(1)}, f32[1,4,1,64,128]{4,3,2,1,0:T(8,128)S(1)}, u32[]{:S(2)}, u32[]{:S(2)}) collective-permute-start(f32[1,4,1,64,128]{4,3,2,1,0:T(8,128)S(1)} %get-tuple-element.51), channel_id=1, source_target_pairs={{1,0},{2,1},{3,2},{5,4},{6,5},{7,6},{9,8},{10,9},{11,10},{13,12},{... | collective-permute-start | bytes 393224 | tf_op jit(solution)/shard_map/ppermute | solution.py:26
  175.7 7.1 %collective-permute-start.30 = (f32[1,4,1,64,128]{4,3,2,1,0:T(8,128)S(1)}, f32[1,4,1,64,128]{4,3,2,1,0:T(8,128)S(1)}, u32[]{:S(2)}, u32[]{:S(2)}) collective-permute-start(f32[1,4,1,64,128]{4,3,2,1,0:T(8,128)S(1)} %get-tuple-element.52), channel_id=1, source_target_pairs={{0,1},{1,2},{2,3},{4,5},{5,6},{6,7},{8,9},{9,10},{10,11},{12,13},{... | collective-permute-start | bytes 393224 | tf_op jit(solution)/shard_map/ppermute | solution.py:23
  185.4 12.6 %collective-permute-start.31 = (f32[1,4,4,64,128]{4,3,2,1,0:T(8,128)S(1)}, f32[1,4,4,64,128]{4,3,2,1,0:T(8,128)S(1)}, u32[]{:S(2)}, u32[]{:S(2)}) collective-permute-start(f32[1,4,4,64,128]{4,3,2,1,0:T(8,128)S(1)} %fusion.65), channel_id=1, source_target_pairs={{0,4},{4,8},{8,12},{12,16},{16,20},{20,24},{24,28},{28,32},{32,36}... | collective-permute-start | bytes 1572872 | tf_op jit(solution)/shard_map/ppermute | solution.py:34
  187.4 6.9 %collective-permute-start.32 = (f32[1,4,1,64,128]{4,3,2,1,0:T(8,128)S(1)}, f32[1,4,1,64,128]{4,3,2,1,0:T(8,128)S(1)}, u32[]{:S(2)}, u32[]{:S(2)}) collective-permute-start(f32[1,4,1,64,128]{4,3,2,1,0:T(8,128)S(1)} %get-tuple-element.47), channel_id=1, source_target_pairs={{1,0},{2,1},{3,2},{5,4},{6,5},{7,6},{9,8},{10,9},{11,10},{13,12},{... | collective-permute-start | bytes 393224 | tf_op jit(solution)/shard_map/ppermute | solution.py:26
  188.7 7.1 %collective-permute-start.33 = (f32[1,4,1,64,128]{4,3,2,1,0:T(8,128)S(1)}, f32[1,4,1,64,128]{4,3,2,1,0:T(8,128)S(1)}, u32[]{:S(2)}, u32[]{:S(2)}) collective-permute-start(f32[1,4,1,64,128]{4,3,2,1,0:T(8,128)S(1)} %get-tuple-element.48), channel_id=1, source_target_pairs={{0,1},{1,2},{2,3},{4,5},{5,6},{6,7},{8,9},{9,10},{10,11},{12,13},{... | collective-permute-start | bytes 393224 | tf_op jit(solution)/shard_map/ppermute | solution.py:23
  198.6 12.6 %collective-permute-start.34 = (f32[1,4,4,64,128]{4,3,2,1,0:T(8,128)S(1)}, f32[1,4,4,64,128]{4,3,2,1,0:T(8,128)S(1)}, u32[]{:S(2)}, u32[]{:S(2)}) collective-permute-start(f32[1,4,4,64,128]{4,3,2,1,0:T(8,128)S(1)} %fusion.51), channel_id=1, source_target_pairs={{0,4},{4,8},{8,12},{12,16},{16,20},{20,24},{24,28},{28,32},{32,36}... | collective-permute-start | bytes 1572872 | tf_op jit(solution)/shard_map/ppermute | solution.py:34
  200.5 6.9 %collective-permute-start.35 = (f32[1,4,1,64,128]{4,3,2,1,0:T(8,128)S(1)}, f32[1,4,1,64,128]{4,3,2,1,0:T(8,128)S(1)}, u32[]{:S(2)}, u32[]{:S(2)}) collective-permute-start(f32[1,4,1,64,128]{4,3,2,1,0:T(8,128)S(1)} %get-tuple-element.43), channel_id=1, source_target_pairs={{1,0},{2,1},{3,2},{5,4},{6,5},{7,6},{9,8},{10,9},{11,10},{13,12},{... | collective-permute-start | bytes 393224 | tf_op jit(solution)/shard_map/ppermute | solution.py:26
  201.8 7.1 %collective-permute-start.36 = (f32[1,4,1,64,128]{4,3,2,1,0:T(8,128)S(1)}, f32[1,4,1,64,128]{4,3,2,1,0:T(8,128)S(1)}, u32[]{:S(2)}, u32[]{:S(2)}) collective-permute-start(f32[1,4,1,64,128]{4,3,2,1,0:T(8,128)S(1)} %get-tuple-element.44), channel_id=1, source_target_pairs={{0,1},{1,2},{2,3},{4,5},{5,6},{6,7},{8,9},{9,10},{10,11},{12,13},{... | collective-permute-start | bytes 393224 | tf_op jit(solution)/shard_map/ppermute | solution.py:23
  212.1 7.8 %collective-permute-start.38 = (f32[1,4,1,32,64]{4,3,2,1,0:T(8,128)S(1)}, f32[1,4,1,32,64]{4,3,2,1,0:T(8,128)S(1)}, u32[]{:S(2)}, u32[]{:S(2)}) collective-permute-start(f32[1,4,1,32,64]{4,3,2,1,0:T(8,128)S(1)} %get-tuple-element.95), channel_id=1, source_target_pairs={{1,0},{2,1},{3,2},{5,4},{6,5},{7,6},{9,8},{10,9},{11,10},{13,12},{... | collective-permute-start | bytes 98312 | tf_op jit(solution)/shard_map/ppermute | solution.py:26
  213.4 6.5 %collective-permute-start.39 = (f32[1,4,1,32,64]{4,3,2,1,0:T(8,128)S(1)}, f32[1,4,1,32,64]{4,3,2,1,0:T(8,128)S(1)}, u32[]{:S(2)}, u32[]{:S(2)}) collective-permute-start(f32[1,4,1,32,64]{4,3,2,1,0:T(8,128)S(1)} %get-tuple-element.96), channel_id=1, source_target_pairs={{0,1},{1,2},{2,3},{4,5},{5,6},{6,7},{8,9},{9,10},{10,11},{12,13},{... | collective-permute-start | bytes 98312 | tf_op jit(solution)/shard_map/ppermute | solution.py:23
  218.0 8.4 %collective-permute-start.37 = (f32[1,4,2,32,64]{4,3,2,1,0:T(8,128)S(1)}, f32[1,4,2,32,64]{4,3,2,1,0:T(8,128)S(1)}, u32[]{:S(2)}, u32[]{:S(2)}) collective-permute-start(f32[1,4,2,32,64]{4,3,2,1,0:T(8,128)S(1)} %fusion.389), channel_id=1, source_target_pairs={{0,4},{4,8},{8,12},{12,16},{16,20},{20,24},{24,28},{28,32},{32,36}... | collective-permute-start | bytes 196616 | tf_op jit(solution)/shard_map/ppermute | solution.py:34
  226.6 7.8 %collective-permute-start.41 = (f32[1,4,1,32,64]{4,3,2,1,0:T(8,128)S(1)}, f32[1,4,1,32,64]{4,3,2,1,0:T(8,128)S(1)}, u32[]{:S(2)}, u32[]{:S(2)}) collective-permute-start(f32[1,4,1,32,64]{4,3,2,1,0:T(8,128)S(1)} %get-tuple-element.91), channel_id=1, source_target_pairs={{1,0},{2,1},{3,2},{5,4},{6,5},{7,6},{9,8},{10,9},{11,10},{13,12},{... | collective-permute-start | bytes 98312 | tf_op jit(solution)/shard_map/ppermute | solution.py:26
  227.9 6.5 %collective-permute-start.42 = (f32[1,4,1,32,64]{4,3,2,1,0:T(8,128)S(1)}, f32[1,4,1,32,64]{4,3,2,1,0:T(8,128)S(1)}, u32[]{:S(2)}, u32[]{:S(2)}) collective-permute-start(f32[1,4,1,32,64]{4,3,2,1,0:T(8,128)S(1)} %get-tuple-element.92), channel_id=1, source_target_pairs={{0,1},{1,2},{2,3},{4,5},{5,6},{6,7},{8,9},{9,10},{10,11},{12,13},{... | collective-permute-start | bytes 98312 | tf_op jit(solution)/shard_map/ppermute | solution.py:23
  232.4 8.4 %collective-permute-start.40 = (f32[1,4,2,32,64]{4,3,2,1,0:T(8,128)S(1)}, f32[1,4,2,32,64]{4,3,2,1,0:T(8,128)S(1)}, u32[]{:S(2)}, u32[]{:S(2)}) collective-permute-start(f32[1,4,2,32,64]{4,3,2,1,0:T(8,128)S(1)} %fusion.166), channel_id=1, source_target_pairs={{0,4},{4,8},{8,12},{12,16},{16,20},{20,24},{24,28},{28,32},{32,36}... | collective-permute-start | bytes 196616 | tf_op jit(solution)/shard_map/ppermute | solution.py:34
  241.5 3.7 %collective-permute-start.43 = (f32[1,2048]{1,0:T(1,128)S(1)}, f32[1,2048]{1,0:T(1,128)S(1)}, u32[]{:S(2)}, u32[]{:S(2)}) collective-permute-start(f32[1,2048]{1,0:T(1,128)S(1)} %reshape.1330), channel_id=1, source_target_pairs={{0,1},{1,0},{2,3},{3,2},{4,5},{5,4},{6,7},{7,6},{8,9},{9,8},{10,11... | collective-permute-start | bytes 24584 | tf_op jit(solution)/shard_map/ppermute | solution.py:196
  245.2 5.3 %collective-permute-start.44 = (f32[1,4096]{1,0:T(1,128)S(1)}, f32[1,4096]{1,0:T(1,128)S(1)}, u32[]{:S(2)}, u32[]{:S(2)}) collective-permute-start(f32[1,4096]{1,0:T(1,128)S(1)} %broadcast_select_fusion.3), channel_id=1, source_target_pairs={{0,2},{1,3},{2,0},{3,1},{4,6},{5,7},{6,4},{7,5},{8,10},{9,11},{10,... | collective-permute-start | bytes 49160 | tf_op jit(solution)/shard_map/ppermute | solution.py:196
  250.6 1.3 collective-permute-start.45
  252.0 4.3 %collective-permute-start.46 = (f32[2,8192]{1,0:T(2,128)S(1)}, f32[2,8192]{1,0:T(2,128)S(1)}, u32[]{:S(2)}, u32[]{:S(2)}) collective-permute-start(f32[2,8192]{1,0:T(2,128)S(1)} %maximum_select_fusion.12), channel_id=1, source_target_pairs={{0,8},{4,12},{8,0},{12,4},{16,24},{20,28},{24,16},{28,20},{32,40},... | collective-permute-start | bytes 196616 | tf_op jit(solution)/shard_map/ppermute | solution.py:196
  256.4 6.6 %collective-permute-start.47 = (f32[4,8192]{1,0:T(4,128)S(1)}, f32[4,8192]{1,0:T(4,128)S(1)}, u32[]{:S(2)}, u32[]{:S(2)}) collective-permute-start(f32[4,8192]{1,0:T(4,128)S(1)} %maximum_select_fusion.10), channel_id=1, source_target_pairs={{0,16},{4,20},{8,24},{12,28},{16,0},{20,4},{24,8},{28,12},{32,48},... | collective-permute-start | bytes 393224 | tf_op jit(solution)/shard_map/ppermute | solution.py:196
  263.1 6.5 %collective-permute-start.48 = (f32[8,8192]{1,0:T(8,128)S(1)}, f32[8,8192]{1,0:T(8,128)S(1)}, u32[]{:S(2)}, u32[]{:S(2)}) collective-permute-start(f32[8,8192]{1,0:T(8,128)S(1)} %maximum_select_fusion.7), channel_id=1, source_target_pairs={{0,32},{4,36},{8,40},{12,44},{16,48},{20,52},{24,56},{28,60},{32,0... | collective-permute-start | bytes 786440 | tf_op jit(solution)/shard_map/ppermute | solution.py:196
  269.6 12.1 %collective-permute-start.49 = (f32[16,8192]{1,0:T(8,128)S(1)}, f32[16,8192]{1,0:T(8,128)S(1)}, u32[]{:S(2)}, u32[]{:S(2)}) collective-permute-start(f32[16,8192]{1,0:T(8,128)S(1)} %maximum_select_fusion.4), channel_id=1, source_target_pairs={{0,64},{4,68},{8,72},{12,76},{16,80},{20,84},{24,88},{28,92},{32,9... | collective-permute-start | bytes 1572872 | tf_op jit(solution)/shard_map/ppermute | solution.py:196
  300.1 7.8 %collective-permute-start.51 = (f32[1,4,1,32,64]{4,3,2,1,0:T(8,128)S(1)}, f32[1,4,1,32,64]{4,3,2,1,0:T(8,128)S(1)}, u32[]{:S(2)}, u32[]{:S(2)}) collective-permute-start(f32[1,4,1,32,64]{4,3,2,1,0:T(8,128)S(1)} %get-tuple-element.87), channel_id=1, source_target_pairs={{1,0},{2,1},{3,2},{5,4},{6,5},{7,6},{9,8},{10,9},{11,10},{13,12},{... | collective-permute-start | bytes 98312 | tf_op jit(solution)/shard_map/ppermute | solution.py:26
  301.4 6.5 %collective-permute-start.52 = (f32[1,4,1,32,64]{4,3,2,1,0:T(8,128)S(1)}, f32[1,4,1,32,64]{4,3,2,1,0:T(8,128)S(1)}, u32[]{:S(2)}, u32[]{:S(2)}) collective-permute-start(f32[1,4,1,32,64]{4,3,2,1,0:T(8,128)S(1)} %get-tuple-element.88), channel_id=1, source_target_pairs={{0,1},{1,2},{2,3},{4,5},{5,6},{6,7},{8,9},{9,10},{10,11},{12,13},{... | collective-permute-start | bytes 98312 | tf_op jit(solution)/shard_map/ppermute | solution.py:23
  306.0 8.4 %collective-permute-start.50 = (f32[1,4,2,32,64]{4,3,2,1,0:T(8,128)S(1)}, f32[1,4,2,32,64]{4,3,2,1,0:T(8,128)S(1)}, u32[]{:S(2)}, u32[]{:S(2)}) collective-permute-start(f32[1,4,2,32,64]{4,3,2,1,0:T(8,128)S(1)} %fusion.233), channel_id=1, source_target_pairs={{0,4},{4,8},{8,12},{12,16},{16,20},{20,24},{24,28},{28,32},{32,36}... | collective-permute-start | bytes 196616 | tf_op jit(solution)/shard_map/ppermute | solution.py:34
  314.9 12.6 %collective-permute-start.53 = (f32[1,4,4,64,128]{4,3,2,1,0:T(8,128)S(1)}, f32[1,4,4,64,128]{4,3,2,1,0:T(8,128)S(1)}, u32[]{:S(2)}, u32[]{:S(2)}) collective-permute-start(f32[1,4,4,64,128]{4,3,2,1,0:T(8,128)S(1)} %add.567), channel_id=1, source_target_pairs={{0,4},{4,8},{8,12},{12,16},{16,20},{20,24},{24,28},{28,32},{32,36}... | collective-permute-start | bytes 1572872 | tf_op jit(solution)/shard_map/ppermute | solution.py:34
  316.9 7.2 %collective-permute-start.54 = (f32[1,4,1,64,128]{4,3,2,1,0:T(8,128)S(1)}, f32[1,4,1,64,128]{4,3,2,1,0:T(8,128)S(1)}, u32[]{:S(2)}, u32[]{:S(2)}) collective-permute-start(f32[1,4,1,64,128]{4,3,2,1,0:T(8,128)S(1)} %get-tuple-element.39), channel_id=1, source_target_pairs={{1,0},{2,1},{3,2},{5,4},{6,5},{7,6},{9,8},{10,9},{11,10},{13,12},{... | collective-permute-start | bytes 393224 | tf_op jit(solution)/shard_map/ppermute | solution.py:26
  318.2 7.1 %collective-permute-start.55 = (f32[1,4,1,64,128]{4,3,2,1,0:T(8,128)S(1)}, f32[1,4,1,64,128]{4,3,2,1,0:T(8,128)S(1)}, u32[]{:S(2)}, u32[]{:S(2)}) collective-permute-start(f32[1,4,1,64,128]{4,3,2,1,0:T(8,128)S(1)} %get-tuple-element.40), channel_id=1, source_target_pairs={{0,1},{1,2},{2,3},{4,5},{5,6},{6,7},{8,9},{9,10},{10,11},{12,13},{... | collective-permute-start | bytes 393224 | tf_op jit(solution)/shard_map/ppermute | solution.py:23
  328.1 12.6 %collective-permute-start.56 = (f32[1,4,4,64,128]{4,3,2,1,0:T(8,128)S(1)}, f32[1,4,4,64,128]{4,3,2,1,0:T(8,128)S(1)}, u32[]{:S(2)}, u32[]{:S(2)}) collective-permute-start(f32[1,4,4,64,128]{4,3,2,1,0:T(8,128)S(1)} %fusion.25), channel_id=1, source_target_pairs={{0,4},{4,8},{8,12},{12,16},{16,20},{20,24},{24,28},{28,32},{32,36}... | collective-permute-start | bytes 1572872 | tf_op jit(solution)/shard_map/ppermute | solution.py:34
  330.1 6.9 %collective-permute-start.57 = (f32[1,4,1,64,128]{4,3,2,1,0:T(8,128)S(1)}, f32[1,4,1,64,128]{4,3,2,1,0:T(8,128)S(1)}, u32[]{:S(2)}, u32[]{:S(2)}) collective-permute-start(f32[1,4,1,64,128]{4,3,2,1,0:T(8,128)S(1)} %get-tuple-element.35), channel_id=1, source_target_pairs={{1,0},{2,1},{3,2},{5,4},{6,5},{7,6},{9,8},{10,9},{11,10},{13,12},{... | collective-permute-start | bytes 393224 | tf_op jit(solution)/shard_map/ppermute | solution.py:26
  331.4 7.1 %collective-permute-start.58 = (f32[1,4,1,64,128]{4,3,2,1,0:T(8,128)S(1)}, f32[1,4,1,64,128]{4,3,2,1,0:T(8,128)S(1)}, u32[]{:S(2)}, u32[]{:S(2)}) collective-permute-start(f32[1,4,1,64,128]{4,3,2,1,0:T(8,128)S(1)} %get-tuple-element.36), channel_id=1, source_target_pairs={{0,1},{1,2},{2,3},{4,5},{5,6},{6,7},{8,9},{9,10},{10,11},{12,13},{... | collective-permute-start | bytes 393224 | tf_op jit(solution)/shard_map/ppermute | solution.py:23

commit v16 on v15

--- a/solution.py
+++ b/solution.py
@@ -218,16 +218,8 @@
     local_dims = source.shape
     local_steps, components, planes, height_y, width_z = local_dims
     source_flat = source.reshape(1, -1)
-    cut = source_flat.shape[1]
-    if "metric" in gathered:
-        flat_source = gather_all(source_flat)
-        flat_metric = gathered["metric"]
-    else:
-        both = jnp.concatenate([source_flat, metric_two.reshape(1, -1)], axis=1)
-        flat_both = gather_all(both)
-        flat_source = flat_both[:, :cut]
-        flat_metric = flat_both[:, cut:]
-        gathered["metric"] = flat_metric
+    flat_source = gather_all(source_flat)
+    flat_metric = gathered["metric"]
     whole_source, whole_metric = assemble(
         flat_source, flat_metric, time_devs, plane_devs, local_dims
     )
@@ -255,7 +247,7 @@
     metric_two = restrict(metric_one)
     metrics = (metric, metric_one)
     pinned_levels = (pinned, None)
-    gathered = {}
+    gathered = {"metric": gather_all(metric_two.reshape(1, -1))}
 
     def sweep(depth, values, source, diagonal):
         if values is None:

time: 344 us -> 338 us (0.983)
  waiting for transfers between devices: 146 us -> 135 us
  starting transfers between devices: 135 us -> 142 us
    ppermute x14 -> x21, starting transfers between devices: 18.1 us -> 25 us  [gather_doubling(): other = lax.ppermute(gathered, axis, [(i, i ^ step) for i in range(size)])]
    ppermute x14 -> x21, waiting for transfers between devices: 67.4 us -> 61.2 us  [gather_doubling(): other = lax.ppermute(gathered, axis, [(i, i ^ step) for i in range(size)])]
  transfers between devices with their start and end apart: 59 -> 66, of which waited for: 47 -> 46; matrix products, arithmetic and copies ran while one was open for 1% -> 3% of each run, Pallas kernels for 0% -> 0%
where the time goes in v16:
time: 338 us; the launch traced here: 336 us
  starting transfers between devices  142 us (42%)
  waiting for transfers between devices  135 us (40%)
  Pallas kernels  28.5 us (8%)
  other arithmetic  16.7 us (5%)
  local copies, waits for them, and re-layouts  10.1 us (3%)
    ppermute x15, starting transfers between devices, with_halo(): lax.ppermute(lax.slice_in_dim(block, block.shape[dim] - width, None, axis...  68.3 us
    ppermute x21, waiting for transfers between devices, gather_doubling(): other = lax.ppermute(gathered, axis, [(i, i ^ step) for i in range(size)])  61.2 us
    ppermute x15, waiting for transfers between devices, from_behind(): return lax.ppermute(array, axis, pairs)  53.3 us
    ppermute x15, starting transfers between devices, from_behind(): return lax.ppermute(array, axis, pairs)  29.5 us
    pallas_call x2, Pallas kernels, coarse_solve(): pl.pallas_call(kernel, out_shape=jax.ShapeDtypeStruct(flat_source.shape,...  28.5 us
    ppermute x21, starting transfers between devices, gather_doubling(): other = lax.ppermute(gathered, axis, [(i, i ^ step) for i in range(size)])  25 us
    ppermute x15, starting transfers between devices, with_halo(): lax.ppermute(lax.slice_in_dim(block, 0, width, axis=dim), axis, backward)  19.4 us
    ppermute x15, waiting for transfers between devices, with_halo(): lax.ppermute(lax.slice_in_dim(block, block.shape[dim] - width, None, axis...  11.9 us
  transfers between devices with their start and end apart: 66, of which 46 were waited for; matrix products, arithmetic and copies ran while one was open for 3% of the time, Pallas kernels for 0%

profile of v16, /device:TPU:2, one launch (start us, length us, event | category | flops | bytes accessed | tf_op | source)
XLA Modules:
  0.0 336.2 jit_solution(923414565981533287)
XLA Ops:
  3.2 1.9 collective-permute-start
  6.5 4.6 %collective-permute-start.2 = (f32[1,4,1,64,128]{4,3,2,1,0:T(8,128)S(1)}, f32[1,4,1,64,128]{4,3,2,1,0:T(8,128)S(1)}, u32[]{:S(2)}, u32[]{:S(2)}) collective-permute-start(f32[1,4,1,64,128]{4,3,2,1,0:T(8,128)S(1)} %get-tuple-element.68), channel_id=1, source_target_pairs={{0,1},{1,2},{2,3},{4,5},{5,6},{6,7},{8,9},{9,10},{10,11},{12,13},{... | collective-permute-start | bytes 393224 | tf_op jit(solution)/shard_map/ppermute | solution.py:23
  16.4 1.9 collective-permute-start.3
  19.6 4.6 %collective-permute-start.5 = (f32[1,4,1,64,128]{4,3,2,1,0:T(8,128)S(1)}, f32[1,4,1,64,128]{4,3,2,1,0:T(8,128)S(1)}, u32[]{:S(2)}, u32[]{:S(2)}) collective-permute-start(f32[1,4,1,64,128]{4,3,2,1,0:T(8,128)S(1)} %get-tuple-element.64), channel_id=1, source_target_pairs={{0,1},{1,2},{2,3},{4,5},{5,6},{6,7},{8,9},{9,10},{10,11},{12,13},{... | collective-permute-start | bytes 393224 | tf_op jit(solution)/shard_map/ppermute | solution.py:23
  24.4 1.9 collective-permute-start.19
  28.0 3.9 %collective-permute-start.20 = (f32[1,1024]{1,0:T(1,128)S(1)}, f32[1,1024]{1,0:T(1,128)S(1)}, u32[]{:S(2)}, u32[]{:S(2)}) collective-permute-start(f32[1,1024]{1,0:T(1,128)S(1)} %broadcast_select_fusion.5), channel_id=1, source_target_pairs={{0,2},{1,3},{2,0},{3,1},{4,6},{5,7},{6,4},{7,5},{8,10},{9,11},{10,... | collective-permute-start | bytes 12296 | tf_op jit(solution)/shard_map/ppermute | solution.py:196
  34.4 4.5 %collective-permute-start.8 = (f32[1,4,1,32,64]{4,3,2,1,0:T(8,128)S(1)}, f32[1,4,1,32,64]{4,3,2,1,0:T(8,128)S(1)}, u32[]{:S(2)}, u32[]{:S(2)}) collective-permute-start(f32[1,4,1,32,64]{4,3,2,1,0:T(8,128)S(1)} %get-tuple-element.108), channel_id=1, source_target_pairs={{0,1},{1,2},{2,3},{4,5},{5,6},{6,7},{8,9},{9,10},{10,11},{12,13},{... | collective-permute-start | bytes 98312 | tf_op jit(solution)/shard_map/ppermute | solution.py:23
  39.0 1.9 collective-permute-start.6
  41.0 6.3 %collective-permute-done.6 = f32[1,4,2,32,64]{4,3,2,1,0:T(8,128)S(1)} collective-permute-done((f32[1,4,2,32,64]{4,3,2,1,0:T(8,128)S(1)}, f32[1,4,2,32,64]{4,3,2,1,0:T(8,128)S(1)}, u32[]{:S(2)}, u32[]{:S(2)}) %collective-permute-start.6) | collective-permute-done | bytes 65568 | tf_op jit(solution)/shard_map/ppermute | solution.py:34
  48.8 4.5 %collective-permute-start.11 = (f32[1,4,1,32,64]{4,3,2,1,0:T(8,128)S(1)}, f32[1,4,1,32,64]{4,3,2,1,0:T(8,128)S(1)}, u32[]{:S(2)}, u32[]{:S(2)}) collective-permute-start(f32[1,4,1,32,64]{4,3,2,1,0:T(8,128)S(1)} %get-tuple-element.104), channel_id=1, source_target_pairs={{0,1},{1,2},{2,3},{4,5},{5,6},{6,7},{8,9},{9,10},{10,11},{12,13},{... | collective-permute-start | bytes 98312 | tf_op jit(solution)/shard_map/ppermute | solution.py:23
  53.5 2.4 collective-permute-start.9
  56.0 5.9 %collective-permute-done.9 = f32[1,4,2,32,64]{4,3,2,1,0:T(8,128)S(1)} collective-permute-done((f32[1,4,2,32,64]{4,3,2,1,0:T(8,128)S(1)}, f32[1,4,2,32,64]{4,3,2,1,0:T(8,128)S(1)}, u32[]{:S(2)}, u32[]{:S(2)}) %collective-permute-start.9) | collective-permute-done | bytes 65568 | tf_op jit(solution)/shard_map/ppermute | solution.py:34
  66.3 1.9 collective-permute-start.13
  68.2 3.5 %collective-permute-done.13 = f32[1,4096]{1,0:T(1,128)S(1)} collective-permute-done((f32[1,4096]{1,0:T(1,128)S(1)}, f32[1,4096]{1,0:T(1,128)S(1)}, u32[]{:S(2)}, u32[]{:S(2)}) %collective-permute-start.13) | collective-permute-done | bytes 16416 | tf_op jit(solution)/shard_map/ppermute | solution.py:196
  73.4 4.0 %collective-permute-done.15 = f32[2,8192]{1,0:T(2,128)S(1)} collective-permute-done((f32[2,8192]{1,0:T(2,128)S(1)}, f32[2,8192]{1,0:T(2,128)S(1)}, u32[]{:S(2)}, u32[]{:S(2)}) %collective-permute-start.15) | collective-permute-done | bytes 65568 | tf_op jit(solution)/shard_map/ppermute | solution.py:196
  77.5 2.6 collective-permute-start.16
  80.2 3.8 %collective-permute-done.16 = f32[4,8192]{1,0:T(4,128)S(1)} collective-permute-done((f32[4,8192]{1,0:T(4,128)S(1)}, f32[4,8192]{1,0:T(4,128)S(1)}, u32[]{:S(2)}, u32[]{:S(2)}) %collective-permute-start.16) | collective-permute-done | bytes 131104 | tf_op jit(solution)/shard_map/ppermute | solution.py:196
  84.5 2.8 collective-permute-start.25
  87.4 4.6 %collective-permute-done.17 = f32[8,8192]{1,0:T(8,128)S(1)} collective-permute-done((f32[8,8192]{1,0:T(8,128)S(1)}, f32[8,8192]{1,0:T(8,128)S(1)}, u32[]{:S(2)}, u32[]{:S(2)}) %collective-permute-start.17) | collective-permute-done | bytes 262176 | tf_op jit(solution)/shard_map/ppermute | solution.py:196
  92.8 3.2 collective-permute-start.18
  98.3 7.4 %collective-permute-done.18 = f32[16,8192]{1,0:T(8,128)} collective-permute-done((f32[16,8192]{1,0:T(8,128)}, f32[16,8192]{1,0:T(8,128)}, u32[]{:S(2)}, u32[]{:S(2)}) %collective-permute-start.18) | collective-permute-done | bytes 524320 | tf_op jit(solution)/shard_map/ppermute | solution.py:196
  108.1 14.3 %shard_map.37 = f32[32,16,512]{2,1,0:T(8,128)} custom-call(f32[32,16,512]{2,1,0:T(8,128)} %maximum_select_fusion.src_ref, f32[32,16,512]{2,1,0:T(8,128)} %reshape.1456.met_ref), custom_call_target="tpu_custom_call" | custom-call | tf_op jit(solution)/shard_map/pallas_call | solution.py:161
  126.5 4.5 %collective-permute-start.28 = (f32[1,4,1,32,64]{4,3,2,1,0:T(8,128)S(1)}, f32[1,4,1,32,64]{4,3,2,1,0:T(8,128)S(1)}, u32[]{:S(2)}, u32[]{:S(2)}) collective-permute-start(f32[1,4,1,32,64]{4,3,2,1,0:T(8,128)S(1)} %get-tuple-element.100), channel_id=1, source_target_pairs={{0,1},{1,2},{2,3},{4,5},{5,6},{6,7},{8,9},{9,10},{10,11},{12,13},{... | collective-permute-start | bytes 98312 | tf_op jit(solution)/shard_map/ppermute | solution.py:23
  131.1 1.9 collective-permute-start.26
  133.1 6.3 %collective-permute-done.26 = f32[1,4,2,32,64]{4,3,2,1,0:T(8,128)S(1)} collective-permute-done((f32[1,4,2,32,64]{4,3,2,1,0:T(8,128)S(1)}, f32[1,4,2,32,64]{4,3,2,1,0:T(8,128)S(1)}, u32[]{:S(2)}, u32[]{:S(2)}) %collective-permute-start.26) | collective-permute-done | bytes 65568 | tf_op jit(solution)/shard_map/ppermute | solution.py:34
  140.0 2.1 collective-permute-start.29
  143.4 4.6 %collective-permute-start.31 = (f32[1,4,1,64,128]{4,3,2,1,0:T(8,128)S(1)}, f32[1,4,1,64,128]{4,3,2,1,0:T(8,128)S(1)}, u32[]{:S(2)}, u32[]{:S(2)}) collective-permute-start(f32[1,4,1,64,128]{4,3,2,1,0:T(8,128)S(1)} %get-tuple-element.60), channel_id=1, source_target_pairs={{0,1},{1,2},{2,3},{4,5},{5,6},{6,7},{8,9},{9,10},{10,11},{12,13},{... | collective-permute-start | bytes 393224 | tf_op jit(solution)/shard_map/ppermute | solution.py:23
  150.7 1.9 collective-permute-done.29
  153.2 1.9 collective-permute-start.32
  156.4 4.6 %collective-permute-start.34 = (f32[1,4,1,64,128]{4,3,2,1,0:T(8,128)S(1)}, f32[1,4,1,64,128]{4,3,2,1,0:T(8,128)S(1)}, u32[]{:S(2)}, u32[]{:S(2)}) collective-permute-start(f32[1,4,1,64,128]{4,3,2,1,0:T(8,128)S(1)} %get-tuple-element.56), channel_id=1, source_target_pairs={{0,1},{1,2},{2,3},{4,5},{5,6},{6,7},{8,9},{9,10},{10,11},{12,13},{... | collective-permute-start | bytes 393224 | tf_op jit(solution)/shard_map/ppermute | solution.py:23
  163.7 2.1 collective-permute-done.32
  166.3 1.9 collective-permute-start.35
  169.6 4.6 %collective-permute-start.37 = (f32[1,4,1,64,128]{4,3,2,1,0:T(8,128)S(1)}, f32[1,4,1,64,128]{4,3,2,1,0:T(8,128)S(1)}, u32[]{:S(2)}, u32[]{:S(2)}) collective-permute-start(f32[1,4,1,64,128]{4,3,2,1,0:T(8,128)S(1)} %get-tuple-element.52), channel_id=1, source_target_pairs={{0,1},{1,2},{2,3},{4,5},{5,6},{6,7},{8,9},{9,10},{10,11},{12,13},{... | collective-permute-start | bytes 393224 | tf_op jit(solution)/shard_map/ppermute | solution.py:23
  176.8 2.1 collective-permute-done.35
  179.5 1.9 collective-permute-start.38
  182.7 4.6 %collective-permute-start.40 = (f32[1,4,1,64,128]{4,3,2,1,0:T(8,128)S(1)}, f32[1,4,1,64,128]{4,3,2,1,0:T(8,128)S(1)}, u32[]{:S(2)}, u32[]{:S(2)}) collective-permute-start(f32[1,4,1,64,128]{4,3,2,1,0:T(8,128)S(1)} %get-tuple-element.48), channel_id=1, source_target_pairs={{0,1},{1,2},{2,3},{4,5},{5,6},{6,7},{8,9},{9,10},{10,11},{12,13},{... | collective-permute-start | bytes 393224 | tf_op jit(solution)/shard_map/ppermute | solution.py:23
  190.0 2.1 collective-permute-done.38
  192.7 1.9 collective-permute-start.41
  195.9 4.6 %collective-permute-start.43 = (f32[1,4,1,64,128]{4,3,2,1,0:T(8,128)S(1)}, f32[1,4,1,64,128]{4,3,2,1,0:T(8,128)S(1)}, u32[]{:S(2)}, u32[]{:S(2)}) collective-permute-start(f32[1,4,1,64,128]{4,3,2,1,0:T(8,128)S(1)} %get-tuple-element.44), channel_id=1, source_target_pairs={{0,1},{1,2},{2,3},{4,5},{5,6},{6,7},{8,9},{9,10},{10,11},{12,13},{... | collective-permute-start | bytes 393224 | tf_op jit(solution)/shard_map/ppermute | solution.py:23
  203.2 2.1 collective-permute-done.41
  207.5 4.5 %collective-permute-start.46 = (f32[1,4,1,32,64]{4,3,2,1,0:T(8,128)S(1)}, f32[1,4,1,32,64]{4,3,2,1,0:T(8,128)S(1)}, u32[]{:S(2)}, u32[]{:S(2)}) collective-permute-start(f32[1,4,1,32,64]{4,3,2,1,0:T(8,128)S(1)} %get-tuple-element.96), channel_id=1, source_target_pairs={{0,1},{1,2},{2,3},{4,5},{5,6},{6,7},{8,9},{9,10},{10,11},{12,13},{... | collective-permute-start | bytes 98312 | tf_op jit(solution)/shard_map/ppermute | solution.py:23
  212.1 1.9 collective-permute-start.44
  214.2 6.3 %collective-permute-done.44 = f32[1,4,2,32,64]{4,3,2,1,0:T(8,128)S(1)} collective-permute-done((f32[1,4,2,32,64]{4,3,2,1,0:T(8,128)S(1)}, f32[1,4,2,32,64]{4,3,2,1,0:T(8,128)S(1)}, u32[]{:S(2)}, u32[]{:S(2)}) %collective-permute-start.44) | collective-permute-done | bytes 65568 | tf_op jit(solution)/shard_map/ppermute | solution.py:34
  222.0 4.5 %collective-permute-start.49 = (f32[1,4,1,32,64]{4,3,2,1,0:T(8,128)S(1)}, f32[1,4,1,32,64]{4,3,2,1,0:T(8,128)S(1)}, u32[]{:S(2)}, u32[]{:S(2)}) collective-permute-start(f32[1,4,1,32,64]{4,3,2,1,0:T(8,128)S(1)} %get-tuple-element.92), channel_id=1, source_target_pairs={{0,1},{1,2},{2,3},{4,5},{5,6},{6,7},{8,9},{9,10},{10,11},{12,13},{... | collective-permute-start | bytes 98312 | tf_op jit(solution)/shard_map/ppermute | solution.py:23
  226.5 1.9 collective-permute-start.47
  228.6 6.3 %collective-permute-done.47 = f32[1,4,2,32,64]{4,3,2,1,0:T(8,128)S(1)} collective-permute-done((f32[1,4,2,32,64]{4,3,2,1,0:T(8,128)S(1)}, f32[1,4,2,32,64]{4,3,2,1,0:T(8,128)S(1)}, u32[]{:S(2)}, u32[]{:S(2)}) %collective-permute-start.47) | collective-permute-done | bytes 65568 | tf_op jit(solution)/shard_map/ppermute | solution.py:34
  237.1 2.2 collective-permute-done.50
  239.3 2.0 collective-permute-start.51
  241.3 3.3 collective-permute-done.51
  246.1 4.3 %collective-permute-done.53 = f32[2,8192]{1,0:T(2,128)S(1)} collective-permute-done((f32[2,8192]{1,0:T(2,128)S(1)}, f32[2,8192]{1,0:T(2,128)S(1)}, u32[]{:S(2)}, u32[]{:S(2)}) %collective-permute-start.53) | collective-permute-done | bytes 65568 | tf_op jit(solution)/shard_map/ppermute | solution.py:196
  250.6 6.5 %collective-permute-done.54 = f32[4,8192]{1,0:T(4,128)S(1)} collective-permute-done((f32[4,8192]{1,0:T(4,128)S(1)}, f32[4,8192]{1,0:T(4,128)S(1)}, u32[]{:S(2)}, u32[]{:S(2)}) %collective-permute-start.54) | collective-permute-done | bytes 131104 | tf_op jit(solution)/shard_map/ppermute | solution.py:196
  257.2 6.4 %collective-permute-done.55 = f32[8,8192]{1,0:T(8,128)S(1)} collective-permute-done((f32[8,8192]{1,0:T(8,128)S(1)}, f32[8,8192]{1,0:T(8,128)S(1)}, u32[]{:S(2)}, u32[]{:S(2)}) %collective-permute-start.55) | collective-permute-done | bytes 262176 | tf_op jit(solution)/shard_map/ppermute | solution.py:196
  263.6 2.3 collective-permute-start.56
  266.3 9.5 %collective-permute-done.56 = f32[16,8192]{1,0:T(8,128)S(1)} collective-permute-done((f32[16,8192]{1,0:T(8,128)S(1)}, f32[16,8192]{1,0:T(8,128)S(1)}, u32[]{:S(2)}, u32[]{:S(2)}) %collective-permute-start.56) | collective-permute-done | bytes 524320 | tf_op jit(solution)/shard_map/ppermute | solution.py:196
  277.2 14.3 %shard_map.38 = f32[32,16,512]{2,1,0:T(8,128)} custom-call(f32[32,16,512]{2,1,0:T(8,128)} %maximum_select_fusion.1.src_ref, f32[32,16,512]{2,1,0:T(8,128)} %reshape.1456.met_ref), custom_call_target="tpu_custom_call" | custom-call | tf_op jit(solution)/shard_map/pallas_call | solution.py:161
  295.6 4.5 %collective-permute-start.59 = (f32[1,4,1,32,64]{4,3,2,1,0:T(8,128)S(1)}, f32[1,4,1,32,64]{4,3,2,1,0:T(8,128)S(1)}, u32[]{:S(2)}, u32[]{:S(2)}) collective-permute-start(f32[1,4,1,32,64]{4,3,2,1,0:T(8,128)S(1)} %get-tuple-element.88), channel_id=1, source_target_pairs={{0,1},{1,2},{2,3},{4,5},{5,6},{6,7},{8,9},{9,10},{10,11},{12,13},{... | collective-permute-start | bytes 98312 | tf_op jit(solution)/shard_map/ppermute | solution.py:23
  300.1 1.9 collective-permute-start.57
  302.2 6.3 %collective-permute-done.57 = f32[1,4,2,32,64]{4,3,2,1,0:T(8,128)S(1)} collective-permute-done((f32[1,4,2,32,64]{4,3,2,1,0:T(8,128)S(1)}, f32[1,4,2,32,64]{4,3,2,1,0:T(8,128)S(1)}, u32[]{:S(2)}, u32[]{:S(2)}) %collective-permute-start.57) | collective-permute-done | bytes 65568 | tf_op jit(solution)/shard_map/ppermute | solution.py:34
  309.1 1.9 collective-permute-start.60
  312.3 4.6 %collective-permute-start.62 = (f32[1,4,1,64,128]{4,3,2,1,0:T(8,128)S(1)}, f32[1,4,1,64,128]{4,3,2,1,0:T(8,128)S(1)}, u32[]{:S(2)}, u32[]{:S(2)}) collective-permute-start(f32[1,4,1,64,128]{4,3,2,1,0:T(8,128)S(1)} %get-tuple-element.40), channel_id=1, source_target_pairs={{0,1},{1,2},{2,3},{4,5},{5,6},{6,7},{8,9},{9,10},{10,11},{12,13},{... | collective-permute-start | bytes 393224 | tf_op jit(solution)/shard_map/ppermute | solution.py:23
  319.6 2.1 collective-permute-done.60
  322.2 1.9 collective-permute-start.63
  325.5 4.6 %collective-permute-start.65 = (f32[1,4,1,64,128]{4,3,2,1,0:T(8,128)S(1)}, f32[1,4,1,64,128]{4,3,2,1,0:T(8,128)S(1)}, u32[]{:S(2)}, u32[]{:S(2)}) collective-permute-start(f32[1,4,1,64,128]{4,3,2,1,0:T(8,128)S(1)} %get-tuple-element.36), channel_id=1, source_target_pairs={{0,1},{1,2},{2,3},{4,5},{5,6},{6,7},{8,9},{9,10},{10,11},{12,13},{... | collective-permute-start | bytes 393224 | tf_op jit(solution)/shard_map/ppermute | solution.py:23
  332.7 2.1 collective-permute-done.63
  (240 shorter events, 80.5 us)
Async XLA Ops:
  3.2 12.6 %collective-permute-start = (f32[1,4,4,64,128]{4,3,2,1,0:T(8,128)S(1)}, f32[1,4,4,64,128]{4,3,2,1,0:T(8,128)S(1)}, u32[]{:S(2)}, u32[]{:S(2)}) collective-permute-start(f32[1,4,4,64,128]{4,3,2,1,0:T(8,128)S(1)} %get-tuple-element.9), channel_id=1, source_target_pairs={{0,4},{4,8},{8,12},{12,16},{16,20},{20,24},{24,28},{28,32},{32,36}... | collective-permute-start | bytes 1572872 | tf_op jit(solution)/shard_map/ppermute | solution.py:34
  5.2 7.4 %collective-permute-start.1 = (f32[1,4,1,64,128]{4,3,2,1,0:T(8,128)S(1)}, f32[1,4,1,64,128]{4,3,2,1,0:T(8,128)S(1)}, u32[]{:S(2)}, u32[]{:S(2)}) collective-permute-start(f32[1,4,1,64,128]{4,3,2,1,0:T(8,128)S(1)} %get-tuple-element.67), channel_id=1, source_target_pairs={{1,0},{2,1},{3,2},{5,4},{6,5},{7,6},{9,8},{10,9},{11,10},{13,12},{... | collective-permute-start | bytes 393224 | tf_op jit(solution)/shard_map/ppermute | solution.py:26
  6.5 7.8 %collective-permute-start.2 = (f32[1,4,1,64,128]{4,3,2,1,0:T(8,128)S(1)}, f32[1,4,1,64,128]{4,3,2,1,0:T(8,128)S(1)}, u32[]{:S(2)}, u32[]{:S(2)}) collective-permute-start(f32[1,4,1,64,128]{4,3,2,1,0:T(8,128)S(1)} %get-tuple-element.68), channel_id=1, source_target_pairs={{0,1},{1,2},{2,3},{4,5},{5,6},{6,7},{8,9},{9,10},{10,11},{12,13},{... | collective-permute-start | bytes 393224 | tf_op jit(solution)/shard_map/ppermute | solution.py:23
  16.4 15.7 %collective-permute-start.3 = (f32[1,4,4,64,128]{4,3,2,1,0:T(8,128)S(1)}, f32[1,4,4,64,128]{4,3,2,1,0:T(8,128)S(1)}, u32[]{:S(2)}, u32[]{:S(2)}) collective-permute-start(f32[1,4,4,64,128]{4,3,2,1,0:T(8,128)S(1)} %fusion.119), channel_id=1, source_target_pairs={{0,4},{4,8},{8,12},{12,16},{16,20},{20,24},{24,28},{28,32},{32,36}... | collective-permute-start | bytes 1572872 | tf_op jit(solution)/shard_map/ppermute | solution.py:34
  18.3 13.6 %collective-permute-start.4 = (f32[1,4,1,64,128]{4,3,2,1,0:T(8,128)S(1)}, f32[1,4,1,64,128]{4,3,2,1,0:T(8,128)S(1)}, u32[]{:S(2)}, u32[]{:S(2)}) collective-permute-start(f32[1,4,1,64,128]{4,3,2,1,0:T(8,128)S(1)} %get-tuple-element.63), channel_id=1, source_target_pairs={{1,0},{2,1},{3,2},{5,4},{6,5},{7,6},{9,8},{10,9},{11,10},{13,12},{... | collective-permute-start | bytes 393224 | tf_op jit(solution)/shard_map/ppermute | solution.py:26
  19.6 12.3 %collective-permute-start.5 = (f32[1,4,1,64,128]{4,3,2,1,0:T(8,128)S(1)}, f32[1,4,1,64,128]{4,3,2,1,0:T(8,128)S(1)}, u32[]{:S(2)}, u32[]{:S(2)}) collective-permute-start(f32[1,4,1,64,128]{4,3,2,1,0:T(8,128)S(1)} %get-tuple-element.64), channel_id=1, source_target_pairs={{0,1},{1,2},{2,3},{4,5},{5,6},{6,7},{8,9},{9,10},{10,11},{12,13},{... | collective-permute-start | bytes 393224 | tf_op jit(solution)/shard_map/ppermute | solution.py:23
  24.4 3.6 %collective-permute-start.19 = (f32[1,512]{1,0:T(1,128)S(1)}, f32[1,512]{1,0:T(1,128)S(1)}, u32[]{:S(2)}, u32[]{:S(2)}) collective-permute-start(f32[1,512]{1,0:T(1,128)S(1)} %reshape.1455), channel_id=1, source_target_pairs={{0,1},{1,0},{2,3},{3,2},{4,5},{5,4},{6,7},{7,6},{8,9},{9,8},{10,11... | collective-permute-start | bytes 6152 | tf_op jit(solution)/shard_map/ppermute | solution.py:196
  28.0 25.4 %collective-permute-start.20 = (f32[1,1024]{1,0:T(1,128)S(1)}, f32[1,1024]{1,0:T(1,128)S(1)}, u32[]{:S(2)}, u32[]{:S(2)}) collective-permute-start(f32[1,1024]{1,0:T(1,128)S(1)} %broadcast_select_fusion.5), channel_id=1, source_target_pairs={{0,2},{1,3},{2,0},{3,1},{4,6},{5,7},{6,4},{7,5},{8,10},{9,11},{10,... | collective-permute-start | bytes 12296 | tf_op jit(solution)/shard_map/ppermute | solution.py:196
  33.1 7.8 %collective-permute-start.7 = (f32[1,4,1,32,64]{4,3,2,1,0:T(8,128)S(1)}, f32[1,4,1,32,64]{4,3,2,1,0:T(8,128)S(1)}, u32[]{:S(2)}, u32[]{:S(2)}) collective-permute-start(f32[1,4,1,32,64]{4,3,2,1,0:T(8,128)S(1)} %get-tuple-element.107), channel_id=1, source_target_pairs={{1,0},{2,1},{3,2},{5,4},{6,5},{7,6},{9,8},{10,9},{11,10},{13,12},{... | collective-permute-start | bytes 98312 | tf_op jit(solution)/shard_map/ppermute | solution.py:26
  34.4 6.5 %collective-permute-start.8 = (f32[1,4,1,32,64]{4,3,2,1,0:T(8,128)S(1)}, f32[1,4,1,32,64]{4,3,2,1,0:T(8,128)S(1)}, u32[]{:S(2)}, u32[]{:S(2)}) collective-permute-start(f32[1,4,1,32,64]{4,3,2,1,0:T(8,128)S(1)} %get-tuple-element.108), channel_id=1, source_target_pairs={{0,1},{1,2},{2,3},{4,5},{5,6},{6,7},{8,9},{9,10},{10,11},{12,13},{... | collective-permute-start | bytes 98312 | tf_op jit(solution)/shard_map/ppermute | solution.py:23
  39.0 8.4 %collective-permute-start.6 = (f32[1,4,2,32,64]{4,3,2,1,0:T(8,128)S(1)}, f32[1,4,2,32,64]{4,3,2,1,0:T(8,128)S(1)}, u32[]{:S(2)}, u32[]{:S(2)}) collective-permute-start(f32[1,4,2,32,64]{4,3,2,1,0:T(8,128)S(1)} %fusion.388), channel_id=1, source_target_pairs={{0,4},{4,8},{8,12},{12,16},{16,20},{20,24},{24,28},{28,32},{32,36}... | collective-permute-start | bytes 196616 | tf_op jit(solution)/shard_map/ppermute | solution.py:34
  47.5 8.4 %collective-permute-start.10 = (f32[1,4,1,32,64]{4,3,2,1,0:T(8,128)S(1)}, f32[1,4,1,32,64]{4,3,2,1,0:T(8,128)S(1)}, u32[]{:S(2)}, u32[]{:S(2)}) collective-permute-start(f32[1,4,1,32,64]{4,3,2,1,0:T(8,128)S(1)} %get-tuple-element.103), channel_id=1, source_target_pairs={{1,0},{2,1},{3,2},{5,4},{6,5},{7,6},{9,8},{10,9},{11,10},{13,12},{... | collective-permute-start | bytes 98312 | tf_op jit(solution)/shard_map/ppermute | solution.py:26
  48.8 7.1 %collective-permute-start.11 = (f32[1,4,1,32,64]{4,3,2,1,0:T(8,128)S(1)}, f32[1,4,1,32,64]{4,3,2,1,0:T(8,128)S(1)}, u32[]{:S(2)}, u32[]{:S(2)}) collective-permute-start(f32[1,4,1,32,64]{4,3,2,1,0:T(8,128)S(1)} %get-tuple-element.104), channel_id=1, source_target_pairs={{0,1},{1,2},{2,3},{4,5},{5,6},{6,7},{8,9},{9,10},{10,11},{12,13},{... | collective-permute-start | bytes 98312 | tf_op jit(solution)/shard_map/ppermute | solution.py:23
  53.4 10.9 %collective-permute-start.21 = (f32[1,2048]{1,0:T(1,128)S(1)}, f32[1,2048]{1,0:T(1,128)S(1)}, u32[]{:S(2)}, u32[]{:S(2)}) collective-permute-start(f32[1,2048]{1,0:T(1,128)S(1)} %broadcast_select_fusion.4), channel_id=1, source_target_pairs={{0,4},{4,0},{8,12},{12,8},{16,20},{20,16},{24,28},{28,24},{32,36},... | collective-permute-start | bytes 24584 | tf_op jit(solution)/shard_map/ppermute | solution.py:196
  53.5 8.4 %collective-permute-start.9 = (f32[1,4,2,32,64]{4,3,2,1,0:T(8,128)S(1)}, f32[1,4,2,32,64]{4,3,2,1,0:T(8,128)S(1)}, u32[]{:S(2)}, u32[]{:S(2)}) collective-permute-start(f32[1,4,2,32,64]{4,3,2,1,0:T(8,128)S(1)} %fusion.207), channel_id=1, source_target_pairs={{0,4},{4,8},{8,12},{12,16},{16,20},{20,24},{24,28},{28,32},{32,36}... | collective-permute-start | bytes 196616 | tf_op jit(solution)/shard_map/ppermute | solution.py:34
  62.5 3.7 %collective-permute-start.12 = (f32[1,2048]{1,0:T(1,128)S(1)}, f32[1,2048]{1,0:T(1,128)S(1)}, u32[]{:S(2)}, u32[]{:S(2)}) collective-permute-start(f32[1,2048]{1,0:T(1,128)S(1)} %reshape.1453), channel_id=1, source_target_pairs={{0,1},{1,0},{2,3},{3,2},{4,5},{5,4},{6,7},{7,6},{8,9},{9,8},{10,11... | collective-permute-start | bytes 24584 | tf_op jit(solution)/shard_map/ppermute | solution.py:196
  64.3 7.4 %collective-permute-start.22 = (f32[2,2048]{1,0:T(2,128)S(1)}, f32[2,2048]{1,0:T(2,128)S(1)}, u32[]{:S(2)}, u32[]{:S(2)}) collective-permute-start(f32[2,2048]{1,0:T(2,128)S(1)} %maximum_select_fusion.24), channel_id=1, source_target_pairs={{0,8},{4,12},{8,0},{12,4},{16,24},{20,28},{24,16},{28,20},{32,40},... | collective-permute-start | bytes 49160 | tf_op jit(solution)/shard_map/ppermute | solution.py:196
  66.3 5.3 %collective-permute-start.13 = (f32[1,4096]{1,0:T(1,128)S(1)}, f32[1,4096]{1,0:T(1,128)S(1)}, u32[]{:S(2)}, u32[]{:S(2)}) collective-permute-start(f32[1,4096]{1,0:T(1,128)S(1)} %broadcast_select_fusion.3), channel_id=1, source_target_pairs={{0,2},{1,3},{2,0},{3,1},{4,6},{5,7},{6,4},{7,5},{8,10},{9,11},{10,... | collective-permute-start | bytes 49160 | tf_op jit(solution)/shard_map/ppermute | solution.py:196
  71.8 8.3 %collective-permute-start.23 = (f32[4,2048]{1,0:T(4,128)S(1)}, f32[4,2048]{1,0:T(4,128)S(1)}, u32[]{:S(2)}, u32[]{:S(2)}) collective-permute-start(f32[4,2048]{1,0:T(4,128)S(1)} %maximum_select_fusion.22), channel_id=1, source_target_pairs={{0,16},{4,20},{8,24},{12,28},{16,0},{20,4},{24,8},{28,12},{32,48},... | collective-permute-start | bytes 98312 | tf_op jit(solution)/shard_map/ppermute | solution.py:196
  73.0 4.3 %collective-permute-start.15 = (f32[2,8192]{1,0:T(2,128)S(1)}, f32[2,8192]{1,0:T(2,128)S(1)}, u32[]{:S(2)}, u32[]{:S(2)}) collective-permute-start(f32[2,8192]{1,0:T(2,128)S(1)} %maximum_select_fusion.17), channel_id=1, source_target_pairs={{0,8},{4,12},{8,0},{12,4},{16,24},{20,28},{24,16},{28,20},{32,40},... | collective-permute-start | bytes 196616 | tf_op jit(solution)/shard_map/ppermute | solution.py:196
  77.5 6.6 %collective-permute-start.16 = (f32[4,8192]{1,0:T(4,128)S(1)}, f32[4,8192]{1,0:T(4,128)S(1)}, u32[]{:S(2)}, u32[]{:S(2)}) collective-permute-start(f32[4,8192]{1,0:T(4,128)S(1)} %maximum_select_fusion.12), channel_id=1, source_target_pairs={{0,16},{4,20},{8,24},{12,28},{16,0},{20,4},{24,8},{28,12},{32,48},... | collective-permute-start | bytes 393224 | tf_op jit(solution)/shard_map/ppermute | solution.py:196
  80.1 4.3 %collective-permute-start.24 = (f32[8,2048]{1,0:T(8,128)S(1)}, f32[8,2048]{1,0:T(8,128)S(1)}, u32[]{:S(2)}, u32[]{:S(2)}) collective-permute-start(f32[8,2048]{1,0:T(8,128)S(1)} %maximum_select_fusion.19), channel_id=1, source_target_pairs={{0,32},{4,36},{8,40},{12,44},{16,48},{20,52},{24,56},{28,60},{32,0... | collective-permute-start | bytes 196616 | tf_op jit(solution)/shard_map/ppermute | solution.py:196
  84.1 7.9 %collective-permute-start.17 = (f32[8,8192]{1,0:T(8,128)S(1)}, f32[8,8192]{1,0:T(8,128)S(1)}, u32[]{:S(2)}, u32[]{:S(2)}) collective-permute-start(f32[8,8192]{1,0:T(8,128)S(1)} %maximum_select_fusion.7), channel_id=1, source_target_pairs={{0,32},{4,36},{8,40},{12,44},{16,48},{20,52},{24,56},{28,60},{32,0... | collective-permute-start | bytes 786440 | tf_op jit(solution)/shard_map/ppermute | solution.py:196
  84.5 11.6 %collective-permute-start.25 = (f32[16,2048]{1,0:T(8,128)S(1)}, f32[16,2048]{1,0:T(8,128)S(1)}, u32[]{:S(2)}, u32[]{:S(2)}) collective-permute-start(f32[16,2048]{1,0:T(8,128)S(1)} %maximum_select_fusion.14), channel_id=1, source_target_pairs={{0,64},{4,68},{8,72},{12,76},{16,80},{20,84},{24,88},{28,92},{32,9... | collective-permute-start | bytes 393224 | tf_op jit(solution)/shard_map/ppermute | solution.py:196
  92.8 12.8 %collective-permute-start.18 = (f32[16,8192]{1,0:T(8,128)}, f32[16,8192]{1,0:T(8,128)}, u32[]{:S(2)}, u32[]{:S(2)}) collective-permute-start(f32[16,8192]{1,0:T(8,128)} %maximum_select_fusion.3), channel_id=1, source_target_pairs={{0,64},{4,68},{8,72},{12,76},{16,80},{20,84},{24,88},{28,92},{32,9... | collective-permute-start | bytes 1572872 | tf_op jit(solution)/shard_map/ppermute | solution.py:196
  125.2 7.8 %collective-permute-start.27 = (f32[1,4,1,32,64]{4,3,2,1,0:T(8,128)S(1)}, f32[1,4,1,32,64]{4,3,2,1,0:T(8,128)S(1)}, u32[]{:S(2)}, u32[]{:S(2)}) collective-permute-start(f32[1,4,1,32,64]{4,3,2,1,0:T(8,128)S(1)} %get-tuple-element.99), channel_id=1, source_target_pairs={{1,0},{2,1},{3,2},{5,4},{6,5},{7,6},{9,8},{10,9},{11,10},{13,12},{... | collective-permute-start | bytes 98312 | tf_op jit(solution)/shard_map/ppermute | solution.py:26
  126.5 6.5 %collective-permute-start.28 = (f32[1,4,1,32,64]{4,3,2,1,0:T(8,128)S(1)}, f32[1,4,1,32,64]{4,3,2,1,0:T(8,128)S(1)}, u32[]{:S(2)}, u32[]{:S(2)}) collective-permute-start(f32[1,4,1,32,64]{4,3,2,1,0:T(8,128)S(1)} %get-tuple-element.100), channel_id=1, source_target_pairs={{0,1},{1,2},{2,3},{4,5},{5,6},{6,7},{8,9},{9,10},{10,11},{12,13},{... | collective-permute-start | bytes 98312 | tf_op jit(solution)/shard_map/ppermute | solution.py:23
  131.1 8.4 %collective-permute-start.26 = (f32[1,4,2,32,64]{4,3,2,1,0:T(8,128)S(1)}, f32[1,4,2,32,64]{4,3,2,1,0:T(8,128)S(1)}, u32[]{:S(2)}, u32[]{:S(2)}) collective-permute-start(f32[1,4,2,32,64]{4,3,2,1,0:T(8,128)S(1)} %fusion.221), channel_id=1, source_target_pairs={{0,4},{4,8},{8,12},{12,16},{16,20},{20,24},{24,28},{28,32},{32,36}... | collective-permute-start | bytes 196616 | tf_op jit(solution)/shard_map/ppermute | solution.py:34
  140.0 12.6 %collective-permute-start.29 = (f32[1,4,4,64,128]{4,3,2,1,0:T(8,128)S(1)}, f32[1,4,4,64,128]{4,3,2,1,0:T(8,128)S(1)}, u32[]{:S(2)}, u32[]{:S(2)}) collective-permute-start(f32[1,4,4,64,128]{4,3,2,1,0:T(8,128)S(1)} %add.517), channel_id=1, source_target_pairs={{0,4},{4,8},{8,12},{12,16},{16,20},{20,24},{24,28},{28,32},{32,36}... | collective-permute-start | bytes 1572872 | tf_op jit(solution)/shard_map/ppermute | solution.py:34
  142.1 6.9 %collective-permute-start.30 = (f32[1,4,1,64,128]{4,3,2,1,0:T(8,128)S(1)}, f32[1,4,1,64,128]{4,3,2,1,0:T(8,128)S(1)}, u32[]{:S(2)}, u32[]{:S(2)}) collective-permute-start(f32[1,4,1,64,128]{4,3,2,1,0:T(8,128)S(1)} %get-tuple-element.59), channel_id=1, source_target_pairs={{1,0},{2,1},{3,2},{5,4},{6,5},{7,6},{9,8},{10,9},{11,10},{13,12},{... | collective-permute-start | bytes 393224 | tf_op jit(solution)/shard_map/ppermute | solution.py:26
  143.4 7.1 %collective-permute-start.31 = (f32[1,4,1,64,128]{4,3,2,1,0:T(8,128)S(1)}, f32[1,4,1,64,128]{4,3,2,1,0:T(8,128)S(1)}, u32[]{:S(2)}, u32[]{:S(2)}) collective-permute-start(f32[1,4,1,64,128]{4,3,2,1,0:T(8,128)S(1)} %get-tuple-element.60), channel_id=1, source_target_pairs={{0,1},{1,2},{2,3},{4,5},{5,6},{6,7},{8,9},{9,10},{10,11},{12,13},{... | collective-permute-start | bytes 393224 | tf_op jit(solution)/shard_map/ppermute | solution.py:23
  153.2 12.6 %collective-permute-start.32 = (f32[1,4,4,64,128]{4,3,2,1,0:T(8,128)S(1)}, f32[1,4,4,64,128]{4,3,2,1,0:T(8,128)S(1)}, u32[]{:S(2)}, u32[]{:S(2)}) collective-permute-start(f32[1,4,4,64,128]{4,3,2,1,0:T(8,128)S(1)} %fusion.93), channel_id=1, source_target_pairs={{0,4},{4,8},{8,12},{12,16},{16,20},{20,24},{24,28},{28,32},{32,36}... | collective-permute-start | bytes 1572872 | tf_op jit(solution)/shard_map/ppermute | solution.py:34
  155.1 6.9 %collective-permute-start.33 = (f32[1,4,1,64,128]{4,3,2,1,0:T(8,128)S(1)}, f32[1,4,1,64,128]{4,3,2,1,0:T(8,128)S(1)}, u32[]{:S(2)}, u32[]{:S(2)}) collective-permute-start(f32[1,4,1,64,128]{4,3,2,1,0:T(8,128)S(1)} %get-tuple-element.55), channel_id=1, source_target_pairs={{1,0},{2,1},{3,2},{5,4},{6,5},{7,6},{9,8},{10,9},{11,10},{13,12},{... | collective-permute-start | bytes 393224 | tf_op jit(solution)/shard_map/ppermute | solution.py:26
  156.4 7.1 %collective-permute-start.34 = (f32[1,4,1,64,128]{4,3,2,1,0:T(8,128)S(1)}, f32[1,4,1,64,128]{4,3,2,1,0:T(8,128)S(1)}, u32[]{:S(2)}, u32[]{:S(2)}) collective-permute-start(f32[1,4,1,64,128]{4,3,2,1,0:T(8,128)S(1)} %get-tuple-element.56), channel_id=1, source_target_pairs={{0,1},{1,2},{2,3},{4,5},{5,6},{6,7},{8,9},{9,10},{10,11},{12,13},{... | collective-permute-start | bytes 393224 | tf_op jit(solution)/shard_map/ppermute | solution.py:23
  166.3 12.6 %collective-permute-start.35 = (f32[1,4,4,64,128]{4,3,2,1,0:T(8,128)S(1)}, f32[1,4,4,64,128]{4,3,2,1,0:T(8,128)S(1)}, u32[]{:S(2)}, u32[]{:S(2)}) collective-permute-start(f32[1,4,4,64,128]{4,3,2,1,0:T(8,128)S(1)} %fusion.79), channel_id=1, source_target_pairs={{0,4},{4,8},{8,12},{12,16},{16,20},{20,24},{24,28},{28,32},{32,36}... | collective-permute-start | bytes 1572872 | tf_op jit(solution)/shard_map/ppermute | solution.py:34
  168.3 6.9 %collective-permute-start.36 = (f32[1,4,1,64,128]{4,3,2,1,0:T(8,128)S(1)}, f32[1,4,1,64,128]{4,3,2,1,0:T(8,128)S(1)}, u32[]{:S(2)}, u32[]{:S(2)}) collective-permute-start(f32[1,4,1,64,128]{4,3,2,1,0:T(8,128)S(1)} %get-tuple-element.51), channel_id=1, source_target_pairs={{1,0},{2,1},{3,2},{5,4},{6,5},{7,6},{9,8},{10,9},{11,10},{13,12},{... | collective-permute-start | bytes 393224 | tf_op jit(solution)/shard_map/ppermute | solution.py:26
  169.6 7.1 %collective-permute-start.37 = (f32[1,4,1,64,128]{4,3,2,1,0:T(8,128)S(1)}, f32[1,4,1,64,128]{4,3,2,1,0:T(8,128)S(1)}, u32[]{:S(2)}, u32[]{:S(2)}) collective-permute-start(f32[1,4,1,64,128]{4,3,2,1,0:T(8,128)S(1)} %get-tuple-element.52), channel_id=1, source_target_pairs={{0,1},{1,2},{2,3},{4,5},{5,6},{6,7},{8,9},{9,10},{10,11},{12,13},{... | collective-permute-start | bytes 393224 | tf_op jit(solution)/shard_map/ppermute | solution.py:23
  179.5 12.6 %collective-permute-start.38 = (f32[1,4,4,64,128]{4,3,2,1,0:T(8,128)S(1)}, f32[1,4,4,64,128]{4,3,2,1,0:T(8,128)S(1)}, u32[]{:S(2)}, u32[]{:S(2)}) collective-permute-start(f32[1,4,4,64,128]{4,3,2,1,0:T(8,128)S(1)} %fusion.65), channel_id=1, source_target_pairs={{0,4},{4,8},{8,12},{12,16},{16,20},{20,24},{24,28},{28,32},{32,36}... | collective-permute-start | bytes 1572872 | tf_op jit(solution)/shard_map/ppermute | solution.py:34
  181.4 6.9 %collective-permute-start.39 = (f32[1,4,1,64,128]{4,3,2,1,0:T(8,128)S(1)}, f32[1,4,1,64,128]{4,3,2,1,0:T(8,128)S(1)}, u32[]{:S(2)}, u32[]{:S(2)}) collective-permute-start(f32[1,4,1,64,128]{4,3,2,1,0:T(8,128)S(1)} %get-tuple-element.47), channel_id=1, source_target_pairs={{1,0},{2,1},{3,2},{5,4},{6,5},{7,6},{9,8},{10,9},{11,10},{13,12},{... | collective-permute-start | bytes 393224 | tf_op jit(solution)/shard_map/ppermute | solution.py:26
  182.7 7.1 %collective-permute-start.40 = (f32[1,4,1,64,128]{4,3,2,1,0:T(8,128)S(1)}, f32[1,4,1,64,128]{4,3,2,1,0:T(8,128)S(1)}, u32[]{:S(2)}, u32[]{:S(2)}) collective-permute-start(f32[1,4,1,64,128]{4,3,2,1,0:T(8,128)S(1)} %get-tuple-element.48), channel_id=1, source_target_pairs={{0,1},{1,2},{2,3},{4,5},{5,6},{6,7},{8,9},{9,10},{10,11},{12,13},{... | collective-permute-start | bytes 393224 | tf_op jit(solution)/shard_map/ppermute | solution.py:23
  192.7 12.6 %collective-permute-start.41 = (f32[1,4,4,64,128]{4,3,2,1,0:T(8,128)S(1)}, f32[1,4,4,64,128]{4,3,2,1,0:T(8,128)S(1)}, u32[]{:S(2)}, u32[]{:S(2)}) collective-permute-start(f32[1,4,4,64,128]{4,3,2,1,0:T(8,128)S(1)} %fusion.51), channel_id=1, source_target_pairs={{0,4},{4,8},{8,12},{12,16},{16,20},{20,24},{24,28},{28,32},{32,36}... | collective-permute-start | bytes 1572872 | tf_op jit(solution)/shard_map/ppermute | solution.py:34
  194.6 6.9 %collective-permute-start.42 = (f32[1,4,1,64,128]{4,3,2,1,0:T(8,128)S(1)}, f32[1,4,1,64,128]{4,3,2,1,0:T(8,128)S(1)}, u32[]{:S(2)}, u32[]{:S(2)}) collective-permute-start(f32[1,4,1,64,128]{4,3,2,1,0:T(8,128)S(1)} %get-tuple-element.43), channel_id=1, source_target_pairs={{1,0},{2,1},{3,2},{5,4},{6,5},{7,6},{9,8},{10,9},{11,10},{13,12},{... | collective-permute-start | bytes 393224 | tf_op jit(solution)/shard_map/ppermute | solution.py:26
  195.9 7.1 %collective-permute-start.43 = (f32[1,4,1,64,128]{4,3,2,1,0:T(8,128)S(1)}, f32[1,4,1,64,128]{4,3,2,1,0:T(8,128)S(1)}, u32[]{:S(2)}, u32[]{:S(2)}) collective-permute-start(f32[1,4,1,64,128]{4,3,2,1,0:T(8,128)S(1)} %get-tuple-element.44), channel_id=1, source_target_pairs={{0,1},{1,2},{2,3},{4,5},{5,6},{6,7},{8,9},{9,10},{10,11},{12,13},{... | collective-permute-start | bytes 393224 | tf_op jit(solution)/shard_map/ppermute | solution.py:23
  206.2 7.8 %collective-permute-start.45 = (f32[1,4,1,32,64]{4,3,2,1,0:T(8,128)S(1)}, f32[1,4,1,32,64]{4,3,2,1,0:T(8,128)S(1)}, u32[]{:S(2)}, u32[]{:S(2)}) collective-permute-start(f32[1,4,1,32,64]{4,3,2,1,0:T(8,128)S(1)} %get-tuple-element.95), channel_id=1, source_target_pairs={{1,0},{2,1},{3,2},{5,4},{6,5},{7,6},{9,8},{10,9},{11,10},{13,12},{... | collective-permute-start | bytes 98312 | tf_op jit(solution)/shard_map/ppermute | solution.py:26
  207.5 6.5 %collective-permute-start.46 = (f32[1,4,1,32,64]{4,3,2,1,0:T(8,128)S(1)}, f32[1,4,1,32,64]{4,3,2,1,0:T(8,128)S(1)}, u32[]{:S(2)}, u32[]{:S(2)}) collective-permute-start(f32[1,4,1,32,64]{4,3,2,1,0:T(8,128)S(1)} %get-tuple-element.96), channel_id=1, source_target_pairs={{0,1},{1,2},{2,3},{4,5},{5,6},{6,7},{8,9},{9,10},{10,11},{12,13},{... | collective-permute-start | bytes 98312 | tf_op jit(solution)/shard_map/ppermute | solution.py:23
  212.1 8.4 %collective-permute-start.44 = (f32[1,4,2,32,64]{4,3,2,1,0:T(8,128)S(1)}, f32[1,4,2,32,64]{4,3,2,1,0:T(8,128)S(1)}, u32[]{:S(2)}, u32[]{:S(2)}) collective-permute-start(f32[1,4,2,32,64]{4,3,2,1,0:T(8,128)S(1)} %fusion.389), channel_id=1, source_target_pairs={{0,4},{4,8},{8,12},{12,16},{16,20},{20,24},{24,28},{28,32},{32,36}... | collective-permute-start | bytes 196616 | tf_op jit(solution)/shard_map/ppermute | solution.py:34
  220.7 7.8 %collective-permute-start.48 = (f32[1,4,1,32,64]{4,3,2,1,0:T(8,128)S(1)}, f32[1,4,1,32,64]{4,3,2,1,0:T(8,128)S(1)}, u32[]{:S(2)}, u32[]{:S(2)}) collective-permute-start(f32[1,4,1,32,64]{4,3,2,1,0:T(8,128)S(1)} %get-tuple-element.91), channel_id=1, source_target_pairs={{1,0},{2,1},{3,2},{5,4},{6,5},{7,6},{9,8},{10,9},{11,10},{13,12},{... | collective-permute-start | bytes 98312 | tf_op jit(solution)/shard_map/ppermute | solution.py:26
  222.0 6.5 %collective-permute-start.49 = (f32[1,4,1,32,64]{4,3,2,1,0:T(8,128)S(1)}, f32[1,4,1,32,64]{4,3,2,1,0:T(8,128)S(1)}, u32[]{:S(2)}, u32[]{:S(2)}) collective-permute-start(f32[1,4,1,32,64]{4,3,2,1,0:T(8,128)S(1)} %get-tuple-element.92), channel_id=1, source_target_pairs={{0,1},{1,2},{2,3},{4,5},{5,6},{6,7},{8,9},{9,10},{10,11},{12,13},{... | collective-permute-start | bytes 98312 | tf_op jit(solution)/shard_map/ppermute | solution.py:23
  226.5 8.4 %collective-permute-start.47 = (f32[1,4,2,32,64]{4,3,2,1,0:T(8,128)S(1)}, f32[1,4,2,32,64]{4,3,2,1,0:T(8,128)S(1)}, u32[]{:S(2)}, u32[]{:S(2)}) collective-permute-start(f32[1,4,2,32,64]{4,3,2,1,0:T(8,128)S(1)} %fusion.166), channel_id=1, source_target_pairs={{0,4},{4,8},{8,12},{12,16},{16,20},{20,24},{24,28},{28,32},{32,36}... | collective-permute-start | bytes 196616 | tf_op jit(solution)/shard_map/ppermute | solution.py:34
  235.5 3.7 %collective-permute-start.50 = (f32[1,2048]{1,0:T(1,128)S(1)}, f32[1,2048]{1,0:T(1,128)S(1)}, u32[]{:S(2)}, u32[]{:S(2)}) collective-permute-start(f32[1,2048]{1,0:T(1,128)S(1)} %reshape.1465), channel_id=1, source_target_pairs={{0,1},{1,0},{2,3},{3,2},{4,5},{5,4},{6,7},{7,6},{8,9},{9,8},{10,11... | collective-permute-start | bytes 24584 | tf_op jit(solution)/shard_map/ppermute | solution.py:196
  239.3 5.3 %collective-permute-start.51 = (f32[1,4096]{1,0:T(1,128)S(1)}, f32[1,4096]{1,0:T(1,128)S(1)}, u32[]{:S(2)}, u32[]{:S(2)}) collective-permute-start(f32[1,4096]{1,0:T(1,128)S(1)} %broadcast_select_fusion.2), channel_id=1, source_target_pairs={{0,2},{1,3},{2,0},{3,1},{4,6},{5,7},{6,4},{7,5},{8,10},{9,11},{10,... | collective-permute-start | bytes 49160 | tf_op jit(solution)/shard_map/ppermute | solution.py:196
  246.1 4.3 %collective-permute-start.53 = (f32[2,8192]{1,0:T(2,128)S(1)}, f32[2,8192]{1,0:T(2,128)S(1)}, u32[]{:S(2)}, u32[]{:S(2)}) collective-permute-start(f32[2,8192]{1,0:T(2,128)S(1)} %maximum_select_fusion.20), channel_id=1, source_target_pairs={{0,8},{4,12},{8,0},{12,4},{16,24},{20,28},{24,16},{28,20},{32,40},... | collective-permute-start | bytes 196616 | tf_op jit(solution)/shard_map/ppermute | solution.py:196
  250.5 6.6 %collective-permute-start.54 = (f32[4,8192]{1,0:T(4,128)S(1)}, f32[4,8192]{1,0:T(4,128)S(1)}, u32[]{:S(2)}, u32[]{:S(2)}) collective-permute-start(f32[4,8192]{1,0:T(4,128)S(1)} %maximum_select_fusion.16), channel_id=1, source_target_pairs={{0,16},{4,20},{8,24},{12,28},{16,0},{20,4},{24,8},{28,12},{32,48},... | collective-permute-start | bytes 393224 | tf_op jit(solution)/shard_map/ppermute | solution.py:196
  257.2 6.5 %collective-permute-start.55 = (f32[8,8192]{1,0:T(8,128)S(1)}, f32[8,8192]{1,0:T(8,128)S(1)}, u32[]{:S(2)}, u32[]{:S(2)}) collective-permute-start(f32[8,8192]{1,0:T(8,128)S(1)} %maximum_select_fusion.10), channel_id=1, source_target_pairs={{0,32},{4,36},{8,40},{12,44},{16,48},{20,52},{24,56},{28,60},{32,0... | collective-permute-start | bytes 786440 | tf_op jit(solution)/shard_map/ppermute | solution.py:196
  263.6 12.1 %collective-permute-start.56 = (f32[16,8192]{1,0:T(8,128)S(1)}, f32[16,8192]{1,0:T(8,128)S(1)}, u32[]{:S(2)}, u32[]{:S(2)}) collective-permute-start(f32[16,8192]{1,0:T(8,128)S(1)} %maximum_select_fusion.5), channel_id=1, source_target_pairs={{0,64},{4,68},{8,72},{12,76},{16,80},{20,84},{24,88},{28,92},{32,9... | collective-permute-start | bytes 1572872 | tf_op jit(solution)/shard_map/ppermute | solution.py:196
  294.3 7.8 %collective-permute-start.58 = (f32[1,4,1,32,64]{4,3,2,1,0:T(8,128)S(1)}, f32[1,4,1,32,64]{4,3,2,1,0:T(8,128)S(1)}, u32[]{:S(2)}, u32[]{:S(2)}) collective-permute-start(f32[1,4,1,32,64]{4,3,2,1,0:T(8,128)S(1)} %get-tuple-element.87), channel_id=1, source_target_pairs={{1,0},{2,1},{3,2},{5,4},{6,5},{7,6},{9,8},{10,9},{11,10},{13,12},{... | collective-permute-start | bytes 98312 | tf_op jit(solution)/shard_map/ppermute | solution.py:26
  295.6 6.5 %collective-permute-start.59 = (f32[1,4,1,32,64]{4,3,2,1,0:T(8,128)S(1)}, f32[1,4,1,32,64]{4,3,2,1,0:T(8,128)S(1)}, u32[]{:S(2)}, u32[]{:S(2)}) collective-permute-start(f32[1,4,1,32,64]{4,3,2,1,0:T(8,128)S(1)} %get-tuple-element.88), channel_id=1, source_target_pairs={{0,1},{1,2},{2,3},{4,5},{5,6},{6,7},{8,9},{9,10},{10,11},{12,13},{... | collective-permute-start | bytes 98312 | tf_op jit(solution)/shard_map/ppermute | solution.py:23
  300.1 8.4 %collective-permute-start.57 = (f32[1,4,2,32,64]{4,3,2,1,0:T(8,128)S(1)}, f32[1,4,2,32,64]{4,3,2,1,0:T(8,128)S(1)}, u32[]{:S(2)}, u32[]{:S(2)}) collective-permute-start(f32[1,4,2,32,64]{4,3,2,1,0:T(8,128)S(1)} %fusion.233), channel_id=1, source_target_pairs={{0,4},{4,8},{8,12},{12,16},{16,20},{20,24},{24,28},{28,32},{32,36}... | collective-permute-start | bytes 196616 | tf_op jit(solution)/shard_map/ppermute | solution.py:34
  309.1 12.6 %collective-permute-start.60 = (f32[1,4,4,64,128]{4,3,2,1,0:T(8,128)S(1)}, f32[1,4,4,64,128]{4,3,2,1,0:T(8,128)S(1)}, u32[]{:S(2)}, u32[]{:S(2)}) collective-permute-start(f32[1,4,4,64,128]{4,3,2,1,0:T(8,128)S(1)} %add.567), channel_id=1, source_target_pairs={{0,4},{4,8},{8,12},{12,16},{16,20},{20,24},{24,28},{28,32},{32,36}... | collective-permute-start | bytes 1572872 | tf_op jit(solution)/shard_map/ppermute | solution.py:34
  311.0 7.2 %collective-permute-start.61 = (f32[1,4,1,64,128]{4,3,2,1,0:T(8,128)S(1)}, f32[1,4,1,64,128]{4,3,2,1,0:T(8,128)S(1)}, u32[]{:S(2)}, u32[]{:S(2)}) collective-permute-start(f32[1,4,1,64,128]{4,3,2,1,0:T(8,128)S(1)} %get-tuple-element.39), channel_id=1, source_target_pairs={{1,0},{2,1},{3,2},{5,4},{6,5},{7,6},{9,8},{10,9},{11,10},{13,12},{... | collective-permute-start | bytes 393224 | tf_op jit(solution)/shard_map/ppermute | solution.py:26
  312.3 7.1 %collective-permute-start.62 = (f32[1,4,1,64,128]{4,3,2,1,0:T(8,128)S(1)}, f32[1,4,1,64,128]{4,3,2,1,0:T(8,128)S(1)}, u32[]{:S(2)}, u32[]{:S(2)}) collective-permute-start(f32[1,4,1,64,128]{4,3,2,1,0:T(8,128)S(1)} %get-tuple-element.40), channel_id=1, source_target_pairs={{0,1},{1,2},{2,3},{4,5},{5,6},{6,7},{8,9},{9,10},{10,11},{12,13},{... | collective-permute-start | bytes 393224 | tf_op jit(solution)/shard_map/ppermute | solution.py:23
  322.2 12.6 %collective-permute-start.63 = (f32[1,4,4,64,128]{4,3,2,1,0:T(8,128)S(1)}, f32[1,4,4,64,128]{4,3,2,1,0:T(8,128)S(1)}, u32[]{:S(2)}, u32[]{:S(2)}) collective-permute-start(f32[1,4,4,64,128]{4,3,2,1,0:T(8,128)S(1)} %fusion.25), channel_id=1, source_target_pairs={{0,4},{4,8},{8,12},{12,16},{16,20},{20,24},{24,28},{28,32},{32,36}... | collective-permute-start | bytes 1572872 | tf_op jit(solution)/shard_map/ppermute | solution.py:34
  324.2 6.9 %collective-permute-start.64 = (f32[1,4,1,64,128]{4,3,2,1,0:T(8,128)S(1)}, f32[1,4,1,64,128]{4,3,2,1,0:T(8,128)S(1)}, u32[]{:S(2)}, u32[]{:S(2)}) collective-permute-start(f32[1,4,1,64,128]{4,3,2,1,0:T(8,128)S(1)} %get-tuple-element.35), channel_id=1, source_target_pairs={{1,0},{2,1},{3,2},{5,4},{6,5},{7,6},{9,8},{10,9},{11,10},{13,12},{... | collective-permute-start | bytes 393224 | tf_op jit(solution)/shard_map/ppermute | solution.py:26
  325.5 7.1 %collective-permute-start.65 = (f32[1,4,1,64,128]{4,3,2,1,0:T(8,128)S(1)}, f32[1,4,1,64,128]{4,3,2,1,0:T(8,128)S(1)}, u32[]{:S(2)}, u32[]{:S(2)}) collective-permute-start(f32[1,4,1,64,128]{4,3,2,1,0:T(8,128)S(1)} %get-tuple-element.36), channel_id=1, source_target_pairs={{0,1},{1,2},{2,3},{4,5},{5,6},{6,7},{8,9},{9,10},{10,11},{12,13},{... | collective-permute-start | bytes 393224 | tf_op jit(solution)/shard_map/ppermute | solution.py:23
  (4 other events, 16.5 us)

commit v17 on v16

--- a/solution.py
+++ b/solution.py
@@ -187,12 +187,18 @@
     return (whole_source, whole_metric)
 
 
-def gather_doubling(flat, axis, dim):
+def gather_doubling(flat, axis, dim, widest_first=False):
     size = lax.axis_size(axis)
     position = lax.axis_index(axis)
-    gathered = flat
+    steps = []
     step = 1
     while step < size:
+        steps.append(step)
+        step *= 2
+    if widest_first:
+        steps = steps[::-1]
+    gathered = flat
+    for step in steps:
         other = lax.ppermute(gathered, axis, [(i, i ^ step) for i in range(size)])
         lower = (position & step) == 0
         gathered = jnp.where(
@@ -200,13 +206,22 @@
             jnp.concatenate([gathered, other], axis=dim),
             jnp.concatenate([other, gathered], axis=dim),
         )
-        step *= 2
+    if widest_first:
+        count = len(steps)
+        shape = gathered.shape
+        split = shape[:dim] + (2,) * count + (shape[dim] // size,) + shape[dim + 1 :]
+        order = (
+            list(range(dim))
+            + list(range(dim + count - 1, dim - 1, -1))
+            + list(range(dim + count, len(split)))
+        )
+        gathered = gathered.reshape(split).transpose(order).reshape(shape)
     return gathered
 
 
 def gather_all(flat):
     across = gather_doubling(flat, "space", 1)
-    whole = gather_doubling(across, "tm", 0)
+    whole = gather_doubling(across, "tm", 0, widest_first=True)
     return whole.reshape(-1, flat.shape[1])
 
 

time: 338 us -> 337 us (level)
  local copies, waits for them, and re-layouts: 10.1 us -> 16.7 us
  waiting for transfers between devices: 135 us -> 131 us
    ppermute x21, waiting for transfers between devices: 61.2 us -> 52.2 us  [gather_doubling(): other = lax.ppermute(gathered, axis, [(i, i ^ step) for i in range(size)])]
    another operation x2 -> x5, local copies, waits for them, and re-layouts: 0.16 us -> 4.2 us  [the longest x2 3.77 us: assemble(): whole_source.transpose(0, 2, 1, 4, 3, 5)]
  transfers between devices with their start and end apart: 66 -> 66, of which waited for: 46 -> 48; matrix products, arithmetic and copies ran while one was open for 3% -> 2% of each run, Pallas kernels for 0% -> 0%
where the time goes in v17:
time: 337 us; the launch traced here: 335 us
  starting transfers between devices  139 us (41%)
  waiting for transfers between devices  131 us (39%)
  Pallas kernels  28.4 us (8%)
  local copies, waits for them, and re-layouts  16.7 us (5%)
  other arithmetic  16.2 us (5%)
    ppermute x15, starting transfers between devices, with_halo(): lax.ppermute(lax.slice_in_dim(block, block.shape[dim] - width, None, axis...  68.3 us
    ppermute x15, waiting for transfers between devices, from_behind(): return lax.ppermute(array, axis, pairs)  54.2 us
    ppermute x21, waiting for transfers between devices, gather_doubling(): other = lax.ppermute(gathered, axis, [(i, i ^ step) for i in range(size)])  52.2 us
    ppermute x15, starting transfers between devices, from_behind(): return lax.ppermute(array, axis, pairs)  29 us
    pallas_call x2, Pallas kernels, coarse_solve(): pl.pallas_call(kernel, out_shape=jax.ShapeDtypeStruct(flat_source.shape,...  28.4 us
    ppermute x21, starting transfers between devices, gather_doubling(): other = lax.ppermute(gathered, axis, [(i, i ^ step) for i in range(size)])  22.3 us
    ppermute x15, starting transfers between devices, with_halo(): lax.ppermute(lax.slice_in_dim(block, 0, width, axis=dim), axis, backward)  19.5 us
    ppermute x15, waiting for transfers between devices, with_halo(): lax.ppermute(lax.slice_in_dim(block, block.shape[dim] - width, None, axis...  13.3 us
  transfers between devices with their start and end apart: 66, of which 48 were waited for; matrix products, arithmetic and copies ran while one was open for 2% of the time, Pallas kernels for 0%

profile of v17, /device:TPU:2, one launch (start us, length us, event | category | flops | bytes accessed | tf_op | source)
XLA Modules:
  0.0 335.1 jit_solution(707223450284876598)
XLA Ops:
  3.2 1.9 collective-permute-start
  6.6 4.6 %collective-permute-start.2 = (f32[1,4,1,64,128]{4,3,2,1,0:T(8,128)S(1)}, f32[1,4,1,64,128]{4,3,2,1,0:T(8,128)S(1)}, u32[]{:S(2)}, u32[]{:S(2)}) collective-permute-start(f32[1,4,1,64,128]{4,3,2,1,0:T(8,128)S(1)} %get-tuple-element.68), channel_id=1, source_target_pairs={{0,1},{1,2},{2,3},{4,5},{5,6},{6,7},{8,9},{9,10},{10,11},{12,13},{... | collective-permute-start | bytes 393224 | tf_op jit(solution)/shard_map/ppermute | solution.py:23
  16.4 1.9 collective-permute-start.3
  19.6 4.6 %collective-permute-start.5 = (f32[1,4,1,64,128]{4,3,2,1,0:T(8,128)S(1)}, f32[1,4,1,64,128]{4,3,2,1,0:T(8,128)S(1)}, u32[]{:S(2)}, u32[]{:S(2)}) collective-permute-start(f32[1,4,1,64,128]{4,3,2,1,0:T(8,128)S(1)} %get-tuple-element.64), channel_id=1, source_target_pairs={{0,1},{1,2},{2,3},{4,5},{5,6},{6,7},{8,9},{9,10},{10,11},{12,13},{... | collective-permute-start | bytes 393224 | tf_op jit(solution)/shard_map/ppermute | solution.py:23
  24.2 2.1 collective-permute-done.4
  31.3 4.5 %collective-permute-start.8 = (f32[1,4,1,32,64]{4,3,2,1,0:T(8,128)S(1)}, f32[1,4,1,32,64]{4,3,2,1,0:T(8,128)S(1)}, u32[]{:S(2)}, u32[]{:S(2)}) collective-permute-start(f32[1,4,1,32,64]{4,3,2,1,0:T(8,128)S(1)} %get-tuple-element.108), channel_id=1, source_target_pairs={{0,1},{1,2},{2,3},{4,5},{5,6},{6,7},{8,9},{9,10},{10,11},{12,13},{... | collective-permute-start | bytes 98312 | tf_op jit(solution)/shard_map/ppermute | solution.py:23
  35.9 1.9 collective-permute-start.6
  38.0 6.3 %collective-permute-done.6 = f32[1,4,2,32,64]{4,3,2,1,0:T(8,128)S(1)} collective-permute-done((f32[1,4,2,32,64]{4,3,2,1,0:T(8,128)S(1)}, f32[1,4,2,32,64]{4,3,2,1,0:T(8,128)S(1)}, u32[]{:S(2)}, u32[]{:S(2)}) %collective-permute-start.6) | collective-permute-done | bytes 65568 | tf_op jit(solution)/shard_map/ppermute | solution.py:34
  45.8 4.5 %collective-permute-start.11 = (f32[1,4,1,32,64]{4,3,2,1,0:T(8,128)S(1)}, f32[1,4,1,32,64]{4,3,2,1,0:T(8,128)S(1)}, u32[]{:S(2)}, u32[]{:S(2)}) collective-permute-start(f32[1,4,1,32,64]{4,3,2,1,0:T(8,128)S(1)} %get-tuple-element.104), channel_id=1, source_target_pairs={{0,1},{1,2},{2,3},{4,5},{5,6},{6,7},{8,9},{9,10},{10,11},{12,13},{... | collective-permute-start | bytes 98312 | tf_op jit(solution)/shard_map/ppermute | solution.py:23
  50.6 1.9 collective-permute-start.19
  52.6 1.9 collective-permute-start.9
  54.6 6.3 %collective-permute-done.9 = f32[1,4,2,32,64]{4,3,2,1,0:T(8,128)S(1)} collective-permute-done((f32[1,4,2,32,64]{4,3,2,1,0:T(8,128)S(1)}, f32[1,4,2,32,64]{4,3,2,1,0:T(8,128)S(1)}, u32[]{:S(2)}, u32[]{:S(2)}) %collective-permute-start.9) | collective-permute-done | bytes 65568 | tf_op jit(solution)/shard_map/ppermute | solution.py:34
  62.5 4.0 %collective-permute-start.20 = (f32[1,1024]{1,0:T(1,128)S(1)}, f32[1,1024]{1,0:T(1,128)S(1)}, u32[]{:S(2)}, u32[]{:S(2)}) collective-permute-start(f32[1,1024]{1,0:T(1,128)S(1)} %broadcast_select_fusion.5), channel_id=1, source_target_pairs={{0,2},{1,3},{2,0},{3,1},{4,6},{5,7},{6,4},{7,5},{8,10},{9,11},{10,... | collective-permute-start | bytes 12296 | tf_op jit(solution)/shard_map/ppermute | solution.py:202
  68.1 3.8 %collective-permute-done.13 = f32[1,4096]{1,0:T(1,128)S(1)} collective-permute-done((f32[1,4096]{1,0:T(1,128)S(1)}, f32[1,4096]{1,0:T(1,128)S(1)}, u32[]{:S(2)}, u32[]{:S(2)}) %collective-permute-start.13) | collective-permute-done | bytes 16416 | tf_op jit(solution)/shard_map/ppermute | solution.py:202
  71.9 2.2 collective-permute-start.14
  74.1 3.3 collective-permute-done.14
  77.6 3.0 collective-permute-start.21
  82.9 2.1 collective-permute-start.22
  85.0 4.9 %collective-permute-done.16 = f32[4,8192]{1,0:T(4,128)S(1)} collective-permute-done((f32[4,8192]{1,0:T(4,128)S(1)}, f32[4,8192]{1,0:T(4,128)S(1)}, u32[]{:S(2)}, u32[]{:S(2)}) %collective-permute-start.16) | collective-permute-done | bytes 131104 | tf_op jit(solution)/shard_map/ppermute | solution.py:202
  90.2 5.4 %collective-permute-done.23 = f32[4,2048]{1,0:T(4,128)S(1)} collective-permute-done((f32[4,2048]{1,0:T(4,128)S(1)}, f32[4,2048]{1,0:T(4,128)S(1)}, u32[]{:S(2)}, u32[]{:S(2)}) %collective-permute-start.23) | collective-permute-done | bytes 32800 | tf_op jit(solution)/shard_map/ppermute | solution.py:202
  95.7 2.1 collective-permute-start.24
  97.9 2.1 collective-permute-done.24
  108.6 14.2 %shard_map.37 = f32[32,16,512]{2,1,0:T(8,128)} custom-call(f32[32,16,512]{2,1,0:T(8,128)} %reshape_transpose_reshape_reshape_reshape.10.src_ref, f32[32,16,512]{2,1,0:T(8,128)} %reshape.1468.met_ref), custom_call_target="tpu_custom_call" | custom-call | tf_op jit(solution)/shard_map/pallas_call | solution.py:161
  127.8 4.5 %collective-permute-start.28 = (f32[1,4,1,32,64]{4,3,2,1,0:T(8,128)S(1)}, f32[1,4,1,32,64]{4,3,2,1,0:T(8,128)S(1)}, u32[]{:S(2)}, u32[]{:S(2)}) collective-permute-start(f32[1,4,1,32,64]{4,3,2,1,0:T(8,128)S(1)} %get-tuple-element.100), channel_id=1, source_target_pairs={{0,1},{1,2},{2,3},{4,5},{5,6},{6,7},{8,9},{9,10},{10,11},{12,13},{... | collective-permute-start | bytes 98312 | tf_op jit(solution)/shard_map/ppermute | solution.py:23
  132.3 1.9 collective-permute-start.26
  134.4 6.3 %collective-permute-done.26 = f32[1,4,2,32,64]{4,3,2,1,0:T(8,128)S(1)} collective-permute-done((f32[1,4,2,32,64]{4,3,2,1,0:T(8,128)S(1)}, f32[1,4,2,32,64]{4,3,2,1,0:T(8,128)S(1)}, u32[]{:S(2)}, u32[]{:S(2)}) %collective-permute-start.26) | collective-permute-done | bytes 65568 | tf_op jit(solution)/shard_map/ppermute | solution.py:34
  141.3 1.9 collective-permute-start.29
  144.6 4.6 %collective-permute-start.31 = (f32[1,4,1,64,128]{4,3,2,1,0:T(8,128)S(1)}, f32[1,4,1,64,128]{4,3,2,1,0:T(8,128)S(1)}, u32[]{:S(2)}, u32[]{:S(2)}) collective-permute-start(f32[1,4,1,64,128]{4,3,2,1,0:T(8,128)S(1)} %get-tuple-element.60), channel_id=1, source_target_pairs={{0,1},{1,2},{2,3},{4,5},{5,6},{6,7},{8,9},{9,10},{10,11},{12,13},{... | collective-permute-start | bytes 393224 | tf_op jit(solution)/shard_map/ppermute | solution.py:23
  151.9 2.0 collective-permute-done.29
  154.5 1.9 collective-permute-start.32
  157.7 4.6 %collective-permute-start.34 = (f32[1,4,1,64,128]{4,3,2,1,0:T(8,128)S(1)}, f32[1,4,1,64,128]{4,3,2,1,0:T(8,128)S(1)}, u32[]{:S(2)}, u32[]{:S(2)}) collective-permute-start(f32[1,4,1,64,128]{4,3,2,1,0:T(8,128)S(1)} %get-tuple-element.56), channel_id=1, source_target_pairs={{0,1},{1,2},{2,3},{4,5},{5,6},{6,7},{8,9},{9,10},{10,11},{12,13},{... | collective-permute-start | bytes 393224 | tf_op jit(solution)/shard_map/ppermute | solution.py:23
  165.0 2.0 collective-permute-done.32
  167.6 1.9 collective-permute-start.35
  170.9 4.6 %collective-permute-start.37 = (f32[1,4,1,64,128]{4,3,2,1,0:T(8,128)S(1)}, f32[1,4,1,64,128]{4,3,2,1,0:T(8,128)S(1)}, u32[]{:S(2)}, u32[]{:S(2)}) collective-permute-start(f32[1,4,1,64,128]{4,3,2,1,0:T(8,128)S(1)} %get-tuple-element.52), channel_id=1, source_target_pairs={{0,1},{1,2},{2,3},{4,5},{5,6},{6,7},{8,9},{9,10},{10,11},{12,13},{... | collective-permute-start | bytes 393224 | tf_op jit(solution)/shard_map/ppermute | solution.py:23
  178.1 2.1 collective-permute-done.35
  180.8 1.9 collective-permute-start.38
  184.0 4.6 %collective-permute-start.40 = (f32[1,4,1,64,128]{4,3,2,1,0:T(8,128)S(1)}, f32[1,4,1,64,128]{4,3,2,1,0:T(8,128)S(1)}, u32[]{:S(2)}, u32[]{:S(2)}) collective-permute-start(f32[1,4,1,64,128]{4,3,2,1,0:T(8,128)S(1)} %get-tuple-element.48), channel_id=1, source_target_pairs={{0,1},{1,2},{2,3},{4,5},{5,6},{6,7},{8,9},{9,10},{10,11},{12,13},{... | collective-permute-start | bytes 393224 | tf_op jit(solution)/shard_map/ppermute | solution.py:23
  191.3 2.1 collective-permute-done.38
  193.9 1.9 collective-permute-start.41
  197.2 4.6 %collective-permute-start.43 = (f32[1,4,1,64,128]{4,3,2,1,0:T(8,128)S(1)}, f32[1,4,1,64,128]{4,3,2,1,0:T(8,128)S(1)}, u32[]{:S(2)}, u32[]{:S(2)}) collective-permute-start(f32[1,4,1,64,128]{4,3,2,1,0:T(8,128)S(1)} %get-tuple-element.44), channel_id=1, source_target_pairs={{0,1},{1,2},{2,3},{4,5},{5,6},{6,7},{8,9},{9,10},{10,11},{12,13},{... | collective-permute-start | bytes 393224 | tf_op jit(solution)/shard_map/ppermute | solution.py:23
  204.5 2.1 collective-permute-done.41
  208.9 4.5 %collective-permute-start.46 = (f32[1,4,1,32,64]{4,3,2,1,0:T(8,128)S(1)}, f32[1,4,1,32,64]{4,3,2,1,0:T(8,128)S(1)}, u32[]{:S(2)}, u32[]{:S(2)}) collective-permute-start(f32[1,4,1,32,64]{4,3,2,1,0:T(8,128)S(1)} %get-tuple-element.96), channel_id=1, source_target_pairs={{0,1},{1,2},{2,3},{4,5},{5,6},{6,7},{8,9},{9,10},{10,11},{12,13},{... | collective-permute-start | bytes 98312 | tf_op jit(solution)/shard_map/ppermute | solution.py:23
  213.4 1.9 collective-permute-start.44
  215.5 6.3 %collective-permute-done.44 = f32[1,4,2,32,64]{4,3,2,1,0:T(8,128)S(1)} collective-permute-done((f32[1,4,2,32,64]{4,3,2,1,0:T(8,128)S(1)}, f32[1,4,2,32,64]{4,3,2,1,0:T(8,128)S(1)}, u32[]{:S(2)}, u32[]{:S(2)}) %collective-permute-start.44) | collective-permute-done | bytes 65568 | tf_op jit(solution)/shard_map/ppermute | solution.py:34
  223.3 4.5 %collective-permute-start.49 = (f32[1,4,1,32,64]{4,3,2,1,0:T(8,128)S(1)}, f32[1,4,1,32,64]{4,3,2,1,0:T(8,128)S(1)}, u32[]{:S(2)}, u32[]{:S(2)}) collective-permute-start(f32[1,4,1,32,64]{4,3,2,1,0:T(8,128)S(1)} %get-tuple-element.92), channel_id=1, source_target_pairs={{0,1},{1,2},{2,3},{4,5},{5,6},{6,7},{8,9},{9,10},{10,11},{12,13},{... | collective-permute-start | bytes 98312 | tf_op jit(solution)/shard_map/ppermute | solution.py:23
  227.9 2.1 collective-permute-start.47
  230.1 6.1 %collective-permute-done.47 = f32[1,4,2,32,64]{4,3,2,1,0:T(8,128)S(1)} collective-permute-done((f32[1,4,2,32,64]{4,3,2,1,0:T(8,128)S(1)}, f32[1,4,2,32,64]{4,3,2,1,0:T(8,128)S(1)}, u32[]{:S(2)}, u32[]{:S(2)}) %collective-permute-start.47) | collective-permute-done | bytes 65568 | tf_op jit(solution)/shard_map/ppermute | solution.py:34
  238.2 3.1 collective-permute-done.50
  241.3 2.3 collective-permute-start.51
  243.6 3.0 collective-permute-done.51
  248.0 4.2 %collective-permute-done.52 = f32[1,8192]{1,0:T(1,128)S(1)} collective-permute-done((f32[1,8192]{1,0:T(1,128)S(1)}, f32[1,8192]{1,0:T(1,128)S(1)}, u32[]{:S(2)}, u32[]{:S(2)}) %collective-permute-start.52) | collective-permute-done | bytes 32800 | tf_op jit(solution)/shard_map/ppermute | solution.py:202
  252.4 4.3 %collective-permute-done.53 = f32[2,8192]{1,0:T(2,128)S(1)} collective-permute-done((f32[2,8192]{1,0:T(2,128)S(1)}, f32[2,8192]{1,0:T(2,128)S(1)}, u32[]{:S(2)}, u32[]{:S(2)}) %collective-permute-start.53) | collective-permute-done | bytes 65568 | tf_op jit(solution)/shard_map/ppermute | solution.py:202
  256.8 6.5 %collective-permute-done.54 = f32[4,8192]{1,0:T(4,128)S(1)} collective-permute-done((f32[4,8192]{1,0:T(4,128)S(1)}, f32[4,8192]{1,0:T(4,128)S(1)}, u32[]{:S(2)}, u32[]{:S(2)}) %collective-permute-start.54) | collective-permute-done | bytes 131104 | tf_op jit(solution)/shard_map/ppermute | solution.py:202
  263.5 6.4 %collective-permute-done.55 = f32[8,8192]{1,0:T(8,128)S(1)} collective-permute-done((f32[8,8192]{1,0:T(8,128)S(1)}, f32[8,8192]{1,0:T(8,128)S(1)}, u32[]{:S(2)}, u32[]{:S(2)}) %collective-permute-start.55) | collective-permute-done | bytes 262176 | tf_op jit(solution)/shard_map/ppermute | solution.py:202
  275.3 14.2 %shard_map.38 = f32[32,16,512]{2,1,0:T(8,128)} custom-call(f32[32,16,512]{2,1,0:T(8,128)} %reshape_transpose_reshape_reshape_reshape.12.src_ref, f32[32,16,512]{2,1,0:T(8,128)} %reshape.1468.met_ref), custom_call_target="tpu_custom_call" | custom-call | tf_op jit(solution)/shard_map/pallas_call | solution.py:161
  294.4 4.5 %collective-permute-start.59 = (f32[1,4,1,32,64]{4,3,2,1,0:T(8,128)S(1)}, f32[1,4,1,32,64]{4,3,2,1,0:T(8,128)S(1)}, u32[]{:S(2)}, u32[]{:S(2)}) collective-permute-start(f32[1,4,1,32,64]{4,3,2,1,0:T(8,128)S(1)} %get-tuple-element.88), channel_id=1, source_target_pairs={{0,1},{1,2},{2,3},{4,5},{5,6},{6,7},{8,9},{9,10},{10,11},{12,13},{... | collective-permute-start | bytes 98312 | tf_op jit(solution)/shard_map/ppermute | solution.py:23
  299.0 1.9 collective-permute-start.57
  301.1 6.3 %collective-permute-done.57 = f32[1,4,2,32,64]{4,3,2,1,0:T(8,128)S(1)} collective-permute-done((f32[1,4,2,32,64]{4,3,2,1,0:T(8,128)S(1)}, f32[1,4,2,32,64]{4,3,2,1,0:T(8,128)S(1)}, u32[]{:S(2)}, u32[]{:S(2)}) %collective-permute-start.57) | collective-permute-done | bytes 65568 | tf_op jit(solution)/shard_map/ppermute | solution.py:34
  308.0 1.9 collective-permute-start.60
  311.2 4.6 %collective-permute-start.62 = (f32[1,4,1,64,128]{4,3,2,1,0:T(8,128)S(1)}, f32[1,4,1,64,128]{4,3,2,1,0:T(8,128)S(1)}, u32[]{:S(2)}, u32[]{:S(2)}) collective-permute-start(f32[1,4,1,64,128]{4,3,2,1,0:T(8,128)S(1)} %get-tuple-element.40), channel_id=1, source_target_pairs={{0,1},{1,2},{2,3},{4,5},{5,6},{6,7},{8,9},{9,10},{10,11},{12,13},{... | collective-permute-start | bytes 393224 | tf_op jit(solution)/shard_map/ppermute | solution.py:23
  318.5 2.1 collective-permute-done.60
  321.1 1.9 collective-permute-start.63
  324.4 4.6 %collective-permute-start.65 = (f32[1,4,1,64,128]{4,3,2,1,0:T(8,128)S(1)}, f32[1,4,1,64,128]{4,3,2,1,0:T(8,128)S(1)}, u32[]{:S(2)}, u32[]{:S(2)}) collective-permute-start(f32[1,4,1,64,128]{4,3,2,1,0:T(8,128)S(1)} %get-tuple-element.36), channel_id=1, source_target_pairs={{0,1},{1,2},{2,3},{4,5},{5,6},{6,7},{8,9},{9,10},{10,11},{12,13},{... | collective-permute-start | bytes 393224 | tf_op jit(solution)/shard_map/ppermute | solution.py:23
  331.6 2.1 collective-permute-done.63
  (269 shorter events, 88.9 us)
Async XLA Ops:
  3.2 12.6 %collective-permute-start = (f32[1,4,4,64,128]{4,3,2,1,0:T(8,128)S(1)}, f32[1,4,4,64,128]{4,3,2,1,0:T(8,128)S(1)}, u32[]{:S(2)}, u32[]{:S(2)}) collective-permute-start(f32[1,4,4,64,128]{4,3,2,1,0:T(8,128)S(1)} %get-tuple-element.9), channel_id=1, source_target_pairs={{0,4},{4,8},{8,12},{12,16},{16,20},{20,24},{24,28},{28,32},{32,36}... | collective-permute-start | bytes 1572872 | tf_op jit(solution)/shard_map/ppermute | solution.py:34
  5.2 7.5 %collective-permute-start.1 = (f32[1,4,1,64,128]{4,3,2,1,0:T(8,128)S(1)}, f32[1,4,1,64,128]{4,3,2,1,0:T(8,128)S(1)}, u32[]{:S(2)}, u32[]{:S(2)}) collective-permute-start(f32[1,4,1,64,128]{4,3,2,1,0:T(8,128)S(1)} %get-tuple-element.67), channel_id=1, source_target_pairs={{1,0},{2,1},{3,2},{5,4},{6,5},{7,6},{9,8},{10,9},{11,10},{13,12},{... | collective-permute-start | bytes 393224 | tf_op jit(solution)/shard_map/ppermute | solution.py:26
  6.6 7.8 %collective-permute-start.2 = (f32[1,4,1,64,128]{4,3,2,1,0:T(8,128)S(1)}, f32[1,4,1,64,128]{4,3,2,1,0:T(8,128)S(1)}, u32[]{:S(2)}, u32[]{:S(2)}) collective-permute-start(f32[1,4,1,64,128]{4,3,2,1,0:T(8,128)S(1)} %get-tuple-element.68), channel_id=1, source_target_pairs={{0,1},{1,2},{2,3},{4,5},{5,6},{6,7},{8,9},{9,10},{10,11},{12,13},{... | collective-permute-start | bytes 393224 | tf_op jit(solution)/shard_map/ppermute | solution.py:23
  16.4 12.6 %collective-permute-start.3 = (f32[1,4,4,64,128]{4,3,2,1,0:T(8,128)S(1)}, f32[1,4,4,64,128]{4,3,2,1,0:T(8,128)S(1)}, u32[]{:S(2)}, u32[]{:S(2)}) collective-permute-start(f32[1,4,4,64,128]{4,3,2,1,0:T(8,128)S(1)} %fusion.119), channel_id=1, source_target_pairs={{0,4},{4,8},{8,12},{12,16},{16,20},{20,24},{24,28},{28,32},{32,36}... | collective-permute-start | bytes 1572872 | tf_op jit(solution)/shard_map/ppermute | solution.py:34
  18.3 8.0 %collective-permute-start.4 = (f32[1,4,1,64,128]{4,3,2,1,0:T(8,128)S(1)}, f32[1,4,1,64,128]{4,3,2,1,0:T(8,128)S(1)}, u32[]{:S(2)}, u32[]{:S(2)}) collective-permute-start(f32[1,4,1,64,128]{4,3,2,1,0:T(8,128)S(1)} %get-tuple-element.63), channel_id=1, source_target_pairs={{1,0},{2,1},{3,2},{5,4},{6,5},{7,6},{9,8},{10,9},{11,10},{13,12},{... | collective-permute-start | bytes 393224 | tf_op jit(solution)/shard_map/ppermute | solution.py:26
  19.6 8.4 %collective-permute-start.5 = (f32[1,4,1,64,128]{4,3,2,1,0:T(8,128)S(1)}, f32[1,4,1,64,128]{4,3,2,1,0:T(8,128)S(1)}, u32[]{:S(2)}, u32[]{:S(2)}) collective-permute-start(f32[1,4,1,64,128]{4,3,2,1,0:T(8,128)S(1)} %get-tuple-element.64), channel_id=1, source_target_pairs={{0,1},{1,2},{2,3},{4,5},{5,6},{6,7},{8,9},{9,10},{10,11},{12,13},{... | collective-permute-start | bytes 393224 | tf_op jit(solution)/shard_map/ppermute | solution.py:23
  30.0 7.8 %collective-permute-start.7 = (f32[1,4,1,32,64]{4,3,2,1,0:T(8,128)S(1)}, f32[1,4,1,32,64]{4,3,2,1,0:T(8,128)S(1)}, u32[]{:S(2)}, u32[]{:S(2)}) collective-permute-start(f32[1,4,1,32,64]{4,3,2,1,0:T(8,128)S(1)} %get-tuple-element.107), channel_id=1, source_target_pairs={{1,0},{2,1},{3,2},{5,4},{6,5},{7,6},{9,8},{10,9},{11,10},{13,12},{... | collective-permute-start | bytes 98312 | tf_op jit(solution)/shard_map/ppermute | solution.py:26
  31.3 6.5 %collective-permute-start.8 = (f32[1,4,1,32,64]{4,3,2,1,0:T(8,128)S(1)}, f32[1,4,1,32,64]{4,3,2,1,0:T(8,128)S(1)}, u32[]{:S(2)}, u32[]{:S(2)}) collective-permute-start(f32[1,4,1,32,64]{4,3,2,1,0:T(8,128)S(1)} %get-tuple-element.108), channel_id=1, source_target_pairs={{0,1},{1,2},{2,3},{4,5},{5,6},{6,7},{8,9},{9,10},{10,11},{12,13},{... | collective-permute-start | bytes 98312 | tf_op jit(solution)/shard_map/ppermute | solution.py:23
  35.9 8.4 %collective-permute-start.6 = (f32[1,4,2,32,64]{4,3,2,1,0:T(8,128)S(1)}, f32[1,4,2,32,64]{4,3,2,1,0:T(8,128)S(1)}, u32[]{:S(2)}, u32[]{:S(2)}) collective-permute-start(f32[1,4,2,32,64]{4,3,2,1,0:T(8,128)S(1)} %fusion.388), channel_id=1, source_target_pairs={{0,4},{4,8},{8,12},{12,16},{16,20},{20,24},{24,28},{28,32},{32,36}... | collective-permute-start | bytes 196616 | tf_op jit(solution)/shard_map/ppermute | solution.py:34
  44.5 10.0 %collective-permute-start.10 = (f32[1,4,1,32,64]{4,3,2,1,0:T(8,128)S(1)}, f32[1,4,1,32,64]{4,3,2,1,0:T(8,128)S(1)}, u32[]{:S(2)}, u32[]{:S(2)}) collective-permute-start(f32[1,4,1,32,64]{4,3,2,1,0:T(8,128)S(1)} %get-tuple-element.103), channel_id=1, source_target_pairs={{1,0},{2,1},{3,2},{5,4},{6,5},{7,6},{9,8},{10,9},{11,10},{13,12},{... | collective-permute-start | bytes 98312 | tf_op jit(solution)/shard_map/ppermute | solution.py:26
  45.8 8.7 %collective-permute-start.11 = (f32[1,4,1,32,64]{4,3,2,1,0:T(8,128)S(1)}, f32[1,4,1,32,64]{4,3,2,1,0:T(8,128)S(1)}, u32[]{:S(2)}, u32[]{:S(2)}) collective-permute-start(f32[1,4,1,32,64]{4,3,2,1,0:T(8,128)S(1)} %get-tuple-element.104), channel_id=1, source_target_pairs={{0,1},{1,2},{2,3},{4,5},{5,6},{6,7},{8,9},{9,10},{10,11},{12,13},{... | collective-permute-start | bytes 98312 | tf_op jit(solution)/shard_map/ppermute | solution.py:23
  50.6 11.9 %collective-permute-start.19 = (f32[1,512]{1,0:T(1,128)S(1)}, f32[1,512]{1,0:T(1,128)S(1)}, u32[]{:S(2)}, u32[]{:S(2)}) collective-permute-start(f32[1,512]{1,0:T(1,128)S(1)} %reshape.1467), channel_id=1, source_target_pairs={{0,1},{1,0},{2,3},{3,2},{4,5},{5,4},{6,7},{7,6},{8,9},{9,8},{10,11... | collective-permute-start | bytes 6152 | tf_op jit(solution)/shard_map/ppermute | solution.py:202
  52.6 8.4 %collective-permute-start.9 = (f32[1,4,2,32,64]{4,3,2,1,0:T(8,128)S(1)}, f32[1,4,2,32,64]{4,3,2,1,0:T(8,128)S(1)}, u32[]{:S(2)}, u32[]{:S(2)}) collective-permute-start(f32[1,4,2,32,64]{4,3,2,1,0:T(8,128)S(1)} %fusion.207), channel_id=1, source_target_pairs={{0,4},{4,8},{8,12},{12,16},{16,20},{20,24},{24,28},{28,32},{32,36}... | collective-permute-start | bytes 196616 | tf_op jit(solution)/shard_map/ppermute | solution.py:34
  62.3 4.2 %collective-permute-start.12 = (f32[1,2048]{1,0:T(1,128)S(1)}, f32[1,2048]{1,0:T(1,128)S(1)}, u32[]{:S(2)}, u32[]{:S(2)}) collective-permute-start(f32[1,2048]{1,0:T(1,128)S(1)} %reshape.1465), channel_id=1, source_target_pairs={{0,1},{1,0},{2,3},{3,2},{4,5},{5,4},{6,7},{7,6},{8,9},{9,8},{10,11... | collective-permute-start | bytes 24584 | tf_op jit(solution)/shard_map/ppermute | solution.py:202
  62.5 15.1 %collective-permute-start.20 = (f32[1,1024]{1,0:T(1,128)S(1)}, f32[1,1024]{1,0:T(1,128)S(1)}, u32[]{:S(2)}, u32[]{:S(2)}) collective-permute-start(f32[1,1024]{1,0:T(1,128)S(1)} %broadcast_select_fusion.5), channel_id=1, source_target_pairs={{0,2},{1,3},{2,0},{3,1},{4,6},{5,7},{6,4},{7,5},{8,10},{9,11},{10,... | collective-permute-start | bytes 12296 | tf_op jit(solution)/shard_map/ppermute | solution.py:202
  66.5 5.3 %collective-permute-start.13 = (f32[1,4096]{1,0:T(1,128)S(1)}, f32[1,4096]{1,0:T(1,128)S(1)}, u32[]{:S(2)}, u32[]{:S(2)}) collective-permute-start(f32[1,4096]{1,0:T(1,128)S(1)} %broadcast_select_fusion.3), channel_id=1, source_target_pairs={{0,2},{1,3},{2,0},{3,1},{4,6},{5,7},{6,4},{7,5},{8,10},{9,11},{10,... | collective-permute-start | bytes 49160 | tf_op jit(solution)/shard_map/ppermute | solution.py:202
  71.9 5.5 %collective-permute-start.14 = (f32[1,8192]{1,0:T(1,128)S(1)}, f32[1,8192]{1,0:T(1,128)S(1)}, u32[]{:S(2)}, u32[]{:S(2)}) collective-permute-start(f32[1,8192]{1,0:T(1,128)S(1)} %broadcast_select_fusion.1), channel_id=1, source_target_pairs={{0,64},{4,68},{8,72},{12,76},{16,80},{20,84},{24,88},{28,92},{32,9... | collective-permute-start | bytes 98312 | tf_op jit(solution)/shard_map/ppermute | solution.py:202
  77.5 4.3 %collective-permute-start.15 = (f32[2,8192]{1,0:T(2,128)S(1)}, f32[2,8192]{1,0:T(2,128)S(1)}, u32[]{:S(2)}, u32[]{:S(2)}) collective-permute-start(f32[2,8192]{1,0:T(2,128)S(1)} %maximum_select_fusion.10), channel_id=1, source_target_pairs={{0,32},{4,36},{8,40},{12,44},{16,48},{20,52},{24,56},{28,60},{32,0... | collective-permute-start | bytes 196616 | tf_op jit(solution)/shard_map/ppermute | solution.py:202
  77.6 5.2 %collective-permute-start.21 = (f32[1,2048]{1,0:T(1,128)S(1)}, f32[1,2048]{1,0:T(1,128)S(1)}, u32[]{:S(2)}, u32[]{:S(2)}) collective-permute-start(f32[1,2048]{1,0:T(1,128)S(1)} %broadcast_select_fusion.4), channel_id=1, source_target_pairs={{0,64},{4,68},{8,72},{12,76},{16,80},{20,84},{24,88},{28,92},{32,9... | collective-permute-start | bytes 24584 | tf_op jit(solution)/shard_map/ppermute | solution.py:202
  81.9 8.0 %collective-permute-start.16 = (f32[4,8192]{1,0:T(4,128)S(1)}, f32[4,8192]{1,0:T(4,128)S(1)}, u32[]{:S(2)}, u32[]{:S(2)}) collective-permute-start(f32[4,8192]{1,0:T(4,128)S(1)} %maximum_select_fusion.7), channel_id=1, source_target_pairs={{0,16},{4,20},{8,24},{12,28},{16,0},{20,4},{24,8},{28,12},{32,48},... | collective-permute-start | bytes 393224 | tf_op jit(solution)/shard_map/ppermute | solution.py:202
  82.9 7.2 %collective-permute-start.22 = (f32[2,2048]{1,0:T(2,128)S(1)}, f32[2,2048]{1,0:T(2,128)S(1)}, u32[]{:S(2)}, u32[]{:S(2)}) collective-permute-start(f32[2,2048]{1,0:T(2,128)S(1)} %maximum_select_fusion.15), channel_id=1, source_target_pairs={{0,32},{4,36},{8,40},{12,44},{16,48},{20,52},{24,56},{28,60},{32,0... | collective-permute-start | bytes 49160 | tf_op jit(solution)/shard_map/ppermute | solution.py:202
  90.0 7.8 %collective-permute-start.17 = (f32[8,8192]{1,0:T(8,128)S(1)}, f32[8,8192]{1,0:T(8,128)S(1)}, u32[]{:S(2)}, u32[]{:S(2)}) collective-permute-start(f32[8,8192]{1,0:T(8,128)S(1)} %maximum_select_fusion.4), channel_id=1, source_target_pairs={{0,8},{4,12},{8,0},{12,4},{16,24},{20,28},{24,16},{28,20},{32,40},... | collective-permute-start | bytes 786440 | tf_op jit(solution)/shard_map/ppermute | solution.py:202
  90.1 5.5 %collective-permute-start.23 = (f32[4,2048]{1,0:T(4,128)S(1)}, f32[4,2048]{1,0:T(4,128)S(1)}, u32[]{:S(2)}, u32[]{:S(2)}) collective-permute-start(f32[4,2048]{1,0:T(4,128)S(1)} %maximum_select_fusion.13), channel_id=1, source_target_pairs={{0,16},{4,20},{8,24},{12,28},{16,0},{20,4},{24,8},{28,12},{32,48},... | collective-permute-start | bytes 98312 | tf_op jit(solution)/shard_map/ppermute | solution.py:202
  95.7 4.3 %collective-permute-start.24 = (f32[8,2048]{1,0:T(8,128)S(1)}, f32[8,2048]{1,0:T(8,128)S(1)}, u32[]{:S(2)}, u32[]{:S(2)}) collective-permute-start(f32[8,2048]{1,0:T(8,128)S(1)} %maximum_select_fusion.11), channel_id=1, source_target_pairs={{0,8},{4,12},{8,0},{12,4},{16,24},{20,28},{24,16},{28,20},{32,40},... | collective-permute-start | bytes 196616 | tf_op jit(solution)/shard_map/ppermute | solution.py:202
  97.8 6.2 %collective-permute-start.18 = (f32[16,8192]{1,0:T(8,128)S(1)}, f32[16,8192]{1,0:T(8,128)}, u32[]{:S(2)}, u32[]{:S(2)}) collective-permute-start(f32[16,8192]{1,0:T(8,128)S(1)} %maximum_select_fusion.2), channel_id=1, source_target_pairs={{0,4},{4,0},{8,12},{12,8},{16,20},{20,16},{24,28},{28,24},{32,36},... | collective-permute-start | bytes 1572872 | tf_op jit(solution)/shard_map/ppermute | solution.py:202
  126.5 7.8 %collective-permute-start.27 = (f32[1,4,1,32,64]{4,3,2,1,0:T(8,128)S(1)}, f32[1,4,1,32,64]{4,3,2,1,0:T(8,128)S(1)}, u32[]{:S(2)}, u32[]{:S(2)}) collective-permute-start(f32[1,4,1,32,64]{4,3,2,1,0:T(8,128)S(1)} %get-tuple-element.99), channel_id=1, source_target_pairs={{1,0},{2,1},{3,2},{5,4},{6,5},{7,6},{9,8},{10,9},{11,10},{13,12},{... | collective-permute-start | bytes 98312 | tf_op jit(solution)/shard_map/ppermute | solution.py:26
  127.8 6.5 %collective-permute-start.28 = (f32[1,4,1,32,64]{4,3,2,1,0:T(8,128)S(1)}, f32[1,4,1,32,64]{4,3,2,1,0:T(8,128)S(1)}, u32[]{:S(2)}, u32[]{:S(2)}) collective-permute-start(f32[1,4,1,32,64]{4,3,2,1,0:T(8,128)S(1)} %get-tuple-element.100), channel_id=1, source_target_pairs={{0,1},{1,2},{2,3},{4,5},{5,6},{6,7},{8,9},{9,10},{10,11},{12,13},{... | collective-permute-start | bytes 98312 | tf_op jit(solution)/shard_map/ppermute | solution.py:23
  132.3 8.4 %collective-permute-start.26 = (f32[1,4,2,32,64]{4,3,2,1,0:T(8,128)S(1)}, f32[1,4,2,32,64]{4,3,2,1,0:T(8,128)S(1)}, u32[]{:S(2)}, u32[]{:S(2)}) collective-permute-start(f32[1,4,2,32,64]{4,3,2,1,0:T(8,128)S(1)} %fusion.221), channel_id=1, source_target_pairs={{0,4},{4,8},{8,12},{12,16},{16,20},{20,24},{24,28},{28,32},{32,36}... | collective-permute-start | bytes 196616 | tf_op jit(solution)/shard_map/ppermute | solution.py:34
  141.3 12.6 %collective-permute-start.29 = (f32[1,4,4,64,128]{4,3,2,1,0:T(8,128)S(1)}, f32[1,4,4,64,128]{4,3,2,1,0:T(8,128)S(1)}, u32[]{:S(2)}, u32[]{:S(2)}) collective-permute-start(f32[1,4,4,64,128]{4,3,2,1,0:T(8,128)S(1)} %add.517), channel_id=1, source_target_pairs={{0,4},{4,8},{8,12},{12,16},{16,20},{20,24},{24,28},{28,32},{32,36}... | collective-permute-start | bytes 1572872 | tf_op jit(solution)/shard_map/ppermute | solution.py:34
  143.3 7.3 %collective-permute-start.30 = (f32[1,4,1,64,128]{4,3,2,1,0:T(8,128)S(1)}, f32[1,4,1,64,128]{4,3,2,1,0:T(8,128)S(1)}, u32[]{:S(2)}, u32[]{:S(2)}) collective-permute-start(f32[1,4,1,64,128]{4,3,2,1,0:T(8,128)S(1)} %get-tuple-element.59), channel_id=1, source_target_pairs={{1,0},{2,1},{3,2},{5,4},{6,5},{7,6},{9,8},{10,9},{11,10},{13,12},{... | collective-permute-start | bytes 393224 | tf_op jit(solution)/shard_map/ppermute | solution.py:26
  144.6 7.2 %collective-permute-start.31 = (f32[1,4,1,64,128]{4,3,2,1,0:T(8,128)S(1)}, f32[1,4,1,64,128]{4,3,2,1,0:T(8,128)S(1)}, u32[]{:S(2)}, u32[]{:S(2)}) collective-permute-start(f32[1,4,1,64,128]{4,3,2,1,0:T(8,128)S(1)} %get-tuple-element.60), channel_id=1, source_target_pairs={{0,1},{1,2},{2,3},{4,5},{5,6},{6,7},{8,9},{9,10},{10,11},{12,13},{... | collective-permute-start | bytes 393224 | tf_op jit(solution)/shard_map/ppermute | solution.py:23
  154.5 12.6 %collective-permute-start.32 = (f32[1,4,4,64,128]{4,3,2,1,0:T(8,128)S(1)}, f32[1,4,4,64,128]{4,3,2,1,0:T(8,128)S(1)}, u32[]{:S(2)}, u32[]{:S(2)}) collective-permute-start(f32[1,4,4,64,128]{4,3,2,1,0:T(8,128)S(1)} %fusion.93), channel_id=1, source_target_pairs={{0,4},{4,8},{8,12},{12,16},{16,20},{20,24},{24,28},{28,32},{32,36}... | collective-permute-start | bytes 1572872 | tf_op jit(solution)/shard_map/ppermute | solution.py:34
  156.4 7.2 %collective-permute-start.33 = (f32[1,4,1,64,128]{4,3,2,1,0:T(8,128)S(1)}, f32[1,4,1,64,128]{4,3,2,1,0:T(8,128)S(1)}, u32[]{:S(2)}, u32[]{:S(2)}) collective-permute-start(f32[1,4,1,64,128]{4,3,2,1,0:T(8,128)S(1)} %get-tuple-element.55), channel_id=1, source_target_pairs={{1,0},{2,1},{3,2},{5,4},{6,5},{7,6},{9,8},{10,9},{11,10},{13,12},{... | collective-permute-start | bytes 393224 | tf_op jit(solution)/shard_map/ppermute | solution.py:26
  157.7 7.1 %collective-permute-start.34 = (f32[1,4,1,64,128]{4,3,2,1,0:T(8,128)S(1)}, f32[1,4,1,64,128]{4,3,2,1,0:T(8,128)S(1)}, u32[]{:S(2)}, u32[]{:S(2)}) collective-permute-start(f32[1,4,1,64,128]{4,3,2,1,0:T(8,128)S(1)} %get-tuple-element.56), channel_id=1, source_target_pairs={{0,1},{1,2},{2,3},{4,5},{5,6},{6,7},{8,9},{9,10},{10,11},{12,13},{... | collective-permute-start | bytes 393224 | tf_op jit(solution)/shard_map/ppermute | solution.py:23
  167.6 12.6 %collective-permute-start.35 = (f32[1,4,4,64,128]{4,3,2,1,0:T(8,128)S(1)}, f32[1,4,4,64,128]{4,3,2,1,0:T(8,128)S(1)}, u32[]{:S(2)}, u32[]{:S(2)}) collective-permute-start(f32[1,4,4,64,128]{4,3,2,1,0:T(8,128)S(1)} %fusion.79), channel_id=1, source_target_pairs={{0,4},{4,8},{8,12},{12,16},{16,20},{20,24},{24,28},{28,32},{32,36}... | collective-permute-start | bytes 1572872 | tf_op jit(solution)/shard_map/ppermute | solution.py:34
  169.6 6.9 %collective-permute-start.36 = (f32[1,4,1,64,128]{4,3,2,1,0:T(8,128)S(1)}, f32[1,4,1,64,128]{4,3,2,1,0:T(8,128)S(1)}, u32[]{:S(2)}, u32[]{:S(2)}) collective-permute-start(f32[1,4,1,64,128]{4,3,2,1,0:T(8,128)S(1)} %get-tuple-element.51), channel_id=1, source_target_pairs={{1,0},{2,1},{3,2},{5,4},{6,5},{7,6},{9,8},{10,9},{11,10},{13,12},{... | collective-permute-start | bytes 393224 | tf_op jit(solution)/shard_map/ppermute | solution.py:26
  170.9 7.1 %collective-permute-start.37 = (f32[1,4,1,64,128]{4,3,2,1,0:T(8,128)S(1)}, f32[1,4,1,64,128]{4,3,2,1,0:T(8,128)S(1)}, u32[]{:S(2)}, u32[]{:S(2)}) collective-permute-start(f32[1,4,1,64,128]{4,3,2,1,0:T(8,128)S(1)} %get-tuple-element.52), channel_id=1, source_target_pairs={{0,1},{1,2},{2,3},{4,5},{5,6},{6,7},{8,9},{9,10},{10,11},{12,13},{... | collective-permute-start | bytes 393224 | tf_op jit(solution)/shard_map/ppermute | solution.py:23
  180.8 12.6 %collective-permute-start.38 = (f32[1,4,4,64,128]{4,3,2,1,0:T(8,128)S(1)}, f32[1,4,4,64,128]{4,3,2,1,0:T(8,128)S(1)}, u32[]{:S(2)}, u32[]{:S(2)}) collective-permute-start(f32[1,4,4,64,128]{4,3,2,1,0:T(8,128)S(1)} %fusion.65), channel_id=1, source_target_pairs={{0,4},{4,8},{8,12},{12,16},{16,20},{20,24},{24,28},{28,32},{32,36}... | collective-permute-start | bytes 1572872 | tf_op jit(solution)/shard_map/ppermute | solution.py:34
  182.7 6.9 %collective-permute-start.39 = (f32[1,4,1,64,128]{4,3,2,1,0:T(8,128)S(1)}, f32[1,4,1,64,128]{4,3,2,1,0:T(8,128)S(1)}, u32[]{:S(2)}, u32[]{:S(2)}) collective-permute-start(f32[1,4,1,64,128]{4,3,2,1,0:T(8,128)S(1)} %get-tuple-element.47), channel_id=1, source_target_pairs={{1,0},{2,1},{3,2},{5,4},{6,5},{7,6},{9,8},{10,9},{11,10},{13,12},{... | collective-permute-start | bytes 393224 | tf_op jit(solution)/shard_map/ppermute | solution.py:26
  184.0 7.1 %collective-permute-start.40 = (f32[1,4,1,64,128]{4,3,2,1,0:T(8,128)S(1)}, f32[1,4,1,64,128]{4,3,2,1,0:T(8,128)S(1)}, u32[]{:S(2)}, u32[]{:S(2)}) collective-permute-start(f32[1,4,1,64,128]{4,3,2,1,0:T(8,128)S(1)} %get-tuple-element.48), channel_id=1, source_target_pairs={{0,1},{1,2},{2,3},{4,5},{5,6},{6,7},{8,9},{9,10},{10,11},{12,13},{... | collective-permute-start | bytes 393224 | tf_op jit(solution)/shard_map/ppermute | solution.py:23
  193.9 12.6 %collective-permute-start.41 = (f32[1,4,4,64,128]{4,3,2,1,0:T(8,128)S(1)}, f32[1,4,4,64,128]{4,3,2,1,0:T(8,128)S(1)}, u32[]{:S(2)}, u32[]{:S(2)}) collective-permute-start(f32[1,4,4,64,128]{4,3,2,1,0:T(8,128)S(1)} %fusion.51), channel_id=1, source_target_pairs={{0,4},{4,8},{8,12},{12,16},{16,20},{20,24},{24,28},{28,32},{32,36}... | collective-permute-start | bytes 1572872 | tf_op jit(solution)/shard_map/ppermute | solution.py:34
  195.9 6.9 %collective-permute-start.42 = (f32[1,4,1,64,128]{4,3,2,1,0:T(8,128)S(1)}, f32[1,4,1,64,128]{4,3,2,1,0:T(8,128)S(1)}, u32[]{:S(2)}, u32[]{:S(2)}) collective-permute-start(f32[1,4,1,64,128]{4,3,2,1,0:T(8,128)S(1)} %get-tuple-element.43), channel_id=1, source_target_pairs={{1,0},{2,1},{3,2},{5,4},{6,5},{7,6},{9,8},{10,9},{11,10},{13,12},{... | collective-permute-start | bytes 393224 | tf_op jit(solution)/shard_map/ppermute | solution.py:26
  197.2 7.1 %collective-permute-start.43 = (f32[1,4,1,64,128]{4,3,2,1,0:T(8,128)S(1)}, f32[1,4,1,64,128]{4,3,2,1,0:T(8,128)S(1)}, u32[]{:S(2)}, u32[]{:S(2)}) collective-permute-start(f32[1,4,1,64,128]{4,3,2,1,0:T(8,128)S(1)} %get-tuple-element.44), channel_id=1, source_target_pairs={{0,1},{1,2},{2,3},{4,5},{5,6},{6,7},{8,9},{9,10},{10,11},{12,13},{... | collective-permute-start | bytes 393224 | tf_op jit(solution)/shard_map/ppermute | solution.py:23
  207.6 7.8 %collective-permute-start.45 = (f32[1,4,1,32,64]{4,3,2,1,0:T(8,128)S(1)}, f32[1,4,1,32,64]{4,3,2,1,0:T(8,128)S(1)}, u32[]{:S(2)}, u32[]{:S(2)}) collective-permute-start(f32[1,4,1,32,64]{4,3,2,1,0:T(8,128)S(1)} %get-tuple-element.95), channel_id=1, source_target_pairs={{1,0},{2,1},{3,2},{5,4},{6,5},{7,6},{9,8},{10,9},{11,10},{13,12},{... | collective-permute-start | bytes 98312 | tf_op jit(solution)/shard_map/ppermute | solution.py:26
  208.9 6.5 %collective-permute-start.46 = (f32[1,4,1,32,64]{4,3,2,1,0:T(8,128)S(1)}, f32[1,4,1,32,64]{4,3,2,1,0:T(8,128)S(1)}, u32[]{:S(2)}, u32[]{:S(2)}) collective-permute-start(f32[1,4,1,32,64]{4,3,2,1,0:T(8,128)S(1)} %get-tuple-element.96), channel_id=1, source_target_pairs={{0,1},{1,2},{2,3},{4,5},{5,6},{6,7},{8,9},{9,10},{10,11},{12,13},{... | collective-permute-start | bytes 98312 | tf_op jit(solution)/shard_map/ppermute | solution.py:23
  213.4 8.4 %collective-permute-start.44 = (f32[1,4,2,32,64]{4,3,2,1,0:T(8,128)S(1)}, f32[1,4,2,32,64]{4,3,2,1,0:T(8,128)S(1)}, u32[]{:S(2)}, u32[]{:S(2)}) collective-permute-start(f32[1,4,2,32,64]{4,3,2,1,0:T(8,128)S(1)} %fusion.389), channel_id=1, source_target_pairs={{0,4},{4,8},{8,12},{12,16},{16,20},{20,24},{24,28},{28,32},{32,36}... | collective-permute-start | bytes 196616 | tf_op jit(solution)/shard_map/ppermute | solution.py:34
  222.0 8.0 %collective-permute-start.48 = (f32[1,4,1,32,64]{4,3,2,1,0:T(8,128)S(1)}, f32[1,4,1,32,64]{4,3,2,1,0:T(8,128)S(1)}, u32[]{:S(2)}, u32[]{:S(2)}) collective-permute-start(f32[1,4,1,32,64]{4,3,2,1,0:T(8,128)S(1)} %get-tuple-element.91), channel_id=1, source_target_pairs={{1,0},{2,1},{3,2},{5,4},{6,5},{7,6},{9,8},{10,9},{11,10},{13,12},{... | collective-permute-start | bytes 98312 | tf_op jit(solution)/shard_map/ppermute | solution.py:26
  223.3 6.7 %collective-permute-start.49 = (f32[1,4,1,32,64]{4,3,2,1,0:T(8,128)S(1)}, f32[1,4,1,32,64]{4,3,2,1,0:T(8,128)S(1)}, u32[]{:S(2)}, u32[]{:S(2)}) collective-permute-start(f32[1,4,1,32,64]{4,3,2,1,0:T(8,128)S(1)} %get-tuple-element.92), channel_id=1, source_target_pairs={{0,1},{1,2},{2,3},{4,5},{5,6},{6,7},{8,9},{9,10},{10,11},{12,13},{... | collective-permute-start | bytes 98312 | tf_op jit(solution)/shard_map/ppermute | solution.py:23
  227.9 8.4 %collective-permute-start.47 = (f32[1,4,2,32,64]{4,3,2,1,0:T(8,128)S(1)}, f32[1,4,2,32,64]{4,3,2,1,0:T(8,128)S(1)}, u32[]{:S(2)}, u32[]{:S(2)}) collective-permute-start(f32[1,4,2,32,64]{4,3,2,1,0:T(8,128)S(1)} %fusion.166), channel_id=1, source_target_pairs={{0,4},{4,8},{8,12},{12,16},{16,20},{20,24},{24,28},{28,32},{32,36}... | collective-permute-start | bytes 196616 | tf_op jit(solution)/shard_map/ppermute | solution.py:34
  237.5 3.7 %collective-permute-start.50 = (f32[1,2048]{1,0:T(1,128)S(1)}, f32[1,2048]{1,0:T(1,128)S(1)}, u32[]{:S(2)}, u32[]{:S(2)}) collective-permute-start(f32[1,2048]{1,0:T(1,128)S(1)} %reshape.1477), channel_id=1, source_target_pairs={{0,1},{1,0},{2,3},{3,2},{4,5},{5,4},{6,7},{7,6},{8,9},{9,8},{10,11... | collective-permute-start | bytes 24584 | tf_op jit(solution)/shard_map/ppermute | solution.py:202
  241.3 5.3 %collective-permute-start.51 = (f32[1,4096]{1,0:T(1,128)S(1)}, f32[1,4096]{1,0:T(1,128)S(1)}, u32[]{:S(2)}, u32[]{:S(2)}) collective-permute-start(f32[1,4096]{1,0:T(1,128)S(1)} %broadcast_select_fusion.2), channel_id=1, source_target_pairs={{0,2},{1,3},{2,0},{3,1},{4,6},{5,7},{6,4},{7,5},{8,10},{9,11},{10,... | collective-permute-start | bytes 49160 | tf_op jit(solution)/shard_map/ppermute | solution.py:202
  246.7 5.5 %collective-permute-start.52 = (f32[1,8192]{1,0:T(1,128)S(1)}, f32[1,8192]{1,0:T(1,128)S(1)}, u32[]{:S(2)}, u32[]{:S(2)}) collective-permute-start(f32[1,8192]{1,0:T(1,128)S(1)} %broadcast_select_fusion), channel_id=1, source_target_pairs={{0,64},{4,68},{8,72},{12,76},{16,80},{20,84},{24,88},{28,92},{32,9... | collective-permute-start | bytes 98312 | tf_op jit(solution)/shard_map/ppermute | solution.py:202
  252.3 4.3 %collective-permute-start.53 = (f32[2,8192]{1,0:T(2,128)S(1)}, f32[2,8192]{1,0:T(2,128)S(1)}, u32[]{:S(2)}, u32[]{:S(2)}) collective-permute-start(f32[2,8192]{1,0:T(2,128)S(1)} %maximum_select_fusion.12), channel_id=1, source_target_pairs={{0,32},{4,36},{8,40},{12,44},{16,48},{20,52},{24,56},{28,60},{32,0... | collective-permute-start | bytes 196616 | tf_op jit(solution)/shard_map/ppermute | solution.py:202
  256.7 6.6 %collective-permute-start.54 = (f32[4,8192]{1,0:T(4,128)S(1)}, f32[4,8192]{1,0:T(4,128)S(1)}, u32[]{:S(2)}, u32[]{:S(2)}) collective-permute-start(f32[4,8192]{1,0:T(4,128)S(1)} %maximum_select_fusion.9), channel_id=1, source_target_pairs={{0,16},{4,20},{8,24},{12,28},{16,0},{20,4},{24,8},{28,12},{32,48},... | collective-permute-start | bytes 393224 | tf_op jit(solution)/shard_map/ppermute | solution.py:202
  263.4 6.5 %collective-permute-start.55 = (f32[8,8192]{1,0:T(8,128)S(1)}, f32[8,8192]{1,0:T(8,128)S(1)}, u32[]{:S(2)}, u32[]{:S(2)}) collective-permute-start(f32[8,8192]{1,0:T(8,128)S(1)} %maximum_select_fusion.6), channel_id=1, source_target_pairs={{0,8},{4,12},{8,0},{12,4},{16,24},{20,28},{24,16},{28,20},{32,40},... | collective-permute-start | bytes 786440 | tf_op jit(solution)/shard_map/ppermute | solution.py:202
  293.1 7.8 %collective-permute-start.58 = (f32[1,4,1,32,64]{4,3,2,1,0:T(8,128)S(1)}, f32[1,4,1,32,64]{4,3,2,1,0:T(8,128)S(1)}, u32[]{:S(2)}, u32[]{:S(2)}) collective-permute-start(f32[1,4,1,32,64]{4,3,2,1,0:T(8,128)S(1)} %get-tuple-element.87), channel_id=1, source_target_pairs={{1,0},{2,1},{3,2},{5,4},{6,5},{7,6},{9,8},{10,9},{11,10},{13,12},{... | collective-permute-start | bytes 98312 | tf_op jit(solution)/shard_map/ppermute | solution.py:26
  294.4 6.5 %collective-permute-start.59 = (f32[1,4,1,32,64]{4,3,2,1,0:T(8,128)S(1)}, f32[1,4,1,32,64]{4,3,2,1,0:T(8,128)S(1)}, u32[]{:S(2)}, u32[]{:S(2)}) collective-permute-start(f32[1,4,1,32,64]{4,3,2,1,0:T(8,128)S(1)} %get-tuple-element.88), channel_id=1, source_target_pairs={{0,1},{1,2},{2,3},{4,5},{5,6},{6,7},{8,9},{9,10},{10,11},{12,13},{... | collective-permute-start | bytes 98312 | tf_op jit(solution)/shard_map/ppermute | solution.py:23
  299.0 8.4 %collective-permute-start.57 = (f32[1,4,2,32,64]{4,3,2,1,0:T(8,128)S(1)}, f32[1,4,2,32,64]{4,3,2,1,0:T(8,128)S(1)}, u32[]{:S(2)}, u32[]{:S(2)}) collective-permute-start(f32[1,4,2,32,64]{4,3,2,1,0:T(8,128)S(1)} %fusion.233), channel_id=1, source_target_pairs={{0,4},{4,8},{8,12},{12,16},{16,20},{20,24},{24,28},{28,32},{32,36}... | collective-permute-start | bytes 196616 | tf_op jit(solution)/shard_map/ppermute | solution.py:34
  308.0 12.6 %collective-permute-start.60 = (f32[1,4,4,64,128]{4,3,2,1,0:T(8,128)S(1)}, f32[1,4,4,64,128]{4,3,2,1,0:T(8,128)S(1)}, u32[]{:S(2)}, u32[]{:S(2)}) collective-permute-start(f32[1,4,4,64,128]{4,3,2,1,0:T(8,128)S(1)} %add.567), channel_id=1, source_target_pairs={{0,4},{4,8},{8,12},{12,16},{16,20},{20,24},{24,28},{28,32},{32,36}... | collective-permute-start | bytes 1572872 | tf_op jit(solution)/shard_map/ppermute | solution.py:34
  309.9 6.9 %collective-permute-start.61 = (f32[1,4,1,64,128]{4,3,2,1,0:T(8,128)S(1)}, f32[1,4,1,64,128]{4,3,2,1,0:T(8,128)S(1)}, u32[]{:S(2)}, u32[]{:S(2)}) collective-permute-start(f32[1,4,1,64,128]{4,3,2,1,0:T(8,128)S(1)} %get-tuple-element.39), channel_id=1, source_target_pairs={{1,0},{2,1},{3,2},{5,4},{6,5},{7,6},{9,8},{10,9},{11,10},{13,12},{... | collective-permute-start | bytes 393224 | tf_op jit(solution)/shard_map/ppermute | solution.py:26
  311.2 7.1 %collective-permute-start.62 = (f32[1,4,1,64,128]{4,3,2,1,0:T(8,128)S(1)}, f32[1,4,1,64,128]{4,3,2,1,0:T(8,128)S(1)}, u32[]{:S(2)}, u32[]{:S(2)}) collective-permute-start(f32[1,4,1,64,128]{4,3,2,1,0:T(8,128)S(1)} %get-tuple-element.40), channel_id=1, source_target_pairs={{0,1},{1,2},{2,3},{4,5},{5,6},{6,7},{8,9},{9,10},{10,11},{12,13},{... | collective-permute-start | bytes 393224 | tf_op jit(solution)/shard_map/ppermute | solution.py:23
  321.1 12.6 %collective-permute-start.63 = (f32[1,4,4,64,128]{4,3,2,1,0:T(8,128)S(1)}, f32[1,4,4,64,128]{4,3,2,1,0:T(8,128)S(1)}, u32[]{:S(2)}, u32[]{:S(2)}) collective-permute-start(f32[1,4,4,64,128]{4,3,2,1,0:T(8,128)S(1)} %fusion.25), channel_id=1, source_target_pairs={{0,4},{4,8},{8,12},{12,16},{16,20},{20,24},{24,28},{28,32},{32,36}... | collective-permute-start | bytes 1572872 | tf_op jit(solution)/shard_map/ppermute | solution.py:34
  323.1 6.9 %collective-permute-start.64 = (f32[1,4,1,64,128]{4,3,2,1,0:T(8,128)S(1)}, f32[1,4,1,64,128]{4,3,2,1,0:T(8,128)S(1)}, u32[]{:S(2)}, u32[]{:S(2)}) collective-permute-start(f32[1,4,1,64,128]{4,3,2,1,0:T(8,128)S(1)} %get-tuple-element.35), channel_id=1, source_target_pairs={{1,0},{2,1},{3,2},{5,4},{6,5},{7,6},{9,8},{10,9},{11,10},{13,12},{... | collective-permute-start | bytes 393224 | tf_op jit(solution)/shard_map/ppermute | solution.py:26
  324.4 7.1 %collective-permute-start.65 = (f32[1,4,1,64,128]{4,3,2,1,0:T(8,128)S(1)}, f32[1,4,1,64,128]{4,3,2,1,0:T(8,128)S(1)}, u32[]{:S(2)}, u32[]{:S(2)}) collective-permute-start(f32[1,4,1,64,128]{4,3,2,1,0:T(8,128)S(1)} %get-tuple-element.36), channel_id=1, source_target_pairs={{0,1},{1,2},{2,3},{4,5},{5,6},{6,7},{8,9},{9,10},{10,11},{12,13},{... | collective-permute-start | bytes 393224 | tf_op jit(solution)/shard_map/ppermute | solution.py:23
  (26 other events, 305.0 us)
